TPU v7x, 32 devices: a whole 2x2x4 slice. The times are simulated.
32 devices in a mesh: dp: 4 (over z), lat: 4 (over y, core), lon: 2 (over x).
Axes of the slice: x: 2, y: 2, z: 4, core: 2. Of those that a mesh axis runs over, the one named last changes fastest.
Arguments:
- projected: bfloat16 [4, 4, 32, 16, 4608], P('dp', None, 'lat', 'lon'), may hold values from -52 to 52
- targets: bfloat16 [4, 4, 32, 16, 160], P('dp', None, 'lat', 'lon'), may hold values from -6 to 6
- valid_cells: int32 [32, 16], P('lat', 'lon'), may hold values 0 or 1
- w_out: bfloat16 [1536, 1536], P('dp'), may hold values from -0.15625 to 0.15625
- unpatch_matrix: bfloat16 [1536, 160], P('dp'), may hold values from -0.15625 to 0.15625
- norm_gain: bfloat16 [1536], P('dp'), may hold values from 0.099609375 to 1.8984375
- var_weight: float32 [5], replicated, may hold values from 0.3 to 3
Outputs:
- grad_context: bfloat16 [4, 4, 32, 16, 1536], P('dp', None, 'lat', 'lon')
- grad_recovery: float32 [1536, 160], P('dp')
- sample_penalty: float32 [4], P('dp')
All inputs are finite; a program needn't handle non-finite values. No bound on the sum of `valid_cells` on one device may be relied on, other than what follows from the above.
Results may differ from a plain program's by a relative error of at most 0.011.
Values may be sent and summed in bfloat16 or wider, within the bound.
No kernel may reach another device: no remote copies, remote signals or barrier semaphores. Data moves between devices by JAX's collectives and lax.ppermute only.
A program may use at most 64 MiB of HBM per device.

v0:
```python
import math

import jax
import jax.numpy as jnp
from jax import lax
from jax.sharding import PartitionSpec as P

HEADS = 48
HDIM = 32
WLEV = 2


def from_behind(array, axis, by):
    length = lax.axis_size(axis)
    return lax.ppermute(array, axis, [(i, (i + by) % length) for i in range(length)])


def shards(projected, targets, valid_cells, w_out, unpatch_matrix, norm_gain, var_weight):
    tile_side = projected.shape[2]
    half_side = tile_side // 2
    levels = projected.shape[1]
    model_width = w_out.shape[1]
    predicted_span = unpatch_matrix.shape[1]
    lat_total = tile_side * lax.axis_size("lat")
    lon_total = tile_side * lax.axis_size("lon")
    lat_place = lax.axis_index("lat")
    moved = from_behind(
        (projected[:, :, :, :half_side], targets[:, :, :, :half_side], valid_cells[:, :half_side]),
        "lon",
        -1,
    )
    strip_proj = jnp.concatenate([projected[:, :, :, half_side:], moved[0]], axis=3)
    strip_goal = jnp.concatenate([targets[:, :, :, half_side:], moved[1]], axis=3)
    strip_valid = jnp.concatenate([valid_cells[:, half_side:], moved[2]], axis=1)
    moved_rows = from_behind(
        (strip_proj[:, :, :half_side], strip_goal[:, :, :half_side], strip_valid[:half_side]),
        "lat",
        -1,
    )
    local_proj = jnp.concatenate([strip_proj[:, :, half_side:], moved_rows[0]], axis=2)
    shard_reference = jnp.concatenate([strip_goal[:, :, half_side:], moved_rows[1]], axis=2)
    local_valid = jnp.concatenate([strip_valid[half_side:], moved_rows[2]], axis=0).astype(
        jnp.float32
    )
    win_count = levels // WLEV
    tokw = WLEV * tile_side * tile_side
    windows = local_proj.reshape(win_count, tokw, 3 * model_width)
    rows_here = lat_place * tile_side + jnp.arange(tile_side)
    region_rows = (rows_here >= lat_total - half_side).astype(jnp.int32)
    region = jnp.broadcast_to(region_rows[None, :, None], (WLEV, tile_side, tile_side)).reshape(-1)
    allowed = region[:, None] == region[None, :]
    queries = windows[..., :model_width].reshape(win_count, tokw, HEADS, -1)
    key_heads = windows[..., model_width : 2 * model_width].reshape(win_count, tokw, HEADS, -1)
    value_heads = windows[..., 2 * model_width :].reshape(win_count, tokw, HEADS, -1)
    scores = jnp.einsum("wqhd,wkhd->whqk", queries, key_heads, preferred_element_type=jnp.float32)
    scores = scores * (1.0 / math.sqrt(HDIM))
    scores = jnp.where(allowed[None, None], scores, -1e30)
    row_peak = jnp.max(scores, axis=-1, keepdims=True)
    lifted = jnp.exp(scores - row_peak)
    attn = (lifted / jnp.sum(lifted, axis=-1, keepdims=True)).astype(jnp.bfloat16)
    context = jnp.einsum("whqk,wkhd->wqhd", attn, value_heads, preferred_element_type=jnp.float32)
    context = context.astype(jnp.bfloat16).reshape(win_count * tokw, model_width)
    element_total = win_count * tokw
    out_all, unprojected_pieces, gain_all = (
        lax.all_gather(w_out, "dp", axis=0, tiled=True),
        lax.all_gather(unpatch_matrix, "dp", axis=0, tiled=True),
        lax.all_gather(norm_gain, "dp", axis=0, tiled=True),
    )
    mixed_rows = jnp.dot(context, out_all, preferred_element_type=jnp.float32)
    centre = jnp.mean(mixed_rows, axis=-1, keepdims=True)
    spread = jnp.mean((mixed_rows - centre) ** 2, axis=-1, keepdims=True)
    inv_spread = lax.rsqrt(spread + 1e-05)
    normed = (mixed_rows - centre) * inv_spread
    gain_f = gain_all.astype(jnp.float32)
    latent_activation = (normed * gain_f).astype(jnp.bfloat16)
    prediction_field = jnp.dot(
        latent_activation, unprojected_pieces, preferred_element_type=jnp.float32
    )
    prediction_misfit = prediction_field - shard_reference.reshape(
        element_total, predicted_span
    ).astype(jnp.float32)
    all_rows = jnp.arange(lat_total).astype(jnp.float32)
    cosine_mean = jnp.mean(jnp.cos(math.pi * ((all_rows + 0.5) / lat_total - 0.5)))
    initial_rows = ((rows_here + half_side) % lat_total).astype(jnp.float32)
    lat_here = jnp.cos(math.pi * ((initial_rows + 0.5) / lat_total - 0.5)) / cosine_mean
    element_factor = jnp.broadcast_to(
        lat_here[None, :, None] * local_valid[None], (levels, tile_side, tile_side)
    ).reshape(element_total, 1)
    variable_factor = jnp.repeat(var_weight, predicted_span // var_weight.shape[0])[None, :]
    shard_penalty = jnp.sum(
        element_factor * variable_factor * prediction_misfit * prediction_misfit
    ) / (levels * lat_total * lon_total * (predicted_span // var_weight.shape[0]))
    prediction_gradient = (2.0 * element_factor * variable_factor * prediction_misfit).astype(
        jnp.bfloat16
    )
    grad_shard = lax.psum_scatter(
        jnp.einsum(
            "td,to->do", latent_activation, prediction_gradient, preferred_element_type=jnp.float32
        ).astype(jnp.bfloat16),
        "dp",
        scatter_dimension=0,
        tiled=True,
    ).astype(jnp.float32)
    grad_sum, loss_sum = lax.psum((grad_shard, shard_penalty), ("lat", "lon"))
    grad_recovery = grad_sum / (levels * lat_total * lon_total)
    grad_hidden = jnp.einsum(
        "to,do->td", prediction_gradient, unprojected_pieces, preferred_element_type=jnp.float32
    )
    scaled_grad = grad_hidden * gain_f
    grad_mixed = inv_spread * (
        scaled_grad
        - jnp.mean(scaled_grad, axis=-1, keepdims=True)
        - normed * jnp.mean(scaled_grad * normed, axis=-1, keepdims=True)
    )
    grad_mixed = grad_mixed.astype(jnp.bfloat16)
    grad_context = jnp.einsum("tj,ij->ti", grad_mixed, out_all, preferred_element_type=jnp.float32)
    grad_context = grad_context.astype(jnp.bfloat16).reshape(
        1, levels, tile_side, tile_side, model_width
    )
    return (grad_context, grad_recovery, loss_sum.reshape(1))


def solution(mesh):
    placed = (
        P("dp", None, "lat", "lon", None),
        P("dp", None, "lat", "lon", None),
        P("lat", "lon"),
        P("dp", None),
        P("dp", None),
        P("dp"),
        P(),
    )
    return jax.shard_map(
        shards,
        mesh=mesh,
        in_specs=placed,
        out_specs=(P("dp", None, "lat", "lon", None), P("dp", None), P("dp")),
        check_vma=False,
    )
```

profile of v0, /device:TPU:0, one launch (start us, length us, event | category | flops | bytes accessed | tf_op | source)
XLA Modules:
  0.0 177.8 jit_solution(18439652945624654499)
XLA Ops:
  7.2 0.0 all-gather.3.cloned.1.call-start
  7.2 0.7 all-gather.3.cloned.1.call-update
  7.9 0.0 reduce-scatter.4.cloned.1.call-start
  7.9 3.3 %fusion.33 = (bf16[1,4,8,4,4608]{4,3,2,1,0:T(4,128)(2,1)S(1)}, bf16[1,4,8,4,4608]{4,3,2,1,0:T(4,128)(2,1)S(1)}) fusion(bf16[1,4,8,8,4608]{4,3,2,1,0:T(8,128)(2,1)} %param.7), kind=kLoop, calls=%fused_computation.70 | loop fusion | bytes 4718592 | tf_op jit(solution)/shard_map/slice | solution.py:32
  11.2 0.0 copy-start.6
  11.2 0.0 copy-start.3
  11.3 0.0 copy-start.7
  11.3 0.0 copy-start.4
  11.3 0.2 copy.37
  11.5 3.0 %collective-permute-start = (bf16[1,4,8,4,4608]{4,2,3,1,0:T(8,128)(2,1)S(1)}, bf16[1,4,8,4,4608]{4,2,3,1,0:T(8,128)(2,1)}, u32[]{:S(2)}, u32[]{:S(2)}) collective-permute-start(bf16[1,4,8,4,4608]{4,2,3,1,0:T(8,128)(2,1)S(1)} %copy.37), channel_id=1, source_target_pairs={{0,1},{1,0},{2,3},{3,2},{4,5},{5,4},{6,7},{7,6},{8,9},{9,8},{10,11... | collective-permute-start | bytes 3538952 | tf_op jit(solution)/shard_map/ppermute | solution.py:15
  14.5 0.6 fusion.36
  15.1 0.4 collective-permute-start.2
  15.5 1.7 collective-permute-start.4
  17.2 0.1 broadcast_in_dim.18
  17.3 0.1 eq.21
  17.4 13.0 %all-gather = bf16[4,1,384]{2,1,0:T(2,128)(2,1)S(1)} all-gather(bf16[1,1,384]{2,1,0:T(2,128)(2,1)S(1)} %reshape.165), channel_id=1, replica_groups=mesh['dp'=4,'lat'=4,'lon'=2] {'dp'}, dimensions={0}, use_global_device_ids=true | all-gather | bytes 3840 | tf_op jit(solution)/shard_map/all_gather | solution.py:67
  30.4 0.6 cosine_reduce_fusion
  31.7 0.6 fusion.27
  32.3 21.7 %all_gather.11 = bf16[1536,160]{0,1:T(8,128)(2,1)S(1)} all-gather(bf16[384,160]{0,1:T(8,128)(2,1)S(1)} %copy-done.4), channel_id=1, replica_groups=mesh['dp'=4,'lat'=4,'lon'=2] {'dp'}, dimensions={0}, use_global_device_ids=true | all-gather | bytes 614400 | tf_op jit(solution)/shard_map/all_gather | solution.py:66
  54.0 0.7 broadcast_compare_fusion
  54.7 0.0 collective-permute-done
  54.7 1.9 %copy.27 = bf16[1,4,8,4,4608]{4,3,2,1,0:T(4,128)(2,1)S(1)} copy(bf16[1,4,8,4,4608]{4,2,3,1,0:T(8,128)(2,1)} %collective-permute-done) | data formatting | bytes 2359296 | tf_op jit(solution)/shard_map/ppermute | solution.py:15
  56.6 0.0 copy-start.8
  56.6 0.0 copy-start.9
  56.6 2.2 %fusion.8 = (bf16[1,4,4,8,4608]{4,3,2,1,0:T(8,128)(2,1)S(1)}, bf16[1,4,4,8,4608]{4,3,2,1,0:T(8,128)(2,1)}) fusion(bf16[1,4,8,4,4608]{4,3,2,1,0:T(4,128)(2,1)S(1)} %get-tuple-element.12, bf16[1,4,8,4,4608]{4,3,2,1,0:T(4,128)(2,1)S(1)} %copy.27), kind=kLoop, calls=%fused_computation.22 | loop fusion | flops 4718592 | bytes 4718592 | tf_op jit(solution)/shard_map/concatenate | solution.py:32
  58.8 0.0 collective-permute-start.1
  58.8 0.0 collective-permute-done.2
  58.8 0.1 pad_add_fusion
  58.9 1.6 collective-permute-start.3
  60.5 0.1 broadcast_in_dim.22
  60.6 0.1 mul.132
  60.6 12.2 %collective-permute-done.3 = s32[4,8]{1,0:T(4,128)S(1)} collective-permute-done((s32[4,8]{1,0:T(4,128)S(1)}, s32[4,8]{1,0:T(4,128)S(1)}, u32[]{:S(2)}, u32[]{:S(2)}) %collective-permute-start.3) | collective-permute-done | bytes 160 | tf_op jit(solution)/shard_map/ppermute | solution.py:15
  72.8 0.0 copy-done.9
  72.8 0.1 fusion.20
  72.9 0.1 reshape.161
  73.0 0.0 collective-permute-done.4
  73.0 0.1 fusion.19
  73.1 2.5 %collective-permute-start.5 = (bf16[1,4,4,8,160]{4,3,2,1,0:T(8,128)(2,1)S(1)}, bf16[1,4,4,8,160]{4,3,2,1,0:T(8,128)(2,1)S(1)}, u32[]{:S(2)}, u32[]{:S(2)}) collective-permute-start(bf16[1,4,4,8,160]{4,3,2,1,0:T(8,128)(2,1)S(1)} %get-tuple-element.17), channel_id=1, source_target_pairs={{0,6},{2,0},{4,2},{6,4},{1,7},{3,1},{5,3},{7,5},{8,14},{10,8},{12,... | collective-permute-start | bytes 122888 | tf_op jit(solution)/shard_map/ppermute | solution.py:15
  75.5 1.9 %collective-permute-done.5 = bf16[1,4,4,8,160]{4,3,2,1,0:T(8,128)(2,1)S(1)} collective-permute-done((bf16[1,4,4,8,160]{4,3,2,1,0:T(8,128)(2,1)S(1)}, bf16[1,4,4,8,160]{4,3,2,1,0:T(8,128)(2,1)S(1)}, u32[]{:S(2)}, u32[]{:S(2)}) %collective-permute-start.5) | collective-permute-done | bytes 40992 | tf_op jit(solution)/shard_map/ppermute | solution.py:15
  77.5 0.1 copy.33
  77.6 0.0 collective-permute-done.1
  77.6 0.2 pad_maximum_fusion
  77.8 0.2 fusion.32
  78.1 1.2 copy.29
  79.2 1.2 copy.30
  80.4 1.2 copy.28
  81.6 4.2 %fusion.37 = (f32[2,48,128]{2,1,0:T(8,128)S(1)}, f32[2,48,128,128]{2,3,1,0:T(8,128)}) fusion(pred[128,128]{0,1:T(8,128)(4,1)S(1)} %copy-done.5, bf16[2,128,48,32]{1,3,2,0:T(8,128)(2,1)S(1)} %bitcast.35, bf16[2,128,48,32]{1,3,2,0:T(8,128)(2,1)S(1)} %bitcast.36), kind=kOutput, calls=%fused_computation.74 | convolution fusion | flops 106954880 | bytes 7929856 | tf_op jit(solution)/shard_map/sub | solution.py:59
  85.7 3.7 %fusion.7 = bf16[2,128,48,32]{1,3,2,0:T(8,128)(2,1)S(1)} fusion(bf16[2,128,48,32]{1,3,2,0:T(8,128)(2,1)S(1)} %bitcast.37, f32[2,48,128,128]{2,3,1,0:T(8,128)} %get-tuple-element.25, f32[2,48,128]{2,1,0:T(8,128)S(1)} %get-tuple-element.24), kind=kOutput, calls=%fused_computation.21 | convolution fusion | flops 104202240 | bytes 7913472 | tf_op jit(solution)/shard_map/whqk,wkhd->wqhd/dot_general | solution.py:61
  89.5 0.8 copy.32
  90.3 19.3 %all-gather.3.cloned.1.call-done = bf16[1536,1536]{1,0:T(8,128)(2,1)} async-done(((bf16[384,1536]{1,0:T(8,128)(2,1)}), bf16[1536,1536]{1,0:T(8,128)(2,1)}) %all-gather.3.cloned.1.call-update) | async-done | bytes 4718608 | tf_op jit(solution)/shard_map/all_gather | solution.py:65
  109.6 3.8 %fusion.38 = (f32[256]{0:T(256)S(1)}, f32[256,1536]{1,0:T(8,128)S(1)}) fusion(bf16[1536,1536]{1,0:T(8,128)(2,1)} %all-gather.3.cloned.1.call-done, bf16[192,8,2,128]{3,2,1,0:T(2,128)(2,1)S(1)} %bitcast.38), kind=kOutput, calls=%fused_computation.75 | convolution fusion | flops 1208352512 | bytes 7078912 | tf_op jit(solution)/shard_map/dot_general | solution.py:69
  113.4 0.3 multiply_reduce_fusion.1
  113.7 0.3 multiply_convert_fusion.1
  114.0 0.4 fusion.39
  114.4 0.7 fusion.18
  115.2 0.3 convolution_convert_fusion.1
  115.5 1.2 copy.35
  116.6 0.0 reduce-scatter.4.cloned.1.call-update
  117.3 0.6 fusion.31
  117.9 4.8 %convolution_convert_fusion = bf16[256,1536]{1,0:T(8,128)(2,1)} fusion(bf16[1536,1536]{1,0:T(8,128)(2,1)} %all-gather.3.cloned.1.call-done, f32[256,1536]{1,0:T(8,128)S(1)} %get-tuple-element.28, f32[256,1536]{1,0:T(8,128)S(1)} %get-tuple-element.27, f32[256]{0:T(256)S(1)} %get-tuple-element.29, f32[256]{0:T(256)S(1)} %get-tuple-element.30, ...), kind=kOutput, calls=%fused_computation.10 | convolution fusion | flops 1211105280 | bytes 8654848 | tf_op jit(solution)/shard_map/tj,ij->ti/dot_general | solution.py:116
  122.7 15.9 %reduce-scatter.4.cloned.1.call-done = bf16[384,160]{1,0:T(8,128)(2,1)} async-done(((bf16[1536,160]{1,0:T(8,128)(2,1)}), bf16[384,160]{1,0:T(8,128)(2,1)}) %reduce-scatter.4.cloned.1.call-update) | async-done | bytes 122896
  138.6 1.1 copy.36
  139.7 30.5 %all-reduce.2 = (f32[384,160]{0,1:T(8,128)S(1)}, f32[1]{0:T(128)}) all-reduce(bf16[384,160]{0,1:T(8,128)(2,1)S(1)} %copy.36, f32[1]{0:T(128)} %bitcast.7), channel_id=1, replica_groups=mesh['dp'=4,'lat'=4,'lon'=2] {'lat','lon'}, use_global_device_ids=true, to_apply=%region_8.9 | all-reduce | flops 61441 | bytes 368648 | tf_op jit(solution)/shard_map/psum | solution.py:104
  170.2 0.7 broadcast_multiply_fusion
  (26 shorter events, 0.2 us)
Async XLA Ops:
  7.2 102.4 %all-gather.3.cloned.1.call-start = ((), (), s32[]{:S(2)}) async-start(), calls=%async_computation.1 | async-start | bytes 5898240 | tf_op jit(solution)/shard_map/all_gather | solution.py:65
  7.9 130.7 %reduce-scatter.4.cloned.1.call-start = ((), (), s32[]{:S(2)}) async-start(), calls=%async_computation.2 | async-start | bytes 983040
  11.2 3.3 %copy-start.6 = (s32[8,8]{1,0:T(8,128)S(1)}, s32[8,8]{1,0:T(8,128)}, u32[]{:S(2)}) copy-start(s32[8,8]{1,0:T(8,128)} %param.9) | copy-start | bytes 772
  11.2 4.2 %copy-start.3 = (bf16[1,4,8,8,160]{4,3,2,1,0:T(8,128)(2,1)S(1)}, bf16[1,4,8,8,160]{4,3,2,1,0:T(8,128)(2,1)}, u32[]{:S(2)}) copy-start(bf16[1,4,8,8,160]{4,3,2,1,0:T(8,128)(2,1)} %param.8) | copy-start | bytes 245764
  11.3 6.1 %copy-start.7 = (bf16[384]{0:T(512)(128)(2,1)S(1)}, bf16[384]{0:T(512)(128)(2,1)}, u32[]{:S(2)}) copy-start(bf16[384]{0:T(512)(128)(2,1)} %param.12) | copy-start | bytes 2308
  11.3 21.0 %copy-start.4 = (bf16[384,160]{0,1:T(8,128)(2,1)S(1)}, bf16[384,160]{0,1:T(8,128)(2,1)}, u32[]{:S(2)}) copy-start(bf16[384,160]{0,1:T(8,128)(2,1)} %param.11) | copy-start | bytes 368644
  11.5 43.2 %collective-permute-start = (bf16[1,4,8,4,4608]{4,2,3,1,0:T(8,128)(2,1)S(1)}, bf16[1,4,8,4,4608]{4,2,3,1,0:T(8,128)(2,1)}, u32[]{:S(2)}, u32[]{:S(2)}) collective-permute-start(bf16[1,4,8,4,4608]{4,2,3,1,0:T(8,128)(2,1)S(1)} %copy.37), channel_id=1, source_target_pairs={{0,1},{1,0},{2,3},{3,2},{4,5},{5,4},{6,7},{7,6},{8,9},{9,8},{10,11... | collective-permute-start | bytes 3538952 | tf_op jit(solution)/shard_map/ppermute | solution.py:15
  15.1 43.7 %collective-permute-start.2 = (s32[8,4]{1,0:T(8,128)}, s32[8,4]{1,0:T(8,128)S(1)}, u32[]{:S(2)}, u32[]{:S(2)}) collective-permute-start(s32[8,4]{1,0:T(8,128)} %get-tuple-element.23), channel_id=1, source_target_pairs={{0,1},{1,0},{2,3},{3,2},{4,5},{5,4},{6,7},{7,6},{8,9},{9,8},{10,11... | collective-permute-start | bytes 392 | tf_op jit(solution)/shard_map/ppermute | solution.py:15
  15.5 57.5 %collective-permute-start.4 = (bf16[1,4,8,4,160]{4,3,2,1,0:T(4,128)(2,1)S(1)}, bf16[1,4,8,4,160]{4,3,2,1,0:T(4,128)(2,1)S(1)}, u32[]{:S(2)}, u32[]{:S(2)}) collective-permute-start(bf16[1,4,8,4,160]{4,3,2,1,0:T(4,128)(2,1)S(1)} %get-tuple-element.19), channel_id=1, source_target_pairs={{0,1},{1,0},{2,3},{3,2},{4,5},{5,4},{6,7},{7,6},{8,9},{9,8},{10,11... | collective-permute-start | bytes 122888 | tf_op jit(solution)/shard_map/ppermute | solution.py:15
  56.6 3.9 %copy-start.8 = (f32[5]{0:T(128)S(1)}, f32[5]{0:T(128)}, u32[]{:S(2)}) copy-start(f32[5]{0:T(128)} %param.13) | copy-start | bytes 64
  56.6 16.2 %copy-start.9 = (f32[8]{0:T(128)S(1)}, f32[8]{0:T(128)}, u32[]{:S(2)}) copy-start(f32[8]{0:T(128)} %fusion.27) | copy-start | bytes 100
  58.8 18.8 %collective-permute-start.1 = (bf16[1,4,4,8,4608]{4,3,2,1,0:T(8,128)(2,1)}, bf16[1,4,4,8,4608]{4,3,2,1,0:T(8,128)(2,1)S(1)}, u32[]{:S(2)}, u32[]{:S(2)}) collective-permute-start(bf16[1,4,4,8,4608]{4,3,2,1,0:T(8,128)(2,1)} %get-tuple-element.11), channel_id=1, source_target_pairs={{0,6},{2,0},{4,2},{6,4},{1,7},{3,1},{5,3},{7,5},{8,14},{10,8},{12,... | collective-permute-start | bytes 3538952 | tf_op jit(solution)/shard_map/ppermute | solution.py:15
  58.9 14.0 %collective-permute-start.3 = (s32[4,8]{1,0:T(4,128)S(1)}, s32[4,8]{1,0:T(4,128)S(1)}, u32[]{:S(2)}, u32[]{:S(2)}) collective-permute-start(s32[4,8]{1,0:T(4,128)S(1)} %get-tuple-element.21), channel_id=1, source_target_pairs={{0,6},{2,0},{4,2},{6,4},{1,7},{3,1},{5,3},{7,5},{8,14},{10,8},{12,... | collective-permute-start | bytes 392 | tf_op jit(solution)/shard_map/ppermute | solution.py:15
  73.1 4.4 %collective-permute-start.5 = (bf16[1,4,4,8,160]{4,3,2,1,0:T(8,128)(2,1)S(1)}, bf16[1,4,4,8,160]{4,3,2,1,0:T(8,128)(2,1)S(1)}, u32[]{:S(2)}, u32[]{:S(2)}) collective-permute-start(bf16[1,4,4,8,160]{4,3,2,1,0:T(8,128)(2,1)S(1)} %get-tuple-element.17), channel_id=1, source_target_pairs={{0,6},{2,0},{4,2},{6,4},{1,7},{3,1},{5,3},{7,5},{8,14},{10,8},{12,... | collective-permute-start | bytes 122888 | tf_op jit(solution)/shard_map/ppermute | solution.py:15
  79.2 2.3 %copy-start = (bf16[2,128,1536]{1,2,0:T(8,128)(2,1)S(1)}, bf16[2,128,1536]{1,2,0:T(8,128)(2,1)}, u32[]{:S(2)}) copy-start(bf16[2,128,1536]{1,2,0:T(8,128)(2,1)} %copy.29) | copy-start | bytes 2359300
  79.2 2.3 %copy-start.5 = (pred[128,128]{0,1:T(8,128)(4,1)S(1)}, pred[128,128]{0,1:T(8,128)(4,1)}, u32[]{:S(2)}) copy-start(pred[128,128]{0,1:T(8,128)(4,1)} %broadcast_compare_fusion) | copy-start | bytes 49156
  80.4 1.2 copy-start.1
  81.6 4.2 %copy-start.2 = (bf16[2,128,1536]{1,2,0:T(8,128)(2,1)S(1)}, bf16[2,128,1536]{1,2,0:T(8,128)(2,1)}, u32[]{:S(2)}) copy-start(bf16[2,128,1536]{1,2,0:T(8,128)(2,1)} %copy.28) | copy-start | bytes 2359300
Sparse Core Ops, SparseCore 0:
  9.6 99.9 all-gather.2
  116.8 21.7 reduce-scatter.3
where the time goes:
time: 178 us
  blocking collectives  65.2 us (37%)
  waiting for transfers between devices  50 us (28%)
  matrix products  17.8 us (10%)
  between operations  15.6 us (9%)
  local copies, waits for them, and re-layouts  13.3 us (7%)
  starting transfers between devices  9.26 us (5%)
  other arithmetic  6.65 us (4%)
    psum x1, blocking collectives, shards(): grad_sum, loss_sum = lax.psum((grad_shard, shard_penalty), ('lat', 'lon'))  30.5 us
    all_gather x1, blocking collectives, shards(): lax.all_gather(unpatch_matrix, 'dp', axis=0, tiled=True)  21.7 us
    all_gather x1, waiting for transfers between devices, shards(): lax.all_gather(w_out, 'dp', axis=0, tiled=True)  19.3 us
    unnamed x3, waiting for transfers between devices  16.6 us
    ppermute x6, waiting for transfers between devices, from_behind(): lax.ppermute(array, axis, [(i, (i + by) % length) for i in range(length)])  14.1 us
    all_gather x1, blocking collectives, shards(): lax.all_gather(norm_gain, 'dp', axis=0, tiled=True)  13 us
    ppermute x6, starting transfers between devices, from_behind(): lax.ppermute(array, axis, [(i, (i + by) % length) for i in range(length)])  9.19 us
    dot_general x1, matrix products, shards(): jnp.einsum('tj,ij->ti', grad_mixed, out_all, preferred_element_type=jnp.f...  4.79 us
  transfers between devices with their start and end apart: 8, of which 4 were waited for; matrix products, arithmetic and copies ran while one was open for 16% of the time, Pallas kernels for 0%

commit v1 on v0

v1 whole, which is shorter than its diff:
```python
import math

import jax
import jax.numpy as jnp
import numpy as np
from jax import lax
from jax.experimental import pallas as pl
from jax.experimental.pallas import tpu as pltpu
from jax.sharding import PartitionSpec as P

HEADS = 48
HDIM = 32
WLEV = 2
BF = jnp.bfloat16
F32 = jnp.float32
EXTRA = 256
UGROWS = 256
VMEM = pl.BlockSpec(memory_space=pltpu.VMEM)
SMEM = pl.BlockSpec(memory_space=pltpu.SMEM)
ANY = pl.BlockSpec(memory_space=pl.ANY)


def from_behind(array, axis, by):
    length = lax.axis_size(axis)
    return lax.ppermute(array, axis, [(i, (i + by) % length) for i in range(length)])


def general_shards(projected, targets, valid_cells, w_out, unpatch_matrix, norm_gain, var_weight):
    tile_side = projected.shape[2]
    half_side = tile_side // 2
    levels = projected.shape[1]
    model_width = w_out.shape[1]
    predicted_span = unpatch_matrix.shape[1]
    lat_total = tile_side * lax.axis_size("lat")
    lon_total = tile_side * lax.axis_size("lon")
    lat_place = lax.axis_index("lat")
    moved = from_behind(
        (projected[:, :, :, :half_side], targets[:, :, :, :half_side], valid_cells[:, :half_side]),
        "lon",
        -1,
    )
    strip_proj = jnp.concatenate([projected[:, :, :, half_side:], moved[0]], axis=3)
    strip_goal = jnp.concatenate([targets[:, :, :, half_side:], moved[1]], axis=3)
    strip_valid = jnp.concatenate([valid_cells[:, half_side:], moved[2]], axis=1)
    moved_rows = from_behind(
        (strip_proj[:, :, :half_side], strip_goal[:, :, :half_side], strip_valid[:half_side]),
        "lat",
        -1,
    )
    local_proj = jnp.concatenate([strip_proj[:, :, half_side:], moved_rows[0]], axis=2)
    shard_reference = jnp.concatenate([strip_goal[:, :, half_side:], moved_rows[1]], axis=2)
    local_valid = jnp.concatenate([strip_valid[half_side:], moved_rows[2]], axis=0).astype(F32)
    win_count = levels // WLEV
    tokw = WLEV * tile_side * tile_side
    windows = local_proj.reshape(win_count, tokw, 3 * model_width)
    rows_here = lat_place * tile_side + jnp.arange(tile_side)
    region_rows = (rows_here >= lat_total - half_side).astype(jnp.int32)
    region = jnp.broadcast_to(region_rows[None, :, None], (WLEV, tile_side, tile_side)).reshape(-1)
    allowed = region[:, None] == region[None, :]
    queries = windows[..., :model_width].reshape(win_count, tokw, HEADS, -1)
    key_heads = windows[..., model_width : 2 * model_width].reshape(win_count, tokw, HEADS, -1)
    value_heads = windows[..., 2 * model_width :].reshape(win_count, tokw, HEADS, -1)
    scores = jnp.einsum("wqhd,wkhd->whqk", queries, key_heads, preferred_element_type=F32)
    scores = scores * (1.0 / math.sqrt(HDIM))
    scores = jnp.where(allowed[None, None], scores, -1e30)
    row_peak = jnp.max(scores, axis=-1, keepdims=True)
    lifted = jnp.exp(scores - row_peak)
    attn = (lifted / jnp.sum(lifted, axis=-1, keepdims=True)).astype(BF)
    context = jnp.einsum("whqk,wkhd->wqhd", attn, value_heads, preferred_element_type=F32)
    context = context.astype(BF).reshape(win_count * tokw, model_width)
    element_total = win_count * tokw
    out_all, unprojected_pieces, gain_all = (
        lax.all_gather(w_out, "dp", axis=0, tiled=True),
        lax.all_gather(unpatch_matrix, "dp", axis=0, tiled=True),
        lax.all_gather(norm_gain, "dp", axis=0, tiled=True),
    )
    mixed_rows = jnp.dot(context, out_all, preferred_element_type=F32)
    centre = jnp.mean(mixed_rows, axis=-1, keepdims=True)
    spread = jnp.mean((mixed_rows - centre) ** 2, axis=-1, keepdims=True)
    inv_spread = lax.rsqrt(spread + 1e-05)
    normed = (mixed_rows - centre) * inv_spread
    gain_f = gain_all.astype(F32)
    latent_activation = (normed * gain_f).astype(BF)
    prediction_field = jnp.dot(latent_activation, unprojected_pieces, preferred_element_type=F32)
    prediction_misfit = prediction_field - shard_reference.reshape(
        element_total, predicted_span
    ).astype(F32)
    all_rows = jnp.arange(lat_total).astype(F32)
    cosine_mean = jnp.mean(jnp.cos(math.pi * ((all_rows + 0.5) / lat_total - 0.5)))
    initial_rows = ((rows_here + half_side) % lat_total).astype(F32)
    lat_here = jnp.cos(math.pi * ((initial_rows + 0.5) / lat_total - 0.5)) / cosine_mean
    element_factor = jnp.broadcast_to(
        lat_here[None, :, None] * local_valid[None], (levels, tile_side, tile_side)
    ).reshape(element_total, 1)
    variable_factor = jnp.repeat(var_weight, predicted_span // var_weight.shape[0])[None, :]
    shard_penalty = jnp.sum(
        element_factor * variable_factor * prediction_misfit * prediction_misfit
    ) / (levels * lat_total * lon_total * (predicted_span // var_weight.shape[0]))
    prediction_gradient = (2.0 * element_factor * variable_factor * prediction_misfit).astype(BF)
    grad_shard = lax.psum_scatter(
        jnp.einsum(
            "td,to->do", latent_activation, prediction_gradient, preferred_element_type=F32
        ).astype(BF),
        "dp",
        scatter_dimension=0,
        tiled=True,
    ).astype(F32)
    grad_sum, loss_sum = lax.psum((grad_shard, shard_penalty), ("lat", "lon"))
    grad_recovery = grad_sum / (levels * lat_total * lon_total)
    grad_hidden = jnp.einsum(
        "to,do->td", prediction_gradient, unprojected_pieces, preferred_element_type=F32
    )
    scaled_grad = grad_hidden * gain_f
    grad_mixed = inv_spread * (
        scaled_grad
        - jnp.mean(scaled_grad, axis=-1, keepdims=True)
        - normed * jnp.mean(scaled_grad * normed, axis=-1, keepdims=True)
    )
    grad_mixed = grad_mixed.astype(BF)
    grad_context = jnp.einsum("tj,ij->ti", grad_mixed, out_all, preferred_element_type=F32)
    grad_context = grad_context.astype(BF).reshape(1, levels, tile_side, tile_side, model_width)
    return (grad_context, grad_recovery, loss_sum.reshape(1))


def params(mib=48):
    return pltpu.CompilerParams(vmem_limit_bytes=mib << 20)


def iota(shape, dim):
    return lax.broadcasted_iota(jnp.int32, shape, dim)


def pack_kernel(x_ref, t_ref, valid_ref, own_ref, east_ref, south_ref, diag_ref):
    count = x_ref.shape[0] * 64
    place = iota((count, count), 0)
    quad, rest = place // (count // 4), place % (count // 4)
    row = (rest // 4) % 4 + jnp.where(quad < 2, 4, 0)
    col = rest % 4 + jnp.where(quad % 2 == 0, 4, 0)
    source = (rest // 16) * 64 + row * 8 + col
    pick = (iota((count, count), 1) == source).astype(F32).astype(BF)
    refs = (own_ref, east_ref, south_ref, diag_ref)
    quarter = count // 4
    width = x_ref.shape[-1]
    step = 512
    for at in range(0, width, step):
        tokens = x_ref[:, :, :, at : at + step].reshape(count, step)
        out = jnp.dot(pick, tokens, preferred_element_type=F32).astype(BF)
        for q, ref in enumerate(refs):
            ref[:, at : at + step] = out[q * quarter : (q + 1) * quarter]
    goal = jnp.dot(pick, t_ref[...].reshape(count, t_ref.shape[-1]), preferred_element_type=F32)
    token = iota((count, 8), 0)
    row_hot = ((token // 8) % 8 == iota((count, 8), 1)).astype(F32)
    by_row = jnp.dot(row_hot, valid_ref[...].astype(F32), preferred_element_type=F32)
    natural = jnp.sum(jnp.where(token % 8 == iota((count, 8), 1), by_row, 0.0), axis=1, keepdims=True)
    spread = jnp.broadcast_to(natural, (count, 128)).astype(BF)
    column = jnp.dot(pick, spread, preferred_element_type=F32)
    span = goal.shape[1]
    extra = jnp.concatenate([goal, column[:, : EXTRA - span]], axis=1).astype(BF)
    for q, ref in enumerate(refs):
        ref[:, width:] = extra[q * quarter : (q + 1) * quarter]


def attention_kernel(last_ref, *refs):
    ctx_ref = refs[12]
    tiles = [refs[3 * q : 3 * q + 3] for q in range(4)]
    is_last = last_ref[0] == 1
    side = iota((128, 512), 0) // 64
    same = side == (iota((128, 512), 1) % 128) // 64
    keep = jnp.logical_or(same, jnp.logical_not(is_last))
    head = iota((128, 128), 1) // HDIM
    factor = math.log2(math.e) / math.sqrt(HDIM)
    for w in range(2):
        q, k, v = [
            jnp.concatenate([tiles[c][i][32 * w : 32 * w + 32] for c in range(4)], axis=0)
            for i in range(3)
        ]
        zero = jnp.zeros_like(k)
        k4 = jnp.concatenate([jnp.where(head == h, k, zero) for h in range(4)], axis=0)
        v4 = jnp.concatenate([jnp.where(head == h, v, zero) for h in range(4)], axis=0)
        s = lax.dot_general(q, k4, (((1,), (1,)), ((), ())), preferred_element_type=F32)
        s = jnp.where(keep, s, -1e30)
        parts = []
        for h in range(4):
            sh = s[:, 128 * h : 128 * h + 128]
            e = jnp.exp2((sh - jnp.max(sh, axis=1, keepdims=True)) * factor)
            parts.append((e / jnp.sum(e, axis=1, keepdims=True)).astype(BF))
        attn = jnp.concatenate(parts, axis=1)
        out = jnp.dot(attn, v4, preferred_element_type=F32)
        ctx_ref[128 * w : 128 * w + 128, :] = out.astype(BF)


def piece_copies(zi, half, own_w, own_ug, rings, swaps, w_all, ug_all, sems):
    rows = own_w.shape[0]
    hr = rows // 2
    steps = len(rings) + 1
    w_copies, u_copies = [], []

    def place(src, dst, to):
        at = sems.at[len(w_copies) + len(u_copies)]
        to.append(pltpu.make_async_copy(src, dst, at))

    base = pl.multiple_of(zi * rows, 128)
    place(own_w, w_all.at[pl.ds(base, rows), :], w_copies)
    place(own_ug, ug_all.at[:, pl.ds(base, rows)], u_copies)
    for k in range(1, steps):
        shard = lax.rem(zi - k + steps, steps)
        base = pl.multiple_of(shard * rows, 128)
        for piece, part in ((rings[k - 1], half), (swaps[k - 1], 1 - half)):
            row = pl.multiple_of(base + part * hr, 64)
            place(piece.at[pl.ds(0, hr), :], w_all.at[pl.ds(row, hr), :], w_copies)
            for j in range(4):
                urow = pl.multiple_of((4 * part + j) * 32, 32)
                place(
                    piece.at[pl.ds(hr, 32), pl.ds(j * rows, rows)],
                    ug_all.at[pl.ds(urow, 32), pl.ds(base, rows)],
                    u_copies,
                )
    return w_copies, u_copies


def split3(x):
    hi = x.astype(BF).astype(F32)
    mid = (x - hi).astype(BF).astype(F32)
    return hi, mid, x - hi - mid


def loss_block(value, rows):
    hi, mid, lo = split3(value)
    lane = iota((rows, 128), 1)
    return jnp.where(lane == 0, hi, jnp.where(lane == 1, mid, jnp.where(lane == 2, lo, 0.0)))


def forward_kernel(
    place_ref, lat_ref, var_ref, ctx_ref, e0, e1, e2, e3, own_w, own_ug, r1, r2, r3, c1, c2, c3,
    t0, t1, t2, t3, normed_ref, inv_ref, dfc_ref, hidden_ref, w_all, ug_all, term, sems,
):
    zi, half, lat_place = place_ref[0], place_ref[1], place_ref[2]
    w_copies, u_copies = piece_copies(
        zi, half, own_w, own_ug, (r1, r2, r3), (c1, c2, c3), w_all, ug_all, sems
    )
    for c in w_copies + u_copies:
        c.start()
    tokens, width = ctx_ref.shape
    span = dfc_ref.shape[1]
    extras = [e0, e1, e2, e3]
    extra = jnp.concatenate(
        [e[32 * w : 32 * w + 32, :] for w in range(2) for e in extras], axis=0
    ).astype(F32)
    goal, valid = extra[:, :span], extra[:, span : span + 1]
    token = iota((tokens, 1), 0)
    row = (token // 4) % 4 + jnp.where((token // 32) % 4 >= 2, 4, 0)
    lat_w = jnp.zeros((tokens, 1), F32)
    for r in range(8):
        lat_w = jnp.where(row == r, lat_ref[lat_place * 8 + r], lat_w)
    lane = iota((1, span), 1) // (span // var_ref.shape[0])
    var_w = jnp.zeros((1, span), F32)
    for n in range(var_ref.shape[0]):
        var_w = jnp.where(lane == n, var_ref[n], var_w)
    weight = lat_w * valid * var_w
    for c in w_copies:
        c.wait()
    mixed = jnp.dot(ctx_ref[...], w_all[...], preferred_element_type=F32)
    centre = jnp.mean(mixed, axis=-1, keepdims=True)
    off = mixed - centre
    inv = lax.rsqrt(jnp.mean(off * off, axis=-1, keepdims=True) + 1e-05)
    normed = off * inv
    normed_ref[...] = normed
    inv_ref[...] = jnp.broadcast_to(inv, inv_ref.shape)
    for c in u_copies:
        c.wait()
    gain = ug_all[pl.ds(span, 16), :][0:1].astype(F32)
    hidden_ref[...] = (normed * gain).astype(BF)
    field = lax.dot_general(
        hidden_ref[...], ug_all[0:span, :], (((1,), (1,)), ((), ())), preferred_element_type=F32
    )
    misfit = field - goal
    dfc = (2.0 * weight * misfit).astype(BF)
    dfc_ref[...] = dfc
    term[...] = lax.dot_general(
        dfc, hidden_ref[...], (((0,), (0,)), ((), ())), preferred_element_type=F32
    )
    loss = jnp.sum(jnp.sum(weight * misfit * misfit, axis=1, keepdims=True), axis=0, keepdims=True)
    rows = t0.shape[0]
    block = loss_block(loss, rows).astype(BF)
    for b, ref in enumerate((t0, t1, t2, t3)):
        at = pl.multiple_of((lat_place ^ b) * rows, 8)
        ref[:, :width] = term[pl.ds(at, rows), :].astype(BF)
        ref[:, width:] = block


def backward_kernel(
    place_ref, normed_ref, inv_ref, dfc_ref, own_w, own_ug, r1, r2, r3, c1, c2, c3,
    out_ref, w_all, ug_all, sems,
):
    zi, half = place_ref[0], place_ref[1]
    w_copies, u_copies = piece_copies(
        zi, half, own_w, own_ug, (r1, r2, r3), (c1, c2, c3), w_all, ug_all, sems
    )
    for c in u_copies + w_copies:
        c.start()
    tokens, width = normed_ref.shape
    span = dfc_ref.shape[1]
    for c in u_copies:
        c.wait()
    gain = ug_all[pl.ds(span, 16), :][0:1].astype(F32)
    g = jnp.dot(dfc_ref[...], ug_all[0:span, :], preferred_element_type=F32) * gain
    normed = normed_ref[...]
    mean_g = jnp.mean(g, axis=-1, keepdims=True)
    mean_gn = jnp.mean(g * normed, axis=-1, keepdims=True)
    dmixed = ((g - mean_g - normed * mean_gn) * inv_ref[:, 0:1]).astype(BF)
    place = iota((tokens, tokens), 0)
    row, col, level = (place // 8) % 8, place % 8, place // 64
    quad = jnp.where(row >= 4, 2, 0) + jnp.where(col >= 4, 1, 0)
    source = (level // 2) * 128 + quad * 32 + (level % 2) * 16 + (row % 4) * 4 + col % 4
    pick = (iota((tokens, tokens), 1) == source).astype(F32).astype(BF)
    dnat = jnp.dot(pick, dmixed, preferred_element_type=F32).astype(BF)
    for c in w_copies:
        c.wait()
    out = lax.dot_general(dnat, w_all[...], (((1,), (1,)), ((), ())), preferred_element_type=F32)
    out_ref[...] = out.astype(BF)


def lat_sum_kernel(a, b, c, d, s_ref):
    total = (a[...].astype(F32) + b[...].astype(F32)) + (c[...].astype(F32) + d[...].astype(F32))
    width = s_ref.shape[1] - 128
    s_ref[:, :width] = total[:, :width].astype(BF)
    loss = jnp.sum(total[0:1, width:], axis=1, keepdims=True)
    s_ref[:, width:] = loss_block(loss, s_ref.shape[0]).astype(BF)


def lon_sum_kernel(denominator, place_ref, a, b, z0, z1, z2, z3, loss_ref, total_ref):
    total = a[...].astype(F32) + b[...].astype(F32)
    total_ref[...] = total
    zi = place_ref[0]
    rows, width = z0.shape
    for k, ref in enumerate((z0, z1, z2, z3)):
        at = pl.multiple_of((zi ^ k) * width, 128)
        ref[...] = total_ref[:, pl.ds(at, width)].astype(BF)
    loss = jnp.sum(total[0:1, 4 * width :], axis=1, keepdims=True) / denominator
    loss_ref[...] = jnp.broadcast_to(loss, loss_ref.shape)


def dp_sum_kernel(denominator, a, b, c, d, o_ref):
    total = (a[...].astype(F32) + b[...].astype(F32)) + (c[...].astype(F32) + d[...].astype(F32))
    o_ref[...] = total / denominator


def join_kernel(place_ref, a, b, c, d, o_ref):
    rows = a.shape[0]
    lat_place = place_ref[2]
    for k, ref in enumerate((a, b, c, d)):
        at = pl.multiple_of((lat_place ^ k) * rows, 8)
        o_ref[pl.ds(at, rows), :] = ref[...]


def swap(array, axis, bit):
    return lax.ppermute(array, axis, [(i, i ^ bit) for i in range(lax.axis_size(axis))])


def shape(dims, dtype):
    return jax.ShapeDtypeStruct(dims, dtype)


def shards(projected, targets, valid_cells, w_out, unpatch_matrix, norm_gain, var_weight):
    dp, lat, lon = lax.axis_size("dp"), lax.axis_size("lat"), lax.axis_size("lon")
    rows, width = w_out.shape
    levels = projected.shape[1]
    span = unpatch_matrix.shape[1]
    tokens = levels * 64
    zi, lat_place = lax.axis_index("dp"), lax.axis_index("lat")
    half = lat_place % 2
    place = jnp.stack([zi, half, lat_place]).astype(jnp.int32)
    last = (lat_place == lat - 1).astype(jnp.int32).reshape(1)
    lat_total = 8 * lat
    angle = math.pi * ((np.arange(lat_total) + 0.5) / lat_total - 0.5)
    cosine = np.cos(angle)
    lat_table = jnp.asarray(np.roll(cosine / cosine.mean(), -4), F32)

    ug = jnp.concatenate(
        [unpatch_matrix.T, norm_gain[None], jnp.zeros((UGROWS - span - 1, rows), BF)], axis=0
    )
    ug_half = lax.dynamic_slice_in_dim(ug, half * (UGROWS // 2), UGROWS // 2, 0)
    ug_half = jnp.concatenate([ug_half[32 * j : 32 * j + 32] for j in range(4)], axis=1)
    payload = jnp.concatenate(
        [lax.dynamic_slice_in_dim(w_out, half * (rows // 2), rows // 2, 0), ug_half], axis=0
    )
    rings, swaps = [], []
    moving = payload
    for _ in range(dp - 1):
        moving = from_behind(moving, "dp", 1)
        rings.append(moving)
        swaps.append(swap(moving, "lat", 1))

    quads = pl.pallas_call(
        pack_kernel,
        out_shape=[shape((tokens // 4, 3 * width + EXTRA), BF)] * 4,
        in_specs=[VMEM] * 3,
        out_specs=[VMEM] * 4,
        compiler_params=params(),
        name="pack",
    )(projected.reshape(levels, 8, 8, 3 * width), targets.reshape(levels, 8, 8, span), valid_cells)
    own = quads[0]
    east = from_behind(quads[1], "lon", -1)
    south = from_behind(quads[2], "lat", -1)
    diag = lax.ppermute(
        quads[3],
        ("lat", "lon"),
        [
            (a * lon + b, ((a - 1) % lat) * lon + (b - 1) % lon)
            for a in range(lat)
            for b in range(lon)
        ],
    )
    tiles = (own, east, south, diag)
    groups = width // 128
    qkv_specs = [
        pl.BlockSpec((tokens // 4, 128), lambda g, i=i: (0, i * groups + g)) for i in range(3)
    ]
    ctx = pl.pallas_call(
        attention_kernel,
        grid=(groups,),
        out_shape=shape((tokens, width), BF),
        in_specs=[SMEM] + qkv_specs * 4,
        out_specs=pl.BlockSpec((tokens, 128), lambda g: (0, g)),
        compiler_params=params(),
        name="attention",
    )(last, *[t for t in tiles for _ in range(3)])

    piece = span // lat
    extra_spec = pl.BlockSpec((tokens // 4, EXTRA), lambda i: (0, 3 * width // EXTRA))
    copies = 2 + 2 * (dp - 1) * 5
    assembly = [
        pltpu.VMEM((dp * rows, width), BF),
        pltpu.VMEM((UGROWS, dp * rows), BF),
    ]
    t0, t1, t2, t3, normed, inv, dfc = pl.pallas_call(
        forward_kernel,
        grid=(1,),
        out_shape=[shape((piece, width + 128), BF)] * 4
        + [shape((tokens, width), F32), shape((tokens, 128), F32), shape((tokens, span), BF)],
        in_specs=[SMEM] * 3 + [VMEM] + [extra_spec] * 4 + [ANY] * 8,
        out_specs=[VMEM] * 7,
        scratch_shapes=[pltpu.VMEM((tokens, width), BF)]
        + assembly
        + [pltpu.VMEM((span, width), F32), pltpu.SemaphoreType.DMA((copies,))],
        compiler_params=params(),
        name="forward",
    )(place, lat_table, var_weight, ctx, *tiles, w_out, ug, *rings, *swaps)

    terms = [t0] + [swap(t, "lat", b) for b, t in ((1, t1), (2, t2), (3, t3))]
    grad_context = pl.pallas_call(
        backward_kernel,
        out_shape=shape((tokens, width), BF),
        in_specs=[SMEM] + [VMEM] * 3 + [ANY] * 8,
        out_specs=VMEM,
        scratch_shapes=assembly + [pltpu.SemaphoreType.DMA((copies,))],
        compiler_params=params(),
        name="backward",
    )(place, normed, inv, dfc, w_out, ug, *rings, *swaps)

    lat_sum = pl.pallas_call(
        lat_sum_kernel,
        out_shape=shape((piece, width + 128), BF),
        in_specs=[VMEM] * 4,
        out_specs=VMEM,
        name="lat_sum",
    )(*terms)
    denominator = levels * lat_total * 8 * lon
    *parts, loss = pl.pallas_call(
        lambda *refs: lon_sum_kernel(float(denominator * (span // var_weight.shape[0])), *refs),
        out_shape=[shape((piece, rows), BF)] * 4 + [shape((8, 128), F32)],
        in_specs=[SMEM] + [VMEM] * 2,
        out_specs=[VMEM] * 5,
        scratch_shapes=[pltpu.VMEM((piece, width + 128), F32)],
        name="lon_sum",
    )(place, lat_sum, swap(lat_sum, "lon", 1))
    parts = [parts[0]] + [swap(parts[k], "dp", k) for k in (1, 2, 3)]
    mine = pl.pallas_call(
        lambda *refs: dp_sum_kernel(float(denominator), *refs),
        out_shape=shape((piece, rows), F32),
        in_specs=[VMEM] * 4,
        out_specs=VMEM,
        name="dp_sum",
    )(*parts)
    joined = pl.pallas_call(
        join_kernel,
        out_shape=shape((span, rows), F32),
        in_specs=[SMEM] + [VMEM] * 4,
        out_specs=VMEM,
        name="join",
    )(place, mine, *[swap(mine, "lat", b) for b in (1, 2, 3)])
    return (
        grad_context.reshape(1, levels, 8, 8, width),
        joined.T,
        loss[0, 0:1],
    )


def solution(mesh):
    placed = (
        P("dp", None, "lat", "lon", None),
        P("dp", None, "lat", "lon", None),
        P("lat", "lon"),
        P("dp", None),
        P("dp", None),
        P("dp"),
        P(),
    )
    fits = mesh.shape["dp"] == 4 and mesh.shape["lat"] == 4 and mesh.shape["lon"] == 2

    def program(*arrays):
        body = shards if fits else general_shards
        return jax.shard_map(
            body,
            mesh=mesh,
            in_specs=placed,
            out_specs=(P("dp", None, "lat", "lon", None), P("dp", None), P("dp")),
            check_vma=False,
        )(*arrays)

    return program
```

time: 178 us -> 143 us (0.80)
  blocking collectives: 65.2 us -> 0 us
  Pallas kernels: 0 us -> 33.6 us
  waiting for transfers between devices: 50 us -> 78.9 us
  matrix products: 17.8 us -> 0 us
  between operations: 15.6 us -> 0.81 us
  starting transfers between devices: 9.26 us -> 16.9 us
  other arithmetic: 6.65 us -> 1.13 us
  local copies, waits for them, and re-layouts: 13.3 us -> 11.5 us
    ppermute x6 -> x5, waiting for transfers between devices: 14.1 us -> 62.4 us  [from_behind(): lax.ppermute(array, axis, [(i, (i + by) % length) for i in range(length)])]
    all_gather x2 -> x0, blocking collectives: 34.7 us -> none  [the longest x1 21.7 us: shards(): lax.all_gather(unpatch_matrix, 'dp', axis=0, tiled=True)]
    pallas_call x0 -> x8, Pallas kernels: none -> 33.6 us  [the longest x1 11.6 us: shards(): pl.pallas_call(attention_kernel, grid=(groups,), out_shape=shape((tokens,...]
    psum x1 -> x0, blocking collectives: 30.5 us -> none  [shards(): grad_sum, loss_sum = lax.psum((grad_shard, shard_penalty), ('lat', 'lon'))]
    all_gather x1 -> x0, waiting for transfers between devices: 19.3 us -> none  [shards(): lax.all_gather(w_out, 'dp', axis=0, tiled=True)]
    unnamed x3 -> x0, waiting for transfers between devices: 16.6 us -> none
    ppermute x0 -> x14, waiting for transfers between devices: none -> 16.4 us  [the longest x13 13.6 us: swap(): lax.ppermute(array, axis, [(i, i ^ bit) for i in range(lax.axis_size(axis...]
    dot_general x6 -> x0, matrix products: 13.6 us -> none  [the longest x1 4.79 us: shards(): jnp.einsum('tj,ij->ti', grad_mixed, out_all, preferred_element_type=jnp.f...]
  transfers between devices with their start and end apart: 8 -> 19, of which waited for: 4 -> 10; matrix products, arithmetic and copies ran while one was open for 16% -> 1% of each run, Pallas kernels for 0% -> 14%
where the time goes in v1:
time: 143 us
  waiting for transfers between devices  78.9 us (55%)
  Pallas kernels  33.6 us (23%)
  starting transfers between devices  16.9 us (12%)
  local copies, waits for them, and re-layouts  11.5 us (8%)
    ppermute x5, waiting for transfers between devices, from_behind(): lax.ppermute(array, axis, [(i, (i + by) % length) for i in range(length)])  62.4 us
    ppermute x13, waiting for transfers between devices, swap(): lax.ppermute(array, axis, [(i, i ^ bit) for i in range(lax.axis_size(axis...  13.6 us
    pallas_call x1, Pallas kernels, shards(): pl.pallas_call(attention_kernel, grid=(groups,), out_shape=shape((tokens,...  11.6 us
    ppermute x13, starting transfers between devices, swap(): lax.ppermute(array, axis, [(i, i ^ bit) for i in range(lax.axis_size(axis...  10.5 us
    unnamed x44, local copies, waits for them, and re-layouts  8.22 us
    pallas_call x1, Pallas kernels, shards(): pl.pallas_call(forward_kernel, grid=(1,), out_shape=[shape((piece, width...  6.72 us
    pallas_call x1, Pallas kernels, shards(): pl.pallas_call(backward_kernel, out_shape=shape((tokens, width), BF), in_...  6.34 us
    ppermute x5, starting transfers between devices, from_behind(): lax.ppermute(array, axis, [(i, (i + by) % length) for i in range(length)])  5.46 us
  transfers between devices with their start and end apart: 19, of which 10 were waited for; matrix products, arithmetic and copies ran while one was open for 1% of the time, Pallas kernels for 14%

profile of v1, /device:TPU:0, one launch (start us, length us, event | category | flops | bytes accessed | tf_op | source)
XLA Modules:
  0.0 142.7 jit_solution(13283666375716535781)
XLA Ops:
  0.7 0.7 broadcast_in_dim.6
  1.3 0.1 pad.7.clone
  1.4 1.3 constant_dynamic-slice_fusion.4
  2.7 1.0 maximum_maximum_fusion.1.own_ug
  3.7 0.1 maximum_maximum_fusion
  3.8 3.1 %collective-permute-start.3 = (bf16[224,1536]{1,0:T(8,128)(2,1)S(1)}, bf16[224,1536]{1,0:T(8,128)(2,1)S(1)}, u32[]{:S(2)}, u32[]{:S(2)}) collective-permute-start(bf16[224,1536]{1,0:T(8,128)(2,1)S(1)} %maximum_maximum_fusion), channel_id=1, source_target_pairs={{0,8},{8,16},{16,24},{24,0},{1,9},{9,17},{17,25},{25,1},{2,10},{10... | collective-permute-start | bytes 2064392 | tf_op jit(solution)/shard_map/ppermute | solution.py:25
  6.9 17.5 %collective-permute-done.3.r1 = bf16[224,1536]{1,0:T(8,128)(2,1)S(1)} collective-permute-done((bf16[224,1536]{1,0:T(8,128)(2,1)S(1)}, bf16[224,1536]{1,0:T(8,128)(2,1)S(1)}, u32[]{:S(2)}, u32[]{:S(2)}) %collective-permute-start.3) | collective-permute-done | bytes 688160 | tf_op jit(solution)/shard_map/ppermute | solution.py:25
  24.3 0.0 collective-permute-start.4
  24.3 18.5 %collective-permute-done.4.r2 = bf16[224,1536]{1,0:T(8,128)(2,1)} collective-permute-done((bf16[224,1536]{1,0:T(8,128)(2,1)S(1)}, bf16[224,1536]{1,0:T(8,128)(2,1)}, u32[]{:S(2)}, u32[]{:S(2)}) %collective-permute-start.4) | collective-permute-done | bytes 688160 | tf_op jit(solution)/shard_map/ppermute | solution.py:25
  42.8 0.0 collective-permute-start.5
  42.9 2.2 %pack.1 = (bf16[64,4864]{1,0:T(8,128)(2,1)S(1)}, bf16[64,4864]{1,0:T(8,128)(2,1)S(1)}, bf16[64,4864]{1,0:T(8,128)(2,1)}, bf16[64,4864]{1,0:T(8,128)(2,1)}) custom-call(bf16[4,8,8,4608]{3,2,1,0:T(8,128)(2,1)S(1)} %bitcast.10, bf16[4,8,8,160]{3,2,1,0:T(8,128)(2,1)S(1)} %bitcast.11, s32[8,8]{1,0:T(8,128)S(1)} %copy-done.9), custom_call_target="tpu_custom_call" | custom-call | tf_op jit(solution)/shard_map/pack/pallas_call | solution.py:394
  45.1 1.2 collective-permute-start
  46.3 0.0 collective-permute-start.6
  46.3 0.5 collective-permute-start.7
  46.8 13.8 %collective-permute-done.5.r3 = bf16[224,1536]{1,0:T(8,128)(2,1)} collective-permute-done((bf16[224,1536]{1,0:T(8,128)(2,1)}, bf16[224,1536]{1,0:T(8,128)(2,1)}, u32[]{:S(2)}, u32[]{:S(2)}) %collective-permute-start.5) | collective-permute-done | bytes 688160 | tf_op jit(solution)/shard_map/ppermute | solution.py:25
  60.7 0.0 collective-permute-start.8
  60.7 1.1 collective-permute-start.1
  61.8 0.0 collective-permute-done.refs_3_.refs_4_.refs_5_.e1
  61.8 0.9 collective-permute-start.2
  62.7 0.1 pad_add_fusion.place_ref.refs_0_
  62.8 12.6 %collective-permute-done.1.refs_6_.refs_7_.refs_8_.e2 = bf16[64,4864]{1,0:T(8,128)(2,1)S(1)} collective-permute-done((bf16[64,4864]{1,0:T(8,128)(2,1)}, bf16[64,4864]{1,0:T(8,128)(2,1)S(1)}, u32[]{:S(2)}, u32[]{:S(2)}) %collective-permute-start.1) | collective-permute-done | bytes 622624 | tf_op jit(solution)/shard_map/ppermute | solution.py:25
  75.5 2.8 %collective-permute-done.2.refs_9_.refs_10_.refs_11_.e3 = bf16[64,4864]{1,0:T(8,128)(2,1)S(1)} collective-permute-done((bf16[64,4864]{1,0:T(8,128)(2,1)}, bf16[64,4864]{1,0:T(8,128)(2,1)S(1)}, u32[]{:S(2)}, u32[]{:S(2)}) %collective-permute-start.2) | collective-permute-done | bytes 622624 | tf_op jit(solution)/shard_map/ppermute | solution.py:405
  78.3 11.6 %attention.1.ctx_ref = bf16[256,1536]{1,0:T(8,128)(2,1)S(1)} custom-call(s32[1]{0:T(128)} %bitcast.3.last_ref, bf16[64,4864]{1,0:T(8,128)(2,1)S(1)} %get-tuple-element.19.refs_0_.refs_1_.refs_2_.e0, bf16[64,4864]{1,0:T(8,128)(2,1)S(1)} %get-tuple-element.19.refs_0_.refs_1_.refs_2_.e0, bf16[64,4864]{1,0:T(8,128)(2,1)S(1)} %get-tuple-element.19.refs_0_.refs_1_.refs_2_.e0, ...), custom_call_target="tpu_custom_call" | custom-call | tf_op jit(solution)/shard_map/attention/pallas_call | solution.py:419
  89.9 0.0 copy-start.1
  89.9 0.9 copy-done.1
  90.7 0.0 collective-permute-done.6.c1
  90.8 0.0 collective-permute-done.7.c2
  90.8 0.0 collective-permute-done.8.c3
  90.8 6.7 %forward.1 = (bf16[40,1664]{1,0:T(8,128)(2,1)S(1)}, bf16[40,1664]{1,0:T(8,128)(2,1)S(1)}, bf16[40,1664]{1,0:T(8,128)(2,1)S(1)}, bf16[40,1664]{1,0:T(8,128)(2,1)S...) custom-call(s32[3]{0:T(128)S(1)} %pad_add_fusion.place_ref.refs_0_, ...), custom_call_target="tpu_custom_call" | custom-call | tf_op jit(solution)/shard_map/forward/pallas_call | solution.py:436
  97.5 0.0 copy-start.3
  97.5 0.6 copy-done.3
  98.2 0.6 copy-done.4
  98.8 0.3 collective-permute-start.9
  99.1 1.0 collective-permute-start.10
  100.1 0.5 collective-permute-start.11
  100.7 4.8 %collective-permute-done.10.c = bf16[40,1664]{1,0:T(8,128)(2,1)S(1)} collective-permute-done((bf16[40,1664]{1,0:T(8,128)(2,1)S(1)}, bf16[40,1664]{1,0:T(8,128)(2,1)S(1)}, u32[]{:S(2)}, u32[]{:S(2)}) %collective-permute-start.10) | collective-permute-done | bytes 133152 | tf_op jit(solution)/shard_map/ppermute | solution.py:357
  105.5 1.4 collective-permute-done.11.d
  106.9 0.7 copy-done.15
  107.6 1.9 %lat_sum.1.refs_1_ = bf16[40,1664]{1,0:T(8,128)(2,1)} custom-call(bf16[40,1664]{1,0:T(8,128)(2,1)} %copy-done.3, bf16[40,1664]{1,0:T(8,128)(2,1)} %copy-done.13, bf16[40,1664]{1,0:T(8,128)(2,1)} %copy-done.14, bf16[40,1664]{1,0:T(8,128)(2,1)} %copy-done.15), custom_call_target="tpu_custom_call" | custom-call | tf_op jit(solution)/shard_map/lat_sum/pallas_call | solution.py:461
  109.5 1.8 %collective-permute-start.12 = (bf16[40,1664]{1,0:T(8,128)(2,1)}, bf16[40,1664]{1,0:T(8,128)(2,1)S(1)}, u32[]{:S(2)}, u32[]{:S(2)}) collective-permute-start(bf16[40,1664]{1,0:T(8,128)(2,1)} %lat_sum.1.refs_1_), channel_id=1, source_target_pairs={{0,1},{1,0},{2,3},{3,2},{4,5},{5,4},{6,7},{7,6},{8,9},{9,8},{10,11... | collective-permute-start | bytes 399368 | tf_op jit(solution)/shard_map/ppermute | solution.py:357
  111.4 4.4 %collective-permute-done.12.refs_2_ = bf16[40,1664]{1,0:T(8,128)(2,1)S(1)} collective-permute-done((bf16[40,1664]{1,0:T(8,128)(2,1)}, bf16[40,1664]{1,0:T(8,128)(2,1)S(1)}, u32[]{:S(2)}, u32[]{:S(2)}) %collective-permute-start.12) | collective-permute-done | bytes 133152 | tf_op jit(solution)/shard_map/ppermute | solution.py:357
  115.7 0.7 copy-done.12
  116.4 1.7 %lon_sum.1 = (bf16[40,384]{1,0:T(8,128)(2,1)}, bf16[40,384]{1,0:T(8,128)(2,1)}, bf16[40,384]{1,0:T(8,128)(2,1)}, bf16[40,384]{1,0:T(8,128)(2,1)}, f32[8,128]{1,0:T(8,128)}) custom-call(s32[3]{0:T(128)} %copy-done.7, bf16[40,1664]{1,0:T(8,128)(2,1)} %lat_sum.1.refs_1_, bf16[40,1664]{1,0:T(8,128)(2,1)} %copy-done.12), custom_call_target="tpu_custom_call" | custom-call | tf_op jit(solution)/shard_map/lon_sum/pallas_call | solution.py:469
  118.1 0.0 collective-permute-start.13
  118.1 1.5 %collective-permute-start.14 = (bf16[40,384]{1,0:T(8,128)(2,1)}, bf16[40,384]{1,0:T(8,128)(2,1)S(1)}, u32[]{:S(2)}, u32[]{:S(2)}) collective-permute-start(bf16[40,384]{1,0:T(8,128)(2,1)} %get-tuple-element.32), channel_id=1, source_target_pairs={{0,16},{8,24},{16,0},{24,8},{1,17},{9,25},{17,1},{25,9},{2,18},{10... | collective-permute-start | bytes 92168 | tf_op jit(solution)/shard_map/ppermute | solution.py:357
  119.6 2.9 %collective-permute-start.15 = (bf16[40,384]{1,0:T(8,128)(2,1)}, bf16[40,384]{1,0:T(8,128)(2,1)S(1)}, u32[]{:S(2)}, u32[]{:S(2)}) collective-permute-start(bf16[40,384]{1,0:T(8,128)(2,1)} %get-tuple-element.33), channel_id=1, source_target_pairs={{0,24},{8,16},{16,8},{24,0},{1,25},{9,17},{17,9},{25,1},{2,26},{10... | collective-permute-start | bytes 92168 | tf_op jit(solution)/shard_map/ppermute | solution.py:357
  122.5 0.0 collective-permute-done.13.refs_1_
  122.5 0.9 collective-permute-done.14.refs_2_
  123.4 2.1 %collective-permute-done.15.refs_3_ = bf16[40,384]{1,0:T(8,128)(2,1)S(1)} collective-permute-done((bf16[40,384]{1,0:T(8,128)(2,1)}, bf16[40,384]{1,0:T(8,128)(2,1)S(1)}, u32[]{:S(2)}, u32[]{:S(2)}) %collective-permute-start.15) | collective-permute-done | bytes 30752 | tf_op jit(solution)/shard_map/ppermute | solution.py:357
  125.5 0.6 copy-done.21
  126.1 1.5 %dp_sum.1.a = f32[40,384]{1,0:T(8,128)} custom-call(bf16[40,384]{1,0:T(8,128)(2,1)} %get-tuple-element.30.refs_0_, bf16[40,384]{1,0:T(8,128)(2,1)} %copy-done.19, bf16[40,384]{1,0:T(8,128)(2,1)} %copy-done.20, bf16[40,384]{1,0:T(8,128)(2,1)} %copy-done.21), custom_call_target="tpu_custom_call" | custom-call | tf_op jit(solution)/shard_map/dp_sum/pallas_call | solution.py:478
  127.5 0.0 collective-permute-start.18
  127.5 1.2 collective-permute-start.17
  128.8 0.6 collective-permute-start.16
  129.4 1.3 copy-done
  130.7 0.9 copy-done.5
  131.6 0.7 copy-done.8
  132.2 6.3 %backward.1 = bf16[256,1536]{1,0:T(8,128)(2,1)} custom-call(s32[3]{0:T(128)S(1)} %copy-done.8, f32[256,1536]{1,0:T(8,128)} %get-tuple-element.23.normed_ref, f32[256,128]{1,0:T(8,128)S(1)} %get-tuple-element.24.inv_ref, bf16[256,160]{1,0:T(8,128)(2,1)S(1)} %copy-done.5, bf16[384,1536]{1,0:T(8,128)(2,1)S(1)} %copy-done, ...), custom_call_target="tpu_custom_call" | custom-call | tf_op jit(solution)/shard_map/backward/pallas_call | solution.py:451
  138.6 1.2 slice.19
  139.8 0.0 collective-permute-done.16.b
  139.8 0.6 copy-done.16
  140.4 0.0 copy-done.17
  140.4 0.6 copy-done.18
  141.1 1.6 %join.1 = f32[160,384]{1,0:T(8,128)} custom-call(s32[3]{0:T(128)} %copy-done.7, f32[40,384]{1,0:T(8,128)} %dp_sum.1.a, f32[40,384]{1,0:T(8,128)} %copy-done.18, f32[40,384]{1,0:T(8,128)} %copy-done.17, f32[40,384]{1,0:T(8,128)} %copy-done.16), custom_call_target="tpu_custom_call" | custom-call | tf_op jit(solution)/shard_map/join/pallas_call | solution.py:485
  (35 shorter events, 0.1 us)
Async XLA Ops:
  1.4 41.4 %copy-start.2 = (bf16[1,4,8,8,4608]{4,3,2,1,0:T(8,128)(2,1)S(1)}, bf16[1,4,8,8,4608]{4,3,2,1,0:T(8,128)(2,1)}, u32[]{:S(2)}) copy-start(bf16[1,4,8,8,4608]{4,3,2,1,0:T(8,128)(2,1)} %param.8) | copy-start | bytes 7077892
  1.4 41.4 %copy-start.6 = (bf16[1,4,8,8,160]{4,3,2,1,0:T(8,128)(2,1)S(1)}, bf16[1,4,8,8,160]{4,3,2,1,0:T(8,128)(2,1)}, u32[]{:S(2)}) copy-start(bf16[1,4,8,8,160]{4,3,2,1,0:T(8,128)(2,1)} %param.9) | copy-start | bytes 245764
  1.4 41.4 %copy-start.9 = (s32[8,8]{1,0:T(8,128)S(1)}, s32[8,8]{1,0:T(8,128)}, u32[]{:S(2)}) copy-start(s32[8,8]{1,0:T(8,128)} %valid_ref.1) | copy-start | bytes 772
  3.8 20.5 %collective-permute-start.3 = (bf16[224,1536]{1,0:T(8,128)(2,1)S(1)}, bf16[224,1536]{1,0:T(8,128)(2,1)S(1)}, u32[]{:S(2)}, u32[]{:S(2)}) collective-permute-start(bf16[224,1536]{1,0:T(8,128)(2,1)S(1)} %maximum_maximum_fusion), channel_id=1, source_target_pairs={{0,8},{8,16},{16,24},{24,0},{1,9},{9,17},{17,25},{25,1},{2,10},{10... | collective-permute-start | bytes 2064392 | tf_op jit(solution)/shard_map/ppermute | solution.py:25
  24.3 18.5 %collective-permute-start.4 = (bf16[224,1536]{1,0:T(8,128)(2,1)S(1)}, bf16[224,1536]{1,0:T(8,128)(2,1)}, u32[]{:S(2)}, u32[]{:S(2)}) collective-permute-start(bf16[224,1536]{1,0:T(8,128)(2,1)S(1)} %collective-permute-done.3.r1), channel_id=1, source_target_pairs={{0,8},{8,16},{16,24},{24,0},{1,9},{9,17},{17,25},{25,1},{2,10},{10... | collective-permute-start | bytes 2064392 | tf_op jit(solution)/shard_map/ppermute | solution.py:25
  42.8 17.8 %collective-permute-start.5 = (bf16[224,1536]{1,0:T(8,128)(2,1)}, bf16[224,1536]{1,0:T(8,128)(2,1)}, u32[]{:S(2)}, u32[]{:S(2)}) collective-permute-start(bf16[224,1536]{1,0:T(8,128)(2,1)} %collective-permute-done.4.r2), channel_id=1, source_target_pairs={{0,8},{8,16},{16,24},{24,0},{1,9},{9,17},{17,25},{25,1},{2,10},{10... | collective-permute-start | bytes 2064392 | tf_op jit(solution)/shard_map/ppermute | solution.py:25
  45.1 16.7 %collective-permute-start = (bf16[64,4864]{1,0:T(8,128)(2,1)S(1)}, bf16[64,4864]{1,0:T(8,128)(2,1)S(1)}, u32[]{:S(2)}, u32[]{:S(2)}) collective-permute-start(bf16[64,4864]{1,0:T(8,128)(2,1)S(1)} %get-tuple-element.20), channel_id=1, source_target_pairs={{0,1},{1,0},{2,3},{3,2},{4,5},{5,4},{6,7},{7,6},{8,9},{9,8},{10,11... | collective-permute-start | bytes 1867784 | tf_op jit(solution)/shard_map/ppermute | solution.py:25
  46.3 44.4 %collective-permute-start.6 = (bf16[224,1536]{1,0:T(8,128)(2,1)S(1)}, bf16[224,1536]{1,0:T(8,128)(2,1)}, u32[]{:S(2)}, u32[]{:S(2)}) collective-permute-start(bf16[224,1536]{1,0:T(8,128)(2,1)S(1)} %collective-permute-done.3.r1), channel_id=1, source_target_pairs={{0,2},{2,0},{4,6},{6,4},{1,3},{3,1},{5,7},{7,5},{8,10},{10,8},{12,... | collective-permute-start | bytes 2064392 | tf_op jit(solution)/shard_map/ppermute | solution.py:357
  46.3 44.4 %collective-permute-start.7 = (bf16[224,1536]{1,0:T(8,128)(2,1)}, bf16[224,1536]{1,0:T(8,128)(2,1)}, u32[]{:S(2)}, u32[]{:S(2)}) collective-permute-start(bf16[224,1536]{1,0:T(8,128)(2,1)} %collective-permute-done.4.r2), channel_id=1, source_target_pairs={{0,2},{2,0},{4,6},{6,4},{1,3},{3,1},{5,7},{7,5},{8,10},{10,8},{12,... | collective-permute-start | bytes 2064392 | tf_op jit(solution)/shard_map/ppermute | solution.py:357
  60.7 30.1 %collective-permute-start.8 = (bf16[224,1536]{1,0:T(8,128)(2,1)}, bf16[224,1536]{1,0:T(8,128)(2,1)}, u32[]{:S(2)}, u32[]{:S(2)}) collective-permute-start(bf16[224,1536]{1,0:T(8,128)(2,1)} %collective-permute-done.5.r3), channel_id=1, source_target_pairs={{0,2},{2,0},{4,6},{6,4},{1,3},{3,1},{5,7},{7,5},{8,10},{10,8},{12,... | collective-permute-start | bytes 2064392 | tf_op jit(solution)/shard_map/ppermute | solution.py:357
  60.7 14.8 %collective-permute-start.1 = (bf16[64,4864]{1,0:T(8,128)(2,1)}, bf16[64,4864]{1,0:T(8,128)(2,1)S(1)}, u32[]{:S(2)}, u32[]{:S(2)}) collective-permute-start(bf16[64,4864]{1,0:T(8,128)(2,1)} %get-tuple-element.21), channel_id=1, source_target_pairs={{0,6},{2,0},{4,2},{6,4},{1,7},{3,1},{5,3},{7,5},{8,14},{10,8},{12,... | collective-permute-start | bytes 1867784 | tf_op jit(solution)/shard_map/ppermute | solution.py:25
  61.8 16.5 %collective-permute-start.2 = (bf16[64,4864]{1,0:T(8,128)(2,1)}, bf16[64,4864]{1,0:T(8,128)(2,1)S(1)}, u32[]{:S(2)}, u32[]{:S(2)}) collective-permute-start(bf16[64,4864]{1,0:T(8,128)(2,1)} %get-tuple-element.22), channel_id=1, source_target_pairs={{0,7},{1,6},{2,1},{3,0},{4,3},{5,2},{6,5},{7,4},{8,15},{9,14},{10,... | collective-permute-start | bytes 1867784 | tf_op jit(solution)/shard_map/ppermute | solution.py:405
  62.8 28.0 %copy-start.7 = (s32[3]{0:T(128)}, s32[3]{0:T(128)S(1)}, u32[]{:S(2)}) copy-start(s32[3]{0:T(128)S(1)} %pad_add_fusion.place_ref.refs_0_) | copy-start | bytes 40
  78.3 12.5 %copy-start.10 = (f32[5]{0:T(128)S(1)}, f32[5]{0:T(128)}, u32[]{:S(2)}) copy-start(f32[5]{0:T(128)} %var_ref.1) | copy-start | bytes 64
  78.3 12.5 %copy-start.11 = (f32[32]{0:T(128)S(1)}, f32[32]{0:T(128)}, u32[]{:S(2)}) copy-start(f32[32]{0:T(128)} %constant.37.clone.lat_ref) | copy-start | bytes 388
  89.9 0.9 copy-start.1
  97.5 0.7 copy-start.3
  98.2 0.6 copy-start.4
  98.8 1.9 %collective-permute-start.9 = (bf16[40,1664]{1,0:T(8,128)(2,1)S(1)}, bf16[40,1664]{1,0:T(8,128)(2,1)S(1)}, u32[]{:S(2)}, u32[]{:S(2)}) collective-permute-start(bf16[40,1664]{1,0:T(8,128)(2,1)S(1)} %get-tuple-element.27), channel_id=1, source_target_pairs={{0,2},{2,0},{4,6},{6,4},{1,3},{3,1},{5,7},{7,5},{8,10},{10,8},{12,... | collective-permute-start | bytes 399368 | tf_op jit(solution)/shard_map/ppermute | solution.py:357
  99.1 6.4 %collective-permute-start.10 = (bf16[40,1664]{1,0:T(8,128)(2,1)S(1)}, bf16[40,1664]{1,0:T(8,128)(2,1)S(1)}, u32[]{:S(2)}, u32[]{:S(2)}) collective-permute-start(bf16[40,1664]{1,0:T(8,128)(2,1)S(1)} %get-tuple-element.28), channel_id=1, source_target_pairs={{0,4},{2,6},{4,0},{6,2},{1,5},{3,7},{5,1},{7,3},{8,12},{10,14},{12... | collective-permute-start | bytes 399368 | tf_op jit(solution)/shard_map/ppermute | solution.py:357
  100.1 6.8 %collective-permute-start.11 = (bf16[40,1664]{1,0:T(8,128)(2,1)S(1)}, bf16[40,1664]{1,0:T(8,128)(2,1)S(1)}, u32[]{:S(2)}, u32[]{:S(2)}) collective-permute-start(bf16[40,1664]{1,0:T(8,128)(2,1)S(1)} %get-tuple-element.29), channel_id=1, source_target_pairs={{0,6},{2,4},{4,2},{6,0},{1,7},{3,5},{5,3},{7,1},{8,14},{10,12},{12... | collective-permute-start | bytes 399368 | tf_op jit(solution)/shard_map/ppermute | solution.py:357
  100.7 6.2 %copy-start.13 = (bf16[40,1664]{1,0:T(8,128)(2,1)}, bf16[40,1664]{1,0:T(8,128)(2,1)S(1)}, u32[]{:S(2)}) copy-start(bf16[40,1664]{1,0:T(8,128)(2,1)S(1)} %collective-permute-done.9.b) | copy-start | bytes 399364
  105.5 1.4 copy-start.14
  106.9 0.7 copy-start.15
  109.5 6.2 %collective-permute-start.12 = (bf16[40,1664]{1,0:T(8,128)(2,1)}, bf16[40,1664]{1,0:T(8,128)(2,1)S(1)}, u32[]{:S(2)}, u32[]{:S(2)}) collective-permute-start(bf16[40,1664]{1,0:T(8,128)(2,1)} %lat_sum.1.refs_1_), channel_id=1, source_target_pairs={{0,1},{1,0},{2,3},{3,2},{4,5},{5,4},{6,7},{7,6},{8,9},{9,8},{10,11... | collective-permute-start | bytes 399368 | tf_op jit(solution)/shard_map/ppermute | solution.py:357
  115.7 0.7 copy-start.12
  118.1 4.4 %collective-permute-start.13 = (bf16[40,384]{1,0:T(8,128)(2,1)}, bf16[40,384]{1,0:T(8,128)(2,1)S(1)}, u32[]{:S(2)}, u32[]{:S(2)}) collective-permute-start(bf16[40,384]{1,0:T(8,128)(2,1)} %get-tuple-element.31), channel_id=1, source_target_pairs={{0,8},{8,0},{16,24},{24,16},{1,9},{9,1},{17,25},{25,17},{2,10},{10... | collective-permute-start | bytes 92168 | tf_op jit(solution)/shard_map/ppermute | solution.py:357
  118.1 5.3 %collective-permute-start.14 = (bf16[40,384]{1,0:T(8,128)(2,1)}, bf16[40,384]{1,0:T(8,128)(2,1)S(1)}, u32[]{:S(2)}, u32[]{:S(2)}) collective-permute-start(bf16[40,384]{1,0:T(8,128)(2,1)} %get-tuple-element.32), channel_id=1, source_target_pairs={{0,16},{8,24},{16,0},{24,8},{1,17},{9,25},{17,1},{25,9},{2,18},{10... | collective-permute-start | bytes 92168 | tf_op jit(solution)/shard_map/ppermute | solution.py:357
  119.6 5.9 %collective-permute-start.15 = (bf16[40,384]{1,0:T(8,128)(2,1)}, bf16[40,384]{1,0:T(8,128)(2,1)S(1)}, u32[]{:S(2)}, u32[]{:S(2)}) collective-permute-start(bf16[40,384]{1,0:T(8,128)(2,1)} %get-tuple-element.33), channel_id=1, source_target_pairs={{0,24},{8,16},{16,8},{24,0},{1,25},{9,17},{17,9},{25,1},{2,26},{10... | collective-permute-start | bytes 92168 | tf_op jit(solution)/shard_map/ppermute | solution.py:357
  122.5 3.0 %copy-start.19 = (bf16[40,384]{1,0:T(8,128)(2,1)}, bf16[40,384]{1,0:T(8,128)(2,1)S(1)}, u32[]{:S(2)}) copy-start(bf16[40,384]{1,0:T(8,128)(2,1)S(1)} %collective-permute-done.13.refs_1_) | copy-start | bytes 92164
  123.4 2.1 %copy-start.20 = (bf16[40,384]{1,0:T(8,128)(2,1)}, bf16[40,384]{1,0:T(8,128)(2,1)S(1)}, u32[]{:S(2)}) copy-start(bf16[40,384]{1,0:T(8,128)(2,1)S(1)} %collective-permute-done.14.refs_2_) | copy-start | bytes 92164
  125.5 0.6 copy-start.21
  127.5 12.2 %collective-permute-start.18 = (f32[40,384]{1,0:T(8,128)}, f32[40,384]{1,0:T(8,128)S(1)}, u32[]{:S(2)}, u32[]{:S(2)}) collective-permute-start(f32[40,384]{1,0:T(8,128)} %dp_sum.1.a), channel_id=1, source_target_pairs={{0,6},{2,4},{4,2},{6,0},{1,7},{3,5},{5,3},{7,1},{8,14},{10,12},{12... | collective-permute-start | bytes 184328 | tf_op jit(solution)/shard_map/ppermute | solution.py:357
  127.5 12.2 %collective-permute-start.17 = (f32[40,384]{1,0:T(8,128)}, f32[40,384]{1,0:T(8,128)S(1)}, u32[]{:S(2)}, u32[]{:S(2)}) collective-permute-start(f32[40,384]{1,0:T(8,128)} %dp_sum.1.a), channel_id=1, source_target_pairs={{0,4},{2,6},{4,0},{6,2},{1,5},{3,7},{5,1},{7,3},{8,12},{10,14},{12... | collective-permute-start | bytes 184328 | tf_op jit(solution)/shard_map/ppermute | solution.py:357
  128.8 11.0 %collective-permute-start.16 = (f32[40,384]{1,0:T(8,128)}, f32[40,384]{1,0:T(8,128)S(1)}, u32[]{:S(2)}, u32[]{:S(2)}) collective-permute-start(f32[40,384]{1,0:T(8,128)} %dp_sum.1.a), channel_id=1, source_target_pairs={{0,2},{2,0},{4,6},{6,4},{1,3},{3,1},{5,7},{7,5},{8,10},{10,8},{12,... | collective-permute-start | bytes 184328 | tf_op jit(solution)/shard_map/ppermute | solution.py:357
  129.4 1.3 copy-start
  130.7 0.9 copy-start.5
  131.6 0.7 copy-start.8
  139.8 0.6 copy-start.16
  139.8 0.6 copy-start.17
  140.4 0.6 copy-start.18

commit v2 on v1

--- a/solution.py
+++ b/solution.py
@@ -122,7 +122,7 @@
     return (grad_context, grad_recovery, loss_sum.reshape(1))
 
 
-def params(mib=48):
+def params(mib):
     return pltpu.CompilerParams(vmem_limit_bytes=mib << 20)
 
 
@@ -130,7 +130,39 @@
     return lax.broadcasted_iota(jnp.int32, shape, dim)
 
 
-def pack_kernel(x_ref, t_ref, valid_ref, own_ref, east_ref, south_ref, diag_ref):
+def pack_kernel(
+    place_ref, x_ref, t_ref, valid_ref, w_ref, unpatch_ref, gain_ref,
+    own0, own1, east0, east1, south0, south1, diag0, diag1, ug_ref, payload_ref, sems,
+):
+    half = place_ref[1]
+    rows, width = w_ref.shape
+    hr = rows // 2
+    start = pl.multiple_of(half * hr, 64)
+    copies = [
+        pltpu.make_async_copy(
+            w_ref.at[pl.ds(start, hr), :], payload_ref.at[pl.ds(0, hr), :], sems.at[0]
+        )
+    ]
+    copies[0].start()
+    span = t_ref.shape[-1]
+    ug_ref[...] = jnp.concatenate(
+        [
+            unpatch_ref[...],
+            jnp.broadcast_to(gain_ref[...], (16, rows)),
+            jnp.zeros((UGROWS - span - 16, rows), BF),
+        ],
+        axis=0,
+    )
+    for j in range(4):
+        at = pl.multiple_of((4 * half + j) * 32, 32)
+        copies.append(
+            pltpu.make_async_copy(
+                ug_ref.at[pl.ds(at, 32), :],
+                payload_ref.at[pl.ds(hr, 32), pl.ds(j * rows, rows)],
+                sems.at[1 + j],
+            )
+        )
+        copies[-1].start()
     count = x_ref.shape[0] * 64
     place = iota((count, count), 0)
     quad, rest = place // (count // 4), place % (count // 4)
@@ -138,26 +170,31 @@
     col = rest % 4 + jnp.where(quad % 2 == 0, 4, 0)
     source = (rest // 16) * 64 + row * 8 + col
     pick = (iota((count, count), 1) == source).astype(F32).astype(BF)
-    refs = (own_ref, east_ref, south_ref, diag_ref)
+    firsts, seconds = (own0, east0, south0, diag0), (own1, east1, south1, diag1)
     quarter = count // 4
-    width = x_ref.shape[-1]
-    step = 512
-    for at in range(0, width, step):
+    part = width // 2
+    step = part // 2
+    for at in range(0, 3 * width, step):
         tokens = x_ref[:, :, :, at : at + step].reshape(count, step)
         out = jnp.dot(pick, tokens, preferred_element_type=F32).astype(BF)
+        which, inner = at // width, at % width
+        refs = firsts if inner < part else seconds
+        to = which * part + inner % part
         for q, ref in enumerate(refs):
-            ref[:, at : at + step] = out[q * quarter : (q + 1) * quarter]
-    goal = jnp.dot(pick, t_ref[...].reshape(count, t_ref.shape[-1]), preferred_element_type=F32)
+            ref[:, to : to + step] = out[q * quarter : (q + 1) * quarter]
+    goal = jnp.dot(pick, t_ref[...].reshape(count, span), preferred_element_type=F32)
     token = iota((count, 8), 0)
     row_hot = ((token // 8) % 8 == iota((count, 8), 1)).astype(F32)
     by_row = jnp.dot(row_hot, valid_ref[...].astype(F32), preferred_element_type=F32)
-    natural = jnp.sum(jnp.where(token % 8 == iota((count, 8), 1), by_row, 0.0), axis=1, keepdims=True)
+    mine = token % 8 == iota((count, 8), 1)
+    natural = jnp.sum(jnp.where(mine, by_row, 0.0), axis=1, keepdims=True)
     spread = jnp.broadcast_to(natural, (count, 128)).astype(BF)
     column = jnp.dot(pick, spread, preferred_element_type=F32)
-    span = goal.shape[1]
     extra = jnp.concatenate([goal, column[:, : EXTRA - span]], axis=1).astype(BF)
-    for q, ref in enumerate(refs):
-        ref[:, width:] = extra[q * quarter : (q + 1) * quarter]
+    for q, ref in enumerate(seconds):
+        ref[:, 3 * part :] = extra[q * quarter : (q + 1) * quarter]
+    for c in copies:
+        c.wait()
 
 
 def attention_kernel(last_ref, *refs):
@@ -231,7 +268,7 @@
 
 
 def forward_kernel(
-    place_ref, lat_ref, var_ref, ctx_ref, e0, e1, e2, e3, own_w, own_ug, r1, r2, r3, c1, c2, c3,
+    place_ref, lat_ref, var_ref, ctx0_ref, ctx1_ref, e0, e1, e2, e3, own_w, own_ug, r1, r2, r3, c1, c2, c3,
     t0, t1, t2, t3, normed_ref, inv_ref, dfc_ref, hidden_ref, w_all, ug_all, term, sems,
 ):
     zi, half, lat_place = place_ref[0], place_ref[1], place_ref[2]
@@ -240,7 +277,7 @@
     )
     for c in w_copies + u_copies:
         c.start()
-    tokens, width = ctx_ref.shape
+    tokens, width = normed_ref.shape
     span = dfc_ref.shape[1]
     extras = [e0, e1, e2, e3]
     extra = jnp.concatenate(
@@ -259,7 +296,9 @@
     weight = lat_w * valid * var_w
     for c in w_copies:
         c.wait()
-    mixed = jnp.dot(ctx_ref[...], w_all[...], preferred_element_type=F32)
+    part = width // 2
+    mixed = jnp.dot(ctx0_ref[...], w_all[0:part, :], preferred_element_type=F32)
+    mixed += jnp.dot(ctx1_ref[...], w_all[part:, :], preferred_element_type=F32)
     centre = jnp.mean(mixed, axis=-1, keepdims=True)
     off = mixed - centre
     inv = lax.rsqrt(jnp.mean(off * off, axis=-1, keepdims=True) + 1e-05)
@@ -376,58 +415,69 @@
     cosine = np.cos(angle)
     lat_table = jnp.asarray(np.roll(cosine / cosine.mean(), -4), F32)
 
-    ug = jnp.concatenate(
-        [unpatch_matrix.T, norm_gain[None], jnp.zeros((UGROWS - span - 1, rows), BF)], axis=0
-    )
-    ug_half = lax.dynamic_slice_in_dim(ug, half * (UGROWS // 2), UGROWS // 2, 0)
-    ug_half = jnp.concatenate([ug_half[32 * j : 32 * j + 32] for j in range(4)], axis=1)
-    payload = jnp.concatenate(
-        [lax.dynamic_slice_in_dim(w_out, half * (rows // 2), rows // 2, 0), ug_half], axis=0
-    )
-    rings, swaps = [], []
-    moving = payload
-    for _ in range(dp - 1):
-        moving = from_behind(moving, "dp", 1)
-        rings.append(moving)
-        swaps.append(swap(moving, "lat", 1))
-
-    quads = pl.pallas_call(
+    part = width // 2
+    quarter = tokens // 4
+    widths = (3 * part, 3 * part + EXTRA)
+    *packed, ug, payload = pl.pallas_call(
         pack_kernel,
-        out_shape=[shape((tokens // 4, 3 * width + EXTRA), BF)] * 4,
-        in_specs=[VMEM] * 3,
-        out_specs=[VMEM] * 4,
-        compiler_params=params(),
+        out_shape=[shape((quarter, w), BF) for _ in range(4) for w in widths]
+        + [shape((UGROWS, rows), BF), shape((rows // 2 + 32, width), BF)],
+        in_specs=[SMEM] + [VMEM] * 3 + [ANY] + [VMEM] * 2,
+        out_specs=[VMEM] * 9 + [ANY],
+        scratch_shapes=[pltpu.SemaphoreType.DMA((5,))],
+        compiler_params=params(20),
         name="pack",
-    )(projected.reshape(levels, 8, 8, 3 * width), targets.reshape(levels, 8, 8, span), valid_cells)
-    own = quads[0]
-    east = from_behind(quads[1], "lon", -1)
-    south = from_behind(quads[2], "lat", -1)
-    diag = lax.ppermute(
-        quads[3],
-        ("lat", "lon"),
-        [
-            (a * lon + b, ((a - 1) % lat) * lon + (b - 1) % lon)
-            for a in range(lat)
-            for b in range(lon)
-        ],
-    )
-    tiles = (own, east, south, diag)
-    groups = width // 128
-    qkv_specs = [
-        pl.BlockSpec((tokens // 4, 128), lambda g, i=i: (0, i * groups + g)) for i in range(3)
+    )(
+        place,
+        projected.reshape(levels, 8, 8, 3 * width),
+        targets.reshape(levels, 8, 8, span),
+        valid_cells,
+        w_out,
+        unpatch_matrix.T,
+        norm_gain.reshape(1, rows),
+    )
+    corner = [
+        (a * lon + b, ((a - 1) % lat) * lon + (b - 1) % lon) for a in range(lat) for b in range(lon)
     ]
-    ctx = pl.pallas_call(
-        attention_kernel,
-        grid=(groups,),
-        out_shape=shape((tokens, width), BF),
-        in_specs=[SMEM] + qkv_specs * 4,
-        out_specs=pl.BlockSpec((tokens, 128), lambda g: (0, g)),
-        compiler_params=params(),
-        name="attention",
-    )(last, *[t for t in tiles for _ in range(3)])
+    tiles = []
+    for g in range(2):
+        own, east, south, diag = packed[g::2]
+        tiles.append(
+            (
+                own,
+                from_behind(east, "lon", -1),
+                from_behind(south, "lat", -1),
+                lax.ppermute(diag, ("lat", "lon"), corner),
+            )
+        )
+    groups = part // 128
+
+    def attend(chunk):
+        specs = [
+            pl.BlockSpec((quarter, 128), lambda g, i=i: (0, i * groups + g)) for i in range(3)
+        ]
+        return pl.pallas_call(
+            attention_kernel,
+            grid=(groups,),
+            out_shape=shape((tokens, part), BF),
+            in_specs=[SMEM] + specs * 4,
+            out_specs=pl.BlockSpec((tokens, 128), lambda g: (0, g)),
+            compiler_params=params(8),
+            name="attention",
+        )(last, *[t for t in chunk for _ in range(3)])
+
+    ring1 = from_behind(payload, "dp", 1)
+    ring1_after, *first = lax.optimization_barrier((ring1, *tiles[0][1:]))
+    ring2 = from_behind(ring1_after, "dp", 1)
+    ctx0 = attend((tiles[0][0], *first))
+    ctx1 = attend(tiles[1])
+    ring2_after, ctx0, ctx1 = lax.optimization_barrier((ring2, ctx0, ctx1))
+    ring3 = from_behind(ring2_after, "dp", 1)
+    rings = [ring1, ring2, ring3]
+    swaps = [swap(r, "lat", 1) for r in rings]
 
     piece = span // lat
-    extra_spec = pl.BlockSpec((tokens // 4, EXTRA), lambda i: (0, 3 * width // EXTRA))
+    extra_spec = pl.BlockSpec((tokens // 4, EXTRA), lambda i: (0, 3 * part // EXTRA))
     copies = 2 + 2 * (dp - 1) * 5
     assembly = [
         pltpu.VMEM((dp * rows, width), BF),
@@ -438,14 +488,14 @@
         grid=(1,),
         out_shape=[shape((piece, width + 128), BF)] * 4
         + [shape((tokens, width), F32), shape((tokens, 128), F32), shape((tokens, span), BF)],
-        in_specs=[SMEM] * 3 + [VMEM] + [extra_spec] * 4 + [ANY] * 8,
+        in_specs=[SMEM] * 3 + [VMEM] * 2 + [extra_spec] * 4 + [ANY] * 8,
         out_specs=[VMEM] * 7,
         scratch_shapes=[pltpu.VMEM((tokens, width), BF)]
         + assembly
         + [pltpu.VMEM((span, width), F32), pltpu.SemaphoreType.DMA((copies,))],
-        compiler_params=params(),
+        compiler_params=params(28),
         name="forward",
-    )(place, lat_table, var_weight, ctx, *tiles, w_out, ug, *rings, *swaps)
+    )(place, lat_table, var_weight, ctx0, ctx1, *tiles[1], w_out, ug, *rings, *swaps)
 
     terms = [t0] + [swap(t, "lat", b) for b, t in ((1, t1), (2, t2), (3, t3))]
     grad_context = pl.pallas_call(
@@ -454,15 +504,17 @@
         in_specs=[SMEM] + [VMEM] * 3 + [ANY] * 8,
         out_specs=VMEM,
         scratch_shapes=assembly + [pltpu.SemaphoreType.DMA((copies,))],
-        compiler_params=params(),
+        compiler_params=params(24),
         name="backward",
     )(place, normed, inv, dfc, w_out, ug, *rings, *swaps)
 
+    *terms, grad_context = lax.optimization_barrier((*terms, grad_context))
     lat_sum = pl.pallas_call(
         lat_sum_kernel,
         out_shape=shape((piece, width + 128), BF),
         in_specs=[VMEM] * 4,
         out_specs=VMEM,
+        compiler_params=params(4),
         name="lat_sum",
     )(*terms)
     denominator = levels * lat_total * 8 * lon
@@ -472,6 +524,7 @@
         in_specs=[SMEM] + [VMEM] * 2,
         out_specs=[VMEM] * 5,
         scratch_shapes=[pltpu.VMEM((piece, width + 128), F32)],
+        compiler_params=params(4),
         name="lon_sum",
     )(place, lat_sum, swap(lat_sum, "lon", 1))
     parts = [parts[0]] + [swap(parts[k], "dp", k) for k in (1, 2, 3)]
@@ -480,6 +533,7 @@
         out_shape=shape((piece, rows), F32),
         in_specs=[VMEM] * 4,
         out_specs=VMEM,
+        compiler_params=params(4),
         name="dp_sum",
     )(*parts)
     joined = pl.pallas_call(
@@ -487,6 +541,7 @@
         out_shape=shape((span, rows), F32),
         in_specs=[SMEM] + [VMEM] * 4,
         out_specs=VMEM,
+        compiler_params=params(4),
         name="join",
     )(place, mine, *[swap(mine, "lat", b) for b in (1, 2, 3)])
     return (

time: 143 us -> 114 us (0.80)
  waiting for transfers between devices: 78.9 us -> 56.1 us
  Pallas kernels: 33.6 us -> 27.4 us
  starting transfers between devices: 16.9 us -> 21.6 us
  local copies, waits for them, and re-layouts: 11.5 us -> 8.09 us
    ppermute x5 -> x7, waiting for transfers between devices: 62.4 us -> 35 us  [from_behind(): lax.ppermute(array, axis, [(i, (i + by) % length) for i in range(length)])]
    ppermute x1 -> x2, waiting for transfers between devices: 2.84 us -> 8.49 us  [shards(): lax.ppermute(diag, ('lat', 'lon'), corner)]
    ppermute x5 -> x7, starting transfers between devices: 5.46 us -> 8.48 us  [from_behind(): lax.ppermute(array, axis, [(i, (i + by) % length) for i in range(length)])]
    ppermute x1 -> x2, starting transfers between devices: 0.93 us -> 2.81 us  [shards(): lax.ppermute(diag, ('lat', 'lon'), corner)]
    pallas_call x1, Pallas kernels: 1.95 us -> 0.18 us  [shards(): pl.pallas_call(lat_sum_kernel, out_shape=shape((piece, width + 128), BF),...]
    pallas_call x1, Pallas kernels: 6.72 us -> 5.14 us  [shards(): pl.pallas_call(forward_kernel, grid=(1,), out_shape=[shape((piece, width...]
    pallas_call x1, Pallas kernels: 1.45 us -> 0.02 us  [shards(): pl.pallas_call(lambda *refs: dp_sum_kernel(float(denominator), *refs), ou...]
    unnamed x44 -> x24, local copies, waits for them, and re-layouts: 8.22 us -> 6.9 us
  transfers between devices with their start and end apart: 19 -> 22, of which waited for: 10 -> 13; matrix products, arithmetic and copies ran while one was open for 1% -> 0% of each run, Pallas kernels for 14% -> 15%
where the time goes in v2:
time: 114 us
  waiting for transfers between devices  56.1 us (49%)
  Pallas kernels  27.4 us (24%)
  starting transfers between devices  21.6 us (19%)
  local copies, waits for them, and re-layouts  8.09 us (7%)
    ppermute x7, waiting for transfers between devices, from_behind(): lax.ppermute(array, axis, [(i, (i + by) % length) for i in range(length)])  35 us
    ppermute x13, waiting for transfers between devices, swap(): lax.ppermute(array, axis, [(i, i ^ bit) for i in range(lax.axis_size(axis...  12.5 us
    pallas_call x2, Pallas kernels, attend(): pl.pallas_call(attention_kernel, grid=(groups,), out_shape=shape((tokens,...  11.6 us
    ppermute x13, starting transfers between devices, swap(): lax.ppermute(array, axis, [(i, i ^ bit) for i in range(lax.axis_size(axis...  10.3 us
    ppermute x2, waiting for transfers between devices, shards(): lax.ppermute(diag, ('lat', 'lon'), corner)  8.49 us
    ppermute x7, starting transfers between devices, from_behind(): lax.ppermute(array, axis, [(i, (i + by) % length) for i in range(length)])  8.48 us
    unnamed x24, local copies, waits for them, and re-layouts  6.9 us
    pallas_call x1, Pallas kernels, shards(): pl.pallas_call(backward_kernel, out_shape=shape((tokens, width), BF), in_...  5.49 us
  transfers between devices with their start and end apart: 22, of which 13 were waited for; matrix products, arithmetic and copies ran while one was open for 0% of the time, Pallas kernels for 15%

profile of v2, /device:TPU:0, one launch (start us, length us, event | category | flops | bytes accessed | tf_op | source)
XLA Modules:
  0.0 114.1 jit_solution(9620715433296869996)
XLA Ops:
  0.6 0.7 reshape.25.gain_ref
  1.3 0.1 pad_add_fusion.place_ref.refs_0_
  1.4 1.3 %copy-done = bf16[384,1536]{1,0:T(8,128)(2,1)S(1)} copy-done((bf16[384,1536]{1,0:T(8,128)(2,1)S(1)}, bf16[384,1536]{1,0:T(8,128)(2,1)}, u32[]{:S(2)}) %copy-start) | copy-done | bytes 1179672
  2.7 1.7 %copy-done.6 = bf16[1,4,8,8,4608]{4,3,2,1,0:T(8,128)(2,1)S(1)} copy-done((bf16[1,4,8,8,4608]{4,3,2,1,0:T(8,128)(2,1)S(1)}, bf16[1,4,8,8,4608]{4,3,2,1,0:T(8,128)(2,1)}, u32[]{:S(2)}) %copy-start.6) | copy-done | bytes 2359320
  4.3 0.9 copy-done.7
  5.2 0.9 copy-done.8
  6.1 0.7 copy-done.9
  6.8 3.1 %pack.1 = (bf16[64,2304]{1,0:T(8,128)(2,1)S(1)}, bf16[64,2560]{1,0:T(8,128)(2,1)S(1)}, bf16[64,2304]{1,0:T(8,128)(2,1)S(1)}, bf16[64,2560]{1,0:T(8,128)(2,1)}, b...) custom-call(s32[3]{0:T(128)S(1)} %pad_add_fusion.place_ref.refs_0_, ...), custom_call_target="tpu_custom_call" | custom-call | tf_op jit(solution)/shard_map/pack/pallas_call | solution.py:421
  9.9 3.1 %collective-permute-start = (bf16[224,1536]{1,0:T(8,128)(2,1)S(1)}, bf16[224,1536]{1,0:T(8,128)(2,1)S(1)}, u32[]{:S(2)}, u32[]{:S(2)}) collective-permute-start(bf16[224,1536]{1,0:T(8,128)(2,1)S(1)} %get-tuple-element.37), channel_id=1, source_target_pairs={{0,8},{8,16},{16,24},{24,0},{1,9},{9,17},{17,25},{25,1},{2,10},{10... | collective-permute-start | bytes 2064392 | tf_op jit(solution)/shard_map/ppermute | solution.py:25
  13.0 1.5 %collective-permute-start.1 = (bf16[64,2304]{1,0:T(8,128)(2,1)S(1)}, bf16[64,2304]{1,0:T(8,128)(2,1)S(1)}, u32[]{:S(2)}, u32[]{:S(2)}) collective-permute-start(bf16[64,2304]{1,0:T(8,128)(2,1)S(1)} %get-tuple-element.38), channel_id=1, source_target_pairs={{0,1},{1,0},{2,3},{3,2},{4,5},{5,4},{6,7},{7,6},{8,9},{9,8},{10,11... | collective-permute-start | bytes 884744 | tf_op jit(solution)/shard_map/ppermute | solution.py:25
  14.5 0.4 collective-permute-start.2
  14.9 1.2 %collective-permute-start.3 = (bf16[64,2304]{1,0:T(8,128)(2,1)S(1)}, bf16[64,2304]{1,0:T(8,128)(2,1)S(1)}, u32[]{:S(2)}, u32[]{:S(2)}) collective-permute-start(bf16[64,2304]{1,0:T(8,128)(2,1)S(1)} %get-tuple-element.40), channel_id=1, source_target_pairs={{0,7},{1,6},{2,1},{3,0},{4,3},{5,2},{6,5},{7,4},{8,15},{9,14},{10,... | collective-permute-start | bytes 884744 | tf_op jit(solution)/shard_map/ppermute | solution.py:450
  16.1 6.8 %collective-permute-done.1.refs_3_.refs_4_.refs_5_ = bf16[64,2304]{1,0:T(8,128)(2,1)S(1)} collective-permute-done((bf16[64,2304]{1,0:T(8,128)(2,1)S(1)}, bf16[64,2304]{1,0:T(8,128)(2,1)S(1)}, u32[]{:S(2)}, u32[]{:S(2)}) %collective-permute-start.1) | collective-permute-done | bytes 294944 | tf_op jit(solution)/shard_map/ppermute | solution.py:25
  22.9 0.0 collective-permute-done.2.refs_6_.refs_7_.refs_8_
  22.9 0.7 copy-done.2
  23.6 3.1 %collective-permute-done.3.refs_9_.refs_10_.refs_11_ = bf16[64,2304]{1,0:T(8,128)(2,1)S(1)} collective-permute-done((bf16[64,2304]{1,0:T(8,128)(2,1)S(1)}, bf16[64,2304]{1,0:T(8,128)(2,1)S(1)}, u32[]{:S(2)}, u32[]{:S(2)}) %collective-permute-start.3) | collective-permute-done | bytes 294944 | tf_op jit(solution)/shard_map/ppermute | solution.py:450
  26.8 0.7 copy-done.4
  27.5 2.9 %collective-permute-done.r1 = bf16[224,1536]{1,0:T(8,128)(2,1)S(1)} collective-permute-done((bf16[224,1536]{1,0:T(8,128)(2,1)S(1)}, bf16[224,1536]{1,0:T(8,128)(2,1)S(1)}, u32[]{:S(2)}, u32[]{:S(2)}) %collective-permute-start) | collective-permute-done | bytes 688160 | tf_op jit(solution)/shard_map/ppermute | solution.py:25
  30.4 0.0 collective-permute-start.4
  30.4 1.5 %collective-permute-start.5 = (bf16[64,2560]{1,0:T(8,128)(2,1)}, bf16[64,2560]{1,0:T(8,128)(2,1)S(1)}, u32[]{:S(2)}, u32[]{:S(2)}) collective-permute-start(bf16[64,2560]{1,0:T(8,128)(2,1)} %get-tuple-element.47), channel_id=1, source_target_pairs={{0,1},{1,0},{2,3},{3,2},{4,5},{5,4},{6,7},{7,6},{8,9},{9,8},{10,11... | collective-permute-start | bytes 983048 | tf_op jit(solution)/shard_map/ppermute | solution.py:25
  31.9 0.0 collective-permute-start.6
  31.9 1.6 %collective-permute-start.7 = (bf16[64,2560]{1,0:T(8,128)(2,1)}, bf16[64,2560]{1,0:T(8,128)(2,1)S(1)}, u32[]{:S(2)}, u32[]{:S(2)}) collective-permute-start(bf16[64,2560]{1,0:T(8,128)(2,1)} %get-tuple-element.49), channel_id=1, source_target_pairs={{0,7},{1,6},{2,1},{3,0},{4,3},{5,2},{6,5},{7,4},{8,15},{9,14},{10,... | collective-permute-start | bytes 983048 | tf_op jit(solution)/shard_map/ppermute | solution.py:450
  33.5 7.7 %collective-permute-done.5.refs_3_.refs_4_.refs_5_.e1 = bf16[64,2560]{1,0:T(8,128)(2,1)S(1)} collective-permute-done((bf16[64,2560]{1,0:T(8,128)(2,1)}, bf16[64,2560]{1,0:T(8,128)(2,1)S(1)}, u32[]{:S(2)}, u32[]{:S(2)}) %collective-permute-start.5) | collective-permute-done | bytes 327712 | tf_op jit(solution)/shard_map/ppermute | solution.py:25
  41.2 0.0 collective-permute-done.6.refs_6_.refs_7_.refs_8_.e2
  41.2 5.4 %collective-permute-done.7.refs_9_.refs_10_.refs_11_.e3 = bf16[64,2560]{1,0:T(8,128)(2,1)S(1)} collective-permute-done((bf16[64,2560]{1,0:T(8,128)(2,1)}, bf16[64,2560]{1,0:T(8,128)(2,1)S(1)}, u32[]{:S(2)}, u32[]{:S(2)}) %collective-permute-start.7) | collective-permute-done | bytes 327712 | tf_op jit(solution)/shard_map/ppermute | solution.py:450
  46.6 5.8 %attention.3.ctx1_ref = bf16[256,768]{1,0:T(8,128)(2,1)S(1)} custom-call(s32[1]{0:T(128)} %bitcast.6.last_ref, bf16[64,2560]{1,0:T(8,128)(2,1)S(1)} %get-tuple-element.46.refs_0_.refs_1_.refs_2_.e0, bf16[64,2560]{1,0:T(8,128)(2,1)S(1)} %get-tuple-element.46.refs_0_.refs_1_.refs_2_.e0, bf16[64,2560]{1,0:T(8,128)(2,1)S(1)} %get-tuple-element.46.refs_0_.refs_1_.refs_2_.e0, ...), custom_call_target="tpu_custom_call" | custom-call | tf_op jit(solution)/shard_map/attention/pallas_call | solution.py:459
  52.4 0.0 copy-start.1
  52.4 0.0 copy-start.10
  52.4 0.0 copy-start.11
  52.4 5.8 %attention.2.ctx0_ref = bf16[256,768]{1,0:T(8,128)(2,1)S(1)} custom-call(s32[1]{0:T(128)} %bitcast.6.last_ref, bf16[64,2304]{1,0:T(8,128)(2,1)S(1)} %get-tuple-element.42.refs_0_.refs_1_.refs_2_, bf16[64,2304]{1,0:T(8,128)(2,1)S(1)} %get-tuple-element.42.refs_0_.refs_1_.refs_2_, bf16[64,2304]{1,0:T(8,128)(2,1)S(1)} %get-tuple-element.42.refs_0_.refs_1_.refs_2_, ...), custom_call_target="tpu_custom_call" | custom-call | tf_op jit(solution)/shard_map/attention/pallas_call | solution.py:459
  58.3 0.0 collective-permute-done.4.r2
  58.3 2.0 %collective-permute-start.8 = (bf16[224,1536]{1,0:T(8,128)(2,1)S(1)}, bf16[224,1536]{1,0:T(8,128)(2,1)S(1)}, u32[]{:S(2)}, u32[]{:S(2)}) collective-permute-start(bf16[224,1536]{1,0:T(8,128)(2,1)S(1)} %collective-permute-done.4.r2), channel_id=1, source_target_pairs={{0,8},{8,16},{16,24},{24,0},{1,9},{9,17},{17,25},{25,1},{2,10},{10... | collective-permute-start | bytes 2064392 | tf_op jit(solution)/shard_map/ppermute | solution.py:25
  60.3 0.0 collective-permute-start.9
  60.3 0.5 collective-permute-start.10
  60.8 17.6 %collective-permute-done.8.r3 = bf16[224,1536]{1,0:T(8,128)(2,1)S(1)} collective-permute-done((bf16[224,1536]{1,0:T(8,128)(2,1)S(1)}, bf16[224,1536]{1,0:T(8,128)(2,1)S(1)}, u32[]{:S(2)}, u32[]{:S(2)}) %collective-permute-start.8) | collective-permute-done | bytes 688160 | tf_op jit(solution)/shard_map/ppermute | solution.py:25
  78.4 0.0 collective-permute-start.11
  78.4 0.0 collective-permute-done.9.c1
  78.4 0.0 collective-permute-done.10.c2
  78.4 2.1 %collective-permute-done.11.c3 = bf16[224,1536]{1,0:T(8,128)(2,1)S(1)} collective-permute-done((bf16[224,1536]{1,0:T(8,128)(2,1)S(1)}, bf16[224,1536]{1,0:T(8,128)(2,1)S(1)}, u32[]{:S(2)}, u32[]{:S(2)}) %collective-permute-start.11) | collective-permute-done | bytes 688160 | tf_op jit(solution)/shard_map/ppermute | solution.py:396
  80.5 5.1 %forward.1 = (bf16[40,1664]{1,0:T(8,128)(2,1)S(1)}, bf16[40,1664]{1,0:T(8,128)(2,1)S(1)}, bf16[40,1664]{1,0:T(8,128)(2,1)S(1)}, bf16[40,1664]{1,0:T(8,128)(2,1)S...) custom-call(s32[3]{0:T(128)S(1)} %pad_add_fusion.place_ref.refs_0_, ...), custom_call_target="tpu_custom_call" | custom-call | tf_op jit(solution)/shard_map/forward/pallas_call | solution.py:486
  85.7 0.2 collective-permute-start.12
  85.8 0.2 collective-permute-start.13
  86.1 1.5 %collective-permute-start.14 = (bf16[40,1664]{1,0:T(8,128)(2,1)S(1)}, bf16[40,1664]{1,0:T(8,128)(2,1)S(1)}, u32[]{:S(2)}, u32[]{:S(2)}) collective-permute-start(bf16[40,1664]{1,0:T(8,128)(2,1)S(1)} %get-tuple-element.57), channel_id=1, source_target_pairs={{0,6},{2,4},{4,2},{6,0},{1,7},{3,5},{5,3},{7,1},{8,14},{10,12},{12... | collective-permute-start | bytes 399368 | tf_op jit(solution)/shard_map/ppermute | solution.py:396
  87.6 5.5 %backward.1 = bf16[256,1536]{1,0:T(8,128)(2,1)} custom-call(s32[3]{0:T(128)S(1)} %pad_add_fusion.place_ref.refs_0_, f32[256,1536]{1,0:T(8,128)S(1)} %get-tuple-element.58.normed_ref, f32[256,128]{1,0:T(8,128)S(1)} %get-tuple-element.59.inv_ref, bf16[256,160]{1,0:T(8,128)(2,1)S(1)} %get-tuple-element.60.dfc_ref, bf16[384,1536]{1,0:T(8,128)(2,1)S(1)} %copy-done.1, ...), custom_call_target="tpu_custom_call" | custom-call | tf_op jit(solution)/shard_map/backward/pallas_call | solution.py:501
  93.1 0.0 collective-permute-done.12.b
  93.1 0.8 collective-permute-done.14.d
  94.0 0.2 lat_sum.1.refs_1_
  94.1 1.5 %collective-permute-start.15 = (bf16[40,1664]{1,0:T(8,128)(2,1)S(1)}, bf16[40,1664]{1,0:T(8,128)(2,1)S(1)}, u32[]{:S(2)}, u32[]{:S(2)}) collective-permute-start(bf16[40,1664]{1,0:T(8,128)(2,1)S(1)} %lat_sum.1.refs_1_), channel_id=1, source_target_pairs={{0,1},{1,0},{2,3},{3,2},{4,5},{5,4},{6,7},{7,6},{8,9},{9,8},{10,11... | collective-permute-start | bytes 399368 | tf_op jit(solution)/shard_map/ppermute | solution.py:396
  95.6 4.4 %collective-permute-done.15.refs_2_ = bf16[40,1664]{1,0:T(8,128)(2,1)S(1)} collective-permute-done((bf16[40,1664]{1,0:T(8,128)(2,1)S(1)}, bf16[40,1664]{1,0:T(8,128)(2,1)S(1)}, u32[]{:S(2)}, u32[]{:S(2)}) %collective-permute-start.15) | collective-permute-done | bytes 133152 | tf_op jit(solution)/shard_map/ppermute | solution.py:396
  100.0 0.7 lon_sum.1
  100.7 0.0 collective-permute-start.16
  100.7 0.9 collective-permute-start.17
  101.6 3.5 %collective-permute-start.18 = (bf16[40,384]{1,0:T(8,128)(2,1)S(1)}, bf16[40,384]{1,0:T(8,128)(2,1)S(1)}, u32[]{:S(2)}, u32[]{:S(2)}) collective-permute-start(bf16[40,384]{1,0:T(8,128)(2,1)S(1)} %get-tuple-element.69), channel_id=1, source_target_pairs={{0,24},{8,16},{16,8},{24,0},{1,25},{9,17},{17,9},{25,1},{2,26},{10... | collective-permute-start | bytes 92168 | tf_op jit(solution)/shard_map/ppermute | solution.py:396
  105.1 0.0 collective-permute-done.16.refs_1_
  105.1 0.9 collective-permute-done.17.refs_2_
  106.0 1.3 %collective-permute-done.18.refs_3_ = bf16[40,384]{1,0:T(8,128)(2,1)S(1)} collective-permute-done((bf16[40,384]{1,0:T(8,128)(2,1)S(1)}, bf16[40,384]{1,0:T(8,128)(2,1)S(1)}, u32[]{:S(2)}, u32[]{:S(2)}) %collective-permute-start.18) | collective-permute-done | bytes 30752 | tf_op jit(solution)/shard_map/ppermute | solution.py:396
  107.3 0.1 collective-permute-start.21
  107.4 1.8 %collective-permute-start.20 = (f32[40,384]{1,0:T(8,128)S(1)}, f32[40,384]{1,0:T(8,128)S(1)}, u32[]{:S(2)}, u32[]{:S(2)}) collective-permute-start(f32[40,384]{1,0:T(8,128)S(1)} %dp_sum.1.a), channel_id=1, source_target_pairs={{0,4},{2,6},{4,0},{6,2},{1,5},{3,7},{5,1},{7,3},{8,12},{10,14},{12... | collective-permute-start | bytes 184328 | tf_op jit(solution)/shard_map/ppermute | solution.py:396
  109.2 0.1 collective-permute-start.19
  109.3 0.5 slice.3
  109.8 1.6 %collective-permute-done.21.d = f32[40,384]{1,0:T(8,128)S(1)} collective-permute-done((f32[40,384]{1,0:T(8,128)S(1)}, f32[40,384]{1,0:T(8,128)S(1)}, u32[]{:S(2)}, u32[]{:S(2)}) %collective-permute-start.21) | collective-permute-done | bytes 61472 | tf_op jit(solution)/shard_map/ppermute | solution.py:396
  111.4 1.4 %collective-permute-done.20.c = f32[40,384]{1,0:T(8,128)S(1)} collective-permute-done((f32[40,384]{1,0:T(8,128)S(1)}, f32[40,384]{1,0:T(8,128)S(1)}, u32[]{:S(2)}, u32[]{:S(2)}) %collective-permute-start.20) | collective-permute-done | bytes 61472 | tf_op jit(solution)/shard_map/ppermute | solution.py:396
  112.8 0.0 collective-permute-done.19.b
  112.8 1.3 %join.1 = f32[160,384]{1,0:T(8,128)} custom-call(s32[3]{0:T(128)S(1)} %pad_add_fusion.place_ref.refs_0_, f32[40,384]{1,0:T(8,128)S(1)} %dp_sum.1.a, f32[40,384]{1,0:T(8,128)S(1)} %collective-permute-done.19.b, f32[40,384]{1,0:T(8,128)S(1)} %collective-permute-done.20.c, f32[40,384]{1,0:T(8,128)S(1)} %collective-permute-done.21.d), custom_call_target="tpu_custom_call" | custom-call | tf_op jit(solution)/shard_map/join/pallas_call | solution.py:539
  (16 shorter events, 0.0 us)
Async XLA Ops:
  1.4 1.3 %copy-start = (bf16[384,1536]{1,0:T(8,128)(2,1)S(1)}, bf16[384,1536]{1,0:T(8,128)(2,1)}, u32[]{:S(2)}) copy-start(bf16[384,1536]{1,0:T(8,128)(2,1)} %own_w.3) | copy-start | bytes 3538948
  2.7 1.7 %copy-start.6 = (bf16[1,4,8,8,4608]{4,3,2,1,0:T(8,128)(2,1)S(1)}, bf16[1,4,8,8,4608]{4,3,2,1,0:T(8,128)(2,1)}, u32[]{:S(2)}) copy-start(bf16[1,4,8,8,4608]{4,3,2,1,0:T(8,128)(2,1)} %param.8) | copy-start | bytes 7077892
  4.3 0.9 copy-start.7
  5.2 0.9 copy-start.8
  6.1 0.7 copy-start.9
  9.9 20.5 %collective-permute-start = (bf16[224,1536]{1,0:T(8,128)(2,1)S(1)}, bf16[224,1536]{1,0:T(8,128)(2,1)S(1)}, u32[]{:S(2)}, u32[]{:S(2)}) collective-permute-start(bf16[224,1536]{1,0:T(8,128)(2,1)S(1)} %get-tuple-element.37), channel_id=1, source_target_pairs={{0,8},{8,16},{16,24},{24,0},{1,9},{9,17},{17,25},{25,1},{2,10},{10... | collective-permute-start | bytes 2064392 | tf_op jit(solution)/shard_map/ppermute | solution.py:25
  13.0 9.9 %collective-permute-start.1 = (bf16[64,2304]{1,0:T(8,128)(2,1)S(1)}, bf16[64,2304]{1,0:T(8,128)(2,1)S(1)}, u32[]{:S(2)}, u32[]{:S(2)}) collective-permute-start(bf16[64,2304]{1,0:T(8,128)(2,1)S(1)} %get-tuple-element.38), channel_id=1, source_target_pairs={{0,1},{1,0},{2,3},{3,2},{4,5},{5,4},{6,7},{7,6},{8,9},{9,8},{10,11... | collective-permute-start | bytes 884744 | tf_op jit(solution)/shard_map/ppermute | solution.py:25
  14.5 8.4 %collective-permute-start.2 = (bf16[64,2304]{1,0:T(8,128)(2,1)S(1)}, bf16[64,2304]{1,0:T(8,128)(2,1)S(1)}, u32[]{:S(2)}, u32[]{:S(2)}) collective-permute-start(bf16[64,2304]{1,0:T(8,128)(2,1)S(1)} %get-tuple-element.39), channel_id=1, source_target_pairs={{0,6},{2,0},{4,2},{6,4},{1,7},{3,1},{5,3},{7,5},{8,14},{10,8},{12,... | collective-permute-start | bytes 884744 | tf_op jit(solution)/shard_map/ppermute | solution.py:25
  14.9 11.9 %collective-permute-start.3 = (bf16[64,2304]{1,0:T(8,128)(2,1)S(1)}, bf16[64,2304]{1,0:T(8,128)(2,1)S(1)}, u32[]{:S(2)}, u32[]{:S(2)}) collective-permute-start(bf16[64,2304]{1,0:T(8,128)(2,1)S(1)} %get-tuple-element.40), channel_id=1, source_target_pairs={{0,7},{1,6},{2,1},{3,0},{4,3},{5,2},{6,5},{7,4},{8,15},{9,14},{10,... | collective-permute-start | bytes 884744 | tf_op jit(solution)/shard_map/ppermute | solution.py:450
  22.9 0.7 copy-start.2
  26.8 0.7 copy-start.4
  30.4 27.8 %collective-permute-start.4 = (bf16[224,1536]{1,0:T(8,128)(2,1)S(1)}, bf16[224,1536]{1,0:T(8,128)(2,1)S(1)}, u32[]{:S(2)}, u32[]{:S(2)}) collective-permute-start(bf16[224,1536]{1,0:T(8,128)(2,1)S(1)} %collective-permute-done.r1), channel_id=1, source_target_pairs={{0,8},{8,16},{16,24},{24,0},{1,9},{9,17},{17,25},{25,1},{2,10},{10... | collective-permute-start | bytes 2064392 | tf_op jit(solution)/shard_map/ppermute | solution.py:25
  30.4 10.8 %collective-permute-start.5 = (bf16[64,2560]{1,0:T(8,128)(2,1)}, bf16[64,2560]{1,0:T(8,128)(2,1)S(1)}, u32[]{:S(2)}, u32[]{:S(2)}) collective-permute-start(bf16[64,2560]{1,0:T(8,128)(2,1)} %get-tuple-element.47), channel_id=1, source_target_pairs={{0,1},{1,0},{2,3},{3,2},{4,5},{5,4},{6,7},{7,6},{8,9},{9,8},{10,11... | collective-permute-start | bytes 983048 | tf_op jit(solution)/shard_map/ppermute | solution.py:25
  31.9 9.3 %collective-permute-start.6 = (bf16[64,2560]{1,0:T(8,128)(2,1)}, bf16[64,2560]{1,0:T(8,128)(2,1)S(1)}, u32[]{:S(2)}, u32[]{:S(2)}) collective-permute-start(bf16[64,2560]{1,0:T(8,128)(2,1)} %get-tuple-element.48), channel_id=1, source_target_pairs={{0,6},{2,0},{4,2},{6,4},{1,7},{3,1},{5,3},{7,5},{8,14},{10,8},{12,... | collective-permute-start | bytes 983048 | tf_op jit(solution)/shard_map/ppermute | solution.py:25
  31.9 14.6 %collective-permute-start.7 = (bf16[64,2560]{1,0:T(8,128)(2,1)}, bf16[64,2560]{1,0:T(8,128)(2,1)S(1)}, u32[]{:S(2)}, u32[]{:S(2)}) collective-permute-start(bf16[64,2560]{1,0:T(8,128)(2,1)} %get-tuple-element.49), channel_id=1, source_target_pairs={{0,7},{1,6},{2,1},{3,0},{4,3},{5,2},{6,5},{7,4},{8,15},{9,14},{10,... | collective-permute-start | bytes 983048 | tf_op jit(solution)/shard_map/ppermute | solution.py:450
  46.6 5.8 %copy-start.3 = (bf16[64,2304]{1,0:T(8,128)(2,1)S(1)}, bf16[64,2304]{1,0:T(8,128)(2,1)}, u32[]{:S(2)}) copy-start(bf16[64,2304]{1,0:T(8,128)(2,1)} %copy-done.2) | copy-start | bytes 884740
  46.6 5.8 %copy-start.5 = (bf16[64,2304]{1,0:T(8,128)(2,1)S(1)}, bf16[64,2304]{1,0:T(8,128)(2,1)}, u32[]{:S(2)}) copy-start(bf16[64,2304]{1,0:T(8,128)(2,1)} %copy-done.4) | copy-start | bytes 884740
  52.4 28.1 %copy-start.1 = (bf16[384,1536]{1,0:T(8,128)(2,1)S(1)}, bf16[384,1536]{1,0:T(8,128)(2,1)}, u32[]{:S(2)}) copy-start(bf16[384,1536]{1,0:T(8,128)(2,1)} %own_w.3) | copy-start | bytes 3538948
  52.4 28.1 %copy-start.10 = (f32[5]{0:T(128)S(1)}, f32[5]{0:T(128)}, u32[]{:S(2)}) copy-start(f32[5]{0:T(128)} %var_ref.1) | copy-start | bytes 64
  52.4 28.1 %copy-start.11 = (f32[32]{0:T(128)S(1)}, f32[32]{0:T(128)}, u32[]{:S(2)}) copy-start(f32[32]{0:T(128)} %constant.26.clone.lat_ref) | copy-start | bytes 388
  58.3 20.1 %collective-permute-start.8 = (bf16[224,1536]{1,0:T(8,128)(2,1)S(1)}, bf16[224,1536]{1,0:T(8,128)(2,1)S(1)}, u32[]{:S(2)}, u32[]{:S(2)}) collective-permute-start(bf16[224,1536]{1,0:T(8,128)(2,1)S(1)} %collective-permute-done.4.r2), channel_id=1, source_target_pairs={{0,8},{8,16},{16,24},{24,0},{1,9},{9,17},{17,25},{25,1},{2,10},{10... | collective-permute-start | bytes 2064392 | tf_op jit(solution)/shard_map/ppermute | solution.py:25
  60.3 18.1 %collective-permute-start.9 = (bf16[224,1536]{1,0:T(8,128)(2,1)S(1)}, bf16[224,1536]{1,0:T(8,128)(2,1)S(1)}, u32[]{:S(2)}, u32[]{:S(2)}) collective-permute-start(bf16[224,1536]{1,0:T(8,128)(2,1)S(1)} %collective-permute-done.r1), channel_id=1, source_target_pairs={{0,2},{2,0},{4,6},{6,4},{1,3},{3,1},{5,7},{7,5},{8,10},{10,8},{12,... | collective-permute-start | bytes 2064392 | tf_op jit(solution)/shard_map/ppermute | solution.py:396
  60.3 18.1 %collective-permute-start.10 = (bf16[224,1536]{1,0:T(8,128)(2,1)S(1)}, bf16[224,1536]{1,0:T(8,128)(2,1)S(1)}, u32[]{:S(2)}, u32[]{:S(2)}) collective-permute-start(bf16[224,1536]{1,0:T(8,128)(2,1)S(1)} %collective-permute-done.4.r2), channel_id=1, source_target_pairs={{0,2},{2,0},{4,6},{6,4},{1,3},{3,1},{5,7},{7,5},{8,10},{10,8},{12,... | collective-permute-start | bytes 2064392 | tf_op jit(solution)/shard_map/ppermute | solution.py:396
  78.4 2.1 %collective-permute-start.11 = (bf16[224,1536]{1,0:T(8,128)(2,1)S(1)}, bf16[224,1536]{1,0:T(8,128)(2,1)S(1)}, u32[]{:S(2)}, u32[]{:S(2)}) collective-permute-start(bf16[224,1536]{1,0:T(8,128)(2,1)S(1)} %collective-permute-done.8.r3), channel_id=1, source_target_pairs={{0,2},{2,0},{4,6},{6,4},{1,3},{3,1},{5,7},{7,5},{8,10},{10,8},{12,... | collective-permute-start | bytes 2064392 | tf_op jit(solution)/shard_map/ppermute | solution.py:396
  85.7 7.4 %collective-permute-start.12 = (bf16[40,1664]{1,0:T(8,128)(2,1)S(1)}, bf16[40,1664]{1,0:T(8,128)(2,1)S(1)}, u32[]{:S(2)}, u32[]{:S(2)}) collective-permute-start(bf16[40,1664]{1,0:T(8,128)(2,1)S(1)} %get-tuple-element.55), channel_id=1, source_target_pairs={{0,2},{2,0},{4,6},{6,4},{1,3},{3,1},{5,7},{7,5},{8,10},{10,8},{12,... | collective-permute-start | bytes 399368 | tf_op jit(solution)/shard_map/ppermute | solution.py:396
  85.8 7.3 %collective-permute-start.13 = (bf16[40,1664]{1,0:T(8,128)(2,1)S(1)}, bf16[40,1664]{1,0:T(8,128)(2,1)S(1)}, u32[]{:S(2)}, u32[]{:S(2)}) collective-permute-start(bf16[40,1664]{1,0:T(8,128)(2,1)S(1)} %get-tuple-element.56), channel_id=1, source_target_pairs={{0,4},{2,6},{4,0},{6,2},{1,5},{3,7},{5,1},{7,3},{8,12},{10,14},{12... | collective-permute-start | bytes 399368 | tf_op jit(solution)/shard_map/ppermute | solution.py:396
  86.1 7.9 %collective-permute-start.14 = (bf16[40,1664]{1,0:T(8,128)(2,1)S(1)}, bf16[40,1664]{1,0:T(8,128)(2,1)S(1)}, u32[]{:S(2)}, u32[]{:S(2)}) collective-permute-start(bf16[40,1664]{1,0:T(8,128)(2,1)S(1)} %get-tuple-element.57), channel_id=1, source_target_pairs={{0,6},{2,4},{4,2},{6,0},{1,7},{3,5},{5,3},{7,1},{8,14},{10,12},{12... | collective-permute-start | bytes 399368 | tf_op jit(solution)/shard_map/ppermute | solution.py:396
  94.1 5.9 %collective-permute-start.15 = (bf16[40,1664]{1,0:T(8,128)(2,1)S(1)}, bf16[40,1664]{1,0:T(8,128)(2,1)S(1)}, u32[]{:S(2)}, u32[]{:S(2)}) collective-permute-start(bf16[40,1664]{1,0:T(8,128)(2,1)S(1)} %lat_sum.1.refs_1_), channel_id=1, source_target_pairs={{0,1},{1,0},{2,3},{3,2},{4,5},{5,4},{6,7},{7,6},{8,9},{9,8},{10,11... | collective-permute-start | bytes 399368 | tf_op jit(solution)/shard_map/ppermute | solution.py:396
  100.7 4.4 %collective-permute-start.16 = (bf16[40,384]{1,0:T(8,128)(2,1)S(1)}, bf16[40,384]{1,0:T(8,128)(2,1)S(1)}, u32[]{:S(2)}, u32[]{:S(2)}) collective-permute-start(bf16[40,384]{1,0:T(8,128)(2,1)S(1)} %get-tuple-element.67), channel_id=1, source_target_pairs={{0,8},{8,0},{16,24},{24,16},{1,9},{9,1},{17,25},{25,17},{2,10},{10... | collective-permute-start | bytes 92168 | tf_op jit(solution)/shard_map/ppermute | solution.py:396
  100.7 5.3 %collective-permute-start.17 = (bf16[40,384]{1,0:T(8,128)(2,1)S(1)}, bf16[40,384]{1,0:T(8,128)(2,1)S(1)}, u32[]{:S(2)}, u32[]{:S(2)}) collective-permute-start(bf16[40,384]{1,0:T(8,128)(2,1)S(1)} %get-tuple-element.68), channel_id=1, source_target_pairs={{0,16},{8,24},{16,0},{24,8},{1,17},{9,25},{17,1},{25,9},{2,18},{10... | collective-permute-start | bytes 92168 | tf_op jit(solution)/shard_map/ppermute | solution.py:396
  101.6 5.7 %collective-permute-start.18 = (bf16[40,384]{1,0:T(8,128)(2,1)S(1)}, bf16[40,384]{1,0:T(8,128)(2,1)S(1)}, u32[]{:S(2)}, u32[]{:S(2)}) collective-permute-start(bf16[40,384]{1,0:T(8,128)(2,1)S(1)} %get-tuple-element.69), channel_id=1, source_target_pairs={{0,24},{8,16},{16,8},{24,0},{1,25},{9,17},{17,9},{25,1},{2,26},{10... | collective-permute-start | bytes 92168 | tf_op jit(solution)/shard_map/ppermute | solution.py:396
  107.3 4.0 %collective-permute-start.21 = (f32[40,384]{1,0:T(8,128)S(1)}, f32[40,384]{1,0:T(8,128)S(1)}, u32[]{:S(2)}, u32[]{:S(2)}) collective-permute-start(f32[40,384]{1,0:T(8,128)S(1)} %dp_sum.1.a), channel_id=1, source_target_pairs={{0,6},{2,4},{4,2},{6,0},{1,7},{3,5},{5,3},{7,1},{8,14},{10,12},{12... | collective-permute-start | bytes 184328 | tf_op jit(solution)/shard_map/ppermute | solution.py:396
  107.4 5.4 %collective-permute-start.20 = (f32[40,384]{1,0:T(8,128)S(1)}, f32[40,384]{1,0:T(8,128)S(1)}, u32[]{:S(2)}, u32[]{:S(2)}) collective-permute-start(f32[40,384]{1,0:T(8,128)S(1)} %dp_sum.1.a), channel_id=1, source_target_pairs={{0,4},{2,6},{4,0},{6,2},{1,5},{3,7},{5,1},{7,3},{8,12},{10,14},{12... | collective-permute-start | bytes 184328 | tf_op jit(solution)/shard_map/ppermute | solution.py:396
  109.2 3.6 %collective-permute-start.19 = (f32[40,384]{1,0:T(8,128)S(1)}, f32[40,384]{1,0:T(8,128)S(1)}, u32[]{:S(2)}, u32[]{:S(2)}) collective-permute-start(f32[40,384]{1,0:T(8,128)S(1)} %dp_sum.1.a), channel_id=1, source_target_pairs={{0,2},{2,0},{4,6},{6,4},{1,3},{3,1},{5,7},{7,5},{8,10},{10,8},{12,... | collective-permute-start | bytes 184328 | tf_op jit(solution)/shard_map/ppermute | solution.py:396

commit v3 on v2

--- a/solution.py
+++ b/solution.py
@@ -15,9 +15,12 @@
 F32 = jnp.float32
 EXTRA = 256
 UGROWS = 256
+CHUNKS = 3
+PIECES = 12
 VMEM = pl.BlockSpec(memory_space=pltpu.VMEM)
 SMEM = pl.BlockSpec(memory_space=pltpu.SMEM)
 ANY = pl.BlockSpec(memory_space=pl.ANY)
+HBM = pl.BlockSpec(memory_space=pltpu.HBM)
 
 
 def from_behind(array, axis, by):
@@ -130,71 +133,76 @@
     return lax.broadcasted_iota(jnp.int32, shape, dim)
 
 
-def pack_kernel(
-    place_ref, x_ref, t_ref, valid_ref, w_ref, unpatch_ref, gain_ref,
-    own0, own1, east0, east1, south0, south1, diag0, diag1, ug_ref, payload_ref, sems,
-):
-    half = place_ref[1]
+def payload_kernel(place_ref, w_ref, unpatch_ref, gain_ref, ug_ref, payload_ref, u_in, sems):
+    part = place_ref[1]
     rows, width = w_ref.shape
-    hr = rows // 2
-    start = pl.multiple_of(half * hr, 64)
-    copies = [
-        pltpu.make_async_copy(
-            w_ref.at[pl.ds(start, hr), :], payload_ref.at[pl.ds(0, hr), :], sems.at[0]
-        )
-    ]
-    copies[0].start()
+    qr = rows // 4
+    span = unpatch_ref.shape[0]
+    start = pl.multiple_of(part * qr, 32)
+    w_copy = pltpu.make_async_copy(
+        w_ref.at[pl.ds(start, qr), :], payload_ref.at[pl.ds(0, qr), :], sems.at[0]
+    )
+    u_copy = pltpu.make_async_copy(unpatch_ref, u_in, sems.at[1])
+    w_copy.start()
+    u_copy.start()
+    gain = jnp.broadcast_to(gain_ref[...].astype(F32).reshape(1, rows), (16, rows)).astype(BF)
+    ug_ref[pl.ds(span, 16), :] = gain
+    ug_ref[pl.ds(span + 16, UGROWS - span - 16), :] = jnp.zeros((UGROWS - span - 16, rows), BF)
+    u_copy.wait()
+    ug_ref[pl.ds(0, span), :] = u_in[...]
+    for j in range(4):
+        at = pl.multiple_of((4 * part + j) * 16, 16)
+        payload_ref[pl.ds(qr, 16), pl.ds(j * rows, rows)] = ug_ref[pl.ds(at, 16), :]
+    w_copy.wait()
+
+
+def pack_kernel(x_ref, t_ref, valid_ref, *refs):
+    outs = refs[: 4 * CHUNKS]
+    x_in, t_in, v_in, sems = refs[4 * CHUNKS :]
+    width = x_ref.shape[-1] // 3
     span = t_ref.shape[-1]
-    ug_ref[...] = jnp.concatenate(
-        [
-            unpatch_ref[...],
-            jnp.broadcast_to(gain_ref[...], (16, rows)),
-            jnp.zeros((UGROWS - span - 16, rows), BF),
-        ],
-        axis=0,
-    )
-    for j in range(4):
-        at = pl.multiple_of((4 * half + j) * 32, 32)
-        copies.append(
-            pltpu.make_async_copy(
-                ug_ref.at[pl.ds(at, 32), :],
-                payload_ref.at[pl.ds(hr, 32), pl.ds(j * rows, rows)],
-                sems.at[1 + j],
+    count = x_ref.shape[0] * 64
+    part = width // CHUNKS
+    copies = []
+    for g in range(CHUNKS):
+        for i in range(3):
+            lanes = pl.ds(i * width + g * part, part)
+            at = (slice(None), slice(None), slice(None), lanes)
+            copies.append(
+                pltpu.make_async_copy(x_ref.at[at], x_in.at[at], sems.at[3 * g + i])
             )
-        )
-        copies[-1].start()
-    count = x_ref.shape[0] * 64
+    copies.append(pltpu.make_async_copy(t_ref, t_in, sems.at[3 * CHUNKS]))
+    copies.append(pltpu.make_async_copy(valid_ref, v_in, sems.at[3 * CHUNKS + 1]))
+    for c in copies:
+        c.start()
     place = iota((count, count), 0)
     quad, rest = place // (count // 4), place % (count // 4)
     row = (rest // 4) % 4 + jnp.where(quad < 2, 4, 0)
     col = rest % 4 + jnp.where(quad % 2 == 0, 4, 0)
     source = (rest // 16) * 64 + row * 8 + col
     pick = (iota((count, count), 1) == source).astype(F32).astype(BF)
-    firsts, seconds = (own0, east0, south0, diag0), (own1, east1, south1, diag1)
     quarter = count // 4
-    part = width // 2
-    step = part // 2
-    for at in range(0, 3 * width, step):
-        tokens = x_ref[:, :, :, at : at + step].reshape(count, step)
-        out = jnp.dot(pick, tokens, preferred_element_type=F32).astype(BF)
-        which, inner = at // width, at % width
-        refs = firsts if inner < part else seconds
-        to = which * part + inner % part
-        for q, ref in enumerate(refs):
-            ref[:, to : to + step] = out[q * quarter : (q + 1) * quarter]
-    goal = jnp.dot(pick, t_ref[...].reshape(count, span), preferred_element_type=F32)
+    for g in range(CHUNKS):
+        for i in range(3):
+            copies[3 * g + i].wait()
+            at = i * width + g * part
+            tokens = x_in[:, :, :, at : at + part].reshape(count, part)
+            out = jnp.dot(pick, tokens, preferred_element_type=F32).astype(BF)
+            for q in range(4):
+                outs[4 * g + q][:, i * part : (i + 1) * part] = out[q * quarter : (q + 1) * quarter]
+    copies[-2].wait()
+    copies[-1].wait()
+    goal = jnp.dot(pick, t_in[...].reshape(count, span), preferred_element_type=F32)
     token = iota((count, 8), 0)
     row_hot = ((token // 8) % 8 == iota((count, 8), 1)).astype(F32)
-    by_row = jnp.dot(row_hot, valid_ref[...].astype(F32), preferred_element_type=F32)
+    by_row = jnp.dot(row_hot, v_in[...].astype(F32), preferred_element_type=F32)
     mine = token % 8 == iota((count, 8), 1)
     natural = jnp.sum(jnp.where(mine, by_row, 0.0), axis=1, keepdims=True)
     spread = jnp.broadcast_to(natural, (count, 128)).astype(BF)
     column = jnp.dot(pick, spread, preferred_element_type=F32)
     extra = jnp.concatenate([goal, column[:, : EXTRA - span]], axis=1).astype(BF)
-    for q, ref in enumerate(seconds):
-        ref[:, 3 * part :] = extra[q * quarter : (q + 1) * quarter]
-    for c in copies:
-        c.wait()
+    for q in range(4):
+        outs[4 * CHUNKS - 4 + q][:, 3 * part :] = extra[q * quarter : (q + 1) * quarter]
 
 
 def attention_kernel(last_ref, *refs):
@@ -226,10 +234,10 @@
         ctx_ref[128 * w : 128 * w + 128, :] = out.astype(BF)
 
 
-def piece_copies(zi, half, own_w, own_ug, rings, swaps, w_all, ug_all, sems):
+def piece_copies(zi, part, own_w, own_ug, pieces, w_all, ug_all, sems):
     rows = own_w.shape[0]
-    hr = rows // 2
-    steps = len(rings) + 1
+    qr = rows // 4
+    steps = len(pieces) // 4 + 1
     w_copies, u_copies = [], []
 
     def place(src, dst, to):
@@ -242,14 +250,15 @@
     for k in range(1, steps):
         shard = lax.rem(zi - k + steps, steps)
         base = pl.multiple_of(shard * rows, 128)
-        for piece, part in ((rings[k - 1], half), (swaps[k - 1], 1 - half)):
-            row = pl.multiple_of(base + part * hr, 64)
-            place(piece.at[pl.ds(0, hr), :], w_all.at[pl.ds(row, hr), :], w_copies)
+        for bits, piece in zip((0, 2, 1, 3), pieces[4 * k - 4 : 4 * k]):
+            from_part = part ^ bits
+            row = pl.multiple_of(base + from_part * qr, 32)
+            place(piece.at[pl.ds(0, qr), :], w_all.at[pl.ds(row, qr), :], w_copies)
             for j in range(4):
-                urow = pl.multiple_of((4 * part + j) * 32, 32)
+                urow = pl.multiple_of((4 * from_part + j) * 16, 16)
                 place(
-                    piece.at[pl.ds(hr, 32), pl.ds(j * rows, rows)],
-                    ug_all.at[pl.ds(urow, 32), pl.ds(base, rows)],
+                    piece.at[pl.ds(qr, 16), pl.ds(j * rows, rows)],
+                    ug_all.at[pl.ds(urow, 16), pl.ds(base, rows)],
                     u_copies,
                 )
     return w_copies, u_copies
@@ -267,19 +276,19 @@
     return jnp.where(lane == 0, hi, jnp.where(lane == 1, mid, jnp.where(lane == 2, lo, 0.0)))
 
 
-def forward_kernel(
-    place_ref, lat_ref, var_ref, ctx0_ref, ctx1_ref, e0, e1, e2, e3, own_w, own_ug, r1, r2, r3, c1, c2, c3,
-    t0, t1, t2, t3, normed_ref, inv_ref, dfc_ref, hidden_ref, w_all, ug_all, term, sems,
-):
-    zi, half, lat_place = place_ref[0], place_ref[1], place_ref[2]
-    w_copies, u_copies = piece_copies(
-        zi, half, own_w, own_ug, (r1, r2, r3), (c1, c2, c3), w_all, ug_all, sems
-    )
+def forward_kernel(place_ref, lat_ref, var_ref, *refs):
+    ctx_refs, refs = refs[:CHUNKS], refs[CHUNKS:]
+    extras, refs = refs[:4], refs[4:]
+    (own_w, own_ug), refs = refs[:2], refs[2:]
+    pieces, refs = refs[:PIECES], refs[PIECES:]
+    ts, refs = refs[:4], refs[4:]
+    normed_ref, inv_ref, dfc_ref, hidden_ref, w_all, ug_all, term, sems = refs
+    zi, lat_place = place_ref[0], place_ref[1]
+    w_copies, u_copies = piece_copies(zi, lat_place, own_w, own_ug, pieces, w_all, ug_all, sems)
     for c in w_copies + u_copies:
         c.start()
     tokens, width = normed_ref.shape
     span = dfc_ref.shape[1]
-    extras = [e0, e1, e2, e3]
     extra = jnp.concatenate(
         [e[32 * w : 32 * w + 32, :] for w in range(2) for e in extras], axis=0
     ).astype(F32)
@@ -296,9 +305,11 @@
     weight = lat_w * valid * var_w
     for c in w_copies:
         c.wait()
-    part = width // 2
-    mixed = jnp.dot(ctx0_ref[...], w_all[0:part, :], preferred_element_type=F32)
-    mixed += jnp.dot(ctx1_ref[...], w_all[part:, :], preferred_element_type=F32)
+    part = width // CHUNKS
+    mixed = jnp.dot(ctx_refs[0][...], w_all[0:part, :], preferred_element_type=F32)
+    for g in range(1, CHUNKS):
+        rows_g = w_all[g * part : (g + 1) * part, :]
+        mixed += jnp.dot(ctx_refs[g][...], rows_g, preferred_element_type=F32)
     centre = jnp.mean(mixed, axis=-1, keepdims=True)
     off = mixed - centre
     inv = lax.rsqrt(jnp.mean(off * off, axis=-1, keepdims=True) + 1e-05)
@@ -319,22 +330,18 @@
         dfc, hidden_ref[...], (((0,), (0,)), ((), ())), preferred_element_type=F32
     )
     loss = jnp.sum(jnp.sum(weight * misfit * misfit, axis=1, keepdims=True), axis=0, keepdims=True)
-    rows = t0.shape[0]
+    rows = ts[0].shape[0]
     block = loss_block(loss, rows).astype(BF)
-    for b, ref in enumerate((t0, t1, t2, t3)):
+    for b, ref in enumerate(ts):
         at = pl.multiple_of((lat_place ^ b) * rows, 8)
         ref[:, :width] = term[pl.ds(at, rows), :].astype(BF)
         ref[:, width:] = block
 
 
-def backward_kernel(
-    place_ref, normed_ref, inv_ref, dfc_ref, own_w, own_ug, r1, r2, r3, c1, c2, c3,
-    out_ref, w_all, ug_all, sems,
-):
-    zi, half = place_ref[0], place_ref[1]
-    w_copies, u_copies = piece_copies(
-        zi, half, own_w, own_ug, (r1, r2, r3), (c1, c2, c3), w_all, ug_all, sems
-    )
+def backward_kernel(place_ref, normed_ref, inv_ref, dfc_ref, own_w, own_ug, *refs):
+    pieces, (out_ref, w_all, ug_all, sems) = refs[:PIECES], refs[PIECES:]
+    zi, part = place_ref[0], place_ref[1]
+    w_copies, u_copies = piece_copies(zi, part, own_w, own_ug, pieces, w_all, ug_all, sems)
     for c in u_copies + w_copies:
         c.start()
     tokens, width = normed_ref.shape
@@ -359,37 +366,41 @@
     out_ref[...] = out.astype(BF)
 
 
-def lat_sum_kernel(a, b, c, d, s_ref):
-    total = (a[...].astype(F32) + b[...].astype(F32)) + (c[...].astype(F32) + d[...].astype(F32))
-    width = s_ref.shape[1] - 128
-    s_ref[:, :width] = total[:, :width].astype(BF)
-    loss = jnp.sum(total[0:1, width:], axis=1, keepdims=True)
-    s_ref[:, width:] = loss_block(loss, s_ref.shape[0]).astype(BF)
-
-
-def lon_sum_kernel(denominator, place_ref, a, b, z0, z1, z2, z3, loss_ref, total_ref):
-    total = a[...].astype(F32) + b[...].astype(F32)
-    total_ref[...] = total
+def add4(a, b, c, d):
+    return (a[...].astype(F32) + b[...].astype(F32)) + (c[...].astype(F32) + d[...].astype(F32))
+
+
+def lat_sum_kernel(place_ref, a, b, c, d, z0, z1, z2, z3, loss_ref, total_ref):
+    total_ref[...] = add4(a, b, c, d)
     zi = place_ref[0]
     rows, width = z0.shape
     for k, ref in enumerate((z0, z1, z2, z3)):
         at = pl.multiple_of((zi ^ k) * width, 128)
         ref[...] = total_ref[:, pl.ds(at, width)].astype(BF)
-    loss = jnp.sum(total[0:1, 4 * width :], axis=1, keepdims=True) / denominator
+    loss = jnp.sum(total_ref[0:1, 4 * width :], axis=1, keepdims=True)
     loss_ref[...] = jnp.broadcast_to(loss, loss_ref.shape)
 
 
-def dp_sum_kernel(denominator, a, b, c, d, o_ref):
-    total = (a[...].astype(F32) + b[...].astype(F32)) + (c[...].astype(F32) + d[...].astype(F32))
-    o_ref[...] = total / denominator
-
-
-def join_kernel(place_ref, a, b, c, d, o_ref):
-    rows = a.shape[0]
-    lat_place = place_ref[2]
-    for k, ref in enumerate((a, b, c, d)):
-        at = pl.multiple_of((lat_place ^ k) * rows, 8)
-        o_ref[pl.ds(at, rows), :] = ref[...]
+def dp_sum_kernel(loss_ref, a, b, c, d, o_ref):
+    rows, width = a.shape
+    o_ref[0:rows, :] = add4(a, b, c, d).astype(BF)
+    block = loss_block(loss_ref[0:1, 0:1], o_ref.shape[0] - rows)
+    zeros = jnp.zeros((block.shape[0], width - 128), F32)
+    o_ref[rows:, :] = jnp.concatenate([block, zeros], axis=1).astype(BF)
+
+
+def join_kernel(counts, place_ref, *refs):
+    pieces, (o_ref, loss_ref) = refs[:8], refs[8:]
+    lat_place = place_ref[1]
+    rows = o_ref.shape[0] // 4
+    for a in range(4):
+        at = pl.multiple_of((lat_place ^ a) * rows, 8)
+        both = [pieces[2 * a + b][0:rows, :].astype(F32) for b in range(2)]
+        o_ref[pl.ds(at, rows), :] = (both[0] + both[1]) / counts[0]
+    sums = [
+        jnp.sum(p[rows : rows + 1, 0:128].astype(F32), axis=1, keepdims=True) for p in pieces[:2]
+    ]
+    loss_ref[...] = jnp.broadcast_to((sums[0] + sums[1]) / counts[1], loss_ref.shape)
 
 
 def swap(array, axis, bit):
@@ -406,49 +417,56 @@
     levels = projected.shape[1]
     span = unpatch_matrix.shape[1]
     tokens = levels * 64
-    zi, lat_place = lax.axis_index("dp"), lax.axis_index("lat")
-    half = lat_place % 2
-    place = jnp.stack([zi, half, lat_place]).astype(jnp.int32)
+    quarter = tokens // 4
+    part = width // CHUNKS
+    lat_place = lax.axis_index("lat")
+    place = jnp.stack([lax.axis_index("dp"), lat_place]).astype(jnp.int32)
     last = (lat_place == lat - 1).astype(jnp.int32).reshape(1)
     lat_total = 8 * lat
     angle = math.pi * ((np.arange(lat_total) + 0.5) / lat_total - 0.5)
     cosine = np.cos(angle)
     lat_table = jnp.asarray(np.roll(cosine / cosine.mean(), -4), F32)
-
-    part = width // 2
-    quarter = tokens // 4
-    widths = (3 * part, 3 * part + EXTRA)
-    *packed, ug, payload = pl.pallas_call(
+    barrier = lax.optimization_barrier
+
+    ug, payload = pl.pallas_call(
+        payload_kernel,
+        out_shape=[shape((UGROWS, rows), BF), shape((rows // 4 + 16, width), BF)],
+        in_specs=[SMEM, HBM, HBM, VMEM],
+        out_specs=[VMEM] * 2,
+        scratch_shapes=[pltpu.VMEM((span, rows), BF), pltpu.SemaphoreType.DMA((2,))],
+        compiler_params=params(62),
+        name="payload",
+    )(place, w_out, unpatch_matrix.T, norm_gain)
+    ring1 = from_behind(payload, "dp", 1)
+
+    widths = [3 * part] * (CHUNKS - 1) + [3 * part + EXTRA]
+    packed = pl.pallas_call(
         pack_kernel,
-        out_shape=[shape((quarter, w), BF) for _ in range(4) for w in widths]
-        + [shape((UGROWS, rows), BF), shape((rows // 2 + 32, width), BF)],
-        in_specs=[SMEM] + [VMEM] * 3 + [ANY] + [VMEM] * 2,
-        out_specs=[VMEM] * 9 + [ANY],
-        scratch_shapes=[pltpu.SemaphoreType.DMA((5,))],
-        compiler_params=params(20),
+        out_shape=[shape((quarter, w), BF) for w in widths for _ in range(4)],
+        in_specs=[HBM] * 3,
+        out_specs=[VMEM] * (4 * CHUNKS),
+        scratch_shapes=[
+            pltpu.VMEM((levels, 8, 8, 3 * width), BF),
+            pltpu.VMEM((levels, 8, 8, span), BF),
+            pltpu.VMEM((8, 8), jnp.int32),
+            pltpu.SemaphoreType.DMA((3 * CHUNKS + 2,)),
+        ],
+        compiler_params=params(60),
         name="pack",
-    )(
-        place,
-        projected.reshape(levels, 8, 8, 3 * width),
-        targets.reshape(levels, 8, 8, span),
-        valid_cells,
-        w_out,
-        unpatch_matrix.T,
-        norm_gain.reshape(1, rows),
-    )
+    )(projected.reshape(levels, 8, 8, 3 * width), targets.reshape(levels, 8, 8, span), valid_cells)
     corner = [
         (a * lon + b, ((a - 1) % lat) * lon + (b - 1) % lon) for a in range(lat) for b in range(lon)
     ]
     tiles = []
-    for g in range(2):
-        own, east, south, diag = packed[g::2]
+    for g in range(CHUNKS):
+        own, east, south, diag = packed[4 * g : 4 * g + 4]
         tiles.append(
-            (
+            [
                 own,
                 from_behind(east, "lon", -1),
                 from_behind(south, "lat", -1),
                 lax.ppermute(diag, ("lat", "lon"), corner),
-            )
+            ]
         )
     groups = part // 128
 
@@ -466,89 +484,91 @@
             name="attention",
         )(last, *[t for t in chunk for _ in range(3)])
 
-    ring1 = from_behind(payload, "dp", 1)
-    ring1_after, *first = lax.optimization_barrier((ring1, *tiles[0][1:]))
+    ring1_after, *tiles[0] = barrier((ring1, *tiles[0]))
     ring2 = from_behind(ring1_after, "dp", 1)
-    ctx0 = attend((tiles[0][0], *first))
+    across1 = swap(ring1, "lat", 2)
+    ctx0 = attend(tiles[0])
+    ring2_after, across1, ctx0, *tiles[1] = barrier((ring2, across1, ctx0, *tiles[1]))
+    ring3 = from_behind(ring2_after, "dp", 1)
+    across2 = swap(ring2, "lat", 2)
     ctx1 = attend(tiles[1])
-    ring2_after, ctx0, ctx1 = lax.optimization_barrier((ring2, ctx0, ctx1))
-    ring3 = from_behind(ring2_after, "dp", 1)
-    rings = [ring1, ring2, ring3]
-    swaps = [swap(r, "lat", 1) for r in rings]
+    ring3_after, across2, ctx1, *tiles[2] = barrier((ring3, across2, ctx1, *tiles[2]))
+    across3 = swap(ring3_after, "lat", 2)
+    ctx2 = attend(tiles[2])
+    pieces = []
+    for ring, across in ((ring1, across1), (ring2, across2), (ring3, across3)):
+        pieces += [ring, across, swap(ring, "lat", 1), swap(across, "lat", 1)]
 
     piece = span // lat
-    extra_spec = pl.BlockSpec((tokens // 4, EXTRA), lambda i: (0, 3 * part // EXTRA))
-    copies = 2 + 2 * (dp - 1) * 5
+    extra_spec = pl.BlockSpec((quarter, EXTRA), lambda i: (0, 3 * part // EXTRA))
+    copies = 2 + PIECES * 5
     assembly = [
         pltpu.VMEM((dp * rows, width), BF),
         pltpu.VMEM((UGROWS, dp * rows), BF),
     ]
-    t0, t1, t2, t3, normed, inv, dfc = pl.pallas_call(
+    *terms, normed, inv, dfc = pl.pallas_call(
         forward_kernel,
         grid=(1,),
         out_shape=[shape((piece, width + 128), BF)] * 4
         + [shape((tokens, width), F32), shape((tokens, 128), F32), shape((tokens, span), BF)],
-        in_specs=[SMEM] * 3 + [VMEM] * 2 + [extra_spec] * 4 + [ANY] * 8,
+        in_specs=[SMEM] * 3 + [VMEM] * CHUNKS + [extra_spec] * 4 + [HBM] + [ANY] * (1 + PIECES),
         out_specs=[VMEM] * 7,
         scratch_shapes=[pltpu.VMEM((tokens, width), BF)]
         + assembly
         + [pltpu.VMEM((span, width), F32), pltpu.SemaphoreType.DMA((copies,))],
         compiler_params=params(28),
         name="forward",
-    )(place, lat_table, var_weight, ctx0, ctx1, *tiles[1], w_out, ug, *rings, *swaps)
-
-    terms = [t0] + [swap(t, "lat", b) for b, t in ((1, t1), (2, t2), (3, t3))]
+    )(place, lat_table, var_weight, ctx0, ctx1, ctx2, *tiles[2], w_out, ug, *pieces)
+
+    terms = [terms[0]] + [swap(terms[b], "lat", b) for b in (1, 2, 3)]
     grad_context = pl.pallas_call(
         backward_kernel,
         out_shape=shape((tokens, width), BF),
-        in_specs=[SMEM] + [VMEM] * 3 + [ANY] * 8,
+        in_specs=[SMEM] + [VMEM] * 3 + [HBM] + [ANY] * (1 + PIECES),
         out_specs=VMEM,
         scratch_shapes=assembly + [pltpu.SemaphoreType.DMA((copies,))],
         compiler_params=params(24),
         name="backward",
-    )(place, normed, inv, dfc, w_out, ug, *rings, *swaps)
-
-    *terms, grad_context = lax.optimization_barrier((*terms, grad_context))
-    lat_sum = pl.pallas_call(
+    )(place, normed, inv, dfc, w_out, ug, *pieces)
+    *terms, grad_context = barrier((*terms, grad_context))
+
+    *parts, loss = pl.pallas_call(
         lat_sum_kernel,
-        out_shape=shape((piece, width + 128), BF),
-        in_specs=[VMEM] * 4,
-        out_specs=VMEM,
-        compiler_params=params(4),
-        name="lat_sum",
-    )(*terms)
-    denominator = levels * lat_total * 8 * lon
-    *parts, loss = pl.pallas_call(
-        lambda *refs: lon_sum_kernel(float(denominator * (span // var_weight.shape[0])), *refs),
         out_shape=[shape((piece, rows), BF)] * 4 + [shape((8, 128), F32)],
-        in_specs=[SMEM] + [VMEM] * 2,
+        in_specs=[SMEM] + [VMEM] * 4,
         out_specs=[VMEM] * 5,
         scratch_shapes=[pltpu.VMEM((piece, width + 128), F32)],
         compiler_params=params(4),
-        name="lon_sum",
-    )(place, lat_sum, swap(lat_sum, "lon", 1))
+        name="lat_sum",
+    )(place, *terms)
     parts = [parts[0]] + [swap(parts[k], "dp", k) for k in (1, 2, 3)]
     mine = pl.pallas_call(
-        lambda *refs: dp_sum_kernel(float(denominator), *refs),
-        out_shape=shape((piece, rows), F32),
-        in_specs=[VMEM] * 4,
+        dp_sum_kernel,
+        out_shape=shape((piece + 8, rows), BF),
+        in_specs=[VMEM] * 5,
         out_specs=VMEM,
         compiler_params=params(4),
         name="dp_sum",
-    )(*parts)
-    joined = pl.pallas_call(
-        join_kernel,
-        out_shape=shape((span, rows), F32),
-        in_specs=[SMEM] + [VMEM] * 4,
-        out_specs=VMEM,
+    )(loss, *parts)
+    plane = [mine]
+    for a in range(4):
+        for b in range(2):
+            if a or b:
+                pairs = [
+                    (i * lon + j, (i ^ a) * lon + (j ^ b)) for i in range(lat) for j in range(lon)
+                ]
+                plane.append(lax.ppermute(mine, ("lat", "lon"), pairs))
+    count = levels * lat_total * 8 * lon
+    counts = (float(count), float(count * (span // var_weight.shape[0])))
+    joined, loss = pl.pallas_call(
+        lambda *refs: join_kernel(counts, *refs),
+        out_shape=[shape((span, rows), F32), shape((1, 1), F32)],
+        in_specs=[SMEM] + [VMEM] * 8,
+        out_specs=[VMEM] * 2,
         compiler_params=params(4),
         name="join",
-    )(place, mine, *[swap(mine, "lat", b) for b in (1, 2, 3)])
-    return (
-        grad_context.reshape(1, levels, 8, 8, width),
-        joined.T,
-        loss[0, 0:1],
-    )
+    )(place, *plane)
+    return grad_context.reshape(1, levels, 8, 8, width), joined.T, loss.reshape(1)
 
 
 def solution(mesh):

time: 114 us -> 101 us (0.89)
  waiting for transfers between devices: 56.1 us -> 32.7 us
  starting transfers between devices: 21.6 us -> 32.9 us
  local copies, waits for them, and re-layouts: 8.09 us -> 0.98 us
  Pallas kernels: 27.4 us -> 32.8 us
    ppermute x7 -> x9, waiting for transfers between devices: 35 us -> 15.3 us  [from_behind(): lax.ppermute(array, axis, [(i, (i + by) % length) for i in range(length)])]
    ppermute x0 -> x7, starting transfers between devices: none -> 6.87 us  [shards(): plane.append(lax.ppermute(mine, ('lat', 'lon'), pairs))]
    ppermute x2 -> x3, waiting for transfers between devices: 8.49 us -> 1.87 us  [shards(): lax.ppermute(diag, ('lat', 'lon'), corner)]
    unnamed x24 -> x22, local copies, waits for them, and re-layouts: 6.9 us -> 0.98 us
    pallas_call x5, Pallas kernels: 5.16 us -> 9.14 us  [the longest x1 4.61 us: shards(): pl.pallas_call(pack_kernel, out_shape=[shape((quarter, w), BF) for w in w...]
    ppermute x7 -> x9, starting transfers between devices: 8.48 us -> 11.6 us  [from_behind(): lax.ppermute(array, axis, [(i, (i + by) % length) for i in range(length)])]
    ppermute x0 -> x7, waiting for transfers between devices: none -> 3.07 us  [shards(): plane.append(lax.ppermute(mine, ('lat', 'lon'), pairs))]
    ppermute x13 -> x15, starting transfers between devices: 10.3 us -> 12.3 us  [swap(): lax.ppermute(array, axis, [(i, i ^ bit) for i in range(lax.axis_size(axis...]
  transfers between devices with their start and end apart: 22 -> 34, of which waited for: 13 -> 13; matrix products, arithmetic and copies ran while one was open for 0% -> 0% of each run, Pallas kernels for 15% -> 22%
where the time goes in v3:
time: 101 us
  starting transfers between devices  32.9 us (33%)
  Pallas kernels  32.8 us (32%)
  waiting for transfers between devices  32.7 us (32%)
    ppermute x9, waiting for transfers between devices, from_behind(): lax.ppermute(array, axis, [(i, (i + by) % length) for i in range(length)])  15.3 us
    ppermute x15, waiting for transfers between devices, swap(): lax.ppermute(array, axis, [(i, i ^ bit) for i in range(lax.axis_size(axis...  12.4 us
    ppermute x15, starting transfers between devices, swap(): lax.ppermute(array, axis, [(i, i ^ bit) for i in range(lax.axis_size(axis...  12.3 us
    pallas_call x3, Pallas kernels, attend(): pl.pallas_call(attention_kernel, grid=(groups,), out_shape=shape((tokens,...  11.6 us
    ppermute x9, starting transfers between devices, from_behind(): lax.ppermute(array, axis, [(i, (i + by) % length) for i in range(length)])  11.6 us
    ppermute x7, starting transfers between devices, shards(): plane.append(lax.ppermute(mine, ('lat', 'lon'), pairs))  6.87 us
    pallas_call x1, Pallas kernels, shards(): pl.pallas_call(backward_kernel, out_shape=shape((tokens, width), BF), in_...  6.24 us
    pallas_call x1, Pallas kernels, shards(): pl.pallas_call(forward_kernel, grid=(1,), out_shape=[shape((piece, width...  5.84 us
  transfers between devices with their start and end apart: 34, of which 13 were waited for; matrix products, arithmetic and copies ran while one was open for 0% of the time, Pallas kernels for 22%

profile of v3, /device:TPU:0, one launch (start us, length us, event | category | flops | bytes accessed | tf_op | source)
XLA Modules:
  0.0 100.9 jit_solution(15997163878658229551)
XLA Ops:
  0.6 0.6 pad_add_fusion.place_ref.refs_0_
  1.2 2.5 %payload.1 = (bf16[256,384]{1,0:T(8,128)(2,1)}, bf16[112,1536]{1,0:T(8,128)(2,1)}) custom-call(s32[2]{0:T(128)} %pad_add_fusion.place_ref.refs_0_, bf16[384,1536]{1,0:T(8,128)(2,1)} %own_w.1, bf16[160,384]{1,0:T(8,128)(2,1)} %bitcast.12, bf16[384]{0:T(512)(128)(2,1)} %gain_ref.1), custom_call_target="tpu_custom_call" | custom-call | tf_op jit(solution)/shard_map/payload/pallas_call | solution.py:431
  3.7 3.1 %collective-permute-start = (bf16[112,1536]{1,0:T(8,128)(2,1)}, bf16[112,1536]{1,0:T(8,128)(2,1)S(1)}, u32[]{:S(2)}, u32[]{:S(2)}) collective-permute-start(bf16[112,1536]{1,0:T(8,128)(2,1)} %get-tuple-element.55), channel_id=1, source_target_pairs={{0,8},{8,16},{16,24},{24,0},{1,9},{9,17},{17,25},{25,1},{2,10},{10... | collective-permute-start | bytes 1032200 | tf_op jit(solution)/shard_map/ppermute | solution.py:28
  6.8 4.6 %pack.1 = (bf16[64,1536]{1,0:T(8,128)(2,1)}, bf16[64,1536]{1,0:T(8,128)(2,1)}, bf16[64,1536]{1,0:T(8,128)(2,1)}, bf16[64,1536]{1,0:T(8,128)(2,1)}, bf16[64,1536]...) custom-call(bf16[4,8,8,4608]{3,2,1,0:T(8,128)(2,1)} %bitcast.9, ...), custom_call_target="tpu_custom_call" | custom-call | tf_op jit(solution)/shard_map/pack/pallas_call | solution.py:443
  11.5 1.6 %collective-permute-start.1 = (bf16[64,1536]{1,0:T(8,128)(2,1)}, bf16[64,1536]{1,0:T(8,128)(2,1)S(1)}, u32[]{:S(2)}, u32[]{:S(2)}) collective-permute-start(bf16[64,1536]{1,0:T(8,128)(2,1)} %get-tuple-element.57), channel_id=1, source_target_pairs={{0,1},{1,0},{2,3},{3,2},{4,5},{5,4},{6,7},{7,6},{8,9},{9,8},{10,11... | collective-permute-start | bytes 589832 | tf_op jit(solution)/shard_map/ppermute | solution.py:28
  13.0 0.4 collective-permute-start.2
  13.4 1.2 %collective-permute-start.3 = (bf16[64,1536]{1,0:T(8,128)(2,1)}, bf16[64,1536]{1,0:T(8,128)(2,1)S(1)}, u32[]{:S(2)}, u32[]{:S(2)}) collective-permute-start(bf16[64,1536]{1,0:T(8,128)(2,1)} %get-tuple-element.59), channel_id=1, source_target_pairs={{0,7},{1,6},{2,1},{3,0},{4,3},{5,2},{6,5},{7,4},{8,15},{9,14},{10,... | collective-permute-start | bytes 589832 | tf_op jit(solution)/shard_map/ppermute | solution.py:468
  14.6 4.9 %collective-permute-done.1.refs_3_.refs_4_.refs_5_ = bf16[64,1536]{1,0:T(8,128)(2,1)S(1)} collective-permute-done((bf16[64,1536]{1,0:T(8,128)(2,1)}, bf16[64,1536]{1,0:T(8,128)(2,1)S(1)}, u32[]{:S(2)}, u32[]{:S(2)}) %collective-permute-start.1) | collective-permute-done | bytes 196640 | tf_op jit(solution)/shard_map/ppermute | solution.py:28
  19.6 0.0 collective-permute-done.2.refs_6_.refs_7_.refs_8_
  19.6 1.9 %collective-permute-done.3.refs_9_.refs_10_.refs_11_ = bf16[64,1536]{1,0:T(8,128)(2,1)S(1)} collective-permute-done((bf16[64,1536]{1,0:T(8,128)(2,1)}, bf16[64,1536]{1,0:T(8,128)(2,1)S(1)}, u32[]{:S(2)}, u32[]{:S(2)}) %collective-permute-start.3) | collective-permute-done | bytes 196640 | tf_op jit(solution)/shard_map/ppermute | solution.py:468
  21.4 0.0 collective-permute-done.refs_9_.refs_0_
  21.4 1.5 %collective-permute-start.5 = (bf16[112,1536]{1,0:T(8,128)(2,1)S(1)}, bf16[112,1536]{1,0:T(8,128)(2,1)S(1)}, u32[]{:S(2)}, u32[]{:S(2)}) collective-permute-start(bf16[112,1536]{1,0:T(8,128)(2,1)S(1)} %collective-permute-done.refs_9_.refs_0_), channel_id=1, source_target_pairs={{0,4},{2,6},{4,0},{6,2},{1,5},{3,7},{5,1},{7,3},{8,12},{10,14},{12... | collective-permute-start | bytes 1032200 | tf_op jit(solution)/shard_map/ppermute | solution.py:407
  22.9 1.6 %collective-permute-start.4 = (bf16[112,1536]{1,0:T(8,128)(2,1)S(1)}, bf16[112,1536]{1,0:T(8,128)(2,1)S(1)}, u32[]{:S(2)}, u32[]{:S(2)}) collective-permute-start(bf16[112,1536]{1,0:T(8,128)(2,1)S(1)} %collective-permute-done.refs_9_.refs_0_), channel_id=1, source_target_pairs={{0,8},{8,16},{16,24},{24,0},{1,9},{9,17},{17,25},{25,1},{2,10},{10... | collective-permute-start | bytes 1032200 | tf_op jit(solution)/shard_map/ppermute | solution.py:28
  24.5 0.9 collective-permute-start.6
  25.4 1.5 %collective-permute-start.7 = (bf16[64,1536]{1,0:T(8,128)(2,1)}, bf16[64,1536]{1,0:T(8,128)(2,1)S(1)}, u32[]{:S(2)}, u32[]{:S(2)}) collective-permute-start(bf16[64,1536]{1,0:T(8,128)(2,1)} %get-tuple-element.67), channel_id=1, source_target_pairs={{0,6},{2,0},{4,2},{6,4},{1,7},{3,1},{5,3},{7,5},{8,14},{10,8},{12,... | collective-permute-start | bytes 589832 | tf_op jit(solution)/shard_map/ppermute | solution.py:28
  27.0 0.9 copy-done.3
  27.9 3.9 %attention.3.refs_0_ = bf16[256,512]{1,0:T(8,128)(2,1)S(1)} custom-call(s32[1]{0:T(128)} %bitcast.5.last_ref, bf16[64,1536]{1,0:T(8,128)(2,1)S(1)} %copy-done.3, bf16[64,1536]{1,0:T(8,128)(2,1)S(1)} %copy-done.3, bf16[64,1536]{1,0:T(8,128)(2,1)S(1)} %copy-done.3, bf16[64,1536]{1,0:T(8,128)(2,1)S(1)} %collective-permute-done.1.refs_3_.refs_4_.refs_5_, ...), custom_call_target="tpu_custom_call" | custom-call | tf_op jit(solution)/shard_map/attention/pallas_call | solution.py:477
  31.8 0.0 copy-start.1
  31.8 0.7 collective-permute-done.6.refs_3_.refs_4_.refs_5_
  32.5 2.9 %collective-permute-done.7.refs_6_.refs_7_.refs_8_ = bf16[64,1536]{1,0:T(8,128)(2,1)S(1)} collective-permute-done((bf16[64,1536]{1,0:T(8,128)(2,1)}, bf16[64,1536]{1,0:T(8,128)(2,1)S(1)}, u32[]{:S(2)}, u32[]{:S(2)}) %collective-permute-start.7) | collective-permute-done | bytes 196640 | tf_op jit(solution)/shard_map/ppermute | solution.py:28
  35.4 0.0 collective-permute-done.4.refs_13_.refs_4_
  35.4 1.6 %collective-permute-start.9 = (bf16[112,1536]{1,0:T(8,128)(2,1)S(1)}, bf16[112,1536]{1,0:T(8,128)(2,1)S(1)}, u32[]{:S(2)}, u32[]{:S(2)}) collective-permute-start(bf16[112,1536]{1,0:T(8,128)(2,1)S(1)} %collective-permute-done.4.refs_13_.refs_4_), channel_id=1, source_target_pairs={{0,8},{8,16},{16,24},{24,0},{1,9},{9,17},{17,25},{25,1},{2,10},{10... | collective-permute-start | bytes 1032200 | tf_op jit(solution)/shard_map/ppermute | solution.py:28
  37.1 1.8 %collective-permute-start.10 = (bf16[112,1536]{1,0:T(8,128)(2,1)S(1)}, bf16[112,1536]{1,0:T(8,128)(2,1)S(1)}, u32[]{:S(2)}, u32[]{:S(2)}) collective-permute-start(bf16[112,1536]{1,0:T(8,128)(2,1)S(1)} %collective-permute-done.4.refs_13_.refs_4_), channel_id=1, source_target_pairs={{0,4},{2,6},{4,0},{6,2},{1,5},{3,7},{5,1},{7,3},{8,12},{10,14},{12... | collective-permute-start | bytes 1032200 | tf_op jit(solution)/shard_map/ppermute | solution.py:407
  38.8 0.9 collective-permute-start.11
  39.7 0.0 collective-permute-start.12
  39.7 0.9 collective-permute-start.13
  40.7 3.9 %attention.4.refs_1_ = bf16[256,512]{1,0:T(8,128)(2,1)S(1)} custom-call(s32[1]{0:T(128)} %bitcast.5.last_ref, bf16[64,1536]{1,0:T(8,128)(2,1)S(1)} %copy-done.2, bf16[64,1536]{1,0:T(8,128)(2,1)S(1)} %copy-done.2, bf16[64,1536]{1,0:T(8,128)(2,1)S(1)} %copy-done.2, bf16[64,1536]{1,0:T(8,128)(2,1)S(1)} %collective-permute-done.6.refs_3_.refs_4_.refs_5_, ...), custom_call_target="tpu_custom_call" | custom-call | tf_op jit(solution)/shard_map/attention/pallas_call | solution.py:477
  44.6 0.0 copy-start
  44.6 0.0 copy-start.6
  44.6 0.0 copy-start.7
  44.6 2.7 %collective-permute-done.11.refs_3_.refs_4_.refs_5_ = bf16[64,1792]{1,0:T(8,128)(2,1)S(1)} collective-permute-done((bf16[64,1792]{1,0:T(8,128)(2,1)S(1)}, bf16[64,1792]{1,0:T(8,128)(2,1)S(1)}, u32[]{:S(2)}, u32[]{:S(2)}) %collective-permute-start.11) | collective-permute-done | bytes 229408 | tf_op jit(solution)/shard_map/ppermute | solution.py:28
  47.3 4.1 %collective-permute-done.12.refs_6_.refs_7_.refs_8_.refs_5_ = bf16[64,1792]{1,0:T(8,128)(2,1)S(1)} collective-permute-done((bf16[64,1792]{1,0:T(8,128)(2,1)S(1)}, bf16[64,1792]{1,0:T(8,128)(2,1)S(1)}, u32[]{:S(2)}, u32[]{:S(2)}) %collective-permute-start.12) | collective-permute-done | bytes 229408 | tf_op jit(solution)/shard_map/ppermute | solution.py:28
  51.4 0.0 collective-permute-done.9.refs_17_.refs_8_
  51.4 0.0 collective-permute-done.10.refs_14_.refs_5_
  51.4 0.9 collective-permute-start.18
  52.3 1.2 %collective-permute-start.15 = (bf16[112,1536]{1,0:T(8,128)(2,1)S(1)}, bf16[112,1536]{1,0:T(8,128)(2,1)S(1)}, u32[]{:S(2)}, u32[]{:S(2)}) collective-permute-start(bf16[112,1536]{1,0:T(8,128)(2,1)S(1)} %collective-permute-done.5.refs_10_.refs_1_), channel_id=1, source_target_pairs={{0,2},{2,0},{4,6},{6,4},{1,3},{3,1},{5,7},{7,5},{8,10},{10,8},{12,... | collective-permute-start | bytes 1032200 | tf_op jit(solution)/shard_map/ppermute | solution.py:407
  53.5 0.5 collective-permute-start.17
  54.0 0.0 collective-permute-done.14.refs_11_.refs_2_
  54.0 0.0 collective-permute-start.19
  54.0 8.3 %collective-permute-done.18.refs_18_.refs_9_ = bf16[112,1536]{1,0:T(8,128)(2,1)S(1)} collective-permute-done((bf16[112,1536]{1,0:T(8,128)(2,1)S(1)}, bf16[112,1536]{1,0:T(8,128)(2,1)S(1)}, u32[]{:S(2)}, u32[]{:S(2)}) %collective-permute-start.18) | collective-permute-done | bytes 344096 | tf_op jit(solution)/shard_map/ppermute | solution.py:407
  62.2 0.1 collective-permute-start.20
  62.4 3.9 %attention.5.refs_2_ = bf16[256,512]{1,0:T(8,128)(2,1)S(1)} custom-call(s32[1]{0:T(128)} %bitcast.5.last_ref, bf16[64,1792]{1,0:T(8,128)(2,1)S(1)} %copy-done.1, bf16[64,1792]{1,0:T(8,128)(2,1)S(1)} %copy-done.1, bf16[64,1792]{1,0:T(8,128)(2,1)S(1)} %copy-done.1, bf16[64,1792]{1,0:T(8,128)(2,1)S(1)} %collective-permute-done.11.refs_3_.refs_4_.refs_5_, ...), custom_call_target="tpu_custom_call" | custom-call | tf_op jit(solution)/shard_map/attention/pallas_call | solution.py:477
  66.3 5.8 %forward.1 = (bf16[40,1664]{1,0:T(8,128)(2,1)S(1)}, bf16[40,1664]{1,0:T(8,128)(2,1)S(1)}, bf16[40,1664]{1,0:T(8,128)(2,1)S(1)}, bf16[40,1664]{1,0:T(8,128)(2,1)S...) custom-call(s32[2]{0:T(128)S(1)} %copy-done.5, f32[32]{0:T(128)S(1)} %copy-done.7, ...), custom_call_target="tpu_custom_call" | custom-call | tf_op jit(solution)/shard_map/forward/pallas_call | solution.py:509
  72.2 0.5 collective-permute-start.21
  72.7 0.5 collective-permute-start.22
  73.2 1.0 collective-permute-start.23
  74.1 6.2 %backward.1 = bf16[256,1536]{1,0:T(8,128)(2,1)} custom-call(s32[2]{0:T(128)S(1)} %copy-done.5, f32[256,1536]{1,0:T(8,128)S(1)} %get-tuple-element.92.normed_ref, f32[256,128]{1,0:T(8,128)S(1)} %get-tuple-element.93.inv_ref, bf16[256,160]{1,0:T(8,128)(2,1)S(1)} %get-tuple-element.94.dfc_ref, bf16[384,1536]{1,0:T(8,128)(2,1)S(1)} %copy-done, ...), custom_call_target="tpu_custom_call" | custom-call | tf_op jit(solution)/shard_map/backward/pallas_call | solution.py:524
  80.4 0.7 lat_sum.1
  81.1 1.3 %collective-permute-start.24 = (bf16[40,384]{1,0:T(8,128)(2,1)S(1)}, bf16[40,384]{1,0:T(8,128)(2,1)S(1)}, u32[]{:S(2)}, u32[]{:S(2)}) collective-permute-start(bf16[40,384]{1,0:T(8,128)(2,1)S(1)} %get-tuple-element.102), channel_id=1, source_target_pairs={{0,8},{8,0},{16,24},{24,16},{1,9},{9,1},{17,25},{25,17},{2,10},{10... | collective-permute-start | bytes 92168 | tf_op jit(solution)/shard_map/ppermute | solution.py:407
  82.4 1.5 %collective-permute-start.25 = (bf16[40,384]{1,0:T(8,128)(2,1)S(1)}, bf16[40,384]{1,0:T(8,128)(2,1)S(1)}, u32[]{:S(2)}, u32[]{:S(2)}) collective-permute-start(bf16[40,384]{1,0:T(8,128)(2,1)S(1)} %get-tuple-element.103), channel_id=1, source_target_pairs={{0,16},{8,24},{16,0},{24,8},{1,17},{9,25},{17,1},{25,9},{2,18},{10... | collective-permute-start | bytes 92168 | tf_op jit(solution)/shard_map/ppermute | solution.py:407
  83.9 1.6 %collective-permute-start.26 = (bf16[40,384]{1,0:T(8,128)(2,1)S(1)}, bf16[40,384]{1,0:T(8,128)(2,1)S(1)}, u32[]{:S(2)}, u32[]{:S(2)}) collective-permute-start(bf16[40,384]{1,0:T(8,128)(2,1)S(1)} %get-tuple-element.104), channel_id=1, source_target_pairs={{0,24},{8,16},{16,8},{24,0},{1,25},{9,17},{17,9},{25,1},{2,26},{10... | collective-permute-start | bytes 92168 | tf_op jit(solution)/shard_map/ppermute | solution.py:407
  85.5 2.4 %collective-permute-done.25.c = bf16[40,384]{1,0:T(8,128)(2,1)S(1)} collective-permute-done((bf16[40,384]{1,0:T(8,128)(2,1)S(1)}, bf16[40,384]{1,0:T(8,128)(2,1)S(1)}, u32[]{:S(2)}, u32[]{:S(2)}) %collective-permute-start.25) | collective-permute-done | bytes 30752 | tf_op jit(solution)/shard_map/ppermute | solution.py:407
  87.9 1.7 %collective-permute-done.26.d = bf16[40,384]{1,0:T(8,128)(2,1)S(1)} collective-permute-done((bf16[40,384]{1,0:T(8,128)(2,1)S(1)}, bf16[40,384]{1,0:T(8,128)(2,1)S(1)}, u32[]{:S(2)}, u32[]{:S(2)}) %collective-permute-start.26) | collective-permute-done | bytes 30752 | tf_op jit(solution)/shard_map/ppermute | solution.py:407
  89.7 0.1 collective-permute-start.33
  89.8 2.3 %collective-permute-start.32 = (bf16[48,384]{1,0:T(8,128)(2,1)S(1)}, bf16[48,384]{1,0:T(8,128)(2,1)S(1)}, u32[]{:S(2)}, u32[]{:S(2)}) collective-permute-start(bf16[48,384]{1,0:T(8,128)(2,1)S(1)} %dp_sum.1.refs_1_), channel_id=1, source_target_pairs={{0,6},{1,7},{2,4},{3,5},{4,2},{5,3},{6,0},{7,1},{8,14},{9,15},{10,... | collective-permute-start | bytes 110600 | tf_op jit(solution)/shard_map/ppermute | solution.py:560
  92.1 1.0 collective-permute-start.31
  93.1 1.4 %collective-permute-start.30 = (bf16[48,384]{1,0:T(8,128)(2,1)S(1)}, bf16[48,384]{1,0:T(8,128)(2,1)S(1)}, u32[]{:S(2)}, u32[]{:S(2)}) collective-permute-start(bf16[48,384]{1,0:T(8,128)(2,1)S(1)} %dp_sum.1.refs_1_), channel_id=1, source_target_pairs={{0,4},{1,5},{2,6},{3,7},{4,0},{5,1},{6,2},{7,3},{8,12},{9,13},{10,... | collective-permute-start | bytes 110600 | tf_op jit(solution)/shard_map/ppermute | solution.py:560
  94.4 1.2 %collective-permute-start.28 = (bf16[48,384]{1,0:T(8,128)(2,1)S(1)}, bf16[48,384]{1,0:T(8,128)(2,1)S(1)}, u32[]{:S(2)}, u32[]{:S(2)}) collective-permute-start(bf16[48,384]{1,0:T(8,128)(2,1)S(1)} %dp_sum.1.refs_1_), channel_id=1, source_target_pairs={{0,2},{1,3},{2,0},{3,1},{4,6},{5,7},{6,4},{7,5},{8,10},{9,11},{10,... | collective-permute-start | bytes 110600 | tf_op jit(solution)/shard_map/ppermute | solution.py:560
  95.7 0.9 collective-permute-start.27
  96.6 0.4 collective-permute-done.31.refs_6_
  96.9 0.4 collective-permute-done.30.refs_5_
  97.3 0.6 collective-permute-done.29.refs_4_
  97.9 1.7 %collective-permute-done.27.refs_2_ = bf16[48,384]{1,0:T(8,128)(2,1)S(1)} collective-permute-done((bf16[48,384]{1,0:T(8,128)(2,1)S(1)}, bf16[48,384]{1,0:T(8,128)(2,1)S(1)}, u32[]{:S(2)}, u32[]{:S(2)}) %collective-permute-start.27) | collective-permute-done | bytes 36896 | tf_op jit(solution)/shard_map/ppermute | solution.py:560
  99.6 1.3 %join.1 = (f32[160,384]{1,0:T(8,128)}, f32[1,1]{1,0:T(1,128)}) custom-call(s32[2]{0:T(128)S(1)} %copy-done.5, bf16[48,384]{1,0:T(8,128)(2,1)S(1)} %dp_sum.1.refs_1_, bf16[48,384]{1,0:T(8,128)(2,1)S(1)} %collective-permute-done.27.refs_2_, bf16[48,384]{1,0:T(8,128)(2,1)S(1)} %collective-permute-done.28.refs_3_, ...), custom_call_target="tpu_custom_call" | custom-call | tf_op jit(solution)/shard_map/join/pallas_call | solution.py:563
  (37 shorter events, 0.1 us)
Async XLA Ops:
  3.7 17.7 %collective-permute-start = (bf16[112,1536]{1,0:T(8,128)(2,1)}, bf16[112,1536]{1,0:T(8,128)(2,1)S(1)}, u32[]{:S(2)}, u32[]{:S(2)}) collective-permute-start(bf16[112,1536]{1,0:T(8,128)(2,1)} %get-tuple-element.55), channel_id=1, source_target_pairs={{0,8},{8,16},{16,24},{24,0},{1,9},{9,17},{17,25},{25,1},{2,10},{10... | collective-permute-start | bytes 1032200 | tf_op jit(solution)/shard_map/ppermute | solution.py:28
  11.4 29.2 %copy-start.2 = (bf16[64,1536]{1,0:T(8,128)(2,1)S(1)}, bf16[64,1536]{1,0:T(8,128)(2,1)}, u32[]{:S(2)}) copy-start(bf16[64,1536]{1,0:T(8,128)(2,1)} %get-tuple-element.71.refs_0_.refs_1_.refs_2_) | copy-start | bytes 589828
  11.5 8.1 %collective-permute-start.1 = (bf16[64,1536]{1,0:T(8,128)(2,1)}, bf16[64,1536]{1,0:T(8,128)(2,1)S(1)}, u32[]{:S(2)}, u32[]{:S(2)}) collective-permute-start(bf16[64,1536]{1,0:T(8,128)(2,1)} %get-tuple-element.57), channel_id=1, source_target_pairs={{0,1},{1,0},{2,3},{3,2},{4,5},{5,4},{6,7},{7,6},{8,9},{9,8},{10,11... | collective-permute-start | bytes 589832 | tf_op jit(solution)/shard_map/ppermute | solution.py:28
  13.0 6.6 %collective-permute-start.2 = (bf16[64,1536]{1,0:T(8,128)(2,1)}, bf16[64,1536]{1,0:T(8,128)(2,1)S(1)}, u32[]{:S(2)}, u32[]{:S(2)}) collective-permute-start(bf16[64,1536]{1,0:T(8,128)(2,1)} %get-tuple-element.58), channel_id=1, source_target_pairs={{0,6},{2,0},{4,2},{6,4},{1,7},{3,1},{5,3},{7,5},{8,14},{10,8},{12,... | collective-permute-start | bytes 589832 | tf_op jit(solution)/shard_map/ppermute | solution.py:28
  13.4 8.0 %collective-permute-start.3 = (bf16[64,1536]{1,0:T(8,128)(2,1)}, bf16[64,1536]{1,0:T(8,128)(2,1)S(1)}, u32[]{:S(2)}, u32[]{:S(2)}) collective-permute-start(bf16[64,1536]{1,0:T(8,128)(2,1)} %get-tuple-element.59), channel_id=1, source_target_pairs={{0,7},{1,6},{2,1},{3,0},{4,3},{5,2},{6,5},{7,4},{8,15},{9,14},{10,... | collective-permute-start | bytes 589832 | tf_op jit(solution)/shard_map/ppermute | solution.py:468
  21.4 14.0 %collective-permute-start.5 = (bf16[112,1536]{1,0:T(8,128)(2,1)S(1)}, bf16[112,1536]{1,0:T(8,128)(2,1)S(1)}, u32[]{:S(2)}, u32[]{:S(2)}) collective-permute-start(bf16[112,1536]{1,0:T(8,128)(2,1)S(1)} %collective-permute-done.refs_9_.refs_0_), channel_id=1, source_target_pairs={{0,4},{2,6},{4,0},{6,2},{1,5},{3,7},{5,1},{7,3},{8,12},{10,14},{12... | collective-permute-start | bytes 1032200 | tf_op jit(solution)/shard_map/ppermute | solution.py:407
  22.9 12.5 %collective-permute-start.4 = (bf16[112,1536]{1,0:T(8,128)(2,1)S(1)}, bf16[112,1536]{1,0:T(8,128)(2,1)S(1)}, u32[]{:S(2)}, u32[]{:S(2)}) collective-permute-start(bf16[112,1536]{1,0:T(8,128)(2,1)S(1)} %collective-permute-done.refs_9_.refs_0_), channel_id=1, source_target_pairs={{0,8},{8,16},{16,24},{24,0},{1,9},{9,17},{17,25},{25,1},{2,10},{10... | collective-permute-start | bytes 1032200 | tf_op jit(solution)/shard_map/ppermute | solution.py:28
  24.5 8.0 %collective-permute-start.6 = (bf16[64,1536]{1,0:T(8,128)(2,1)}, bf16[64,1536]{1,0:T(8,128)(2,1)S(1)}, u32[]{:S(2)}, u32[]{:S(2)}) collective-permute-start(bf16[64,1536]{1,0:T(8,128)(2,1)} %get-tuple-element.66), channel_id=1, source_target_pairs={{0,1},{1,0},{2,3},{3,2},{4,5},{5,4},{6,7},{7,6},{8,9},{9,8},{10,11... | collective-permute-start | bytes 589832 | tf_op jit(solution)/shard_map/ppermute | solution.py:28
  25.4 10.0 %collective-permute-start.7 = (bf16[64,1536]{1,0:T(8,128)(2,1)}, bf16[64,1536]{1,0:T(8,128)(2,1)S(1)}, u32[]{:S(2)}, u32[]{:S(2)}) collective-permute-start(bf16[64,1536]{1,0:T(8,128)(2,1)} %get-tuple-element.67), channel_id=1, source_target_pairs={{0,6},{2,0},{4,2},{6,4},{1,7},{3,1},{5,3},{7,5},{8,14},{10,8},{12,... | collective-permute-start | bytes 589832 | tf_op jit(solution)/shard_map/ppermute | solution.py:28
  26.9 8.5 %collective-permute-start.8 = (bf16[64,1536]{1,0:T(8,128)(2,1)}, bf16[64,1536]{1,0:T(8,128)(2,1)S(1)}, u32[]{:S(2)}, u32[]{:S(2)}) collective-permute-start(bf16[64,1536]{1,0:T(8,128)(2,1)} %get-tuple-element.68), channel_id=1, source_target_pairs={{0,7},{1,6},{2,1},{3,0},{4,3},{5,2},{6,5},{7,4},{8,15},{9,14},{10,... | collective-permute-start | bytes 589832 | tf_op jit(solution)/shard_map/ppermute | solution.py:468
  26.9 0.9 copy-start.3
  27.9 10.9 %copy-start.10 = (bf16[64,1792]{1,0:T(8,128)(2,1)S(1)}, bf16[64,1792]{1,0:T(8,128)(2,1)}, u32[]{:S(2)}) copy-start(bf16[64,1792]{1,0:T(8,128)(2,1)} %get-tuple-element.76) | copy-start | bytes 688132
  27.9 11.8 %copy-start.9 = (bf16[64,1792]{1,0:T(8,128)(2,1)S(1)}, bf16[64,1792]{1,0:T(8,128)(2,1)}, u32[]{:S(2)}) copy-start(bf16[64,1792]{1,0:T(8,128)(2,1)} %get-tuple-element.77) | copy-start | bytes 688132
  27.9 11.8 %copy-start.8 = (bf16[64,1792]{1,0:T(8,128)(2,1)S(1)}, bf16[64,1792]{1,0:T(8,128)(2,1)}, u32[]{:S(2)}) copy-start(bf16[64,1792]{1,0:T(8,128)(2,1)} %get-tuple-element.78) | copy-start | bytes 688132
  31.8 30.6 %copy-start.1 = (bf16[64,1792]{1,0:T(8,128)(2,1)S(1)}, bf16[64,1792]{1,0:T(8,128)(2,1)}, u32[]{:S(2)}) copy-start(bf16[64,1792]{1,0:T(8,128)(2,1)} %get-tuple-element.80.refs_0_.refs_1_.refs_2_.refs_3_) | copy-start | bytes 688132
  35.4 15.9 %collective-permute-start.9 = (bf16[112,1536]{1,0:T(8,128)(2,1)S(1)}, bf16[112,1536]{1,0:T(8,128)(2,1)S(1)}, u32[]{:S(2)}, u32[]{:S(2)}) collective-permute-start(bf16[112,1536]{1,0:T(8,128)(2,1)S(1)} %collective-permute-done.4.refs_13_.refs_4_), channel_id=1, source_target_pairs={{0,8},{8,16},{16,24},{24,0},{1,9},{9,17},{17,25},{25,1},{2,10},{10... | collective-permute-start | bytes 1032200 | tf_op jit(solution)/shard_map/ppermute | solution.py:28
  37.1 14.3 %collective-permute-start.10 = (bf16[112,1536]{1,0:T(8,128)(2,1)S(1)}, bf16[112,1536]{1,0:T(8,128)(2,1)S(1)}, u32[]{:S(2)}, u32[]{:S(2)}) collective-permute-start(bf16[112,1536]{1,0:T(8,128)(2,1)S(1)} %collective-permute-done.4.refs_13_.refs_4_), channel_id=1, source_target_pairs={{0,4},{2,6},{4,0},{6,2},{1,5},{3,7},{5,1},{7,3},{8,12},{10,14},{12... | collective-permute-start | bytes 1032200 | tf_op jit(solution)/shard_map/ppermute | solution.py:407
  38.8 8.5 %collective-permute-start.11 = (bf16[64,1792]{1,0:T(8,128)(2,1)S(1)}, bf16[64,1792]{1,0:T(8,128)(2,1)S(1)}, u32[]{:S(2)}, u32[]{:S(2)}) collective-permute-start(bf16[64,1792]{1,0:T(8,128)(2,1)S(1)} %copy-done.10), channel_id=1, source_target_pairs={{0,1},{1,0},{2,3},{3,2},{4,5},{5,4},{6,7},{7,6},{8,9},{9,8},{10,11... | collective-permute-start | bytes 688136 | tf_op jit(solution)/shard_map/ppermute | solution.py:28
  39.7 11.6 %collective-permute-start.12 = (bf16[64,1792]{1,0:T(8,128)(2,1)S(1)}, bf16[64,1792]{1,0:T(8,128)(2,1)S(1)}, u32[]{:S(2)}, u32[]{:S(2)}) collective-permute-start(bf16[64,1792]{1,0:T(8,128)(2,1)S(1)} %copy-done.9), channel_id=1, source_target_pairs={{0,6},{2,0},{4,2},{6,4},{1,7},{3,1},{5,3},{7,5},{8,14},{10,8},{12,... | collective-permute-start | bytes 688136 | tf_op jit(solution)/shard_map/ppermute | solution.py:28
  39.7 11.6 %collective-permute-start.13 = (bf16[64,1792]{1,0:T(8,128)(2,1)S(1)}, bf16[64,1792]{1,0:T(8,128)(2,1)S(1)}, u32[]{:S(2)}, u32[]{:S(2)}) collective-permute-start(bf16[64,1792]{1,0:T(8,128)(2,1)S(1)} %copy-done.8), channel_id=1, source_target_pairs={{0,7},{1,6},{2,1},{3,0},{4,3},{5,2},{6,5},{7,4},{8,15},{9,14},{10,... | collective-permute-start | bytes 688136 | tf_op jit(solution)/shard_map/ppermute | solution.py:468
  44.6 21.7 %copy-start = (bf16[384,1536]{1,0:T(8,128)(2,1)S(1)}, bf16[384,1536]{1,0:T(8,128)(2,1)}, u32[]{:S(2)}) copy-start(bf16[384,1536]{1,0:T(8,128)(2,1)} %own_w.1) | copy-start | bytes 3538948
  44.6 21.7 %copy-start.4 = (bf16[256,384]{1,0:T(8,128)(2,1)S(1)}, bf16[256,384]{1,0:T(8,128)(2,1)}, u32[]{:S(2)}) copy-start(bf16[256,384]{1,0:T(8,128)(2,1)} %get-tuple-element.84.refs_8_.own_ug) | copy-start | bytes 589828
  44.6 21.7 %copy-start.5 = (s32[2]{0:T(128)S(1)}, s32[2]{0:T(128)}, u32[]{:S(2)}) copy-start(s32[2]{0:T(128)} %pad_add_fusion.place_ref.refs_0_) | copy-start | bytes 28
  44.6 21.7 %copy-start.6 = (f32[5]{0:T(128)S(1)}, f32[5]{0:T(128)}, u32[]{:S(2)}) copy-start(f32[5]{0:T(128)} %var_ref.1) | copy-start | bytes 64
  44.6 21.7 %copy-start.7 = (f32[32]{0:T(128)S(1)}, f32[32]{0:T(128)}, u32[]{:S(2)}) copy-start(f32[32]{0:T(128)} %constant.13.clone.lat_ref) | copy-start | bytes 388
  47.3 6.7 %collective-permute-start.14 = (bf16[112,1536]{1,0:T(8,128)(2,1)S(1)}, bf16[112,1536]{1,0:T(8,128)(2,1)S(1)}, u32[]{:S(2)}, u32[]{:S(2)}) collective-permute-start(bf16[112,1536]{1,0:T(8,128)(2,1)S(1)} %collective-permute-done.refs_9_.refs_0_), channel_id=1, source_target_pairs={{0,2},{2,0},{4,6},{6,4},{1,3},{3,1},{5,7},{7,5},{8,10},{10,8},{12,... | collective-permute-start | bytes 1032200 | tf_op jit(solution)/shard_map/ppermute | solution.py:407
  51.4 10.9 %collective-permute-start.18 = (bf16[112,1536]{1,0:T(8,128)(2,1)S(1)}, bf16[112,1536]{1,0:T(8,128)(2,1)S(1)}, u32[]{:S(2)}, u32[]{:S(2)}) collective-permute-start(bf16[112,1536]{1,0:T(8,128)(2,1)S(1)} %collective-permute-done.9.refs_17_.refs_8_), channel_id=1, source_target_pairs={{0,4},{2,6},{4,0},{6,2},{1,5},{3,7},{5,1},{7,3},{8,12},{10,14},{12... | collective-permute-start | bytes 1032200 | tf_op jit(solution)/shard_map/ppermute | solution.py:407
  52.3 14.0 %collective-permute-start.15 = (bf16[112,1536]{1,0:T(8,128)(2,1)S(1)}, bf16[112,1536]{1,0:T(8,128)(2,1)S(1)}, u32[]{:S(2)}, u32[]{:S(2)}) collective-permute-start(bf16[112,1536]{1,0:T(8,128)(2,1)S(1)} %collective-permute-done.5.refs_10_.refs_1_), channel_id=1, source_target_pairs={{0,2},{2,0},{4,6},{6,4},{1,3},{3,1},{5,7},{7,5},{8,10},{10,8},{12,... | collective-permute-start | bytes 1032200 | tf_op jit(solution)/shard_map/ppermute | solution.py:407
  53.5 12.8 %collective-permute-start.16 = (bf16[112,1536]{1,0:T(8,128)(2,1)S(1)}, bf16[112,1536]{1,0:T(8,128)(2,1)S(1)}, u32[]{:S(2)}, u32[]{:S(2)}) collective-permute-start(bf16[112,1536]{1,0:T(8,128)(2,1)S(1)} %collective-permute-done.4.refs_13_.refs_4_), channel_id=1, source_target_pairs={{0,2},{2,0},{4,6},{6,4},{1,3},{3,1},{5,7},{7,5},{8,10},{10,8},{12,... | collective-permute-start | bytes 1032200 | tf_op jit(solution)/shard_map/ppermute | solution.py:407
  53.5 12.8 %collective-permute-start.17 = (bf16[112,1536]{1,0:T(8,128)(2,1)S(1)}, bf16[112,1536]{1,0:T(8,128)(2,1)S(1)}, u32[]{:S(2)}, u32[]{:S(2)}) collective-permute-start(bf16[112,1536]{1,0:T(8,128)(2,1)S(1)} %collective-permute-done.10.refs_14_.refs_5_), channel_id=1, source_target_pairs={{0,2},{2,0},{4,6},{6,4},{1,3},{3,1},{5,7},{7,5},{8,10},{10,8},{12,... | collective-permute-start | bytes 1032200 | tf_op jit(solution)/shard_map/ppermute | solution.py:407
  54.0 12.3 %collective-permute-start.19 = (bf16[112,1536]{1,0:T(8,128)(2,1)S(1)}, bf16[112,1536]{1,0:T(8,128)(2,1)S(1)}, u32[]{:S(2)}, u32[]{:S(2)}) collective-permute-start(bf16[112,1536]{1,0:T(8,128)(2,1)S(1)} %collective-permute-done.9.refs_17_.refs_8_), channel_id=1, source_target_pairs={{0,2},{2,0},{4,6},{6,4},{1,3},{3,1},{5,7},{7,5},{8,10},{10,8},{12,... | collective-permute-start | bytes 1032200 | tf_op jit(solution)/shard_map/ppermute | solution.py:407
  62.2 4.0 %collective-permute-start.20 = (bf16[112,1536]{1,0:T(8,128)(2,1)S(1)}, bf16[112,1536]{1,0:T(8,128)(2,1)S(1)}, u32[]{:S(2)}, u32[]{:S(2)}) collective-permute-start(bf16[112,1536]{1,0:T(8,128)(2,1)S(1)} %collective-permute-done.18.refs_18_.refs_9_), channel_id=1, source_target_pairs={{0,2},{2,0},{4,6},{6,4},{1,3},{3,1},{5,7},{7,5},{8,10},{10,8},{12,... | collective-permute-start | bytes 1032200 | tf_op jit(solution)/shard_map/ppermute | solution.py:407
  72.2 8.2 %collective-permute-start.21 = (bf16[40,1664]{1,0:T(8,128)(2,1)S(1)}, bf16[40,1664]{1,0:T(8,128)(2,1)S(1)}, u32[]{:S(2)}, u32[]{:S(2)}) collective-permute-start(bf16[40,1664]{1,0:T(8,128)(2,1)S(1)} %get-tuple-element.89), channel_id=1, source_target_pairs={{0,2},{2,0},{4,6},{6,4},{1,3},{3,1},{5,7},{7,5},{8,10},{10,8},{12,... | collective-permute-start | bytes 399368 | tf_op jit(solution)/shard_map/ppermute | solution.py:407
  72.7 7.7 %collective-permute-start.22 = (bf16[40,1664]{1,0:T(8,128)(2,1)S(1)}, bf16[40,1664]{1,0:T(8,128)(2,1)S(1)}, u32[]{:S(2)}, u32[]{:S(2)}) collective-permute-start(bf16[40,1664]{1,0:T(8,128)(2,1)S(1)} %get-tuple-element.90), channel_id=1, source_target_pairs={{0,4},{2,6},{4,0},{6,2},{1,5},{3,7},{5,1},{7,3},{8,12},{10,14},{12... | collective-permute-start | bytes 399368 | tf_op jit(solution)/shard_map/ppermute | solution.py:407
  73.2 7.2 %collective-permute-start.23 = (bf16[40,1664]{1,0:T(8,128)(2,1)S(1)}, bf16[40,1664]{1,0:T(8,128)(2,1)S(1)}, u32[]{:S(2)}, u32[]{:S(2)}) collective-permute-start(bf16[40,1664]{1,0:T(8,128)(2,1)S(1)} %get-tuple-element.91), channel_id=1, source_target_pairs={{0,6},{2,4},{4,2},{6,0},{1,7},{3,5},{5,3},{7,1},{8,14},{10,12},{12... | collective-permute-start | bytes 399368 | tf_op jit(solution)/shard_map/ppermute | solution.py:407
  81.1 4.4 %collective-permute-start.24 = (bf16[40,384]{1,0:T(8,128)(2,1)S(1)}, bf16[40,384]{1,0:T(8,128)(2,1)S(1)}, u32[]{:S(2)}, u32[]{:S(2)}) collective-permute-start(bf16[40,384]{1,0:T(8,128)(2,1)S(1)} %get-tuple-element.102), channel_id=1, source_target_pairs={{0,8},{8,0},{16,24},{24,16},{1,9},{9,1},{17,25},{25,17},{2,10},{10... | collective-permute-start | bytes 92168 | tf_op jit(solution)/shard_map/ppermute | solution.py:407
  82.4 5.5 %collective-permute-start.25 = (bf16[40,384]{1,0:T(8,128)(2,1)S(1)}, bf16[40,384]{1,0:T(8,128)(2,1)S(1)}, u32[]{:S(2)}, u32[]{:S(2)}) collective-permute-start(bf16[40,384]{1,0:T(8,128)(2,1)S(1)} %get-tuple-element.103), channel_id=1, source_target_pairs={{0,16},{8,24},{16,0},{24,8},{1,17},{9,25},{17,1},{25,9},{2,18},{10... | collective-permute-start | bytes 92168 | tf_op jit(solution)/shard_map/ppermute | solution.py:407
  83.9 5.7 %collective-permute-start.26 = (bf16[40,384]{1,0:T(8,128)(2,1)S(1)}, bf16[40,384]{1,0:T(8,128)(2,1)S(1)}, u32[]{:S(2)}, u32[]{:S(2)}) collective-permute-start(bf16[40,384]{1,0:T(8,128)(2,1)S(1)} %get-tuple-element.104), channel_id=1, source_target_pairs={{0,24},{8,16},{16,8},{24,0},{1,25},{9,17},{17,9},{25,1},{2,26},{10... | collective-permute-start | bytes 92168 | tf_op jit(solution)/shard_map/ppermute | solution.py:407
  89.7 4.7 %collective-permute-start.33 = (bf16[48,384]{1,0:T(8,128)(2,1)S(1)}, bf16[48,384]{1,0:T(8,128)(2,1)S(1)}, u32[]{:S(2)}, u32[]{:S(2)}) collective-permute-start(bf16[48,384]{1,0:T(8,128)(2,1)S(1)} %dp_sum.1.refs_1_), channel_id=1, source_target_pairs={{0,7},{1,6},{2,5},{3,4},{4,3},{5,2},{6,1},{7,0},{8,15},{9,14},{10,... | collective-permute-start | bytes 110600 | tf_op jit(solution)/shard_map/ppermute | solution.py:560
  89.8 5.9 %collective-permute-start.32 = (bf16[48,384]{1,0:T(8,128)(2,1)S(1)}, bf16[48,384]{1,0:T(8,128)(2,1)S(1)}, u32[]{:S(2)}, u32[]{:S(2)}) collective-permute-start(bf16[48,384]{1,0:T(8,128)(2,1)S(1)} %dp_sum.1.refs_1_), channel_id=1, source_target_pairs={{0,6},{1,7},{2,4},{3,5},{4,2},{5,3},{6,0},{7,1},{8,14},{9,15},{10,... | collective-permute-start | bytes 110600 | tf_op jit(solution)/shard_map/ppermute | solution.py:560
  92.1 4.9 %collective-permute-start.31 = (bf16[48,384]{1,0:T(8,128)(2,1)S(1)}, bf16[48,384]{1,0:T(8,128)(2,1)S(1)}, u32[]{:S(2)}, u32[]{:S(2)}) collective-permute-start(bf16[48,384]{1,0:T(8,128)(2,1)S(1)} %dp_sum.1.refs_1_), channel_id=1, source_target_pairs={{0,5},{1,4},{2,7},{3,6},{4,1},{5,0},{6,3},{7,2},{8,13},{9,12},{10,... | collective-permute-start | bytes 110600 | tf_op jit(solution)/shard_map/ppermute | solution.py:560
  93.1 4.3 %collective-permute-start.30 = (bf16[48,384]{1,0:T(8,128)(2,1)S(1)}, bf16[48,384]{1,0:T(8,128)(2,1)S(1)}, u32[]{:S(2)}, u32[]{:S(2)}) collective-permute-start(bf16[48,384]{1,0:T(8,128)(2,1)S(1)} %dp_sum.1.refs_1_), channel_id=1, source_target_pairs={{0,4},{1,5},{2,6},{3,7},{4,0},{5,1},{6,2},{7,3},{8,12},{9,13},{10,... | collective-permute-start | bytes 110600 | tf_op jit(solution)/shard_map/ppermute | solution.py:560
  94.4 3.5 %collective-permute-start.29 = (bf16[48,384]{1,0:T(8,128)(2,1)S(1)}, bf16[48,384]{1,0:T(8,128)(2,1)S(1)}, u32[]{:S(2)}, u32[]{:S(2)}) collective-permute-start(bf16[48,384]{1,0:T(8,128)(2,1)S(1)} %dp_sum.1.refs_1_), channel_id=1, source_target_pairs={{0,3},{1,2},{2,1},{3,0},{4,7},{5,6},{6,5},{7,4},{8,11},{9,10},{10,... | collective-permute-start | bytes 110600 | tf_op jit(solution)/shard_map/ppermute | solution.py:560
  94.4 3.5 %collective-permute-start.28 = (bf16[48,384]{1,0:T(8,128)(2,1)S(1)}, bf16[48,384]{1,0:T(8,128)(2,1)S(1)}, u32[]{:S(2)}, u32[]{:S(2)}) collective-permute-start(bf16[48,384]{1,0:T(8,128)(2,1)S(1)} %dp_sum.1.refs_1_), channel_id=1, source_target_pairs={{0,2},{1,3},{2,0},{3,1},{4,6},{5,7},{6,4},{7,5},{8,10},{9,11},{10,... | collective-permute-start | bytes 110600 | tf_op jit(solution)/shard_map/ppermute | solution.py:560
  95.7 4.0 %collective-permute-start.27 = (bf16[48,384]{1,0:T(8,128)(2,1)S(1)}, bf16[48,384]{1,0:T(8,128)(2,1)S(1)}, u32[]{:S(2)}, u32[]{:S(2)}) collective-permute-start(bf16[48,384]{1,0:T(8,128)(2,1)S(1)} %dp_sum.1.refs_1_), channel_id=1, source_target_pairs={{0,1},{1,0},{2,3},{3,2},{4,5},{5,4},{6,7},{7,6},{8,9},{9,8},{10,11... | collective-permute-start | bytes 110600 | tf_op jit(solution)/shard_map/ppermute | solution.py:560

commit v4 on v3

--- a/solution.py
+++ b/solution.py
@@ -1,3 +1,4 @@
+import functools
 import math
 
 import jax
@@ -15,7 +16,8 @@
 F32 = jnp.float32
 EXTRA = 256
 UGROWS = 256
-CHUNKS = 3
+CHUNKS = (1, 4, 4, 3)
+WITH_EXTRA = 2
 PIECES = 12
 VMEM = pl.BlockSpec(memory_space=pltpu.VMEM)
 SMEM = pl.BlockSpec(memory_space=pltpu.SMEM)
@@ -133,7 +135,49 @@
     return lax.broadcasted_iota(jnp.int32, shape, dim)
 
 
-def payload_kernel(place_ref, w_ref, unpatch_ref, gain_ref, ug_ref, payload_ref, u_in, sems):
+def chunk_copies(x_ref, x_in, groups, sems, at):
+    width = x_ref.shape[-1] // 3
+    unit = width // sum(CHUNKS)
+    copies = []
+    to = 0
+    for g in groups:
+        part = unit * CHUNKS[g]
+        base = unit * sum(CHUNKS[:g])
+        for i in range(3):
+            source = (slice(None),) * 3 + (pl.ds(i * width + base, part),)
+            target = (slice(None),) * 3 + (pl.ds(to, part),)
+            sem = sems.at[at + len(copies)]
+            copies.append(
+                (to, part, pltpu.make_async_copy(x_ref.at[source], x_in.at[target], sem))
+            )
+            to += part
+    return copies
+
+
+def quadrant_pick(count):
+    place = iota((count, count), 0)
+    quad, rest = place // (count // 4), place % (count // 4)
+    row = (rest // 4) % 4 + jnp.where(quad < 2, 4, 0)
+    col = rest % 4 + jnp.where(quad % 2 == 0, 4, 0)
+    source = (rest // 16) * 64 + row * 8 + col
+    return (iota((count, count), 1) == source).astype(F32).astype(BF)
+
+
+def pack_chunk(pick, x_in, copies, outs):
+    count = pick.shape[0]
+    quarter = count // 4
+    for i, (at, part, copy) in enumerate(copies):
+        copy.wait()
+        tokens = x_in[:, :, :, at : at + part].reshape(count, part)
+        out = jnp.dot(pick, tokens, preferred_element_type=F32).astype(BF)
+        for q in range(4):
+            outs[q][:, i * part : (i + 1) * part] = out[q * quarter : (q + 1) * quarter]
+
+
+def lead_kernel(
+    place_ref, w_ref, unpatch_ref, gain_ref, x_ref, ug_ref, payload_ref, o0, o1, o2, o3,
+    u_in, x_in, sems,
+):
     part = place_ref[1]
     rows, width = w_ref.shape
     qr = rows // 4
@@ -143,8 +187,12 @@
         w_ref.at[pl.ds(start, qr), :], payload_ref.at[pl.ds(0, qr), :], sems.at[0]
     )
     u_copy = pltpu.make_async_copy(unpatch_ref, u_in, sems.at[1])
+    u_copy.start()
     w_copy.start()
-    u_copy.start()
+    copies = chunk_copies(x_ref, x_in, (0,), sems, 2)
+    for _, _, c in copies:
+        c.start()
+    pick = quadrant_pick(x_ref.shape[0] * 64)
     gain = jnp.broadcast_to(gain_ref[...].astype(F32).reshape(1, rows), (16, rows)).astype(BF)
     ug_ref[pl.ds(span, 16), :] = gain
     ug_ref[pl.ds(span + 16, UGROWS - span - 16), :] = jnp.zeros((UGROWS - span - 16, rows), BF)
@@ -153,45 +201,29 @@
     for j in range(4):
         at = pl.multiple_of((4 * part + j) * 16, 16)
         payload_ref[pl.ds(qr, 16), pl.ds(j * rows, rows)] = ug_ref[pl.ds(at, 16), :]
+    pack_chunk(pick, x_in, copies, (o0, o1, o2, o3))
     w_copy.wait()
 
 
 def pack_kernel(x_ref, t_ref, valid_ref, *refs):
-    outs = refs[: 4 * CHUNKS]
-    x_in, t_in, v_in, sems = refs[4 * CHUNKS :]
-    width = x_ref.shape[-1] // 3
+    later = range(1, len(CHUNKS))
+    outs = refs[: 4 * len(later)]
+    x_in, t_in, v_in, sems = refs[4 * len(later) :]
     span = t_ref.shape[-1]
     count = x_ref.shape[0] * 64
-    part = width // CHUNKS
-    copies = []
-    for g in range(CHUNKS):
-        for i in range(3):
-            lanes = pl.ds(i * width + g * part, part)
-            at = (slice(None), slice(None), slice(None), lanes)
-            copies.append(
-                pltpu.make_async_copy(x_ref.at[at], x_in.at[at], sems.at[3 * g + i])
-            )
-    copies.append(pltpu.make_async_copy(t_ref, t_in, sems.at[3 * CHUNKS]))
-    copies.append(pltpu.make_async_copy(valid_ref, v_in, sems.at[3 * CHUNKS + 1]))
-    for c in copies:
+    quarter = count // 4
+    copies = chunk_copies(x_ref, x_in, later, sems, 2)
+    t_copy = pltpu.make_async_copy(t_ref, t_in, sems.at[0])
+    v_copy = pltpu.make_async_copy(valid_ref, v_in, sems.at[1])
+    for _, _, c in copies:
         c.start()
-    place = iota((count, count), 0)
-    quad, rest = place // (count // 4), place % (count // 4)
-    row = (rest // 4) % 4 + jnp.where(quad < 2, 4, 0)
-    col = rest % 4 + jnp.where(quad % 2 == 0, 4, 0)
-    source = (rest // 16) * 64 + row * 8 + col
-    pick = (iota((count, count), 1) == source).astype(F32).astype(BF)
-    quarter = count // 4
-    for g in range(CHUNKS):
-        for i in range(3):
-            copies[3 * g + i].wait()
-            at = i * width + g * part
-            tokens = x_in[:, :, :, at : at + part].reshape(count, part)
-            out = jnp.dot(pick, tokens, preferred_element_type=F32).astype(BF)
-            for q in range(4):
-                outs[4 * g + q][:, i * part : (i + 1) * part] = out[q * quarter : (q + 1) * quarter]
-    copies[-2].wait()
-    copies[-1].wait()
+    t_copy.start()
+    v_copy.start()
+    pick = quadrant_pick(count)
+    for n in range(len(later)):
+        pack_chunk(pick, x_in, copies[3 * n : 3 * n + 3], outs[4 * n : 4 * n + 4])
+    t_copy.wait()
+    v_copy.wait()
     goal = jnp.dot(pick, t_in[...].reshape(count, span), preferred_element_type=F32)
     token = iota((count, 8), 0)
     row_hot = ((token // 8) % 8 == iota((count, 8), 1)).astype(F32)
@@ -202,7 +234,8 @@
     column = jnp.dot(pick, spread, preferred_element_type=F32)
     extra = jnp.concatenate([goal, column[:, : EXTRA - span]], axis=1).astype(BF)
     for q in range(4):
-        outs[4 * CHUNKS - 4 + q][:, 3 * part :] = extra[q * quarter : (q + 1) * quarter]
+        ref = outs[4 * (WITH_EXTRA - 1) + q]
+        ref[:, ref.shape[1] - EXTRA :] = extra[q * quarter : (q + 1) * quarter]
 
 
 def attention_kernel(last_ref, *refs):
@@ -277,7 +310,7 @@
 
 
 def forward_kernel(place_ref, lat_ref, var_ref, *refs):
-    ctx_refs, refs = refs[:CHUNKS], refs[CHUNKS:]
+    ctx_refs, refs = refs[: len(CHUNKS)], refs[len(CHUNKS) :]
     extras, refs = refs[:4], refs[4:]
     (own_w, own_ug), refs = refs[:2], refs[2:]
     pieces, refs = refs[:PIECES], refs[PIECES:]
@@ -305,11 +338,13 @@
     weight = lat_w * valid * var_w
     for c in w_copies:
         c.wait()
-    part = width // CHUNKS
-    mixed = jnp.dot(ctx_refs[0][...], w_all[0:part, :], preferred_element_type=F32)
-    for g in range(1, CHUNKS):
-        rows_g = w_all[g * part : (g + 1) * part, :]
-        mixed += jnp.dot(ctx_refs[g][...], rows_g, preferred_element_type=F32)
+    at = 0
+    mixed = None
+    for ref in ctx_refs:
+        part = ref.shape[1]
+        term_g = jnp.dot(ref[...], w_all[at : at + part, :], preferred_element_type=F32)
+        mixed = term_g if mixed is None else mixed + term_g
+        at += part
     centre = jnp.mean(mixed, axis=-1, keepdims=True)
     off = mixed - centre
     inv = lax.rsqrt(jnp.mean(off * off, axis=-1, keepdims=True) + 1e-05)
@@ -418,7 +453,6 @@
     span = unpatch_matrix.shape[1]
     tokens = levels * 64
     quarter = tokens // 4
-    part = width // CHUNKS
     lat_place = lax.axis_index("lat")
     place = jnp.stack([lax.axis_index("dp"), lat_place]).astype(jnp.int32)
     last = (lat_place == lat - 1).astype(jnp.int32).reshape(1)
@@ -428,49 +462,53 @@
     lat_table = jnp.asarray(np.roll(cosine / cosine.mean(), -4), F32)
     barrier = lax.optimization_barrier
 
-    ug, payload = pl.pallas_call(
-        payload_kernel,
-        out_shape=[shape((UGROWS, rows), BF), shape((rows // 4 + 16, width), BF)],
-        in_specs=[SMEM, HBM, HBM, VMEM],
-        out_specs=[VMEM] * 2,
-        scratch_shapes=[pltpu.VMEM((span, rows), BF), pltpu.SemaphoreType.DMA((2,))],
+    x = projected.reshape(levels, 8, 8, 3 * width)
+    parts_of = [width // sum(CHUNKS) * n for n in CHUNKS]
+    widths = [3 * part + (EXTRA if g == WITH_EXTRA else 0) for g, part in enumerate(parts_of)]
+    ug, payload, *packed = pl.pallas_call(
+        lead_kernel,
+        out_shape=[shape((UGROWS, rows), BF), shape((rows // 4 + 16, width), BF)]
+        + [shape((quarter, widths[0]), BF)] * 4,
+        in_specs=[SMEM, HBM, HBM, VMEM, HBM],
+        out_specs=[VMEM] * 6,
+        scratch_shapes=[
+            pltpu.VMEM((span, rows), BF),
+            pltpu.VMEM((levels, 8, 8, widths[0]), BF),
+            pltpu.SemaphoreType.DMA((5,)),
+        ],
         compiler_params=params(62),
-        name="payload",
-    )(place, w_out, unpatch_matrix.T, norm_gain)
+        name="lead",
+    )(place, w_out, unpatch_matrix.T, norm_gain, x)
     ring1 = from_behind(payload, "dp", 1)
-
-    widths = [3 * part] * (CHUNKS - 1) + [3 * part + EXTRA]
-    packed = pl.pallas_call(
+    later = sum(parts_of[1:])
+    packed += pl.pallas_call(
         pack_kernel,
-        out_shape=[shape((quarter, w), BF) for w in widths for _ in range(4)],
+        out_shape=[shape((quarter, w), BF) for w in widths[1:] for _ in range(4)],
         in_specs=[HBM] * 3,
-        out_specs=[VMEM] * (4 * CHUNKS),
+        out_specs=[VMEM] * (4 * len(CHUNKS) - 4),
         scratch_shapes=[
-            pltpu.VMEM((levels, 8, 8, 3 * width), BF),
+            pltpu.VMEM((levels, 8, 8, 3 * later), BF),
             pltpu.VMEM((levels, 8, 8, span), BF),
             pltpu.VMEM((8, 8), jnp.int32),
-            pltpu.SemaphoreType.DMA((3 * CHUNKS + 2,)),
+            pltpu.SemaphoreType.DMA((3 * len(CHUNKS) - 1,)),
         ],
-        compiler_params=params(60),
+        compiler_params=params(62),
         name="pack",
-    )(projected.reshape(levels, 8, 8, 3 * width), targets.reshape(levels, 8, 8, span), valid_cells)
+    )(x, targets.reshape(levels, 8, 8, span), valid_cells)
     corner = [
         (a * lon + b, ((a - 1) % lat) * lon + (b - 1) % lon) for a in range(lat) for b in range(lon)
     ]
-    tiles = []
-    for g in range(CHUNKS):
-        own, east, south, diag = packed[4 * g : 4 * g + 4]
-        tiles.append(
-            [
-                own,
-                from_behind(east, "lon", -1),
-                from_behind(south, "lat", -1),
-                lax.ppermute(diag, ("lat", "lon"), corner),
-            ]
-        )
-    groups = part // 128
-
-    def attend(chunk):
+
+    def halo(east, south, diag):
+        return [
+            from_behind(east, "lon", -1),
+            from_behind(south, "lat", -1),
+            lax.ppermute(diag, ("lat", "lon"), corner),
+        ]
+
+    def attend(*chunk):
+        part = chunk[0].shape[1] // 384 * 128
+        groups = part // 128
         specs = [
             pl.BlockSpec((quarter, 128), lambda g, i=i: (0, i * groups + g)) for i in range(3)
         ]
@@ -484,23 +522,34 @@
             name="attention",
         )(last, *[t for t in chunk for _ in range(3)])
 
-    ring1_after, *tiles[0] = barrier((ring1, *tiles[0]))
+    owns = packed[0::4]
+    sends = [packed[4 * g + 1 : 4 * g + 4] for g in range(len(CHUNKS))]
+    tiles0 = halo(*sends[0])
+    ring1_after, sends[1][0], *tiles0 = barrier((ring1, sends[1][0], *tiles0))
     ring2 = from_behind(ring1_after, "dp", 1)
     across1 = swap(ring1, "lat", 2)
-    ctx0 = attend(tiles[0])
-    ring2_after, across1, ctx0, *tiles[1] = barrier((ring2, across1, ctx0, *tiles[1]))
+    *sends[1], tiles0[0] = barrier((*sends[1], tiles0[0]))
+    tiles1 = halo(*sends[1])
+    ctx0 = attend(owns[0], *tiles0)
+    ring2_after, ctx0, *tiles1 = barrier((ring2, ctx0, *tiles1))
     ring3 = from_behind(ring2_after, "dp", 1)
     across2 = swap(ring2, "lat", 2)
-    ctx1 = attend(tiles[1])
-    ring3_after, across2, ctx1, *tiles[2] = barrier((ring3, across2, ctx1, *tiles[2]))
+    *sends[2], across1, tiles1[0] = barrier((*sends[2], across1, tiles1[0]))
+    tiles2 = halo(*sends[2])
+    ctx1 = attend(owns[1], *tiles1)
+    ring3_after, ctx1, *tiles2 = barrier((ring3, ctx1, *tiles2))
     across3 = swap(ring3_after, "lat", 2)
-    ctx2 = attend(tiles[2])
+    *sends[3], across2, tiles2[0] = barrier((*sends[3], across2, tiles2[0]))
+    tiles3 = halo(*sends[3])
+    ctx2 = attend(owns[2], *tiles2)
+    ctx3 = attend(owns[3], *tiles3)
+    across3, ctx2, ctx3 = barrier((across3, ctx2, ctx3))
     pieces = []
     for ring, across in ((ring1, across1), (ring2, across2), (ring3, across3)):
         pieces += [ring, across, swap(ring, "lat", 1), swap(across, "lat", 1)]
 
     piece = span // lat
-    extra_spec = pl.BlockSpec((quarter, EXTRA), lambda i: (0, 3 * part // EXTRA))
+    extra_spec = pl.BlockSpec((quarter, EXTRA), lambda i: (0, 3 * parts_of[WITH_EXTRA] // EXTRA))
     copies = 2 + PIECES * 5
     assembly = [
         pltpu.VMEM((dp * rows, width), BF),
@@ -511,14 +560,14 @@
         grid=(1,),
         out_shape=[shape((piece, width + 128), BF)] * 4
         + [shape((tokens, width), F32), shape((tokens, 128), F32), shape((tokens, span), BF)],
-        in_specs=[SMEM] * 3 + [VMEM] * CHUNKS + [extra_spec] * 4 + [HBM] + [ANY] * (1 + PIECES),
+        in_specs=[SMEM] * 3 + [VMEM] * len(CHUNKS) + [extra_spec] * 4 + [HBM] + [ANY] * (1 + PIECES),
         out_specs=[VMEM] * 7,
         scratch_shapes=[pltpu.VMEM((tokens, width), BF)]
         + assembly
         + [pltpu.VMEM((span, width), F32), pltpu.SemaphoreType.DMA((copies,))],
         compiler_params=params(28),
         name="forward",
-    )(place, lat_table, var_weight, ctx0, ctx1, ctx2, *tiles[2], w_out, ug, *pieces)
+    )(place, lat_table, var_weight, ctx0, ctx1, ctx2, ctx3, owns[2], *tiles2, w_out, ug, *pieces)
 
     terms = [terms[0]] + [swap(terms[b], "lat", b) for b in (1, 2, 3)]
     grad_context = pl.pallas_call(

time: 101 us -> 99.4 us (0.984)
  waiting for transfers between devices: 32.7 us -> 29 us
  starting transfers between devices: 32.9 us -> 34.1 us
    ppermute x3 -> x4, starting transfers between devices: 2.16 us -> 4.96 us  [halo(): lax.ppermute(diag, ('lat', 'lon'), corner)]
    ppermute x9 -> x11, waiting for transfers between devices: 15.3 us -> 12.6 us  [from_behind(): lax.ppermute(array, axis, [(i, (i + by) % length) for i in range(length)])]
    ppermute x15, waiting for transfers between devices: 12.4 us -> 11 us  [swap(): lax.ppermute(array, axis, [(i, i ^ bit) for i in range(lax.axis_size(axis...]
    ppermute x9 -> x11, starting transfers between devices: 11.6 us -> 10.2 us  [from_behind(): lax.ppermute(array, axis, [(i, (i + by) % length) for i in range(length)])]
    ppermute x3 -> x4, waiting for transfers between devices: 1.87 us -> 2.73 us  [halo(): lax.ppermute(diag, ('lat', 'lon'), corner)]
    pallas_call x3 -> x4, Pallas kernels: 11.6 us -> 11.5 us  [attend(): pl.pallas_call(attention_kernel, grid=(groups,), out_shape=shape((tokens,...]
  transfers between devices with their start and end apart: 34 -> 37, of which waited for: 13 -> 15; matrix products, arithmetic and copies ran while one was open for 0% -> 0% of each run, Pallas kernels for 22% -> 23%
where the time goes in v4:
time: 99.4 us; the launch traced here: 99.2 us
  starting transfers between devices  34.1 us (34%)
  Pallas kernels  33.7 us (34%)
  waiting for transfers between devices  29 us (29%)
    ppermute x11, waiting for transfers between devices, from_behind(): lax.ppermute(array, axis, [(i, (i + by) % length) for i in range(length)])  12.6 us
    ppermute x15, starting transfers between devices, swap(): lax.ppermute(array, axis, [(i, i ^ bit) for i in range(lax.axis_size(axis...  12 us
    pallas_call x4, Pallas kernels, attend(): pl.pallas_call(attention_kernel, grid=(groups,), out_shape=shape((tokens,...  11.5 us
    ppermute x15, waiting for transfers between devices, swap(): lax.ppermute(array, axis, [(i, i ^ bit) for i in range(lax.axis_size(axis...  11 us
    ppermute x11, starting transfers between devices, from_behind(): lax.ppermute(array, axis, [(i, (i + by) % length) for i in range(length)])  10.2 us
    ppermute x7, starting transfers between devices, shards(): plane.append(lax.ppermute(mine, ('lat', 'lon'), pairs))  6.88 us
    pallas_call x1, Pallas kernels, shards(): pl.pallas_call(backward_kernel, out_shape=shape((tokens, width), BF), in_...  6.24 us
    pallas_call x1, Pallas kernels, shards(): pl.pallas_call(forward_kernel, grid=(1,), out_shape=[shape((piece, width...  6.06 us
  transfers between devices with their start and end apart: 37, of which 15 were waited for; matrix products, arithmetic and copies ran while one was open for 0% of the time, Pallas kernels for 23%

profile of v4, /device:TPU:0, one launch (start us, length us, event | category | flops | bytes accessed | tf_op | source)
XLA Modules:
  0.0 99.2 jit_solution(10901001807617653469)
XLA Ops:
  0.6 0.7 pad_add_fusion.place_ref.refs_0_
  1.3 3.1 %lead.1 = (bf16[256,384]{1,0:T(8,128)(2,1)}, bf16[112,1536]{1,0:T(8,128)(2,1)}, bf16[64,384]{1,0:T(8,128)(2,1)}, bf16[64,384]{1,0:T(8,128)(2,1)}, bf16[64,384]{1,0:T(8,128)(2,1)}, /*index=5*/bf16[64,384]{1,0:T(8,128)(2,1)}) custom-call(s32[2]{0:T(128)} %pad_add_fusion.place_ref.refs_0_, bf16[384,1536]{1,0:T(8,128)(2,1)} %own_w.1, bf16[160,384]{1,0:T(8,128)(2,1)} %bitcast.13, ...), custom_call_target="tpu_custom_call" | custom-call | tf_op jit(solution)/shard_map/lead/pallas_call | solution.py:468
  4.4 3.1 %collective-permute-start = (bf16[112,1536]{1,0:T(8,128)(2,1)}, bf16[112,1536]{1,0:T(8,128)(2,1)S(1)}, u32[]{:S(2)}, u32[]{:S(2)}) collective-permute-start(bf16[112,1536]{1,0:T(8,128)(2,1)} %get-tuple-element.72), channel_id=1, source_target_pairs={{0,8},{8,16},{16,24},{24,0},{1,9},{9,17},{17,25},{25,1},{2,10},{10... | collective-permute-start | bytes 1032200 | tf_op jit(solution)/shard_map/ppermute | solution.py:30
  7.5 1.5 %collective-permute-start.1 = (bf16[64,384]{1,0:T(8,128)(2,1)}, bf16[64,384]{1,0:T(8,128)(2,1)S(1)}, u32[]{:S(2)}, u32[]{:S(2)}) collective-permute-start(bf16[64,384]{1,0:T(8,128)(2,1)} %get-tuple-element.74), channel_id=1, source_target_pairs={{0,1},{1,0},{2,3},{3,2},{4,5},{5,4},{6,7},{7,6},{8,9},{9,8},{10,11... | collective-permute-start | bytes 147464 | tf_op jit(solution)/shard_map/ppermute | solution.py:30
  9.0 0.4 collective-permute-start.2
  9.4 1.2 %collective-permute-start.3 = (bf16[64,384]{1,0:T(8,128)(2,1)}, bf16[64,384]{1,0:T(8,128)(2,1)S(1)}, u32[]{:S(2)}, u32[]{:S(2)}) collective-permute-start(bf16[64,384]{1,0:T(8,128)(2,1)} %get-tuple-element.76), channel_id=1, source_target_pairs={{0,7},{1,6},{2,1},{3,0},{4,3},{5,2},{6,5},{7,4},{8,15},{9,14},{10,... | collective-permute-start | bytes 147464 | tf_op jit(solution)/shard_map/ppermute | solution.py:506
  10.6 4.7 %pack.1 = (bf16[64,1536]{1,0:T(8,128)(2,1)}, bf16[64,1536]{1,0:T(8,128)(2,1)}, bf16[64,1536]{1,0:T(8,128)(2,1)}, bf16[64,1536]{1,0:T(8,128)(2,1)}, bf16[64,1792]...) custom-call(bf16[4,8,8,4608]{3,2,1,0:T(8,128)(2,1)} %bitcast.10, ...), custom_call_target="tpu_custom_call" | custom-call | tf_op jit(solution)/shard_map/pack/pallas_call | solution.py:484
  15.3 0.0 collective-permute-done.1.refs_3_.refs_4_.refs_5_
  15.3 0.0 collective-permute-done.2.refs_6_.refs_7_.refs_8_
  15.3 2.5 %collective-permute-done.refs_10_.refs_0_ = bf16[112,1536]{1,0:T(8,128)(2,1)S(1)} collective-permute-done((bf16[112,1536]{1,0:T(8,128)(2,1)}, bf16[112,1536]{1,0:T(8,128)(2,1)S(1)}, u32[]{:S(2)}, u32[]{:S(2)}) %collective-permute-start) | collective-permute-done | bytes 344096 | tf_op jit(solution)/shard_map/ppermute | solution.py:30
  17.8 0.0 collective-permute-start.4
  17.8 1.5 %collective-permute-start.9 = (bf16[112,1536]{1,0:T(8,128)(2,1)S(1)}, bf16[112,1536]{1,0:T(8,128)(2,1)S(1)}, u32[]{:S(2)}, u32[]{:S(2)}) collective-permute-start(bf16[112,1536]{1,0:T(8,128)(2,1)S(1)} %collective-permute-done.refs_10_.refs_0_), channel_id=1, source_target_pairs={{0,4},{2,6},{4,0},{6,2},{1,5},{3,7},{5,1},{7,3},{8,12},{10,14},{12... | collective-permute-start | bytes 1032200 | tf_op jit(solution)/shard_map/ppermute | solution.py:442
  19.3 1.5 %collective-permute-start.5 = (bf16[64,1536]{1,0:T(8,128)(2,1)}, bf16[64,1536]{1,0:T(8,128)(2,1)S(1)}, u32[]{:S(2)}, u32[]{:S(2)}) collective-permute-start(bf16[64,1536]{1,0:T(8,128)(2,1)} %get-tuple-element.86), channel_id=1, source_target_pairs={{0,1},{1,0},{2,3},{3,2},{4,5},{5,4},{6,7},{7,6},{8,9},{9,8},{10,11... | collective-permute-start | bytes 589832 | tf_op jit(solution)/shard_map/ppermute | solution.py:30
  20.8 0.6 collective-permute-start.7
  21.4 0.9 attention.4.refs_0_
  22.3 4.1 %collective-permute-done.5.refs_3_.refs_4_.refs_5_ = bf16[64,1536]{1,0:T(8,128)(2,1)S(1)} collective-permute-done((bf16[64,1536]{1,0:T(8,128)(2,1)}, bf16[64,1536]{1,0:T(8,128)(2,1)S(1)}, u32[]{:S(2)}, u32[]{:S(2)}) %collective-permute-start.5) | collective-permute-done | bytes 196640 | tf_op jit(solution)/shard_map/ppermute | solution.py:30
  26.4 3.8 %collective-permute-done.6.refs_6_.refs_7_.refs_8_ = bf16[64,1536]{1,0:T(8,128)(2,1)S(1)} collective-permute-done((bf16[64,1536]{1,0:T(8,128)(2,1)}, bf16[64,1536]{1,0:T(8,128)(2,1)S(1)}, u32[]{:S(2)}, u32[]{:S(2)}) %collective-permute-start.6) | collective-permute-done | bytes 196640 | tf_op jit(solution)/shard_map/ppermute | solution.py:30
  30.2 0.9 collective-permute-start.8
  31.1 1.5 %collective-permute-start.10 = (bf16[64,1792]{1,0:T(8,128)(2,1)}, bf16[64,1792]{1,0:T(8,128)(2,1)S(1)}, u32[]{:S(2)}, u32[]{:S(2)}) collective-permute-start(bf16[64,1792]{1,0:T(8,128)(2,1)} %get-tuple-element.99), channel_id=1, source_target_pairs={{0,1},{1,0},{2,3},{3,2},{4,5},{5,4},{6,7},{7,6},{8,9},{9,8},{10,11... | collective-permute-start | bytes 688136 | tf_op jit(solution)/shard_map/ppermute | solution.py:30
  32.6 1.2 %collective-permute-start.11 = (bf16[64,1792]{1,0:T(8,128)(2,1)}, bf16[64,1792]{1,0:T(8,128)(2,1)S(1)}, u32[]{:S(2)}, u32[]{:S(2)}) collective-permute-start(bf16[64,1792]{1,0:T(8,128)(2,1)} %get-tuple-element.100), channel_id=1, source_target_pairs={{0,6},{2,0},{4,2},{6,4},{1,7},{3,1},{5,3},{7,5},{8,14},{10,8},{12,... | collective-permute-start | bytes 688136 | tf_op jit(solution)/shard_map/ppermute | solution.py:30
  33.9 0.9 collective-permute-start.14
  34.7 0.9 copy-done.2
  35.7 3.9 %attention.5.refs_1_ = bf16[256,512]{1,0:T(8,128)(2,1)S(1)} custom-call(s32[1]{0:T(128)} %bitcast.5.last_ref, bf16[64,1536]{1,0:T(8,128)(2,1)S(1)} %copy-done.2, bf16[64,1536]{1,0:T(8,128)(2,1)S(1)} %copy-done.2, bf16[64,1536]{1,0:T(8,128)(2,1)S(1)} %copy-done.2, bf16[64,1536]{1,0:T(8,128)(2,1)S(1)} %collective-permute-done.5.refs_3_.refs_4_.refs_5_, ...), custom_call_target="tpu_custom_call" | custom-call | tf_op jit(solution)/shard_map/attention/pallas_call | solution.py:515
  39.6 0.2 collective-permute-done.10.refs_3_.refs_4_.refs_5_
  39.8 1.2 %collective-permute-done.11.refs_6_.refs_7_.refs_8_ = bf16[64,1792]{1,0:T(8,128)(2,1)S(1)} collective-permute-done((bf16[64,1792]{1,0:T(8,128)(2,1)}, bf16[64,1792]{1,0:T(8,128)(2,1)S(1)}, u32[]{:S(2)}, u32[]{:S(2)}) %collective-permute-start.11) | collective-permute-done | bytes 229408 | tf_op jit(solution)/shard_map/ppermute | solution.py:30
  41.0 2.7 %collective-permute-done.12.refs_9_.refs_10_.refs_11_.refs_7_ = bf16[64,1792]{1,0:T(8,128)(2,1)S(1)} collective-permute-done((bf16[64,1792]{1,0:T(8,128)(2,1)}, bf16[64,1792]{1,0:T(8,128)(2,1)S(1)}, u32[]{:S(2)}, u32[]{:S(2)}) %collective-permute-start.12) | collective-permute-done | bytes 229408 | tf_op jit(solution)/shard_map/ppermute | solution.py:506
  43.7 1.5 %collective-permute-start.13 = (bf16[112,1536]{1,0:T(8,128)(2,1)S(1)}, bf16[112,1536]{1,0:T(8,128)(2,1)S(1)}, u32[]{:S(2)}, u32[]{:S(2)}) collective-permute-start(bf16[112,1536]{1,0:T(8,128)(2,1)S(1)} %collective-permute-done.8.refs_18_.refs_8_), channel_id=1, source_target_pairs={{0,4},{2,6},{4,0},{6,2},{1,5},{3,7},{5,1},{7,3},{8,12},{10,14},{12... | collective-permute-start | bytes 1032200 | tf_op jit(solution)/shard_map/ppermute | solution.py:442
  45.2 0.1 collective-permute-start.18
  45.3 4.6 %collective-permute-done.14.refs_15_.refs_5_ = bf16[112,1536]{1,0:T(8,128)(2,1)S(1)} collective-permute-done((bf16[112,1536]{1,0:T(8,128)(2,1)S(1)}, bf16[112,1536]{1,0:T(8,128)(2,1)S(1)}, u32[]{:S(2)}, u32[]{:S(2)}) %collective-permute-start.14) | collective-permute-done | bytes 344096 | tf_op jit(solution)/shard_map/ppermute | solution.py:442
  50.0 0.1 collective-permute-start.16
  50.0 3.2 %collective-permute-start.17 = (bf16[64,1152]{1,0:T(8,128)(2,1)S(1)}, bf16[64,1152]{1,0:T(8,128)(2,1)S(1)}, u32[]{:S(2)}, u32[]{:S(2)}) collective-permute-start(bf16[64,1152]{1,0:T(8,128)(2,1)S(1)} %copy-done.9), channel_id=1, source_target_pairs={{0,7},{1,6},{2,1},{3,0},{4,3},{5,2},{6,5},{7,4},{8,15},{9,14},{10,... | collective-permute-start | bytes 442376 | tf_op jit(solution)/shard_map/ppermute | solution.py:506
  53.2 3.9 %attention.6.refs_2_ = bf16[256,512]{1,0:T(8,128)(2,1)S(1)} custom-call(s32[1]{0:T(128)} %bitcast.5.last_ref, bf16[64,1792]{1,0:T(8,128)(2,1)S(1)} %copy-done.1, bf16[64,1792]{1,0:T(8,128)(2,1)S(1)} %copy-done.1, bf16[64,1792]{1,0:T(8,128)(2,1)S(1)} %copy-done.1, bf16[64,1792]{1,0:T(8,128)(2,1)S(1)} %collective-permute-done.10.refs_3_.refs_4_.refs_5_, ...), custom_call_target="tpu_custom_call" | custom-call | tf_op jit(solution)/shard_map/attention/pallas_call | solution.py:515
  57.1 0.0 copy-start
  57.1 0.0 copy-start.7
  57.1 0.0 copy-start.8
  57.1 0.1 collective-permute-start.19
  57.2 0.8 collective-permute-done.16.refs_6_.refs_7_.refs_8_
  58.0 1.0 %collective-permute-start.21 = (bf16[112,1536]{1,0:T(8,128)(2,1)S(1)}, bf16[112,1536]{1,0:T(8,128)(2,1)S(1)}, u32[]{:S(2)}, u32[]{:S(2)}) collective-permute-start(bf16[112,1536]{1,0:T(8,128)(2,1)S(1)} %collective-permute-done.14.refs_15_.refs_5_), channel_id=1, source_target_pairs={{0,2},{2,0},{4,6},{6,4},{1,3},{3,1},{5,7},{7,5},{8,10},{10,8},{12,... | collective-permute-start | bytes 1032200 | tf_op jit(solution)/shard_map/ppermute | solution.py:442
  59.0 2.9 %attention.7.refs_3_ = bf16[256,384]{1,0:T(8,128)(2,1)S(1)} custom-call(s32[1]{0:T(128)} %bitcast.5.last_ref, bf16[64,1152]{1,0:T(8,128)(2,1)S(1)} %copy-done.3, bf16[64,1152]{1,0:T(8,128)(2,1)S(1)} %copy-done.3, bf16[64,1152]{1,0:T(8,128)(2,1)S(1)} %copy-done.3, bf16[64,1152]{1,0:T(8,128)(2,1)S(1)} %collective-permute-done.15.refs_3_.refs_4_.refs_5_, ...), custom_call_target="tpu_custom_call" | custom-call | tf_op jit(solution)/shard_map/attention/pallas_call | solution.py:515
  61.9 0.1 collective-permute-start.22
  62.0 0.5 collective-permute-start.23
  62.5 1.1 %collective-permute-done.22.refs_20_.refs_10_ = bf16[112,1536]{1,0:T(8,128)(2,1)S(1)} collective-permute-done((bf16[112,1536]{1,0:T(8,128)(2,1)S(1)}, bf16[112,1536]{1,0:T(8,128)(2,1)S(1)}, u32[]{:S(2)}, u32[]{:S(2)}) %collective-permute-start.22) | collective-permute-done | bytes 344096 | tf_op jit(solution)/shard_map/ppermute | solution.py:442
  63.7 0.5 collective-permute-done.23.refs_21_.refs_11_
  64.2 6.1 %forward.1 = (bf16[40,1664]{1,0:T(8,128)(2,1)S(1)}, bf16[40,1664]{1,0:T(8,128)(2,1)S(1)}, bf16[40,1664]{1,0:T(8,128)(2,1)S(1)}, bf16[40,1664]{1,0:T(8,128)(2,1)S...) custom-call(s32[2]{0:T(128)S(1)} %copy-done.6, f32[32]{0:T(128)S(1)} %copy-done.8, ...), custom_call_target="tpu_custom_call" | custom-call | tf_op jit(solution)/shard_map/forward/pallas_call | solution.py:558
  70.2 0.2 collective-permute-start.24
  70.4 1.7 %collective-permute-start.25 = (bf16[40,1664]{1,0:T(8,128)(2,1)S(1)}, bf16[40,1664]{1,0:T(8,128)(2,1)S(1)}, u32[]{:S(2)}, u32[]{:S(2)}) collective-permute-start(bf16[40,1664]{1,0:T(8,128)(2,1)S(1)} %get-tuple-element.124), channel_id=1, source_target_pairs={{0,4},{2,6},{4,0},{6,2},{1,5},{3,7},{5,1},{7,3},{8,12},{10,14},{12... | collective-permute-start | bytes 399368 | tf_op jit(solution)/shard_map/ppermute | solution.py:442
  72.1 0.1 collective-permute-start.26
  72.2 6.2 %backward.1 = bf16[256,1536]{1,0:T(8,128)(2,1)} custom-call(s32[2]{0:T(128)S(1)} %copy-done.6, f32[256,1536]{1,0:T(8,128)S(1)} %get-tuple-element.126.normed_ref, f32[256,128]{1,0:T(8,128)S(1)} %get-tuple-element.127.inv_ref, bf16[256,160]{1,0:T(8,128)(2,1)S(1)} %get-tuple-element.128.dfc_ref, bf16[384,1536]{1,0:T(8,128)(2,1)S(1)} %copy-done, ...), custom_call_target="tpu_custom_call" | custom-call | tf_op jit(solution)/shard_map/backward/pallas_call | solution.py:573
  78.4 0.1 collective-permute-done.26.d
  78.6 0.7 lat_sum.1
  79.3 1.6 %collective-permute-start.27 = (bf16[40,384]{1,0:T(8,128)(2,1)S(1)}, bf16[40,384]{1,0:T(8,128)(2,1)S(1)}, u32[]{:S(2)}, u32[]{:S(2)}) collective-permute-start(bf16[40,384]{1,0:T(8,128)(2,1)S(1)} %get-tuple-element.136), channel_id=1, source_target_pairs={{0,8},{8,0},{16,24},{24,16},{1,9},{9,1},{17,25},{25,17},{2,10},{10... | collective-permute-start | bytes 92168 | tf_op jit(solution)/shard_map/ppermute | solution.py:442
  80.9 1.8 %collective-permute-start.28 = (bf16[40,384]{1,0:T(8,128)(2,1)S(1)}, bf16[40,384]{1,0:T(8,128)(2,1)S(1)}, u32[]{:S(2)}, u32[]{:S(2)}) collective-permute-start(bf16[40,384]{1,0:T(8,128)(2,1)S(1)} %get-tuple-element.137), channel_id=1, source_target_pairs={{0,16},{8,24},{16,0},{24,8},{1,17},{9,25},{17,1},{25,9},{2,18},{10... | collective-permute-start | bytes 92168 | tf_op jit(solution)/shard_map/ppermute | solution.py:442
  82.6 1.1 %collective-permute-start.29 = (bf16[40,384]{1,0:T(8,128)(2,1)S(1)}, bf16[40,384]{1,0:T(8,128)(2,1)S(1)}, u32[]{:S(2)}, u32[]{:S(2)}) collective-permute-start(bf16[40,384]{1,0:T(8,128)(2,1)S(1)} %get-tuple-element.138), channel_id=1, source_target_pairs={{0,24},{8,16},{16,8},{24,0},{1,25},{9,17},{17,9},{25,1},{2,26},{10... | collective-permute-start | bytes 92168 | tf_op jit(solution)/shard_map/ppermute | solution.py:442
  83.7 2.0 %collective-permute-done.28.c = bf16[40,384]{1,0:T(8,128)(2,1)S(1)} collective-permute-done((bf16[40,384]{1,0:T(8,128)(2,1)S(1)}, bf16[40,384]{1,0:T(8,128)(2,1)S(1)}, u32[]{:S(2)}, u32[]{:S(2)}) %collective-permute-start.28) | collective-permute-done | bytes 30752 | tf_op jit(solution)/shard_map/ppermute | solution.py:442
  85.7 2.6 %collective-permute-done.29.d = bf16[40,384]{1,0:T(8,128)(2,1)S(1)} collective-permute-done((bf16[40,384]{1,0:T(8,128)(2,1)S(1)}, bf16[40,384]{1,0:T(8,128)(2,1)S(1)}, u32[]{:S(2)}, u32[]{:S(2)}) %collective-permute-start.29) | collective-permute-done | bytes 30752 | tf_op jit(solution)/shard_map/ppermute | solution.py:442
  88.4 0.1 collective-permute-start.36
  88.5 1.9 %collective-permute-start.35 = (bf16[48,384]{1,0:T(8,128)(2,1)S(1)}, bf16[48,384]{1,0:T(8,128)(2,1)S(1)}, u32[]{:S(2)}, u32[]{:S(2)}) collective-permute-start(bf16[48,384]{1,0:T(8,128)(2,1)S(1)} %dp_sum.1.refs_1_), channel_id=1, source_target_pairs={{0,6},{1,7},{2,4},{3,5},{4,2},{5,3},{6,0},{7,1},{8,14},{9,15},{10,... | collective-permute-start | bytes 110600 | tf_op jit(solution)/shard_map/ppermute | solution.py:609
  90.4 2.2 %collective-permute-start.34 = (bf16[48,384]{1,0:T(8,128)(2,1)S(1)}, bf16[48,384]{1,0:T(8,128)(2,1)S(1)}, u32[]{:S(2)}, u32[]{:S(2)}) collective-permute-start(bf16[48,384]{1,0:T(8,128)(2,1)S(1)} %dp_sum.1.refs_1_), channel_id=1, source_target_pairs={{0,5},{1,4},{2,7},{3,6},{4,1},{5,0},{6,3},{7,2},{8,13},{9,12},{10,... | collective-permute-start | bytes 110600 | tf_op jit(solution)/shard_map/ppermute | solution.py:609
  92.6 0.5 collective-permute-start.33
  93.1 0.9 collective-permute-start.31
  94.0 1.3 %collective-permute-start.30 = (bf16[48,384]{1,0:T(8,128)(2,1)S(1)}, bf16[48,384]{1,0:T(8,128)(2,1)S(1)}, u32[]{:S(2)}, u32[]{:S(2)}) collective-permute-start(bf16[48,384]{1,0:T(8,128)(2,1)S(1)} %dp_sum.1.refs_1_), channel_id=1, source_target_pairs={{0,1},{1,0},{2,3},{3,2},{4,5},{5,4},{6,7},{7,6},{8,9},{9,8},{10,11... | collective-permute-start | bytes 110600 | tf_op jit(solution)/shard_map/ppermute | solution.py:609
  95.3 1.3 %collective-permute-done.33.refs_5_ = bf16[48,384]{1,0:T(8,128)(2,1)S(1)} collective-permute-done((bf16[48,384]{1,0:T(8,128)(2,1)S(1)}, bf16[48,384]{1,0:T(8,128)(2,1)S(1)}, u32[]{:S(2)}, u32[]{:S(2)}) %collective-permute-start.33) | collective-permute-done | bytes 36896 | tf_op jit(solution)/shard_map/ppermute | solution.py:609
  96.6 1.4 %collective-permute-done.30.refs_2_ = bf16[48,384]{1,0:T(8,128)(2,1)S(1)} collective-permute-done((bf16[48,384]{1,0:T(8,128)(2,1)S(1)}, bf16[48,384]{1,0:T(8,128)(2,1)S(1)}, u32[]{:S(2)}, u32[]{:S(2)}) %collective-permute-start.30) | collective-permute-done | bytes 36896 | tf_op jit(solution)/shard_map/ppermute | solution.py:609
  98.0 1.3 %join.1 = (f32[160,384]{1,0:T(8,128)}, f32[1,1]{1,0:T(1,128)}) custom-call(s32[2]{0:T(128)S(1)} %copy-done.6, bf16[48,384]{1,0:T(8,128)(2,1)S(1)} %dp_sum.1.refs_1_, bf16[48,384]{1,0:T(8,128)(2,1)S(1)} %collective-permute-done.30.refs_2_, bf16[48,384]{1,0:T(8,128)(2,1)S(1)} %collective-permute-done.31.refs_3_, ...), custom_call_target="tpu_custom_call" | custom-call | tf_op jit(solution)/shard_map/join/pallas_call | solution.py:612
  (46 shorter events, 0.2 us)
Async XLA Ops:
  4.4 17.0 %copy-start.5 = (bf16[64,384]{1,0:T(8,128)(2,1)S(1)}, bf16[64,384]{1,0:T(8,128)(2,1)}, u32[]{:S(2)}) copy-start(bf16[64,384]{1,0:T(8,128)(2,1)} %get-tuple-element.78.refs_0_.refs_1_.refs_2_) | copy-start | bytes 147460
  4.4 13.4 %collective-permute-start = (bf16[112,1536]{1,0:T(8,128)(2,1)}, bf16[112,1536]{1,0:T(8,128)(2,1)S(1)}, u32[]{:S(2)}, u32[]{:S(2)}) collective-permute-start(bf16[112,1536]{1,0:T(8,128)(2,1)} %get-tuple-element.72), channel_id=1, source_target_pairs={{0,8},{8,16},{16,24},{24,0},{1,9},{9,17},{17,25},{25,1},{2,10},{10... | collective-permute-start | bytes 1032200 | tf_op jit(solution)/shard_map/ppermute | solution.py:30
  7.5 7.8 %collective-permute-start.1 = (bf16[64,384]{1,0:T(8,128)(2,1)}, bf16[64,384]{1,0:T(8,128)(2,1)S(1)}, u32[]{:S(2)}, u32[]{:S(2)}) collective-permute-start(bf16[64,384]{1,0:T(8,128)(2,1)} %get-tuple-element.74), channel_id=1, source_target_pairs={{0,1},{1,0},{2,3},{3,2},{4,5},{5,4},{6,7},{7,6},{8,9},{9,8},{10,11... | collective-permute-start | bytes 147464 | tf_op jit(solution)/shard_map/ppermute | solution.py:30
  9.0 6.3 %collective-permute-start.2 = (bf16[64,384]{1,0:T(8,128)(2,1)}, bf16[64,384]{1,0:T(8,128)(2,1)S(1)}, u32[]{:S(2)}, u32[]{:S(2)}) collective-permute-start(bf16[64,384]{1,0:T(8,128)(2,1)} %get-tuple-element.75), channel_id=1, source_target_pairs={{0,6},{2,0},{4,2},{6,4},{1,7},{3,1},{5,3},{7,5},{8,14},{10,8},{12,... | collective-permute-start | bytes 147464 | tf_op jit(solution)/shard_map/ppermute | solution.py:30
  9.4 5.9 %collective-permute-start.3 = (bf16[64,384]{1,0:T(8,128)(2,1)}, bf16[64,384]{1,0:T(8,128)(2,1)S(1)}, u32[]{:S(2)}, u32[]{:S(2)}) collective-permute-start(bf16[64,384]{1,0:T(8,128)(2,1)} %get-tuple-element.76), channel_id=1, source_target_pairs={{0,7},{1,6},{2,1},{3,0},{4,3},{5,2},{6,5},{7,4},{8,15},{9,14},{10,... | collective-permute-start | bytes 147464 | tf_op jit(solution)/shard_map/ppermute | solution.py:506
  17.8 12.4 %collective-permute-start.4 = (bf16[112,1536]{1,0:T(8,128)(2,1)S(1)}, bf16[112,1536]{1,0:T(8,128)(2,1)S(1)}, u32[]{:S(2)}, u32[]{:S(2)}) collective-permute-start(bf16[112,1536]{1,0:T(8,128)(2,1)S(1)} %collective-permute-done.refs_10_.refs_0_), channel_id=1, source_target_pairs={{0,8},{8,16},{16,24},{24,0},{1,9},{9,17},{17,25},{25,1},{2,10},{10... | collective-permute-start | bytes 1032200 | tf_op jit(solution)/shard_map/ppermute | solution.py:30
  17.8 13.3 %collective-permute-start.9 = (bf16[112,1536]{1,0:T(8,128)(2,1)S(1)}, bf16[112,1536]{1,0:T(8,128)(2,1)S(1)}, u32[]{:S(2)}, u32[]{:S(2)}) collective-permute-start(bf16[112,1536]{1,0:T(8,128)(2,1)S(1)} %collective-permute-done.refs_10_.refs_0_), channel_id=1, source_target_pairs={{0,4},{2,6},{4,0},{6,2},{1,5},{3,7},{5,1},{7,3},{8,12},{10,14},{12... | collective-permute-start | bytes 1032200 | tf_op jit(solution)/shard_map/ppermute | solution.py:442
  19.3 30.6 %copy-start.11 = (bf16[64,1152]{1,0:T(8,128)(2,1)S(1)}, bf16[64,1152]{1,0:T(8,128)(2,1)}, u32[]{:S(2)}) copy-start(bf16[64,1152]{1,0:T(8,128)(2,1)} %get-tuple-element.113) | copy-start | bytes 442372
  19.3 7.1 %collective-permute-start.5 = (bf16[64,1536]{1,0:T(8,128)(2,1)}, bf16[64,1536]{1,0:T(8,128)(2,1)S(1)}, u32[]{:S(2)}, u32[]{:S(2)}) collective-permute-start(bf16[64,1536]{1,0:T(8,128)(2,1)} %get-tuple-element.86), channel_id=1, source_target_pairs={{0,1},{1,0},{2,3},{3,2},{4,5},{5,4},{6,7},{7,6},{8,9},{9,8},{10,11... | collective-permute-start | bytes 589832 | tf_op jit(solution)/shard_map/ppermute | solution.py:30
  20.8 9.4 %collective-permute-start.6 = (bf16[64,1536]{1,0:T(8,128)(2,1)}, bf16[64,1536]{1,0:T(8,128)(2,1)S(1)}, u32[]{:S(2)}, u32[]{:S(2)}) collective-permute-start(bf16[64,1536]{1,0:T(8,128)(2,1)} %get-tuple-element.87), channel_id=1, source_target_pairs={{0,6},{2,0},{4,2},{6,4},{1,7},{3,1},{5,3},{7,5},{8,14},{10,8},{12,... | collective-permute-start | bytes 589832 | tf_op jit(solution)/shard_map/ppermute | solution.py:30
  20.8 9.4 %collective-permute-start.7 = (bf16[64,1536]{1,0:T(8,128)(2,1)}, bf16[64,1536]{1,0:T(8,128)(2,1)S(1)}, u32[]{:S(2)}, u32[]{:S(2)}) collective-permute-start(bf16[64,1536]{1,0:T(8,128)(2,1)} %get-tuple-element.88), channel_id=1, source_target_pairs={{0,7},{1,6},{2,1},{3,0},{4,3},{5,2},{6,5},{7,4},{8,15},{9,14},{10,... | collective-permute-start | bytes 589832 | tf_op jit(solution)/shard_map/ppermute | solution.py:506
  21.4 28.5 %copy-start.10 = (bf16[64,1152]{1,0:T(8,128)(2,1)S(1)}, bf16[64,1152]{1,0:T(8,128)(2,1)}, u32[]{:S(2)}) copy-start(bf16[64,1152]{1,0:T(8,128)(2,1)} %get-tuple-element.114) | copy-start | bytes 442372
  21.4 28.6 %copy-start.9 = (bf16[64,1152]{1,0:T(8,128)(2,1)S(1)}, bf16[64,1152]{1,0:T(8,128)(2,1)}, u32[]{:S(2)}) copy-start(bf16[64,1152]{1,0:T(8,128)(2,1)} %get-tuple-element.115) | copy-start | bytes 442372
  21.4 31.8 %copy-start.1 = (bf16[64,1792]{1,0:T(8,128)(2,1)S(1)}, bf16[64,1792]{1,0:T(8,128)(2,1)}, u32[]{:S(2)}) copy-start(bf16[64,1792]{1,0:T(8,128)(2,1)} %get-tuple-element.104.refs_0_.refs_1_.refs_2_.refs_4_) | copy-start | bytes 688132
  30.2 13.5 %collective-permute-start.8 = (bf16[112,1536]{1,0:T(8,128)(2,1)S(1)}, bf16[112,1536]{1,0:T(8,128)(2,1)S(1)}, u32[]{:S(2)}, u32[]{:S(2)}) collective-permute-start(bf16[112,1536]{1,0:T(8,128)(2,1)S(1)} %collective-permute-done.4.refs_14_.refs_4_), channel_id=1, source_target_pairs={{0,8},{8,16},{16,24},{24,0},{1,9},{9,17},{17,25},{25,1},{2,10},{10... | collective-permute-start | bytes 1032200 | tf_op jit(solution)/shard_map/ppermute | solution.py:30
  31.1 8.6 %collective-permute-start.10 = (bf16[64,1792]{1,0:T(8,128)(2,1)}, bf16[64,1792]{1,0:T(8,128)(2,1)S(1)}, u32[]{:S(2)}, u32[]{:S(2)}) collective-permute-start(bf16[64,1792]{1,0:T(8,128)(2,1)} %get-tuple-element.99), channel_id=1, source_target_pairs={{0,1},{1,0},{2,3},{3,2},{4,5},{5,4},{6,7},{7,6},{8,9},{9,8},{10,11... | collective-permute-start | bytes 688136 | tf_op jit(solution)/shard_map/ppermute | solution.py:30
  32.6 8.4 %collective-permute-start.11 = (bf16[64,1792]{1,0:T(8,128)(2,1)}, bf16[64,1792]{1,0:T(8,128)(2,1)S(1)}, u32[]{:S(2)}, u32[]{:S(2)}) collective-permute-start(bf16[64,1792]{1,0:T(8,128)(2,1)} %get-tuple-element.100), channel_id=1, source_target_pairs={{0,6},{2,0},{4,2},{6,4},{1,7},{3,1},{5,3},{7,5},{8,14},{10,8},{12,... | collective-permute-start | bytes 688136 | tf_op jit(solution)/shard_map/ppermute | solution.py:30
  33.9 9.9 %collective-permute-start.12 = (bf16[64,1792]{1,0:T(8,128)(2,1)}, bf16[64,1792]{1,0:T(8,128)(2,1)S(1)}, u32[]{:S(2)}, u32[]{:S(2)}) collective-permute-start(bf16[64,1792]{1,0:T(8,128)(2,1)} %get-tuple-element.101), channel_id=1, source_target_pairs={{0,7},{1,6},{2,1},{3,0},{4,3},{5,2},{6,5},{7,4},{8,15},{9,14},{10,... | collective-permute-start | bytes 688136 | tf_op jit(solution)/shard_map/ppermute | solution.py:506
  33.9 16.1 %collective-permute-start.14 = (bf16[112,1536]{1,0:T(8,128)(2,1)S(1)}, bf16[112,1536]{1,0:T(8,128)(2,1)S(1)}, u32[]{:S(2)}, u32[]{:S(2)}) collective-permute-start(bf16[112,1536]{1,0:T(8,128)(2,1)S(1)} %collective-permute-done.4.refs_14_.refs_4_), channel_id=1, source_target_pairs={{0,4},{2,6},{4,0},{6,2},{1,5},{3,7},{5,1},{7,3},{8,12},{10,14},{12... | collective-permute-start | bytes 1032200 | tf_op jit(solution)/shard_map/ppermute | solution.py:442
  34.7 0.9 copy-start.2
  39.5 19.5 %copy-start.3 = (bf16[64,1152]{1,0:T(8,128)(2,1)S(1)}, bf16[64,1152]{1,0:T(8,128)(2,1)}, u32[]{:S(2)}) copy-start(bf16[64,1152]{1,0:T(8,128)(2,1)} %get-tuple-element.112.refs_0_.refs_1_.refs_2_) | copy-start | bytes 442372
  43.7 18.2 %collective-permute-start.13 = (bf16[112,1536]{1,0:T(8,128)(2,1)S(1)}, bf16[112,1536]{1,0:T(8,128)(2,1)S(1)}, u32[]{:S(2)}, u32[]{:S(2)}) collective-permute-start(bf16[112,1536]{1,0:T(8,128)(2,1)S(1)} %collective-permute-done.8.refs_18_.refs_8_), channel_id=1, source_target_pairs={{0,4},{2,6},{4,0},{6,2},{1,5},{3,7},{5,1},{7,3},{8,12},{10,14},{12... | collective-permute-start | bytes 1032200 | tf_op jit(solution)/shard_map/ppermute | solution.py:442
  45.2 16.8 %collective-permute-start.18 = (bf16[112,1536]{1,0:T(8,128)(2,1)S(1)}, bf16[112,1536]{1,0:T(8,128)(2,1)S(1)}, u32[]{:S(2)}, u32[]{:S(2)}) collective-permute-start(bf16[112,1536]{1,0:T(8,128)(2,1)S(1)} %collective-permute-done.refs_10_.refs_0_), channel_id=1, source_target_pairs={{0,2},{2,0},{4,6},{6,4},{1,3},{3,1},{5,7},{7,5},{8,10},{10,8},{12,... | collective-permute-start | bytes 1032200 | tf_op jit(solution)/shard_map/ppermute | solution.py:442
  49.9 7.2 %collective-permute-start.15 = (bf16[64,1152]{1,0:T(8,128)(2,1)S(1)}, bf16[64,1152]{1,0:T(8,128)(2,1)S(1)}, u32[]{:S(2)}, u32[]{:S(2)}) collective-permute-start(bf16[64,1152]{1,0:T(8,128)(2,1)S(1)} %copy-done.11), channel_id=1, source_target_pairs={{0,1},{1,0},{2,3},{3,2},{4,5},{5,4},{6,7},{7,6},{8,9},{9,8},{10,11... | collective-permute-start | bytes 442376 | tf_op jit(solution)/shard_map/ppermute | solution.py:30
  50.0 8.0 %collective-permute-start.16 = (bf16[64,1152]{1,0:T(8,128)(2,1)S(1)}, bf16[64,1152]{1,0:T(8,128)(2,1)S(1)}, u32[]{:S(2)}, u32[]{:S(2)}) collective-permute-start(bf16[64,1152]{1,0:T(8,128)(2,1)S(1)} %copy-done.10), channel_id=1, source_target_pairs={{0,6},{2,0},{4,2},{6,4},{1,7},{3,1},{5,3},{7,5},{8,14},{10,8},{12,... | collective-permute-start | bytes 442376 | tf_op jit(solution)/shard_map/ppermute | solution.py:30
  50.0 8.0 %collective-permute-start.17 = (bf16[64,1152]{1,0:T(8,128)(2,1)S(1)}, bf16[64,1152]{1,0:T(8,128)(2,1)S(1)}, u32[]{:S(2)}, u32[]{:S(2)}) collective-permute-start(bf16[64,1152]{1,0:T(8,128)(2,1)S(1)} %copy-done.9), channel_id=1, source_target_pairs={{0,7},{1,6},{2,1},{3,0},{4,3},{5,2},{6,5},{7,4},{8,15},{9,14},{10,... | collective-permute-start | bytes 442376 | tf_op jit(solution)/shard_map/ppermute | solution.py:506
  57.1 7.1 %copy-start = (bf16[384,1536]{1,0:T(8,128)(2,1)S(1)}, bf16[384,1536]{1,0:T(8,128)(2,1)}, u32[]{:S(2)}) copy-start(bf16[384,1536]{1,0:T(8,128)(2,1)} %own_w.1) | copy-start | bytes 3538948
  57.1 7.1 %copy-start.4 = (bf16[256,384]{1,0:T(8,128)(2,1)S(1)}, bf16[256,384]{1,0:T(8,128)(2,1)}, u32[]{:S(2)}) copy-start(bf16[256,384]{1,0:T(8,128)(2,1)} %get-tuple-element.118.refs_9_.own_ug) | copy-start | bytes 589828
  57.1 7.1 %copy-start.6 = (s32[2]{0:T(128)S(1)}, s32[2]{0:T(128)}, u32[]{:S(2)}) copy-start(s32[2]{0:T(128)} %pad_add_fusion.place_ref.refs_0_) | copy-start | bytes 28
  57.1 7.1 %copy-start.7 = (f32[5]{0:T(128)S(1)}, f32[5]{0:T(128)}, u32[]{:S(2)}) copy-start(f32[5]{0:T(128)} %var_ref.1) | copy-start | bytes 64
  57.1 7.0 %copy-start.8 = (f32[32]{0:T(128)S(1)}, f32[32]{0:T(128)}, u32[]{:S(2)}) copy-start(f32[32]{0:T(128)} %constant.13.clone.lat_ref) | copy-start | bytes 388
  57.1 5.4 %collective-permute-start.19 = (bf16[112,1536]{1,0:T(8,128)(2,1)S(1)}, bf16[112,1536]{1,0:T(8,128)(2,1)S(1)}, u32[]{:S(2)}, u32[]{:S(2)}) collective-permute-start(bf16[112,1536]{1,0:T(8,128)(2,1)S(1)} %collective-permute-done.9.refs_11_.refs_1_), channel_id=1, source_target_pairs={{0,2},{2,0},{4,6},{6,4},{1,3},{3,1},{5,7},{7,5},{8,10},{10,8},{12,... | collective-permute-start | bytes 1032200 | tf_op jit(solution)/shard_map/ppermute | solution.py:442
  58.0 4.5 %collective-permute-start.20 = (bf16[112,1536]{1,0:T(8,128)(2,1)S(1)}, bf16[112,1536]{1,0:T(8,128)(2,1)S(1)}, u32[]{:S(2)}, u32[]{:S(2)}) collective-permute-start(bf16[112,1536]{1,0:T(8,128)(2,1)S(1)} %collective-permute-done.4.refs_14_.refs_4_), channel_id=1, source_target_pairs={{0,2},{2,0},{4,6},{6,4},{1,3},{3,1},{5,7},{7,5},{8,10},{10,8},{12,... | collective-permute-start | bytes 1032200 | tf_op jit(solution)/shard_map/ppermute | solution.py:442
  58.0 5.7 %collective-permute-start.21 = (bf16[112,1536]{1,0:T(8,128)(2,1)S(1)}, bf16[112,1536]{1,0:T(8,128)(2,1)S(1)}, u32[]{:S(2)}, u32[]{:S(2)}) collective-permute-start(bf16[112,1536]{1,0:T(8,128)(2,1)S(1)} %collective-permute-done.14.refs_15_.refs_5_), channel_id=1, source_target_pairs={{0,2},{2,0},{4,6},{6,4},{1,3},{3,1},{5,7},{7,5},{8,10},{10,8},{12,... | collective-permute-start | bytes 1032200 | tf_op jit(solution)/shard_map/ppermute | solution.py:442
  61.9 1.7 %collective-permute-start.22 = (bf16[112,1536]{1,0:T(8,128)(2,1)S(1)}, bf16[112,1536]{1,0:T(8,128)(2,1)S(1)}, u32[]{:S(2)}, u32[]{:S(2)}) collective-permute-start(bf16[112,1536]{1,0:T(8,128)(2,1)S(1)} %collective-permute-done.8.refs_18_.refs_8_), channel_id=1, source_target_pairs={{0,2},{2,0},{4,6},{6,4},{1,3},{3,1},{5,7},{7,5},{8,10},{10,8},{12,... | collective-permute-start | bytes 1032200 | tf_op jit(solution)/shard_map/ppermute | solution.py:442
  62.0 2.1 %collective-permute-start.23 = (bf16[112,1536]{1,0:T(8,128)(2,1)S(1)}, bf16[112,1536]{1,0:T(8,128)(2,1)S(1)}, u32[]{:S(2)}, u32[]{:S(2)}) collective-permute-start(bf16[112,1536]{1,0:T(8,128)(2,1)S(1)} %collective-permute-done.13.refs_19_.refs_9_), channel_id=1, source_target_pairs={{0,2},{2,0},{4,6},{6,4},{1,3},{3,1},{5,7},{7,5},{8,10},{10,8},{12,... | collective-permute-start | bytes 1032200 | tf_op jit(solution)/shard_map/ppermute | solution.py:442
  70.2 8.2 %collective-permute-start.24 = (bf16[40,1664]{1,0:T(8,128)(2,1)S(1)}, bf16[40,1664]{1,0:T(8,128)(2,1)S(1)}, u32[]{:S(2)}, u32[]{:S(2)}) collective-permute-start(bf16[40,1664]{1,0:T(8,128)(2,1)S(1)} %get-tuple-element.123), channel_id=1, source_target_pairs={{0,2},{2,0},{4,6},{6,4},{1,3},{3,1},{5,7},{7,5},{8,10},{10,8},{12,... | collective-permute-start | bytes 399368 | tf_op jit(solution)/shard_map/ppermute | solution.py:442
  70.4 8.0 %collective-permute-start.25 = (bf16[40,1664]{1,0:T(8,128)(2,1)S(1)}, bf16[40,1664]{1,0:T(8,128)(2,1)S(1)}, u32[]{:S(2)}, u32[]{:S(2)}) collective-permute-start(bf16[40,1664]{1,0:T(8,128)(2,1)S(1)} %get-tuple-element.124), channel_id=1, source_target_pairs={{0,4},{2,6},{4,0},{6,2},{1,5},{3,7},{5,1},{7,3},{8,12},{10,14},{12... | collective-permute-start | bytes 399368 | tf_op jit(solution)/shard_map/ppermute | solution.py:442
  72.1 6.5 %collective-permute-start.26 = (bf16[40,1664]{1,0:T(8,128)(2,1)S(1)}, bf16[40,1664]{1,0:T(8,128)(2,1)S(1)}, u32[]{:S(2)}, u32[]{:S(2)}) collective-permute-start(bf16[40,1664]{1,0:T(8,128)(2,1)S(1)} %get-tuple-element.125), channel_id=1, source_target_pairs={{0,6},{2,4},{4,2},{6,0},{1,7},{3,5},{5,3},{7,1},{8,14},{10,12},{12... | collective-permute-start | bytes 399368 | tf_op jit(solution)/shard_map/ppermute | solution.py:442
  79.3 4.5 %collective-permute-start.27 = (bf16[40,384]{1,0:T(8,128)(2,1)S(1)}, bf16[40,384]{1,0:T(8,128)(2,1)S(1)}, u32[]{:S(2)}, u32[]{:S(2)}) collective-permute-start(bf16[40,384]{1,0:T(8,128)(2,1)S(1)} %get-tuple-element.136), channel_id=1, source_target_pairs={{0,8},{8,0},{16,24},{24,16},{1,9},{9,1},{17,25},{25,17},{2,10},{10... | collective-permute-start | bytes 92168 | tf_op jit(solution)/shard_map/ppermute | solution.py:442
  80.9 4.8 %collective-permute-start.28 = (bf16[40,384]{1,0:T(8,128)(2,1)S(1)}, bf16[40,384]{1,0:T(8,128)(2,1)S(1)}, u32[]{:S(2)}, u32[]{:S(2)}) collective-permute-start(bf16[40,384]{1,0:T(8,128)(2,1)S(1)} %get-tuple-element.137), channel_id=1, source_target_pairs={{0,16},{8,24},{16,0},{24,8},{1,17},{9,25},{17,1},{25,9},{2,18},{10... | collective-permute-start | bytes 92168 | tf_op jit(solution)/shard_map/ppermute | solution.py:442
  82.6 5.7 %collective-permute-start.29 = (bf16[40,384]{1,0:T(8,128)(2,1)S(1)}, bf16[40,384]{1,0:T(8,128)(2,1)S(1)}, u32[]{:S(2)}, u32[]{:S(2)}) collective-permute-start(bf16[40,384]{1,0:T(8,128)(2,1)S(1)} %get-tuple-element.138), channel_id=1, source_target_pairs={{0,24},{8,16},{16,8},{24,0},{1,25},{9,17},{17,9},{25,1},{2,26},{10... | collective-permute-start | bytes 92168 | tf_op jit(solution)/shard_map/ppermute | solution.py:442
  88.4 4.7 %collective-permute-start.36 = (bf16[48,384]{1,0:T(8,128)(2,1)S(1)}, bf16[48,384]{1,0:T(8,128)(2,1)S(1)}, u32[]{:S(2)}, u32[]{:S(2)}) collective-permute-start(bf16[48,384]{1,0:T(8,128)(2,1)S(1)} %dp_sum.1.refs_1_), channel_id=1, source_target_pairs={{0,7},{1,6},{2,5},{3,4},{4,3},{5,2},{6,1},{7,0},{8,15},{9,14},{10,... | collective-permute-start | bytes 110600 | tf_op jit(solution)/shard_map/ppermute | solution.py:609
  88.5 5.5 %collective-permute-start.35 = (bf16[48,384]{1,0:T(8,128)(2,1)S(1)}, bf16[48,384]{1,0:T(8,128)(2,1)S(1)}, u32[]{:S(2)}, u32[]{:S(2)}) collective-permute-start(bf16[48,384]{1,0:T(8,128)(2,1)S(1)} %dp_sum.1.refs_1_), channel_id=1, source_target_pairs={{0,6},{1,7},{2,4},{3,5},{4,2},{5,3},{6,0},{7,1},{8,14},{9,15},{10,... | collective-permute-start | bytes 110600 | tf_op jit(solution)/shard_map/ppermute | solution.py:609
  90.4 4.9 %collective-permute-start.34 = (bf16[48,384]{1,0:T(8,128)(2,1)S(1)}, bf16[48,384]{1,0:T(8,128)(2,1)S(1)}, u32[]{:S(2)}, u32[]{:S(2)}) collective-permute-start(bf16[48,384]{1,0:T(8,128)(2,1)S(1)} %dp_sum.1.refs_1_), channel_id=1, source_target_pairs={{0,5},{1,4},{2,7},{3,6},{4,1},{5,0},{6,3},{7,2},{8,13},{9,12},{10,... | collective-permute-start | bytes 110600 | tf_op jit(solution)/shard_map/ppermute | solution.py:609
  92.6 4.0 %collective-permute-start.33 = (bf16[48,384]{1,0:T(8,128)(2,1)S(1)}, bf16[48,384]{1,0:T(8,128)(2,1)S(1)}, u32[]{:S(2)}, u32[]{:S(2)}) collective-permute-start(bf16[48,384]{1,0:T(8,128)(2,1)S(1)} %dp_sum.1.refs_1_), channel_id=1, source_target_pairs={{0,4},{1,5},{2,6},{3,7},{4,0},{5,1},{6,2},{7,3},{8,12},{9,13},{10,... | collective-permute-start | bytes 110600 | tf_op jit(solution)/shard_map/ppermute | solution.py:609
  93.1 3.4 %collective-permute-start.32 = (bf16[48,384]{1,0:T(8,128)(2,1)S(1)}, bf16[48,384]{1,0:T(8,128)(2,1)S(1)}, u32[]{:S(2)}, u32[]{:S(2)}) collective-permute-start(bf16[48,384]{1,0:T(8,128)(2,1)S(1)} %dp_sum.1.refs_1_), channel_id=1, source_target_pairs={{0,3},{1,2},{2,1},{3,0},{4,7},{5,6},{6,5},{7,4},{8,11},{9,10},{10,... | collective-permute-start | bytes 110600 | tf_op jit(solution)/shard_map/ppermute | solution.py:609
  93.1 3.4 %collective-permute-start.31 = (bf16[48,384]{1,0:T(8,128)(2,1)S(1)}, bf16[48,384]{1,0:T(8,128)(2,1)S(1)}, u32[]{:S(2)}, u32[]{:S(2)}) collective-permute-start(bf16[48,384]{1,0:T(8,128)(2,1)S(1)} %dp_sum.1.refs_1_), channel_id=1, source_target_pairs={{0,2},{1,3},{2,0},{3,1},{4,6},{5,7},{6,4},{7,5},{8,10},{9,11},{10,... | collective-permute-start | bytes 110600 | tf_op jit(solution)/shard_map/ppermute | solution.py:609
  94.0 4.0 %collective-permute-start.30 = (bf16[48,384]{1,0:T(8,128)(2,1)S(1)}, bf16[48,384]{1,0:T(8,128)(2,1)S(1)}, u32[]{:S(2)}, u32[]{:S(2)}) collective-permute-start(bf16[48,384]{1,0:T(8,128)(2,1)S(1)} %dp_sum.1.refs_1_), channel_id=1, source_target_pairs={{0,1},{1,0},{2,3},{3,2},{4,5},{5,4},{6,7},{7,6},{8,9},{9,8},{10,11... | collective-permute-start | bytes 110600 | tf_op jit(solution)/shard_map/ppermute | solution.py:609

commit v5 on v4

--- a/solution.py
+++ b/solution.py
@@ -175,10 +175,10 @@
 
 
 def lead_kernel(
-    place_ref, w_ref, unpatch_ref, gain_ref, x_ref, ug_ref, payload_ref, o0, o1, o2, o3,
+    w_ref, unpatch_ref, gain_ref, x_ref, ug_ref, payload_ref, o0, o1, o2, o3,
     u_in, x_in, sems,
 ):
-    part = place_ref[1]
+    part = lax.axis_index("lat")
     rows, width = w_ref.shape
     qr = rows // 4
     span = unpatch_ref.shape[0]
@@ -238,33 +238,36 @@
         ref[:, ref.shape[1] - EXTRA :] = extra[q * quarter : (q + 1) * quarter]
 
 
-def attention_kernel(last_ref, *refs):
-    ctx_ref = refs[12]
-    tiles = [refs[3 * q : 3 * q + 3] for q in range(4)]
-    is_last = last_ref[0] == 1
-    side = iota((128, 512), 0) // 64
-    same = side == (iota((128, 512), 1) % 128) // 64
-    keep = jnp.logical_or(same, jnp.logical_not(is_last))
+def attention_kernel(own_ref, east_ref, south_ref, diag_ref, ctx_ref):
+    tiles = (own_ref, east_ref, south_ref, diag_ref)
+    part = ctx_ref.shape[1]
+    is_last = lax.axis_index("lat") == lax.axis_size("lat") - 1
+    same = (iota((512, 128), 0) % 128) // 64 == iota((512, 128), 1) // 64
+    bias = jnp.where(jnp.logical_or(same, jnp.logical_not(is_last)), 0.0, -1e30)
     head = iota((128, 128), 1) // HDIM
     factor = math.log2(math.e) / math.sqrt(HDIM)
-    for w in range(2):
-        q, k, v = [
-            jnp.concatenate([tiles[c][i][32 * w : 32 * w + 32] for c in range(4)], axis=0)
-            for i in range(3)
-        ]
-        zero = jnp.zeros_like(k)
-        k4 = jnp.concatenate([jnp.where(head == h, k, zero) for h in range(4)], axis=0)
-        v4 = jnp.concatenate([jnp.where(head == h, v, zero) for h in range(4)], axis=0)
-        s = lax.dot_general(q, k4, (((1,), (1,)), ((), ())), preferred_element_type=F32)
-        s = jnp.where(keep, s, -1e30)
-        parts = []
-        for h in range(4):
-            sh = s[:, 128 * h : 128 * h + 128]
-            e = jnp.exp2((sh - jnp.max(sh, axis=1, keepdims=True)) * factor)
-            parts.append((e / jnp.sum(e, axis=1, keepdims=True)).astype(BF))
-        attn = jnp.concatenate(parts, axis=1)
-        out = jnp.dot(attn, v4, preferred_element_type=F32)
-        ctx_ref[128 * w : 128 * w + 128, :] = out.astype(BF)
+    for at in range(0, part, 128):
+        for w in range(2):
+            q, k, v = [
+                jnp.concatenate(
+                    [t[32 * w : 32 * w + 32, i * part + at : i * part + at + 128] for t in tiles],
+                    axis=0,
+                )
+                for i in range(3)
+            ]
+            zero = jnp.zeros_like(k)
+            k4 = jnp.concatenate([jnp.where(head == h, k, zero) for h in range(4)], axis=0)
+            v4 = jnp.concatenate([jnp.where(head == h, v, zero) for h in range(4)], axis=0)
+            s = lax.dot_general(k4, q, (((1,), (1,)), ((), ())), preferred_element_type=F32)
+            s = s + bias
+            parts = []
+            for h in range(4):
+                sh = s[128 * h : 128 * h + 128]
+                e = jnp.exp2((sh - jnp.max(sh, axis=0, keepdims=True)) * factor)
+                parts.append((e * (1.0 / jnp.sum(e, axis=0, keepdims=True))).astype(BF))
+            attn = jnp.concatenate(parts, axis=0)
+            out = lax.dot_general(attn, v4, (((0,), (0,)), ((), ())), preferred_element_type=F32)
+            ctx_ref[128 * w : 128 * w + 128, at : at + 128] = out.astype(BF)
 
 
 def piece_copies(zi, part, own_w, own_ug, pieces, w_all, ug_all, sems):
@@ -309,14 +312,14 @@
     return jnp.where(lane == 0, hi, jnp.where(lane == 1, mid, jnp.where(lane == 2, lo, 0.0)))
 
 
-def forward_kernel(place_ref, lat_ref, var_ref, *refs):
+def forward_kernel(lat_ref, var_ref, *refs):
     ctx_refs, refs = refs[: len(CHUNKS)], refs[len(CHUNKS) :]
     extras, refs = refs[:4], refs[4:]
     (own_w, own_ug), refs = refs[:2], refs[2:]
     pieces, refs = refs[:PIECES], refs[PIECES:]
     ts, refs = refs[:4], refs[4:]
     normed_ref, inv_ref, dfc_ref, hidden_ref, w_all, ug_all, term, sems = refs
-    zi, lat_place = place_ref[0], place_ref[1]
+    zi, lat_place = lax.axis_index("dp"), lax.axis_index("lat")
     w_copies, u_copies = piece_copies(zi, lat_place, own_w, own_ug, pieces, w_all, ug_all, sems)
     for c in w_copies + u_copies:
         c.start()
@@ -373,9 +376,9 @@
         ref[:, width:] = block
 
 
-def backward_kernel(place_ref, normed_ref, inv_ref, dfc_ref, own_w, own_ug, *refs):
+def backward_kernel(normed_ref, inv_ref, dfc_ref, own_w, own_ug, *refs):
     pieces, (out_ref, w_all, ug_all, sems) = refs[:PIECES], refs[PIECES:]
-    zi, part = place_ref[0], place_ref[1]
+    zi, part = lax.axis_index("dp"), lax.axis_index("lat")
     w_copies, u_copies = piece_copies(zi, part, own_w, own_ug, pieces, w_all, ug_all, sems)
     for c in u_copies + w_copies:
         c.start()
@@ -405,9 +408,9 @@
     return (a[...].astype(F32) + b[...].astype(F32)) + (c[...].astype(F32) + d[...].astype(F32))
 
 
-def lat_sum_kernel(place_ref, a, b, c, d, z0, z1, z2, z3, loss_ref, total_ref):
+def lat_sum_kernel(a, b, c, d, z0, z1, z2, z3, loss_ref, total_ref):
     total_ref[...] = add4(a, b, c, d)
-    zi = place_ref[0]
+    zi = lax.axis_index("dp")
     rows, width = z0.shape
     for k, ref in enumerate((z0, z1, z2, z3)):
         at = pl.multiple_of((zi ^ k) * width, 128)
@@ -424,9 +427,9 @@
     o_ref[rows:, :] = jnp.concatenate([block, zeros], axis=1).astype(BF)
 
 
-def join_kernel(counts, place_ref, *refs):
+def join_kernel(counts, *refs):
     pieces, (o_ref, loss_ref) = refs[:8], refs[8:]
-    lat_place = place_ref[1]
+    lat_place = lax.axis_index("lat")
     rows = o_ref.shape[0] // 4
     for a in range(4):
         at = pl.multiple_of((lat_place ^ a) * rows, 8)
@@ -453,9 +456,6 @@
     span = unpatch_matrix.shape[1]
     tokens = levels * 64
     quarter = tokens // 4
-    lat_place = lax.axis_index("lat")
-    place = jnp.stack([lax.axis_index("dp"), lat_place]).astype(jnp.int32)
-    last = (lat_place == lat - 1).astype(jnp.int32).reshape(1)
     lat_total = 8 * lat
     angle = math.pi * ((np.arange(lat_total) + 0.5) / lat_total - 0.5)
     cosine = np.cos(angle)
@@ -469,7 +469,7 @@
         lead_kernel,
         out_shape=[shape((UGROWS, rows), BF), shape((rows // 4 + 16, width), BF)]
         + [shape((quarter, widths[0]), BF)] * 4,
-        in_specs=[SMEM, HBM, HBM, VMEM, HBM],
+        in_specs=[HBM, HBM, VMEM, HBM],
         out_specs=[VMEM] * 6,
         scratch_shapes=[
             pltpu.VMEM((span, rows), BF),
@@ -478,7 +478,7 @@
         ],
         compiler_params=params(62),
         name="lead",
-    )(place, w_out, unpatch_matrix.T, norm_gain, x)
+    )(w_out, unpatch_matrix.T, norm_gain, x)
     ring1 = from_behind(payload, "dp", 1)
     later = sum(parts_of[1:])
     packed += pl.pallas_call(
@@ -508,19 +508,14 @@
 
     def attend(*chunk):
         part = chunk[0].shape[1] // 384 * 128
-        groups = part // 128
-        specs = [
-            pl.BlockSpec((quarter, 128), lambda g, i=i: (0, i * groups + g)) for i in range(3)
-        ]
         return pl.pallas_call(
             attention_kernel,
-            grid=(groups,),
             out_shape=shape((tokens, part), BF),
-            in_specs=[SMEM] + specs * 4,
-            out_specs=pl.BlockSpec((tokens, 128), lambda g: (0, g)),
+            in_specs=[VMEM] * 4,
+            out_specs=VMEM,
             compiler_params=params(8),
             name="attention",
-        )(last, *[t for t in chunk for _ in range(3)])
+        )(*chunk)
 
     owns = packed[0::4]
     sends = [packed[4 * g + 1 : 4 * g + 4] for g in range(len(CHUNKS))]
@@ -539,9 +534,10 @@
     ctx1 = attend(owns[1], *tiles1)
     ring3_after, ctx1, *tiles2 = barrier((ring3, ctx1, *tiles2))
     across3 = swap(ring3_after, "lat", 2)
-    *sends[3], across2, tiles2[0] = barrier((*sends[3], across2, tiles2[0]))
+    *sends[3], tiles2[0] = barrier((*sends[3], tiles2[0]))
     tiles3 = halo(*sends[3])
     ctx2 = attend(owns[2], *tiles2)
+    ring1, across1, tiles3[0] = barrier((ring1, across1, tiles3[0]))
     ctx3 = attend(owns[3], *tiles3)
     across3, ctx2, ctx3 = barrier((across3, ctx2, ctx3))
     pieces = []
@@ -560,36 +556,36 @@
         grid=(1,),
         out_shape=[shape((piece, width + 128), BF)] * 4
         + [shape((tokens, width), F32), shape((tokens, 128), F32), shape((tokens, span), BF)],
-        in_specs=[SMEM] * 3 + [VMEM] * len(CHUNKS) + [extra_spec] * 4 + [HBM] + [ANY] * (1 + PIECES),
+        in_specs=[SMEM] * 2 + [VMEM] * len(CHUNKS) + [extra_spec] * 4 + [HBM] + [ANY] * (1 + PIECES),
         out_specs=[VMEM] * 7,
         scratch_shapes=[pltpu.VMEM((tokens, width), BF)]
         + assembly
         + [pltpu.VMEM((span, width), F32), pltpu.SemaphoreType.DMA((copies,))],
         compiler_params=params(28),
         name="forward",
-    )(place, lat_table, var_weight, ctx0, ctx1, ctx2, ctx3, owns[2], *tiles2, w_out, ug, *pieces)
+    )(lat_table, var_weight, ctx0, ctx1, ctx2, ctx3, owns[2], *tiles2, w_out, ug, *pieces)
 
     terms = [terms[0]] + [swap(terms[b], "lat", b) for b in (1, 2, 3)]
     grad_context = pl.pallas_call(
         backward_kernel,
         out_shape=shape((tokens, width), BF),
-        in_specs=[SMEM] + [VMEM] * 3 + [HBM] + [ANY] * (1 + PIECES),
+        in_specs=[VMEM] * 3 + [HBM] + [ANY] * (1 + PIECES),
         out_specs=VMEM,
         scratch_shapes=assembly + [pltpu.SemaphoreType.DMA((copies,))],
         compiler_params=params(24),
         name="backward",
-    )(place, normed, inv, dfc, w_out, ug, *pieces)
+    )(normed, inv, dfc, w_out, ug, *pieces)
     *terms, grad_context = barrier((*terms, grad_context))
 
     *parts, loss = pl.pallas_call(
         lat_sum_kernel,
         out_shape=[shape((piece, rows), BF)] * 4 + [shape((8, 128), F32)],
-        in_specs=[SMEM] + [VMEM] * 4,
+        in_specs=[VMEM] * 4,
         out_specs=[VMEM] * 5,
         scratch_shapes=[pltpu.VMEM((piece, width + 128), F32)],
         compiler_params=params(4),
         name="lat_sum",
-    )(place, *terms)
+    )(*terms)
     parts = [parts[0]] + [swap(parts[k], "dp", k) for k in (1, 2, 3)]
     mine = pl.pallas_call(
         dp_sum_kernel,
@@ -612,11 +608,11 @@
     joined, loss = pl.pallas_call(
         lambda *refs: join_kernel(counts, *refs),
         out_shape=[shape((span, rows), F32), shape((1, 1), F32)],
-        in_specs=[SMEM] + [VMEM] * 8,
+        in_specs=[VMEM] * 8,
         out_specs=[VMEM] * 2,
         compiler_params=params(4),
         name="join",
-    )(place, *plane)
+    )(*plane)
     return grad_context.reshape(1, levels, 8, 8, width), joined.T, loss.reshape(1)
 
 

time: 99.4 us -> 96.6 us (0.972)
  Pallas kernels: 33.7 us -> 25 us
  waiting for transfers between devices: 29 us -> 33.4 us
  local copies, waits for them, and re-layouts: 0.98 us -> 2.8 us
    ppermute x11, waiting for transfers between devices: 12.6 us -> 21.4 us  [from_behind(): lax.ppermute(array, axis, [(i, (i + by) % length) for i in range(length)])]
    pallas_call x4, Pallas kernels: 11.5 us -> 4.54 us  [attend(): pl.pallas_call(attention_kernel, out_shape=shape((tokens, part), BF), in_...]
    ppermute x15, waiting for transfers between devices: 11 us -> 6.67 us  [swap(): lax.ppermute(array, axis, [(i, i ^ bit) for i in range(lax.axis_size(axis...]
    ppermute x4, starting transfers between devices: 4.96 us -> 2.39 us  [halo(): lax.ppermute(diag, ('lat', 'lon'), corner)]
    unnamed x24 -> x18, local copies, waits for them, and re-layouts: 0.98 us -> 2.8 us
    ppermute x11, starting transfers between devices: 10.2 us -> 11.9 us  [from_behind(): lax.ppermute(array, axis, [(i, (i + by) % length) for i in range(length)])]
    ppermute x15, starting transfers between devices: 12 us -> 13.2 us  [swap(): lax.ppermute(array, axis, [(i, i ^ bit) for i in range(lax.axis_size(axis...]
  transfers between devices with their start and end apart: 37 -> 37, of which waited for: 15 -> 15; matrix products, arithmetic and copies ran while one was open for 0% -> 0% of each run, Pallas kernels for 23% -> 15%
where the time goes in v5:
time: 96.6 us; the launch traced here: 96.4 us
  starting transfers between devices  34.4 us (36%)
  waiting for transfers between devices  33.4 us (35%)
  Pallas kernels  25 us (26%)
  local copies, waits for them, and re-layouts  2.8 us (3%)
    ppermute x11, waiting for transfers between devices, from_behind(): lax.ppermute(array, axis, [(i, (i + by) % length) for i in range(length)])  21.4 us
    ppermute x15, starting transfers between devices, swap(): lax.ppermute(array, axis, [(i, i ^ bit) for i in range(lax.axis_size(axis...  13.2 us
    ppermute x11, starting transfers between devices, from_behind(): lax.ppermute(array, axis, [(i, (i + by) % length) for i in range(length)])  11.9 us
    ppermute x7, starting transfers between devices, shards(): plane.append(lax.ppermute(mine, ('lat', 'lon'), pairs))  6.87 us
    ppermute x15, waiting for transfers between devices, swap(): lax.ppermute(array, axis, [(i, i ^ bit) for i in range(lax.axis_size(axis...  6.67 us
    pallas_call x1, Pallas kernels, shards(): pl.pallas_call(forward_kernel, grid=(1,), out_shape=[shape((piece, width...  6.02 us
    pallas_call x1, Pallas kernels, shards(): pl.pallas_call(backward_kernel, out_shape=shape((tokens, width), BF), in_...  5.67 us
    pallas_call x1, Pallas kernels, shards(): pl.pallas_call(pack_kernel, out_shape=[shape((quarter, w), BF) for w in w...  4.7 us
  transfers between devices with their start and end apart: 37, of which 15 were waited for; matrix products, arithmetic and copies ran while one was open for 0% of the time, Pallas kernels for 15%

profile of v5, /device:TPU:0, one launch (start us, length us, event | category | flops | bytes accessed | tf_op | source)
XLA Modules:
  0.0 96.4 jit_solution(8730910518482459924)
XLA Ops:
  0.6 3.1 %lead.1 = (bf16[256,384]{1,0:T(8,128)(2,1)}, bf16[112,1536]{1,0:T(8,128)(2,1)}, bf16[64,384]{1,0:T(8,128)(2,1)}, bf16[64,384]{1,0:T(8,128)(2,1)}, bf16[64,384]{1,0:T(8,128)(2,1)}, /*index=5*/bf16[64,384]{1,0:T(8,128)(2,1)}) custom-call(bf16[384,1536]{1,0:T(8,128)(2,1)} %own_w.1, bf16[160,384]{1,0:T(8,128)(2,1)} %bitcast.10, bf16[384]{0:T(512)(128)(2,1)} %gain_ref.1, ...), custom_call_target="tpu_custom_call" | custom-call | tf_op jit(solution)/shard_map/lead/pallas_call | solution.py:468
  3.8 3.1 %collective-permute-start = (bf16[112,1536]{1,0:T(8,128)(2,1)}, bf16[112,1536]{1,0:T(8,128)(2,1)S(1)}, u32[]{:S(2)}, u32[]{:S(2)}) collective-permute-start(bf16[112,1536]{1,0:T(8,128)(2,1)} %get-tuple-element.74), channel_id=1, source_target_pairs={{0,8},{8,16},{16,24},{24,0},{1,9},{9,17},{17,25},{25,1},{2,10},{10... | collective-permute-start | bytes 1032200 | tf_op jit(solution)/shard_map/ppermute | solution.py:30
  6.9 1.5 %collective-permute-start.1 = (bf16[64,384]{1,0:T(8,128)(2,1)}, bf16[64,384]{1,0:T(8,128)(2,1)S(1)}, u32[]{:S(2)}, u32[]{:S(2)}) collective-permute-start(bf16[64,384]{1,0:T(8,128)(2,1)} %get-tuple-element.76), channel_id=1, source_target_pairs={{0,1},{1,0},{2,3},{3,2},{4,5},{5,4},{6,7},{7,6},{8,9},{9,8},{10,11... | collective-permute-start | bytes 147464 | tf_op jit(solution)/shard_map/ppermute | solution.py:30
  8.3 0.4 collective-permute-start.2
  8.7 1.2 %collective-permute-start.3 = (bf16[64,384]{1,0:T(8,128)(2,1)}, bf16[64,384]{1,0:T(8,128)(2,1)S(1)}, u32[]{:S(2)}, u32[]{:S(2)}) collective-permute-start(bf16[64,384]{1,0:T(8,128)(2,1)} %get-tuple-element.78), channel_id=1, source_target_pairs={{0,7},{1,6},{2,1},{3,0},{4,3},{5,2},{6,5},{7,4},{8,15},{9,14},{10,... | collective-permute-start | bytes 147464 | tf_op jit(solution)/shard_map/ppermute | solution.py:506
  10.0 4.7 %pack.1 = (bf16[64,1536]{1,0:T(8,128)(2,1)}, bf16[64,1536]{1,0:T(8,128)(2,1)}, bf16[64,1536]{1,0:T(8,128)(2,1)}, bf16[64,1536]{1,0:T(8,128)(2,1)}, bf16[64,1792]...) custom-call(bf16[4,8,8,4608]{3,2,1,0:T(8,128)(2,1)} %bitcast.7, ...), custom_call_target="tpu_custom_call" | custom-call | tf_op jit(solution)/shard_map/pack/pallas_call | solution.py:484
  14.7 0.0 collective-permute-done.1.east_ref
  14.7 0.0 collective-permute-done.3.diag_ref
  14.7 2.5 %collective-permute-done.refs_10_.refs_0_ = bf16[112,1536]{1,0:T(8,128)(2,1)S(1)} collective-permute-done((bf16[112,1536]{1,0:T(8,128)(2,1)}, bf16[112,1536]{1,0:T(8,128)(2,1)S(1)}, u32[]{:S(2)}, u32[]{:S(2)}) %collective-permute-start) | collective-permute-done | bytes 344096 | tf_op jit(solution)/shard_map/ppermute | solution.py:30
  17.2 1.5 %collective-permute-start.9 = (bf16[112,1536]{1,0:T(8,128)(2,1)S(1)}, bf16[112,1536]{1,0:T(8,128)(2,1)S(1)}, u32[]{:S(2)}, u32[]{:S(2)}) collective-permute-start(bf16[112,1536]{1,0:T(8,128)(2,1)S(1)} %collective-permute-done.refs_10_.refs_0_), channel_id=1, source_target_pairs={{0,4},{2,6},{4,0},{6,2},{1,5},{3,7},{5,1},{7,3},{8,12},{10,14},{12... | collective-permute-start | bytes 1032200 | tf_op jit(solution)/shard_map/ppermute | solution.py:445
  18.7 1.5 %collective-permute-start.5 = (bf16[64,1536]{1,0:T(8,128)(2,1)}, bf16[64,1536]{1,0:T(8,128)(2,1)S(1)}, u32[]{:S(2)}, u32[]{:S(2)}) collective-permute-start(bf16[64,1536]{1,0:T(8,128)(2,1)} %get-tuple-element.88), channel_id=1, source_target_pairs={{0,1},{1,0},{2,3},{3,2},{4,5},{5,4},{6,7},{7,6},{8,9},{9,8},{10,11... | collective-permute-start | bytes 589832 | tf_op jit(solution)/shard_map/ppermute | solution.py:30
  20.2 0.6 collective-permute-start.7
  20.8 0.8 attention.4.refs_0_
  21.6 0.0 copy-start
  21.6 4.1 %collective-permute-done.5.east_ref = bf16[64,1536]{1,0:T(8,128)(2,1)S(1)} collective-permute-done((bf16[64,1536]{1,0:T(8,128)(2,1)}, bf16[64,1536]{1,0:T(8,128)(2,1)S(1)}, u32[]{:S(2)}, u32[]{:S(2)}) %collective-permute-start.5) | collective-permute-done | bytes 196640 | tf_op jit(solution)/shard_map/ppermute | solution.py:30
  25.7 3.8 %collective-permute-done.6.south_ref = bf16[64,1536]{1,0:T(8,128)(2,1)S(1)} collective-permute-done((bf16[64,1536]{1,0:T(8,128)(2,1)}, bf16[64,1536]{1,0:T(8,128)(2,1)S(1)}, u32[]{:S(2)}, u32[]{:S(2)}) %collective-permute-start.6) | collective-permute-done | bytes 196640 | tf_op jit(solution)/shard_map/ppermute | solution.py:30
  29.5 0.9 collective-permute-start.8
  30.5 1.5 %collective-permute-start.10 = (bf16[64,1792]{1,0:T(8,128)(2,1)}, bf16[64,1792]{1,0:T(8,128)(2,1)S(1)}, u32[]{:S(2)}, u32[]{:S(2)}) collective-permute-start(bf16[64,1792]{1,0:T(8,128)(2,1)} %get-tuple-element.101), channel_id=1, source_target_pairs={{0,1},{1,0},{2,3},{3,2},{4,5},{5,4},{6,7},{7,6},{8,9},{9,8},{10,11... | collective-permute-start | bytes 688136 | tf_op jit(solution)/shard_map/ppermute | solution.py:30
  32.0 1.2 %collective-permute-start.11 = (bf16[64,1792]{1,0:T(8,128)(2,1)}, bf16[64,1792]{1,0:T(8,128)(2,1)S(1)}, u32[]{:S(2)}, u32[]{:S(2)}) collective-permute-start(bf16[64,1792]{1,0:T(8,128)(2,1)} %get-tuple-element.102), channel_id=1, source_target_pairs={{0,6},{2,0},{4,2},{6,4},{1,7},{3,1},{5,3},{7,5},{8,14},{10,8},{12,... | collective-permute-start | bytes 688136 | tf_op jit(solution)/shard_map/ppermute | solution.py:30
  33.2 0.9 collective-permute-start.19
  34.1 0.9 copy-done.4
  35.0 1.3 %attention.5.refs_1_ = bf16[256,512]{1,0:T(8,128)(2,1)S(1)} custom-call(bf16[64,1536]{1,0:T(8,128)(2,1)S(1)} %copy-done.4, bf16[64,1536]{1,0:T(8,128)(2,1)S(1)} %collective-permute-done.5.east_ref, bf16[64,1536]{1,0:T(8,128)(2,1)S(1)} %collective-permute-done.6.south_ref, bf16[64,1536]{1,0:T(8,128)(2,1)S(1)} %collective-permute-done.7.diag_ref), custom_call_target="tpu_custom_call" | custom-call | tf_op jit(solution)/shard_map/attention/pallas_call | solution.py:511
  36.3 2.8 %collective-permute-done.10.east_ref.refs_5_ = bf16[64,1792]{1,0:T(8,128)(2,1)S(1)} collective-permute-done((bf16[64,1792]{1,0:T(8,128)(2,1)}, bf16[64,1792]{1,0:T(8,128)(2,1)S(1)}, u32[]{:S(2)}, u32[]{:S(2)}) %collective-permute-start.10) | collective-permute-done | bytes 229408 | tf_op jit(solution)/shard_map/ppermute | solution.py:30
  39.1 1.2 %collective-permute-done.11.south_ref.refs_6_ = bf16[64,1792]{1,0:T(8,128)(2,1)S(1)} collective-permute-done((bf16[64,1792]{1,0:T(8,128)(2,1)}, bf16[64,1792]{1,0:T(8,128)(2,1)S(1)}, u32[]{:S(2)}, u32[]{:S(2)}) %collective-permute-start.11) | collective-permute-done | bytes 229408 | tf_op jit(solution)/shard_map/ppermute | solution.py:30
  40.3 2.6 %collective-permute-done.12.diag_ref.refs_7_ = bf16[64,1792]{1,0:T(8,128)(2,1)S(1)} collective-permute-done((bf16[64,1792]{1,0:T(8,128)(2,1)}, bf16[64,1792]{1,0:T(8,128)(2,1)S(1)}, u32[]{:S(2)}, u32[]{:S(2)}) %collective-permute-start.12) | collective-permute-done | bytes 229408 | tf_op jit(solution)/shard_map/ppermute | solution.py:506
  42.9 1.6 %collective-permute-start.13 = (bf16[112,1536]{1,0:T(8,128)(2,1)S(1)}, bf16[112,1536]{1,0:T(8,128)(2,1)S(1)}, u32[]{:S(2)}, u32[]{:S(2)}) collective-permute-start(bf16[112,1536]{1,0:T(8,128)(2,1)S(1)} %collective-permute-done.8.refs_18_.refs_8_), channel_id=1, source_target_pairs={{0,4},{2,6},{4,0},{6,2},{1,5},{3,7},{5,1},{7,3},{8,12},{10,14},{12... | collective-permute-start | bytes 1032200 | tf_op jit(solution)/shard_map/ppermute | solution.py:445
  44.6 0.0 collective-permute-start.20
  44.6 1.5 %collective-permute-start.14 = (bf16[64,1152]{1,0:T(8,128)(2,1)}, bf16[64,1152]{1,0:T(8,128)(2,1)S(1)}, u32[]{:S(2)}, u32[]{:S(2)}) collective-permute-start(bf16[64,1152]{1,0:T(8,128)(2,1)} %get-tuple-element.116), channel_id=1, source_target_pairs={{0,1},{1,0},{2,3},{3,2},{4,5},{5,4},{6,7},{7,6},{8,9},{9,8},{10,11... | collective-permute-start | bytes 442376 | tf_op jit(solution)/shard_map/ppermute | solution.py:30
  46.1 0.3 collective-permute-start.15
  46.4 4.6 %collective-permute-done.14.east_ref = bf16[64,1152]{1,0:T(8,128)(2,1)S(1)} collective-permute-done((bf16[64,1152]{1,0:T(8,128)(2,1)}, bf16[64,1152]{1,0:T(8,128)(2,1)S(1)}, u32[]{:S(2)}, u32[]{:S(2)}) %collective-permute-start.14) | collective-permute-done | bytes 147488 | tf_op jit(solution)/shard_map/ppermute | solution.py:30
  51.0 0.6 collective-permute-start.16
  51.6 0.9 copy-done.1
  52.6 1.3 %attention.6.refs_2_ = bf16[256,512]{1,0:T(8,128)(2,1)S(1)} custom-call(bf16[64,1792]{1,0:T(8,128)(2,1)S(1)} %copy-done.1, bf16[64,1792]{1,0:T(8,128)(2,1)S(1)} %collective-permute-done.10.east_ref.refs_5_, bf16[64,1792]{1,0:T(8,128)(2,1)S(1)} %collective-permute-done.11.south_ref.refs_6_, bf16[64,1792]{1,0:T(8,128)(2,1)S(1)} %collective-permute-done.12.diag_ref.refs_7_), custom_call_target="tpu_custom_call" | custom-call | tf_op jit(solution)/shard_map/attention/pallas_call | solution.py:511
  53.9 1.1 %collective-permute-start.22 = (bf16[112,1536]{1,0:T(8,128)(2,1)S(1)}, bf16[112,1536]{1,0:T(8,128)(2,1)S(1)}, u32[]{:S(2)}, u32[]{:S(2)}) collective-permute-start(bf16[112,1536]{1,0:T(8,128)(2,1)S(1)} %collective-permute-done.8.refs_18_.refs_8_), channel_id=1, source_target_pairs={{0,2},{2,0},{4,6},{6,4},{1,3},{3,1},{5,7},{7,5},{8,10},{10,8},{12,... | collective-permute-start | bytes 1032200 | tf_op jit(solution)/shard_map/ppermute | solution.py:445
  55.0 2.4 %collective-permute-done.15.south_ref = bf16[64,1152]{1,0:T(8,128)(2,1)S(1)} collective-permute-done((bf16[64,1152]{1,0:T(8,128)(2,1)}, bf16[64,1152]{1,0:T(8,128)(2,1)S(1)}, u32[]{:S(2)}, u32[]{:S(2)}) %collective-permute-start.15) | collective-permute-done | bytes 147488 | tf_op jit(solution)/shard_map/ppermute | solution.py:30
  57.4 0.7 collective-permute-start.21
  58.1 0.0 collective-permute-start.17
  58.1 0.9 copy-done.5
  59.0 1.1 %attention.7.refs_3_ = bf16[256,384]{1,0:T(8,128)(2,1)S(1)} custom-call(bf16[64,1152]{1,0:T(8,128)(2,1)S(1)} %copy-done.5, bf16[64,1152]{1,0:T(8,128)(2,1)S(1)} %collective-permute-done.14.east_ref, bf16[64,1152]{1,0:T(8,128)(2,1)S(1)} %collective-permute-done.15.south_ref, bf16[64,1152]{1,0:T(8,128)(2,1)S(1)} %collective-permute-done.16.diag_ref), custom_call_target="tpu_custom_call" | custom-call | tf_op jit(solution)/shard_map/attention/pallas_call | solution.py:511
  60.2 0.6 collective-permute-start.18
  60.8 0.1 collective-permute-start.23
  60.9 1.2 %collective-permute-done.18.refs_13_.refs_3_ = bf16[112,1536]{1,0:T(8,128)(2,1)S(1)} collective-permute-done((bf16[112,1536]{1,0:T(8,128)(2,1)S(1)}, bf16[112,1536]{1,0:T(8,128)(2,1)S(1)}, u32[]{:S(2)}, u32[]{:S(2)}) %collective-permute-start.18) | collective-permute-done | bytes 344096 | tf_op jit(solution)/shard_map/ppermute | solution.py:445
  62.0 0.5 collective-permute-done.23.refs_21_.refs_11_
  62.5 6.0 %forward.1 = (bf16[40,1664]{1,0:T(8,128)(2,1)S(1)}, bf16[40,1664]{1,0:T(8,128)(2,1)S(1)}, bf16[40,1664]{1,0:T(8,128)(2,1)S(1)}, bf16[40,1664]{1,0:T(8,128)(2,1)S...) custom-call(f32[32]{0:T(128)S(1)} %copy-done.8, f32[5]{0:T(128)S(1)} %copy-done.7, ...), custom_call_target="tpu_custom_call" | custom-call | tf_op jit(solution)/shard_map/forward/pallas_call | solution.py:554
  68.6 0.4 collective-permute-start.24
  69.0 1.5 %collective-permute-start.25 = (bf16[40,1664]{1,0:T(8,128)(2,1)S(1)}, bf16[40,1664]{1,0:T(8,128)(2,1)S(1)}, u32[]{:S(2)}, u32[]{:S(2)}) collective-permute-start(bf16[40,1664]{1,0:T(8,128)(2,1)S(1)} %get-tuple-element.128), channel_id=1, source_target_pairs={{0,4},{2,6},{4,0},{6,2},{1,5},{3,7},{5,1},{7,3},{8,12},{10,14},{12... | collective-permute-start | bytes 399368 | tf_op jit(solution)/shard_map/ppermute | solution.py:445
  70.5 0.0 collective-permute-start.26
  70.5 5.7 %backward.1 = bf16[256,1536]{1,0:T(8,128)(2,1)} custom-call(f32[256,1536]{1,0:T(8,128)S(1)} %get-tuple-element.130.normed_ref, f32[256,128]{1,0:T(8,128)S(1)} %get-tuple-element.131.inv_ref, bf16[256,160]{1,0:T(8,128)(2,1)S(1)} %get-tuple-element.132.dfc_ref, bf16[384,1536]{1,0:T(8,128)(2,1)S(1)} %copy-done, bf16[256,384]{1,0:T(8,128)(2,1)S(1)} %copy-done.3, ...), custom_call_target="tpu_custom_call" | custom-call | tf_op jit(solution)/shard_map/backward/pallas_call | solution.py:569
  76.2 0.4 collective-permute-done.26.d
  76.6 0.2 lat_sum.1
  76.8 1.6 %collective-permute-start.27 = (bf16[40,384]{1,0:T(8,128)(2,1)S(1)}, bf16[40,384]{1,0:T(8,128)(2,1)S(1)}, u32[]{:S(2)}, u32[]{:S(2)}) collective-permute-start(bf16[40,384]{1,0:T(8,128)(2,1)S(1)} %get-tuple-element.140), channel_id=1, source_target_pairs={{0,8},{8,0},{16,24},{24,16},{1,9},{9,1},{17,25},{25,17},{2,10},{10... | collective-permute-start | bytes 92168 | tf_op jit(solution)/shard_map/ppermute | solution.py:445
  78.4 1.9 %collective-permute-start.28 = (bf16[40,384]{1,0:T(8,128)(2,1)S(1)}, bf16[40,384]{1,0:T(8,128)(2,1)S(1)}, u32[]{:S(2)}, u32[]{:S(2)}) collective-permute-start(bf16[40,384]{1,0:T(8,128)(2,1)S(1)} %get-tuple-element.141), channel_id=1, source_target_pairs={{0,16},{8,24},{16,0},{24,8},{1,17},{9,25},{17,1},{25,9},{2,18},{10... | collective-permute-start | bytes 92168 | tf_op jit(solution)/shard_map/ppermute | solution.py:445
  80.3 1.1 %collective-permute-start.29 = (bf16[40,384]{1,0:T(8,128)(2,1)S(1)}, bf16[40,384]{1,0:T(8,128)(2,1)S(1)}, u32[]{:S(2)}, u32[]{:S(2)}) collective-permute-start(bf16[40,384]{1,0:T(8,128)(2,1)S(1)} %get-tuple-element.142), channel_id=1, source_target_pairs={{0,24},{8,16},{16,8},{24,0},{1,25},{9,17},{17,9},{25,1},{2,26},{10... | collective-permute-start | bytes 92168 | tf_op jit(solution)/shard_map/ppermute | solution.py:445
  81.5 1.9 %collective-permute-done.28.c = bf16[40,384]{1,0:T(8,128)(2,1)S(1)} collective-permute-done((bf16[40,384]{1,0:T(8,128)(2,1)S(1)}, bf16[40,384]{1,0:T(8,128)(2,1)S(1)}, u32[]{:S(2)}, u32[]{:S(2)}) %collective-permute-start.28) | collective-permute-done | bytes 30752 | tf_op jit(solution)/shard_map/ppermute | solution.py:445
  83.4 2.6 %collective-permute-done.29.d = bf16[40,384]{1,0:T(8,128)(2,1)S(1)} collective-permute-done((bf16[40,384]{1,0:T(8,128)(2,1)S(1)}, bf16[40,384]{1,0:T(8,128)(2,1)S(1)}, u32[]{:S(2)}, u32[]{:S(2)}) %collective-permute-start.29) | collective-permute-done | bytes 30752 | tf_op jit(solution)/shard_map/ppermute | solution.py:445
  86.1 0.1 collective-permute-start.36
  86.2 1.9 %collective-permute-start.35 = (bf16[48,384]{1,0:T(8,128)(2,1)S(1)}, bf16[48,384]{1,0:T(8,128)(2,1)S(1)}, u32[]{:S(2)}, u32[]{:S(2)}) collective-permute-start(bf16[48,384]{1,0:T(8,128)(2,1)S(1)} %dp_sum.1.refs_0_), channel_id=1, source_target_pairs={{0,6},{1,7},{2,4},{3,5},{4,2},{5,3},{6,0},{7,1},{8,14},{9,15},{10,... | collective-permute-start | bytes 110600 | tf_op jit(solution)/shard_map/ppermute | solution.py:605
  88.1 2.2 %collective-permute-start.34 = (bf16[48,384]{1,0:T(8,128)(2,1)S(1)}, bf16[48,384]{1,0:T(8,128)(2,1)S(1)}, u32[]{:S(2)}, u32[]{:S(2)}) collective-permute-start(bf16[48,384]{1,0:T(8,128)(2,1)S(1)} %dp_sum.1.refs_0_), channel_id=1, source_target_pairs={{0,5},{1,4},{2,7},{3,6},{4,1},{5,0},{6,3},{7,2},{8,13},{9,12},{10,... | collective-permute-start | bytes 110600 | tf_op jit(solution)/shard_map/ppermute | solution.py:605
  90.3 0.5 collective-permute-start.33
  90.8 0.9 collective-permute-start.31
  91.7 1.3 %collective-permute-start.30 = (bf16[48,384]{1,0:T(8,128)(2,1)S(1)}, bf16[48,384]{1,0:T(8,128)(2,1)S(1)}, u32[]{:S(2)}, u32[]{:S(2)}) collective-permute-start(bf16[48,384]{1,0:T(8,128)(2,1)S(1)} %dp_sum.1.refs_0_), channel_id=1, source_target_pairs={{0,1},{1,0},{2,3},{3,2},{4,5},{5,4},{6,7},{7,6},{8,9},{9,8},{10,11... | collective-permute-start | bytes 110600 | tf_op jit(solution)/shard_map/ppermute | solution.py:605
  93.0 1.3 %collective-permute-done.33.refs_4_ = bf16[48,384]{1,0:T(8,128)(2,1)S(1)} collective-permute-done((bf16[48,384]{1,0:T(8,128)(2,1)S(1)}, bf16[48,384]{1,0:T(8,128)(2,1)S(1)}, u32[]{:S(2)}, u32[]{:S(2)}) %collective-permute-start.33) | collective-permute-done | bytes 36896 | tf_op jit(solution)/shard_map/ppermute | solution.py:605
  94.3 1.4 %collective-permute-done.30.refs_1_ = bf16[48,384]{1,0:T(8,128)(2,1)S(1)} collective-permute-done((bf16[48,384]{1,0:T(8,128)(2,1)S(1)}, bf16[48,384]{1,0:T(8,128)(2,1)S(1)}, u32[]{:S(2)}, u32[]{:S(2)}) %collective-permute-start.30) | collective-permute-done | bytes 36896 | tf_op jit(solution)/shard_map/ppermute | solution.py:605
  95.7 0.7 join.1
  (39 shorter events, 0.1 us)
Async XLA Ops:
  3.8 17.0 %copy-start.6 = (bf16[64,384]{1,0:T(8,128)(2,1)S(1)}, bf16[64,384]{1,0:T(8,128)(2,1)}, u32[]{:S(2)}) copy-start(bf16[64,384]{1,0:T(8,128)(2,1)} %get-tuple-element.80.own_ref) | copy-start | bytes 147460
  3.8 13.4 %collective-permute-start = (bf16[112,1536]{1,0:T(8,128)(2,1)}, bf16[112,1536]{1,0:T(8,128)(2,1)S(1)}, u32[]{:S(2)}, u32[]{:S(2)}) collective-permute-start(bf16[112,1536]{1,0:T(8,128)(2,1)} %get-tuple-element.74), channel_id=1, source_target_pairs={{0,8},{8,16},{16,24},{24,0},{1,9},{9,17},{17,25},{25,1},{2,10},{10... | collective-permute-start | bytes 1032200 | tf_op jit(solution)/shard_map/ppermute | solution.py:30
  6.9 7.8 %collective-permute-start.1 = (bf16[64,384]{1,0:T(8,128)(2,1)}, bf16[64,384]{1,0:T(8,128)(2,1)S(1)}, u32[]{:S(2)}, u32[]{:S(2)}) collective-permute-start(bf16[64,384]{1,0:T(8,128)(2,1)} %get-tuple-element.76), channel_id=1, source_target_pairs={{0,1},{1,0},{2,3},{3,2},{4,5},{5,4},{6,7},{7,6},{8,9},{9,8},{10,11... | collective-permute-start | bytes 147464 | tf_op jit(solution)/shard_map/ppermute | solution.py:30
  8.3 6.3 %collective-permute-start.2 = (bf16[64,384]{1,0:T(8,128)(2,1)}, bf16[64,384]{1,0:T(8,128)(2,1)S(1)}, u32[]{:S(2)}, u32[]{:S(2)}) collective-permute-start(bf16[64,384]{1,0:T(8,128)(2,1)} %get-tuple-element.77), channel_id=1, source_target_pairs={{0,6},{2,0},{4,2},{6,4},{1,7},{3,1},{5,3},{7,5},{8,14},{10,8},{12,... | collective-permute-start | bytes 147464 | tf_op jit(solution)/shard_map/ppermute | solution.py:30
  8.7 5.9 %collective-permute-start.3 = (bf16[64,384]{1,0:T(8,128)(2,1)}, bf16[64,384]{1,0:T(8,128)(2,1)S(1)}, u32[]{:S(2)}, u32[]{:S(2)}) collective-permute-start(bf16[64,384]{1,0:T(8,128)(2,1)} %get-tuple-element.78), channel_id=1, source_target_pairs={{0,7},{1,6},{2,1},{3,0},{4,3},{5,2},{6,5},{7,4},{8,15},{9,14},{10,... | collective-permute-start | bytes 147464 | tf_op jit(solution)/shard_map/ppermute | solution.py:506
  10.0 52.6 %copy-start.3 = (bf16[256,384]{1,0:T(8,128)(2,1)S(1)}, bf16[256,384]{1,0:T(8,128)(2,1)}, u32[]{:S(2)}) copy-start(bf16[256,384]{1,0:T(8,128)(2,1)} %get-tuple-element.122.refs_9_.own_ug) | copy-start | bytes 589828
  17.1 12.4 %collective-permute-start.4 = (bf16[112,1536]{1,0:T(8,128)(2,1)S(1)}, bf16[112,1536]{1,0:T(8,128)(2,1)S(1)}, u32[]{:S(2)}, u32[]{:S(2)}) collective-permute-start(bf16[112,1536]{1,0:T(8,128)(2,1)S(1)} %collective-permute-done.refs_10_.refs_0_), channel_id=1, source_target_pairs={{0,8},{8,16},{16,24},{24,0},{1,9},{9,17},{17,25},{25,1},{2,10},{10... | collective-permute-start | bytes 1032200 | tf_op jit(solution)/shard_map/ppermute | solution.py:30
  17.2 13.3 %collective-permute-start.9 = (bf16[112,1536]{1,0:T(8,128)(2,1)S(1)}, bf16[112,1536]{1,0:T(8,128)(2,1)S(1)}, u32[]{:S(2)}, u32[]{:S(2)}) collective-permute-start(bf16[112,1536]{1,0:T(8,128)(2,1)S(1)} %collective-permute-done.refs_10_.refs_0_), channel_id=1, source_target_pairs={{0,4},{2,6},{4,0},{6,2},{1,5},{3,7},{5,1},{7,3},{8,12},{10,14},{12... | collective-permute-start | bytes 1032200 | tf_op jit(solution)/shard_map/ppermute | solution.py:445
  18.7 7.1 %collective-permute-start.5 = (bf16[64,1536]{1,0:T(8,128)(2,1)}, bf16[64,1536]{1,0:T(8,128)(2,1)S(1)}, u32[]{:S(2)}, u32[]{:S(2)}) collective-permute-start(bf16[64,1536]{1,0:T(8,128)(2,1)} %get-tuple-element.88), channel_id=1, source_target_pairs={{0,1},{1,0},{2,3},{3,2},{4,5},{5,4},{6,7},{7,6},{8,9},{9,8},{10,11... | collective-permute-start | bytes 589832 | tf_op jit(solution)/shard_map/ppermute | solution.py:30
  20.2 9.3 %collective-permute-start.6 = (bf16[64,1536]{1,0:T(8,128)(2,1)}, bf16[64,1536]{1,0:T(8,128)(2,1)S(1)}, u32[]{:S(2)}, u32[]{:S(2)}) collective-permute-start(bf16[64,1536]{1,0:T(8,128)(2,1)} %get-tuple-element.89), channel_id=1, source_target_pairs={{0,6},{2,0},{4,2},{6,4},{1,7},{3,1},{5,3},{7,5},{8,14},{10,8},{12,... | collective-permute-start | bytes 589832 | tf_op jit(solution)/shard_map/ppermute | solution.py:30
  20.2 9.3 %collective-permute-start.7 = (bf16[64,1536]{1,0:T(8,128)(2,1)}, bf16[64,1536]{1,0:T(8,128)(2,1)S(1)}, u32[]{:S(2)}, u32[]{:S(2)}) collective-permute-start(bf16[64,1536]{1,0:T(8,128)(2,1)} %get-tuple-element.90), channel_id=1, source_target_pairs={{0,7},{1,6},{2,1},{3,0},{4,3},{5,2},{6,5},{7,4},{8,15},{9,14},{10,... | collective-permute-start | bytes 589832 | tf_op jit(solution)/shard_map/ppermute | solution.py:506
  20.8 41.8 %copy-start.2 = (bf16[64,1792]{1,0:T(8,128)(2,1)S(1)}, bf16[64,1792]{1,0:T(8,128)(2,1)}, u32[]{:S(2)}) copy-start(bf16[64,1792]{1,0:T(8,128)(2,1)} %get-tuple-element.106.own_ref.refs_4_) | copy-start | bytes 688132
  20.8 41.8 %copy-start.7 = (f32[5]{0:T(128)S(1)}, f32[5]{0:T(128)}, u32[]{:S(2)}) copy-start(f32[5]{0:T(128)} %var_ref.1) | copy-start | bytes 64
  20.8 41.8 %copy-start.8 = (f32[32]{0:T(128)S(1)}, f32[32]{0:T(128)}, u32[]{:S(2)}) copy-start(f32[32]{0:T(128)} %constant.2.clone.lat_ref) | copy-start | bytes 388
  21.6 41.0 %copy-start = (bf16[384,1536]{1,0:T(8,128)(2,1)S(1)}, bf16[384,1536]{1,0:T(8,128)(2,1)}, u32[]{:S(2)}) copy-start(bf16[384,1536]{1,0:T(8,128)(2,1)} %own_w.1) | copy-start | bytes 3538948
  29.5 13.4 %collective-permute-start.8 = (bf16[112,1536]{1,0:T(8,128)(2,1)S(1)}, bf16[112,1536]{1,0:T(8,128)(2,1)S(1)}, u32[]{:S(2)}, u32[]{:S(2)}) collective-permute-start(bf16[112,1536]{1,0:T(8,128)(2,1)S(1)} %collective-permute-done.4.refs_14_.refs_4_), channel_id=1, source_target_pairs={{0,8},{8,16},{16,24},{24,0},{1,9},{9,17},{17,25},{25,1},{2,10},{10... | collective-permute-start | bytes 1032200 | tf_op jit(solution)/shard_map/ppermute | solution.py:30
  30.5 8.7 %collective-permute-start.10 = (bf16[64,1792]{1,0:T(8,128)(2,1)}, bf16[64,1792]{1,0:T(8,128)(2,1)S(1)}, u32[]{:S(2)}, u32[]{:S(2)}) collective-permute-start(bf16[64,1792]{1,0:T(8,128)(2,1)} %get-tuple-element.101), channel_id=1, source_target_pairs={{0,1},{1,0},{2,3},{3,2},{4,5},{5,4},{6,7},{7,6},{8,9},{9,8},{10,11... | collective-permute-start | bytes 688136 | tf_op jit(solution)/shard_map/ppermute | solution.py:30
  32.0 8.3 %collective-permute-start.11 = (bf16[64,1792]{1,0:T(8,128)(2,1)}, bf16[64,1792]{1,0:T(8,128)(2,1)S(1)}, u32[]{:S(2)}, u32[]{:S(2)}) collective-permute-start(bf16[64,1792]{1,0:T(8,128)(2,1)} %get-tuple-element.102), channel_id=1, source_target_pairs={{0,6},{2,0},{4,2},{6,4},{1,7},{3,1},{5,3},{7,5},{8,14},{10,8},{12,... | collective-permute-start | bytes 688136 | tf_op jit(solution)/shard_map/ppermute | solution.py:30
  33.2 9.7 %collective-permute-start.12 = (bf16[64,1792]{1,0:T(8,128)(2,1)}, bf16[64,1792]{1,0:T(8,128)(2,1)S(1)}, u32[]{:S(2)}, u32[]{:S(2)}) collective-permute-start(bf16[64,1792]{1,0:T(8,128)(2,1)} %get-tuple-element.103), channel_id=1, source_target_pairs={{0,7},{1,6},{2,1},{3,0},{4,3},{5,2},{6,5},{7,4},{8,15},{9,14},{10,... | collective-permute-start | bytes 688136 | tf_op jit(solution)/shard_map/ppermute | solution.py:506
  33.2 20.7 %collective-permute-start.19 = (bf16[112,1536]{1,0:T(8,128)(2,1)S(1)}, bf16[112,1536]{1,0:T(8,128)(2,1)S(1)}, u32[]{:S(2)}, u32[]{:S(2)}) collective-permute-start(bf16[112,1536]{1,0:T(8,128)(2,1)S(1)} %collective-permute-done.4.refs_14_.refs_4_), channel_id=1, source_target_pairs={{0,4},{2,6},{4,0},{6,2},{1,5},{3,7},{5,1},{7,3},{8,12},{10,14},{12... | collective-permute-start | bytes 1032200 | tf_op jit(solution)/shard_map/ppermute | solution.py:445
  34.1 0.9 copy-start.4
  42.9 17.2 %collective-permute-start.13 = (bf16[112,1536]{1,0:T(8,128)(2,1)S(1)}, bf16[112,1536]{1,0:T(8,128)(2,1)S(1)}, u32[]{:S(2)}, u32[]{:S(2)}) collective-permute-start(bf16[112,1536]{1,0:T(8,128)(2,1)S(1)} %collective-permute-done.8.refs_18_.refs_8_), channel_id=1, source_target_pairs={{0,4},{2,6},{4,0},{6,2},{1,5},{3,7},{5,1},{7,3},{8,12},{10,14},{12... | collective-permute-start | bytes 1032200 | tf_op jit(solution)/shard_map/ppermute | solution.py:445
  44.6 16.2 %collective-permute-start.20 = (bf16[112,1536]{1,0:T(8,128)(2,1)S(1)}, bf16[112,1536]{1,0:T(8,128)(2,1)S(1)}, u32[]{:S(2)}, u32[]{:S(2)}) collective-permute-start(bf16[112,1536]{1,0:T(8,128)(2,1)S(1)} %collective-permute-done.4.refs_14_.refs_4_), channel_id=1, source_target_pairs={{0,2},{2,0},{4,6},{6,4},{1,3},{3,1},{5,7},{7,5},{8,10},{10,8},{12,... | collective-permute-start | bytes 1032200 | tf_op jit(solution)/shard_map/ppermute | solution.py:445
  44.6 6.4 %collective-permute-start.14 = (bf16[64,1152]{1,0:T(8,128)(2,1)}, bf16[64,1152]{1,0:T(8,128)(2,1)S(1)}, u32[]{:S(2)}, u32[]{:S(2)}) collective-permute-start(bf16[64,1152]{1,0:T(8,128)(2,1)} %get-tuple-element.116), channel_id=1, source_target_pairs={{0,1},{1,0},{2,3},{3,2},{4,5},{5,4},{6,7},{7,6},{8,9},{9,8},{10,11... | collective-permute-start | bytes 442376 | tf_op jit(solution)/shard_map/ppermute | solution.py:30
  46.1 11.2 %collective-permute-start.15 = (bf16[64,1152]{1,0:T(8,128)(2,1)}, bf16[64,1152]{1,0:T(8,128)(2,1)S(1)}, u32[]{:S(2)}, u32[]{:S(2)}) collective-permute-start(bf16[64,1152]{1,0:T(8,128)(2,1)} %get-tuple-element.118), channel_id=1, source_target_pairs={{0,6},{2,0},{4,2},{6,4},{1,7},{3,1},{5,3},{7,5},{8,14},{10,8},{12,... | collective-permute-start | bytes 442376 | tf_op jit(solution)/shard_map/ppermute | solution.py:30
  51.0 7.1 %collective-permute-start.16 = (bf16[64,1152]{1,0:T(8,128)(2,1)}, bf16[64,1152]{1,0:T(8,128)(2,1)S(1)}, u32[]{:S(2)}, u32[]{:S(2)}) collective-permute-start(bf16[64,1152]{1,0:T(8,128)(2,1)} %get-tuple-element.119), channel_id=1, source_target_pairs={{0,7},{1,6},{2,1},{3,0},{4,3},{5,2},{6,5},{7,4},{8,15},{9,14},{10,... | collective-permute-start | bytes 442376 | tf_op jit(solution)/shard_map/ppermute | solution.py:506
  51.6 0.9 copy-start.1
  53.9 6.9 %collective-permute-start.22 = (bf16[112,1536]{1,0:T(8,128)(2,1)S(1)}, bf16[112,1536]{1,0:T(8,128)(2,1)S(1)}, u32[]{:S(2)}, u32[]{:S(2)}) collective-permute-start(bf16[112,1536]{1,0:T(8,128)(2,1)S(1)} %collective-permute-done.8.refs_18_.refs_8_), channel_id=1, source_target_pairs={{0,2},{2,0},{4,6},{6,4},{1,3},{3,1},{5,7},{7,5},{8,10},{10,8},{12,... | collective-permute-start | bytes 1032200 | tf_op jit(solution)/shard_map/ppermute | solution.py:445
  57.4 3.5 %collective-permute-start.21 = (bf16[112,1536]{1,0:T(8,128)(2,1)S(1)}, bf16[112,1536]{1,0:T(8,128)(2,1)S(1)}, u32[]{:S(2)}, u32[]{:S(2)}) collective-permute-start(bf16[112,1536]{1,0:T(8,128)(2,1)S(1)} %collective-permute-done.19.refs_15_.refs_5_), channel_id=1, source_target_pairs={{0,2},{2,0},{4,6},{6,4},{1,3},{3,1},{5,7},{7,5},{8,10},{10,8},{12,... | collective-permute-start | bytes 1032200 | tf_op jit(solution)/shard_map/ppermute | solution.py:445
  58.1 2.7 %collective-permute-start.17 = (bf16[112,1536]{1,0:T(8,128)(2,1)S(1)}, bf16[112,1536]{1,0:T(8,128)(2,1)S(1)}, u32[]{:S(2)}, u32[]{:S(2)}) collective-permute-start(bf16[112,1536]{1,0:T(8,128)(2,1)S(1)} %collective-permute-done.refs_10_.refs_0_), channel_id=1, source_target_pairs={{0,2},{2,0},{4,6},{6,4},{1,3},{3,1},{5,7},{7,5},{8,10},{10,8},{12,... | collective-permute-start | bytes 1032200 | tf_op jit(solution)/shard_map/ppermute | solution.py:445
  58.1 0.9 copy-start.5
  60.2 1.9 %collective-permute-start.18 = (bf16[112,1536]{1,0:T(8,128)(2,1)S(1)}, bf16[112,1536]{1,0:T(8,128)(2,1)S(1)}, u32[]{:S(2)}, u32[]{:S(2)}) collective-permute-start(bf16[112,1536]{1,0:T(8,128)(2,1)S(1)} %collective-permute-done.9.refs_11_.refs_1_), channel_id=1, source_target_pairs={{0,2},{2,0},{4,6},{6,4},{1,3},{3,1},{5,7},{7,5},{8,10},{10,8},{12,... | collective-permute-start | bytes 1032200 | tf_op jit(solution)/shard_map/ppermute | solution.py:445
  60.8 1.8 %collective-permute-start.23 = (bf16[112,1536]{1,0:T(8,128)(2,1)S(1)}, bf16[112,1536]{1,0:T(8,128)(2,1)S(1)}, u32[]{:S(2)}, u32[]{:S(2)}) collective-permute-start(bf16[112,1536]{1,0:T(8,128)(2,1)S(1)} %collective-permute-done.13.refs_19_.refs_9_), channel_id=1, source_target_pairs={{0,2},{2,0},{4,6},{6,4},{1,3},{3,1},{5,7},{7,5},{8,10},{10,8},{12,... | collective-permute-start | bytes 1032200 | tf_op jit(solution)/shard_map/ppermute | solution.py:445
  68.6 7.6 %collective-permute-start.24 = (bf16[40,1664]{1,0:T(8,128)(2,1)S(1)}, bf16[40,1664]{1,0:T(8,128)(2,1)S(1)}, u32[]{:S(2)}, u32[]{:S(2)}) collective-permute-start(bf16[40,1664]{1,0:T(8,128)(2,1)S(1)} %get-tuple-element.127), channel_id=1, source_target_pairs={{0,2},{2,0},{4,6},{6,4},{1,3},{3,1},{5,7},{7,5},{8,10},{10,8},{12,... | collective-permute-start | bytes 399368 | tf_op jit(solution)/shard_map/ppermute | solution.py:445
  69.0 7.2 %collective-permute-start.25 = (bf16[40,1664]{1,0:T(8,128)(2,1)S(1)}, bf16[40,1664]{1,0:T(8,128)(2,1)S(1)}, u32[]{:S(2)}, u32[]{:S(2)}) collective-permute-start(bf16[40,1664]{1,0:T(8,128)(2,1)S(1)} %get-tuple-element.128), channel_id=1, source_target_pairs={{0,4},{2,6},{4,0},{6,2},{1,5},{3,7},{5,1},{7,3},{8,12},{10,14},{12... | collective-permute-start | bytes 399368 | tf_op jit(solution)/shard_map/ppermute | solution.py:445
  70.5 6.1 %collective-permute-start.26 = (bf16[40,1664]{1,0:T(8,128)(2,1)S(1)}, bf16[40,1664]{1,0:T(8,128)(2,1)S(1)}, u32[]{:S(2)}, u32[]{:S(2)}) collective-permute-start(bf16[40,1664]{1,0:T(8,128)(2,1)S(1)} %get-tuple-element.129), channel_id=1, source_target_pairs={{0,6},{2,4},{4,2},{6,0},{1,7},{3,5},{5,3},{7,1},{8,14},{10,12},{12... | collective-permute-start | bytes 399368 | tf_op jit(solution)/shard_map/ppermute | solution.py:445
  76.8 4.7 %collective-permute-start.27 = (bf16[40,384]{1,0:T(8,128)(2,1)S(1)}, bf16[40,384]{1,0:T(8,128)(2,1)S(1)}, u32[]{:S(2)}, u32[]{:S(2)}) collective-permute-start(bf16[40,384]{1,0:T(8,128)(2,1)S(1)} %get-tuple-element.140), channel_id=1, source_target_pairs={{0,8},{8,0},{16,24},{24,16},{1,9},{9,1},{17,25},{25,17},{2,10},{10... | collective-permute-start | bytes 92168 | tf_op jit(solution)/shard_map/ppermute | solution.py:445
  78.4 5.0 %collective-permute-start.28 = (bf16[40,384]{1,0:T(8,128)(2,1)S(1)}, bf16[40,384]{1,0:T(8,128)(2,1)S(1)}, u32[]{:S(2)}, u32[]{:S(2)}) collective-permute-start(bf16[40,384]{1,0:T(8,128)(2,1)S(1)} %get-tuple-element.141), channel_id=1, source_target_pairs={{0,16},{8,24},{16,0},{24,8},{1,17},{9,25},{17,1},{25,9},{2,18},{10... | collective-permute-start | bytes 92168 | tf_op jit(solution)/shard_map/ppermute | solution.py:445
  80.3 5.7 %collective-permute-start.29 = (bf16[40,384]{1,0:T(8,128)(2,1)S(1)}, bf16[40,384]{1,0:T(8,128)(2,1)S(1)}, u32[]{:S(2)}, u32[]{:S(2)}) collective-permute-start(bf16[40,384]{1,0:T(8,128)(2,1)S(1)} %get-tuple-element.142), channel_id=1, source_target_pairs={{0,24},{8,16},{16,8},{24,0},{1,25},{9,17},{17,9},{25,1},{2,26},{10... | collective-permute-start | bytes 92168 | tf_op jit(solution)/shard_map/ppermute | solution.py:445
  86.1 4.7 %collective-permute-start.36 = (bf16[48,384]{1,0:T(8,128)(2,1)S(1)}, bf16[48,384]{1,0:T(8,128)(2,1)S(1)}, u32[]{:S(2)}, u32[]{:S(2)}) collective-permute-start(bf16[48,384]{1,0:T(8,128)(2,1)S(1)} %dp_sum.1.refs_0_), channel_id=1, source_target_pairs={{0,7},{1,6},{2,5},{3,4},{4,3},{5,2},{6,1},{7,0},{8,15},{9,14},{10,... | collective-permute-start | bytes 110600 | tf_op jit(solution)/shard_map/ppermute | solution.py:605
  86.2 5.6 %collective-permute-start.35 = (bf16[48,384]{1,0:T(8,128)(2,1)S(1)}, bf16[48,384]{1,0:T(8,128)(2,1)S(1)}, u32[]{:S(2)}, u32[]{:S(2)}) collective-permute-start(bf16[48,384]{1,0:T(8,128)(2,1)S(1)} %dp_sum.1.refs_0_), channel_id=1, source_target_pairs={{0,6},{1,7},{2,4},{3,5},{4,2},{5,3},{6,0},{7,1},{8,14},{9,15},{10,... | collective-permute-start | bytes 110600 | tf_op jit(solution)/shard_map/ppermute | solution.py:605
  88.1 4.9 %collective-permute-start.34 = (bf16[48,384]{1,0:T(8,128)(2,1)S(1)}, bf16[48,384]{1,0:T(8,128)(2,1)S(1)}, u32[]{:S(2)}, u32[]{:S(2)}) collective-permute-start(bf16[48,384]{1,0:T(8,128)(2,1)S(1)} %dp_sum.1.refs_0_), channel_id=1, source_target_pairs={{0,5},{1,4},{2,7},{3,6},{4,1},{5,0},{6,3},{7,2},{8,13},{9,12},{10,... | collective-permute-start | bytes 110600 | tf_op jit(solution)/shard_map/ppermute | solution.py:605
  90.3 4.0 %collective-permute-start.33 = (bf16[48,384]{1,0:T(8,128)(2,1)S(1)}, bf16[48,384]{1,0:T(8,128)(2,1)S(1)}, u32[]{:S(2)}, u32[]{:S(2)}) collective-permute-start(bf16[48,384]{1,0:T(8,128)(2,1)S(1)} %dp_sum.1.refs_0_), channel_id=1, source_target_pairs={{0,4},{1,5},{2,6},{3,7},{4,0},{5,1},{6,2},{7,3},{8,12},{9,13},{10,... | collective-permute-start | bytes 110600 | tf_op jit(solution)/shard_map/ppermute | solution.py:605
  90.8 3.4 %collective-permute-start.32 = (bf16[48,384]{1,0:T(8,128)(2,1)S(1)}, bf16[48,384]{1,0:T(8,128)(2,1)S(1)}, u32[]{:S(2)}, u32[]{:S(2)}) collective-permute-start(bf16[48,384]{1,0:T(8,128)(2,1)S(1)} %dp_sum.1.refs_0_), channel_id=1, source_target_pairs={{0,3},{1,2},{2,1},{3,0},{4,7},{5,6},{6,5},{7,4},{8,11},{9,10},{10,... | collective-permute-start | bytes 110600 | tf_op jit(solution)/shard_map/ppermute | solution.py:605
  90.8 3.4 %collective-permute-start.31 = (bf16[48,384]{1,0:T(8,128)(2,1)S(1)}, bf16[48,384]{1,0:T(8,128)(2,1)S(1)}, u32[]{:S(2)}, u32[]{:S(2)}) collective-permute-start(bf16[48,384]{1,0:T(8,128)(2,1)S(1)} %dp_sum.1.refs_0_), channel_id=1, source_target_pairs={{0,2},{1,3},{2,0},{3,1},{4,6},{5,7},{6,4},{7,5},{8,10},{9,11},{10,... | collective-permute-start | bytes 110600 | tf_op jit(solution)/shard_map/ppermute | solution.py:605
  91.7 4.0 %collective-permute-start.30 = (bf16[48,384]{1,0:T(8,128)(2,1)S(1)}, bf16[48,384]{1,0:T(8,128)(2,1)S(1)}, u32[]{:S(2)}, u32[]{:S(2)}) collective-permute-start(bf16[48,384]{1,0:T(8,128)(2,1)S(1)} %dp_sum.1.refs_0_), channel_id=1, source_target_pairs={{0,1},{1,0},{2,3},{3,2},{4,5},{5,4},{6,7},{7,6},{8,9},{9,8},{10,11... | collective-permute-start | bytes 110600 | tf_op jit(solution)/shard_map/ppermute | solution.py:605

commit v6 on v5

--- a/solution.py
+++ b/solution.py
@@ -16,8 +16,6 @@
 F32 = jnp.float32
 EXTRA = 256
 UGROWS = 256
-CHUNKS = (1, 4, 4, 3)
-WITH_EXTRA = 2
 PIECES = 12
 VMEM = pl.BlockSpec(memory_space=pltpu.VMEM)
 SMEM = pl.BlockSpec(memory_space=pltpu.SMEM)
@@ -135,49 +133,7 @@
     return lax.broadcasted_iota(jnp.int32, shape, dim)
 
 
-def chunk_copies(x_ref, x_in, groups, sems, at):
-    width = x_ref.shape[-1] // 3
-    unit = width // sum(CHUNKS)
-    copies = []
-    to = 0
-    for g in groups:
-        part = unit * CHUNKS[g]
-        base = unit * sum(CHUNKS[:g])
-        for i in range(3):
-            source = (slice(None),) * 3 + (pl.ds(i * width + base, part),)
-            target = (slice(None),) * 3 + (pl.ds(to, part),)
-            sem = sems.at[at + len(copies)]
-            copies.append(
-                (to, part, pltpu.make_async_copy(x_ref.at[source], x_in.at[target], sem))
-            )
-            to += part
-    return copies
-
-
-def quadrant_pick(count):
-    place = iota((count, count), 0)
-    quad, rest = place // (count // 4), place % (count // 4)
-    row = (rest // 4) % 4 + jnp.where(quad < 2, 4, 0)
-    col = rest % 4 + jnp.where(quad % 2 == 0, 4, 0)
-    source = (rest // 16) * 64 + row * 8 + col
-    return (iota((count, count), 1) == source).astype(F32).astype(BF)
-
-
-def pack_chunk(pick, x_in, copies, outs):
-    count = pick.shape[0]
-    quarter = count // 4
-    for i, (at, part, copy) in enumerate(copies):
-        copy.wait()
-        tokens = x_in[:, :, :, at : at + part].reshape(count, part)
-        out = jnp.dot(pick, tokens, preferred_element_type=F32).astype(BF)
-        for q in range(4):
-            outs[q][:, i * part : (i + 1) * part] = out[q * quarter : (q + 1) * quarter]
-
-
-def lead_kernel(
-    w_ref, unpatch_ref, gain_ref, x_ref, ug_ref, payload_ref, o0, o1, o2, o3,
-    u_in, x_in, sems,
-):
+def payload_kernel(w_ref, unpatch_ref, gain_ref, ug_ref, payload_ref, u_in, sems):
     part = lax.axis_index("lat")
     rows, width = w_ref.shape
     qr = rows // 4
@@ -189,10 +145,6 @@
     u_copy = pltpu.make_async_copy(unpatch_ref, u_in, sems.at[1])
     u_copy.start()
     w_copy.start()
-    copies = chunk_copies(x_ref, x_in, (0,), sems, 2)
-    for _, _, c in copies:
-        c.start()
-    pick = quadrant_pick(x_ref.shape[0] * 64)
     gain = jnp.broadcast_to(gain_ref[...].astype(F32).reshape(1, rows), (16, rows)).astype(BF)
     ug_ref[pl.ds(span, 16), :] = gain
     ug_ref[pl.ds(span + 16, UGROWS - span - 16), :] = jnp.zeros((UGROWS - span - 16, rows), BF)
@@ -201,29 +153,35 @@
     for j in range(4):
         at = pl.multiple_of((4 * part + j) * 16, 16)
         payload_ref[pl.ds(qr, 16), pl.ds(j * rows, rows)] = ug_ref[pl.ds(at, 16), :]
-    pack_chunk(pick, x_in, copies, (o0, o1, o2, o3))
     w_copy.wait()
 
 
-def pack_kernel(x_ref, t_ref, valid_ref, *refs):
-    later = range(1, len(CHUNKS))
-    outs = refs[: 4 * len(later)]
-    x_in, t_in, v_in, sems = refs[4 * len(later) :]
+def pack_kernel(x_ref, t_ref, valid_ref, o0, o1, o2, o3, x_in, t_in, v_in, sems):
+    outs = (o0, o1, o2, o3)
     span = t_ref.shape[-1]
     count = x_ref.shape[0] * 64
     quarter = count // 4
-    copies = chunk_copies(x_ref, x_in, later, sems, 2)
-    t_copy = pltpu.make_async_copy(t_ref, t_in, sems.at[0])
-    v_copy = pltpu.make_async_copy(valid_ref, v_in, sems.at[1])
-    for _, _, c in copies:
+    step = 512
+    width = x_ref.shape[-1]
+    copies = [
+        pltpu.make_async_copy(t_ref, t_in, sems.at[0]),
+        pltpu.make_async_copy(valid_ref, v_in, sems.at[1]),
+    ]
+    for at in range(0, width, step):
+        lanes = (slice(None),) * 3 + (pl.ds(at, step),)
+        copies.append(
+            pltpu.make_async_copy(x_ref.at[lanes], x_in.at[lanes], sems.at[len(copies)])
+        )
+    for c in copies:
         c.start()
-    t_copy.start()
-    v_copy.start()
-    pick = quadrant_pick(count)
-    for n in range(len(later)):
-        pack_chunk(pick, x_in, copies[3 * n : 3 * n + 3], outs[4 * n : 4 * n + 4])
-    t_copy.wait()
-    v_copy.wait()
+    place = iota((count, count), 0)
+    quad, rest = place // quarter, place % quarter
+    row = (rest // 4) % 4 + jnp.where(quad < 2, 4, 0)
+    col = rest % 4 + jnp.where(quad % 2 == 0, 4, 0)
+    source = (rest // 16) * 64 + row * 8 + col
+    pick = (iota((count, count), 1) == source).astype(F32).astype(BF)
+    copies[0].wait()
+    copies[1].wait()
     goal = jnp.dot(pick, t_in[...].reshape(count, span), preferred_element_type=F32)
     token = iota((count, 8), 0)
     row_hot = ((token // 8) % 8 == iota((count, 8), 1)).astype(F32)
@@ -234,8 +192,13 @@
     column = jnp.dot(pick, spread, preferred_element_type=F32)
     extra = jnp.concatenate([goal, column[:, : EXTRA - span]], axis=1).astype(BF)
     for q in range(4):
-        ref = outs[4 * (WITH_EXTRA - 1) + q]
-        ref[:, ref.shape[1] - EXTRA :] = extra[q * quarter : (q + 1) * quarter]
+        outs[q][:, width:] = extra[q * quarter : (q + 1) * quarter]
+    for n, at in enumerate(range(0, width, step)):
+        copies[2 + n].wait()
+        tokens = x_in[:, :, :, at : at + step].reshape(count, step)
+        out = jnp.dot(pick, tokens, preferred_element_type=F32).astype(BF)
+        for q in range(4):
+            outs[q][:, at : at + step] = out[q * quarter : (q + 1) * quarter]
 
 
 def attention_kernel(own_ref, east_ref, south_ref, diag_ref, ctx_ref):
@@ -313,7 +276,7 @@
 
 
 def forward_kernel(lat_ref, var_ref, *refs):
-    ctx_refs, refs = refs[: len(CHUNKS)], refs[len(CHUNKS) :]
+    ctx_ref, refs = refs[0], refs[1:]
     extras, refs = refs[:4], refs[4:]
     (own_w, own_ug), refs = refs[:2], refs[2:]
     pieces, refs = refs[:PIECES], refs[PIECES:]
@@ -341,13 +304,7 @@
     weight = lat_w * valid * var_w
     for c in w_copies:
         c.wait()
-    at = 0
-    mixed = None
-    for ref in ctx_refs:
-        part = ref.shape[1]
-        term_g = jnp.dot(ref[...], w_all[at : at + part, :], preferred_element_type=F32)
-        mixed = term_g if mixed is None else mixed + term_g
-        at += part
+    mixed = jnp.dot(ctx_ref[...], w_all[...], preferred_element_type=F32)
     centre = jnp.mean(mixed, axis=-1, keepdims=True)
     off = mixed - centre
     inv = lax.rsqrt(jnp.mean(off * off, axis=-1, keepdims=True) + 1e-05)
@@ -462,90 +419,66 @@
     lat_table = jnp.asarray(np.roll(cosine / cosine.mean(), -4), F32)
     barrier = lax.optimization_barrier
 
-    x = projected.reshape(levels, 8, 8, 3 * width)
-    parts_of = [width // sum(CHUNKS) * n for n in CHUNKS]
-    widths = [3 * part + (EXTRA if g == WITH_EXTRA else 0) for g, part in enumerate(parts_of)]
-    ug, payload, *packed = pl.pallas_call(
-        lead_kernel,
-        out_shape=[shape((UGROWS, rows), BF), shape((rows // 4 + 16, width), BF)]
-        + [shape((quarter, widths[0]), BF)] * 4,
-        in_specs=[HBM, HBM, VMEM, HBM],
-        out_specs=[VMEM] * 6,
+    ug, payload = pl.pallas_call(
+        payload_kernel,
+        out_shape=[shape((UGROWS, rows), BF), shape((rows // 4 + 16, width), BF)],
+        in_specs=[HBM, HBM, VMEM],
+        out_specs=[VMEM] * 2,
+        scratch_shapes=[pltpu.VMEM((span, rows), BF), pltpu.SemaphoreType.DMA((2,))],
+        compiler_params=params(62),
+        name="payload",
+    )(w_out, unpatch_matrix.T, norm_gain)
+    ring1 = from_behind(payload, "dp", 1)
+    own, *send = pl.pallas_call(
+        pack_kernel,
+        out_shape=[shape((quarter, 3 * width + EXTRA), BF)] * 4,
+        in_specs=[HBM] * 3,
+        out_specs=[VMEM] * 4,
         scratch_shapes=[
-            pltpu.VMEM((span, rows), BF),
-            pltpu.VMEM((levels, 8, 8, widths[0]), BF),
-            pltpu.SemaphoreType.DMA((5,)),
-        ],
-        compiler_params=params(62),
-        name="lead",
-    )(w_out, unpatch_matrix.T, norm_gain, x)
-    ring1 = from_behind(payload, "dp", 1)
-    later = sum(parts_of[1:])
-    packed += pl.pallas_call(
-        pack_kernel,
-        out_shape=[shape((quarter, w), BF) for w in widths[1:] for _ in range(4)],
-        in_specs=[HBM] * 3,
-        out_specs=[VMEM] * (4 * len(CHUNKS) - 4),
-        scratch_shapes=[
-            pltpu.VMEM((levels, 8, 8, 3 * later), BF),
+            pltpu.VMEM((levels, 8, 8, 3 * width), BF),
             pltpu.VMEM((levels, 8, 8, span), BF),
             pltpu.VMEM((8, 8), jnp.int32),
-            pltpu.SemaphoreType.DMA((3 * len(CHUNKS) - 1,)),
+            pltpu.SemaphoreType.DMA((2 + 3 * width // 512,)),
         ],
         compiler_params=params(62),
         name="pack",
-    )(x, targets.reshape(levels, 8, 8, span), valid_cells)
+    )(
+        projected.reshape(levels, 8, 8, 3 * width),
+        targets.reshape(levels, 8, 8, span),
+        valid_cells,
+    )
     corner = [
         (a * lon + b, ((a - 1) % lat) * lon + (b - 1) % lon) for a in range(lat) for b in range(lon)
     ]
-
-    def halo(east, south, diag):
-        return [
-            from_behind(east, "lon", -1),
-            from_behind(south, "lat", -1),
-            lax.ppermute(diag, ("lat", "lon"), corner),
-        ]
-
-    def attend(*chunk):
-        part = chunk[0].shape[1] // 384 * 128
-        return pl.pallas_call(
-            attention_kernel,
-            out_shape=shape((tokens, part), BF),
-            in_specs=[VMEM] * 4,
-            out_specs=VMEM,
-            compiler_params=params(8),
-            name="attention",
-        )(*chunk)
-
-    owns = packed[0::4]
-    sends = [packed[4 * g + 1 : 4 * g + 4] for g in range(len(CHUNKS))]
-    tiles0 = halo(*sends[0])
-    ring1_after, sends[1][0], *tiles0 = barrier((ring1, sends[1][0], *tiles0))
+    ring1_after, _ = barrier((ring1, send[0]))
+    tiles = (
+        own,
+        from_behind(send[0], "lon", -1),
+        from_behind(send[1], "lat", -1),
+        lax.ppermute(send[2], ("lat", "lon"), corner),
+    )
     ring2 = from_behind(ring1_after, "dp", 1)
     across1 = swap(ring1, "lat", 2)
-    *sends[1], tiles0[0] = barrier((*sends[1], tiles0[0]))
-    tiles1 = halo(*sends[1])
-    ctx0 = attend(owns[0], *tiles0)
-    ring2_after, ctx0, *tiles1 = barrier((ring2, ctx0, *tiles1))
+    ring2_after, across1 = barrier((ring2, across1))
     ring3 = from_behind(ring2_after, "dp", 1)
     across2 = swap(ring2, "lat", 2)
-    *sends[2], across1, tiles1[0] = barrier((*sends[2], across1, tiles1[0]))
-    tiles2 = halo(*sends[2])
-    ctx1 = attend(owns[1], *tiles1)
-    ring3_after, ctx1, *tiles2 = barrier((ring3, ctx1, *tiles2))
-    across3 = swap(ring3_after, "lat", 2)
-    *sends[3], tiles2[0] = barrier((*sends[3], tiles2[0]))
-    tiles3 = halo(*sends[3])
-    ctx2 = attend(owns[2], *tiles2)
-    ring1, across1, tiles3[0] = barrier((ring1, across1, tiles3[0]))
-    ctx3 = attend(owns[3], *tiles3)
-    across3, ctx2, ctx3 = barrier((across3, ctx2, ctx3))
+    across3 = swap(ring3, "lat", 2)
+    ring1, across1, ring2, *tiles = barrier((ring1, across1, ring2, *tiles))
+    ctx = pl.pallas_call(
+        attention_kernel,
+        out_shape=shape((tokens, width), BF),
+        in_specs=[VMEM] * 4,
+        out_specs=VMEM,
+        compiler_params=params(16),
+        name="attention",
+    )(*tiles)
+    across3, ctx = barrier((across3, ctx))
     pieces = []
     for ring, across in ((ring1, across1), (ring2, across2), (ring3, across3)):
         pieces += [ring, across, swap(ring, "lat", 1), swap(across, "lat", 1)]
 
     piece = span // lat
-    extra_spec = pl.BlockSpec((quarter, EXTRA), lambda i: (0, 3 * parts_of[WITH_EXTRA] // EXTRA))
+    extra_spec = pl.BlockSpec((quarter, EXTRA), lambda i: (0, 3 * width // EXTRA))
     copies = 2 + PIECES * 5
     assembly = [
         pltpu.VMEM((dp * rows, width), BF),
@@ -556,14 +489,14 @@
         grid=(1,),
         out_shape=[shape((piece, width + 128), BF)] * 4
         + [shape((tokens, width), F32), shape((tokens, 128), F32), shape((tokens, span), BF)],
-        in_specs=[SMEM] * 2 + [VMEM] * len(CHUNKS) + [extra_spec] * 4 + [HBM] + [ANY] * (1 + PIECES),
+        in_specs=[SMEM] * 2 + [VMEM] + [extra_spec] * 4 + [HBM] + [ANY] * (1 + PIECES),
         out_specs=[VMEM] * 7,
         scratch_shapes=[pltpu.VMEM((tokens, width), BF)]
         + assembly
         + [pltpu.VMEM((span, width), F32), pltpu.SemaphoreType.DMA((copies,))],
         compiler_params=params(28),
         name="forward",
-    )(lat_table, var_weight, ctx0, ctx1, ctx2, ctx3, owns[2], *tiles2, w_out, ug, *pieces)
+    )(lat_table, var_weight, ctx, *tiles, w_out, ug, *pieces)
 
     terms = [terms[0]] + [swap(terms[b], "lat", b) for b in (1, 2, 3)]
     grad_context = pl.pallas_call(

time: 96.6 us -> 90.8 us (0.940)
  starting transfers between devices: 34.4 us -> 26.7 us
  waiting for transfers between devices: 33.4 us -> 39.2 us
  Pallas kernels: 25 us -> 22.9 us
  local copies, waits for them, and re-layouts: 2.8 us -> 1.09 us
    ppermute x15, waiting for transfers between devices: 6.67 us -> 16.4 us  [swap(): lax.ppermute(array, axis, [(i, i ^ bit) for i in range(lax.axis_size(axis...]
    ppermute x11 -> x5, starting transfers between devices: 11.9 us -> 3.62 us  [from_behind(): lax.ppermute(array, axis, [(i, (i + by) % length) for i in range(length)])]
    ppermute x4 -> x1, waiting for transfers between devices: 2.64 us -> 0.01 us  [shards(): lax.ppermute(send[2], ('lat', 'lon'), corner)]
    pallas_call x6 -> x3, Pallas kernels: 12.4 us -> 10.4 us  [the longest x1 4.99 us: shards(): pl.pallas_call(pack_kernel, out_shape=[shape((quarter, 3 * width + EXTRA)...]
    ppermute x11 -> x5, waiting for transfers between devices: 21.4 us -> 19.4 us  [from_behind(): lax.ppermute(array, axis, [(i, (i + by) % length) for i in range(length)])]
    unnamed x18 -> x12, local copies, waits for them, and re-layouts: 2.8 us -> 1.09 us
    ppermute x15, starting transfers between devices: 13.2 us -> 14.6 us  [swap(): lax.ppermute(array, axis, [(i, i ^ bit) for i in range(lax.axis_size(axis...]
    ppermute x4 -> x1, starting transfers between devices: 2.39 us -> 1.55 us  [shards(): lax.ppermute(send[2], ('lat', 'lon'), corner)]
  transfers between devices with their start and end apart: 37 -> 28, of which waited for: 15 -> 14; matrix products, arithmetic and copies ran while one was open for 0% -> 0% of each run, Pallas kernels for 15% -> 15%
where the time goes in v6:
time: 90.8 us; the launch traced here: 90.6 us
  waiting for transfers between devices  39.2 us (43%)
  starting transfers between devices  26.7 us (29%)
  Pallas kernels  22.9 us (25%)
  local copies, waits for them, and re-layouts  1.09 us (1%)
    ppermute x5, waiting for transfers between devices, from_behind(): lax.ppermute(array, axis, [(i, (i + by) % length) for i in range(length)])  19.4 us
    ppermute x15, waiting for transfers between devices, swap(): lax.ppermute(array, axis, [(i, i ^ bit) for i in range(lax.axis_size(axis...  16.4 us
    ppermute x15, starting transfers between devices, swap(): lax.ppermute(array, axis, [(i, i ^ bit) for i in range(lax.axis_size(axis...  14.6 us
    ppermute x7, starting transfers between devices, shards(): plane.append(lax.ppermute(mine, ('lat', 'lon'), pairs))  6.87 us
    pallas_call x1, Pallas kernels, shards(): pl.pallas_call(forward_kernel, grid=(1,), out_shape=[shape((piece, width...  5.89 us
    pallas_call x1, Pallas kernels, shards(): pl.pallas_call(backward_kernel, out_shape=shape((tokens, width), BF), in_...  5.67 us
    pallas_call x1, Pallas kernels, shards(): pl.pallas_call(pack_kernel, out_shape=[shape((quarter, 3 * width + EXTRA)...  4.99 us
    ppermute x5, starting transfers between devices, from_behind(): lax.ppermute(array, axis, [(i, (i + by) % length) for i in range(length)])  3.62 us
  transfers between devices with their start and end apart: 28, of which 14 were waited for; matrix products, arithmetic and copies ran while one was open for 0% of the time, Pallas kernels for 15%

profile of v6, /device:TPU:0, one launch (start us, length us, event | category | flops | bytes accessed | tf_op | source)
XLA Modules:
  0.0 90.6 jit_solution(15071521340539894474)
XLA Ops:
  0.6 2.5 %payload.1 = (bf16[256,384]{1,0:T(8,128)(2,1)}, bf16[112,1536]{1,0:T(8,128)(2,1)}) custom-call(bf16[384,1536]{1,0:T(8,128)(2,1)} %own_w.1, bf16[160,384]{1,0:T(8,128)(2,1)} %bitcast.9, bf16[384]{0:T(512)(128)(2,1)} %gain_ref.1), custom_call_target="tpu_custom_call" | custom-call | tf_op jit(solution)/shard_map/payload/pallas_call | solution.py:422
  3.2 3.1 %collective-permute-start = (bf16[112,1536]{1,0:T(8,128)(2,1)}, bf16[112,1536]{1,0:T(8,128)(2,1)S(1)}, u32[]{:S(2)}, u32[]{:S(2)}) collective-permute-start(bf16[112,1536]{1,0:T(8,128)(2,1)} %get-tuple-element.40), channel_id=1, source_target_pairs={{0,8},{8,16},{16,24},{24,0},{1,9},{9,17},{17,25},{25,1},{2,10},{10... | collective-permute-start | bytes 1032200 | tf_op jit(solution)/shard_map/ppermute | solution.py:28
  6.2 5.0 %pack.1 = (bf16[64,4864]{1,0:T(8,128)(2,1)}, bf16[64,4864]{1,0:T(8,128)(2,1)}, bf16[64,4864]{1,0:T(8,128)(2,1)}, bf16[64,4864]{1,0:T(8,128)(2,1)}) custom-call(bf16[4,8,8,4608]{3,2,1,0:T(8,128)(2,1)} %bitcast.6, bf16[4,8,8,160]{3,2,1,0:T(8,128)(2,1)} %bitcast.8, s32[8,8]{1,0:T(8,128)} %valid_ref.1), custom_call_target="tpu_custom_call" | custom-call | tf_op jit(solution)/shard_map/pack/pallas_call | solution.py:432
  11.2 5.3 %collective-permute-done.refs_7_.refs_0_ = bf16[112,1536]{1,0:T(8,128)(2,1)S(1)} collective-permute-done((bf16[112,1536]{1,0:T(8,128)(2,1)}, bf16[112,1536]{1,0:T(8,128)(2,1)S(1)}, u32[]{:S(2)}, u32[]{:S(2)}) %collective-permute-start) | collective-permute-done | bytes 344096 | tf_op jit(solution)/shard_map/ppermute | solution.py:28
  16.5 1.5 %collective-permute-start.2 = (bf16[112,1536]{1,0:T(8,128)(2,1)S(1)}, bf16[112,1536]{1,0:T(8,128)(2,1)S(1)}, u32[]{:S(2)}, u32[]{:S(2)}) collective-permute-start(bf16[112,1536]{1,0:T(8,128)(2,1)S(1)} %collective-permute-done.refs_7_.refs_0_), channel_id=1, source_target_pairs={{0,4},{2,6},{4,0},{6,2},{1,5},{3,7},{5,1},{7,3},{8,12},{10,14},{12... | collective-permute-start | bytes 1032200 | tf_op jit(solution)/shard_map/ppermute | solution.py:402
  18.0 0.0 collective-permute-start.1
  18.0 0.0 collective-permute-start.6
  18.1 1.5 %collective-permute-start.7 = (bf16[64,4864]{1,0:T(8,128)(2,1)}, bf16[64,4864]{1,0:T(8,128)(2,1)S(1)}, u32[]{:S(2)}, u32[]{:S(2)}) collective-permute-start(bf16[64,4864]{1,0:T(8,128)(2,1)} %get-tuple-element.47), channel_id=1, source_target_pairs={{0,7},{1,6},{2,1},{3,0},{4,3},{5,2},{6,5},{7,4},{8,15},{9,14},{10,... | collective-permute-start | bytes 1867784 | tf_op jit(solution)/shard_map/ppermute | solution.py:458
  19.6 0.5 collective-permute-start.5
  20.1 8.5 %collective-permute-done.2.refs_8_.refs_1_ = bf16[112,1536]{1,0:T(8,128)(2,1)S(1)} collective-permute-done((bf16[112,1536]{1,0:T(8,128)(2,1)S(1)}, bf16[112,1536]{1,0:T(8,128)(2,1)S(1)}, u32[]{:S(2)}, u32[]{:S(2)}) %collective-permute-start.2) | collective-permute-done | bytes 344096 | tf_op jit(solution)/shard_map/ppermute | solution.py:402
  28.6 0.0 collective-permute-done.1.refs_11_.refs_4_
  28.6 0.0 collective-permute-start.3
  28.6 2.8 %collective-permute-start.10 = (bf16[112,1536]{1,0:T(8,128)(2,1)S(1)}, bf16[112,1536]{1,0:T(8,128)(2,1)S(1)}, u32[]{:S(2)}, u32[]{:S(2)}) collective-permute-start(bf16[112,1536]{1,0:T(8,128)(2,1)S(1)} %collective-permute-done.1.refs_11_.refs_4_), channel_id=1, source_target_pairs={{0,4},{2,6},{4,0},{6,2},{1,5},{3,7},{5,1},{7,3},{8,12},{10,14},{12... | collective-permute-start | bytes 1032200 | tf_op jit(solution)/shard_map/ppermute | solution.py:402
  31.5 6.7 %collective-permute-done.3.refs_15_.refs_8_ = bf16[112,1536]{1,0:T(8,128)(2,1)S(1)} collective-permute-done((bf16[112,1536]{1,0:T(8,128)(2,1)S(1)}, bf16[112,1536]{1,0:T(8,128)(2,1)S(1)}, u32[]{:S(2)}, u32[]{:S(2)}) %collective-permute-start.3) | collective-permute-done | bytes 344096 | tf_op jit(solution)/shard_map/ppermute | solution.py:28
  38.2 2.4 %collective-permute-start.4 = (bf16[112,1536]{1,0:T(8,128)(2,1)S(1)}, bf16[112,1536]{1,0:T(8,128)(2,1)S(1)}, u32[]{:S(2)}, u32[]{:S(2)}) collective-permute-start(bf16[112,1536]{1,0:T(8,128)(2,1)S(1)} %collective-permute-done.3.refs_15_.refs_8_), channel_id=1, source_target_pairs={{0,4},{2,6},{4,0},{6,2},{1,5},{3,7},{5,1},{7,3},{8,12},{10,14},{12... | collective-permute-start | bytes 1032200 | tf_op jit(solution)/shard_map/ppermute | solution.py:402
  40.5 4.5 %collective-permute-done.6.south_ref.refs_3_ = bf16[64,4864]{1,0:T(8,128)(2,1)S(1)} collective-permute-done((bf16[64,4864]{1,0:T(8,128)(2,1)}, bf16[64,4864]{1,0:T(8,128)(2,1)S(1)}, u32[]{:S(2)}, u32[]{:S(2)}) %collective-permute-start.6) | collective-permute-done | bytes 622624 | tf_op jit(solution)/shard_map/ppermute | solution.py:28
  45.0 0.0 collective-permute-done.7.diag_ref.refs_4_
  45.0 2.9 %collective-permute-done.5.east_ref.refs_2_ = bf16[64,4864]{1,0:T(8,128)(2,1)S(1)} collective-permute-done((bf16[64,4864]{1,0:T(8,128)(2,1)}, bf16[64,4864]{1,0:T(8,128)(2,1)S(1)}, u32[]{:S(2)}, u32[]{:S(2)}) %collective-permute-start.5) | collective-permute-done | bytes 622624 | tf_op jit(solution)/shard_map/ppermute | solution.py:28
  47.9 0.0 collective-permute-start.8
  48.0 0.5 collective-permute-start.9
  48.5 0.1 collective-permute-start.11
  48.5 1.1 %copy-done.1 = bf16[64,4864]{1,0:T(8,128)(2,1)S(1)} copy-done((bf16[64,4864]{1,0:T(8,128)(2,1)S(1)}, bf16[64,4864]{1,0:T(8,128)(2,1)}, u32[]{:S(2)}) %copy-start.1) | copy-done | bytes 622616
  49.6 2.9 %attention.1.refs_0_ = bf16[256,1536]{1,0:T(8,128)(2,1)S(1)} custom-call(bf16[64,4864]{1,0:T(8,128)(2,1)S(1)} %copy-done.1, bf16[64,4864]{1,0:T(8,128)(2,1)S(1)} %collective-permute-done.5.east_ref.refs_2_, bf16[64,4864]{1,0:T(8,128)(2,1)S(1)} %collective-permute-done.6.south_ref.refs_3_, bf16[64,4864]{1,0:T(8,128)(2,1)S(1)} %collective-permute-done.7.diag_ref.refs_4_), custom_call_target="tpu_custom_call" | custom-call | tf_op jit(solution)/shard_map/attention/pallas_call | solution.py:467
  52.5 0.0 collective-permute-done.10.refs_12_.refs_5_
  52.5 0.5 collective-permute-start.13
  53.0 0.9 collective-permute-done.4.refs_16_.refs_9_
  53.9 0.0 collective-permute-start.12
  53.9 0.0 collective-permute-done.8.refs_9_.refs_2_
  53.9 0.5 collective-permute-start.14
  54.4 0.0 collective-permute-done.9.refs_10_.refs_3_
  54.4 0.0 collective-permute-done.11.refs_13_.refs_6_
  54.4 0.0 collective-permute-done.13.refs_17_.refs_10_
  54.4 1.1 %collective-permute-done.12.refs_14_.refs_7_ = bf16[112,1536]{1,0:T(8,128)(2,1)S(1)} collective-permute-done((bf16[112,1536]{1,0:T(8,128)(2,1)S(1)}, bf16[112,1536]{1,0:T(8,128)(2,1)S(1)}, u32[]{:S(2)}, u32[]{:S(2)}) %collective-permute-start.12) | collective-permute-done | bytes 344096 | tf_op jit(solution)/shard_map/ppermute | solution.py:402
  55.5 0.5 collective-permute-done.14.refs_18_.refs_11_
  56.0 5.9 %forward.1 = (bf16[40,1664]{1,0:T(8,128)(2,1)S(1)}, bf16[40,1664]{1,0:T(8,128)(2,1)S(1)}, bf16[40,1664]{1,0:T(8,128)(2,1)S(1)}, bf16[40,1664]{1,0:T(8,128)(2,1)S...) custom-call(f32[32]{0:T(128)S(1)} %copy-done.5, f32[5]{0:T(128)S(1)} %copy-done.4, ...), custom_call_target="tpu_custom_call" | custom-call | tf_op jit(solution)/shard_map/forward/pallas_call | solution.py:487
  61.9 0.2 collective-permute-start.15
  62.1 1.3 %collective-permute-start.16 = (bf16[40,1664]{1,0:T(8,128)(2,1)S(1)}, bf16[40,1664]{1,0:T(8,128)(2,1)S(1)}, u32[]{:S(2)}, u32[]{:S(2)}) collective-permute-start(bf16[40,1664]{1,0:T(8,128)(2,1)S(1)} %get-tuple-element.60), channel_id=1, source_target_pairs={{0,4},{2,6},{4,0},{6,2},{1,5},{3,7},{5,1},{7,3},{8,12},{10,14},{12... | collective-permute-start | bytes 399368 | tf_op jit(solution)/shard_map/ppermute | solution.py:402
  63.4 0.4 collective-permute-start.17
  63.9 5.7 %backward.1 = bf16[256,1536]{1,0:T(8,128)(2,1)} custom-call(f32[256,1536]{1,0:T(8,128)S(1)} %get-tuple-element.62.normed_ref, f32[256,128]{1,0:T(8,128)S(1)} %get-tuple-element.63.inv_ref, bf16[256,160]{1,0:T(8,128)(2,1)S(1)} %get-tuple-element.64.dfc_ref, bf16[384,1536]{1,0:T(8,128)(2,1)S(1)} %copy-done, bf16[256,384]{1,0:T(8,128)(2,1)S(1)} %copy-done.3, ...), custom_call_target="tpu_custom_call" | custom-call | tf_op jit(solution)/shard_map/backward/pallas_call | solution.py:502
  69.5 0.0 collective-permute-done.15.b
  69.6 0.0 collective-permute-done.16.c
  69.6 0.7 collective-permute-done.17.d
  70.3 0.2 lat_sum.1
  70.4 0.3 collective-permute-start.18
  70.7 3.1 %collective-permute-start.19 = (bf16[40,384]{1,0:T(8,128)(2,1)S(1)}, bf16[40,384]{1,0:T(8,128)(2,1)S(1)}, u32[]{:S(2)}, u32[]{:S(2)}) collective-permute-start(bf16[40,384]{1,0:T(8,128)(2,1)S(1)} %get-tuple-element.73), channel_id=1, source_target_pairs={{0,16},{8,24},{16,0},{24,8},{1,17},{9,25},{17,1},{25,9},{2,18},{10... | collective-permute-start | bytes 92168 | tf_op jit(solution)/shard_map/ppermute | solution.py:402
  73.8 1.0 %collective-permute-start.20 = (bf16[40,384]{1,0:T(8,128)(2,1)S(1)}, bf16[40,384]{1,0:T(8,128)(2,1)S(1)}, u32[]{:S(2)}, u32[]{:S(2)}) collective-permute-start(bf16[40,384]{1,0:T(8,128)(2,1)S(1)} %get-tuple-element.74), channel_id=1, source_target_pairs={{0,24},{8,16},{16,8},{24,0},{1,25},{9,17},{17,9},{25,1},{2,26},{10... | collective-permute-start | bytes 92168 | tf_op jit(solution)/shard_map/ppermute | solution.py:402
  74.8 0.0 collective-permute-done.18.b
  74.8 1.2 %collective-permute-done.19.c = bf16[40,384]{1,0:T(8,128)(2,1)S(1)} collective-permute-done((bf16[40,384]{1,0:T(8,128)(2,1)S(1)}, bf16[40,384]{1,0:T(8,128)(2,1)S(1)}, u32[]{:S(2)}, u32[]{:S(2)}) %collective-permute-start.19) | collective-permute-done | bytes 30752 | tf_op jit(solution)/shard_map/ppermute | solution.py:402
  76.0 3.5 %collective-permute-done.20.d = bf16[40,384]{1,0:T(8,128)(2,1)S(1)} collective-permute-done((bf16[40,384]{1,0:T(8,128)(2,1)S(1)}, bf16[40,384]{1,0:T(8,128)(2,1)S(1)}, u32[]{:S(2)}, u32[]{:S(2)}) %collective-permute-start.20) | collective-permute-done | bytes 30752 | tf_op jit(solution)/shard_map/ppermute | solution.py:402
  79.5 0.1 collective-permute-start.27
  79.6 2.6 %collective-permute-start.26 = (bf16[48,384]{1,0:T(8,128)(2,1)S(1)}, bf16[48,384]{1,0:T(8,128)(2,1)S(1)}, u32[]{:S(2)}, u32[]{:S(2)}) collective-permute-start(bf16[48,384]{1,0:T(8,128)(2,1)S(1)} %dp_sum.1.refs_0_), channel_id=1, source_target_pairs={{0,6},{1,7},{2,4},{3,5},{4,2},{5,3},{6,0},{7,1},{8,14},{9,15},{10,... | collective-permute-start | bytes 110600 | tf_op jit(solution)/shard_map/ppermute | solution.py:538
  82.3 0.5 collective-permute-start.25
  82.8 1.5 %collective-permute-start.24 = (bf16[48,384]{1,0:T(8,128)(2,1)S(1)}, bf16[48,384]{1,0:T(8,128)(2,1)S(1)}, u32[]{:S(2)}, u32[]{:S(2)}) collective-permute-start(bf16[48,384]{1,0:T(8,128)(2,1)S(1)} %dp_sum.1.refs_0_), channel_id=1, source_target_pairs={{0,4},{1,5},{2,6},{3,7},{4,0},{5,1},{6,2},{7,3},{8,12},{9,13},{10,... | collective-permute-start | bytes 110600 | tf_op jit(solution)/shard_map/ppermute | solution.py:538
  84.3 0.0 collective-permute-start.23
  84.3 0.0 collective-permute-done.27.refs_7_
  84.3 1.6 %collective-permute-start.22 = (bf16[48,384]{1,0:T(8,128)(2,1)S(1)}, bf16[48,384]{1,0:T(8,128)(2,1)S(1)}, u32[]{:S(2)}, u32[]{:S(2)}) collective-permute-start(bf16[48,384]{1,0:T(8,128)(2,1)S(1)} %dp_sum.1.refs_0_), channel_id=1, source_target_pairs={{0,2},{1,3},{2,0},{3,1},{4,6},{5,7},{6,4},{7,5},{8,10},{9,11},{10,... | collective-permute-start | bytes 110600 | tf_op jit(solution)/shard_map/ppermute | solution.py:538
  85.9 0.0 collective-permute-done.26.refs_6_
  85.9 0.5 collective-permute-start.21
  86.4 0.7 collective-permute-done.25.refs_5_
  87.1 0.0 collective-permute-done.24.refs_4_
  87.1 0.9 collective-permute-done.23.refs_3_
  88.0 0.0 collective-permute-done.22.refs_2_
  88.0 1.8 %collective-permute-done.21.refs_1_ = bf16[48,384]{1,0:T(8,128)(2,1)S(1)} collective-permute-done((bf16[48,384]{1,0:T(8,128)(2,1)S(1)}, bf16[48,384]{1,0:T(8,128)(2,1)S(1)}, u32[]{:S(2)}, u32[]{:S(2)}) %collective-permute-start.21) | collective-permute-done | bytes 36896 | tf_op jit(solution)/shard_map/ppermute | solution.py:538
  89.8 0.7 join.1
  (12 shorter events, 0.1 us)
Async XLA Ops:
  3.2 13.4 %collective-permute-start = (bf16[112,1536]{1,0:T(8,128)(2,1)}, bf16[112,1536]{1,0:T(8,128)(2,1)S(1)}, u32[]{:S(2)}, u32[]{:S(2)}) collective-permute-start(bf16[112,1536]{1,0:T(8,128)(2,1)} %get-tuple-element.40), channel_id=1, source_target_pairs={{0,8},{8,16},{16,24},{24,0},{1,9},{9,17},{17,25},{25,1},{2,10},{10... | collective-permute-start | bytes 1032200 | tf_op jit(solution)/shard_map/ppermute | solution.py:28
  16.5 12.1 %collective-permute-start.2 = (bf16[112,1536]{1,0:T(8,128)(2,1)S(1)}, bf16[112,1536]{1,0:T(8,128)(2,1)S(1)}, u32[]{:S(2)}, u32[]{:S(2)}) collective-permute-start(bf16[112,1536]{1,0:T(8,128)(2,1)S(1)} %collective-permute-done.refs_7_.refs_0_), channel_id=1, source_target_pairs={{0,4},{2,6},{4,0},{6,2},{1,5},{3,7},{5,1},{7,3},{8,12},{10,14},{12... | collective-permute-start | bytes 1032200 | tf_op jit(solution)/shard_map/ppermute | solution.py:402
  18.0 10.6 %collective-permute-start.1 = (bf16[112,1536]{1,0:T(8,128)(2,1)S(1)}, bf16[112,1536]{1,0:T(8,128)(2,1)S(1)}, u32[]{:S(2)}, u32[]{:S(2)}) collective-permute-start(bf16[112,1536]{1,0:T(8,128)(2,1)S(1)} %collective-permute-done.refs_7_.refs_0_), channel_id=1, source_target_pairs={{0,8},{8,16},{16,24},{24,0},{1,9},{9,17},{17,25},{25,1},{2,10},{10... | collective-permute-start | bytes 1032200 | tf_op jit(solution)/shard_map/ppermute | solution.py:28
  18.0 27.0 %collective-permute-start.6 = (bf16[64,4864]{1,0:T(8,128)(2,1)}, bf16[64,4864]{1,0:T(8,128)(2,1)S(1)}, u32[]{:S(2)}, u32[]{:S(2)}) collective-permute-start(bf16[64,4864]{1,0:T(8,128)(2,1)} %get-tuple-element.46), channel_id=1, source_target_pairs={{0,6},{2,0},{4,2},{6,4},{1,7},{3,1},{5,3},{7,5},{8,14},{10,8},{12,... | collective-permute-start | bytes 1867784 | tf_op jit(solution)/shard_map/ppermute | solution.py:28
  18.1 27.0 %collective-permute-start.7 = (bf16[64,4864]{1,0:T(8,128)(2,1)}, bf16[64,4864]{1,0:T(8,128)(2,1)S(1)}, u32[]{:S(2)}, u32[]{:S(2)}) collective-permute-start(bf16[64,4864]{1,0:T(8,128)(2,1)} %get-tuple-element.47), channel_id=1, source_target_pairs={{0,7},{1,6},{2,1},{3,0},{4,3},{5,2},{6,5},{7,4},{8,15},{9,14},{10,... | collective-permute-start | bytes 1867784 | tf_op jit(solution)/shard_map/ppermute | solution.py:458
  19.6 28.3 %collective-permute-start.5 = (bf16[64,4864]{1,0:T(8,128)(2,1)}, bf16[64,4864]{1,0:T(8,128)(2,1)S(1)}, u32[]{:S(2)}, u32[]{:S(2)}) collective-permute-start(bf16[64,4864]{1,0:T(8,128)(2,1)} %get-tuple-element.41), channel_id=1, source_target_pairs={{0,1},{1,0},{2,3},{3,2},{4,5},{5,4},{6,7},{7,6},{8,9},{9,8},{10,11... | collective-permute-start | bytes 1867784 | tf_op jit(solution)/shard_map/ppermute | solution.py:28
  28.6 9.5 %collective-permute-start.3 = (bf16[112,1536]{1,0:T(8,128)(2,1)S(1)}, bf16[112,1536]{1,0:T(8,128)(2,1)S(1)}, u32[]{:S(2)}, u32[]{:S(2)}) collective-permute-start(bf16[112,1536]{1,0:T(8,128)(2,1)S(1)} %collective-permute-done.1.refs_11_.refs_4_), channel_id=1, source_target_pairs={{0,8},{8,16},{16,24},{24,0},{1,9},{9,17},{17,25},{25,1},{2,10},{10... | collective-permute-start | bytes 1032200 | tf_op jit(solution)/shard_map/ppermute | solution.py:28
  28.6 23.8 %collective-permute-start.10 = (bf16[112,1536]{1,0:T(8,128)(2,1)S(1)}, bf16[112,1536]{1,0:T(8,128)(2,1)S(1)}, u32[]{:S(2)}, u32[]{:S(2)}) collective-permute-start(bf16[112,1536]{1,0:T(8,128)(2,1)S(1)} %collective-permute-done.1.refs_11_.refs_4_), channel_id=1, source_target_pairs={{0,4},{2,6},{4,0},{6,2},{1,5},{3,7},{5,1},{7,3},{8,12},{10,14},{12... | collective-permute-start | bytes 1032200 | tf_op jit(solution)/shard_map/ppermute | solution.py:402
  38.2 15.7 %collective-permute-start.4 = (bf16[112,1536]{1,0:T(8,128)(2,1)S(1)}, bf16[112,1536]{1,0:T(8,128)(2,1)S(1)}, u32[]{:S(2)}, u32[]{:S(2)}) collective-permute-start(bf16[112,1536]{1,0:T(8,128)(2,1)S(1)} %collective-permute-done.3.refs_15_.refs_8_), channel_id=1, source_target_pairs={{0,4},{2,6},{4,0},{6,2},{1,5},{3,7},{5,1},{7,3},{8,12},{10,14},{12... | collective-permute-start | bytes 1032200 | tf_op jit(solution)/shard_map/ppermute | solution.py:402
  47.9 8.1 %copy-start.4 = (f32[5]{0:T(128)S(1)}, f32[5]{0:T(128)}, u32[]{:S(2)}) copy-start(f32[5]{0:T(128)} %var_ref.1) | copy-start | bytes 64
  47.9 8.1 %copy-start.5 = (f32[32]{0:T(128)S(1)}, f32[32]{0:T(128)}, u32[]{:S(2)}) copy-start(f32[32]{0:T(128)} %constant.2.clone.lat_ref) | copy-start | bytes 388
  47.9 8.1 %copy-start = (bf16[384,1536]{1,0:T(8,128)(2,1)S(1)}, bf16[384,1536]{1,0:T(8,128)(2,1)}, u32[]{:S(2)}) copy-start(bf16[384,1536]{1,0:T(8,128)(2,1)} %own_w.1) | copy-start | bytes 3538948
  47.9 5.9 %collective-permute-start.8 = (bf16[112,1536]{1,0:T(8,128)(2,1)S(1)}, bf16[112,1536]{1,0:T(8,128)(2,1)S(1)}, u32[]{:S(2)}, u32[]{:S(2)}) collective-permute-start(bf16[112,1536]{1,0:T(8,128)(2,1)S(1)} %collective-permute-done.refs_7_.refs_0_), channel_id=1, source_target_pairs={{0,2},{2,0},{4,6},{6,4},{1,3},{3,1},{5,7},{7,5},{8,10},{10,8},{12,... | collective-permute-start | bytes 1032200 | tf_op jit(solution)/shard_map/ppermute | solution.py:402
  48.0 6.4 %collective-permute-start.9 = (bf16[112,1536]{1,0:T(8,128)(2,1)S(1)}, bf16[112,1536]{1,0:T(8,128)(2,1)S(1)}, u32[]{:S(2)}, u32[]{:S(2)}) collective-permute-start(bf16[112,1536]{1,0:T(8,128)(2,1)S(1)} %collective-permute-done.2.refs_8_.refs_1_), channel_id=1, source_target_pairs={{0,2},{2,0},{4,6},{6,4},{1,3},{3,1},{5,7},{7,5},{8,10},{10,8},{12,... | collective-permute-start | bytes 1032200 | tf_op jit(solution)/shard_map/ppermute | solution.py:402
  48.5 5.9 %collective-permute-start.11 = (bf16[112,1536]{1,0:T(8,128)(2,1)S(1)}, bf16[112,1536]{1,0:T(8,128)(2,1)S(1)}, u32[]{:S(2)}, u32[]{:S(2)}) collective-permute-start(bf16[112,1536]{1,0:T(8,128)(2,1)S(1)} %collective-permute-done.1.refs_11_.refs_4_), channel_id=1, source_target_pairs={{0,2},{2,0},{4,6},{6,4},{1,3},{3,1},{5,7},{7,5},{8,10},{10,8},{12,... | collective-permute-start | bytes 1032200 | tf_op jit(solution)/shard_map/ppermute | solution.py:402
  48.5 1.1 %copy-start.1 = (bf16[64,4864]{1,0:T(8,128)(2,1)S(1)}, bf16[64,4864]{1,0:T(8,128)(2,1)}, u32[]{:S(2)}) copy-start(bf16[64,4864]{1,0:T(8,128)(2,1)} %get-tuple-element.48.own_ref.refs_1_) | copy-start | bytes 1867780
  49.6 6.4 %copy-start.2 = (bf16[64,4864]{1,0:T(8,128)(2,1)S(1)}, bf16[64,4864]{1,0:T(8,128)(2,1)}, u32[]{:S(2)}) copy-start(bf16[64,4864]{1,0:T(8,128)(2,1)} %get-tuple-element.48.own_ref.refs_1_) | copy-start | bytes 1867780
  49.6 6.4 %copy-start.3 = (bf16[256,384]{1,0:T(8,128)(2,1)S(1)}, bf16[256,384]{1,0:T(8,128)(2,1)}, u32[]{:S(2)}) copy-start(bf16[256,384]{1,0:T(8,128)(2,1)} %get-tuple-element.53.refs_6_.own_ug) | copy-start | bytes 589828
  52.5 1.9 %collective-permute-start.13 = (bf16[112,1536]{1,0:T(8,128)(2,1)S(1)}, bf16[112,1536]{1,0:T(8,128)(2,1)S(1)}, u32[]{:S(2)}, u32[]{:S(2)}) collective-permute-start(bf16[112,1536]{1,0:T(8,128)(2,1)S(1)} %collective-permute-done.3.refs_15_.refs_8_), channel_id=1, source_target_pairs={{0,2},{2,0},{4,6},{6,4},{1,3},{3,1},{5,7},{7,5},{8,10},{10,8},{12,... | collective-permute-start | bytes 1032200 | tf_op jit(solution)/shard_map/ppermute | solution.py:402
  53.9 1.7 %collective-permute-start.12 = (bf16[112,1536]{1,0:T(8,128)(2,1)S(1)}, bf16[112,1536]{1,0:T(8,128)(2,1)S(1)}, u32[]{:S(2)}, u32[]{:S(2)}) collective-permute-start(bf16[112,1536]{1,0:T(8,128)(2,1)S(1)} %collective-permute-done.10.refs_12_.refs_5_), channel_id=1, source_target_pairs={{0,2},{2,0},{4,6},{6,4},{1,3},{3,1},{5,7},{7,5},{8,10},{10,8},{12,... | collective-permute-start | bytes 1032200 | tf_op jit(solution)/shard_map/ppermute | solution.py:402
  53.9 2.1 %collective-permute-start.14 = (bf16[112,1536]{1,0:T(8,128)(2,1)S(1)}, bf16[112,1536]{1,0:T(8,128)(2,1)S(1)}, u32[]{:S(2)}, u32[]{:S(2)}) collective-permute-start(bf16[112,1536]{1,0:T(8,128)(2,1)S(1)} %collective-permute-done.4.refs_16_.refs_9_), channel_id=1, source_target_pairs={{0,2},{2,0},{4,6},{6,4},{1,3},{3,1},{5,7},{7,5},{8,10},{10,8},{12,... | collective-permute-start | bytes 1032200 | tf_op jit(solution)/shard_map/ppermute | solution.py:402
  61.9 7.6 %collective-permute-start.15 = (bf16[40,1664]{1,0:T(8,128)(2,1)S(1)}, bf16[40,1664]{1,0:T(8,128)(2,1)S(1)}, u32[]{:S(2)}, u32[]{:S(2)}) collective-permute-start(bf16[40,1664]{1,0:T(8,128)(2,1)S(1)} %get-tuple-element.59), channel_id=1, source_target_pairs={{0,2},{2,0},{4,6},{6,4},{1,3},{3,1},{5,7},{7,5},{8,10},{10,8},{12,... | collective-permute-start | bytes 399368 | tf_op jit(solution)/shard_map/ppermute | solution.py:402
  62.1 7.4 %collective-permute-start.16 = (bf16[40,1664]{1,0:T(8,128)(2,1)S(1)}, bf16[40,1664]{1,0:T(8,128)(2,1)S(1)}, u32[]{:S(2)}, u32[]{:S(2)}) collective-permute-start(bf16[40,1664]{1,0:T(8,128)(2,1)S(1)} %get-tuple-element.60), channel_id=1, source_target_pairs={{0,4},{2,6},{4,0},{6,2},{1,5},{3,7},{5,1},{7,3},{8,12},{10,14},{12... | collective-permute-start | bytes 399368 | tf_op jit(solution)/shard_map/ppermute | solution.py:402
  63.4 6.8 %collective-permute-start.17 = (bf16[40,1664]{1,0:T(8,128)(2,1)S(1)}, bf16[40,1664]{1,0:T(8,128)(2,1)S(1)}, u32[]{:S(2)}, u32[]{:S(2)}) collective-permute-start(bf16[40,1664]{1,0:T(8,128)(2,1)S(1)} %get-tuple-element.61), channel_id=1, source_target_pairs={{0,6},{2,4},{4,2},{6,0},{1,7},{3,5},{5,3},{7,1},{8,14},{10,12},{12... | collective-permute-start | bytes 399368 | tf_op jit(solution)/shard_map/ppermute | solution.py:402
  70.4 4.4 %collective-permute-start.18 = (bf16[40,384]{1,0:T(8,128)(2,1)S(1)}, bf16[40,384]{1,0:T(8,128)(2,1)S(1)}, u32[]{:S(2)}, u32[]{:S(2)}) collective-permute-start(bf16[40,384]{1,0:T(8,128)(2,1)S(1)} %get-tuple-element.72), channel_id=1, source_target_pairs={{0,8},{8,0},{16,24},{24,16},{1,9},{9,1},{17,25},{25,17},{2,10},{10... | collective-permute-start | bytes 92168 | tf_op jit(solution)/shard_map/ppermute | solution.py:402
  70.7 5.3 %collective-permute-start.19 = (bf16[40,384]{1,0:T(8,128)(2,1)S(1)}, bf16[40,384]{1,0:T(8,128)(2,1)S(1)}, u32[]{:S(2)}, u32[]{:S(2)}) collective-permute-start(bf16[40,384]{1,0:T(8,128)(2,1)S(1)} %get-tuple-element.73), channel_id=1, source_target_pairs={{0,16},{8,24},{16,0},{24,8},{1,17},{9,25},{17,1},{25,9},{2,18},{10... | collective-permute-start | bytes 92168 | tf_op jit(solution)/shard_map/ppermute | solution.py:402
  73.8 5.7 %collective-permute-start.20 = (bf16[40,384]{1,0:T(8,128)(2,1)S(1)}, bf16[40,384]{1,0:T(8,128)(2,1)S(1)}, u32[]{:S(2)}, u32[]{:S(2)}) collective-permute-start(bf16[40,384]{1,0:T(8,128)(2,1)S(1)} %get-tuple-element.74), channel_id=1, source_target_pairs={{0,24},{8,16},{16,8},{24,0},{1,25},{9,17},{17,9},{25,1},{2,26},{10... | collective-permute-start | bytes 92168 | tf_op jit(solution)/shard_map/ppermute | solution.py:402
  79.5 4.7 %collective-permute-start.27 = (bf16[48,384]{1,0:T(8,128)(2,1)S(1)}, bf16[48,384]{1,0:T(8,128)(2,1)S(1)}, u32[]{:S(2)}, u32[]{:S(2)}) collective-permute-start(bf16[48,384]{1,0:T(8,128)(2,1)S(1)} %dp_sum.1.refs_0_), channel_id=1, source_target_pairs={{0,7},{1,6},{2,5},{3,4},{4,3},{5,2},{6,1},{7,0},{8,15},{9,14},{10,... | collective-permute-start | bytes 110600 | tf_op jit(solution)/shard_map/ppermute | solution.py:538
  79.6 6.3 %collective-permute-start.26 = (bf16[48,384]{1,0:T(8,128)(2,1)S(1)}, bf16[48,384]{1,0:T(8,128)(2,1)S(1)}, u32[]{:S(2)}, u32[]{:S(2)}) collective-permute-start(bf16[48,384]{1,0:T(8,128)(2,1)S(1)} %dp_sum.1.refs_0_), channel_id=1, source_target_pairs={{0,6},{1,7},{2,4},{3,5},{4,2},{5,3},{6,0},{7,1},{8,14},{9,15},{10,... | collective-permute-start | bytes 110600 | tf_op jit(solution)/shard_map/ppermute | solution.py:538
  82.3 4.9 %collective-permute-start.25 = (bf16[48,384]{1,0:T(8,128)(2,1)S(1)}, bf16[48,384]{1,0:T(8,128)(2,1)S(1)}, u32[]{:S(2)}, u32[]{:S(2)}) collective-permute-start(bf16[48,384]{1,0:T(8,128)(2,1)S(1)} %dp_sum.1.refs_0_), channel_id=1, source_target_pairs={{0,5},{1,4},{2,7},{3,6},{4,1},{5,0},{6,3},{7,2},{8,13},{9,12},{10,... | collective-permute-start | bytes 110600 | tf_op jit(solution)/shard_map/ppermute | solution.py:538
  82.8 4.4 %collective-permute-start.24 = (bf16[48,384]{1,0:T(8,128)(2,1)S(1)}, bf16[48,384]{1,0:T(8,128)(2,1)S(1)}, u32[]{:S(2)}, u32[]{:S(2)}) collective-permute-start(bf16[48,384]{1,0:T(8,128)(2,1)S(1)} %dp_sum.1.refs_0_), channel_id=1, source_target_pairs={{0,4},{1,5},{2,6},{3,7},{4,0},{5,1},{6,2},{7,3},{8,12},{9,13},{10,... | collective-permute-start | bytes 110600 | tf_op jit(solution)/shard_map/ppermute | solution.py:538
  84.3 3.7 %collective-permute-start.23 = (bf16[48,384]{1,0:T(8,128)(2,1)S(1)}, bf16[48,384]{1,0:T(8,128)(2,1)S(1)}, u32[]{:S(2)}, u32[]{:S(2)}) collective-permute-start(bf16[48,384]{1,0:T(8,128)(2,1)S(1)} %dp_sum.1.refs_0_), channel_id=1, source_target_pairs={{0,3},{1,2},{2,1},{3,0},{4,7},{5,6},{6,5},{7,4},{8,11},{9,10},{10,... | collective-permute-start | bytes 110600 | tf_op jit(solution)/shard_map/ppermute | solution.py:538
  84.3 3.7 %collective-permute-start.22 = (bf16[48,384]{1,0:T(8,128)(2,1)S(1)}, bf16[48,384]{1,0:T(8,128)(2,1)S(1)}, u32[]{:S(2)}, u32[]{:S(2)}) collective-permute-start(bf16[48,384]{1,0:T(8,128)(2,1)S(1)} %dp_sum.1.refs_0_), channel_id=1, source_target_pairs={{0,2},{1,3},{2,0},{3,1},{4,6},{5,7},{6,4},{7,5},{8,10},{9,11},{10,... | collective-permute-start | bytes 110600 | tf_op jit(solution)/shard_map/ppermute | solution.py:538
  85.9 4.0 %collective-permute-start.21 = (bf16[48,384]{1,0:T(8,128)(2,1)S(1)}, bf16[48,384]{1,0:T(8,128)(2,1)S(1)}, u32[]{:S(2)}, u32[]{:S(2)}) collective-permute-start(bf16[48,384]{1,0:T(8,128)(2,1)S(1)} %dp_sum.1.refs_0_), channel_id=1, source_target_pairs={{0,1},{1,0},{2,3},{3,2},{4,5},{5,4},{6,7},{7,6},{8,9},{9,8},{10,11... | collective-permute-start | bytes 110600 | tf_op jit(solution)/shard_map/ppermute | solution.py:538

commit v7 on v6

--- a/solution.py
+++ b/solution.py
@@ -133,31 +133,41 @@
     return lax.broadcasted_iota(jnp.int32, shape, dim)
 
 
-def payload_kernel(w_ref, unpatch_ref, gain_ref, ug_ref, payload_ref, u_in, sems):
+def payload_kernel(w_ref, unpatch_ref, gain_ref, payload_ref, ug, sems):
     part = lax.axis_index("lat")
     rows, width = w_ref.shape
     qr = rows // 4
     span = unpatch_ref.shape[0]
     start = pl.multiple_of(part * qr, 32)
+    u_copy = pltpu.make_async_copy(unpatch_ref, ug.at[pl.ds(0, span), :], sems.at[0])
+    u_copy.start()
     w_copy = pltpu.make_async_copy(
-        w_ref.at[pl.ds(start, qr), :], payload_ref.at[pl.ds(0, qr), :], sems.at[0]
-    )
-    u_copy = pltpu.make_async_copy(unpatch_ref, u_in, sems.at[1])
-    u_copy.start()
+        w_ref.at[pl.ds(start, qr), :], payload_ref.at[pl.ds(0, qr), :], sems.at[1]
+    )
     w_copy.start()
-    gain = jnp.broadcast_to(gain_ref[...].astype(F32).reshape(1, rows), (16, rows)).astype(BF)
-    ug_ref[pl.ds(span, 16), :] = gain
-    ug_ref[pl.ds(span + 16, UGROWS - span - 16), :] = jnp.zeros((UGROWS - span - 16, rows), BF)
+    ug[pl.ds(span, 16), :] = gain_rows(gain_ref, rows)
+    ug[pl.ds(span + 16, UGROWS - span - 16), :] = jnp.zeros((UGROWS - span - 16, rows), BF)
     u_copy.wait()
-    ug_ref[pl.ds(0, span), :] = u_in[...]
+    copies = [w_copy]
     for j in range(4):
         at = pl.multiple_of((4 * part + j) * 16, 16)
-        payload_ref[pl.ds(qr, 16), pl.ds(j * rows, rows)] = ug_ref[pl.ds(at, 16), :]
-    w_copy.wait()
-
-
-def pack_kernel(x_ref, t_ref, valid_ref, o0, o1, o2, o3, x_in, t_in, v_in, sems):
-    outs = (o0, o1, o2, o3)
+        copies.append(
+            pltpu.make_async_copy(
+                ug.at[pl.ds(at, 16), :],
+                payload_ref.at[pl.ds(qr, 16), pl.ds(j * rows, rows)],
+                sems.at[2 + j],
+            )
+        )
+        copies[-1].start()
+    for c in copies:
+        c.wait()
+
+
+def gain_rows(gain_ref, rows):
+    return jnp.broadcast_to(gain_ref[...].astype(F32).reshape(1, rows), (16, rows)).astype(BF)
+
+
+def pack_kernel(x_ref, t_ref, valid_ref, o0, o1, o2, o3, o4, x_in, t_in, v_in, sems):
     span = t_ref.shape[-1]
     count = x_ref.shape[0] * 64
     quarter = count // 4
@@ -191,18 +201,21 @@
     spread = jnp.broadcast_to(natural, (count, 128)).astype(BF)
     column = jnp.dot(pick, spread, preferred_element_type=F32)
     extra = jnp.concatenate([goal, column[:, : EXTRA - span]], axis=1).astype(BF)
-    for q in range(4):
-        outs[q][:, width:] = extra[q * quarter : (q + 1) * quarter]
+    outs = [(o0, 0), (o1, quarter), (o2, 2 * quarter), (o3, 3 * quarter), (o4, 7 * quarter // 2)]
+    for ref, row in outs:
+        ref[:, width:] = extra[row : row + ref.shape[0]]
     for n, at in enumerate(range(0, width, step)):
         copies[2 + n].wait()
         tokens = x_in[:, :, :, at : at + step].reshape(count, step)
         out = jnp.dot(pick, tokens, preferred_element_type=F32).astype(BF)
-        for q in range(4):
-            outs[q][:, at : at + step] = out[q * quarter : (q + 1) * quarter]
-
-
-def attention_kernel(own_ref, east_ref, south_ref, diag_ref, ctx_ref):
-    tiles = (own_ref, east_ref, south_ref, diag_ref)
+        for ref, row in outs:
+            ref[:, at : at + step] = out[row : row + ref.shape[0]]
+
+
+def attention_kernel(own_ref, east_ref, south_ref, diag0_ref, diag1_ref, ctx_ref):
+    tiles = [[r.at[32 * w : 32 * w + 32] for r in (own_ref, east_ref, south_ref)] for w in range(2)]
+    tiles[0].append(diag0_ref)
+    tiles[1].append(diag1_ref)
     part = ctx_ref.shape[1]
     is_last = lax.axis_index("lat") == lax.axis_size("lat") - 1
     same = (iota((512, 128), 0) % 128) // 64 == iota((512, 128), 1) // 64
@@ -213,7 +226,7 @@
         for w in range(2):
             q, k, v = [
                 jnp.concatenate(
-                    [t[32 * w : 32 * w + 32, i * part + at : i * part + at + 128] for t in tiles],
+                    [t[:, i * part + at : i * part + at + 128] for t in tiles[w]],
                     axis=0,
                 )
                 for i in range(3)
@@ -233,34 +246,28 @@
             ctx_ref[128 * w : 128 * w + 128, at : at + 128] = out.astype(BF)
 
 
-def piece_copies(zi, part, own_w, own_ug, pieces, w_all, ug_all, sems):
+def assemble(own_w, own_u, own_gain, pieces, w_all, ug_all):
+    zi, part = lax.axis_index("dp"), lax.axis_index("lat")
     rows = own_w.shape[0]
     qr = rows // 4
     steps = len(pieces) // 4 + 1
-    w_copies, u_copies = [], []
-
-    def place(src, dst, to):
-        at = sems.at[len(w_copies) + len(u_copies)]
-        to.append(pltpu.make_async_copy(src, dst, at))
-
     base = pl.multiple_of(zi * rows, 128)
-    place(own_w, w_all.at[pl.ds(base, rows), :], w_copies)
-    place(own_ug, ug_all.at[:, pl.ds(base, rows)], u_copies)
+    w_all[pl.ds(base, rows), :] = own_w[...]
+    span = own_u.shape[0]
+    ug_all[0:span, pl.ds(base, rows)] = own_u[...]
+    ug_all[span : span + 16, pl.ds(base, rows)] = gain_rows(own_gain, rows)
     for k in range(1, steps):
         shard = lax.rem(zi - k + steps, steps)
         base = pl.multiple_of(shard * rows, 128)
         for bits, piece in zip((0, 2, 1, 3), pieces[4 * k - 4 : 4 * k]):
             from_part = part ^ bits
             row = pl.multiple_of(base + from_part * qr, 32)
-            place(piece.at[pl.ds(0, qr), :], w_all.at[pl.ds(row, qr), :], w_copies)
+            w_all[pl.ds(row, qr), :] = piece[0:qr, :]
             for j in range(4):
                 urow = pl.multiple_of((4 * from_part + j) * 16, 16)
-                place(
-                    piece.at[pl.ds(qr, 16), pl.ds(j * rows, rows)],
-                    ug_all.at[pl.ds(urow, 16), pl.ds(base, rows)],
-                    u_copies,
-                )
-    return w_copies, u_copies
+                ug_all[pl.ds(urow, 16), pl.ds(base, rows)] = piece[
+                    qr : qr + 16, j * rows : (j + 1) * rows
+                ]
 
 
 def split3(x):
@@ -277,19 +284,19 @@
 
 def forward_kernel(lat_ref, var_ref, *refs):
     ctx_ref, refs = refs[0], refs[1:]
-    extras, refs = refs[:4], refs[4:]
-    (own_w, own_ug), refs = refs[:2], refs[2:]
+    extras, refs = refs[:5], refs[5:]
+    owned, refs = refs[:3], refs[3:]
     pieces, refs = refs[:PIECES], refs[PIECES:]
     ts, refs = refs[:4], refs[4:]
-    normed_ref, inv_ref, dfc_ref, hidden_ref, w_all, ug_all, term, sems = refs
-    zi, lat_place = lax.axis_index("dp"), lax.axis_index("lat")
-    w_copies, u_copies = piece_copies(zi, lat_place, own_w, own_ug, pieces, w_all, ug_all, sems)
-    for c in w_copies + u_copies:
-        c.start()
+    normed_ref, inv_ref, dfc_ref, hidden_ref, w_all, ug_all, term = refs
+    lat_place = lax.axis_index("lat")
+    assemble(*owned, pieces, w_all, ug_all)
     tokens, width = normed_ref.shape
     span = dfc_ref.shape[1]
     extra = jnp.concatenate(
-        [e[32 * w : 32 * w + 32, :] for w in range(2) for e in extras], axis=0
+        [e[32 * w : 32 * w + 32, :] if n < 3 else extras[3 + w][...]
+         for w in range(2) for n, e in enumerate(extras[:4])],
+        axis=0,
     ).astype(F32)
     goal, valid = extra[:, :span], extra[:, span : span + 1]
     token = iota((tokens, 1), 0)
@@ -302,8 +309,6 @@
     for n in range(var_ref.shape[0]):
         var_w = jnp.where(lane == n, var_ref[n], var_w)
     weight = lat_w * valid * var_w
-    for c in w_copies:
-        c.wait()
     mixed = jnp.dot(ctx_ref[...], w_all[...], preferred_element_type=F32)
     centre = jnp.mean(mixed, axis=-1, keepdims=True)
     off = mixed - centre
@@ -311,8 +316,6 @@
     normed = off * inv
     normed_ref[...] = normed
     inv_ref[...] = jnp.broadcast_to(inv, inv_ref.shape)
-    for c in u_copies:
-        c.wait()
     gain = ug_all[pl.ds(span, 16), :][0:1].astype(F32)
     hidden_ref[...] = (normed * gain).astype(BF)
     field = lax.dot_general(
@@ -333,16 +336,12 @@
         ref[:, width:] = block
 
 
-def backward_kernel(normed_ref, inv_ref, dfc_ref, own_w, own_ug, *refs):
-    pieces, (out_ref, w_all, ug_all, sems) = refs[:PIECES], refs[PIECES:]
-    zi, part = lax.axis_index("dp"), lax.axis_index("lat")
-    w_copies, u_copies = piece_copies(zi, part, own_w, own_ug, pieces, w_all, ug_all, sems)
-    for c in u_copies + w_copies:
-        c.start()
+def backward_kernel(normed_ref, inv_ref, dfc_ref, *refs):
+    owned, refs = refs[:3], refs[3:]
+    pieces, (out_ref, w_all, ug_all) = refs[:PIECES], refs[PIECES:]
+    assemble(*owned, pieces, w_all, ug_all)
     tokens, width = normed_ref.shape
     span = dfc_ref.shape[1]
-    for c in u_copies:
-        c.wait()
     gain = ug_all[pl.ds(span, 16), :][0:1].astype(F32)
     g = jnp.dot(dfc_ref[...], ug_all[0:span, :], preferred_element_type=F32) * gain
     normed = normed_ref[...]
@@ -355,8 +354,6 @@
     source = (level // 2) * 128 + quad * 32 + (level % 2) * 16 + (row % 4) * 4 + col % 4
     pick = (iota((tokens, tokens), 1) == source).astype(F32).astype(BF)
     dnat = jnp.dot(pick, dmixed, preferred_element_type=F32).astype(BF)
-    for c in w_copies:
-        c.wait()
     out = lax.dot_general(dnat, w_all[...], (((1,), (1,)), ((), ())), preferred_element_type=F32)
     out_ref[...] = out.astype(BF)
 
@@ -419,21 +416,23 @@
     lat_table = jnp.asarray(np.roll(cosine / cosine.mean(), -4), F32)
     barrier = lax.optimization_barrier
 
-    ug, payload = pl.pallas_call(
+    unpatch_t = unpatch_matrix.T
+    payload = pl.pallas_call(
         payload_kernel,
-        out_shape=[shape((UGROWS, rows), BF), shape((rows // 4 + 16, width), BF)],
+        out_shape=shape((rows // 4 + 16, width), BF),
         in_specs=[HBM, HBM, VMEM],
-        out_specs=[VMEM] * 2,
-        scratch_shapes=[pltpu.VMEM((span, rows), BF), pltpu.SemaphoreType.DMA((2,))],
+        out_specs=HBM,
+        scratch_shapes=[pltpu.VMEM((UGROWS, rows), BF), pltpu.SemaphoreType.DMA((6,))],
         compiler_params=params(62),
         name="payload",
-    )(w_out, unpatch_matrix.T, norm_gain)
+    )(w_out, unpatch_t, norm_gain)
     ring1 = from_behind(payload, "dp", 1)
     own, *send = pl.pallas_call(
         pack_kernel,
-        out_shape=[shape((quarter, 3 * width + EXTRA), BF)] * 4,
+        out_shape=[shape((quarter, 3 * width + EXTRA), BF)] * 3
+        + [shape((quarter // 2, 3 * width + EXTRA), BF)] * 2,
         in_specs=[HBM] * 3,
-        out_specs=[VMEM] * 4,
+        out_specs=[VMEM] * 5,
         scratch_shapes=[
             pltpu.VMEM((levels, 8, 8, 3 * width), BF),
             pltpu.VMEM((levels, 8, 8, span), BF),
@@ -450,36 +449,38 @@
     corner = [
         (a * lon + b, ((a - 1) % lat) * lon + (b - 1) % lon) for a in range(lat) for b in range(lon)
     ]
-    ring1_after, _ = barrier((ring1, send[0]))
-    tiles = (
+    tiles = [
         own,
         from_behind(send[0], "lon", -1),
         from_behind(send[1], "lat", -1),
         lax.ppermute(send[2], ("lat", "lon"), corner),
-    )
+        lax.ppermute(send[3], ("lat", "lon"), corner),
+    ]
+    ring1_after, tiles[3] = barrier((ring1, tiles[3]))
     ring2 = from_behind(ring1_after, "dp", 1)
     across1 = swap(ring1, "lat", 2)
     ring2_after, across1 = barrier((ring2, across1))
     ring3 = from_behind(ring2_after, "dp", 1)
     across2 = swap(ring2, "lat", 2)
     across3 = swap(ring3, "lat", 2)
-    ring1, across1, ring2, *tiles = barrier((ring1, across1, ring2, *tiles))
+    *tiles, ring1, across1, ring2 = barrier((*tiles, ring1, across1, ring2))
     ctx = pl.pallas_call(
         attention_kernel,
         out_shape=shape((tokens, width), BF),
-        in_specs=[VMEM] * 4,
+        in_specs=[VMEM] * 5,
         out_specs=VMEM,
         compiler_params=params(16),
         name="attention",
     )(*tiles)
-    across3, ctx = barrier((across3, ctx))
+    ctx, across3 = barrier((ctx, across3))
     pieces = []
     for ring, across in ((ring1, across1), (ring2, across2), (ring3, across3)):
         pieces += [ring, across, swap(ring, "lat", 1), swap(across, "lat", 1)]
 
     piece = span // lat
-    extra_spec = pl.BlockSpec((quarter, EXTRA), lambda i: (0, 3 * width // EXTRA))
-    copies = 2 + PIECES * 5
+    extra_specs = [
+        pl.BlockSpec((t.shape[0], EXTRA), lambda i: (0, 3 * width // EXTRA)) for t in tiles
+    ]
     assembly = [
         pltpu.VMEM((dp * rows, width), BF),
         pltpu.VMEM((UGROWS, dp * rows), BF),
@@ -489,25 +490,25 @@
         grid=(1,),
         out_shape=[shape((piece, width + 128), BF)] * 4
         + [shape((tokens, width), F32), shape((tokens, 128), F32), shape((tokens, span), BF)],
-        in_specs=[SMEM] * 2 + [VMEM] + [extra_spec] * 4 + [HBM] + [ANY] * (1 + PIECES),
+        in_specs=[SMEM] * 2 + [VMEM] + extra_specs + [VMEM] * (3 + PIECES),
         out_specs=[VMEM] * 7,
         scratch_shapes=[pltpu.VMEM((tokens, width), BF)]
         + assembly
-        + [pltpu.VMEM((span, width), F32), pltpu.SemaphoreType.DMA((copies,))],
+        + [pltpu.VMEM((span, width), F32)],
         compiler_params=params(28),
         name="forward",
-    )(lat_table, var_weight, ctx, *tiles, w_out, ug, *pieces)
+    )(lat_table, var_weight, ctx, *tiles, w_out, unpatch_t, norm_gain, *pieces)
 
     terms = [terms[0]] + [swap(terms[b], "lat", b) for b in (1, 2, 3)]
     grad_context = pl.pallas_call(
         backward_kernel,
         out_shape=shape((tokens, width), BF),
-        in_specs=[VMEM] * 3 + [HBM] + [ANY] * (1 + PIECES),
+        in_specs=[VMEM] * (6 + PIECES),
         out_specs=VMEM,
-        scratch_shapes=assembly + [pltpu.SemaphoreType.DMA((copies,))],
+        scratch_shapes=assembly,
         compiler_params=params(24),
         name="backward",
-    )(normed, inv, dfc, w_out, ug, *pieces)
+    )(normed, inv, dfc, w_out, unpatch_t, norm_gain, *pieces)
     *terms, grad_context = barrier((*terms, grad_context))
 
     *parts, loss = pl.pallas_call(

time: 90.8 us -> 99.3 us (1.094)
  Pallas kernels: 22.9 us -> 26.9 us
  waiting for transfers between devices: 39.2 us -> 41.5 us
  starting transfers between devices: 26.7 us -> 28.9 us
    pallas_call x1, Pallas kernels: 2.51 us -> 10.8 us  [shards(): pl.pallas_call(payload_kernel, out_shape=shape((rows // 4 + 16, width), B...]
    ppermute x5, waiting for transfers between devices: 19.4 us -> 11.6 us  [from_behind(): lax.ppermute(array, axis, [(i, (i + by) % length) for i in range(length)])]
    ppermute x1, waiting for transfers between devices: 0.01 us -> 7.61 us  [shards(): lax.ppermute(send[2], ('lat', 'lon'), corner)]
    ppermute x15, waiting for transfers between devices: 16.4 us -> 19.8 us  [swap(): lax.ppermute(array, axis, [(i, i ^ bit) for i in range(lax.axis_size(axis...]
    ppermute x5, starting transfers between devices: 3.62 us -> 5.89 us  [from_behind(): lax.ppermute(array, axis, [(i, (i + by) % length) for i in range(length)])]
    pallas_call x1, Pallas kernels: 5.89 us -> 3.71 us  [shards(): pl.pallas_call(forward_kernel, grid=(1,), out_shape=[shape((piece, width...]
    pallas_call x1, Pallas kernels: 5.67 us -> 3.63 us  [shards(): pl.pallas_call(backward_kernel, out_shape=shape((tokens, width), BF), in_...]
    ppermute x15, starting transfers between devices: 14.6 us -> 13.4 us  [swap(): lax.ppermute(array, axis, [(i, i ^ bit) for i in range(lax.axis_size(axis...]
  transfers between devices with their start and end apart: 28 -> 29, of which waited for: 14 -> 14; matrix products, arithmetic and copies ran while one was open for 0% -> 0% of each run, Pallas kernels for 15% -> 12%
where the time goes in v7:
time: 99.3 us; the launch traced here: 99.1 us
  waiting for transfers between devices  41.5 us (42%)
  starting transfers between devices  28.9 us (29%)
  Pallas kernels  26.9 us (27%)
  local copies, waits for them, and re-layouts  1.11 us (1%)
    ppermute x15, waiting for transfers between devices, swap(): lax.ppermute(array, axis, [(i, i ^ bit) for i in range(lax.axis_size(axis...  19.8 us
    ppermute x15, starting transfers between devices, swap(): lax.ppermute(array, axis, [(i, i ^ bit) for i in range(lax.axis_size(axis...  13.4 us
    ppermute x5, waiting for transfers between devices, from_behind(): lax.ppermute(array, axis, [(i, (i + by) % length) for i in range(length)])  11.6 us
    pallas_call x1, Pallas kernels, shards(): pl.pallas_call(payload_kernel, out_shape=shape((rows // 4 + 16, width), B...  10.8 us
    ppermute x1, waiting for transfers between devices, shards(): lax.ppermute(send[2], ('lat', 'lon'), corner)  7.61 us
    ppermute x7, starting transfers between devices, shards(): plane.append(lax.ppermute(mine, ('lat', 'lon'), pairs))  6.87 us
    ppermute x5, starting transfers between devices, from_behind(): lax.ppermute(array, axis, [(i, (i + by) % length) for i in range(length)])  5.89 us
    pallas_call x1, Pallas kernels, shards(): pl.pallas_call(pack_kernel, out_shape=[shape((quarter, 3 * width + EXTRA)...  4.97 us
  transfers between devices with their start and end apart: 29, of which 14 were waited for; matrix products, arithmetic and copies ran while one was open for 0% of the time, Pallas kernels for 12%

profile of v7, /device:TPU:0, one launch (start us, length us, event | category | flops | bytes accessed | tf_op | source)
XLA Modules:
  0.0 99.1 jit_solution(6947244926065305589)
XLA Ops:
  0.6 10.8 %payload.1 = bf16[112,1536]{1,0:T(8,128)(2,1)} custom-call(bf16[384,1536]{1,0:T(8,128)(2,1)} %refs_0_.1, bf16[160,384]{1,0:T(8,128)(2,1)} %bitcast.6, bf16[384]{0:T(512)(128)(2,1)} %refs_2_.1), custom_call_target="tpu_custom_call" | custom-call | tf_op jit(solution)/shard_map/payload/pallas_call | solution.py:420
  11.4 3.1 %collective-permute-start.2 = (bf16[112,1536]{1,0:T(8,128)(2,1)}, bf16[112,1536]{1,0:T(8,128)(2,1)S(1)}, u32[]{:S(2)}, u32[]{:S(2)}) collective-permute-start(bf16[112,1536]{1,0:T(8,128)(2,1)} %payload.1), channel_id=1, source_target_pairs={{0,8},{8,16},{16,24},{24,0},{1,9},{9,17},{17,25},{25,1},{2,10},{10... | collective-permute-start | bytes 1032200 | tf_op jit(solution)/shard_map/ppermute | solution.py:28
  14.5 5.0 %pack.1 = (bf16[64,4864]{1,0:T(8,128)(2,1)}, bf16[64,4864]{1,0:T(8,128)(2,1)}, bf16[64,4864]{1,0:T(8,128)(2,1)}, bf16[32,4864]{1,0:T(8,128)(2,1)}, bf16[32,4864]{1,0:T(8,128)(2,1)}) custom-call(bf16[4,8,8,4608]{3,2,1,0:T(8,128)(2,1)} %bitcast.9, bf16[4,8,8,160]{3,2,1,0:T(8,128)(2,1)} %bitcast.11, s32[8,8]{1,0:T(8,128)} %valid_ref.1), custom_call_target="tpu_custom_call" | custom-call | tf_op jit(solution)/shard_map/pack/pallas_call | solution.py:430
  19.5 1.7 %collective-permute-start.3 = (bf16[32,4864]{1,0:T(8,128)(2,1)}, bf16[32,4864]{1,0:T(8,128)(2,1)S(1)}, u32[]{:S(2)}, u32[]{:S(2)}) collective-permute-start(bf16[32,4864]{1,0:T(8,128)(2,1)} %get-tuple-element.44), channel_id=1, source_target_pairs={{0,7},{1,6},{2,1},{3,0},{4,3},{5,2},{6,5},{7,4},{8,15},{9,14},{10,... | collective-permute-start | bytes 933896 | tf_op jit(solution)/shard_map/ppermute | solution.py:456
  21.1 7.6 %collective-permute-done.3.diag0_ref.refs_4_ = bf16[32,4864]{1,0:T(8,128)(2,1)S(1)} collective-permute-done((bf16[32,4864]{1,0:T(8,128)(2,1)}, bf16[32,4864]{1,0:T(8,128)(2,1)S(1)}, u32[]{:S(2)}, u32[]{:S(2)}) %collective-permute-start.3) | collective-permute-done | bytes 311328 | tf_op jit(solution)/shard_map/ppermute | solution.py:456
  28.7 0.0 collective-permute-done.2.refs_9_.refs_3_
  28.7 2.1 %collective-permute-start.6 = (bf16[112,1536]{1,0:T(8,128)(2,1)S(1)}, bf16[112,1536]{1,0:T(8,128)(2,1)S(1)}, u32[]{:S(2)}, u32[]{:S(2)}) collective-permute-start(bf16[112,1536]{1,0:T(8,128)(2,1)S(1)} %collective-permute-done.2.refs_9_.refs_3_), channel_id=1, source_target_pairs={{0,4},{2,6},{4,0},{6,2},{1,5},{3,7},{5,1},{7,3},{8,12},{10,14},{12... | collective-permute-start | bytes 1032200 | tf_op jit(solution)/shard_map/ppermute | solution.py:399
  30.9 1.6 %collective-permute-start.5 = (bf16[112,1536]{1,0:T(8,128)(2,1)S(1)}, bf16[112,1536]{1,0:T(8,128)(2,1)S(1)}, u32[]{:S(2)}, u32[]{:S(2)}) collective-permute-start(bf16[112,1536]{1,0:T(8,128)(2,1)S(1)} %collective-permute-done.2.refs_9_.refs_3_), channel_id=1, source_target_pairs={{0,8},{8,16},{16,24},{24,0},{1,9},{9,17},{17,25},{25,1},{2,10},{10... | collective-permute-start | bytes 1032200 | tf_op jit(solution)/shard_map/ppermute | solution.py:28
  32.4 1.2 %collective-permute-start = (bf16[64,4864]{1,0:T(8,128)(2,1)}, bf16[64,4864]{1,0:T(8,128)(2,1)S(1)}, u32[]{:S(2)}, u32[]{:S(2)}) collective-permute-start(bf16[64,4864]{1,0:T(8,128)(2,1)} %get-tuple-element.42), channel_id=1, source_target_pairs={{0,1},{1,0},{2,3},{3,2},{4,5},{5,4},{6,7},{7,6},{8,9},{9,8},{10,11... | collective-permute-start | bytes 1867784 | tf_op jit(solution)/shard_map/ppermute | solution.py:28
  33.7 0.0 collective-permute-start.1
  33.7 5.8 %collective-permute-done.6.refs_10_.refs_4_ = bf16[112,1536]{1,0:T(8,128)(2,1)S(1)} collective-permute-done((bf16[112,1536]{1,0:T(8,128)(2,1)S(1)}, bf16[112,1536]{1,0:T(8,128)(2,1)S(1)}, u32[]{:S(2)}, u32[]{:S(2)}) %collective-permute-start.6) | collective-permute-done | bytes 344096 | tf_op jit(solution)/shard_map/ppermute | solution.py:399
  39.5 2.7 %collective-permute-done.5.refs_13_.refs_7_ = bf16[112,1536]{1,0:T(8,128)(2,1)S(1)} collective-permute-done((bf16[112,1536]{1,0:T(8,128)(2,1)S(1)}, bf16[112,1536]{1,0:T(8,128)(2,1)S(1)}, u32[]{:S(2)}, u32[]{:S(2)}) %collective-permute-start.5) | collective-permute-done | bytes 344096 | tf_op jit(solution)/shard_map/ppermute | solution.py:28
  42.2 0.0 collective-permute-start.7
  42.2 1.1 %collective-permute-start.4 = (bf16[32,4864]{1,0:T(8,128)(2,1)}, bf16[32,4864]{1,0:T(8,128)(2,1)S(1)}, u32[]{:S(2)}, u32[]{:S(2)}) collective-permute-start(bf16[32,4864]{1,0:T(8,128)(2,1)} %get-tuple-element.46), channel_id=1, source_target_pairs={{0,7},{1,6},{2,1},{3,0},{4,3},{5,2},{6,5},{7,4},{8,15},{9,14},{10,... | collective-permute-start | bytes 933896 | tf_op jit(solution)/shard_map/ppermute | solution.py:457
  43.2 0.5 collective-permute-start.11
  43.7 8.9 %collective-permute-done.7.refs_17_.refs_11_ = bf16[112,1536]{1,0:T(8,128)(2,1)S(1)} collective-permute-done((bf16[112,1536]{1,0:T(8,128)(2,1)S(1)}, bf16[112,1536]{1,0:T(8,128)(2,1)S(1)}, u32[]{:S(2)}, u32[]{:S(2)}) %collective-permute-start.7) | collective-permute-done | bytes 344096 | tf_op jit(solution)/shard_map/ppermute | solution.py:28
  52.6 2.8 %collective-permute-start.8 = (bf16[112,1536]{1,0:T(8,128)(2,1)S(1)}, bf16[112,1536]{1,0:T(8,128)(2,1)S(1)}, u32[]{:S(2)}, u32[]{:S(2)}) collective-permute-start(bf16[112,1536]{1,0:T(8,128)(2,1)S(1)} %collective-permute-done.7.refs_17_.refs_11_), channel_id=1, source_target_pairs={{0,4},{2,6},{4,0},{6,2},{1,5},{3,7},{5,1},{7,3},{8,12},{10,14},{12... | collective-permute-start | bytes 1032200 | tf_op jit(solution)/shard_map/ppermute | solution.py:399
  55.4 0.0 collective-permute-done.4.diag1_ref.refs_5_
  55.4 0.0 collective-permute-done.east_ref.refs_2_
  55.4 0.0 collective-permute-done.1.south_ref.refs_3_
  55.4 0.0 copy-start.4
  55.4 0.0 copy-start.5
  55.4 0.0 copy-start
  55.4 0.1 collective-permute-start.9
  55.5 0.5 collective-permute-start.10
  56.0 0.1 collective-permute-start.12
  56.1 1.1 %copy-done.1 = bf16[64,4864]{1,0:T(8,128)(2,1)S(1)} copy-done((bf16[64,4864]{1,0:T(8,128)(2,1)S(1)}, bf16[64,4864]{1,0:T(8,128)(2,1)}, u32[]{:S(2)}) %copy-start.1) | copy-done | bytes 622616
  57.2 2.8 %attention.1.refs_0_ = bf16[256,1536]{1,0:T(8,128)(2,1)S(1)} custom-call(bf16[64,4864]{1,0:T(8,128)(2,1)S(1)} %copy-done.1, bf16[64,4864]{1,0:T(8,128)(2,1)S(1)} %collective-permute-done.east_ref.refs_2_, bf16[64,4864]{1,0:T(8,128)(2,1)S(1)} %collective-permute-done.1.south_ref.refs_3_, bf16[32,4864]{1,0:T(8,128)(2,1)S(1)} %collective-permute-done.3.diag0_ref.refs_4_, ...), custom_call_target="tpu_custom_call" | custom-call | tf_op jit(solution)/shard_map/attention/pallas_call | solution.py:467
  60.0 0.5 collective-permute-start.14
  60.5 4.0 %collective-permute-done.8.refs_18_.refs_12_ = bf16[112,1536]{1,0:T(8,128)(2,1)S(1)} collective-permute-done((bf16[112,1536]{1,0:T(8,128)(2,1)S(1)}, bf16[112,1536]{1,0:T(8,128)(2,1)S(1)}, u32[]{:S(2)}, u32[]{:S(2)}) %collective-permute-start.8) | collective-permute-done | bytes 344096 | tf_op jit(solution)/shard_map/ppermute | solution.py:399
  64.5 0.0 collective-permute-start.13
  64.5 0.0 collective-permute-done.9.refs_11_.refs_5_
  64.5 0.5 collective-permute-start.15
  65.0 0.0 collective-permute-done.10.refs_12_.refs_6_
  65.0 0.0 collective-permute-done.12.refs_15_.refs_9_
  65.0 0.0 collective-permute-done.14.refs_19_.refs_13_
  65.0 1.1 %collective-permute-done.13.refs_16_.refs_10_ = bf16[112,1536]{1,0:T(8,128)(2,1)S(1)} collective-permute-done((bf16[112,1536]{1,0:T(8,128)(2,1)S(1)}, bf16[112,1536]{1,0:T(8,128)(2,1)S(1)}, u32[]{:S(2)}, u32[]{:S(2)}) %collective-permute-start.13) | collective-permute-done | bytes 344096 | tf_op jit(solution)/shard_map/ppermute | solution.py:399
  66.2 0.5 collective-permute-done.15.refs_20_.refs_14_
  66.7 3.7 %forward.1 = (bf16[40,1664]{1,0:T(8,128)(2,1)S(1)}, bf16[40,1664]{1,0:T(8,128)(2,1)S(1)}, bf16[40,1664]{1,0:T(8,128)(2,1)S(1)}, bf16[40,1664]{1,0:T(8,128)(2,1)S...) custom-call(f32[32]{0:T(128)S(1)} %copy-done.6, f32[5]{0:T(128)S(1)} %copy-done.5, ...), custom_call_target="tpu_custom_call" | custom-call | tf_op jit(solution)/shard_map/forward/pallas_call | solution.py:488
  70.4 0.2 collective-permute-start.16
  70.6 0.9 collective-permute-start.17
  71.5 0.8 collective-permute-start.18
  72.4 3.6 %backward.1 = bf16[256,1536]{1,0:T(8,128)(2,1)} custom-call(f32[256,1536]{1,0:T(8,128)S(1)} %get-tuple-element.64.normed_ref, f32[256,128]{1,0:T(8,128)S(1)} %get-tuple-element.65.inv_ref, bf16[256,160]{1,0:T(8,128)(2,1)S(1)} %get-tuple-element.66.dfc_ref, bf16[384,1536]{1,0:T(8,128)(2,1)S(1)} %copy-done, bf16[160,384]{1,0:T(8,128)(2,1)S(1)} %bitcast.8, ...), custom_call_target="tpu_custom_call" | custom-call | tf_op jit(solution)/shard_map/backward/pallas_call | solution.py:503
  76.0 1.0 %collective-permute-done.17.c = bf16[40,1664]{1,0:T(8,128)(2,1)S(1)} collective-permute-done((bf16[40,1664]{1,0:T(8,128)(2,1)S(1)}, bf16[40,1664]{1,0:T(8,128)(2,1)S(1)}, u32[]{:S(2)}, u32[]{:S(2)}) %collective-permute-start.17) | collective-permute-done | bytes 133152 | tf_op jit(solution)/shard_map/ppermute | solution.py:399
  77.0 1.7 %collective-permute-done.18.d = bf16[40,1664]{1,0:T(8,128)(2,1)S(1)} collective-permute-done((bf16[40,1664]{1,0:T(8,128)(2,1)S(1)}, bf16[40,1664]{1,0:T(8,128)(2,1)S(1)}, u32[]{:S(2)}, u32[]{:S(2)}) %collective-permute-start.18) | collective-permute-done | bytes 133152 | tf_op jit(solution)/shard_map/ppermute | solution.py:399
  78.7 0.2 lat_sum.1
  78.9 1.6 %collective-permute-start.19 = (bf16[40,384]{1,0:T(8,128)(2,1)S(1)}, bf16[40,384]{1,0:T(8,128)(2,1)S(1)}, u32[]{:S(2)}, u32[]{:S(2)}) collective-permute-start(bf16[40,384]{1,0:T(8,128)(2,1)S(1)} %get-tuple-element.74), channel_id=1, source_target_pairs={{0,8},{8,0},{16,24},{24,16},{1,9},{9,1},{17,25},{25,17},{2,10},{10... | collective-permute-start | bytes 92168 | tf_op jit(solution)/shard_map/ppermute | solution.py:399
  80.5 2.8 %collective-permute-start.20 = (bf16[40,384]{1,0:T(8,128)(2,1)S(1)}, bf16[40,384]{1,0:T(8,128)(2,1)S(1)}, u32[]{:S(2)}, u32[]{:S(2)}) collective-permute-start(bf16[40,384]{1,0:T(8,128)(2,1)S(1)} %get-tuple-element.75), channel_id=1, source_target_pairs={{0,16},{8,24},{16,0},{24,8},{1,17},{9,25},{17,1},{25,9},{2,18},{10... | collective-permute-start | bytes 92168 | tf_op jit(solution)/shard_map/ppermute | solution.py:399
  83.3 0.1 collective-permute-start.21
  83.3 2.4 %collective-permute-done.20.c = bf16[40,384]{1,0:T(8,128)(2,1)S(1)} collective-permute-done((bf16[40,384]{1,0:T(8,128)(2,1)S(1)}, bf16[40,384]{1,0:T(8,128)(2,1)S(1)}, u32[]{:S(2)}, u32[]{:S(2)}) %collective-permute-start.20) | collective-permute-done | bytes 30752 | tf_op jit(solution)/shard_map/ppermute | solution.py:399
  85.7 3.3 %collective-permute-done.21.d = bf16[40,384]{1,0:T(8,128)(2,1)S(1)} collective-permute-done((bf16[40,384]{1,0:T(8,128)(2,1)S(1)}, bf16[40,384]{1,0:T(8,128)(2,1)S(1)}, u32[]{:S(2)}, u32[]{:S(2)}) %collective-permute-start.21) | collective-permute-done | bytes 30752 | tf_op jit(solution)/shard_map/ppermute | solution.py:399
  89.0 0.1 collective-permute-start.28
  89.1 1.7 %collective-permute-start.27 = (bf16[48,384]{1,0:T(8,128)(2,1)S(1)}, bf16[48,384]{1,0:T(8,128)(2,1)S(1)}, u32[]{:S(2)}, u32[]{:S(2)}) collective-permute-start(bf16[48,384]{1,0:T(8,128)(2,1)S(1)} %dp_sum.1.refs_0_), channel_id=1, source_target_pairs={{0,6},{1,7},{2,4},{3,5},{4,2},{5,3},{6,0},{7,1},{8,14},{9,15},{10,... | collective-permute-start | bytes 110600 | tf_op jit(solution)/shard_map/ppermute | solution.py:539
  90.8 1.5 %collective-permute-start.26 = (bf16[48,384]{1,0:T(8,128)(2,1)S(1)}, bf16[48,384]{1,0:T(8,128)(2,1)S(1)}, u32[]{:S(2)}, u32[]{:S(2)}) collective-permute-start(bf16[48,384]{1,0:T(8,128)(2,1)S(1)} %dp_sum.1.refs_0_), channel_id=1, source_target_pairs={{0,5},{1,4},{2,7},{3,6},{4,1},{5,0},{6,3},{7,2},{8,13},{9,12},{10,... | collective-permute-start | bytes 110600 | tf_op jit(solution)/shard_map/ppermute | solution.py:539
  92.3 1.5 %collective-permute-start.25 = (bf16[48,384]{1,0:T(8,128)(2,1)S(1)}, bf16[48,384]{1,0:T(8,128)(2,1)S(1)}, u32[]{:S(2)}, u32[]{:S(2)}) collective-permute-start(bf16[48,384]{1,0:T(8,128)(2,1)S(1)} %dp_sum.1.refs_0_), channel_id=1, source_target_pairs={{0,4},{1,5},{2,6},{3,7},{4,0},{5,1},{6,2},{7,3},{8,12},{9,13},{10,... | collective-permute-start | bytes 110600 | tf_op jit(solution)/shard_map/ppermute | solution.py:539
  93.8 0.0 collective-permute-start.24
  93.8 0.0 collective-permute-done.28.refs_7_
  93.8 0.6 collective-permute-start.23
  94.4 1.5 %collective-permute-start.22 = (bf16[48,384]{1,0:T(8,128)(2,1)S(1)}, bf16[48,384]{1,0:T(8,128)(2,1)S(1)}, u32[]{:S(2)}, u32[]{:S(2)}) collective-permute-start(bf16[48,384]{1,0:T(8,128)(2,1)S(1)} %dp_sum.1.refs_0_), channel_id=1, source_target_pairs={{0,1},{1,0},{2,3},{3,2},{4,5},{5,4},{6,7},{7,6},{8,9},{9,8},{10,11... | collective-permute-start | bytes 110600 | tf_op jit(solution)/shard_map/ppermute | solution.py:539
  95.9 0.0 collective-permute-done.26.refs_5_
  95.9 0.3 collective-permute-done.25.refs_4_
  96.2 0.9 collective-permute-done.24.refs_3_
  97.1 1.2 %collective-permute-done.22.refs_1_ = bf16[48,384]{1,0:T(8,128)(2,1)S(1)} collective-permute-done((bf16[48,384]{1,0:T(8,128)(2,1)S(1)}, bf16[48,384]{1,0:T(8,128)(2,1)S(1)}, u32[]{:S(2)}, u32[]{:S(2)}) %collective-permute-start.22) | collective-permute-done | bytes 36896 | tf_op jit(solution)/shard_map/ppermute | solution.py:539
  98.4 0.7 join.1
  (16 shorter events, 0.1 us)
Async XLA Ops:
  11.4 17.3 %collective-permute-start.2 = (bf16[112,1536]{1,0:T(8,128)(2,1)}, bf16[112,1536]{1,0:T(8,128)(2,1)S(1)}, u32[]{:S(2)}, u32[]{:S(2)}) collective-permute-start(bf16[112,1536]{1,0:T(8,128)(2,1)} %payload.1), channel_id=1, source_target_pairs={{0,8},{8,16},{16,24},{24,0},{1,9},{9,17},{17,25},{25,1},{2,10},{10... | collective-permute-start | bytes 1032200 | tf_op jit(solution)/shard_map/ppermute | solution.py:28
  19.5 9.3 %collective-permute-start.3 = (bf16[32,4864]{1,0:T(8,128)(2,1)}, bf16[32,4864]{1,0:T(8,128)(2,1)S(1)}, u32[]{:S(2)}, u32[]{:S(2)}) collective-permute-start(bf16[32,4864]{1,0:T(8,128)(2,1)} %get-tuple-element.44), channel_id=1, source_target_pairs={{0,7},{1,6},{2,1},{3,0},{4,3},{5,2},{6,5},{7,4},{8,15},{9,14},{10,... | collective-permute-start | bytes 933896 | tf_op jit(solution)/shard_map/ppermute | solution.py:456
  28.7 10.7 %collective-permute-start.6 = (bf16[112,1536]{1,0:T(8,128)(2,1)S(1)}, bf16[112,1536]{1,0:T(8,128)(2,1)S(1)}, u32[]{:S(2)}, u32[]{:S(2)}) collective-permute-start(bf16[112,1536]{1,0:T(8,128)(2,1)S(1)} %collective-permute-done.2.refs_9_.refs_3_), channel_id=1, source_target_pairs={{0,4},{2,6},{4,0},{6,2},{1,5},{3,7},{5,1},{7,3},{8,12},{10,14},{12... | collective-permute-start | bytes 1032200 | tf_op jit(solution)/shard_map/ppermute | solution.py:399
  30.9 11.3 %collective-permute-start.5 = (bf16[112,1536]{1,0:T(8,128)(2,1)S(1)}, bf16[112,1536]{1,0:T(8,128)(2,1)S(1)}, u32[]{:S(2)}, u32[]{:S(2)}) collective-permute-start(bf16[112,1536]{1,0:T(8,128)(2,1)S(1)} %collective-permute-done.2.refs_9_.refs_3_), channel_id=1, source_target_pairs={{0,8},{8,16},{16,24},{24,0},{1,9},{9,17},{17,25},{25,1},{2,10},{10... | collective-permute-start | bytes 1032200 | tf_op jit(solution)/shard_map/ppermute | solution.py:28
  32.4 23.0 %collective-permute-start = (bf16[64,4864]{1,0:T(8,128)(2,1)}, bf16[64,4864]{1,0:T(8,128)(2,1)S(1)}, u32[]{:S(2)}, u32[]{:S(2)}) collective-permute-start(bf16[64,4864]{1,0:T(8,128)(2,1)} %get-tuple-element.42), channel_id=1, source_target_pairs={{0,1},{1,0},{2,3},{3,2},{4,5},{5,4},{6,7},{7,6},{8,9},{9,8},{10,11... | collective-permute-start | bytes 1867784 | tf_op jit(solution)/shard_map/ppermute | solution.py:28
  33.7 21.7 %collective-permute-start.1 = (bf16[64,4864]{1,0:T(8,128)(2,1)}, bf16[64,4864]{1,0:T(8,128)(2,1)S(1)}, u32[]{:S(2)}, u32[]{:S(2)}) collective-permute-start(bf16[64,4864]{1,0:T(8,128)(2,1)} %get-tuple-element.43), channel_id=1, source_target_pairs={{0,6},{2,0},{4,2},{6,4},{1,7},{3,1},{5,3},{7,5},{8,14},{10,8},{12,... | collective-permute-start | bytes 1867784 | tf_op jit(solution)/shard_map/ppermute | solution.py:28
  42.2 10.4 %collective-permute-start.7 = (bf16[112,1536]{1,0:T(8,128)(2,1)S(1)}, bf16[112,1536]{1,0:T(8,128)(2,1)S(1)}, u32[]{:S(2)}, u32[]{:S(2)}) collective-permute-start(bf16[112,1536]{1,0:T(8,128)(2,1)S(1)} %collective-permute-done.5.refs_13_.refs_7_), channel_id=1, source_target_pairs={{0,8},{8,16},{16,24},{24,0},{1,9},{9,17},{17,25},{25,1},{2,10},{10... | collective-permute-start | bytes 1032200 | tf_op jit(solution)/shard_map/ppermute | solution.py:28
  42.2 13.2 %collective-permute-start.4 = (bf16[32,4864]{1,0:T(8,128)(2,1)}, bf16[32,4864]{1,0:T(8,128)(2,1)S(1)}, u32[]{:S(2)}, u32[]{:S(2)}) collective-permute-start(bf16[32,4864]{1,0:T(8,128)(2,1)} %get-tuple-element.46), channel_id=1, source_target_pairs={{0,7},{1,6},{2,1},{3,0},{4,3},{5,2},{6,5},{7,4},{8,15},{9,14},{10,... | collective-permute-start | bytes 933896 | tf_op jit(solution)/shard_map/ppermute | solution.py:457
  43.2 16.8 %collective-permute-start.11 = (bf16[112,1536]{1,0:T(8,128)(2,1)S(1)}, bf16[112,1536]{1,0:T(8,128)(2,1)S(1)}, u32[]{:S(2)}, u32[]{:S(2)}) collective-permute-start(bf16[112,1536]{1,0:T(8,128)(2,1)S(1)} %collective-permute-done.5.refs_13_.refs_7_), channel_id=1, source_target_pairs={{0,4},{2,6},{4,0},{6,2},{1,5},{3,7},{5,1},{7,3},{8,12},{10,14},{12... | collective-permute-start | bytes 1032200 | tf_op jit(solution)/shard_map/ppermute | solution.py:399
  52.6 12.0 %collective-permute-start.8 = (bf16[112,1536]{1,0:T(8,128)(2,1)S(1)}, bf16[112,1536]{1,0:T(8,128)(2,1)S(1)}, u32[]{:S(2)}, u32[]{:S(2)}) collective-permute-start(bf16[112,1536]{1,0:T(8,128)(2,1)S(1)} %collective-permute-done.7.refs_17_.refs_11_), channel_id=1, source_target_pairs={{0,4},{2,6},{4,0},{6,2},{1,5},{3,7},{5,1},{7,3},{8,12},{10,14},{12... | collective-permute-start | bytes 1032200 | tf_op jit(solution)/shard_map/ppermute | solution.py:399
  55.4 11.3 %copy-start.4 = (bf16[384]{0:T(512)(128)(2,1)S(1)}, bf16[384]{0:T(512)(128)(2,1)}, u32[]{:S(2)}) copy-start(bf16[384]{0:T(512)(128)(2,1)} %refs_2_.1) | copy-start | bytes 2308
  55.4 11.3 %copy-start.5 = (f32[5]{0:T(128)S(1)}, f32[5]{0:T(128)}, u32[]{:S(2)}) copy-start(f32[5]{0:T(128)} %var_ref.1) | copy-start | bytes 64
  55.4 11.3 %copy-start = (bf16[384,1536]{1,0:T(8,128)(2,1)S(1)}, bf16[384,1536]{1,0:T(8,128)(2,1)}, u32[]{:S(2)}) copy-start(bf16[384,1536]{1,0:T(8,128)(2,1)} %refs_0_.1) | copy-start | bytes 3538948
  55.4 9.1 %collective-permute-start.9 = (bf16[112,1536]{1,0:T(8,128)(2,1)S(1)}, bf16[112,1536]{1,0:T(8,128)(2,1)S(1)}, u32[]{:S(2)}, u32[]{:S(2)}) collective-permute-start(bf16[112,1536]{1,0:T(8,128)(2,1)S(1)} %collective-permute-done.2.refs_9_.refs_3_), channel_id=1, source_target_pairs={{0,2},{2,0},{4,6},{6,4},{1,3},{3,1},{5,7},{7,5},{8,10},{10,8},{12,... | collective-permute-start | bytes 1032200 | tf_op jit(solution)/shard_map/ppermute | solution.py:399
  55.5 9.5 %collective-permute-start.10 = (bf16[112,1536]{1,0:T(8,128)(2,1)S(1)}, bf16[112,1536]{1,0:T(8,128)(2,1)S(1)}, u32[]{:S(2)}, u32[]{:S(2)}) collective-permute-start(bf16[112,1536]{1,0:T(8,128)(2,1)S(1)} %collective-permute-done.6.refs_10_.refs_4_), channel_id=1, source_target_pairs={{0,2},{2,0},{4,6},{6,4},{1,3},{3,1},{5,7},{7,5},{8,10},{10,8},{12,... | collective-permute-start | bytes 1032200 | tf_op jit(solution)/shard_map/ppermute | solution.py:399
  56.0 9.0 %collective-permute-start.12 = (bf16[112,1536]{1,0:T(8,128)(2,1)S(1)}, bf16[112,1536]{1,0:T(8,128)(2,1)S(1)}, u32[]{:S(2)}, u32[]{:S(2)}) collective-permute-start(bf16[112,1536]{1,0:T(8,128)(2,1)S(1)} %collective-permute-done.5.refs_13_.refs_7_), channel_id=1, source_target_pairs={{0,2},{2,0},{4,6},{6,4},{1,3},{3,1},{5,7},{7,5},{8,10},{10,8},{12,... | collective-permute-start | bytes 1032200 | tf_op jit(solution)/shard_map/ppermute | solution.py:399
  56.1 1.1 %copy-start.1 = (bf16[64,4864]{1,0:T(8,128)(2,1)S(1)}, bf16[64,4864]{1,0:T(8,128)(2,1)}, u32[]{:S(2)}) copy-start(bf16[64,4864]{1,0:T(8,128)(2,1)} %get-tuple-element.49.own_ref.refs_1_) | copy-start | bytes 1867780
  57.2 9.5 %copy-start.2 = (bf16[64,4864]{1,0:T(8,128)(2,1)S(1)}, bf16[64,4864]{1,0:T(8,128)(2,1)}, u32[]{:S(2)}) copy-start(bf16[64,4864]{1,0:T(8,128)(2,1)} %get-tuple-element.49.own_ref.refs_1_) | copy-start | bytes 1867780
  57.2 9.5 %copy-start.3 = (bf16[384,160]{0,1:T(8,128)(2,1)S(1)}, bf16[384,160]{0,1:T(8,128)(2,1)}, u32[]{:S(2)}) copy-start(bf16[384,160]{0,1:T(8,128)(2,1)} %param.12) | copy-start | bytes 368644
  57.2 9.5 %copy-start.6 = (f32[32]{0:T(128)S(1)}, f32[32]{0:T(128)}, u32[]{:S(2)}) copy-start(f32[32]{0:T(128)} %constant.2.clone.lat_ref) | copy-start | bytes 388
  60.0 5.0 %collective-permute-start.14 = (bf16[112,1536]{1,0:T(8,128)(2,1)S(1)}, bf16[112,1536]{1,0:T(8,128)(2,1)S(1)}, u32[]{:S(2)}, u32[]{:S(2)}) collective-permute-start(bf16[112,1536]{1,0:T(8,128)(2,1)S(1)} %collective-permute-done.7.refs_17_.refs_11_), channel_id=1, source_target_pairs={{0,2},{2,0},{4,6},{6,4},{1,3},{3,1},{5,7},{7,5},{8,10},{10,8},{12,... | collective-permute-start | bytes 1032200 | tf_op jit(solution)/shard_map/ppermute | solution.py:399
  64.5 1.7 %collective-permute-start.13 = (bf16[112,1536]{1,0:T(8,128)(2,1)S(1)}, bf16[112,1536]{1,0:T(8,128)(2,1)S(1)}, u32[]{:S(2)}, u32[]{:S(2)}) collective-permute-start(bf16[112,1536]{1,0:T(8,128)(2,1)S(1)} %collective-permute-done.11.refs_14_.refs_8_), channel_id=1, source_target_pairs={{0,2},{2,0},{4,6},{6,4},{1,3},{3,1},{5,7},{7,5},{8,10},{10,8},{12,... | collective-permute-start | bytes 1032200 | tf_op jit(solution)/shard_map/ppermute | solution.py:399
  64.5 2.1 %collective-permute-start.15 = (bf16[112,1536]{1,0:T(8,128)(2,1)S(1)}, bf16[112,1536]{1,0:T(8,128)(2,1)S(1)}, u32[]{:S(2)}, u32[]{:S(2)}) collective-permute-start(bf16[112,1536]{1,0:T(8,128)(2,1)S(1)} %collective-permute-done.8.refs_18_.refs_12_), channel_id=1, source_target_pairs={{0,2},{2,0},{4,6},{6,4},{1,3},{3,1},{5,7},{7,5},{8,10},{10,8},{12,... | collective-permute-start | bytes 1032200 | tf_op jit(solution)/shard_map/ppermute | solution.py:399
  70.4 5.6 %collective-permute-start.16 = (bf16[40,1664]{1,0:T(8,128)(2,1)S(1)}, bf16[40,1664]{1,0:T(8,128)(2,1)S(1)}, u32[]{:S(2)}, u32[]{:S(2)}) collective-permute-start(bf16[40,1664]{1,0:T(8,128)(2,1)S(1)} %get-tuple-element.61), channel_id=1, source_target_pairs={{0,2},{2,0},{4,6},{6,4},{1,3},{3,1},{5,7},{7,5},{8,10},{10,8},{12,... | collective-permute-start | bytes 399368 | tf_op jit(solution)/shard_map/ppermute | solution.py:399
  70.6 6.4 %collective-permute-start.17 = (bf16[40,1664]{1,0:T(8,128)(2,1)S(1)}, bf16[40,1664]{1,0:T(8,128)(2,1)S(1)}, u32[]{:S(2)}, u32[]{:S(2)}) collective-permute-start(bf16[40,1664]{1,0:T(8,128)(2,1)S(1)} %get-tuple-element.62), channel_id=1, source_target_pairs={{0,4},{2,6},{4,0},{6,2},{1,5},{3,7},{5,1},{7,3},{8,12},{10,14},{12... | collective-permute-start | bytes 399368 | tf_op jit(solution)/shard_map/ppermute | solution.py:399
  71.5 7.2 %collective-permute-start.18 = (bf16[40,1664]{1,0:T(8,128)(2,1)S(1)}, bf16[40,1664]{1,0:T(8,128)(2,1)S(1)}, u32[]{:S(2)}, u32[]{:S(2)}) collective-permute-start(bf16[40,1664]{1,0:T(8,128)(2,1)S(1)} %get-tuple-element.63), channel_id=1, source_target_pairs={{0,6},{2,4},{4,2},{6,0},{1,7},{3,5},{5,3},{7,1},{8,14},{10,12},{12... | collective-permute-start | bytes 399368 | tf_op jit(solution)/shard_map/ppermute | solution.py:399
  78.9 4.4 %collective-permute-start.19 = (bf16[40,384]{1,0:T(8,128)(2,1)S(1)}, bf16[40,384]{1,0:T(8,128)(2,1)S(1)}, u32[]{:S(2)}, u32[]{:S(2)}) collective-permute-start(bf16[40,384]{1,0:T(8,128)(2,1)S(1)} %get-tuple-element.74), channel_id=1, source_target_pairs={{0,8},{8,0},{16,24},{24,16},{1,9},{9,1},{17,25},{25,17},{2,10},{10... | collective-permute-start | bytes 92168 | tf_op jit(solution)/shard_map/ppermute | solution.py:399
  80.5 5.2 %collective-permute-start.20 = (bf16[40,384]{1,0:T(8,128)(2,1)S(1)}, bf16[40,384]{1,0:T(8,128)(2,1)S(1)}, u32[]{:S(2)}, u32[]{:S(2)}) collective-permute-start(bf16[40,384]{1,0:T(8,128)(2,1)S(1)} %get-tuple-element.75), channel_id=1, source_target_pairs={{0,16},{8,24},{16,0},{24,8},{1,17},{9,25},{17,1},{25,9},{2,18},{10... | collective-permute-start | bytes 92168 | tf_op jit(solution)/shard_map/ppermute | solution.py:399
  83.3 5.7 %collective-permute-start.21 = (bf16[40,384]{1,0:T(8,128)(2,1)S(1)}, bf16[40,384]{1,0:T(8,128)(2,1)S(1)}, u32[]{:S(2)}, u32[]{:S(2)}) collective-permute-start(bf16[40,384]{1,0:T(8,128)(2,1)S(1)} %get-tuple-element.76), channel_id=1, source_target_pairs={{0,24},{8,16},{16,8},{24,0},{1,25},{9,17},{17,9},{25,1},{2,26},{10... | collective-permute-start | bytes 92168 | tf_op jit(solution)/shard_map/ppermute | solution.py:399
  89.0 4.7 %collective-permute-start.28 = (bf16[48,384]{1,0:T(8,128)(2,1)S(1)}, bf16[48,384]{1,0:T(8,128)(2,1)S(1)}, u32[]{:S(2)}, u32[]{:S(2)}) collective-permute-start(bf16[48,384]{1,0:T(8,128)(2,1)S(1)} %dp_sum.1.refs_0_), channel_id=1, source_target_pairs={{0,7},{1,6},{2,5},{3,4},{4,3},{5,2},{6,1},{7,0},{8,15},{9,14},{10,... | collective-permute-start | bytes 110600 | tf_op jit(solution)/shard_map/ppermute | solution.py:539
  89.1 5.3 %collective-permute-start.27 = (bf16[48,384]{1,0:T(8,128)(2,1)S(1)}, bf16[48,384]{1,0:T(8,128)(2,1)S(1)}, u32[]{:S(2)}, u32[]{:S(2)}) collective-permute-start(bf16[48,384]{1,0:T(8,128)(2,1)S(1)} %dp_sum.1.refs_0_), channel_id=1, source_target_pairs={{0,6},{1,7},{2,4},{3,5},{4,2},{5,3},{6,0},{7,1},{8,14},{9,15},{10,... | collective-permute-start | bytes 110600 | tf_op jit(solution)/shard_map/ppermute | solution.py:539
  90.8 5.1 %collective-permute-start.26 = (bf16[48,384]{1,0:T(8,128)(2,1)S(1)}, bf16[48,384]{1,0:T(8,128)(2,1)S(1)}, u32[]{:S(2)}, u32[]{:S(2)}) collective-permute-start(bf16[48,384]{1,0:T(8,128)(2,1)S(1)} %dp_sum.1.refs_0_), channel_id=1, source_target_pairs={{0,5},{1,4},{2,7},{3,6},{4,1},{5,0},{6,3},{7,2},{8,13},{9,12},{10,... | collective-permute-start | bytes 110600 | tf_op jit(solution)/shard_map/ppermute | solution.py:539
  92.3 4.0 %collective-permute-start.25 = (bf16[48,384]{1,0:T(8,128)(2,1)S(1)}, bf16[48,384]{1,0:T(8,128)(2,1)S(1)}, u32[]{:S(2)}, u32[]{:S(2)}) collective-permute-start(bf16[48,384]{1,0:T(8,128)(2,1)S(1)} %dp_sum.1.refs_0_), channel_id=1, source_target_pairs={{0,4},{1,5},{2,6},{3,7},{4,0},{5,1},{6,2},{7,3},{8,12},{9,13},{10,... | collective-permute-start | bytes 110600 | tf_op jit(solution)/shard_map/ppermute | solution.py:539
  93.8 3.4 %collective-permute-start.24 = (bf16[48,384]{1,0:T(8,128)(2,1)S(1)}, bf16[48,384]{1,0:T(8,128)(2,1)S(1)}, u32[]{:S(2)}, u32[]{:S(2)}) collective-permute-start(bf16[48,384]{1,0:T(8,128)(2,1)S(1)} %dp_sum.1.refs_0_), channel_id=1, source_target_pairs={{0,3},{1,2},{2,1},{3,0},{4,7},{5,6},{6,5},{7,4},{8,11},{9,10},{10,... | collective-permute-start | bytes 110600 | tf_op jit(solution)/shard_map/ppermute | solution.py:539
  93.8 3.4 %collective-permute-start.23 = (bf16[48,384]{1,0:T(8,128)(2,1)S(1)}, bf16[48,384]{1,0:T(8,128)(2,1)S(1)}, u32[]{:S(2)}, u32[]{:S(2)}) collective-permute-start(bf16[48,384]{1,0:T(8,128)(2,1)S(1)} %dp_sum.1.refs_0_), channel_id=1, source_target_pairs={{0,2},{1,3},{2,0},{3,1},{4,6},{5,7},{6,4},{7,5},{8,10},{9,11},{10,... | collective-permute-start | bytes 110600 | tf_op jit(solution)/shard_map/ppermute | solution.py:539
  94.4 4.0 %collective-permute-start.22 = (bf16[48,384]{1,0:T(8,128)(2,1)S(1)}, bf16[48,384]{1,0:T(8,128)(2,1)S(1)}, u32[]{:S(2)}, u32[]{:S(2)}) collective-permute-start(bf16[48,384]{1,0:T(8,128)(2,1)S(1)} %dp_sum.1.refs_0_), channel_id=1, source_target_pairs={{0,1},{1,0},{2,3},{3,2},{4,5},{5,4},{6,7},{7,6},{8,9},{9,8},{10,11... | collective-permute-start | bytes 110600 | tf_op jit(solution)/shard_map/ppermute | solution.py:539

commit v8 on v7

--- a/solution.py
+++ b/solution.py
@@ -148,19 +148,10 @@
     ug[pl.ds(span, 16), :] = gain_rows(gain_ref, rows)
     ug[pl.ds(span + 16, UGROWS - span - 16), :] = jnp.zeros((UGROWS - span - 16, rows), BF)
     u_copy.wait()
-    copies = [w_copy]
     for j in range(4):
         at = pl.multiple_of((4 * part + j) * 16, 16)
-        copies.append(
-            pltpu.make_async_copy(
-                ug.at[pl.ds(at, 16), :],
-                payload_ref.at[pl.ds(qr, 16), pl.ds(j * rows, rows)],
-                sems.at[2 + j],
-            )
-        )
-        copies[-1].start()
-    for c in copies:
-        c.wait()
+        payload_ref[pl.ds(qr, 16), pl.ds(j * rows, rows)] = ug[pl.ds(at, 16), :]
+    w_copy.wait()
 
 
 def gain_rows(gain_ref, rows):
@@ -201,7 +192,7 @@
     spread = jnp.broadcast_to(natural, (count, 128)).astype(BF)
     column = jnp.dot(pick, spread, preferred_element_type=F32)
     extra = jnp.concatenate([goal, column[:, : EXTRA - span]], axis=1).astype(BF)
-    outs = [(o0, 0), (o1, quarter), (o2, 2 * quarter), (o3, 3 * quarter), (o4, 7 * quarter // 2)]
+    outs = [(o0, 0), (o1, quarter), (o2, 2 * quarter), (o3, 5 * quarter // 2), (o4, 3 * quarter)]
     for ref, row in outs:
         ref[:, width:] = extra[row : row + ref.shape[0]]
     for n, at in enumerate(range(0, width, step)):
@@ -212,10 +203,20 @@
             ref[:, at : at + step] = out[row : row + ref.shape[0]]
 
 
-def attention_kernel(own_ref, east_ref, south_ref, diag0_ref, diag1_ref, ctx_ref):
-    tiles = [[r.at[32 * w : 32 * w + 32] for r in (own_ref, east_ref, south_ref)] for w in range(2)]
-    tiles[0].append(diag0_ref)
-    tiles[1].append(diag1_ref)
+def windows_of(own_ref, east_ref, south0_ref, south1_ref, diag_ref):
+    return [
+        (
+            own_ref.at[32 * w : 32 * w + 32],
+            east_ref.at[32 * w : 32 * w + 32],
+            south,
+            diag_ref.at[32 * w : 32 * w + 32],
+        )
+        for w, south in enumerate((south0_ref, south1_ref))
+    ]
+
+
+def attention_kernel(own_ref, east_ref, south0_ref, south1_ref, diag_ref, ctx_ref):
+    tiles = windows_of(own_ref, east_ref, south0_ref, south1_ref, diag_ref)
     part = ctx_ref.shape[1]
     is_last = lax.axis_index("lat") == lax.axis_size("lat") - 1
     same = (iota((512, 128), 0) % 128) // 64 == iota((512, 128), 1) // 64
@@ -293,11 +294,8 @@
     assemble(*owned, pieces, w_all, ug_all)
     tokens, width = normed_ref.shape
     span = dfc_ref.shape[1]
-    extra = jnp.concatenate(
-        [e[32 * w : 32 * w + 32, :] if n < 3 else extras[3 + w][...]
-         for w in range(2) for n, e in enumerate(extras[:4])],
-        axis=0,
-    ).astype(F32)
+    extra = jnp.concatenate([t[...] for tiles in windows_of(*extras) for t in tiles], axis=0)
+    extra = extra.astype(F32)
     goal, valid = extra[:, :span], extra[:, span : span + 1]
     token = iota((tokens, 1), 0)
     row = (token // 4) % 4 + jnp.where((token // 32) % 4 >= 2, 4, 0)
@@ -421,16 +419,17 @@
         payload_kernel,
         out_shape=shape((rows // 4 + 16, width), BF),
         in_specs=[HBM, HBM, VMEM],
-        out_specs=HBM,
-        scratch_shapes=[pltpu.VMEM((UGROWS, rows), BF), pltpu.SemaphoreType.DMA((6,))],
-        compiler_params=params(62),
+        out_specs=VMEM,
+        scratch_shapes=[pltpu.VMEM((UGROWS, rows), BF), pltpu.SemaphoreType.DMA((2,))],
+        compiler_params=params(60),
         name="payload",
     )(w_out, unpatch_t, norm_gain)
     ring1 = from_behind(payload, "dp", 1)
     own, *send = pl.pallas_call(
         pack_kernel,
-        out_shape=[shape((quarter, 3 * width + EXTRA), BF)] * 3
-        + [shape((quarter // 2, 3 * width + EXTRA), BF)] * 2,
+        out_shape=[shape((quarter, 3 * width + EXTRA), BF)] * 2
+        + [shape((quarter // 2, 3 * width + EXTRA), BF)] * 2
+        + [shape((quarter, 3 * width + EXTRA), BF)],
         in_specs=[HBM] * 3,
         out_specs=[VMEM] * 5,
         scratch_shapes=[
@@ -453,10 +452,10 @@
         own,
         from_behind(send[0], "lon", -1),
         from_behind(send[1], "lat", -1),
-        lax.ppermute(send[2], ("lat", "lon"), corner),
+        from_behind(send[2], "lat", -1),
         lax.ppermute(send[3], ("lat", "lon"), corner),
     ]
-    ring1_after, tiles[3] = barrier((ring1, tiles[3]))
+    ring1_after, tiles[2] = barrier((ring1, tiles[2]))
     ring2 = from_behind(ring1_after, "dp", 1)
     across1 = swap(ring1, "lat", 2)
     ring2_after, across1 = barrier((ring2, across1))

time: 99.3 us -> 93.8 us (0.945)
  Pallas kernels: 26.9 us -> 18.6 us
  waiting for transfers between devices: 41.5 us -> 47.6 us
  starting transfers between devices: 28.9 us -> 25.6 us
    pallas_call x1, Pallas kernels: 10.8 us -> 2.46 us  [shards(): pl.pallas_call(payload_kernel, out_shape=shape((rows // 4 + 16, width), B...]
    ppermute x1 -> x0, waiting for transfers between devices: 7.61 us -> none  [shards(): lax.ppermute(send[2], ('lat', 'lon'), corner)]
    ppermute x1, waiting for transfers between devices: 0.01 us -> 6.37 us  [shards(): lax.ppermute(send[3], ('lat', 'lon'), corner)]
    ppermute x5 -> x6, waiting for transfers between devices: 11.6 us -> 17.7 us  [from_behind(): lax.ppermute(array, axis, [(i, (i + by) % length) for i in range(length)])]
    ppermute x15, starting transfers between devices: 13.4 us -> 11.1 us  [swap(): lax.ppermute(array, axis, [(i, i ^ bit) for i in range(lax.axis_size(axis...]
    ppermute x1 -> x0, starting transfers between devices: 1.66 us -> none  [shards(): lax.ppermute(send[2], ('lat', 'lon'), corner)]
    ppermute x5 -> x6, starting transfers between devices: 5.89 us -> 6.73 us  [from_behind(): lax.ppermute(array, axis, [(i, (i + by) % length) for i in range(length)])]
  transfers between devices with their start and end apart: 29 -> 29, of which waited for: 14 -> 17; matrix products, arithmetic and copies ran while one was open for 0% -> 0% of each run, Pallas kernels for 12% -> 12%
where the time goes in v8:
time: 93.8 us; the launch traced here: 93.6 us
  waiting for transfers between devices  47.6 us (51%)
  starting transfers between devices  25.6 us (27%)
  Pallas kernels  18.6 us (20%)
  local copies, waits for them, and re-layouts  1.1 us (1%)
    ppermute x15, waiting for transfers between devices, swap(): lax.ppermute(array, axis, [(i, i ^ bit) for i in range(lax.axis_size(axis...  20.1 us
    ppermute x6, waiting for transfers between devices, from_behind(): lax.ppermute(array, axis, [(i, (i + by) % length) for i in range(length)])  17.7 us
    ppermute x15, starting transfers between devices, swap(): lax.ppermute(array, axis, [(i, i ^ bit) for i in range(lax.axis_size(axis...  11.1 us
    ppermute x7, starting transfers between devices, shards(): plane.append(lax.ppermute(mine, ('lat', 'lon'), pairs))  6.88 us
    ppermute x6, starting transfers between devices, from_behind(): lax.ppermute(array, axis, [(i, (i + by) % length) for i in range(length)])  6.73 us
    ppermute x1, waiting for transfers between devices, shards(): lax.ppermute(send[3], ('lat', 'lon'), corner)  6.37 us
    pallas_call x1, Pallas kernels, shards(): pl.pallas_call(pack_kernel, out_shape=[shape((quarter, 3 * width + EXTRA)...  5.01 us
    pallas_call x1, Pallas kernels, shards(): pl.pallas_call(forward_kernel, grid=(1,), out_shape=[shape((piece, width...  3.71 us
  transfers between devices with their start and end apart: 29, of which 17 were waited for; matrix products, arithmetic and copies ran while one was open for 0% of the time, Pallas kernels for 12%

profile of v8, /device:TPU:0, one launch (start us, length us, event | category | flops | bytes accessed | tf_op | source)
XLA Modules:
  0.0 93.6 jit_solution(8353590043083518146)
XLA Ops:
  0.6 2.5 %payload.1 = bf16[112,1536]{1,0:T(8,128)(2,1)} custom-call(bf16[384,1536]{1,0:T(8,128)(2,1)} %refs_0_.1, bf16[160,384]{1,0:T(8,128)(2,1)} %bitcast.6, bf16[384]{0:T(512)(128)(2,1)} %refs_2_.1), custom_call_target="tpu_custom_call" | custom-call | tf_op jit(solution)/shard_map/payload/pallas_call | solution.py:418
  3.1 3.1 %collective-permute-start.1 = (bf16[112,1536]{1,0:T(8,128)(2,1)}, bf16[112,1536]{1,0:T(8,128)(2,1)S(1)}, u32[]{:S(2)}, u32[]{:S(2)}) collective-permute-start(bf16[112,1536]{1,0:T(8,128)(2,1)} %payload.1), channel_id=1, source_target_pairs={{0,8},{8,16},{16,24},{24,0},{1,9},{9,17},{17,25},{25,1},{2,10},{10... | collective-permute-start | bytes 1032200 | tf_op jit(solution)/shard_map/ppermute | solution.py:28
  6.2 5.0 %pack.1 = (bf16[64,4864]{1,0:T(8,128)(2,1)}, bf16[64,4864]{1,0:T(8,128)(2,1)}, bf16[32,4864]{1,0:T(8,128)(2,1)}, bf16[32,4864]{1,0:T(8,128)(2,1)}, bf16[64,4864]{1,0:T(8,128)(2,1)}) custom-call(bf16[4,8,8,4608]{3,2,1,0:T(8,128)(2,1)} %bitcast.9, bf16[4,8,8,160]{3,2,1,0:T(8,128)(2,1)} %bitcast.11, s32[8,8]{1,0:T(8,128)} %valid_ref.1), custom_call_target="tpu_custom_call" | custom-call | tf_op jit(solution)/shard_map/pack/pallas_call | solution.py:428
  11.2 0.7 collective-permute-start.2
  11.9 4.7 %collective-permute-done.2.south0_ref.refs_3_ = bf16[32,4864]{1,0:T(8,128)(2,1)S(1)} collective-permute-done((bf16[32,4864]{1,0:T(8,128)(2,1)}, bf16[32,4864]{1,0:T(8,128)(2,1)S(1)}, u32[]{:S(2)}, u32[]{:S(2)}) %collective-permute-start.2) | collective-permute-done | bytes 311328 | tf_op jit(solution)/shard_map/ppermute | solution.py:28
  16.7 0.0 collective-permute-done.1.refs_9_.refs_3_
  16.7 1.3 %collective-permute-start.6 = (bf16[112,1536]{1,0:T(8,128)(2,1)S(1)}, bf16[112,1536]{1,0:T(8,128)(2,1)S(1)}, u32[]{:S(2)}, u32[]{:S(2)}) collective-permute-start(bf16[112,1536]{1,0:T(8,128)(2,1)S(1)} %collective-permute-done.1.refs_9_.refs_3_), channel_id=1, source_target_pairs={{0,4},{2,6},{4,0},{6,2},{1,5},{3,7},{5,1},{7,3},{8,12},{10,14},{12... | collective-permute-start | bytes 1032200 | tf_op jit(solution)/shard_map/ppermute | solution.py:397
  18.0 1.1 %collective-permute-start.5 = (bf16[112,1536]{1,0:T(8,128)(2,1)S(1)}, bf16[112,1536]{1,0:T(8,128)(2,1)S(1)}, u32[]{:S(2)}, u32[]{:S(2)}) collective-permute-start(bf16[112,1536]{1,0:T(8,128)(2,1)S(1)} %collective-permute-done.1.refs_9_.refs_3_), channel_id=1, source_target_pairs={{0,8},{8,16},{16,24},{24,0},{1,9},{9,17},{17,25},{25,1},{2,10},{10... | collective-permute-start | bytes 1032200 | tf_op jit(solution)/shard_map/ppermute | solution.py:28
  19.1 1.5 %collective-permute-start = (bf16[64,4864]{1,0:T(8,128)(2,1)}, bf16[64,4864]{1,0:T(8,128)(2,1)S(1)}, u32[]{:S(2)}, u32[]{:S(2)}) collective-permute-start(bf16[64,4864]{1,0:T(8,128)(2,1)} %get-tuple-element.42), channel_id=1, source_target_pairs={{0,1},{1,0},{2,3},{3,2},{4,5},{5,4},{6,7},{7,6},{8,9},{9,8},{10,11... | collective-permute-start | bytes 1867784 | tf_op jit(solution)/shard_map/ppermute | solution.py:28
  20.6 0.9 collective-permute-start.4
  21.5 6.0 %collective-permute-done.6.refs_10_.refs_4_ = bf16[112,1536]{1,0:T(8,128)(2,1)S(1)} collective-permute-done((bf16[112,1536]{1,0:T(8,128)(2,1)S(1)}, bf16[112,1536]{1,0:T(8,128)(2,1)S(1)}, u32[]{:S(2)}, u32[]{:S(2)}) %collective-permute-start.6) | collective-permute-done | bytes 344096 | tf_op jit(solution)/shard_map/ppermute | solution.py:397
  27.6 2.8 %collective-permute-done.5.refs_13_.refs_7_ = bf16[112,1536]{1,0:T(8,128)(2,1)S(1)} collective-permute-done((bf16[112,1536]{1,0:T(8,128)(2,1)S(1)}, bf16[112,1536]{1,0:T(8,128)(2,1)S(1)}, u32[]{:S(2)}, u32[]{:S(2)}) %collective-permute-start.5) | collective-permute-done | bytes 344096 | tf_op jit(solution)/shard_map/ppermute | solution.py:28
  30.4 0.0 collective-permute-start.7
  30.4 0.3 collective-permute-start.3
  30.7 1.1 %collective-permute-start.11 = (bf16[112,1536]{1,0:T(8,128)(2,1)S(1)}, bf16[112,1536]{1,0:T(8,128)(2,1)S(1)}, u32[]{:S(2)}, u32[]{:S(2)}) collective-permute-start(bf16[112,1536]{1,0:T(8,128)(2,1)S(1)} %collective-permute-done.5.refs_13_.refs_7_), channel_id=1, source_target_pairs={{0,4},{2,6},{4,0},{6,2},{1,5},{3,7},{5,1},{7,3},{8,12},{10,14},{12... | collective-permute-start | bytes 1032200 | tf_op jit(solution)/shard_map/ppermute | solution.py:397
  31.8 10.1 %collective-permute-done.7.refs_17_.refs_11_ = bf16[112,1536]{1,0:T(8,128)(2,1)S(1)} collective-permute-done((bf16[112,1536]{1,0:T(8,128)(2,1)S(1)}, bf16[112,1536]{1,0:T(8,128)(2,1)S(1)}, u32[]{:S(2)}, u32[]{:S(2)}) %collective-permute-start.7) | collective-permute-done | bytes 344096 | tf_op jit(solution)/shard_map/ppermute | solution.py:28
  41.9 0.9 collective-permute-start.8
  42.8 0.0 collective-permute-done.3.south1_ref.refs_4_
  42.8 6.4 %collective-permute-done.4.diag_ref.refs_5_ = bf16[64,4864]{1,0:T(8,128)(2,1)S(1)} collective-permute-done((bf16[64,4864]{1,0:T(8,128)(2,1)}, bf16[64,4864]{1,0:T(8,128)(2,1)S(1)}, u32[]{:S(2)}, u32[]{:S(2)}) %collective-permute-start.4) | collective-permute-done | bytes 622624 | tf_op jit(solution)/shard_map/ppermute | solution.py:456
  49.2 0.4 collective-permute-start.9
  49.6 0.1 collective-permute-start.10
  49.7 0.4 collective-permute-start.12
  50.1 1.1 %copy-done.1 = bf16[64,4864]{1,0:T(8,128)(2,1)S(1)} copy-done((bf16[64,4864]{1,0:T(8,128)(2,1)S(1)}, bf16[64,4864]{1,0:T(8,128)(2,1)}, u32[]{:S(2)}) %copy-start.1) | copy-done | bytes 622616
  51.2 2.8 %attention.1.refs_0_ = bf16[256,1536]{1,0:T(8,128)(2,1)S(1)} custom-call(bf16[64,4864]{1,0:T(8,128)(2,1)S(1)} %copy-done.1, bf16[64,4864]{1,0:T(8,128)(2,1)S(1)} %collective-permute-done.east_ref.refs_2_, bf16[32,4864]{1,0:T(8,128)(2,1)S(1)} %collective-permute-done.2.south0_ref.refs_3_, bf16[32,4864]{1,0:T(8,128)(2,1)S(1)} %collective-permute-done.3.south1_ref.refs_4_, ...), custom_call_target="tpu_custom_call" | custom-call | tf_op jit(solution)/shard_map/attention/pallas_call | solution.py:466
  54.0 0.2 collective-permute-done.11.refs_14_.refs_8_
  54.3 0.0 collective-permute-start.14
  54.3 3.9 %collective-permute-done.8.refs_18_.refs_12_ = bf16[112,1536]{1,0:T(8,128)(2,1)S(1)} collective-permute-done((bf16[112,1536]{1,0:T(8,128)(2,1)S(1)}, bf16[112,1536]{1,0:T(8,128)(2,1)S(1)}, u32[]{:S(2)}, u32[]{:S(2)}) %collective-permute-start.8) | collective-permute-done | bytes 344096 | tf_op jit(solution)/shard_map/ppermute | solution.py:397
  58.2 0.0 collective-permute-start.13
  58.2 0.0 collective-permute-done.9.refs_11_.refs_5_
  58.2 0.5 collective-permute-start.15
  58.7 0.0 collective-permute-done.10.refs_12_.refs_6_
  58.7 0.0 collective-permute-done.12.refs_15_.refs_9_
  58.7 0.0 collective-permute-done.14.refs_19_.refs_13_
  58.7 1.1 %collective-permute-done.13.refs_16_.refs_10_ = bf16[112,1536]{1,0:T(8,128)(2,1)S(1)} collective-permute-done((bf16[112,1536]{1,0:T(8,128)(2,1)S(1)}, bf16[112,1536]{1,0:T(8,128)(2,1)S(1)}, u32[]{:S(2)}, u32[]{:S(2)}) %collective-permute-start.13) | collective-permute-done | bytes 344096 | tf_op jit(solution)/shard_map/ppermute | solution.py:397
  59.9 0.5 collective-permute-done.15.refs_20_.refs_14_
  60.4 3.7 %forward.1 = (bf16[40,1664]{1,0:T(8,128)(2,1)S(1)}, bf16[40,1664]{1,0:T(8,128)(2,1)S(1)}, bf16[40,1664]{1,0:T(8,128)(2,1)S(1)}, bf16[40,1664]{1,0:T(8,128)(2,1)S...) custom-call(f32[32]{0:T(128)S(1)} %copy-done.6, f32[5]{0:T(128)S(1)} %copy-done.5, ...), custom_call_target="tpu_custom_call" | custom-call | tf_op jit(solution)/shard_map/forward/pallas_call | solution.py:487
  64.1 0.2 collective-permute-start.16
  64.3 0.9 collective-permute-start.17
  65.2 0.9 collective-permute-start.18
  66.0 3.6 %backward.1 = bf16[256,1536]{1,0:T(8,128)(2,1)} custom-call(f32[256,1536]{1,0:T(8,128)S(1)} %get-tuple-element.64.normed_ref, f32[256,128]{1,0:T(8,128)S(1)} %get-tuple-element.65.inv_ref, bf16[256,160]{1,0:T(8,128)(2,1)S(1)} %get-tuple-element.66.dfc_ref, bf16[384,1536]{1,0:T(8,128)(2,1)S(1)} %copy-done, bf16[160,384]{1,0:T(8,128)(2,1)S(1)} %bitcast.8, ...), custom_call_target="tpu_custom_call" | custom-call | tf_op jit(solution)/shard_map/backward/pallas_call | solution.py:502
  69.7 0.0 collective-permute-done.16.b
  69.7 1.0 %collective-permute-done.17.c = bf16[40,1664]{1,0:T(8,128)(2,1)S(1)} collective-permute-done((bf16[40,1664]{1,0:T(8,128)(2,1)S(1)}, bf16[40,1664]{1,0:T(8,128)(2,1)S(1)}, u32[]{:S(2)}, u32[]{:S(2)}) %collective-permute-start.17) | collective-permute-done | bytes 133152 | tf_op jit(solution)/shard_map/ppermute | solution.py:397
  70.7 1.7 %collective-permute-done.18.d = bf16[40,1664]{1,0:T(8,128)(2,1)S(1)} collective-permute-done((bf16[40,1664]{1,0:T(8,128)(2,1)S(1)}, bf16[40,1664]{1,0:T(8,128)(2,1)S(1)}, u32[]{:S(2)}, u32[]{:S(2)}) %collective-permute-start.18) | collective-permute-done | bytes 133152 | tf_op jit(solution)/shard_map/ppermute | solution.py:397
  72.4 0.2 lat_sum.1
  72.6 1.2 %collective-permute-start.19 = (bf16[40,384]{1,0:T(8,128)(2,1)S(1)}, bf16[40,384]{1,0:T(8,128)(2,1)S(1)}, u32[]{:S(2)}, u32[]{:S(2)}) collective-permute-start(bf16[40,384]{1,0:T(8,128)(2,1)S(1)} %get-tuple-element.74), channel_id=1, source_target_pairs={{0,8},{8,0},{16,24},{24,16},{1,9},{9,1},{17,25},{25,17},{2,10},{10... | collective-permute-start | bytes 92168 | tf_op jit(solution)/shard_map/ppermute | solution.py:397
  73.8 3.1 %collective-permute-start.20 = (bf16[40,384]{1,0:T(8,128)(2,1)S(1)}, bf16[40,384]{1,0:T(8,128)(2,1)S(1)}, u32[]{:S(2)}, u32[]{:S(2)}) collective-permute-start(bf16[40,384]{1,0:T(8,128)(2,1)S(1)} %get-tuple-element.75), channel_id=1, source_target_pairs={{0,16},{8,24},{16,0},{24,8},{1,17},{9,25},{17,1},{25,9},{2,18},{10... | collective-permute-start | bytes 92168 | tf_op jit(solution)/shard_map/ppermute | solution.py:397
  76.8 0.2 collective-permute-start.21
  77.0 0.0 collective-permute-done.19.b
  77.0 2.1 %collective-permute-done.20.c = bf16[40,384]{1,0:T(8,128)(2,1)S(1)} collective-permute-done((bf16[40,384]{1,0:T(8,128)(2,1)S(1)}, bf16[40,384]{1,0:T(8,128)(2,1)S(1)}, u32[]{:S(2)}, u32[]{:S(2)}) %collective-permute-start.20) | collective-permute-done | bytes 30752 | tf_op jit(solution)/shard_map/ppermute | solution.py:397
  79.1 3.4 %collective-permute-done.21.d = bf16[40,384]{1,0:T(8,128)(2,1)S(1)} collective-permute-done((bf16[40,384]{1,0:T(8,128)(2,1)S(1)}, bf16[40,384]{1,0:T(8,128)(2,1)S(1)}, u32[]{:S(2)}, u32[]{:S(2)}) %collective-permute-start.21) | collective-permute-done | bytes 30752 | tf_op jit(solution)/shard_map/ppermute | solution.py:397
  82.6 0.1 collective-permute-start.28
  82.7 2.6 %collective-permute-start.27 = (bf16[48,384]{1,0:T(8,128)(2,1)S(1)}, bf16[48,384]{1,0:T(8,128)(2,1)S(1)}, u32[]{:S(2)}, u32[]{:S(2)}) collective-permute-start(bf16[48,384]{1,0:T(8,128)(2,1)S(1)} %dp_sum.1.refs_0_), channel_id=1, source_target_pairs={{0,6},{1,7},{2,4},{3,5},{4,2},{5,3},{6,0},{7,1},{8,14},{9,15},{10,... | collective-permute-start | bytes 110600 | tf_op jit(solution)/shard_map/ppermute | solution.py:538
  85.3 0.9 collective-permute-start.26
  86.2 1.1 %collective-permute-start.25 = (bf16[48,384]{1,0:T(8,128)(2,1)S(1)}, bf16[48,384]{1,0:T(8,128)(2,1)S(1)}, u32[]{:S(2)}, u32[]{:S(2)}) collective-permute-start(bf16[48,384]{1,0:T(8,128)(2,1)S(1)} %dp_sum.1.refs_0_), channel_id=1, source_target_pairs={{0,4},{1,5},{2,6},{3,7},{4,0},{5,1},{6,2},{7,3},{8,12},{9,13},{10,... | collective-permute-start | bytes 110600 | tf_op jit(solution)/shard_map/ppermute | solution.py:538
  87.3 0.0 collective-permute-start.24
  87.3 1.6 %collective-permute-start.23 = (bf16[48,384]{1,0:T(8,128)(2,1)S(1)}, bf16[48,384]{1,0:T(8,128)(2,1)S(1)}, u32[]{:S(2)}, u32[]{:S(2)}) collective-permute-start(bf16[48,384]{1,0:T(8,128)(2,1)S(1)} %dp_sum.1.refs_0_), channel_id=1, source_target_pairs={{0,2},{1,3},{2,0},{3,1},{4,6},{5,7},{6,4},{7,5},{8,10},{9,11},{10,... | collective-permute-start | bytes 110600 | tf_op jit(solution)/shard_map/ppermute | solution.py:538
  88.9 0.0 collective-permute-done.27.refs_6_
  88.9 0.5 collective-permute-start.22
  89.5 0.8 collective-permute-done.26.refs_5_
  90.3 0.3 collective-permute-done.25.refs_4_
  90.5 0.5 collective-permute-done.24.refs_3_
  91.1 0.0 collective-permute-done.23.refs_2_
  91.1 1.8 %collective-permute-done.22.refs_1_ = bf16[48,384]{1,0:T(8,128)(2,1)S(1)} collective-permute-done((bf16[48,384]{1,0:T(8,128)(2,1)S(1)}, bf16[48,384]{1,0:T(8,128)(2,1)S(1)}, u32[]{:S(2)}, u32[]{:S(2)}) %collective-permute-start.22) | collective-permute-done | bytes 36896 | tf_op jit(solution)/shard_map/ppermute | solution.py:538
  92.9 0.7 join.1
  (16 shorter events, 0.1 us)
Async XLA Ops:
  3.1 13.6 %collective-permute-start.1 = (bf16[112,1536]{1,0:T(8,128)(2,1)}, bf16[112,1536]{1,0:T(8,128)(2,1)S(1)}, u32[]{:S(2)}, u32[]{:S(2)}) collective-permute-start(bf16[112,1536]{1,0:T(8,128)(2,1)} %payload.1), channel_id=1, source_target_pairs={{0,8},{8,16},{16,24},{24,0},{1,9},{9,17},{17,25},{25,1},{2,10},{10... | collective-permute-start | bytes 1032200 | tf_op jit(solution)/shard_map/ppermute | solution.py:28
  11.2 5.5 %collective-permute-start.2 = (bf16[32,4864]{1,0:T(8,128)(2,1)}, bf16[32,4864]{1,0:T(8,128)(2,1)S(1)}, u32[]{:S(2)}, u32[]{:S(2)}) collective-permute-start(bf16[32,4864]{1,0:T(8,128)(2,1)} %get-tuple-element.43), channel_id=1, source_target_pairs={{0,6},{2,0},{4,2},{6,4},{1,7},{3,1},{5,3},{7,5},{8,14},{10,8},{12,... | collective-permute-start | bytes 933896 | tf_op jit(solution)/shard_map/ppermute | solution.py:28
  16.7 10.9 %collective-permute-start.6 = (bf16[112,1536]{1,0:T(8,128)(2,1)S(1)}, bf16[112,1536]{1,0:T(8,128)(2,1)S(1)}, u32[]{:S(2)}, u32[]{:S(2)}) collective-permute-start(bf16[112,1536]{1,0:T(8,128)(2,1)S(1)} %collective-permute-done.1.refs_9_.refs_3_), channel_id=1, source_target_pairs={{0,4},{2,6},{4,0},{6,2},{1,5},{3,7},{5,1},{7,3},{8,12},{10,14},{12... | collective-permute-start | bytes 1032200 | tf_op jit(solution)/shard_map/ppermute | solution.py:397
  18.0 12.4 %collective-permute-start.5 = (bf16[112,1536]{1,0:T(8,128)(2,1)S(1)}, bf16[112,1536]{1,0:T(8,128)(2,1)S(1)}, u32[]{:S(2)}, u32[]{:S(2)}) collective-permute-start(bf16[112,1536]{1,0:T(8,128)(2,1)S(1)} %collective-permute-done.1.refs_9_.refs_3_), channel_id=1, source_target_pairs={{0,8},{8,16},{16,24},{24,0},{1,9},{9,17},{17,25},{25,1},{2,10},{10... | collective-permute-start | bytes 1032200 | tf_op jit(solution)/shard_map/ppermute | solution.py:28
  19.1 23.7 %collective-permute-start = (bf16[64,4864]{1,0:T(8,128)(2,1)}, bf16[64,4864]{1,0:T(8,128)(2,1)S(1)}, u32[]{:S(2)}, u32[]{:S(2)}) collective-permute-start(bf16[64,4864]{1,0:T(8,128)(2,1)} %get-tuple-element.42), channel_id=1, source_target_pairs={{0,1},{1,0},{2,3},{3,2},{4,5},{5,4},{6,7},{7,6},{8,9},{9,8},{10,11... | collective-permute-start | bytes 1867784 | tf_op jit(solution)/shard_map/ppermute | solution.py:28
  20.6 28.6 %collective-permute-start.4 = (bf16[64,4864]{1,0:T(8,128)(2,1)}, bf16[64,4864]{1,0:T(8,128)(2,1)S(1)}, u32[]{:S(2)}, u32[]{:S(2)}) collective-permute-start(bf16[64,4864]{1,0:T(8,128)(2,1)} %get-tuple-element.46), channel_id=1, source_target_pairs={{0,7},{1,6},{2,1},{3,0},{4,3},{5,2},{6,5},{7,4},{8,15},{9,14},{10,... | collective-permute-start | bytes 1867784 | tf_op jit(solution)/shard_map/ppermute | solution.py:456
  30.4 11.6 %collective-permute-start.7 = (bf16[112,1536]{1,0:T(8,128)(2,1)S(1)}, bf16[112,1536]{1,0:T(8,128)(2,1)S(1)}, u32[]{:S(2)}, u32[]{:S(2)}) collective-permute-start(bf16[112,1536]{1,0:T(8,128)(2,1)S(1)} %collective-permute-done.5.refs_13_.refs_7_), channel_id=1, source_target_pairs={{0,8},{8,16},{16,24},{24,0},{1,9},{9,17},{17,25},{25,1},{2,10},{10... | collective-permute-start | bytes 1032200 | tf_op jit(solution)/shard_map/ppermute | solution.py:28
  30.4 12.5 %collective-permute-start.3 = (bf16[32,4864]{1,0:T(8,128)(2,1)}, bf16[32,4864]{1,0:T(8,128)(2,1)S(1)}, u32[]{:S(2)}, u32[]{:S(2)}) collective-permute-start(bf16[32,4864]{1,0:T(8,128)(2,1)} %get-tuple-element.45), channel_id=1, source_target_pairs={{0,6},{2,0},{4,2},{6,4},{1,7},{3,1},{5,3},{7,5},{8,14},{10,8},{12,... | collective-permute-start | bytes 933896 | tf_op jit(solution)/shard_map/ppermute | solution.py:28
  30.7 23.6 %collective-permute-start.11 = (bf16[112,1536]{1,0:T(8,128)(2,1)S(1)}, bf16[112,1536]{1,0:T(8,128)(2,1)S(1)}, u32[]{:S(2)}, u32[]{:S(2)}) collective-permute-start(bf16[112,1536]{1,0:T(8,128)(2,1)S(1)} %collective-permute-done.5.refs_13_.refs_7_), channel_id=1, source_target_pairs={{0,4},{2,6},{4,0},{6,2},{1,5},{3,7},{5,1},{7,3},{8,12},{10,14},{12... | collective-permute-start | bytes 1032200 | tf_op jit(solution)/shard_map/ppermute | solution.py:397
  41.9 16.3 %collective-permute-start.8 = (bf16[112,1536]{1,0:T(8,128)(2,1)S(1)}, bf16[112,1536]{1,0:T(8,128)(2,1)S(1)}, u32[]{:S(2)}, u32[]{:S(2)}) collective-permute-start(bf16[112,1536]{1,0:T(8,128)(2,1)S(1)} %collective-permute-done.7.refs_17_.refs_11_), channel_id=1, source_target_pairs={{0,4},{2,6},{4,0},{6,2},{1,5},{3,7},{5,1},{7,3},{8,12},{10,14},{12... | collective-permute-start | bytes 1032200 | tf_op jit(solution)/shard_map/ppermute | solution.py:397
  49.2 11.1 %copy-start.4 = (bf16[384]{0:T(512)(128)(2,1)S(1)}, bf16[384]{0:T(512)(128)(2,1)}, u32[]{:S(2)}) copy-start(bf16[384]{0:T(512)(128)(2,1)} %refs_2_.1) | copy-start | bytes 2308
  49.2 11.1 %copy-start.5 = (f32[5]{0:T(128)S(1)}, f32[5]{0:T(128)}, u32[]{:S(2)}) copy-start(f32[5]{0:T(128)} %var_ref.1) | copy-start | bytes 64
  49.2 11.2 %copy-start = (bf16[384,1536]{1,0:T(8,128)(2,1)S(1)}, bf16[384,1536]{1,0:T(8,128)(2,1)}, u32[]{:S(2)}) copy-start(bf16[384,1536]{1,0:T(8,128)(2,1)} %refs_0_.1) | copy-start | bytes 3538948
  49.2 9.0 %collective-permute-start.9 = (bf16[112,1536]{1,0:T(8,128)(2,1)S(1)}, bf16[112,1536]{1,0:T(8,128)(2,1)S(1)}, u32[]{:S(2)}, u32[]{:S(2)}) collective-permute-start(bf16[112,1536]{1,0:T(8,128)(2,1)S(1)} %collective-permute-done.1.refs_9_.refs_3_), channel_id=1, source_target_pairs={{0,2},{2,0},{4,6},{6,4},{1,3},{3,1},{5,7},{7,5},{8,10},{10,8},{12,... | collective-permute-start | bytes 1032200 | tf_op jit(solution)/shard_map/ppermute | solution.py:397
  49.6 9.1 %collective-permute-start.10 = (bf16[112,1536]{1,0:T(8,128)(2,1)S(1)}, bf16[112,1536]{1,0:T(8,128)(2,1)S(1)}, u32[]{:S(2)}, u32[]{:S(2)}) collective-permute-start(bf16[112,1536]{1,0:T(8,128)(2,1)S(1)} %collective-permute-done.6.refs_10_.refs_4_), channel_id=1, source_target_pairs={{0,2},{2,0},{4,6},{6,4},{1,3},{3,1},{5,7},{7,5},{8,10},{10,8},{12,... | collective-permute-start | bytes 1032200 | tf_op jit(solution)/shard_map/ppermute | solution.py:397
  49.7 9.0 %collective-permute-start.12 = (bf16[112,1536]{1,0:T(8,128)(2,1)S(1)}, bf16[112,1536]{1,0:T(8,128)(2,1)S(1)}, u32[]{:S(2)}, u32[]{:S(2)}) collective-permute-start(bf16[112,1536]{1,0:T(8,128)(2,1)S(1)} %collective-permute-done.5.refs_13_.refs_7_), channel_id=1, source_target_pairs={{0,2},{2,0},{4,6},{6,4},{1,3},{3,1},{5,7},{7,5},{8,10},{10,8},{12,... | collective-permute-start | bytes 1032200 | tf_op jit(solution)/shard_map/ppermute | solution.py:397
  50.1 1.1 %copy-start.1 = (bf16[64,4864]{1,0:T(8,128)(2,1)S(1)}, bf16[64,4864]{1,0:T(8,128)(2,1)}, u32[]{:S(2)}) copy-start(bf16[64,4864]{1,0:T(8,128)(2,1)} %get-tuple-element.49.own_ref.refs_1_) | copy-start | bytes 1867780
  51.2 9.2 %copy-start.2 = (bf16[64,4864]{1,0:T(8,128)(2,1)S(1)}, bf16[64,4864]{1,0:T(8,128)(2,1)}, u32[]{:S(2)}) copy-start(bf16[64,4864]{1,0:T(8,128)(2,1)} %get-tuple-element.49.own_ref.refs_1_) | copy-start | bytes 1867780
  51.2 9.2 %copy-start.3 = (bf16[384,160]{0,1:T(8,128)(2,1)S(1)}, bf16[384,160]{0,1:T(8,128)(2,1)}, u32[]{:S(2)}) copy-start(bf16[384,160]{0,1:T(8,128)(2,1)} %param.12) | copy-start | bytes 368644
  51.2 9.2 %copy-start.6 = (f32[32]{0:T(128)S(1)}, f32[32]{0:T(128)}, u32[]{:S(2)}) copy-start(f32[32]{0:T(128)} %constant.2.clone.lat_ref) | copy-start | bytes 388
  54.3 4.5 %collective-permute-start.14 = (bf16[112,1536]{1,0:T(8,128)(2,1)S(1)}, bf16[112,1536]{1,0:T(8,128)(2,1)S(1)}, u32[]{:S(2)}, u32[]{:S(2)}) collective-permute-start(bf16[112,1536]{1,0:T(8,128)(2,1)S(1)} %collective-permute-done.7.refs_17_.refs_11_), channel_id=1, source_target_pairs={{0,2},{2,0},{4,6},{6,4},{1,3},{3,1},{5,7},{7,5},{8,10},{10,8},{12,... | collective-permute-start | bytes 1032200 | tf_op jit(solution)/shard_map/ppermute | solution.py:397
  58.2 1.7 %collective-permute-start.13 = (bf16[112,1536]{1,0:T(8,128)(2,1)S(1)}, bf16[112,1536]{1,0:T(8,128)(2,1)S(1)}, u32[]{:S(2)}, u32[]{:S(2)}) collective-permute-start(bf16[112,1536]{1,0:T(8,128)(2,1)S(1)} %collective-permute-done.11.refs_14_.refs_8_), channel_id=1, source_target_pairs={{0,2},{2,0},{4,6},{6,4},{1,3},{3,1},{5,7},{7,5},{8,10},{10,8},{12,... | collective-permute-start | bytes 1032200 | tf_op jit(solution)/shard_map/ppermute | solution.py:397
  58.2 2.1 %collective-permute-start.15 = (bf16[112,1536]{1,0:T(8,128)(2,1)S(1)}, bf16[112,1536]{1,0:T(8,128)(2,1)S(1)}, u32[]{:S(2)}, u32[]{:S(2)}) collective-permute-start(bf16[112,1536]{1,0:T(8,128)(2,1)S(1)} %collective-permute-done.8.refs_18_.refs_12_), channel_id=1, source_target_pairs={{0,2},{2,0},{4,6},{6,4},{1,3},{3,1},{5,7},{7,5},{8,10},{10,8},{12,... | collective-permute-start | bytes 1032200 | tf_op jit(solution)/shard_map/ppermute | solution.py:397
  64.1 5.6 %collective-permute-start.16 = (bf16[40,1664]{1,0:T(8,128)(2,1)S(1)}, bf16[40,1664]{1,0:T(8,128)(2,1)S(1)}, u32[]{:S(2)}, u32[]{:S(2)}) collective-permute-start(bf16[40,1664]{1,0:T(8,128)(2,1)S(1)} %get-tuple-element.61), channel_id=1, source_target_pairs={{0,2},{2,0},{4,6},{6,4},{1,3},{3,1},{5,7},{7,5},{8,10},{10,8},{12,... | collective-permute-start | bytes 399368 | tf_op jit(solution)/shard_map/ppermute | solution.py:397
  64.3 6.4 %collective-permute-start.17 = (bf16[40,1664]{1,0:T(8,128)(2,1)S(1)}, bf16[40,1664]{1,0:T(8,128)(2,1)S(1)}, u32[]{:S(2)}, u32[]{:S(2)}) collective-permute-start(bf16[40,1664]{1,0:T(8,128)(2,1)S(1)} %get-tuple-element.62), channel_id=1, source_target_pairs={{0,4},{2,6},{4,0},{6,2},{1,5},{3,7},{5,1},{7,3},{8,12},{10,14},{12... | collective-permute-start | bytes 399368 | tf_op jit(solution)/shard_map/ppermute | solution.py:397
  65.2 7.3 %collective-permute-start.18 = (bf16[40,1664]{1,0:T(8,128)(2,1)S(1)}, bf16[40,1664]{1,0:T(8,128)(2,1)S(1)}, u32[]{:S(2)}, u32[]{:S(2)}) collective-permute-start(bf16[40,1664]{1,0:T(8,128)(2,1)S(1)} %get-tuple-element.63), channel_id=1, source_target_pairs={{0,6},{2,4},{4,2},{6,0},{1,7},{3,5},{5,3},{7,1},{8,14},{10,12},{12... | collective-permute-start | bytes 399368 | tf_op jit(solution)/shard_map/ppermute | solution.py:397
  72.6 4.4 %collective-permute-start.19 = (bf16[40,384]{1,0:T(8,128)(2,1)S(1)}, bf16[40,384]{1,0:T(8,128)(2,1)S(1)}, u32[]{:S(2)}, u32[]{:S(2)}) collective-permute-start(bf16[40,384]{1,0:T(8,128)(2,1)S(1)} %get-tuple-element.74), channel_id=1, source_target_pairs={{0,8},{8,0},{16,24},{24,16},{1,9},{9,1},{17,25},{25,17},{2,10},{10... | collective-permute-start | bytes 92168 | tf_op jit(solution)/shard_map/ppermute | solution.py:397
  73.8 5.4 %collective-permute-start.20 = (bf16[40,384]{1,0:T(8,128)(2,1)S(1)}, bf16[40,384]{1,0:T(8,128)(2,1)S(1)}, u32[]{:S(2)}, u32[]{:S(2)}) collective-permute-start(bf16[40,384]{1,0:T(8,128)(2,1)S(1)} %get-tuple-element.75), channel_id=1, source_target_pairs={{0,16},{8,24},{16,0},{24,8},{1,17},{9,25},{17,1},{25,9},{2,18},{10... | collective-permute-start | bytes 92168 | tf_op jit(solution)/shard_map/ppermute | solution.py:397
  76.8 5.7 %collective-permute-start.21 = (bf16[40,384]{1,0:T(8,128)(2,1)S(1)}, bf16[40,384]{1,0:T(8,128)(2,1)S(1)}, u32[]{:S(2)}, u32[]{:S(2)}) collective-permute-start(bf16[40,384]{1,0:T(8,128)(2,1)S(1)} %get-tuple-element.76), channel_id=1, source_target_pairs={{0,24},{8,16},{16,8},{24,0},{1,25},{9,17},{17,9},{25,1},{2,26},{10... | collective-permute-start | bytes 92168 | tf_op jit(solution)/shard_map/ppermute | solution.py:397
  82.6 4.7 %collective-permute-start.28 = (bf16[48,384]{1,0:T(8,128)(2,1)S(1)}, bf16[48,384]{1,0:T(8,128)(2,1)S(1)}, u32[]{:S(2)}, u32[]{:S(2)}) collective-permute-start(bf16[48,384]{1,0:T(8,128)(2,1)S(1)} %dp_sum.1.refs_0_), channel_id=1, source_target_pairs={{0,7},{1,6},{2,5},{3,4},{4,3},{5,2},{6,1},{7,0},{8,15},{9,14},{10,... | collective-permute-start | bytes 110600 | tf_op jit(solution)/shard_map/ppermute | solution.py:538
  82.7 6.2 %collective-permute-start.27 = (bf16[48,384]{1,0:T(8,128)(2,1)S(1)}, bf16[48,384]{1,0:T(8,128)(2,1)S(1)}, u32[]{:S(2)}, u32[]{:S(2)}) collective-permute-start(bf16[48,384]{1,0:T(8,128)(2,1)S(1)} %dp_sum.1.refs_0_), channel_id=1, source_target_pairs={{0,6},{1,7},{2,4},{3,5},{4,2},{5,3},{6,0},{7,1},{8,14},{9,15},{10,... | collective-permute-start | bytes 110600 | tf_op jit(solution)/shard_map/ppermute | solution.py:538
  85.3 5.0 %collective-permute-start.26 = (bf16[48,384]{1,0:T(8,128)(2,1)S(1)}, bf16[48,384]{1,0:T(8,128)(2,1)S(1)}, u32[]{:S(2)}, u32[]{:S(2)}) collective-permute-start(bf16[48,384]{1,0:T(8,128)(2,1)S(1)} %dp_sum.1.refs_0_), channel_id=1, source_target_pairs={{0,5},{1,4},{2,7},{3,6},{4,1},{5,0},{6,3},{7,2},{8,13},{9,12},{10,... | collective-permute-start | bytes 110600 | tf_op jit(solution)/shard_map/ppermute | solution.py:538
  86.2 4.4 %collective-permute-start.25 = (bf16[48,384]{1,0:T(8,128)(2,1)S(1)}, bf16[48,384]{1,0:T(8,128)(2,1)S(1)}, u32[]{:S(2)}, u32[]{:S(2)}) collective-permute-start(bf16[48,384]{1,0:T(8,128)(2,1)S(1)} %dp_sum.1.refs_0_), channel_id=1, source_target_pairs={{0,4},{1,5},{2,6},{3,7},{4,0},{5,1},{6,2},{7,3},{8,12},{9,13},{10,... | collective-permute-start | bytes 110600 | tf_op jit(solution)/shard_map/ppermute | solution.py:538
  87.3 3.7 %collective-permute-start.24 = (bf16[48,384]{1,0:T(8,128)(2,1)S(1)}, bf16[48,384]{1,0:T(8,128)(2,1)S(1)}, u32[]{:S(2)}, u32[]{:S(2)}) collective-permute-start(bf16[48,384]{1,0:T(8,128)(2,1)S(1)} %dp_sum.1.refs_0_), channel_id=1, source_target_pairs={{0,3},{1,2},{2,1},{3,0},{4,7},{5,6},{6,5},{7,4},{8,11},{9,10},{10,... | collective-permute-start | bytes 110600 | tf_op jit(solution)/shard_map/ppermute | solution.py:538
  87.3 3.7 %collective-permute-start.23 = (bf16[48,384]{1,0:T(8,128)(2,1)S(1)}, bf16[48,384]{1,0:T(8,128)(2,1)S(1)}, u32[]{:S(2)}, u32[]{:S(2)}) collective-permute-start(bf16[48,384]{1,0:T(8,128)(2,1)S(1)} %dp_sum.1.refs_0_), channel_id=1, source_target_pairs={{0,2},{1,3},{2,0},{3,1},{4,6},{5,7},{6,4},{7,5},{8,10},{9,11},{10,... | collective-permute-start | bytes 110600 | tf_op jit(solution)/shard_map/ppermute | solution.py:538
  88.9 4.0 %collective-permute-start.22 = (bf16[48,384]{1,0:T(8,128)(2,1)S(1)}, bf16[48,384]{1,0:T(8,128)(2,1)S(1)}, u32[]{:S(2)}, u32[]{:S(2)}) collective-permute-start(bf16[48,384]{1,0:T(8,128)(2,1)S(1)} %dp_sum.1.refs_0_), channel_id=1, source_target_pairs={{0,1},{1,0},{2,3},{3,2},{4,5},{5,4},{6,7},{7,6},{8,9},{9,8},{10,11... | collective-permute-start | bytes 110600 | tf_op jit(solution)/shard_map/ppermute | solution.py:538

commit v9 on v8

--- a/solution.py
+++ b/solution.py
@@ -458,7 +458,7 @@
     ring1_after, tiles[2] = barrier((ring1, tiles[2]))
     ring2 = from_behind(ring1_after, "dp", 1)
     across1 = swap(ring1, "lat", 2)
-    ring2_after, across1 = barrier((ring2, across1))
+    ring2_after, across1, tiles[3] = barrier((ring2, across1, tiles[3]))
     ring3 = from_behind(ring2_after, "dp", 1)
     across2 = swap(ring2, "lat", 2)
     across3 = swap(ring3, "lat", 2)

time: 93.8 us -> 90.6 us (0.966)
  waiting for transfers between devices: 47.6 us -> 42.7 us
  starting transfers between devices: 25.6 us -> 27.3 us
    ppermute x15, waiting for transfers between devices: 20.1 us -> 10.7 us  [swap(): lax.ppermute(array, axis, [(i, i ^ bit) for i in range(lax.axis_size(axis...]
    ppermute x6, waiting for transfers between devices: 17.7 us -> 23.9 us  [from_behind(): lax.ppermute(array, axis, [(i, (i + by) % length) for i in range(length)])]
    ppermute x1, waiting for transfers between devices: 6.37 us -> 4.73 us  [shards(): lax.ppermute(send[3], ('lat', 'lon'), corner)]
    ppermute x6, starting transfers between devices: 6.73 us -> 8.29 us  [from_behind(): lax.ppermute(array, axis, [(i, (i + by) % length) for i in range(length)])]
    ppermute x15, starting transfers between devices: 11.1 us -> 12.1 us  [swap(): lax.ppermute(array, axis, [(i, i ^ bit) for i in range(lax.axis_size(axis...]
  transfers between devices with their start and end apart: 29 -> 29, of which waited for: 17 -> 16; matrix products, arithmetic and copies ran while one was open for 0% -> 0% of each run, Pallas kernels for 12% -> 13%
where the time goes in v9:
time: 90.6 us; the launch traced here: 90.4 us
  waiting for transfers between devices  42.7 us (47%)
  starting transfers between devices  27.3 us (30%)
  Pallas kernels  18.6 us (21%)
  local copies, waits for them, and re-layouts  1.1 us (1%)
    ppermute x6, waiting for transfers between devices, from_behind(): lax.ppermute(array, axis, [(i, (i + by) % length) for i in range(length)])  23.9 us
    ppermute x15, starting transfers between devices, swap(): lax.ppermute(array, axis, [(i, i ^ bit) for i in range(lax.axis_size(axis...  12.1 us
    ppermute x15, waiting for transfers between devices, swap(): lax.ppermute(array, axis, [(i, i ^ bit) for i in range(lax.axis_size(axis...  10.7 us
    ppermute x6, starting transfers between devices, from_behind(): lax.ppermute(array, axis, [(i, (i + by) % length) for i in range(length)])  8.29 us
    ppermute x7, starting transfers between devices, shards(): plane.append(lax.ppermute(mine, ('lat', 'lon'), pairs))  6.88 us
    pallas_call x1, Pallas kernels, shards(): pl.pallas_call(pack_kernel, out_shape=[shape((quarter, 3 * width + EXTRA)...  5.01 us
    ppermute x1, waiting for transfers between devices, shards(): lax.ppermute(send[3], ('lat', 'lon'), corner)  4.73 us
    pallas_call x1, Pallas kernels, shards(): pl.pallas_call(forward_kernel, grid=(1,), out_shape=[shape((piece, width...  3.71 us
  transfers between devices with their start and end apart: 29, of which 16 were waited for; matrix products, arithmetic and copies ran while one was open for 0% of the time, Pallas kernels for 13%

profile of v9, /device:TPU:0, one launch (start us, length us, event | category | flops | bytes accessed | tf_op | source)
XLA Modules:
  0.0 90.4 jit_solution(5398105396971819642)
XLA Ops:
  0.6 2.5 %payload.1 = bf16[112,1536]{1,0:T(8,128)(2,1)} custom-call(bf16[384,1536]{1,0:T(8,128)(2,1)} %refs_0_.1, bf16[160,384]{1,0:T(8,128)(2,1)} %bitcast.6, bf16[384]{0:T(512)(128)(2,1)} %refs_2_.1), custom_call_target="tpu_custom_call" | custom-call | tf_op jit(solution)/shard_map/payload/pallas_call | solution.py:418
  3.1 3.1 %collective-permute-start.1 = (bf16[112,1536]{1,0:T(8,128)(2,1)}, bf16[112,1536]{1,0:T(8,128)(2,1)S(1)}, u32[]{:S(2)}, u32[]{:S(2)}) collective-permute-start(bf16[112,1536]{1,0:T(8,128)(2,1)} %payload.1), channel_id=1, source_target_pairs={{0,8},{8,16},{16,24},{24,0},{1,9},{9,17},{17,25},{25,1},{2,10},{10... | collective-permute-start | bytes 1032200 | tf_op jit(solution)/shard_map/ppermute | solution.py:28
  6.2 5.0 %pack.1 = (bf16[64,4864]{1,0:T(8,128)(2,1)}, bf16[64,4864]{1,0:T(8,128)(2,1)}, bf16[32,4864]{1,0:T(8,128)(2,1)}, bf16[32,4864]{1,0:T(8,128)(2,1)}, bf16[64,4864]{1,0:T(8,128)(2,1)}) custom-call(bf16[4,8,8,4608]{3,2,1,0:T(8,128)(2,1)} %bitcast.9, bf16[4,8,8,160]{3,2,1,0:T(8,128)(2,1)} %bitcast.11, s32[8,8]{1,0:T(8,128)} %valid_ref.1), custom_call_target="tpu_custom_call" | custom-call | tf_op jit(solution)/shard_map/pack/pallas_call | solution.py:428
  11.2 0.7 collective-permute-start.2
  11.9 4.7 %collective-permute-done.2.south0_ref.refs_3_ = bf16[32,4864]{1,0:T(8,128)(2,1)S(1)} collective-permute-done((bf16[32,4864]{1,0:T(8,128)(2,1)}, bf16[32,4864]{1,0:T(8,128)(2,1)S(1)}, u32[]{:S(2)}, u32[]{:S(2)}) %collective-permute-start.2) | collective-permute-done | bytes 311328 | tf_op jit(solution)/shard_map/ppermute | solution.py:28
  16.7 0.0 collective-permute-done.1.refs_9_.refs_3_
  16.7 1.3 %collective-permute-start.4 = (bf16[112,1536]{1,0:T(8,128)(2,1)S(1)}, bf16[112,1536]{1,0:T(8,128)(2,1)S(1)}, u32[]{:S(2)}, u32[]{:S(2)}) collective-permute-start(bf16[112,1536]{1,0:T(8,128)(2,1)S(1)} %collective-permute-done.1.refs_9_.refs_3_), channel_id=1, source_target_pairs={{0,4},{2,6},{4,0},{6,2},{1,5},{3,7},{5,1},{7,3},{8,12},{10,14},{12... | collective-permute-start | bytes 1032200 | tf_op jit(solution)/shard_map/ppermute | solution.py:397
  18.0 1.1 %collective-permute-start.3 = (bf16[112,1536]{1,0:T(8,128)(2,1)S(1)}, bf16[112,1536]{1,0:T(8,128)(2,1)S(1)}, u32[]{:S(2)}, u32[]{:S(2)}) collective-permute-start(bf16[112,1536]{1,0:T(8,128)(2,1)S(1)} %collective-permute-done.1.refs_9_.refs_3_), channel_id=1, source_target_pairs={{0,8},{8,16},{16,24},{24,0},{1,9},{9,17},{17,25},{25,1},{2,10},{10... | collective-permute-start | bytes 1032200 | tf_op jit(solution)/shard_map/ppermute | solution.py:28
  19.1 1.2 %collective-permute-start.5 = (bf16[32,4864]{1,0:T(8,128)(2,1)}, bf16[32,4864]{1,0:T(8,128)(2,1)S(1)}, u32[]{:S(2)}, u32[]{:S(2)}) collective-permute-start(bf16[32,4864]{1,0:T(8,128)(2,1)} %get-tuple-element.47), channel_id=1, source_target_pairs={{0,6},{2,0},{4,2},{6,4},{1,7},{3,1},{5,3},{7,5},{8,14},{10,8},{12,... | collective-permute-start | bytes 933896 | tf_op jit(solution)/shard_map/ppermute | solution.py:28
  20.3 1.5 %collective-permute-start = (bf16[64,4864]{1,0:T(8,128)(2,1)}, bf16[64,4864]{1,0:T(8,128)(2,1)S(1)}, u32[]{:S(2)}, u32[]{:S(2)}) collective-permute-start(bf16[64,4864]{1,0:T(8,128)(2,1)} %get-tuple-element.43), channel_id=1, source_target_pairs={{0,1},{1,0},{2,3},{3,2},{4,5},{5,4},{6,7},{7,6},{8,9},{9,8},{10,11... | collective-permute-start | bytes 1867784 | tf_op jit(solution)/shard_map/ppermute | solution.py:28
  21.8 0.0 collective-permute-start.6
  21.8 8.0 %collective-permute-done.5.south1_ref.refs_4_ = bf16[32,4864]{1,0:T(8,128)(2,1)S(1)} collective-permute-done((bf16[32,4864]{1,0:T(8,128)(2,1)}, bf16[32,4864]{1,0:T(8,128)(2,1)S(1)}, u32[]{:S(2)}, u32[]{:S(2)}) %collective-permute-start.5) | collective-permute-done | bytes 311328 | tf_op jit(solution)/shard_map/ppermute | solution.py:28
  29.8 0.0 collective-permute-done.4.refs_10_.refs_4_
  29.8 0.6 collective-permute-done.3.refs_13_.refs_7_
  30.4 0.6 collective-permute-start.7
  31.0 1.2 %collective-permute-start.11 = (bf16[112,1536]{1,0:T(8,128)(2,1)S(1)}, bf16[112,1536]{1,0:T(8,128)(2,1)S(1)}, u32[]{:S(2)}, u32[]{:S(2)}) collective-permute-start(bf16[112,1536]{1,0:T(8,128)(2,1)S(1)} %collective-permute-done.3.refs_13_.refs_7_), channel_id=1, source_target_pairs={{0,4},{2,6},{4,0},{6,2},{1,5},{3,7},{5,1},{7,3},{8,12},{10,14},{12... | collective-permute-start | bytes 1032200 | tf_op jit(solution)/shard_map/ppermute | solution.py:397
  32.2 10.6 %collective-permute-done.7.refs_17_.refs_11_ = bf16[112,1536]{1,0:T(8,128)(2,1)S(1)} collective-permute-done((bf16[112,1536]{1,0:T(8,128)(2,1)S(1)}, bf16[112,1536]{1,0:T(8,128)(2,1)S(1)}, u32[]{:S(2)}, u32[]{:S(2)}) %collective-permute-start.7) | collective-permute-done | bytes 344096 | tf_op jit(solution)/shard_map/ppermute | solution.py:28
  42.8 1.0 %collective-permute-start.8 = (bf16[112,1536]{1,0:T(8,128)(2,1)S(1)}, bf16[112,1536]{1,0:T(8,128)(2,1)S(1)}, u32[]{:S(2)}, u32[]{:S(2)}) collective-permute-start(bf16[112,1536]{1,0:T(8,128)(2,1)S(1)} %collective-permute-done.7.refs_17_.refs_11_), channel_id=1, source_target_pairs={{0,4},{2,6},{4,0},{6,2},{1,5},{3,7},{5,1},{7,3},{8,12},{10,14},{12... | collective-permute-start | bytes 1032200 | tf_op jit(solution)/shard_map/ppermute | solution.py:397
  43.8 4.7 %collective-permute-done.6.diag_ref.refs_5_ = bf16[64,4864]{1,0:T(8,128)(2,1)S(1)} collective-permute-done((bf16[64,4864]{1,0:T(8,128)(2,1)}, bf16[64,4864]{1,0:T(8,128)(2,1)S(1)}, u32[]{:S(2)}, u32[]{:S(2)}) %collective-permute-start.6) | collective-permute-done | bytes 622624 | tf_op jit(solution)/shard_map/ppermute | solution.py:456
  48.5 1.1 %collective-permute-start.9 = (bf16[112,1536]{1,0:T(8,128)(2,1)S(1)}, bf16[112,1536]{1,0:T(8,128)(2,1)S(1)}, u32[]{:S(2)}, u32[]{:S(2)}) collective-permute-start(bf16[112,1536]{1,0:T(8,128)(2,1)S(1)} %collective-permute-done.1.refs_9_.refs_3_), channel_id=1, source_target_pairs={{0,2},{2,0},{4,6},{6,4},{1,3},{3,1},{5,7},{7,5},{8,10},{10,8},{12,... | collective-permute-start | bytes 1032200 | tf_op jit(solution)/shard_map/ppermute | solution.py:397
  49.7 0.1 collective-permute-start.10
  49.7 0.4 collective-permute-start.12
  50.2 1.1 %copy-done.1 = bf16[64,4864]{1,0:T(8,128)(2,1)S(1)} copy-done((bf16[64,4864]{1,0:T(8,128)(2,1)S(1)}, bf16[64,4864]{1,0:T(8,128)(2,1)}, u32[]{:S(2)}) %copy-start.1) | copy-done | bytes 622616
  51.2 2.8 %attention.1.refs_0_ = bf16[256,1536]{1,0:T(8,128)(2,1)S(1)} custom-call(bf16[64,4864]{1,0:T(8,128)(2,1)S(1)} %copy-done.1, bf16[64,4864]{1,0:T(8,128)(2,1)S(1)} %collective-permute-done.east_ref.refs_2_, bf16[32,4864]{1,0:T(8,128)(2,1)S(1)} %collective-permute-done.2.south0_ref.refs_3_, bf16[32,4864]{1,0:T(8,128)(2,1)S(1)} %collective-permute-done.5.south1_ref.refs_4_, ...), custom_call_target="tpu_custom_call" | custom-call | tf_op jit(solution)/shard_map/attention/pallas_call | solution.py:466
  54.1 0.0 collective-permute-done.11.refs_14_.refs_8_
  54.1 0.1 collective-permute-start.14
  54.2 1.7 %collective-permute-done.8.refs_18_.refs_12_ = bf16[112,1536]{1,0:T(8,128)(2,1)S(1)} collective-permute-done((bf16[112,1536]{1,0:T(8,128)(2,1)S(1)}, bf16[112,1536]{1,0:T(8,128)(2,1)S(1)}, u32[]{:S(2)}, u32[]{:S(2)}) %collective-permute-start.8) | collective-permute-done | bytes 344096 | tf_op jit(solution)/shard_map/ppermute | solution.py:397
  56.0 0.0 collective-permute-start.13
  56.0 0.0 collective-permute-done.9.refs_11_.refs_5_
  56.0 0.5 collective-permute-start.15
  56.5 0.0 collective-permute-done.10.refs_12_.refs_6_
  56.5 0.0 collective-permute-done.12.refs_15_.refs_9_
  56.5 0.0 collective-permute-done.14.refs_19_.refs_13_
  56.5 1.1 %collective-permute-done.13.refs_16_.refs_10_ = bf16[112,1536]{1,0:T(8,128)(2,1)S(1)} collective-permute-done((bf16[112,1536]{1,0:T(8,128)(2,1)S(1)}, bf16[112,1536]{1,0:T(8,128)(2,1)S(1)}, u32[]{:S(2)}, u32[]{:S(2)}) %collective-permute-start.13) | collective-permute-done | bytes 344096 | tf_op jit(solution)/shard_map/ppermute | solution.py:397
  57.6 0.5 collective-permute-done.15.refs_20_.refs_14_
  58.2 3.7 %forward.1 = (bf16[40,1664]{1,0:T(8,128)(2,1)S(1)}, bf16[40,1664]{1,0:T(8,128)(2,1)S(1)}, bf16[40,1664]{1,0:T(8,128)(2,1)S(1)}, bf16[40,1664]{1,0:T(8,128)(2,1)S...) custom-call(f32[32]{0:T(128)S(1)} %copy-done.6, f32[5]{0:T(128)S(1)} %copy-done.5, ...), custom_call_target="tpu_custom_call" | custom-call | tf_op jit(solution)/shard_map/forward/pallas_call | solution.py:487
  61.9 0.2 collective-permute-start.16
  62.1 1.2 %collective-permute-start.17 = (bf16[40,1664]{1,0:T(8,128)(2,1)S(1)}, bf16[40,1664]{1,0:T(8,128)(2,1)S(1)}, u32[]{:S(2)}, u32[]{:S(2)}) collective-permute-start(bf16[40,1664]{1,0:T(8,128)(2,1)S(1)} %get-tuple-element.64), channel_id=1, source_target_pairs={{0,4},{2,6},{4,0},{6,2},{1,5},{3,7},{5,1},{7,3},{8,12},{10,14},{12... | collective-permute-start | bytes 399368 | tf_op jit(solution)/shard_map/ppermute | solution.py:397
  63.3 0.5 collective-permute-start.18
  63.8 3.6 %backward.1 = bf16[256,1536]{1,0:T(8,128)(2,1)} custom-call(f32[256,1536]{1,0:T(8,128)S(1)} %get-tuple-element.66.normed_ref, f32[256,128]{1,0:T(8,128)S(1)} %get-tuple-element.67.inv_ref, bf16[256,160]{1,0:T(8,128)(2,1)S(1)} %get-tuple-element.68.dfc_ref, bf16[384,1536]{1,0:T(8,128)(2,1)S(1)} %copy-done, bf16[160,384]{1,0:T(8,128)(2,1)S(1)} %bitcast.8, ...), custom_call_target="tpu_custom_call" | custom-call | tf_op jit(solution)/shard_map/backward/pallas_call | solution.py:502
  67.4 0.0 collective-permute-done.16.b
  67.4 1.0 %collective-permute-done.17.c = bf16[40,1664]{1,0:T(8,128)(2,1)S(1)} collective-permute-done((bf16[40,1664]{1,0:T(8,128)(2,1)S(1)}, bf16[40,1664]{1,0:T(8,128)(2,1)S(1)}, u32[]{:S(2)}, u32[]{:S(2)}) %collective-permute-start.17) | collective-permute-done | bytes 133152 | tf_op jit(solution)/shard_map/ppermute | solution.py:397
  68.5 1.7 %collective-permute-done.18.d = bf16[40,1664]{1,0:T(8,128)(2,1)S(1)} collective-permute-done((bf16[40,1664]{1,0:T(8,128)(2,1)S(1)}, bf16[40,1664]{1,0:T(8,128)(2,1)S(1)}, u32[]{:S(2)}, u32[]{:S(2)}) %collective-permute-start.18) | collective-permute-done | bytes 133152 | tf_op jit(solution)/shard_map/ppermute | solution.py:397
  70.2 0.2 lat_sum.1
  70.4 1.3 %collective-permute-start.19 = (bf16[40,384]{1,0:T(8,128)(2,1)S(1)}, bf16[40,384]{1,0:T(8,128)(2,1)S(1)}, u32[]{:S(2)}, u32[]{:S(2)}) collective-permute-start(bf16[40,384]{1,0:T(8,128)(2,1)S(1)} %get-tuple-element.76), channel_id=1, source_target_pairs={{0,8},{8,0},{16,24},{24,16},{1,9},{9,1},{17,25},{25,17},{2,10},{10... | collective-permute-start | bytes 92168 | tf_op jit(solution)/shard_map/ppermute | solution.py:397
  71.6 2.0 %collective-permute-start.20 = (bf16[40,384]{1,0:T(8,128)(2,1)S(1)}, bf16[40,384]{1,0:T(8,128)(2,1)S(1)}, u32[]{:S(2)}, u32[]{:S(2)}) collective-permute-start(bf16[40,384]{1,0:T(8,128)(2,1)S(1)} %get-tuple-element.77), channel_id=1, source_target_pairs={{0,16},{8,24},{16,0},{24,8},{1,17},{9,25},{17,1},{25,9},{2,18},{10... | collective-permute-start | bytes 92168 | tf_op jit(solution)/shard_map/ppermute | solution.py:397
  73.6 1.2 %collective-permute-start.21 = (bf16[40,384]{1,0:T(8,128)(2,1)S(1)}, bf16[40,384]{1,0:T(8,128)(2,1)S(1)}, u32[]{:S(2)}, u32[]{:S(2)}) collective-permute-start(bf16[40,384]{1,0:T(8,128)(2,1)S(1)} %get-tuple-element.78), channel_id=1, source_target_pairs={{0,24},{8,16},{16,8},{24,0},{1,25},{9,17},{17,9},{25,1},{2,26},{10... | collective-permute-start | bytes 92168 | tf_op jit(solution)/shard_map/ppermute | solution.py:397
  74.8 0.0 collective-permute-done.19.b
  74.8 2.1 %collective-permute-done.20.c = bf16[40,384]{1,0:T(8,128)(2,1)S(1)} collective-permute-done((bf16[40,384]{1,0:T(8,128)(2,1)S(1)}, bf16[40,384]{1,0:T(8,128)(2,1)S(1)}, u32[]{:S(2)}, u32[]{:S(2)}) %collective-permute-start.20) | collective-permute-done | bytes 30752 | tf_op jit(solution)/shard_map/ppermute | solution.py:397
  76.9 2.4 %collective-permute-done.21.d = bf16[40,384]{1,0:T(8,128)(2,1)S(1)} collective-permute-done((bf16[40,384]{1,0:T(8,128)(2,1)S(1)}, bf16[40,384]{1,0:T(8,128)(2,1)S(1)}, u32[]{:S(2)}, u32[]{:S(2)}) %collective-permute-start.21) | collective-permute-done | bytes 30752 | tf_op jit(solution)/shard_map/ppermute | solution.py:397
  79.4 0.5 collective-permute-start.28
  79.8 2.3 %collective-permute-start.27 = (bf16[48,384]{1,0:T(8,128)(2,1)S(1)}, bf16[48,384]{1,0:T(8,128)(2,1)S(1)}, u32[]{:S(2)}, u32[]{:S(2)}) collective-permute-start(bf16[48,384]{1,0:T(8,128)(2,1)S(1)} %dp_sum.1.refs_0_), channel_id=1, source_target_pairs={{0,6},{1,7},{2,4},{3,5},{4,2},{5,3},{6,0},{7,1},{8,14},{9,15},{10,... | collective-permute-start | bytes 110600 | tf_op jit(solution)/shard_map/ppermute | solution.py:538
  82.1 1.2 %collective-permute-start.26 = (bf16[48,384]{1,0:T(8,128)(2,1)S(1)}, bf16[48,384]{1,0:T(8,128)(2,1)S(1)}, u32[]{:S(2)}, u32[]{:S(2)}) collective-permute-start(bf16[48,384]{1,0:T(8,128)(2,1)S(1)} %dp_sum.1.refs_0_), channel_id=1, source_target_pairs={{0,5},{1,4},{2,7},{3,6},{4,1},{5,0},{6,3},{7,2},{8,13},{9,12},{10,... | collective-permute-start | bytes 110600 | tf_op jit(solution)/shard_map/ppermute | solution.py:538
  83.3 0.8 collective-permute-start.25
  84.1 0.1 collective-permute-start.24
  84.2 1.5 %collective-permute-start.23 = (bf16[48,384]{1,0:T(8,128)(2,1)S(1)}, bf16[48,384]{1,0:T(8,128)(2,1)S(1)}, u32[]{:S(2)}, u32[]{:S(2)}) collective-permute-start(bf16[48,384]{1,0:T(8,128)(2,1)S(1)} %dp_sum.1.refs_0_), channel_id=1, source_target_pairs={{0,2},{1,3},{2,0},{3,1},{4,6},{5,7},{6,4},{7,5},{8,10},{9,11},{10,... | collective-permute-start | bytes 110600 | tf_op jit(solution)/shard_map/ppermute | solution.py:538
  85.7 0.0 collective-permute-done.27.refs_6_
  85.7 0.5 collective-permute-start.22
  86.3 0.7 collective-permute-done.26.refs_5_
  87.0 0.4 collective-permute-done.25.refs_4_
  87.4 0.5 collective-permute-done.24.refs_3_
  87.8 0.0 collective-permute-done.23.refs_2_
  87.8 1.8 %collective-permute-done.22.refs_1_ = bf16[48,384]{1,0:T(8,128)(2,1)S(1)} collective-permute-done((bf16[48,384]{1,0:T(8,128)(2,1)S(1)}, bf16[48,384]{1,0:T(8,128)(2,1)S(1)}, u32[]{:S(2)}, u32[]{:S(2)}) %collective-permute-start.22) | collective-permute-done | bytes 36896 | tf_op jit(solution)/shard_map/ppermute | solution.py:538
  89.7 0.7 join.1
  (16 shorter events, 0.1 us)
Async XLA Ops:
  3.1 13.6 %collective-permute-start.1 = (bf16[112,1536]{1,0:T(8,128)(2,1)}, bf16[112,1536]{1,0:T(8,128)(2,1)S(1)}, u32[]{:S(2)}, u32[]{:S(2)}) collective-permute-start(bf16[112,1536]{1,0:T(8,128)(2,1)} %payload.1), channel_id=1, source_target_pairs={{0,8},{8,16},{16,24},{24,0},{1,9},{9,17},{17,25},{25,1},{2,10},{10... | collective-permute-start | bytes 1032200 | tf_op jit(solution)/shard_map/ppermute | solution.py:28
  11.2 5.5 %collective-permute-start.2 = (bf16[32,4864]{1,0:T(8,128)(2,1)}, bf16[32,4864]{1,0:T(8,128)(2,1)S(1)}, u32[]{:S(2)}, u32[]{:S(2)}) collective-permute-start(bf16[32,4864]{1,0:T(8,128)(2,1)} %get-tuple-element.44), channel_id=1, source_target_pairs={{0,6},{2,0},{4,2},{6,4},{1,7},{3,1},{5,3},{7,5},{8,14},{10,8},{12,... | collective-permute-start | bytes 933896 | tf_op jit(solution)/shard_map/ppermute | solution.py:28
  16.7 13.1 %collective-permute-start.4 = (bf16[112,1536]{1,0:T(8,128)(2,1)S(1)}, bf16[112,1536]{1,0:T(8,128)(2,1)S(1)}, u32[]{:S(2)}, u32[]{:S(2)}) collective-permute-start(bf16[112,1536]{1,0:T(8,128)(2,1)S(1)} %collective-permute-done.1.refs_9_.refs_3_), channel_id=1, source_target_pairs={{0,4},{2,6},{4,0},{6,2},{1,5},{3,7},{5,1},{7,3},{8,12},{10,14},{12... | collective-permute-start | bytes 1032200 | tf_op jit(solution)/shard_map/ppermute | solution.py:397
  18.0 12.4 %collective-permute-start.3 = (bf16[112,1536]{1,0:T(8,128)(2,1)S(1)}, bf16[112,1536]{1,0:T(8,128)(2,1)S(1)}, u32[]{:S(2)}, u32[]{:S(2)}) collective-permute-start(bf16[112,1536]{1,0:T(8,128)(2,1)S(1)} %collective-permute-done.1.refs_9_.refs_3_), channel_id=1, source_target_pairs={{0,8},{8,16},{16,24},{24,0},{1,9},{9,17},{17,25},{25,1},{2,10},{10... | collective-permute-start | bytes 1032200 | tf_op jit(solution)/shard_map/ppermute | solution.py:28
  19.1 10.7 %collective-permute-start.5 = (bf16[32,4864]{1,0:T(8,128)(2,1)}, bf16[32,4864]{1,0:T(8,128)(2,1)S(1)}, u32[]{:S(2)}, u32[]{:S(2)}) collective-permute-start(bf16[32,4864]{1,0:T(8,128)(2,1)} %get-tuple-element.47), channel_id=1, source_target_pairs={{0,6},{2,0},{4,2},{6,4},{1,7},{3,1},{5,3},{7,5},{8,14},{10,8},{12,... | collective-permute-start | bytes 933896 | tf_op jit(solution)/shard_map/ppermute | solution.py:28
  20.3 23.5 %collective-permute-start = (bf16[64,4864]{1,0:T(8,128)(2,1)}, bf16[64,4864]{1,0:T(8,128)(2,1)S(1)}, u32[]{:S(2)}, u32[]{:S(2)}) collective-permute-start(bf16[64,4864]{1,0:T(8,128)(2,1)} %get-tuple-element.43), channel_id=1, source_target_pairs={{0,1},{1,0},{2,3},{3,2},{4,5},{5,4},{6,7},{7,6},{8,9},{9,8},{10,11... | collective-permute-start | bytes 1867784 | tf_op jit(solution)/shard_map/ppermute | solution.py:28
  21.8 26.7 %collective-permute-start.6 = (bf16[64,4864]{1,0:T(8,128)(2,1)}, bf16[64,4864]{1,0:T(8,128)(2,1)S(1)}, u32[]{:S(2)}, u32[]{:S(2)}) collective-permute-start(bf16[64,4864]{1,0:T(8,128)(2,1)} %get-tuple-element.49), channel_id=1, source_target_pairs={{0,7},{1,6},{2,1},{3,0},{4,3},{5,2},{6,5},{7,4},{8,15},{9,14},{10,... | collective-permute-start | bytes 1867784 | tf_op jit(solution)/shard_map/ppermute | solution.py:456
  30.4 12.5 %collective-permute-start.7 = (bf16[112,1536]{1,0:T(8,128)(2,1)S(1)}, bf16[112,1536]{1,0:T(8,128)(2,1)S(1)}, u32[]{:S(2)}, u32[]{:S(2)}) collective-permute-start(bf16[112,1536]{1,0:T(8,128)(2,1)S(1)} %collective-permute-done.3.refs_13_.refs_7_), channel_id=1, source_target_pairs={{0,8},{8,16},{16,24},{24,0},{1,9},{9,17},{17,25},{25,1},{2,10},{10... | collective-permute-start | bytes 1032200 | tf_op jit(solution)/shard_map/ppermute | solution.py:28
  31.0 23.1 %collective-permute-start.11 = (bf16[112,1536]{1,0:T(8,128)(2,1)S(1)}, bf16[112,1536]{1,0:T(8,128)(2,1)S(1)}, u32[]{:S(2)}, u32[]{:S(2)}) collective-permute-start(bf16[112,1536]{1,0:T(8,128)(2,1)S(1)} %collective-permute-done.3.refs_13_.refs_7_), channel_id=1, source_target_pairs={{0,4},{2,6},{4,0},{6,2},{1,5},{3,7},{5,1},{7,3},{8,12},{10,14},{12... | collective-permute-start | bytes 1032200 | tf_op jit(solution)/shard_map/ppermute | solution.py:397
  42.8 13.1 %collective-permute-start.8 = (bf16[112,1536]{1,0:T(8,128)(2,1)S(1)}, bf16[112,1536]{1,0:T(8,128)(2,1)S(1)}, u32[]{:S(2)}, u32[]{:S(2)}) collective-permute-start(bf16[112,1536]{1,0:T(8,128)(2,1)S(1)} %collective-permute-done.7.refs_17_.refs_11_), channel_id=1, source_target_pairs={{0,4},{2,6},{4,0},{6,2},{1,5},{3,7},{5,1},{7,3},{8,12},{10,14},{12... | collective-permute-start | bytes 1032200 | tf_op jit(solution)/shard_map/ppermute | solution.py:397
  48.5 9.6 %copy-start.4 = (bf16[384]{0:T(512)(128)(2,1)S(1)}, bf16[384]{0:T(512)(128)(2,1)}, u32[]{:S(2)}) copy-start(bf16[384]{0:T(512)(128)(2,1)} %refs_2_.1) | copy-start | bytes 2308
  48.5 9.6 %copy-start.5 = (f32[5]{0:T(128)S(1)}, f32[5]{0:T(128)}, u32[]{:S(2)}) copy-start(f32[5]{0:T(128)} %var_ref.1) | copy-start | bytes 64
  48.5 9.6 %copy-start = (bf16[384,1536]{1,0:T(8,128)(2,1)S(1)}, bf16[384,1536]{1,0:T(8,128)(2,1)}, u32[]{:S(2)}) copy-start(bf16[384,1536]{1,0:T(8,128)(2,1)} %refs_0_.1) | copy-start | bytes 3538948
  48.5 7.4 %collective-permute-start.9 = (bf16[112,1536]{1,0:T(8,128)(2,1)S(1)}, bf16[112,1536]{1,0:T(8,128)(2,1)S(1)}, u32[]{:S(2)}, u32[]{:S(2)}) collective-permute-start(bf16[112,1536]{1,0:T(8,128)(2,1)S(1)} %collective-permute-done.1.refs_9_.refs_3_), channel_id=1, source_target_pairs={{0,2},{2,0},{4,6},{6,4},{1,3},{3,1},{5,7},{7,5},{8,10},{10,8},{12,... | collective-permute-start | bytes 1032200 | tf_op jit(solution)/shard_map/ppermute | solution.py:397
  49.7 6.8 %collective-permute-start.10 = (bf16[112,1536]{1,0:T(8,128)(2,1)S(1)}, bf16[112,1536]{1,0:T(8,128)(2,1)S(1)}, u32[]{:S(2)}, u32[]{:S(2)}) collective-permute-start(bf16[112,1536]{1,0:T(8,128)(2,1)S(1)} %collective-permute-done.4.refs_10_.refs_4_), channel_id=1, source_target_pairs={{0,2},{2,0},{4,6},{6,4},{1,3},{3,1},{5,7},{7,5},{8,10},{10,8},{12,... | collective-permute-start | bytes 1032200 | tf_op jit(solution)/shard_map/ppermute | solution.py:397
  49.7 6.8 %collective-permute-start.12 = (bf16[112,1536]{1,0:T(8,128)(2,1)S(1)}, bf16[112,1536]{1,0:T(8,128)(2,1)S(1)}, u32[]{:S(2)}, u32[]{:S(2)}) collective-permute-start(bf16[112,1536]{1,0:T(8,128)(2,1)S(1)} %collective-permute-done.3.refs_13_.refs_7_), channel_id=1, source_target_pairs={{0,2},{2,0},{4,6},{6,4},{1,3},{3,1},{5,7},{7,5},{8,10},{10,8},{12,... | collective-permute-start | bytes 1032200 | tf_op jit(solution)/shard_map/ppermute | solution.py:397
  50.2 1.1 %copy-start.1 = (bf16[64,4864]{1,0:T(8,128)(2,1)S(1)}, bf16[64,4864]{1,0:T(8,128)(2,1)}, u32[]{:S(2)}) copy-start(bf16[64,4864]{1,0:T(8,128)(2,1)} %get-tuple-element.51.own_ref.refs_1_) | copy-start | bytes 1867780
  51.2 6.9 %copy-start.2 = (bf16[64,4864]{1,0:T(8,128)(2,1)S(1)}, bf16[64,4864]{1,0:T(8,128)(2,1)}, u32[]{:S(2)}) copy-start(bf16[64,4864]{1,0:T(8,128)(2,1)} %get-tuple-element.51.own_ref.refs_1_) | copy-start | bytes 1867780
  51.2 6.9 %copy-start.3 = (bf16[384,160]{0,1:T(8,128)(2,1)S(1)}, bf16[384,160]{0,1:T(8,128)(2,1)}, u32[]{:S(2)}) copy-start(bf16[384,160]{0,1:T(8,128)(2,1)} %param.12) | copy-start | bytes 368644
  51.2 6.9 %copy-start.6 = (f32[32]{0:T(128)S(1)}, f32[32]{0:T(128)}, u32[]{:S(2)}) copy-start(f32[32]{0:T(128)} %constant.2.clone.lat_ref) | copy-start | bytes 388
  54.1 2.4 %collective-permute-start.14 = (bf16[112,1536]{1,0:T(8,128)(2,1)S(1)}, bf16[112,1536]{1,0:T(8,128)(2,1)S(1)}, u32[]{:S(2)}, u32[]{:S(2)}) collective-permute-start(bf16[112,1536]{1,0:T(8,128)(2,1)S(1)} %collective-permute-done.7.refs_17_.refs_11_), channel_id=1, source_target_pairs={{0,2},{2,0},{4,6},{6,4},{1,3},{3,1},{5,7},{7,5},{8,10},{10,8},{12,... | collective-permute-start | bytes 1032200 | tf_op jit(solution)/shard_map/ppermute | solution.py:397
  56.0 1.7 %collective-permute-start.13 = (bf16[112,1536]{1,0:T(8,128)(2,1)S(1)}, bf16[112,1536]{1,0:T(8,128)(2,1)S(1)}, u32[]{:S(2)}, u32[]{:S(2)}) collective-permute-start(bf16[112,1536]{1,0:T(8,128)(2,1)S(1)} %collective-permute-done.11.refs_14_.refs_8_), channel_id=1, source_target_pairs={{0,2},{2,0},{4,6},{6,4},{1,3},{3,1},{5,7},{7,5},{8,10},{10,8},{12,... | collective-permute-start | bytes 1032200 | tf_op jit(solution)/shard_map/ppermute | solution.py:397
  56.0 2.1 %collective-permute-start.15 = (bf16[112,1536]{1,0:T(8,128)(2,1)S(1)}, bf16[112,1536]{1,0:T(8,128)(2,1)S(1)}, u32[]{:S(2)}, u32[]{:S(2)}) collective-permute-start(bf16[112,1536]{1,0:T(8,128)(2,1)S(1)} %collective-permute-done.8.refs_18_.refs_12_), channel_id=1, source_target_pairs={{0,2},{2,0},{4,6},{6,4},{1,3},{3,1},{5,7},{7,5},{8,10},{10,8},{12,... | collective-permute-start | bytes 1032200 | tf_op jit(solution)/shard_map/ppermute | solution.py:397
  61.9 5.6 %collective-permute-start.16 = (bf16[40,1664]{1,0:T(8,128)(2,1)S(1)}, bf16[40,1664]{1,0:T(8,128)(2,1)S(1)}, u32[]{:S(2)}, u32[]{:S(2)}) collective-permute-start(bf16[40,1664]{1,0:T(8,128)(2,1)S(1)} %get-tuple-element.63), channel_id=1, source_target_pairs={{0,2},{2,0},{4,6},{6,4},{1,3},{3,1},{5,7},{7,5},{8,10},{10,8},{12,... | collective-permute-start | bytes 399368 | tf_op jit(solution)/shard_map/ppermute | solution.py:397
  62.1 6.4 %collective-permute-start.17 = (bf16[40,1664]{1,0:T(8,128)(2,1)S(1)}, bf16[40,1664]{1,0:T(8,128)(2,1)S(1)}, u32[]{:S(2)}, u32[]{:S(2)}) collective-permute-start(bf16[40,1664]{1,0:T(8,128)(2,1)S(1)} %get-tuple-element.64), channel_id=1, source_target_pairs={{0,4},{2,6},{4,0},{6,2},{1,5},{3,7},{5,1},{7,3},{8,12},{10,14},{12... | collective-permute-start | bytes 399368 | tf_op jit(solution)/shard_map/ppermute | solution.py:397
  63.3 6.9 %collective-permute-start.18 = (bf16[40,1664]{1,0:T(8,128)(2,1)S(1)}, bf16[40,1664]{1,0:T(8,128)(2,1)S(1)}, u32[]{:S(2)}, u32[]{:S(2)}) collective-permute-start(bf16[40,1664]{1,0:T(8,128)(2,1)S(1)} %get-tuple-element.65), channel_id=1, source_target_pairs={{0,6},{2,4},{4,2},{6,0},{1,7},{3,5},{5,3},{7,1},{8,14},{10,12},{12... | collective-permute-start | bytes 399368 | tf_op jit(solution)/shard_map/ppermute | solution.py:397
  70.4 4.4 %collective-permute-start.19 = (bf16[40,384]{1,0:T(8,128)(2,1)S(1)}, bf16[40,384]{1,0:T(8,128)(2,1)S(1)}, u32[]{:S(2)}, u32[]{:S(2)}) collective-permute-start(bf16[40,384]{1,0:T(8,128)(2,1)S(1)} %get-tuple-element.76), channel_id=1, source_target_pairs={{0,8},{8,0},{16,24},{24,16},{1,9},{9,1},{17,25},{25,17},{2,10},{10... | collective-permute-start | bytes 92168 | tf_op jit(solution)/shard_map/ppermute | solution.py:397
  71.6 5.2 %collective-permute-start.20 = (bf16[40,384]{1,0:T(8,128)(2,1)S(1)}, bf16[40,384]{1,0:T(8,128)(2,1)S(1)}, u32[]{:S(2)}, u32[]{:S(2)}) collective-permute-start(bf16[40,384]{1,0:T(8,128)(2,1)S(1)} %get-tuple-element.77), channel_id=1, source_target_pairs={{0,16},{8,24},{16,0},{24,8},{1,17},{9,25},{17,1},{25,9},{2,18},{10... | collective-permute-start | bytes 92168 | tf_op jit(solution)/shard_map/ppermute | solution.py:397
  73.6 5.7 %collective-permute-start.21 = (bf16[40,384]{1,0:T(8,128)(2,1)S(1)}, bf16[40,384]{1,0:T(8,128)(2,1)S(1)}, u32[]{:S(2)}, u32[]{:S(2)}) collective-permute-start(bf16[40,384]{1,0:T(8,128)(2,1)S(1)} %get-tuple-element.78), channel_id=1, source_target_pairs={{0,24},{8,16},{16,8},{24,0},{1,25},{9,17},{17,9},{25,1},{2,26},{10... | collective-permute-start | bytes 92168 | tf_op jit(solution)/shard_map/ppermute | solution.py:397
  79.4 4.9 %collective-permute-start.28 = (bf16[48,384]{1,0:T(8,128)(2,1)S(1)}, bf16[48,384]{1,0:T(8,128)(2,1)S(1)}, u32[]{:S(2)}, u32[]{:S(2)}) collective-permute-start(bf16[48,384]{1,0:T(8,128)(2,1)S(1)} %dp_sum.1.refs_0_), channel_id=1, source_target_pairs={{0,7},{1,6},{2,5},{3,4},{4,3},{5,2},{6,1},{7,0},{8,15},{9,14},{10,... | collective-permute-start | bytes 110600 | tf_op jit(solution)/shard_map/ppermute | solution.py:538
  79.8 5.9 %collective-permute-start.27 = (bf16[48,384]{1,0:T(8,128)(2,1)S(1)}, bf16[48,384]{1,0:T(8,128)(2,1)S(1)}, u32[]{:S(2)}, u32[]{:S(2)}) collective-permute-start(bf16[48,384]{1,0:T(8,128)(2,1)S(1)} %dp_sum.1.refs_0_), channel_id=1, source_target_pairs={{0,6},{1,7},{2,4},{3,5},{4,2},{5,3},{6,0},{7,1},{8,14},{9,15},{10,... | collective-permute-start | bytes 110600 | tf_op jit(solution)/shard_map/ppermute | solution.py:538
  82.1 4.9 %collective-permute-start.26 = (bf16[48,384]{1,0:T(8,128)(2,1)S(1)}, bf16[48,384]{1,0:T(8,128)(2,1)S(1)}, u32[]{:S(2)}, u32[]{:S(2)}) collective-permute-start(bf16[48,384]{1,0:T(8,128)(2,1)S(1)} %dp_sum.1.refs_0_), channel_id=1, source_target_pairs={{0,5},{1,4},{2,7},{3,6},{4,1},{5,0},{6,3},{7,2},{8,13},{9,12},{10,... | collective-permute-start | bytes 110600 | tf_op jit(solution)/shard_map/ppermute | solution.py:538
  83.3 4.1 %collective-permute-start.25 = (bf16[48,384]{1,0:T(8,128)(2,1)S(1)}, bf16[48,384]{1,0:T(8,128)(2,1)S(1)}, u32[]{:S(2)}, u32[]{:S(2)}) collective-permute-start(bf16[48,384]{1,0:T(8,128)(2,1)S(1)} %dp_sum.1.refs_0_), channel_id=1, source_target_pairs={{0,4},{1,5},{2,6},{3,7},{4,0},{5,1},{6,2},{7,3},{8,12},{9,13},{10,... | collective-permute-start | bytes 110600 | tf_op jit(solution)/shard_map/ppermute | solution.py:538
  84.1 3.7 %collective-permute-start.24 = (bf16[48,384]{1,0:T(8,128)(2,1)S(1)}, bf16[48,384]{1,0:T(8,128)(2,1)S(1)}, u32[]{:S(2)}, u32[]{:S(2)}) collective-permute-start(bf16[48,384]{1,0:T(8,128)(2,1)S(1)} %dp_sum.1.refs_0_), channel_id=1, source_target_pairs={{0,3},{1,2},{2,1},{3,0},{4,7},{5,6},{6,5},{7,4},{8,11},{9,10},{10,... | collective-permute-start | bytes 110600 | tf_op jit(solution)/shard_map/ppermute | solution.py:538
  84.2 3.6 %collective-permute-start.23 = (bf16[48,384]{1,0:T(8,128)(2,1)S(1)}, bf16[48,384]{1,0:T(8,128)(2,1)S(1)}, u32[]{:S(2)}, u32[]{:S(2)}) collective-permute-start(bf16[48,384]{1,0:T(8,128)(2,1)S(1)} %dp_sum.1.refs_0_), channel_id=1, source_target_pairs={{0,2},{1,3},{2,0},{3,1},{4,6},{5,7},{6,4},{7,5},{8,10},{9,11},{10,... | collective-permute-start | bytes 110600 | tf_op jit(solution)/shard_map/ppermute | solution.py:538
  85.7 4.0 %collective-permute-start.22 = (bf16[48,384]{1,0:T(8,128)(2,1)S(1)}, bf16[48,384]{1,0:T(8,128)(2,1)S(1)}, u32[]{:S(2)}, u32[]{:S(2)}) collective-permute-start(bf16[48,384]{1,0:T(8,128)(2,1)S(1)} %dp_sum.1.refs_0_), channel_id=1, source_target_pairs={{0,1},{1,0},{2,3},{3,2},{4,5},{5,4},{6,7},{7,6},{8,9},{9,8},{10,11... | collective-permute-start | bytes 110600 | tf_op jit(solution)/shard_map/ppermute | solution.py:538

commit v10 on v9

--- a/solution.py
+++ b/solution.py
@@ -158,7 +158,8 @@
     return jnp.broadcast_to(gain_ref[...].astype(F32).reshape(1, rows), (16, rows)).astype(BF)
 
 
-def pack_kernel(x_ref, t_ref, valid_ref, o0, o1, o2, o3, o4, x_in, t_in, v_in, sems):
+def pack_kernel(x_ref, t_ref, valid_ref, *refs):
+    outs, (x_in, t_in, v_in, sems) = refs[:4], refs[4:]
     span = t_ref.shape[-1]
     count = x_ref.shape[0] * 64
     quarter = count // 4
@@ -192,7 +193,8 @@
     spread = jnp.broadcast_to(natural, (count, 128)).astype(BF)
     column = jnp.dot(pick, spread, preferred_element_type=F32)
     extra = jnp.concatenate([goal, column[:, : EXTRA - span]], axis=1).astype(BF)
-    outs = [(o0, 0), (o1, quarter), (o2, 2 * quarter), (o3, 5 * quarter // 2), (o4, 3 * quarter)]
+    starts = [sum(o.shape[0] for o in outs[:n]) for n in range(4)]
+    outs = list(zip(outs, starts))
     for ref, row in outs:
         ref[:, width:] = extra[row : row + ref.shape[0]]
     for n, at in enumerate(range(0, width, step)):
@@ -203,20 +205,12 @@
             ref[:, at : at + step] = out[row : row + ref.shape[0]]
 
 
-def windows_of(own_ref, east_ref, south0_ref, south1_ref, diag_ref):
-    return [
-        (
-            own_ref.at[32 * w : 32 * w + 32],
-            east_ref.at[32 * w : 32 * w + 32],
-            south,
-            diag_ref.at[32 * w : 32 * w + 32],
-        )
-        for w, south in enumerate((south0_ref, south1_ref))
-    ]
-
-
-def attention_kernel(own_ref, east_ref, south0_ref, south1_ref, diag_ref, ctx_ref):
-    tiles = windows_of(own_ref, east_ref, south0_ref, south1_ref, diag_ref)
+def windows_of(*tiles):
+    return [[t.at[32 * w : 32 * w + 32] for t in tiles] for w in range(2)]
+
+
+def attention_kernel(*refs):
+    tiles, ctx_ref = windows_of(*refs[:4]), refs[4]
     part = ctx_ref.shape[1]
     is_last = lax.axis_index("lat") == lax.axis_size("lat") - 1
     same = (iota((512, 128), 0) % 128) // 64 == iota((512, 128), 1) // 64
@@ -285,7 +279,7 @@
 
 def forward_kernel(lat_ref, var_ref, *refs):
     ctx_ref, refs = refs[0], refs[1:]
-    extras, refs = refs[:5], refs[5:]
+    extras, refs = refs[:4], refs[4:]
     owned, refs = refs[:3], refs[3:]
     pieces, refs = refs[:PIECES], refs[PIECES:]
     ts, refs = refs[:4], refs[4:]
@@ -407,7 +401,6 @@
     levels = projected.shape[1]
     span = unpatch_matrix.shape[1]
     tokens = levels * 64
-    quarter = tokens // 4
     lat_total = 8 * lat
     angle = math.pi * ((np.arange(lat_total) + 0.5) / lat_total - 0.5)
     cosine = np.cos(angle)
@@ -427,11 +420,9 @@
     ring1 = from_behind(payload, "dp", 1)
     own, *send = pl.pallas_call(
         pack_kernel,
-        out_shape=[shape((quarter, 3 * width + EXTRA), BF)] * 2
-        + [shape((quarter // 2, 3 * width + EXTRA), BF)] * 2
-        + [shape((quarter, 3 * width + EXTRA), BF)],
+        out_shape=[shape((n, 3 * width + EXTRA), BF) for n in (64, 64, 64, 64)],
         in_specs=[HBM] * 3,
-        out_specs=[VMEM] * 5,
+        out_specs=[VMEM] * 4,
         scratch_shapes=[
             pltpu.VMEM((levels, 8, 8, 3 * width), BF),
             pltpu.VMEM((levels, 8, 8, span), BF),
@@ -448,25 +439,22 @@
     corner = [
         (a * lon + b, ((a - 1) % lat) * lon + (b - 1) % lon) for a in range(lat) for b in range(lon)
     ]
-    tiles = [
-        own,
-        from_behind(send[0], "lon", -1),
-        from_behind(send[1], "lat", -1),
-        from_behind(send[2], "lat", -1),
-        lax.ppermute(send[3], ("lat", "lon"), corner),
-    ]
-    ring1_after, tiles[2] = barrier((ring1, tiles[2]))
-    ring2 = from_behind(ring1_after, "dp", 1)
-    across1 = swap(ring1, "lat", 2)
-    ring2_after, across1, tiles[3] = barrier((ring2, across1, tiles[3]))
+    south = from_behind(send[1], "lat", -1)
+    diag = lax.ppermute(send[2], ("lat", "lon"), corner)
+    ring2 = from_behind(ring1, "dp", 1)
+    across2 = swap(ring2, "lat", 2)
+    ring2_after, east, south, diag = barrier((ring2, send[0], south, diag))
     ring3 = from_behind(ring2_after, "dp", 1)
-    across2 = swap(ring2, "lat", 2)
-    across3 = swap(ring3, "lat", 2)
+    east = from_behind(east, "lon", -1)
+    across3 = from_behind(across2, "dp", 1)
+    ring1_late, across2 = barrier((ring1, across2))
+    across1 = swap(ring1_late, "lat", 2)
+    tiles = [own, east, south, diag]
     *tiles, ring1, across1, ring2 = barrier((*tiles, ring1, across1, ring2))
     ctx = pl.pallas_call(
         attention_kernel,
         out_shape=shape((tokens, width), BF),
-        in_specs=[VMEM] * 5,
+        in_specs=[VMEM] * 4,
         out_specs=VMEM,
         compiler_params=params(16),
         name="attention",

time: 90.6 us -> 83.5 us (0.922)
  waiting for transfers between devices: 42.7 us -> 38 us
  starting transfers between devices: 27.3 us -> 24.9 us
    ppermute x1, waiting for transfers between devices: 4.73 us -> 0.01 us  [shards(): diag = lax.ppermute(send[2], ('lat', 'lon'), corner)]
    ppermute x15 -> x14, waiting for transfers between devices: 10.7 us -> 14.1 us  [swap(): lax.ppermute(array, axis, [(i, i ^ bit) for i in range(lax.axis_size(axis...]
    ppermute x6, waiting for transfers between devices: 23.9 us -> 20.5 us  [from_behind(): lax.ppermute(array, axis, [(i, (i + by) % length) for i in range(length)])]
    ppermute x15 -> x14, starting transfers between devices: 12.1 us -> 9.89 us  [swap(): lax.ppermute(array, axis, [(i, i ^ bit) for i in range(lax.axis_size(axis...]
    ppermute x6, starting transfers between devices: 8.29 us -> 6.26 us  [from_behind(): lax.ppermute(array, axis, [(i, (i + by) % length) for i in range(length)])]
    ppermute x1, starting transfers between devices: 0.01 us -> 1.89 us  [shards(): diag = lax.ppermute(send[2], ('lat', 'lon'), corner)]
  transfers between devices with their start and end apart: 29 -> 28, of which waited for: 16 -> 15; matrix products, arithmetic and copies ran while one was open for 0% -> 0% of each run, Pallas kernels for 13% -> 14%
where the time goes in v10:
time: 83.5 us; the launch traced here: 83.3 us
  waiting for transfers between devices  38 us (46%)
  starting transfers between devices  24.9 us (30%)
  Pallas kernels  18.5 us (22%)
  local copies, waits for them, and re-layouts  1.1 us (1%)
    ppermute x6, waiting for transfers between devices, from_behind(): lax.ppermute(array, axis, [(i, (i + by) % length) for i in range(length)])  20.5 us
    ppermute x14, waiting for transfers between devices, swap(): lax.ppermute(array, axis, [(i, i ^ bit) for i in range(lax.axis_size(axis...  14.1 us
    ppermute x14, starting transfers between devices, swap(): lax.ppermute(array, axis, [(i, i ^ bit) for i in range(lax.axis_size(axis...  9.89 us
    ppermute x7, starting transfers between devices, shards(): plane.append(lax.ppermute(mine, ('lat', 'lon'), pairs))  6.88 us
    ppermute x6, starting transfers between devices, from_behind(): lax.ppermute(array, axis, [(i, (i + by) % length) for i in range(length)])  6.26 us
    pallas_call x1, Pallas kernels, shards(): pl.pallas_call(pack_kernel, out_shape=[shape((n, 3 * width + EXTRA), BF)...  4.99 us
    pallas_call x1, Pallas kernels, shards(): pl.pallas_call(forward_kernel, grid=(1,), out_shape=[shape((piece, width...  3.68 us
    pallas_call x1, Pallas kernels, shards(): pl.pallas_call(backward_kernel, out_shape=shape((tokens, width), BF), in_...  3.61 us
  transfers between devices with their start and end apart: 28, of which 15 were waited for; matrix products, arithmetic and copies ran while one was open for 0% of the time, Pallas kernels for 14%

profile of v10, /device:TPU:0, one launch (start us, length us, event | category | flops | bytes accessed | tf_op | source)
XLA Modules:
  0.0 83.3 jit_solution(10678888557912255336)
XLA Ops:
  0.6 2.4 %payload.1 = bf16[112,1536]{1,0:T(8,128)(2,1)} custom-call(bf16[384,1536]{1,0:T(8,128)(2,1)} %refs_0_.1, bf16[160,384]{1,0:T(8,128)(2,1)} %bitcast.6, bf16[384]{0:T(512)(128)(2,1)} %refs_2_.1), custom_call_target="tpu_custom_call" | custom-call | tf_op jit(solution)/shard_map/payload/pallas_call | solution.py:411
  3.1 3.1 %collective-permute-start = (bf16[112,1536]{1,0:T(8,128)(2,1)}, bf16[112,1536]{1,0:T(8,128)(2,1)S(1)}, u32[]{:S(2)}, u32[]{:S(2)}) collective-permute-start(bf16[112,1536]{1,0:T(8,128)(2,1)} %payload.1), channel_id=1, source_target_pairs={{0,8},{8,16},{16,24},{24,0},{1,9},{9,17},{17,25},{25,1},{2,10},{10... | collective-permute-start | bytes 1032200 | tf_op jit(solution)/shard_map/ppermute | solution.py:28
  6.2 5.0 %pack.1 = (bf16[64,4864]{1,0:T(8,128)(2,1)}, bf16[64,4864]{1,0:T(8,128)(2,1)}, bf16[64,4864]{1,0:T(8,128)(2,1)}, bf16[64,4864]{1,0:T(8,128)(2,1)}) custom-call(bf16[4,8,8,4608]{3,2,1,0:T(8,128)(2,1)} %bitcast.9, bf16[4,8,8,160]{3,2,1,0:T(8,128)(2,1)} %bitcast.11, s32[8,8]{1,0:T(8,128)} %valid_ref.1), custom_call_target="tpu_custom_call" | custom-call | tf_op jit(solution)/shard_map/pack/pallas_call | solution.py:421
  11.2 0.7 collective-permute-start.2
  11.9 1.9 %collective-permute-start.3 = (bf16[64,4864]{1,0:T(8,128)(2,1)}, bf16[64,4864]{1,0:T(8,128)(2,1)S(1)}, u32[]{:S(2)}, u32[]{:S(2)}) collective-permute-start(bf16[64,4864]{1,0:T(8,128)(2,1)} %get-tuple-element.44), channel_id=1, source_target_pairs={{0,7},{1,6},{2,1},{3,0},{4,3},{5,2},{6,5},{7,4},{8,15},{9,14},{10,... | collective-permute-start | bytes 1867784 | tf_op jit(solution)/shard_map/ppermute | solution.py:443
  13.8 2.7 %collective-permute-done.refs_8_.refs_3_ = bf16[112,1536]{1,0:T(8,128)(2,1)S(1)} collective-permute-done((bf16[112,1536]{1,0:T(8,128)(2,1)}, bf16[112,1536]{1,0:T(8,128)(2,1)S(1)}, u32[]{:S(2)}, u32[]{:S(2)}) %collective-permute-start) | collective-permute-done | bytes 344096 | tf_op jit(solution)/shard_map/ppermute | solution.py:28
  16.5 0.0 collective-permute-start.1
  16.5 11.0 %collective-permute-done.1.refs_12_.refs_7_ = bf16[112,1536]{1,0:T(8,128)(2,1)S(1)} collective-permute-done((bf16[112,1536]{1,0:T(8,128)(2,1)S(1)}, bf16[112,1536]{1,0:T(8,128)(2,1)S(1)}, u32[]{:S(2)}, u32[]{:S(2)}) %collective-permute-start.1) | collective-permute-done | bytes 344096 | tf_op jit(solution)/shard_map/ppermute | solution.py:28
  27.5 1.3 %collective-permute-start.5 = (bf16[112,1536]{1,0:T(8,128)(2,1)S(1)}, bf16[112,1536]{1,0:T(8,128)(2,1)S(1)}, u32[]{:S(2)}, u32[]{:S(2)}) collective-permute-start(bf16[112,1536]{1,0:T(8,128)(2,1)S(1)} %collective-permute-done.1.refs_12_.refs_7_), channel_id=1, source_target_pairs={{0,4},{2,6},{4,0},{6,2},{1,5},{3,7},{5,1},{7,3},{8,12},{10,14},{12... | collective-permute-start | bytes 1032200 | tf_op jit(solution)/shard_map/ppermute | solution.py:391
  28.8 0.0 collective-permute-done.2.refs_2_.refs_3_
  28.8 0.0 collective-permute-done.3.refs_3_.refs_4_
  28.8 1.5 %collective-permute-start.4 = (bf16[64,4864]{1,0:T(8,128)(2,1)}, bf16[64,4864]{1,0:T(8,128)(2,1)S(1)}, u32[]{:S(2)}, u32[]{:S(2)}) collective-permute-start(bf16[64,4864]{1,0:T(8,128)(2,1)} %get-tuple-element.45), channel_id=1, source_target_pairs={{0,1},{1,0},{2,3},{3,2},{4,5},{5,4},{6,7},{7,6},{8,9},{9,8},{10,11... | collective-permute-start | bytes 1867784 | tf_op jit(solution)/shard_map/ppermute | solution.py:28
  30.3 0.3 collective-permute-start.12
  30.5 5.6 %collective-permute-done.5.refs_13_.refs_8_ = bf16[112,1536]{1,0:T(8,128)(2,1)S(1)} collective-permute-done((bf16[112,1536]{1,0:T(8,128)(2,1)S(1)}, bf16[112,1536]{1,0:T(8,128)(2,1)S(1)}, u32[]{:S(2)}, u32[]{:S(2)}) %collective-permute-start.5) | collective-permute-done | bytes 344096 | tf_op jit(solution)/shard_map/ppermute | solution.py:391
  36.2 1.1 %collective-permute-start.6 = (bf16[112,1536]{1,0:T(8,128)(2,1)S(1)}, bf16[112,1536]{1,0:T(8,128)(2,1)S(1)}, u32[]{:S(2)}, u32[]{:S(2)}) collective-permute-start(bf16[112,1536]{1,0:T(8,128)(2,1)S(1)} %collective-permute-done.refs_8_.refs_3_), channel_id=1, source_target_pairs={{0,4},{2,6},{4,0},{6,2},{1,5},{3,7},{5,1},{7,3},{8,12},{10,14},{12... | collective-permute-start | bytes 1032200 | tf_op jit(solution)/shard_map/ppermute | solution.py:391
  37.3 0.7 collective-permute-start.7
  38.0 0.0 collective-permute-start.11
  38.0 5.1 %collective-permute-done.12.refs_16_.refs_11_ = bf16[112,1536]{1,0:T(8,128)(2,1)S(1)} collective-permute-done((bf16[112,1536]{1,0:T(8,128)(2,1)S(1)}, bf16[112,1536]{1,0:T(8,128)(2,1)S(1)}, u32[]{:S(2)}, u32[]{:S(2)}) %collective-permute-start.12) | collective-permute-done | bytes 344096 | tf_op jit(solution)/shard_map/ppermute | solution.py:28
  43.1 0.0 collective-permute-start.13
  43.1 1.7 %collective-permute-done.4.refs_1_.refs_2_ = bf16[64,4864]{1,0:T(8,128)(2,1)S(1)} collective-permute-done((bf16[64,4864]{1,0:T(8,128)(2,1)}, bf16[64,4864]{1,0:T(8,128)(2,1)S(1)}, u32[]{:S(2)}, u32[]{:S(2)}) %collective-permute-start.4) | collective-permute-done | bytes 622624 | tf_op jit(solution)/shard_map/ppermute | solution.py:28
  44.8 0.0 collective-permute-done.6.refs_9_.refs_4_
  44.8 0.1 collective-permute-start.8
  44.9 0.5 collective-permute-start.9
  45.4 1.1 %copy-done.1 = bf16[64,4864]{1,0:T(8,128)(2,1)S(1)} copy-done((bf16[64,4864]{1,0:T(8,128)(2,1)S(1)}, bf16[64,4864]{1,0:T(8,128)(2,1)}, u32[]{:S(2)}) %copy-start.1) | copy-done | bytes 622616
  46.5 2.8 %attention.1.refs_0_ = bf16[256,1536]{1,0:T(8,128)(2,1)S(1)} custom-call(bf16[64,4864]{1,0:T(8,128)(2,1)S(1)} %copy-done.1, bf16[64,4864]{1,0:T(8,128)(2,1)S(1)} %collective-permute-done.4.refs_1_.refs_2_, bf16[64,4864]{1,0:T(8,128)(2,1)S(1)} %collective-permute-done.2.refs_2_.refs_3_, bf16[64,4864]{1,0:T(8,128)(2,1)S(1)} %collective-permute-done.3.refs_3_.refs_4_), custom_call_target="tpu_custom_call" | custom-call | tf_op jit(solution)/shard_map/attention/pallas_call | solution.py:454
  49.3 0.0 collective-permute-done.7.refs_17_.refs_12_
  49.3 0.1 collective-permute-start.10
  49.4 0.0 collective-permute-done.11.refs_15_.refs_10_
  49.4 0.4 collective-permute-start.14
  49.9 0.0 collective-permute-done.13.refs_18_.refs_13_
  49.9 0.0 collective-permute-done.8.refs_10_.refs_5_
  49.9 0.0 collective-permute-done.9.refs_11_.refs_6_
  49.9 1.1 %collective-permute-done.10.refs_14_.refs_9_ = bf16[112,1536]{1,0:T(8,128)(2,1)S(1)} collective-permute-done((bf16[112,1536]{1,0:T(8,128)(2,1)S(1)}, bf16[112,1536]{1,0:T(8,128)(2,1)S(1)}, u32[]{:S(2)}, u32[]{:S(2)}) %collective-permute-start.10) | collective-permute-done | bytes 344096 | tf_op jit(solution)/shard_map/ppermute | solution.py:391
  51.0 0.5 collective-permute-done.14.refs_19_.refs_14_
  51.6 3.7 %forward.1 = (bf16[40,1664]{1,0:T(8,128)(2,1)S(1)}, bf16[40,1664]{1,0:T(8,128)(2,1)S(1)}, bf16[40,1664]{1,0:T(8,128)(2,1)S(1)}, bf16[40,1664]{1,0:T(8,128)(2,1)S...) custom-call(f32[32]{0:T(128)S(1)} %copy-done.6, f32[5]{0:T(128)S(1)} %copy-done.5, ...), custom_call_target="tpu_custom_call" | custom-call | tf_op jit(solution)/shard_map/forward/pallas_call | solution.py:475
  55.2 0.2 collective-permute-start.15
  55.4 1.1 %collective-permute-start.16 = (bf16[40,1664]{1,0:T(8,128)(2,1)S(1)}, bf16[40,1664]{1,0:T(8,128)(2,1)S(1)}, u32[]{:S(2)}, u32[]{:S(2)}) collective-permute-start(bf16[40,1664]{1,0:T(8,128)(2,1)S(1)} %get-tuple-element.62), channel_id=1, source_target_pairs={{0,4},{2,6},{4,0},{6,2},{1,5},{3,7},{5,1},{7,3},{8,12},{10,14},{12... | collective-permute-start | bytes 399368 | tf_op jit(solution)/shard_map/ppermute | solution.py:391
  56.6 0.6 collective-permute-start.17
  57.2 3.6 %backward.1 = bf16[256,1536]{1,0:T(8,128)(2,1)} custom-call(f32[256,1536]{1,0:T(8,128)S(1)} %get-tuple-element.64.normed_ref, f32[256,128]{1,0:T(8,128)S(1)} %get-tuple-element.65.inv_ref, bf16[256,160]{1,0:T(8,128)(2,1)S(1)} %get-tuple-element.66.dfc_ref, bf16[384,1536]{1,0:T(8,128)(2,1)S(1)} %copy-done, bf16[160,384]{1,0:T(8,128)(2,1)S(1)} %bitcast.8, ...), custom_call_target="tpu_custom_call" | custom-call | tf_op jit(solution)/shard_map/backward/pallas_call | solution.py:490
  60.8 0.0 collective-permute-done.15.b
  60.8 1.0 %collective-permute-done.16.c = bf16[40,1664]{1,0:T(8,128)(2,1)S(1)} collective-permute-done((bf16[40,1664]{1,0:T(8,128)(2,1)S(1)}, bf16[40,1664]{1,0:T(8,128)(2,1)S(1)}, u32[]{:S(2)}, u32[]{:S(2)}) %collective-permute-start.16) | collective-permute-done | bytes 133152 | tf_op jit(solution)/shard_map/ppermute | solution.py:391
  61.8 1.7 %collective-permute-done.17.d = bf16[40,1664]{1,0:T(8,128)(2,1)S(1)} collective-permute-done((bf16[40,1664]{1,0:T(8,128)(2,1)S(1)}, bf16[40,1664]{1,0:T(8,128)(2,1)S(1)}, u32[]{:S(2)}, u32[]{:S(2)}) %collective-permute-start.17) | collective-permute-done | bytes 133152 | tf_op jit(solution)/shard_map/ppermute | solution.py:391
  63.6 0.2 lat_sum.1
  63.7 1.2 %collective-permute-start.18 = (bf16[40,384]{1,0:T(8,128)(2,1)S(1)}, bf16[40,384]{1,0:T(8,128)(2,1)S(1)}, u32[]{:S(2)}, u32[]{:S(2)}) collective-permute-start(bf16[40,384]{1,0:T(8,128)(2,1)S(1)} %get-tuple-element.74), channel_id=1, source_target_pairs={{0,8},{8,0},{16,24},{24,16},{1,9},{9,1},{17,25},{25,17},{2,10},{10... | collective-permute-start | bytes 92168 | tf_op jit(solution)/shard_map/ppermute | solution.py:391
  65.0 1.5 %collective-permute-start.19 = (bf16[40,384]{1,0:T(8,128)(2,1)S(1)}, bf16[40,384]{1,0:T(8,128)(2,1)S(1)}, u32[]{:S(2)}, u32[]{:S(2)}) collective-permute-start(bf16[40,384]{1,0:T(8,128)(2,1)S(1)} %get-tuple-element.75), channel_id=1, source_target_pairs={{0,16},{8,24},{16,0},{24,8},{1,17},{9,25},{17,1},{25,9},{2,18},{10... | collective-permute-start | bytes 92168 | tf_op jit(solution)/shard_map/ppermute | solution.py:391
  66.5 1.6 %collective-permute-start.20 = (bf16[40,384]{1,0:T(8,128)(2,1)S(1)}, bf16[40,384]{1,0:T(8,128)(2,1)S(1)}, u32[]{:S(2)}, u32[]{:S(2)}) collective-permute-start(bf16[40,384]{1,0:T(8,128)(2,1)S(1)} %get-tuple-element.76), channel_id=1, source_target_pairs={{0,24},{8,16},{16,8},{24,0},{1,25},{9,17},{17,9},{25,1},{2,26},{10... | collective-permute-start | bytes 92168 | tf_op jit(solution)/shard_map/ppermute | solution.py:391
  68.1 0.0 collective-permute-done.18.b
  68.1 2.0 %collective-permute-done.19.c = bf16[40,384]{1,0:T(8,128)(2,1)S(1)} collective-permute-done((bf16[40,384]{1,0:T(8,128)(2,1)S(1)}, bf16[40,384]{1,0:T(8,128)(2,1)S(1)}, u32[]{:S(2)}, u32[]{:S(2)}) %collective-permute-start.19) | collective-permute-done | bytes 30752 | tf_op jit(solution)/shard_map/ppermute | solution.py:391
  70.1 2.1 %collective-permute-done.20.d = bf16[40,384]{1,0:T(8,128)(2,1)S(1)} collective-permute-done((bf16[40,384]{1,0:T(8,128)(2,1)S(1)}, bf16[40,384]{1,0:T(8,128)(2,1)S(1)}, u32[]{:S(2)}, u32[]{:S(2)}) %collective-permute-start.20) | collective-permute-done | bytes 30752 | tf_op jit(solution)/shard_map/ppermute | solution.py:391
  72.2 0.6 collective-permute-start.27
  72.8 2.1 %collective-permute-start.26 = (bf16[48,384]{1,0:T(8,128)(2,1)S(1)}, bf16[48,384]{1,0:T(8,128)(2,1)S(1)}, u32[]{:S(2)}, u32[]{:S(2)}) collective-permute-start(bf16[48,384]{1,0:T(8,128)(2,1)S(1)} %dp_sum.1.refs_0_), channel_id=1, source_target_pairs={{0,6},{1,7},{2,4},{3,5},{4,2},{5,3},{6,0},{7,1},{8,14},{9,15},{10,... | collective-permute-start | bytes 110600 | tf_op jit(solution)/shard_map/ppermute | solution.py:526
  75.0 1.3 %collective-permute-start.25 = (bf16[48,384]{1,0:T(8,128)(2,1)S(1)}, bf16[48,384]{1,0:T(8,128)(2,1)S(1)}, u32[]{:S(2)}, u32[]{:S(2)}) collective-permute-start(bf16[48,384]{1,0:T(8,128)(2,1)S(1)} %dp_sum.1.refs_0_), channel_id=1, source_target_pairs={{0,5},{1,4},{2,7},{3,6},{4,1},{5,0},{6,3},{7,2},{8,13},{9,12},{10,... | collective-permute-start | bytes 110600 | tf_op jit(solution)/shard_map/ppermute | solution.py:526
  76.2 0.7 collective-permute-start.24
  77.0 0.0 collective-permute-start.23
  77.0 0.0 collective-permute-done.27.refs_7_
  77.0 1.6 %collective-permute-start.22 = (bf16[48,384]{1,0:T(8,128)(2,1)S(1)}, bf16[48,384]{1,0:T(8,128)(2,1)S(1)}, u32[]{:S(2)}, u32[]{:S(2)}) collective-permute-start(bf16[48,384]{1,0:T(8,128)(2,1)S(1)} %dp_sum.1.refs_0_), channel_id=1, source_target_pairs={{0,2},{1,3},{2,0},{3,1},{4,6},{5,7},{6,4},{7,5},{8,10},{9,11},{10,... | collective-permute-start | bytes 110600 | tf_op jit(solution)/shard_map/ppermute | solution.py:526
  78.6 0.0 collective-permute-done.26.refs_6_
  78.6 0.5 collective-permute-start.21
  79.1 0.7 collective-permute-done.25.refs_5_
  79.8 0.4 collective-permute-done.24.refs_4_
  80.2 0.5 collective-permute-done.23.refs_3_
  80.7 0.0 collective-permute-done.22.refs_2_
  80.7 1.8 %collective-permute-done.21.refs_1_ = bf16[48,384]{1,0:T(8,128)(2,1)S(1)} collective-permute-done((bf16[48,384]{1,0:T(8,128)(2,1)S(1)}, bf16[48,384]{1,0:T(8,128)(2,1)S(1)}, u32[]{:S(2)}, u32[]{:S(2)}) %collective-permute-start.21) | collective-permute-done | bytes 36896 | tf_op jit(solution)/shard_map/ppermute | solution.py:526
  82.6 0.7 join.1
  (14 shorter events, 0.1 us)
Async XLA Ops:
  3.1 13.4 %collective-permute-start = (bf16[112,1536]{1,0:T(8,128)(2,1)}, bf16[112,1536]{1,0:T(8,128)(2,1)S(1)}, u32[]{:S(2)}, u32[]{:S(2)}) collective-permute-start(bf16[112,1536]{1,0:T(8,128)(2,1)} %payload.1), channel_id=1, source_target_pairs={{0,8},{8,16},{16,24},{24,0},{1,9},{9,17},{17,25},{25,1},{2,10},{10... | collective-permute-start | bytes 1032200 | tf_op jit(solution)/shard_map/ppermute | solution.py:28
  11.2 17.6 %collective-permute-start.2 = (bf16[64,4864]{1,0:T(8,128)(2,1)}, bf16[64,4864]{1,0:T(8,128)(2,1)S(1)}, u32[]{:S(2)}, u32[]{:S(2)}) collective-permute-start(bf16[64,4864]{1,0:T(8,128)(2,1)} %get-tuple-element.43), channel_id=1, source_target_pairs={{0,6},{2,0},{4,2},{6,4},{1,7},{3,1},{5,3},{7,5},{8,14},{10,8},{12,... | collective-permute-start | bytes 1867784 | tf_op jit(solution)/shard_map/ppermute | solution.py:28
  11.9 16.9 %collective-permute-start.3 = (bf16[64,4864]{1,0:T(8,128)(2,1)}, bf16[64,4864]{1,0:T(8,128)(2,1)S(1)}, u32[]{:S(2)}, u32[]{:S(2)}) collective-permute-start(bf16[64,4864]{1,0:T(8,128)(2,1)} %get-tuple-element.44), channel_id=1, source_target_pairs={{0,7},{1,6},{2,1},{3,0},{4,3},{5,2},{6,5},{7,4},{8,15},{9,14},{10,... | collective-permute-start | bytes 1867784 | tf_op jit(solution)/shard_map/ppermute | solution.py:443
  16.5 11.0 %collective-permute-start.1 = (bf16[112,1536]{1,0:T(8,128)(2,1)S(1)}, bf16[112,1536]{1,0:T(8,128)(2,1)S(1)}, u32[]{:S(2)}, u32[]{:S(2)}) collective-permute-start(bf16[112,1536]{1,0:T(8,128)(2,1)S(1)} %collective-permute-done.refs_8_.refs_3_), channel_id=1, source_target_pairs={{0,8},{8,16},{16,24},{24,0},{1,9},{9,17},{17,25},{25,1},{2,10},{10... | collective-permute-start | bytes 1032200 | tf_op jit(solution)/shard_map/ppermute | solution.py:28
  27.5 8.7 %collective-permute-start.5 = (bf16[112,1536]{1,0:T(8,128)(2,1)S(1)}, bf16[112,1536]{1,0:T(8,128)(2,1)S(1)}, u32[]{:S(2)}, u32[]{:S(2)}) collective-permute-start(bf16[112,1536]{1,0:T(8,128)(2,1)S(1)} %collective-permute-done.1.refs_12_.refs_7_), channel_id=1, source_target_pairs={{0,4},{2,6},{4,0},{6,2},{1,5},{3,7},{5,1},{7,3},{8,12},{10,14},{12... | collective-permute-start | bytes 1032200 | tf_op jit(solution)/shard_map/ppermute | solution.py:391
  28.8 16.0 %collective-permute-start.4 = (bf16[64,4864]{1,0:T(8,128)(2,1)}, bf16[64,4864]{1,0:T(8,128)(2,1)S(1)}, u32[]{:S(2)}, u32[]{:S(2)}) collective-permute-start(bf16[64,4864]{1,0:T(8,128)(2,1)} %get-tuple-element.45), channel_id=1, source_target_pairs={{0,1},{1,0},{2,3},{3,2},{4,5},{5,4},{6,7},{7,6},{8,9},{9,8},{10,11... | collective-permute-start | bytes 1867784 | tf_op jit(solution)/shard_map/ppermute | solution.py:28
  30.3 12.8 %collective-permute-start.12 = (bf16[112,1536]{1,0:T(8,128)(2,1)S(1)}, bf16[112,1536]{1,0:T(8,128)(2,1)S(1)}, u32[]{:S(2)}, u32[]{:S(2)}) collective-permute-start(bf16[112,1536]{1,0:T(8,128)(2,1)S(1)} %collective-permute-done.1.refs_12_.refs_7_), channel_id=1, source_target_pairs={{0,8},{8,16},{16,24},{24,0},{1,9},{9,17},{17,25},{25,1},{2,10},{10... | collective-permute-start | bytes 1032200 | tf_op jit(solution)/shard_map/ppermute | solution.py:28
  36.2 8.6 %collective-permute-start.6 = (bf16[112,1536]{1,0:T(8,128)(2,1)S(1)}, bf16[112,1536]{1,0:T(8,128)(2,1)S(1)}, u32[]{:S(2)}, u32[]{:S(2)}) collective-permute-start(bf16[112,1536]{1,0:T(8,128)(2,1)S(1)} %collective-permute-done.refs_8_.refs_3_), channel_id=1, source_target_pairs={{0,4},{2,6},{4,0},{6,2},{1,5},{3,7},{5,1},{7,3},{8,12},{10,14},{12... | collective-permute-start | bytes 1032200 | tf_op jit(solution)/shard_map/ppermute | solution.py:391
  37.3 12.0 %collective-permute-start.7 = (bf16[112,1536]{1,0:T(8,128)(2,1)S(1)}, bf16[112,1536]{1,0:T(8,128)(2,1)S(1)}, u32[]{:S(2)}, u32[]{:S(2)}) collective-permute-start(bf16[112,1536]{1,0:T(8,128)(2,1)S(1)} %collective-permute-done.5.refs_13_.refs_8_), channel_id=1, source_target_pairs={{0,8},{8,16},{16,24},{24,0},{1,9},{9,17},{17,25},{25,1},{2,10},{10... | collective-permute-start | bytes 1032200 | tf_op jit(solution)/shard_map/ppermute | solution.py:28
  38.0 11.5 %collective-permute-start.11 = (bf16[112,1536]{1,0:T(8,128)(2,1)S(1)}, bf16[112,1536]{1,0:T(8,128)(2,1)S(1)}, u32[]{:S(2)}, u32[]{:S(2)}) collective-permute-start(bf16[112,1536]{1,0:T(8,128)(2,1)S(1)} %collective-permute-done.5.refs_13_.refs_8_), channel_id=1, source_target_pairs={{0,2},{2,0},{4,6},{6,4},{1,3},{3,1},{5,7},{7,5},{8,10},{10,8},{12,... | collective-permute-start | bytes 1032200 | tf_op jit(solution)/shard_map/ppermute | solution.py:391
  43.1 6.8 %collective-permute-start.13 = (bf16[112,1536]{1,0:T(8,128)(2,1)S(1)}, bf16[112,1536]{1,0:T(8,128)(2,1)S(1)}, u32[]{:S(2)}, u32[]{:S(2)}) collective-permute-start(bf16[112,1536]{1,0:T(8,128)(2,1)S(1)} %collective-permute-done.12.refs_16_.refs_11_), channel_id=1, source_target_pairs={{0,2},{2,0},{4,6},{6,4},{1,3},{3,1},{5,7},{7,5},{8,10},{10,8},{12,... | collective-permute-start | bytes 1032200 | tf_op jit(solution)/shard_map/ppermute | solution.py:391
  44.8 6.7 %copy-start.4 = (bf16[384]{0:T(512)(128)(2,1)S(1)}, bf16[384]{0:T(512)(128)(2,1)}, u32[]{:S(2)}) copy-start(bf16[384]{0:T(512)(128)(2,1)} %refs_2_.1) | copy-start | bytes 2308
  44.8 6.7 %copy-start.5 = (f32[5]{0:T(128)S(1)}, f32[5]{0:T(128)}, u32[]{:S(2)}) copy-start(f32[5]{0:T(128)} %var_ref.1) | copy-start | bytes 64
  44.8 6.7 %copy-start = (bf16[384,1536]{1,0:T(8,128)(2,1)S(1)}, bf16[384,1536]{1,0:T(8,128)(2,1)}, u32[]{:S(2)}) copy-start(bf16[384,1536]{1,0:T(8,128)(2,1)} %refs_0_.1) | copy-start | bytes 3538948
  44.8 5.1 %collective-permute-start.8 = (bf16[112,1536]{1,0:T(8,128)(2,1)S(1)}, bf16[112,1536]{1,0:T(8,128)(2,1)S(1)}, u32[]{:S(2)}, u32[]{:S(2)}) collective-permute-start(bf16[112,1536]{1,0:T(8,128)(2,1)S(1)} %collective-permute-done.refs_8_.refs_3_), channel_id=1, source_target_pairs={{0,2},{2,0},{4,6},{6,4},{1,3},{3,1},{5,7},{7,5},{8,10},{10,8},{12,... | collective-permute-start | bytes 1032200 | tf_op jit(solution)/shard_map/ppermute | solution.py:391
  44.9 5.0 %collective-permute-start.9 = (bf16[112,1536]{1,0:T(8,128)(2,1)S(1)}, bf16[112,1536]{1,0:T(8,128)(2,1)S(1)}, u32[]{:S(2)}, u32[]{:S(2)}) collective-permute-start(bf16[112,1536]{1,0:T(8,128)(2,1)S(1)} %collective-permute-done.6.refs_9_.refs_4_), channel_id=1, source_target_pairs={{0,2},{2,0},{4,6},{6,4},{1,3},{3,1},{5,7},{7,5},{8,10},{10,8},{12,... | collective-permute-start | bytes 1032200 | tf_op jit(solution)/shard_map/ppermute | solution.py:391
  45.4 1.1 %copy-start.1 = (bf16[64,4864]{1,0:T(8,128)(2,1)S(1)}, bf16[64,4864]{1,0:T(8,128)(2,1)}, u32[]{:S(2)}) copy-start(bf16[64,4864]{1,0:T(8,128)(2,1)} %get-tuple-element.49.refs_0_.refs_1_) | copy-start | bytes 1867780
  46.5 5.1 %copy-start.2 = (bf16[64,4864]{1,0:T(8,128)(2,1)S(1)}, bf16[64,4864]{1,0:T(8,128)(2,1)}, u32[]{:S(2)}) copy-start(bf16[64,4864]{1,0:T(8,128)(2,1)} %get-tuple-element.49.refs_0_.refs_1_) | copy-start | bytes 1867780
  46.5 5.1 %copy-start.3 = (bf16[384,160]{0,1:T(8,128)(2,1)S(1)}, bf16[384,160]{0,1:T(8,128)(2,1)}, u32[]{:S(2)}) copy-start(bf16[384,160]{0,1:T(8,128)(2,1)} %param.12) | copy-start | bytes 368644
  46.5 5.1 %copy-start.6 = (f32[32]{0:T(128)S(1)}, f32[32]{0:T(128)}, u32[]{:S(2)}) copy-start(f32[32]{0:T(128)} %constant.2.clone.lat_ref) | copy-start | bytes 388
  49.3 1.7 %collective-permute-start.10 = (bf16[112,1536]{1,0:T(8,128)(2,1)S(1)}, bf16[112,1536]{1,0:T(8,128)(2,1)S(1)}, u32[]{:S(2)}, u32[]{:S(2)}) collective-permute-start(bf16[112,1536]{1,0:T(8,128)(2,1)S(1)} %collective-permute-done.1.refs_12_.refs_7_), channel_id=1, source_target_pairs={{0,2},{2,0},{4,6},{6,4},{1,3},{3,1},{5,7},{7,5},{8,10},{10,8},{12,... | collective-permute-start | bytes 1032200 | tf_op jit(solution)/shard_map/ppermute | solution.py:391
  49.4 2.1 %collective-permute-start.14 = (bf16[112,1536]{1,0:T(8,128)(2,1)S(1)}, bf16[112,1536]{1,0:T(8,128)(2,1)S(1)}, u32[]{:S(2)}, u32[]{:S(2)}) collective-permute-start(bf16[112,1536]{1,0:T(8,128)(2,1)S(1)} %collective-permute-done.7.refs_17_.refs_12_), channel_id=1, source_target_pairs={{0,2},{2,0},{4,6},{6,4},{1,3},{3,1},{5,7},{7,5},{8,10},{10,8},{12,... | collective-permute-start | bytes 1032200 | tf_op jit(solution)/shard_map/ppermute | solution.py:391
  55.2 5.5 %collective-permute-start.15 = (bf16[40,1664]{1,0:T(8,128)(2,1)S(1)}, bf16[40,1664]{1,0:T(8,128)(2,1)S(1)}, u32[]{:S(2)}, u32[]{:S(2)}) collective-permute-start(bf16[40,1664]{1,0:T(8,128)(2,1)S(1)} %get-tuple-element.61), channel_id=1, source_target_pairs={{0,2},{2,0},{4,6},{6,4},{1,3},{3,1},{5,7},{7,5},{8,10},{10,8},{12,... | collective-permute-start | bytes 399368 | tf_op jit(solution)/shard_map/ppermute | solution.py:391
  55.4 6.4 %collective-permute-start.16 = (bf16[40,1664]{1,0:T(8,128)(2,1)S(1)}, bf16[40,1664]{1,0:T(8,128)(2,1)S(1)}, u32[]{:S(2)}, u32[]{:S(2)}) collective-permute-start(bf16[40,1664]{1,0:T(8,128)(2,1)S(1)} %get-tuple-element.62), channel_id=1, source_target_pairs={{0,4},{2,6},{4,0},{6,2},{1,5},{3,7},{5,1},{7,3},{8,12},{10,14},{12... | collective-permute-start | bytes 399368 | tf_op jit(solution)/shard_map/ppermute | solution.py:391
  56.6 7.0 %collective-permute-start.17 = (bf16[40,1664]{1,0:T(8,128)(2,1)S(1)}, bf16[40,1664]{1,0:T(8,128)(2,1)S(1)}, u32[]{:S(2)}, u32[]{:S(2)}) collective-permute-start(bf16[40,1664]{1,0:T(8,128)(2,1)S(1)} %get-tuple-element.63), channel_id=1, source_target_pairs={{0,6},{2,4},{4,2},{6,0},{1,7},{3,5},{5,3},{7,1},{8,14},{10,12},{12... | collective-permute-start | bytes 399368 | tf_op jit(solution)/shard_map/ppermute | solution.py:391
  63.7 4.4 %collective-permute-start.18 = (bf16[40,384]{1,0:T(8,128)(2,1)S(1)}, bf16[40,384]{1,0:T(8,128)(2,1)S(1)}, u32[]{:S(2)}, u32[]{:S(2)}) collective-permute-start(bf16[40,384]{1,0:T(8,128)(2,1)S(1)} %get-tuple-element.74), channel_id=1, source_target_pairs={{0,8},{8,0},{16,24},{24,16},{1,9},{9,1},{17,25},{25,17},{2,10},{10... | collective-permute-start | bytes 92168 | tf_op jit(solution)/shard_map/ppermute | solution.py:391
  65.0 5.2 %collective-permute-start.19 = (bf16[40,384]{1,0:T(8,128)(2,1)S(1)}, bf16[40,384]{1,0:T(8,128)(2,1)S(1)}, u32[]{:S(2)}, u32[]{:S(2)}) collective-permute-start(bf16[40,384]{1,0:T(8,128)(2,1)S(1)} %get-tuple-element.75), channel_id=1, source_target_pairs={{0,16},{8,24},{16,0},{24,8},{1,17},{9,25},{17,1},{25,9},{2,18},{10... | collective-permute-start | bytes 92168 | tf_op jit(solution)/shard_map/ppermute | solution.py:391
  66.5 5.7 %collective-permute-start.20 = (bf16[40,384]{1,0:T(8,128)(2,1)S(1)}, bf16[40,384]{1,0:T(8,128)(2,1)S(1)}, u32[]{:S(2)}, u32[]{:S(2)}) collective-permute-start(bf16[40,384]{1,0:T(8,128)(2,1)S(1)} %get-tuple-element.76), channel_id=1, source_target_pairs={{0,24},{8,16},{16,8},{24,0},{1,25},{9,17},{17,9},{25,1},{2,26},{10... | collective-permute-start | bytes 92168 | tf_op jit(solution)/shard_map/ppermute | solution.py:391
  72.2 4.8 %collective-permute-start.27 = (bf16[48,384]{1,0:T(8,128)(2,1)S(1)}, bf16[48,384]{1,0:T(8,128)(2,1)S(1)}, u32[]{:S(2)}, u32[]{:S(2)}) collective-permute-start(bf16[48,384]{1,0:T(8,128)(2,1)S(1)} %dp_sum.1.refs_0_), channel_id=1, source_target_pairs={{0,7},{1,6},{2,5},{3,4},{4,3},{5,2},{6,1},{7,0},{8,15},{9,14},{10,... | collective-permute-start | bytes 110600 | tf_op jit(solution)/shard_map/ppermute | solution.py:526
  72.8 5.8 %collective-permute-start.26 = (bf16[48,384]{1,0:T(8,128)(2,1)S(1)}, bf16[48,384]{1,0:T(8,128)(2,1)S(1)}, u32[]{:S(2)}, u32[]{:S(2)}) collective-permute-start(bf16[48,384]{1,0:T(8,128)(2,1)S(1)} %dp_sum.1.refs_0_), channel_id=1, source_target_pairs={{0,6},{1,7},{2,4},{3,5},{4,2},{5,3},{6,0},{7,1},{8,14},{9,15},{10,... | collective-permute-start | bytes 110600 | tf_op jit(solution)/shard_map/ppermute | solution.py:526
  75.0 4.9 %collective-permute-start.25 = (bf16[48,384]{1,0:T(8,128)(2,1)S(1)}, bf16[48,384]{1,0:T(8,128)(2,1)S(1)}, u32[]{:S(2)}, u32[]{:S(2)}) collective-permute-start(bf16[48,384]{1,0:T(8,128)(2,1)S(1)} %dp_sum.1.refs_0_), channel_id=1, source_target_pairs={{0,5},{1,4},{2,7},{3,6},{4,1},{5,0},{6,3},{7,2},{8,13},{9,12},{10,... | collective-permute-start | bytes 110600 | tf_op jit(solution)/shard_map/ppermute | solution.py:526
  76.2 4.0 %collective-permute-start.24 = (bf16[48,384]{1,0:T(8,128)(2,1)S(1)}, bf16[48,384]{1,0:T(8,128)(2,1)S(1)}, u32[]{:S(2)}, u32[]{:S(2)}) collective-permute-start(bf16[48,384]{1,0:T(8,128)(2,1)S(1)} %dp_sum.1.refs_0_), channel_id=1, source_target_pairs={{0,4},{1,5},{2,6},{3,7},{4,0},{5,1},{6,2},{7,3},{8,12},{9,13},{10,... | collective-permute-start | bytes 110600 | tf_op jit(solution)/shard_map/ppermute | solution.py:526
  77.0 3.7 %collective-permute-start.23 = (bf16[48,384]{1,0:T(8,128)(2,1)S(1)}, bf16[48,384]{1,0:T(8,128)(2,1)S(1)}, u32[]{:S(2)}, u32[]{:S(2)}) collective-permute-start(bf16[48,384]{1,0:T(8,128)(2,1)S(1)} %dp_sum.1.refs_0_), channel_id=1, source_target_pairs={{0,3},{1,2},{2,1},{3,0},{4,7},{5,6},{6,5},{7,4},{8,11},{9,10},{10,... | collective-permute-start | bytes 110600 | tf_op jit(solution)/shard_map/ppermute | solution.py:526
  77.0 3.7 %collective-permute-start.22 = (bf16[48,384]{1,0:T(8,128)(2,1)S(1)}, bf16[48,384]{1,0:T(8,128)(2,1)S(1)}, u32[]{:S(2)}, u32[]{:S(2)}) collective-permute-start(bf16[48,384]{1,0:T(8,128)(2,1)S(1)} %dp_sum.1.refs_0_), channel_id=1, source_target_pairs={{0,2},{1,3},{2,0},{3,1},{4,6},{5,7},{6,4},{7,5},{8,10},{9,11},{10,... | collective-permute-start | bytes 110600 | tf_op jit(solution)/shard_map/ppermute | solution.py:526
  78.6 4.0 %collective-permute-start.21 = (bf16[48,384]{1,0:T(8,128)(2,1)S(1)}, bf16[48,384]{1,0:T(8,128)(2,1)S(1)}, u32[]{:S(2)}, u32[]{:S(2)}) collective-permute-start(bf16[48,384]{1,0:T(8,128)(2,1)S(1)} %dp_sum.1.refs_0_), channel_id=1, source_target_pairs={{0,1},{1,0},{2,3},{3,2},{4,5},{5,4},{6,7},{7,6},{8,9},{9,8},{10,11... | collective-permute-start | bytes 110600 | tf_op jit(solution)/shard_map/ppermute | solution.py:526

commit v11 on v10

--- a/solution.py
+++ b/solution.py
@@ -373,14 +373,23 @@
     o_ref[rows:, :] = jnp.concatenate([block, zeros], axis=1).astype(BF)
 
 
+def pair_kernel(mine_ref, other_ref, o_ref):
+    rows = mine_ref.shape[0]
+    odd = lax.axis_index("lat") % 2
+    o_ref[pl.ds(pl.multiple_of(odd * rows, 8), rows), :] = mine_ref[...]
+    o_ref[pl.ds(pl.multiple_of((1 - odd) * rows, 8), rows), :] = other_ref[...]
+
+
 def join_kernel(counts, *refs):
-    pieces, (o_ref, loss_ref) = refs[:8], refs[8:]
-    lat_place = lax.axis_index("lat")
-    rows = o_ref.shape[0] // 4
-    for a in range(4):
-        at = pl.multiple_of((lat_place ^ a) * rows, 8)
-        both = [pieces[2 * a + b][0:rows, :].astype(F32) for b in range(2)]
-        o_ref[pl.ds(at, rows), :] = (both[0] + both[1]) / counts[0]
+    pieces, (o_ref, loss_ref) = refs[:4], refs[4:]
+    chip = lax.axis_index("lat") // 2
+    held = pieces[0].shape[0] // 2
+    rows = held - 8
+    for a in range(2):
+        for n in range(2):
+            at = pl.multiple_of((2 * (chip ^ a) + n) * rows, 8)
+            both = [pieces[2 * a + b][held * n : held * n + rows, :].astype(F32) for b in range(2)]
+            o_ref[pl.ds(at, rows), :] = (both[0] + both[1]) / counts[0]
     sums = [
         jnp.sum(p[rows : rows + 1, 0:128].astype(F32), axis=1, keepdims=True) for p in pieces[:2]
     ]
@@ -450,7 +459,7 @@
     ring1_late, across2 = barrier((ring1, across2))
     across1 = swap(ring1_late, "lat", 2)
     tiles = [own, east, south, diag]
-    *tiles, ring1, across1, ring2 = barrier((*tiles, ring1, across1, ring2))
+    *tiles, ring1, across1, ring2, across3 = barrier((*tiles, ring1, across1, ring2, across3))
     ctx = pl.pallas_call(
         attention_kernel,
         out_shape=shape((tokens, width), BF),
@@ -459,7 +468,6 @@
         compiler_params=params(16),
         name="attention",
     )(*tiles)
-    ctx, across3 = barrier((ctx, across3))
     pieces = []
     for ring, across in ((ring1, across1), (ring2, across2), (ring3, across3)):
         pieces += [ring, across, swap(ring, "lat", 1), swap(across, "lat", 1)]
@@ -516,20 +524,24 @@
         compiler_params=params(4),
         name="dp_sum",
     )(loss, *parts)
-    plane = [mine]
-    for a in range(4):
-        for b in range(2):
-            if a or b:
-                pairs = [
-                    (i * lon + j, (i ^ a) * lon + (j ^ b)) for i in range(lat) for j in range(lon)
-                ]
-                plane.append(lax.ppermute(mine, ("lat", "lon"), pairs))
+    chip = pl.pallas_call(
+        pair_kernel,
+        out_shape=shape((2 * piece + 16, rows), BF),
+        in_specs=[VMEM] * 2,
+        out_specs=VMEM,
+        compiler_params=params(4),
+        name="pair",
+    )(mine, swap(mine, "lat", 1))
+    plane = [chip]
+    for a, b in ((0, 1), (2, 0), (2, 1)):
+        pairs = [(i * lon + j, (i ^ a) * lon + (j ^ b)) for i in range(lat) for j in range(lon)]
+        plane.append(lax.ppermute(chip, ("lat", "lon"), pairs))
     count = levels * lat_total * 8 * lon
     counts = (float(count), float(count * (span // var_weight.shape[0])))
     joined, loss = pl.pallas_call(
         lambda *refs: join_kernel(counts, *refs),
         out_shape=[shape((span, rows), F32), shape((1, 1), F32)],
-        in_specs=[VMEM] * 8,
+        in_specs=[VMEM] * 4,
         out_specs=[VMEM] * 2,
         compiler_params=params(4),
         name="join",

time: 83.5 us -> 82.3 us (0.986)
  starting transfers between devices: 24.9 us -> 21.6 us
  waiting for transfers between devices: 38 us -> 40.1 us
    ppermute x6, waiting for transfers between devices: 20.5 us -> 24.7 us  [from_behind(): lax.ppermute(array, axis, [(i, (i + by) % length) for i in range(length)])]
    ppermute x7 -> x3, starting transfers between devices: 6.88 us -> 3.55 us  [shards(): plane.append(lax.ppermute(chip, ('lat', 'lon'), pairs))]
    ppermute x14 -> x15, waiting for transfers between devices: 14.1 us -> 12.1 us  [swap(): lax.ppermute(array, axis, [(i, i ^ bit) for i in range(lax.axis_size(axis...]
    ppermute x7 -> x3, waiting for transfers between devices: 3.43 us -> 3.21 us  [shards(): plane.append(lax.ppermute(chip, ('lat', 'lon'), pairs))]
    ppermute x14 -> x15, starting transfers between devices: 9.89 us -> 9.82 us  [swap(): lax.ppermute(array, axis, [(i, i ^ bit) for i in range(lax.axis_size(axis...]
  transfers between devices with their start and end apart: 28 -> 25, of which waited for: 15 -> 13; matrix products, arithmetic and copies ran while one was open for 0% -> 0% of each run, Pallas kernels for 14% -> 14%
where the time goes in v11:
time: 82.3 us; the launch traced here: 82.1 us
  waiting for transfers between devices  40.1 us (49%)
  starting transfers between devices  21.6 us (26%)
  Pallas kernels  18.5 us (22%)
  local copies, waits for them, and re-layouts  1.1 us (1%)
    ppermute x6, waiting for transfers between devices, from_behind(): lax.ppermute(array, axis, [(i, (i + by) % length) for i in range(length)])  24.7 us
    ppermute x15, waiting for transfers between devices, swap(): lax.ppermute(array, axis, [(i, i ^ bit) for i in range(lax.axis_size(axis...  12.1 us
    ppermute x15, starting transfers between devices, swap(): lax.ppermute(array, axis, [(i, i ^ bit) for i in range(lax.axis_size(axis...  9.82 us
    ppermute x6, starting transfers between devices, from_behind(): lax.ppermute(array, axis, [(i, (i + by) % length) for i in range(length)])  6.3 us
    pallas_call x1, Pallas kernels, shards(): pl.pallas_call(pack_kernel, out_shape=[shape((n, 3 * width + EXTRA), BF)...  5.01 us
    pallas_call x1, Pallas kernels, shards(): pl.pallas_call(forward_kernel, grid=(1,), out_shape=[shape((piece, width...  3.68 us
    pallas_call x1, Pallas kernels, shards(): pl.pallas_call(backward_kernel, out_shape=shape((tokens, width), BF), in_...  3.61 us
    ppermute x3, starting transfers between devices, shards(): plane.append(lax.ppermute(chip, ('lat', 'lon'), pairs))  3.55 us
  transfers between devices with their start and end apart: 25, of which 13 were waited for; matrix products, arithmetic and copies ran while one was open for 0% of the time, Pallas kernels for 14%

profile of v11, /device:TPU:0, one launch (start us, length us, event | category | flops | bytes accessed | tf_op | source)
XLA Modules:
  0.0 82.1 jit_solution(1999062559797623805)
XLA Ops:
  0.6 2.5 %payload.1 = bf16[112,1536]{1,0:T(8,128)(2,1)} custom-call(bf16[384,1536]{1,0:T(8,128)(2,1)} %refs_0_.1, bf16[160,384]{1,0:T(8,128)(2,1)} %bitcast.6, bf16[384]{0:T(512)(128)(2,1)} %refs_2_.1), custom_call_target="tpu_custom_call" | custom-call | tf_op jit(solution)/shard_map/payload/pallas_call | solution.py:420
  3.1 3.1 %collective-permute-start = (bf16[112,1536]{1,0:T(8,128)(2,1)}, bf16[112,1536]{1,0:T(8,128)(2,1)S(1)}, u32[]{:S(2)}, u32[]{:S(2)}) collective-permute-start(bf16[112,1536]{1,0:T(8,128)(2,1)} %payload.1), channel_id=1, source_target_pairs={{0,8},{8,16},{16,24},{24,0},{1,9},{9,17},{17,25},{25,1},{2,10},{10... | collective-permute-start | bytes 1032200 | tf_op jit(solution)/shard_map/ppermute | solution.py:28
  6.2 5.0 %pack.1 = (bf16[64,4864]{1,0:T(8,128)(2,1)}, bf16[64,4864]{1,0:T(8,128)(2,1)}, bf16[64,4864]{1,0:T(8,128)(2,1)}, bf16[64,4864]{1,0:T(8,128)(2,1)}) custom-call(bf16[4,8,8,4608]{3,2,1,0:T(8,128)(2,1)} %bitcast.9, bf16[4,8,8,160]{3,2,1,0:T(8,128)(2,1)} %bitcast.11, s32[8,8]{1,0:T(8,128)} %valid_ref.1), custom_call_target="tpu_custom_call" | custom-call | tf_op jit(solution)/shard_map/pack/pallas_call | solution.py:430
  11.2 0.7 collective-permute-start.2
  11.9 1.9 %collective-permute-start.3 = (bf16[64,4864]{1,0:T(8,128)(2,1)}, bf16[64,4864]{1,0:T(8,128)(2,1)S(1)}, u32[]{:S(2)}, u32[]{:S(2)}) collective-permute-start(bf16[64,4864]{1,0:T(8,128)(2,1)} %get-tuple-element.43), channel_id=1, source_target_pairs={{0,7},{1,6},{2,1},{3,0},{4,3},{5,2},{6,5},{7,4},{8,15},{9,14},{10,... | collective-permute-start | bytes 1867784 | tf_op jit(solution)/shard_map/ppermute | solution.py:452
  13.8 2.7 %collective-permute-done.refs_8_.refs_3_ = bf16[112,1536]{1,0:T(8,128)(2,1)S(1)} collective-permute-done((bf16[112,1536]{1,0:T(8,128)(2,1)}, bf16[112,1536]{1,0:T(8,128)(2,1)S(1)}, u32[]{:S(2)}, u32[]{:S(2)}) %collective-permute-start) | collective-permute-done | bytes 344096 | tf_op jit(solution)/shard_map/ppermute | solution.py:28
  16.5 0.0 collective-permute-start.1
  16.5 11.0 %collective-permute-done.1.refs_12_.refs_7_ = bf16[112,1536]{1,0:T(8,128)(2,1)S(1)} collective-permute-done((bf16[112,1536]{1,0:T(8,128)(2,1)S(1)}, bf16[112,1536]{1,0:T(8,128)(2,1)S(1)}, u32[]{:S(2)}, u32[]{:S(2)}) %collective-permute-start.1) | collective-permute-done | bytes 344096 | tf_op jit(solution)/shard_map/ppermute | solution.py:28
  27.5 1.3 %collective-permute-start.5 = (bf16[112,1536]{1,0:T(8,128)(2,1)S(1)}, bf16[112,1536]{1,0:T(8,128)(2,1)S(1)}, u32[]{:S(2)}, u32[]{:S(2)}) collective-permute-start(bf16[112,1536]{1,0:T(8,128)(2,1)S(1)} %collective-permute-done.1.refs_12_.refs_7_), channel_id=1, source_target_pairs={{0,4},{2,6},{4,0},{6,2},{1,5},{3,7},{5,1},{7,3},{8,12},{10,14},{12... | collective-permute-start | bytes 1032200 | tf_op jit(solution)/shard_map/ppermute | solution.py:400
  28.8 0.0 collective-permute-done.2.refs_2_.refs_3_
  28.8 0.0 collective-permute-done.3.refs_3_.refs_4_
  28.8 1.5 %collective-permute-start.4 = (bf16[64,4864]{1,0:T(8,128)(2,1)}, bf16[64,4864]{1,0:T(8,128)(2,1)S(1)}, u32[]{:S(2)}, u32[]{:S(2)}) collective-permute-start(bf16[64,4864]{1,0:T(8,128)(2,1)} %get-tuple-element.44), channel_id=1, source_target_pairs={{0,1},{1,0},{2,3},{3,2},{4,5},{5,4},{6,7},{7,6},{8,9},{9,8},{10,11... | collective-permute-start | bytes 1867784 | tf_op jit(solution)/shard_map/ppermute | solution.py:28
  30.3 0.3 collective-permute-start.12
  30.6 5.6 %collective-permute-done.5.refs_13_.refs_8_ = bf16[112,1536]{1,0:T(8,128)(2,1)S(1)} collective-permute-done((bf16[112,1536]{1,0:T(8,128)(2,1)S(1)}, bf16[112,1536]{1,0:T(8,128)(2,1)S(1)}, u32[]{:S(2)}, u32[]{:S(2)}) %collective-permute-start.5) | collective-permute-done | bytes 344096 | tf_op jit(solution)/shard_map/ppermute | solution.py:400
  36.2 1.1 %collective-permute-start.6 = (bf16[112,1536]{1,0:T(8,128)(2,1)S(1)}, bf16[112,1536]{1,0:T(8,128)(2,1)S(1)}, u32[]{:S(2)}, u32[]{:S(2)}) collective-permute-start(bf16[112,1536]{1,0:T(8,128)(2,1)S(1)} %collective-permute-done.refs_8_.refs_3_), channel_id=1, source_target_pairs={{0,4},{2,6},{4,0},{6,2},{1,5},{3,7},{5,1},{7,3},{8,12},{10,14},{12... | collective-permute-start | bytes 1032200 | tf_op jit(solution)/shard_map/ppermute | solution.py:400
  37.3 0.7 collective-permute-start.7
  38.0 0.0 collective-permute-start.11
  38.0 5.1 %collective-permute-done.12.refs_16_.refs_11_ = bf16[112,1536]{1,0:T(8,128)(2,1)S(1)} collective-permute-done((bf16[112,1536]{1,0:T(8,128)(2,1)S(1)}, bf16[112,1536]{1,0:T(8,128)(2,1)S(1)}, u32[]{:S(2)}, u32[]{:S(2)}) %collective-permute-start.12) | collective-permute-done | bytes 344096 | tf_op jit(solution)/shard_map/ppermute | solution.py:28
  43.1 0.0 collective-permute-start.13
  43.1 1.7 %collective-permute-done.4.refs_1_.refs_2_ = bf16[64,4864]{1,0:T(8,128)(2,1)S(1)} collective-permute-done((bf16[64,4864]{1,0:T(8,128)(2,1)}, bf16[64,4864]{1,0:T(8,128)(2,1)S(1)}, u32[]{:S(2)}, u32[]{:S(2)}) %collective-permute-start.4) | collective-permute-done | bytes 622624 | tf_op jit(solution)/shard_map/ppermute | solution.py:28
  44.8 0.0 collective-permute-done.6.refs_9_.refs_4_
  44.8 4.2 %collective-permute-done.7.refs_17_.refs_12_ = bf16[112,1536]{1,0:T(8,128)(2,1)S(1)} collective-permute-done((bf16[112,1536]{1,0:T(8,128)(2,1)S(1)}, bf16[112,1536]{1,0:T(8,128)(2,1)S(1)}, u32[]{:S(2)}, u32[]{:S(2)}) %collective-permute-start.7) | collective-permute-done | bytes 344096 | tf_op jit(solution)/shard_map/ppermute | solution.py:28
  49.0 0.0 collective-permute-start.8
  49.1 0.5 collective-permute-start.9
  49.6 0.1 collective-permute-start.10
  49.6 0.0 collective-permute-done.11.refs_15_.refs_10_
  49.6 0.4 collective-permute-start.14
  50.1 1.1 %copy-done.1 = bf16[64,4864]{1,0:T(8,128)(2,1)S(1)} copy-done((bf16[64,4864]{1,0:T(8,128)(2,1)S(1)}, bf16[64,4864]{1,0:T(8,128)(2,1)}, u32[]{:S(2)}) %copy-start.1) | copy-done | bytes 622616
  51.2 2.8 %attention.1.refs_0_ = bf16[256,1536]{1,0:T(8,128)(2,1)S(1)} custom-call(bf16[64,4864]{1,0:T(8,128)(2,1)S(1)} %copy-done.1, bf16[64,4864]{1,0:T(8,128)(2,1)S(1)} %collective-permute-done.4.refs_1_.refs_2_, bf16[64,4864]{1,0:T(8,128)(2,1)S(1)} %collective-permute-done.2.refs_2_.refs_3_, bf16[64,4864]{1,0:T(8,128)(2,1)S(1)} %collective-permute-done.3.refs_3_.refs_4_), custom_call_target="tpu_custom_call" | custom-call | tf_op jit(solution)/shard_map/attention/pallas_call | solution.py:463
  54.0 0.0 collective-permute-done.13.refs_18_.refs_13_
  54.0 0.0 collective-permute-done.8.refs_10_.refs_5_
  54.0 0.0 collective-permute-done.9.refs_11_.refs_6_
  54.0 0.0 collective-permute-done.10.refs_14_.refs_9_
  54.0 0.0 collective-permute-done.14.refs_19_.refs_14_
  54.0 0.0 copy-done.4
  54.0 0.0 copy-done.5
  54.1 0.0 copy-done
  54.1 0.0 copy-done.2
  54.1 0.0 copy-done.3
  54.1 0.0 copy-done.6
  54.1 3.7 %forward.1 = (bf16[40,1664]{1,0:T(8,128)(2,1)S(1)}, bf16[40,1664]{1,0:T(8,128)(2,1)S(1)}, bf16[40,1664]{1,0:T(8,128)(2,1)S(1)}, bf16[40,1664]{1,0:T(8,128)(2,1)S...) custom-call(f32[32]{0:T(128)S(1)} %copy-done.6, f32[5]{0:T(128)S(1)} %copy-done.5, ...), custom_call_target="tpu_custom_call" | custom-call | tf_op jit(solution)/shard_map/forward/pallas_call | solution.py:483
  57.8 0.1 collective-permute-start.15
  57.9 1.1 %collective-permute-start.16 = (bf16[40,1664]{1,0:T(8,128)(2,1)S(1)}, bf16[40,1664]{1,0:T(8,128)(2,1)S(1)}, u32[]{:S(2)}, u32[]{:S(2)}) collective-permute-start(bf16[40,1664]{1,0:T(8,128)(2,1)S(1)} %get-tuple-element.60), channel_id=1, source_target_pairs={{0,4},{2,6},{4,0},{6,2},{1,5},{3,7},{5,1},{7,3},{8,12},{10,14},{12... | collective-permute-start | bytes 399368 | tf_op jit(solution)/shard_map/ppermute | solution.py:400
  59.1 0.7 collective-permute-start.17
  59.7 3.6 %backward.1 = bf16[256,1536]{1,0:T(8,128)(2,1)} custom-call(f32[256,1536]{1,0:T(8,128)S(1)} %get-tuple-element.62.normed_ref, f32[256,128]{1,0:T(8,128)S(1)} %get-tuple-element.63.inv_ref, bf16[256,160]{1,0:T(8,128)(2,1)S(1)} %get-tuple-element.64.dfc_ref, bf16[384,1536]{1,0:T(8,128)(2,1)S(1)} %copy-done, bf16[160,384]{1,0:T(8,128)(2,1)S(1)} %bitcast.8, ...), custom_call_target="tpu_custom_call" | custom-call | tf_op jit(solution)/shard_map/backward/pallas_call | solution.py:498
  63.3 0.0 collective-permute-done.15.b
  63.3 0.9 %collective-permute-done.16.c = bf16[40,1664]{1,0:T(8,128)(2,1)S(1)} collective-permute-done((bf16[40,1664]{1,0:T(8,128)(2,1)S(1)}, bf16[40,1664]{1,0:T(8,128)(2,1)S(1)}, u32[]{:S(2)}, u32[]{:S(2)}) %collective-permute-start.16) | collective-permute-done | bytes 133152 | tf_op jit(solution)/shard_map/ppermute | solution.py:400
  64.3 1.9 %collective-permute-done.17.d = bf16[40,1664]{1,0:T(8,128)(2,1)S(1)} collective-permute-done((bf16[40,1664]{1,0:T(8,128)(2,1)S(1)}, bf16[40,1664]{1,0:T(8,128)(2,1)S(1)}, u32[]{:S(2)}, u32[]{:S(2)}) %collective-permute-start.17) | collective-permute-done | bytes 133152 | tf_op jit(solution)/shard_map/ppermute | solution.py:400
  66.2 0.2 lat_sum.1
  66.4 0.0 collective-permute-start.18
  66.4 1.1 %collective-permute-start.19 = (bf16[40,384]{1,0:T(8,128)(2,1)S(1)}, bf16[40,384]{1,0:T(8,128)(2,1)S(1)}, u32[]{:S(2)}, u32[]{:S(2)}) collective-permute-start(bf16[40,384]{1,0:T(8,128)(2,1)S(1)} %get-tuple-element.73), channel_id=1, source_target_pairs={{0,16},{8,24},{16,0},{24,8},{1,17},{9,25},{17,1},{25,9},{2,18},{10... | collective-permute-start | bytes 92168 | tf_op jit(solution)/shard_map/ppermute | solution.py:400
  67.5 3.3 %collective-permute-start.20 = (bf16[40,384]{1,0:T(8,128)(2,1)S(1)}, bf16[40,384]{1,0:T(8,128)(2,1)S(1)}, u32[]{:S(2)}, u32[]{:S(2)}) collective-permute-start(bf16[40,384]{1,0:T(8,128)(2,1)S(1)} %get-tuple-element.74), channel_id=1, source_target_pairs={{0,24},{8,16},{16,8},{24,0},{1,25},{9,17},{17,9},{25,1},{2,26},{10... | collective-permute-start | bytes 92168 | tf_op jit(solution)/shard_map/ppermute | solution.py:400
  70.8 0.0 collective-permute-done.18.b
  70.8 1.4 %collective-permute-done.19.c = bf16[40,384]{1,0:T(8,128)(2,1)S(1)} collective-permute-done((bf16[40,384]{1,0:T(8,128)(2,1)S(1)}, bf16[40,384]{1,0:T(8,128)(2,1)S(1)}, u32[]{:S(2)}, u32[]{:S(2)}) %collective-permute-start.19) | collective-permute-done | bytes 30752 | tf_op jit(solution)/shard_map/ppermute | solution.py:400
  72.2 1.1 %collective-permute-done.20.d = bf16[40,384]{1,0:T(8,128)(2,1)S(1)} collective-permute-done((bf16[40,384]{1,0:T(8,128)(2,1)S(1)}, bf16[40,384]{1,0:T(8,128)(2,1)S(1)}, u32[]{:S(2)}, u32[]{:S(2)}) %collective-permute-start.20) | collective-permute-done | bytes 30752 | tf_op jit(solution)/shard_map/ppermute | solution.py:400
  73.3 0.1 collective-permute-start.21
  73.4 1.2 %collective-permute-done.21.other_ref = bf16[48,384]{1,0:T(8,128)(2,1)S(1)} collective-permute-done((bf16[48,384]{1,0:T(8,128)(2,1)S(1)}, bf16[48,384]{1,0:T(8,128)(2,1)S(1)}, u32[]{:S(2)}, u32[]{:S(2)}) %collective-permute-start.21) | collective-permute-done | bytes 36896 | tf_op jit(solution)/shard_map/ppermute | solution.py:400
  74.6 1.1 %collective-permute-start.24 = (bf16[96,384]{1,0:T(8,128)(2,1)S(1)}, bf16[96,384]{1,0:T(8,128)(2,1)S(1)}, u32[]{:S(2)}, u32[]{:S(2)}) collective-permute-start(bf16[96,384]{1,0:T(8,128)(2,1)S(1)} %pair.1.refs_0_), channel_id=1, source_target_pairs={{0,5},{1,4},{2,7},{3,6},{4,1},{5,0},{6,3},{7,2},{8,13},{9,12},{10,... | collective-permute-start | bytes 221192 | tf_op jit(solution)/shard_map/ppermute | solution.py:538
  75.7 1.0 %collective-permute-start.23 = (bf16[96,384]{1,0:T(8,128)(2,1)S(1)}, bf16[96,384]{1,0:T(8,128)(2,1)S(1)}, u32[]{:S(2)}, u32[]{:S(2)}) collective-permute-start(bf16[96,384]{1,0:T(8,128)(2,1)S(1)} %pair.1.refs_0_), channel_id=1, source_target_pairs={{0,4},{1,5},{2,6},{3,7},{4,0},{5,1},{6,2},{7,3},{8,12},{9,13},{10,... | collective-permute-start | bytes 221192 | tf_op jit(solution)/shard_map/ppermute | solution.py:538
  76.7 1.5 %collective-permute-start.22 = (bf16[96,384]{1,0:T(8,128)(2,1)S(1)}, bf16[96,384]{1,0:T(8,128)(2,1)S(1)}, u32[]{:S(2)}, u32[]{:S(2)}) collective-permute-start(bf16[96,384]{1,0:T(8,128)(2,1)S(1)} %pair.1.refs_0_), channel_id=1, source_target_pairs={{0,1},{1,0},{2,3},{3,2},{4,5},{5,4},{6,7},{7,6},{8,9},{9,8},{10,11... | collective-permute-start | bytes 221192 | tf_op jit(solution)/shard_map/ppermute | solution.py:538
  78.2 2.3 %collective-permute-done.24.refs_3_ = bf16[96,384]{1,0:T(8,128)(2,1)S(1)} collective-permute-done((bf16[96,384]{1,0:T(8,128)(2,1)S(1)}, bf16[96,384]{1,0:T(8,128)(2,1)S(1)}, u32[]{:S(2)}, u32[]{:S(2)}) %collective-permute-start.24) | collective-permute-done | bytes 73760 | tf_op jit(solution)/shard_map/ppermute | solution.py:538
  80.5 0.9 %collective-permute-done.23.refs_2_ = bf16[96,384]{1,0:T(8,128)(2,1)S(1)} collective-permute-done((bf16[96,384]{1,0:T(8,128)(2,1)S(1)}, bf16[96,384]{1,0:T(8,128)(2,1)S(1)}, u32[]{:S(2)}, u32[]{:S(2)}) %collective-permute-start.23) | collective-permute-done | bytes 73760 | tf_op jit(solution)/shard_map/ppermute | solution.py:538
  81.4 0.0 collective-permute-done.22.refs_1_
  81.4 0.7 join.1
  (9 shorter events, 0.1 us)
Async XLA Ops:
  3.1 13.4 %collective-permute-start = (bf16[112,1536]{1,0:T(8,128)(2,1)}, bf16[112,1536]{1,0:T(8,128)(2,1)S(1)}, u32[]{:S(2)}, u32[]{:S(2)}) collective-permute-start(bf16[112,1536]{1,0:T(8,128)(2,1)} %payload.1), channel_id=1, source_target_pairs={{0,8},{8,16},{16,24},{24,0},{1,9},{9,17},{17,25},{25,1},{2,10},{10... | collective-permute-start | bytes 1032200 | tf_op jit(solution)/shard_map/ppermute | solution.py:28
  11.2 17.6 %collective-permute-start.2 = (bf16[64,4864]{1,0:T(8,128)(2,1)}, bf16[64,4864]{1,0:T(8,128)(2,1)S(1)}, u32[]{:S(2)}, u32[]{:S(2)}) collective-permute-start(bf16[64,4864]{1,0:T(8,128)(2,1)} %get-tuple-element.42), channel_id=1, source_target_pairs={{0,6},{2,0},{4,2},{6,4},{1,7},{3,1},{5,3},{7,5},{8,14},{10,8},{12,... | collective-permute-start | bytes 1867784 | tf_op jit(solution)/shard_map/ppermute | solution.py:28
  11.9 16.9 %collective-permute-start.3 = (bf16[64,4864]{1,0:T(8,128)(2,1)}, bf16[64,4864]{1,0:T(8,128)(2,1)S(1)}, u32[]{:S(2)}, u32[]{:S(2)}) collective-permute-start(bf16[64,4864]{1,0:T(8,128)(2,1)} %get-tuple-element.43), channel_id=1, source_target_pairs={{0,7},{1,6},{2,1},{3,0},{4,3},{5,2},{6,5},{7,4},{8,15},{9,14},{10,... | collective-permute-start | bytes 1867784 | tf_op jit(solution)/shard_map/ppermute | solution.py:452
  16.5 11.0 %collective-permute-start.1 = (bf16[112,1536]{1,0:T(8,128)(2,1)S(1)}, bf16[112,1536]{1,0:T(8,128)(2,1)S(1)}, u32[]{:S(2)}, u32[]{:S(2)}) collective-permute-start(bf16[112,1536]{1,0:T(8,128)(2,1)S(1)} %collective-permute-done.refs_8_.refs_3_), channel_id=1, source_target_pairs={{0,8},{8,16},{16,24},{24,0},{1,9},{9,17},{17,25},{25,1},{2,10},{10... | collective-permute-start | bytes 1032200 | tf_op jit(solution)/shard_map/ppermute | solution.py:28
  27.5 8.7 %collective-permute-start.5 = (bf16[112,1536]{1,0:T(8,128)(2,1)S(1)}, bf16[112,1536]{1,0:T(8,128)(2,1)S(1)}, u32[]{:S(2)}, u32[]{:S(2)}) collective-permute-start(bf16[112,1536]{1,0:T(8,128)(2,1)S(1)} %collective-permute-done.1.refs_12_.refs_7_), channel_id=1, source_target_pairs={{0,4},{2,6},{4,0},{6,2},{1,5},{3,7},{5,1},{7,3},{8,12},{10,14},{12... | collective-permute-start | bytes 1032200 | tf_op jit(solution)/shard_map/ppermute | solution.py:400
  28.8 16.0 %collective-permute-start.4 = (bf16[64,4864]{1,0:T(8,128)(2,1)}, bf16[64,4864]{1,0:T(8,128)(2,1)S(1)}, u32[]{:S(2)}, u32[]{:S(2)}) collective-permute-start(bf16[64,4864]{1,0:T(8,128)(2,1)} %get-tuple-element.44), channel_id=1, source_target_pairs={{0,1},{1,0},{2,3},{3,2},{4,5},{5,4},{6,7},{7,6},{8,9},{9,8},{10,11... | collective-permute-start | bytes 1867784 | tf_op jit(solution)/shard_map/ppermute | solution.py:28
  30.3 12.8 %collective-permute-start.12 = (bf16[112,1536]{1,0:T(8,128)(2,1)S(1)}, bf16[112,1536]{1,0:T(8,128)(2,1)S(1)}, u32[]{:S(2)}, u32[]{:S(2)}) collective-permute-start(bf16[112,1536]{1,0:T(8,128)(2,1)S(1)} %collective-permute-done.1.refs_12_.refs_7_), channel_id=1, source_target_pairs={{0,8},{8,16},{16,24},{24,0},{1,9},{9,17},{17,25},{25,1},{2,10},{10... | collective-permute-start | bytes 1032200 | tf_op jit(solution)/shard_map/ppermute | solution.py:28
  36.2 8.6 %collective-permute-start.6 = (bf16[112,1536]{1,0:T(8,128)(2,1)S(1)}, bf16[112,1536]{1,0:T(8,128)(2,1)S(1)}, u32[]{:S(2)}, u32[]{:S(2)}) collective-permute-start(bf16[112,1536]{1,0:T(8,128)(2,1)S(1)} %collective-permute-done.refs_8_.refs_3_), channel_id=1, source_target_pairs={{0,4},{2,6},{4,0},{6,2},{1,5},{3,7},{5,1},{7,3},{8,12},{10,14},{12... | collective-permute-start | bytes 1032200 | tf_op jit(solution)/shard_map/ppermute | solution.py:400
  37.3 11.7 %collective-permute-start.7 = (bf16[112,1536]{1,0:T(8,128)(2,1)S(1)}, bf16[112,1536]{1,0:T(8,128)(2,1)S(1)}, u32[]{:S(2)}, u32[]{:S(2)}) collective-permute-start(bf16[112,1536]{1,0:T(8,128)(2,1)S(1)} %collective-permute-done.5.refs_13_.refs_8_), channel_id=1, source_target_pairs={{0,8},{8,16},{16,24},{24,0},{1,9},{9,17},{17,25},{25,1},{2,10},{10... | collective-permute-start | bytes 1032200 | tf_op jit(solution)/shard_map/ppermute | solution.py:28
  38.0 11.6 %collective-permute-start.11 = (bf16[112,1536]{1,0:T(8,128)(2,1)S(1)}, bf16[112,1536]{1,0:T(8,128)(2,1)S(1)}, u32[]{:S(2)}, u32[]{:S(2)}) collective-permute-start(bf16[112,1536]{1,0:T(8,128)(2,1)S(1)} %collective-permute-done.5.refs_13_.refs_8_), channel_id=1, source_target_pairs={{0,2},{2,0},{4,6},{6,4},{1,3},{3,1},{5,7},{7,5},{8,10},{10,8},{12,... | collective-permute-start | bytes 1032200 | tf_op jit(solution)/shard_map/ppermute | solution.py:400
  43.1 10.9 %collective-permute-start.13 = (bf16[112,1536]{1,0:T(8,128)(2,1)S(1)}, bf16[112,1536]{1,0:T(8,128)(2,1)S(1)}, u32[]{:S(2)}, u32[]{:S(2)}) collective-permute-start(bf16[112,1536]{1,0:T(8,128)(2,1)S(1)} %collective-permute-done.12.refs_16_.refs_11_), channel_id=1, source_target_pairs={{0,2},{2,0},{4,6},{6,4},{1,3},{3,1},{5,7},{7,5},{8,10},{10,8},{12,... | collective-permute-start | bytes 1032200 | tf_op jit(solution)/shard_map/ppermute | solution.py:400
  49.0 5.0 %copy-start.4 = (bf16[384]{0:T(512)(128)(2,1)S(1)}, bf16[384]{0:T(512)(128)(2,1)}, u32[]{:S(2)}) copy-start(bf16[384]{0:T(512)(128)(2,1)} %refs_2_.1) | copy-start | bytes 2308
  49.0 5.0 %copy-start.5 = (f32[5]{0:T(128)S(1)}, f32[5]{0:T(128)}, u32[]{:S(2)}) copy-start(f32[5]{0:T(128)} %var_ref.1) | copy-start | bytes 64
  49.0 5.0 %copy-start = (bf16[384,1536]{1,0:T(8,128)(2,1)S(1)}, bf16[384,1536]{1,0:T(8,128)(2,1)}, u32[]{:S(2)}) copy-start(bf16[384,1536]{1,0:T(8,128)(2,1)} %refs_0_.1) | copy-start | bytes 3538948
  49.0 5.0 %collective-permute-start.8 = (bf16[112,1536]{1,0:T(8,128)(2,1)S(1)}, bf16[112,1536]{1,0:T(8,128)(2,1)S(1)}, u32[]{:S(2)}, u32[]{:S(2)}) collective-permute-start(bf16[112,1536]{1,0:T(8,128)(2,1)S(1)} %collective-permute-done.refs_8_.refs_3_), channel_id=1, source_target_pairs={{0,2},{2,0},{4,6},{6,4},{1,3},{3,1},{5,7},{7,5},{8,10},{10,8},{12,... | collective-permute-start | bytes 1032200 | tf_op jit(solution)/shard_map/ppermute | solution.py:400
  49.1 5.0 %collective-permute-start.9 = (bf16[112,1536]{1,0:T(8,128)(2,1)S(1)}, bf16[112,1536]{1,0:T(8,128)(2,1)S(1)}, u32[]{:S(2)}, u32[]{:S(2)}) collective-permute-start(bf16[112,1536]{1,0:T(8,128)(2,1)S(1)} %collective-permute-done.6.refs_9_.refs_4_), channel_id=1, source_target_pairs={{0,2},{2,0},{4,6},{6,4},{1,3},{3,1},{5,7},{7,5},{8,10},{10,8},{12,... | collective-permute-start | bytes 1032200 | tf_op jit(solution)/shard_map/ppermute | solution.py:400
  49.6 4.5 %collective-permute-start.10 = (bf16[112,1536]{1,0:T(8,128)(2,1)S(1)}, bf16[112,1536]{1,0:T(8,128)(2,1)S(1)}, u32[]{:S(2)}, u32[]{:S(2)}) collective-permute-start(bf16[112,1536]{1,0:T(8,128)(2,1)S(1)} %collective-permute-done.1.refs_12_.refs_7_), channel_id=1, source_target_pairs={{0,2},{2,0},{4,6},{6,4},{1,3},{3,1},{5,7},{7,5},{8,10},{10,8},{12,... | collective-permute-start | bytes 1032200 | tf_op jit(solution)/shard_map/ppermute | solution.py:400
  49.6 4.4 %collective-permute-start.14 = (bf16[112,1536]{1,0:T(8,128)(2,1)S(1)}, bf16[112,1536]{1,0:T(8,128)(2,1)S(1)}, u32[]{:S(2)}, u32[]{:S(2)}) collective-permute-start(bf16[112,1536]{1,0:T(8,128)(2,1)S(1)} %collective-permute-done.7.refs_17_.refs_12_), channel_id=1, source_target_pairs={{0,2},{2,0},{4,6},{6,4},{1,3},{3,1},{5,7},{7,5},{8,10},{10,8},{12,... | collective-permute-start | bytes 1032200 | tf_op jit(solution)/shard_map/ppermute | solution.py:400
  50.1 1.1 %copy-start.1 = (bf16[64,4864]{1,0:T(8,128)(2,1)S(1)}, bf16[64,4864]{1,0:T(8,128)(2,1)}, u32[]{:S(2)}) copy-start(bf16[64,4864]{1,0:T(8,128)(2,1)} %get-tuple-element.48.refs_0_.refs_1_) | copy-start | bytes 1867780
  51.1 2.9 %copy-start.2 = (bf16[64,4864]{1,0:T(8,128)(2,1)S(1)}, bf16[64,4864]{1,0:T(8,128)(2,1)}, u32[]{:S(2)}) copy-start(bf16[64,4864]{1,0:T(8,128)(2,1)} %get-tuple-element.48.refs_0_.refs_1_) | copy-start | bytes 1867780
  51.1 2.9 %copy-start.3 = (bf16[384,160]{0,1:T(8,128)(2,1)S(1)}, bf16[384,160]{0,1:T(8,128)(2,1)}, u32[]{:S(2)}) copy-start(bf16[384,160]{0,1:T(8,128)(2,1)} %param.12) | copy-start | bytes 368644
  51.1 2.9 %copy-start.6 = (f32[32]{0:T(128)S(1)}, f32[32]{0:T(128)}, u32[]{:S(2)}) copy-start(f32[32]{0:T(128)} %constant.2.clone.lat_ref) | copy-start | bytes 388
  57.8 5.6 %collective-permute-start.15 = (bf16[40,1664]{1,0:T(8,128)(2,1)S(1)}, bf16[40,1664]{1,0:T(8,128)(2,1)S(1)}, u32[]{:S(2)}, u32[]{:S(2)}) collective-permute-start(bf16[40,1664]{1,0:T(8,128)(2,1)S(1)} %get-tuple-element.59), channel_id=1, source_target_pairs={{0,2},{2,0},{4,6},{6,4},{1,3},{3,1},{5,7},{7,5},{8,10},{10,8},{12,... | collective-permute-start | bytes 399368 | tf_op jit(solution)/shard_map/ppermute | solution.py:400
  57.9 6.3 %collective-permute-start.16 = (bf16[40,1664]{1,0:T(8,128)(2,1)S(1)}, bf16[40,1664]{1,0:T(8,128)(2,1)S(1)}, u32[]{:S(2)}, u32[]{:S(2)}) collective-permute-start(bf16[40,1664]{1,0:T(8,128)(2,1)S(1)} %get-tuple-element.60), channel_id=1, source_target_pairs={{0,4},{2,6},{4,0},{6,2},{1,5},{3,7},{5,1},{7,3},{8,12},{10,14},{12... | collective-permute-start | bytes 399368 | tf_op jit(solution)/shard_map/ppermute | solution.py:400
  59.1 7.2 %collective-permute-start.17 = (bf16[40,1664]{1,0:T(8,128)(2,1)S(1)}, bf16[40,1664]{1,0:T(8,128)(2,1)S(1)}, u32[]{:S(2)}, u32[]{:S(2)}) collective-permute-start(bf16[40,1664]{1,0:T(8,128)(2,1)S(1)} %get-tuple-element.61), channel_id=1, source_target_pairs={{0,6},{2,4},{4,2},{6,0},{1,7},{3,5},{5,3},{7,1},{8,14},{10,12},{12... | collective-permute-start | bytes 399368 | tf_op jit(solution)/shard_map/ppermute | solution.py:400
  66.4 4.4 %collective-permute-start.18 = (bf16[40,384]{1,0:T(8,128)(2,1)S(1)}, bf16[40,384]{1,0:T(8,128)(2,1)S(1)}, u32[]{:S(2)}, u32[]{:S(2)}) collective-permute-start(bf16[40,384]{1,0:T(8,128)(2,1)S(1)} %get-tuple-element.72), channel_id=1, source_target_pairs={{0,8},{8,0},{16,24},{24,16},{1,9},{9,1},{17,25},{25,17},{2,10},{10... | collective-permute-start | bytes 92168 | tf_op jit(solution)/shard_map/ppermute | solution.py:400
  66.4 5.8 %collective-permute-start.19 = (bf16[40,384]{1,0:T(8,128)(2,1)S(1)}, bf16[40,384]{1,0:T(8,128)(2,1)S(1)}, u32[]{:S(2)}, u32[]{:S(2)}) collective-permute-start(bf16[40,384]{1,0:T(8,128)(2,1)S(1)} %get-tuple-element.73), channel_id=1, source_target_pairs={{0,16},{8,24},{16,0},{24,8},{1,17},{9,25},{17,1},{25,9},{2,18},{10... | collective-permute-start | bytes 92168 | tf_op jit(solution)/shard_map/ppermute | solution.py:400
  67.5 5.7 %collective-permute-start.20 = (bf16[40,384]{1,0:T(8,128)(2,1)S(1)}, bf16[40,384]{1,0:T(8,128)(2,1)S(1)}, u32[]{:S(2)}, u32[]{:S(2)}) collective-permute-start(bf16[40,384]{1,0:T(8,128)(2,1)S(1)} %get-tuple-element.74), channel_id=1, source_target_pairs={{0,24},{8,16},{16,8},{24,0},{1,25},{9,17},{17,9},{25,1},{2,26},{10... | collective-permute-start | bytes 92168 | tf_op jit(solution)/shard_map/ppermute | solution.py:400
  73.3 1.3 %collective-permute-start.21 = (bf16[48,384]{1,0:T(8,128)(2,1)S(1)}, bf16[48,384]{1,0:T(8,128)(2,1)S(1)}, u32[]{:S(2)}, u32[]{:S(2)}) collective-permute-start(bf16[48,384]{1,0:T(8,128)(2,1)S(1)} %dp_sum.1.mine_ref), channel_id=1, source_target_pairs={{0,2},{2,0},{4,6},{6,4},{1,3},{3,1},{5,7},{7,5},{8,10},{10,8},{12,... | collective-permute-start | bytes 110600 | tf_op jit(solution)/shard_map/ppermute | solution.py:400
  74.6 5.9 %collective-permute-start.24 = (bf16[96,384]{1,0:T(8,128)(2,1)S(1)}, bf16[96,384]{1,0:T(8,128)(2,1)S(1)}, u32[]{:S(2)}, u32[]{:S(2)}) collective-permute-start(bf16[96,384]{1,0:T(8,128)(2,1)S(1)} %pair.1.refs_0_), channel_id=1, source_target_pairs={{0,5},{1,4},{2,7},{3,6},{4,1},{5,0},{6,3},{7,2},{8,13},{9,12},{10,... | collective-permute-start | bytes 221192 | tf_op jit(solution)/shard_map/ppermute | solution.py:538
  75.7 5.6 %collective-permute-start.23 = (bf16[96,384]{1,0:T(8,128)(2,1)S(1)}, bf16[96,384]{1,0:T(8,128)(2,1)S(1)}, u32[]{:S(2)}, u32[]{:S(2)}) collective-permute-start(bf16[96,384]{1,0:T(8,128)(2,1)S(1)} %pair.1.refs_0_), channel_id=1, source_target_pairs={{0,4},{1,5},{2,6},{3,7},{4,0},{5,1},{6,2},{7,3},{8,12},{9,13},{10,... | collective-permute-start | bytes 221192 | tf_op jit(solution)/shard_map/ppermute | solution.py:538
  76.7 4.7 %collective-permute-start.22 = (bf16[96,384]{1,0:T(8,128)(2,1)S(1)}, bf16[96,384]{1,0:T(8,128)(2,1)S(1)}, u32[]{:S(2)}, u32[]{:S(2)}) collective-permute-start(bf16[96,384]{1,0:T(8,128)(2,1)S(1)} %pair.1.refs_0_), channel_id=1, source_target_pairs={{0,1},{1,0},{2,3},{3,2},{4,5},{5,4},{6,7},{7,6},{8,9},{9,8},{10,11... | collective-permute-start | bytes 221192 | tf_op jit(solution)/shard_map/ppermute | solution.py:538

commit v12 on v11

--- a/solution.py
+++ b/solution.py
@@ -133,8 +133,8 @@
     return lax.broadcasted_iota(jnp.int32, shape, dim)
 
 
-def payload_kernel(w_ref, unpatch_ref, gain_ref, payload_ref, ug, sems):
-    part = lax.axis_index("lat")
+def payload_kernel(bits, w_ref, unpatch_ref, gain_ref, payload_ref, ug, sems):
+    part = lax.axis_index("lat") ^ bits
     rows, width = w_ref.shape
     qr = rows // 4
     span = unpatch_ref.shape[0]
@@ -417,15 +417,20 @@
     barrier = lax.optimization_barrier
 
     unpatch_t = unpatch_matrix.T
-    payload = pl.pallas_call(
-        payload_kernel,
-        out_shape=shape((rows // 4 + 16, width), BF),
-        in_specs=[HBM, HBM, VMEM],
-        out_specs=VMEM,
-        scratch_shapes=[pltpu.VMEM((UGROWS, rows), BF), pltpu.SemaphoreType.DMA((2,))],
-        compiler_params=params(60),
-        name="payload",
-    )(w_out, unpatch_t, norm_gain)
+
+    def quarter_of(bits):
+        return pl.pallas_call(
+            functools.partial(payload_kernel, bits),
+            out_shape=shape((rows // 4 + 16, width), BF),
+            in_specs=[HBM, HBM, VMEM],
+            out_specs=VMEM,
+            scratch_shapes=[pltpu.VMEM((UGROWS, rows), BF), pltpu.SemaphoreType.DMA((2,))],
+            compiler_params=params(62),
+            name="payload",
+        )(w_out, unpatch_t, norm_gain)
+
+    payload = quarter_of(0)
+    second = quarter_of(2)
     ring1 = from_behind(payload, "dp", 1)
     own, *send = pl.pallas_call(
         pack_kernel,
@@ -443,23 +448,23 @@
     )(
         projected.reshape(levels, 8, 8, 3 * width),
         targets.reshape(levels, 8, 8, span),
-        valid_cells,
+        barrier((valid_cells, payload))[0],
     )
     corner = [
         (a * lon + b, ((a - 1) % lat) * lon + (b - 1) % lon) for a in range(lat) for b in range(lon)
     ]
     south = from_behind(send[1], "lat", -1)
     diag = lax.ppermute(send[2], ("lat", "lon"), corner)
-    ring2 = from_behind(ring1, "dp", 1)
+    ring1_after, second = barrier((ring1, second))
+    ring2 = from_behind(ring1_after, "dp", 1)
     across2 = swap(ring2, "lat", 2)
-    ring2_after, east, south, diag = barrier((ring2, send[0], south, diag))
-    ring3 = from_behind(ring2_after, "dp", 1)
+    ring2_late, east, south, diag = barrier((ring2, send[0], south, diag))
     east = from_behind(east, "lon", -1)
-    across3 = from_behind(across2, "dp", 1)
-    ring1_late, across2 = barrier((ring1, across2))
+    first, second, ring1_late, ring2 = barrier((payload, second, ring1, ring2_late))
+    back = from_behind(first, "dp", -1)
+    back_across = from_behind(second, "dp", -1)
     across1 = swap(ring1_late, "lat", 2)
-    tiles = [own, east, south, diag]
-    *tiles, ring1, across1, ring2, across3 = barrier((*tiles, ring1, across1, ring2, across3))
+    tiles = barrier((own, east, south, diag))
     ctx = pl.pallas_call(
         attention_kernel,
         out_shape=shape((tokens, width), BF),
@@ -468,8 +473,9 @@
         compiler_params=params(16),
         name="attention",
     )(*tiles)
+    across2, back_across, ctx = barrier((across2, back_across, ctx))
     pieces = []
-    for ring, across in ((ring1, across1), (ring2, across2), (ring3, across3)):
+    for ring, across in ((ring1, across1), (ring2, across2), (back, back_across)):
         pieces += [ring, across, swap(ring, "lat", 1), swap(across, "lat", 1)]
 
     piece = span // lat

time: 82.3 us -> 83.3 us (1.012)
  waiting for transfers between devices: 40.1 us -> 34 us
  starting transfers between devices: 21.6 us -> 25.7 us
  Pallas kernels: 18.5 us -> 22.5 us
  local copies, waits for them, and re-layouts: 1.1 us -> 0.04 us
    ppermute x6, waiting for transfers between devices: 24.7 us -> 17.3 us  [from_behind(): lax.ppermute(array, axis, [(i, (i + by) % length) for i in range(length)])]
    ppermute x6, starting transfers between devices: 6.3 us -> 10.2 us  [from_behind(): lax.ppermute(array, axis, [(i, (i + by) % length) for i in range(length)])]
    ppermute x1, waiting for transfers between devices: 0.01 us -> 2.91 us  [shards(): diag = lax.ppermute(send[2], ('lat', 'lon'), corner)]
    pallas_call x1 -> x2, Pallas kernels: 2.46 us -> 4.92 us  [quarter_of(): pl.pallas_call(functools.partial(payload_kernel, bits), out_shape=shape((...]
    ppermute x15, waiting for transfers between devices: 12.1 us -> 10.5 us  [swap(): lax.ppermute(array, axis, [(i, i ^ bit) for i in range(lax.axis_size(axis...]
    unnamed x14 -> x12, local copies, waits for them, and re-layouts: 1.1 us -> 0.04 us
    pallas_call x1, Pallas kernels: 3.61 us -> 4.61 us  [shards(): pl.pallas_call(backward_kernel, out_shape=shape((tokens, width), BF), in_...]
  transfers between devices with their start and end apart: 25 -> 25, of which waited for: 13 -> 18; matrix products, arithmetic and copies ran while one was open for 0% -> 0% of each run, Pallas kernels for 14% -> 18%
where the time goes in v12:
time: 83.3 us; the launch traced here: 83 us
  waiting for transfers between devices  34 us (41%)
  starting transfers between devices  25.7 us (31%)
  Pallas kernels  22.5 us (27%)
    ppermute x6, waiting for transfers between devices, from_behind(): lax.ppermute(array, axis, [(i, (i + by) % length) for i in range(length)])  17.3 us
    ppermute x15, waiting for transfers between devices, swap(): lax.ppermute(array, axis, [(i, i ^ bit) for i in range(lax.axis_size(axis...  10.5 us
    ppermute x6, starting transfers between devices, from_behind(): lax.ppermute(array, axis, [(i, (i + by) % length) for i in range(length)])  10.2 us
    ppermute x15, starting transfers between devices, swap(): lax.ppermute(array, axis, [(i, i ^ bit) for i in range(lax.axis_size(axis...  10.1 us
    pallas_call x1, Pallas kernels, shards(): pl.pallas_call(pack_kernel, out_shape=[shape((n, 3 * width + EXTRA), BF)...  5.01 us
    pallas_call x2, Pallas kernels, quarter_of(): pl.pallas_call(functools.partial(payload_kernel, bits), out_shape=shape((...  4.92 us
    pallas_call x1, Pallas kernels, shards(): pl.pallas_call(backward_kernel, out_shape=shape((tokens, width), BF), in_...  4.61 us
    pallas_call x1, Pallas kernels, shards(): pl.pallas_call(forward_kernel, grid=(1,), out_shape=[shape((piece, width...  4.18 us
  transfers between devices with their start and end apart: 25, of which 18 were waited for; matrix products, arithmetic and copies ran while one was open for 0% of the time, Pallas kernels for 18%

profile of v12, /device:TPU:0, one launch (start us, length us, event | category | flops | bytes accessed | tf_op | source)
XLA Modules:
  0.0 83.0 jit_solution(10751926108656213622)
XLA Ops:
  0.6 2.5 %payload.2 = bf16[112,1536]{1,0:T(8,128)(2,1)} custom-call(bf16[384,1536]{1,0:T(8,128)(2,1)} %refs_0_.1, bf16[160,384]{1,0:T(8,128)(2,1)} %bitcast.6, bf16[384]{0:T(512)(128)(2,1)} %refs_2_.1), custom_call_target="tpu_custom_call" | custom-call | tf_op jit(solution)/shard_map/payload/pallas_call | solution.py:422
  3.1 3.1 %collective-permute-start = (bf16[112,1536]{1,0:T(8,128)(2,1)}, bf16[112,1536]{1,0:T(8,128)(2,1)}, u32[]{:S(2)}, u32[]{:S(2)}) collective-permute-start(bf16[112,1536]{1,0:T(8,128)(2,1)} %payload.2), channel_id=1, source_target_pairs={{0,8},{8,16},{16,24},{24,0},{1,9},{9,17},{17,25},{25,1},{2,10},{10... | collective-permute-start | bytes 1032200 | tf_op jit(solution)/shard_map/ppermute | solution.py:28
  6.2 5.0 %pack.1 = (bf16[64,4864]{1,0:T(8,128)(2,1)}, bf16[64,4864]{1,0:T(8,128)(2,1)}, bf16[64,4864]{1,0:T(8,128)(2,1)}, bf16[64,4864]{1,0:T(8,128)(2,1)}) custom-call(bf16[4,8,8,4608]{3,2,1,0:T(8,128)(2,1)} %bitcast.10, bf16[4,8,8,160]{3,2,1,0:T(8,128)(2,1)} %bitcast.12, s32[8,8]{1,0:T(8,128)} %valid_ref), custom_call_target="tpu_custom_call" | custom-call | tf_op jit(solution)/shard_map/pack/pallas_call | solution.py:435
  11.2 0.0 copy-start.1
  11.2 0.7 collective-permute-start.3
  11.9 1.9 %collective-permute-start.4 = (bf16[64,4864]{1,0:T(8,128)(2,1)}, bf16[64,4864]{1,0:T(8,128)(2,1)S(1)}, u32[]{:S(2)}, u32[]{:S(2)}) collective-permute-start(bf16[64,4864]{1,0:T(8,128)(2,1)} %get-tuple-element.49), channel_id=1, source_target_pairs={{0,7},{1,6},{2,1},{3,0},{4,3},{5,2},{6,5},{7,4},{8,15},{9,14},{10,... | collective-permute-start | bytes 1867784 | tf_op jit(solution)/shard_map/ppermute | solution.py:457
  13.8 2.5 %payload.3 = bf16[112,1536]{1,0:T(8,128)(2,1)} custom-call(bf16[384,1536]{1,0:T(8,128)(2,1)} %refs_0_.1, bf16[160,384]{1,0:T(8,128)(2,1)} %bitcast.7, bf16[384]{0:T(512)(128)(2,1)} %refs_2_.1), custom_call_target="tpu_custom_call" | custom-call | tf_op jit(solution)/shard_map/payload/pallas_call | solution.py:422
  16.3 0.3 collective-permute-done.refs_8_.refs_3_
  16.6 1.4 %collective-permute-start.1 = (bf16[112,1536]{1,0:T(8,128)(2,1)}, bf16[112,1536]{1,0:T(8,128)(2,1)S(1)}, u32[]{:S(2)}, u32[]{:S(2)}) collective-permute-start(bf16[112,1536]{1,0:T(8,128)(2,1)} %collective-permute-done.refs_8_.refs_3_), channel_id=1, source_target_pairs={{0,8},{8,16},{16,24},{24,0},{1,9},{9,17},{17,25},{25,1},{2,10},{10... | collective-permute-start | bytes 1032200 | tf_op jit(solution)/shard_map/ppermute | solution.py:28
  17.9 6.8 %collective-permute-done.3.refs_2_.refs_3_ = bf16[64,4864]{1,0:T(8,128)(2,1)S(1)} collective-permute-done((bf16[64,4864]{1,0:T(8,128)(2,1)}, bf16[64,4864]{1,0:T(8,128)(2,1)S(1)}, u32[]{:S(2)}, u32[]{:S(2)}) %collective-permute-start.3) | collective-permute-done | bytes 622624 | tf_op jit(solution)/shard_map/ppermute | solution.py:28
  24.7 2.9 %collective-permute-done.4.refs_3_.refs_4_ = bf16[64,4864]{1,0:T(8,128)(2,1)S(1)} collective-permute-done((bf16[64,4864]{1,0:T(8,128)(2,1)}, bf16[64,4864]{1,0:T(8,128)(2,1)S(1)}, u32[]{:S(2)}, u32[]{:S(2)}) %collective-permute-start.4) | collective-permute-done | bytes 622624 | tf_op jit(solution)/shard_map/ppermute | solution.py:457
  27.6 0.5 collective-permute-done.1.refs_12_.refs_7_
  28.1 1.0 %collective-permute-start.6 = (bf16[64,4864]{1,0:T(8,128)(2,1)}, bf16[64,4864]{1,0:T(8,128)(2,1)S(1)}, u32[]{:S(2)}, u32[]{:S(2)}) collective-permute-start(bf16[64,4864]{1,0:T(8,128)(2,1)} %get-tuple-element.53), channel_id=1, source_target_pairs={{0,1},{1,0},{2,3},{3,2},{4,5},{5,4},{6,7},{7,6},{8,9},{9,8},{10,11... | collective-permute-start | bytes 1867784 | tf_op jit(solution)/shard_map/ppermute | solution.py:28
  29.1 1.5 %collective-permute-start.2 = (bf16[112,1536]{1,0:T(8,128)(2,1)S(1)}, bf16[112,1536]{1,0:T(8,128)(2,1)S(1)}, u32[]{:S(2)}, u32[]{:S(2)}) collective-permute-start(bf16[112,1536]{1,0:T(8,128)(2,1)S(1)} %collective-permute-done.1.refs_12_.refs_7_), channel_id=1, source_target_pairs={{0,4},{2,6},{4,0},{6,2},{1,5},{3,7},{5,1},{7,3},{8,12},{10,14},{12... | collective-permute-start | bytes 1032200 | tf_op jit(solution)/shard_map/ppermute | solution.py:400
  30.6 0.5 collective-permute-start.7
  31.1 2.4 %collective-permute-start.12 = (bf16[112,1536]{1,0:T(8,128)(2,1)}, bf16[112,1536]{1,0:T(8,128)(2,1)S(1)}, u32[]{:S(2)}, u32[]{:S(2)}) collective-permute-start(bf16[112,1536]{1,0:T(8,128)(2,1)} %payload.2), channel_id=1, source_target_pairs={{0,24},{8,0},{16,8},{24,16},{1,25},{9,1},{17,9},{25,17},{2,26},{10... | collective-permute-start | bytes 1032200 | tf_op jit(solution)/shard_map/ppermute | solution.py:28
  33.5 1.6 %collective-permute-start.5 = (bf16[112,1536]{1,0:T(8,128)(2,1)}, bf16[112,1536]{1,0:T(8,128)(2,1)S(1)}, u32[]{:S(2)}, u32[]{:S(2)}) collective-permute-start(bf16[112,1536]{1,0:T(8,128)(2,1)} %payload.3), channel_id=1, source_target_pairs={{0,24},{8,0},{16,8},{24,16},{1,25},{9,1},{17,9},{25,17},{2,26},{10... | collective-permute-start | bytes 1032200 | tf_op jit(solution)/shard_map/ppermute | solution.py:28
  35.1 9.7 %collective-permute-done.6.refs_1_.refs_2_ = bf16[64,4864]{1,0:T(8,128)(2,1)S(1)} collective-permute-done((bf16[64,4864]{1,0:T(8,128)(2,1)}, bf16[64,4864]{1,0:T(8,128)(2,1)S(1)}, u32[]{:S(2)}, u32[]{:S(2)}) %collective-permute-start.6) | collective-permute-done | bytes 622624 | tf_op jit(solution)/shard_map/ppermute | solution.py:28
  44.8 0.0 collective-permute-start.8
  44.8 0.0 copy-done.1
  44.8 0.0 copy-start.2
  44.8 0.0 copy-start.3
  44.8 0.0 copy-start.4
  44.8 0.0 copy-start.5
  44.9 2.8 %attention.1.refs_0_ = bf16[256,1536]{1,0:T(8,128)(2,1)S(1)} custom-call(bf16[64,4864]{1,0:T(8,128)(2,1)S(1)} %copy-done.1, bf16[64,4864]{1,0:T(8,128)(2,1)S(1)} %collective-permute-done.6.refs_1_.refs_2_, bf16[64,4864]{1,0:T(8,128)(2,1)S(1)} %collective-permute-done.3.refs_2_.refs_3_, bf16[64,4864]{1,0:T(8,128)(2,1)S(1)} %collective-permute-done.4.refs_3_.refs_4_), custom_call_target="tpu_custom_call" | custom-call | tf_op jit(solution)/shard_map/attention/pallas_call | solution.py:468
  47.7 0.0 collective-permute-done.2.refs_13_.refs_8_
  47.7 0.6 collective-permute-start.10
  48.3 0.0 collective-permute-done.7.refs_9_.refs_4_
  48.3 0.1 collective-permute-start.9
  48.3 0.0 collective-permute-done.12.refs_16_.refs_11_
  48.4 0.4 collective-permute-start.13
  48.8 0.1 collective-permute-done.5.refs_17_.refs_12_
  48.9 0.0 collective-permute-start.11
  48.9 0.0 collective-permute-done.8.refs_10_.refs_5_
  48.9 0.5 collective-permute-start.14
  49.4 0.1 collective-permute-done.10.refs_14_.refs_9_
  49.5 0.5 collective-permute-done.9.refs_11_.refs_6_
  50.0 0.5 collective-permute-done.13.refs_18_.refs_13_
  50.5 0.5 collective-permute-done.11.refs_15_.refs_10_
  51.0 0.5 collective-permute-done.14.refs_19_.refs_14_
  51.5 4.2 %forward.1 = (bf16[40,1664]{1,0:T(8,128)(2,1)S(1)}, bf16[40,1664]{1,0:T(8,128)(2,1)S(1)}, bf16[40,1664]{1,0:T(8,128)(2,1)S(1)}, bf16[40,1664]{1,0:T(8,128)(2,1)S...) custom-call(f32[32]{0:T(128)S(1)} %copy-done.5, f32[5]{0:T(128)S(1)} %copy-done.4, ...), custom_call_target="tpu_custom_call" | custom-call | tf_op jit(solution)/shard_map/forward/pallas_call | solution.py:489
  55.7 0.4 collective-permute-start.15
  56.2 1.1 %collective-permute-start.16 = (bf16[40,1664]{1,0:T(8,128)(2,1)S(1)}, bf16[40,1664]{1,0:T(8,128)(2,1)S(1)}, u32[]{:S(2)}, u32[]{:S(2)}) collective-permute-start(bf16[40,1664]{1,0:T(8,128)(2,1)S(1)} %get-tuple-element.68), channel_id=1, source_target_pairs={{0,4},{2,6},{4,0},{6,2},{1,5},{3,7},{5,1},{7,3},{8,12},{10,14},{12... | collective-permute-start | bytes 399368 | tf_op jit(solution)/shard_map/ppermute | solution.py:400
  57.3 0.4 collective-permute-start.17
  57.6 4.6 %backward.1 = bf16[256,1536]{1,0:T(8,128)(2,1)} custom-call(f32[256,1536]{1,0:T(8,128)S(1)} %get-tuple-element.70.normed_ref, f32[256,128]{1,0:T(8,128)S(1)} %get-tuple-element.71.inv_ref, bf16[256,160]{1,0:T(8,128)(2,1)S(1)} %get-tuple-element.72.dfc_ref, bf16[384,1536]{1,0:T(8,128)(2,1)S(1)} %copy-done, bf16[160,384]{1,0:T(8,128)(2,1)S(1)} %bitcast.9, ...), custom_call_target="tpu_custom_call" | custom-call | tf_op jit(solution)/shard_map/backward/pallas_call | solution.py:504
  62.3 0.0 collective-permute-done.15.b
  62.3 0.3 collective-permute-done.16.c
  62.6 1.2 %collective-permute-done.17.d = bf16[40,1664]{1,0:T(8,128)(2,1)S(1)} collective-permute-done((bf16[40,1664]{1,0:T(8,128)(2,1)S(1)}, bf16[40,1664]{1,0:T(8,128)(2,1)S(1)}, u32[]{:S(2)}, u32[]{:S(2)}) %collective-permute-start.17) | collective-permute-done | bytes 133152 | tf_op jit(solution)/shard_map/ppermute | solution.py:400
  63.8 0.2 lat_sum.1
  63.9 1.6 %collective-permute-start.18 = (bf16[40,384]{1,0:T(8,128)(2,1)S(1)}, bf16[40,384]{1,0:T(8,128)(2,1)S(1)}, u32[]{:S(2)}, u32[]{:S(2)}) collective-permute-start(bf16[40,384]{1,0:T(8,128)(2,1)S(1)} %get-tuple-element.80), channel_id=1, source_target_pairs={{0,8},{8,0},{16,24},{24,16},{1,9},{9,1},{17,25},{25,17},{2,10},{10... | collective-permute-start | bytes 92168 | tf_op jit(solution)/shard_map/ppermute | solution.py:400
  65.5 2.9 %collective-permute-start.19 = (bf16[40,384]{1,0:T(8,128)(2,1)S(1)}, bf16[40,384]{1,0:T(8,128)(2,1)S(1)}, u32[]{:S(2)}, u32[]{:S(2)}) collective-permute-start(bf16[40,384]{1,0:T(8,128)(2,1)S(1)} %get-tuple-element.81), channel_id=1, source_target_pairs={{0,16},{8,24},{16,0},{24,8},{1,17},{9,25},{17,1},{25,9},{2,18},{10... | collective-permute-start | bytes 92168 | tf_op jit(solution)/shard_map/ppermute | solution.py:400
  68.4 0.0 collective-permute-start.20
  68.4 0.0 collective-permute-done.18.b
  68.4 2.4 %collective-permute-done.19.c = bf16[40,384]{1,0:T(8,128)(2,1)S(1)} collective-permute-done((bf16[40,384]{1,0:T(8,128)(2,1)S(1)}, bf16[40,384]{1,0:T(8,128)(2,1)S(1)}, u32[]{:S(2)}, u32[]{:S(2)}) %collective-permute-start.19) | collective-permute-done | bytes 30752 | tf_op jit(solution)/shard_map/ppermute | solution.py:400
  70.8 3.3 %collective-permute-done.20.d = bf16[40,384]{1,0:T(8,128)(2,1)S(1)} collective-permute-done((bf16[40,384]{1,0:T(8,128)(2,1)S(1)}, bf16[40,384]{1,0:T(8,128)(2,1)S(1)}, u32[]{:S(2)}, u32[]{:S(2)}) %collective-permute-start.20) | collective-permute-done | bytes 30752 | tf_op jit(solution)/shard_map/ppermute | solution.py:400
  74.1 0.1 collective-permute-start.21
  74.2 1.2 %collective-permute-done.21.other_ref = bf16[48,384]{1,0:T(8,128)(2,1)S(1)} collective-permute-done((bf16[48,384]{1,0:T(8,128)(2,1)S(1)}, bf16[48,384]{1,0:T(8,128)(2,1)S(1)}, u32[]{:S(2)}, u32[]{:S(2)}) %collective-permute-start.21) | collective-permute-done | bytes 36896 | tf_op jit(solution)/shard_map/ppermute | solution.py:400
  75.4 1.2 %collective-permute-start.24 = (bf16[96,384]{1,0:T(8,128)(2,1)S(1)}, bf16[96,384]{1,0:T(8,128)(2,1)S(1)}, u32[]{:S(2)}, u32[]{:S(2)}) collective-permute-start(bf16[96,384]{1,0:T(8,128)(2,1)S(1)} %pair.1.refs_0_), channel_id=1, source_target_pairs={{0,5},{1,4},{2,7},{3,6},{4,1},{5,0},{6,3},{7,2},{8,13},{9,12},{10,... | collective-permute-start | bytes 221192 | tf_op jit(solution)/shard_map/ppermute | solution.py:544
  76.7 0.8 collective-permute-start.23
  77.5 1.5 %collective-permute-start.22 = (bf16[96,384]{1,0:T(8,128)(2,1)S(1)}, bf16[96,384]{1,0:T(8,128)(2,1)S(1)}, u32[]{:S(2)}, u32[]{:S(2)}) collective-permute-start(bf16[96,384]{1,0:T(8,128)(2,1)S(1)} %pair.1.refs_0_), channel_id=1, source_target_pairs={{0,1},{1,0},{2,3},{3,2},{4,5},{5,4},{6,7},{7,6},{8,9},{9,8},{10,11... | collective-permute-start | bytes 221192 | tf_op jit(solution)/shard_map/ppermute | solution.py:544
  79.0 2.3 %collective-permute-done.24.refs_3_ = bf16[96,384]{1,0:T(8,128)(2,1)S(1)} collective-permute-done((bf16[96,384]{1,0:T(8,128)(2,1)S(1)}, bf16[96,384]{1,0:T(8,128)(2,1)S(1)}, u32[]{:S(2)}, u32[]{:S(2)}) %collective-permute-start.24) | collective-permute-done | bytes 73760 | tf_op jit(solution)/shard_map/ppermute | solution.py:544
  81.3 1.0 %collective-permute-done.23.refs_2_ = bf16[96,384]{1,0:T(8,128)(2,1)S(1)} collective-permute-done((bf16[96,384]{1,0:T(8,128)(2,1)S(1)}, bf16[96,384]{1,0:T(8,128)(2,1)S(1)}, u32[]{:S(2)}, u32[]{:S(2)}) %collective-permute-start.23) | collective-permute-done | bytes 73760 | tf_op jit(solution)/shard_map/ppermute | solution.py:544
  82.3 0.0 collective-permute-done.22.refs_1_
  82.3 0.7 join.1
  (8 shorter events, 0.1 us)
Async XLA Ops:
  3.1 13.5 %collective-permute-start = (bf16[112,1536]{1,0:T(8,128)(2,1)}, bf16[112,1536]{1,0:T(8,128)(2,1)}, u32[]{:S(2)}, u32[]{:S(2)}) collective-permute-start(bf16[112,1536]{1,0:T(8,128)(2,1)} %payload.2), channel_id=1, source_target_pairs={{0,8},{8,16},{16,24},{24,0},{1,9},{9,17},{17,25},{25,1},{2,10},{10... | collective-permute-start | bytes 1032200 | tf_op jit(solution)/shard_map/ppermute | solution.py:28
  11.2 33.6 %copy-start.1 = (bf16[64,4864]{1,0:T(8,128)(2,1)S(1)}, bf16[64,4864]{1,0:T(8,128)(2,1)}, u32[]{:S(2)}) copy-start(bf16[64,4864]{1,0:T(8,128)(2,1)} %get-tuple-element.56.refs_0_.refs_1_) | copy-start | bytes 1867780
  11.2 13.5 %collective-permute-start.3 = (bf16[64,4864]{1,0:T(8,128)(2,1)}, bf16[64,4864]{1,0:T(8,128)(2,1)S(1)}, u32[]{:S(2)}, u32[]{:S(2)}) collective-permute-start(bf16[64,4864]{1,0:T(8,128)(2,1)} %get-tuple-element.48), channel_id=1, source_target_pairs={{0,6},{2,0},{4,2},{6,4},{1,7},{3,1},{5,3},{7,5},{8,14},{10,8},{12,... | collective-permute-start | bytes 1867784 | tf_op jit(solution)/shard_map/ppermute | solution.py:28
  11.9 15.7 %collective-permute-start.4 = (bf16[64,4864]{1,0:T(8,128)(2,1)}, bf16[64,4864]{1,0:T(8,128)(2,1)S(1)}, u32[]{:S(2)}, u32[]{:S(2)}) collective-permute-start(bf16[64,4864]{1,0:T(8,128)(2,1)} %get-tuple-element.49), channel_id=1, source_target_pairs={{0,7},{1,6},{2,1},{3,0},{4,3},{5,2},{6,5},{7,4},{8,15},{9,14},{10,... | collective-permute-start | bytes 1867784 | tf_op jit(solution)/shard_map/ppermute | solution.py:457
  16.6 11.5 %collective-permute-start.1 = (bf16[112,1536]{1,0:T(8,128)(2,1)}, bf16[112,1536]{1,0:T(8,128)(2,1)S(1)}, u32[]{:S(2)}, u32[]{:S(2)}) collective-permute-start(bf16[112,1536]{1,0:T(8,128)(2,1)} %collective-permute-done.refs_8_.refs_3_), channel_id=1, source_target_pairs={{0,8},{8,16},{16,24},{24,0},{1,9},{9,17},{17,25},{25,1},{2,10},{10... | collective-permute-start | bytes 1032200 | tf_op jit(solution)/shard_map/ppermute | solution.py:28
  28.1 16.7 %collective-permute-start.6 = (bf16[64,4864]{1,0:T(8,128)(2,1)}, bf16[64,4864]{1,0:T(8,128)(2,1)S(1)}, u32[]{:S(2)}, u32[]{:S(2)}) collective-permute-start(bf16[64,4864]{1,0:T(8,128)(2,1)} %get-tuple-element.53), channel_id=1, source_target_pairs={{0,1},{1,0},{2,3},{3,2},{4,5},{5,4},{6,7},{7,6},{8,9},{9,8},{10,11... | collective-permute-start | bytes 1867784 | tf_op jit(solution)/shard_map/ppermute | solution.py:28
  29.1 18.6 %collective-permute-start.2 = (bf16[112,1536]{1,0:T(8,128)(2,1)S(1)}, bf16[112,1536]{1,0:T(8,128)(2,1)S(1)}, u32[]{:S(2)}, u32[]{:S(2)}) collective-permute-start(bf16[112,1536]{1,0:T(8,128)(2,1)S(1)} %collective-permute-done.1.refs_12_.refs_7_), channel_id=1, source_target_pairs={{0,4},{2,6},{4,0},{6,2},{1,5},{3,7},{5,1},{7,3},{8,12},{10,14},{12... | collective-permute-start | bytes 1032200 | tf_op jit(solution)/shard_map/ppermute | solution.py:400
  30.6 17.6 %collective-permute-start.7 = (bf16[112,1536]{1,0:T(8,128)(2,1)}, bf16[112,1536]{1,0:T(8,128)(2,1)S(1)}, u32[]{:S(2)}, u32[]{:S(2)}) collective-permute-start(bf16[112,1536]{1,0:T(8,128)(2,1)} %collective-permute-done.refs_8_.refs_3_), channel_id=1, source_target_pairs={{0,4},{2,6},{4,0},{6,2},{1,5},{3,7},{5,1},{7,3},{8,12},{10,14},{12... | collective-permute-start | bytes 1032200 | tf_op jit(solution)/shard_map/ppermute | solution.py:400
  31.1 17.2 %collective-permute-start.12 = (bf16[112,1536]{1,0:T(8,128)(2,1)}, bf16[112,1536]{1,0:T(8,128)(2,1)S(1)}, u32[]{:S(2)}, u32[]{:S(2)}) collective-permute-start(bf16[112,1536]{1,0:T(8,128)(2,1)} %payload.2), channel_id=1, source_target_pairs={{0,24},{8,0},{16,8},{24,16},{1,25},{9,1},{17,9},{25,17},{2,26},{10... | collective-permute-start | bytes 1032200 | tf_op jit(solution)/shard_map/ppermute | solution.py:28
  33.5 15.4 %collective-permute-start.5 = (bf16[112,1536]{1,0:T(8,128)(2,1)}, bf16[112,1536]{1,0:T(8,128)(2,1)S(1)}, u32[]{:S(2)}, u32[]{:S(2)}) collective-permute-start(bf16[112,1536]{1,0:T(8,128)(2,1)} %payload.3), channel_id=1, source_target_pairs={{0,24},{8,0},{16,8},{24,16},{1,25},{9,1},{17,9},{25,17},{2,26},{10... | collective-permute-start | bytes 1032200 | tf_op jit(solution)/shard_map/ppermute | solution.py:28
  44.8 4.1 %collective-permute-start.8 = (bf16[112,1536]{1,0:T(8,128)(2,1)}, bf16[112,1536]{1,0:T(8,128)(2,1)S(1)}, u32[]{:S(2)}, u32[]{:S(2)}) collective-permute-start(bf16[112,1536]{1,0:T(8,128)(2,1)} %collective-permute-done.refs_8_.refs_3_), channel_id=1, source_target_pairs={{0,2},{2,0},{4,6},{6,4},{1,3},{3,1},{5,7},{7,5},{8,10},{10,8},{12,... | collective-permute-start | bytes 1032200 | tf_op jit(solution)/shard_map/ppermute | solution.py:400
  44.8 6.7 %copy-start = (bf16[384,1536]{1,0:T(8,128)(2,1)S(1)}, bf16[384,1536]{1,0:T(8,128)(2,1)}, u32[]{:S(2)}) copy-start(bf16[384,1536]{1,0:T(8,128)(2,1)} %refs_0_.1) | copy-start | bytes 3538948
  44.8 6.7 %copy-start.2 = (bf16[384,160]{0,1:T(8,128)(2,1)S(1)}, bf16[384,160]{0,1:T(8,128)(2,1)}, u32[]{:S(2)}) copy-start(bf16[384,160]{0,1:T(8,128)(2,1)} %param.12) | copy-start | bytes 368644
  44.8 6.7 %copy-start.3 = (bf16[384]{0:T(512)(128)(2,1)S(1)}, bf16[384]{0:T(512)(128)(2,1)}, u32[]{:S(2)}) copy-start(bf16[384]{0:T(512)(128)(2,1)} %refs_2_.1) | copy-start | bytes 2308
  44.8 6.7 %copy-start.4 = (f32[5]{0:T(128)S(1)}, f32[5]{0:T(128)}, u32[]{:S(2)}) copy-start(f32[5]{0:T(128)} %var_ref.1) | copy-start | bytes 64
  44.8 6.7 %copy-start.5 = (f32[32]{0:T(128)S(1)}, f32[32]{0:T(128)}, u32[]{:S(2)}) copy-start(f32[32]{0:T(128)} %constant.2.clone.lat_ref) | copy-start | bytes 388
  47.7 1.8 %collective-permute-start.10 = (bf16[112,1536]{1,0:T(8,128)(2,1)S(1)}, bf16[112,1536]{1,0:T(8,128)(2,1)S(1)}, u32[]{:S(2)}, u32[]{:S(2)}) collective-permute-start(bf16[112,1536]{1,0:T(8,128)(2,1)S(1)} %collective-permute-done.1.refs_12_.refs_7_), channel_id=1, source_target_pairs={{0,2},{2,0},{4,6},{6,4},{1,3},{3,1},{5,7},{7,5},{8,10},{10,8},{12,... | collective-permute-start | bytes 1032200 | tf_op jit(solution)/shard_map/ppermute | solution.py:400
  48.3 1.8 %collective-permute-start.9 = (bf16[112,1536]{1,0:T(8,128)(2,1)S(1)}, bf16[112,1536]{1,0:T(8,128)(2,1)S(1)}, u32[]{:S(2)}, u32[]{:S(2)}) collective-permute-start(bf16[112,1536]{1,0:T(8,128)(2,1)S(1)} %collective-permute-done.7.refs_9_.refs_4_), channel_id=1, source_target_pairs={{0,2},{2,0},{4,6},{6,4},{1,3},{3,1},{5,7},{7,5},{8,10},{10,8},{12,... | collective-permute-start | bytes 1032200 | tf_op jit(solution)/shard_map/ppermute | solution.py:400
  48.4 2.2 %collective-permute-start.13 = (bf16[112,1536]{1,0:T(8,128)(2,1)S(1)}, bf16[112,1536]{1,0:T(8,128)(2,1)S(1)}, u32[]{:S(2)}, u32[]{:S(2)}) collective-permute-start(bf16[112,1536]{1,0:T(8,128)(2,1)S(1)} %collective-permute-done.12.refs_16_.refs_11_), channel_id=1, source_target_pairs={{0,2},{2,0},{4,6},{6,4},{1,3},{3,1},{5,7},{7,5},{8,10},{10,8},{12,... | collective-permute-start | bytes 1032200 | tf_op jit(solution)/shard_map/ppermute | solution.py:400
  48.9 2.1 %collective-permute-start.11 = (bf16[112,1536]{1,0:T(8,128)(2,1)S(1)}, bf16[112,1536]{1,0:T(8,128)(2,1)S(1)}, u32[]{:S(2)}, u32[]{:S(2)}) collective-permute-start(bf16[112,1536]{1,0:T(8,128)(2,1)S(1)} %collective-permute-done.2.refs_13_.refs_8_), channel_id=1, source_target_pairs={{0,2},{2,0},{4,6},{6,4},{1,3},{3,1},{5,7},{7,5},{8,10},{10,8},{12,... | collective-permute-start | bytes 1032200 | tf_op jit(solution)/shard_map/ppermute | solution.py:400
  48.9 2.6 %collective-permute-start.14 = (bf16[112,1536]{1,0:T(8,128)(2,1)S(1)}, bf16[112,1536]{1,0:T(8,128)(2,1)S(1)}, u32[]{:S(2)}, u32[]{:S(2)}) collective-permute-start(bf16[112,1536]{1,0:T(8,128)(2,1)S(1)} %collective-permute-done.5.refs_17_.refs_12_), channel_id=1, source_target_pairs={{0,2},{2,0},{4,6},{6,4},{1,3},{3,1},{5,7},{7,5},{8,10},{10,8},{12,... | collective-permute-start | bytes 1032200 | tf_op jit(solution)/shard_map/ppermute | solution.py:400
  55.7 6.5 %collective-permute-start.15 = (bf16[40,1664]{1,0:T(8,128)(2,1)S(1)}, bf16[40,1664]{1,0:T(8,128)(2,1)S(1)}, u32[]{:S(2)}, u32[]{:S(2)}) collective-permute-start(bf16[40,1664]{1,0:T(8,128)(2,1)S(1)} %get-tuple-element.67), channel_id=1, source_target_pairs={{0,2},{2,0},{4,6},{6,4},{1,3},{3,1},{5,7},{7,5},{8,10},{10,8},{12,... | collective-permute-start | bytes 399368 | tf_op jit(solution)/shard_map/ppermute | solution.py:400
  56.2 6.4 %collective-permute-start.16 = (bf16[40,1664]{1,0:T(8,128)(2,1)S(1)}, bf16[40,1664]{1,0:T(8,128)(2,1)S(1)}, u32[]{:S(2)}, u32[]{:S(2)}) collective-permute-start(bf16[40,1664]{1,0:T(8,128)(2,1)S(1)} %get-tuple-element.68), channel_id=1, source_target_pairs={{0,4},{2,6},{4,0},{6,2},{1,5},{3,7},{5,1},{7,3},{8,12},{10,14},{12... | collective-permute-start | bytes 399368 | tf_op jit(solution)/shard_map/ppermute | solution.py:400
  57.3 6.5 %collective-permute-start.17 = (bf16[40,1664]{1,0:T(8,128)(2,1)S(1)}, bf16[40,1664]{1,0:T(8,128)(2,1)S(1)}, u32[]{:S(2)}, u32[]{:S(2)}) collective-permute-start(bf16[40,1664]{1,0:T(8,128)(2,1)S(1)} %get-tuple-element.69), channel_id=1, source_target_pairs={{0,6},{2,4},{4,2},{6,0},{1,7},{3,5},{5,3},{7,1},{8,14},{10,12},{12... | collective-permute-start | bytes 399368 | tf_op jit(solution)/shard_map/ppermute | solution.py:400
  63.9 4.5 %collective-permute-start.18 = (bf16[40,384]{1,0:T(8,128)(2,1)S(1)}, bf16[40,384]{1,0:T(8,128)(2,1)S(1)}, u32[]{:S(2)}, u32[]{:S(2)}) collective-permute-start(bf16[40,384]{1,0:T(8,128)(2,1)S(1)} %get-tuple-element.80), channel_id=1, source_target_pairs={{0,8},{8,0},{16,24},{24,16},{1,9},{9,1},{17,25},{25,17},{2,10},{10... | collective-permute-start | bytes 92168 | tf_op jit(solution)/shard_map/ppermute | solution.py:400
  65.5 5.3 %collective-permute-start.19 = (bf16[40,384]{1,0:T(8,128)(2,1)S(1)}, bf16[40,384]{1,0:T(8,128)(2,1)S(1)}, u32[]{:S(2)}, u32[]{:S(2)}) collective-permute-start(bf16[40,384]{1,0:T(8,128)(2,1)S(1)} %get-tuple-element.81), channel_id=1, source_target_pairs={{0,16},{8,24},{16,0},{24,8},{1,17},{9,25},{17,1},{25,9},{2,18},{10... | collective-permute-start | bytes 92168 | tf_op jit(solution)/shard_map/ppermute | solution.py:400
  68.4 5.7 %collective-permute-start.20 = (bf16[40,384]{1,0:T(8,128)(2,1)S(1)}, bf16[40,384]{1,0:T(8,128)(2,1)S(1)}, u32[]{:S(2)}, u32[]{:S(2)}) collective-permute-start(bf16[40,384]{1,0:T(8,128)(2,1)S(1)} %get-tuple-element.82), channel_id=1, source_target_pairs={{0,24},{8,16},{16,8},{24,0},{1,25},{9,17},{17,9},{25,1},{2,26},{10... | collective-permute-start | bytes 92168 | tf_op jit(solution)/shard_map/ppermute | solution.py:400
  74.1 1.3 %collective-permute-start.21 = (bf16[48,384]{1,0:T(8,128)(2,1)S(1)}, bf16[48,384]{1,0:T(8,128)(2,1)S(1)}, u32[]{:S(2)}, u32[]{:S(2)}) collective-permute-start(bf16[48,384]{1,0:T(8,128)(2,1)S(1)} %dp_sum.1.mine_ref), channel_id=1, source_target_pairs={{0,2},{2,0},{4,6},{6,4},{1,3},{3,1},{5,7},{7,5},{8,10},{10,8},{12,... | collective-permute-start | bytes 110600 | tf_op jit(solution)/shard_map/ppermute | solution.py:400
  75.4 5.8 %collective-permute-start.24 = (bf16[96,384]{1,0:T(8,128)(2,1)S(1)}, bf16[96,384]{1,0:T(8,128)(2,1)S(1)}, u32[]{:S(2)}, u32[]{:S(2)}) collective-permute-start(bf16[96,384]{1,0:T(8,128)(2,1)S(1)} %pair.1.refs_0_), channel_id=1, source_target_pairs={{0,5},{1,4},{2,7},{3,6},{4,1},{5,0},{6,3},{7,2},{8,13},{9,12},{10,... | collective-permute-start | bytes 221192 | tf_op jit(solution)/shard_map/ppermute | solution.py:544
  76.7 5.6 %collective-permute-start.23 = (bf16[96,384]{1,0:T(8,128)(2,1)S(1)}, bf16[96,384]{1,0:T(8,128)(2,1)S(1)}, u32[]{:S(2)}, u32[]{:S(2)}) collective-permute-start(bf16[96,384]{1,0:T(8,128)(2,1)S(1)} %pair.1.refs_0_), channel_id=1, source_target_pairs={{0,4},{1,5},{2,6},{3,7},{4,0},{5,1},{6,2},{7,3},{8,12},{9,13},{10,... | collective-permute-start | bytes 221192 | tf_op jit(solution)/shard_map/ppermute | solution.py:544
  77.5 4.8 %collective-permute-start.22 = (bf16[96,384]{1,0:T(8,128)(2,1)S(1)}, bf16[96,384]{1,0:T(8,128)(2,1)S(1)}, u32[]{:S(2)}, u32[]{:S(2)}) collective-permute-start(bf16[96,384]{1,0:T(8,128)(2,1)S(1)} %pair.1.refs_0_), channel_id=1, source_target_pairs={{0,1},{1,0},{2,3},{3,2},{4,5},{5,4},{6,7},{7,6},{8,9},{9,8},{10,11... | collective-permute-start | bytes 221192 | tf_op jit(solution)/shard_map/ppermute | solution.py:544

commit v13 on v11

--- a/solution.py
+++ b/solution.py
@@ -438,7 +438,7 @@
             pltpu.VMEM((8, 8), jnp.int32),
             pltpu.SemaphoreType.DMA((2 + 3 * width // 512,)),
         ],
-        compiler_params=params(62),
+        compiler_params=params(50),
         name="pack",
     )(
         projected.reshape(levels, 8, 8, 3 * width),
@@ -459,7 +459,7 @@
     ring1_late, across2 = barrier((ring1, across2))
     across1 = swap(ring1_late, "lat", 2)
     tiles = [own, east, south, diag]
-    *tiles, ring1, across1, ring2, across3 = barrier((*tiles, ring1, across1, ring2, across3))
+    *tiles, ring1, across1, ring2 = barrier((*tiles, ring1, across1, ring2))
     ctx = pl.pallas_call(
         attention_kernel,
         out_shape=shape((tokens, width), BF),
@@ -468,6 +468,7 @@
         compiler_params=params(16),
         name="attention",
     )(*tiles)
+    ctx, across3 = barrier((ctx, across3))
     pieces = []
     for ring, across in ((ring1, across1), (ring2, across2), (ring3, across3)):
         pieces += [ring, across, swap(ring, "lat", 1), swap(across, "lat", 1)]

time: 82.3 us -> 78.8 us (0.957)
  Pallas kernels: 18.5 us -> 16.9 us
  local copies, waits for them, and re-layouts: 1.1 us -> 0.03 us
  starting transfers between devices: 21.6 us -> 20.7 us
    ppermute x6, waiting for transfers between devices: 24.7 us -> 22.1 us  [from_behind(): lax.ppermute(array, axis, [(i, (i + by) % length) for i in range(length)])]
    ppermute x15, waiting for transfers between devices: 12.1 us -> 14.4 us  [swap(): lax.ppermute(array, axis, [(i, i ^ bit) for i in range(lax.axis_size(axis...]
    pallas_call x1, Pallas kernels: 5.01 us -> 3.32 us  [shards(): pl.pallas_call(pack_kernel, out_shape=[shape((n, 3 * width + EXTRA), BF)...]
    unnamed x14, local copies, waits for them, and re-layouts: 1.1 us -> 0.03 us
    ppermute x6, starting transfers between devices: 6.3 us -> 5.31 us  [from_behind(): lax.ppermute(array, axis, [(i, (i + by) % length) for i in range(length)])]
  transfers between devices with their start and end apart: 25 -> 25, of which waited for: 13 -> 17; matrix products, arithmetic and copies ran while one was open for 0% -> 0% of each run, Pallas kernels for 14% -> 12%
where the time goes in v13:
time: 78.8 us; the launch traced here: 78.6 us
  waiting for transfers between devices  40.3 us (51%)
  starting transfers between devices  20.7 us (26%)
  Pallas kernels  16.9 us (21%)
    ppermute x6, waiting for transfers between devices, from_behind(): lax.ppermute(array, axis, [(i, (i + by) % length) for i in range(length)])  22.1 us
    ppermute x15, waiting for transfers between devices, swap(): lax.ppermute(array, axis, [(i, i ^ bit) for i in range(lax.axis_size(axis...  14.4 us
    ppermute x15, starting transfers between devices, swap(): lax.ppermute(array, axis, [(i, i ^ bit) for i in range(lax.axis_size(axis...  9.95 us
    ppermute x6, starting transfers between devices, from_behind(): lax.ppermute(array, axis, [(i, (i + by) % length) for i in range(length)])  5.31 us
    ppermute x3, waiting for transfers between devices, shards(): plane.append(lax.ppermute(chip, ('lat', 'lon'), pairs))  3.83 us
    pallas_call x1, Pallas kernels, shards(): pl.pallas_call(forward_kernel, grid=(1,), out_shape=[shape((piece, width...  3.73 us
    pallas_call x1, Pallas kernels, shards(): pl.pallas_call(backward_kernel, out_shape=shape((tokens, width), BF), in_...  3.63 us
    ppermute x3, starting transfers between devices, shards(): plane.append(lax.ppermute(chip, ('lat', 'lon'), pairs))  3.55 us
  transfers between devices with their start and end apart: 25, of which 17 were waited for; matrix products, arithmetic and copies ran while one was open for 0% of the time, Pallas kernels for 12%

profile of v13, /device:TPU:0, one launch (start us, length us, event | category | flops | bytes accessed | tf_op | source)
XLA Modules:
  0.0 78.6 jit_solution(11898091643733168031)
XLA Ops:
  0.6 0.0 copy-start.4
  0.6 0.0 copy-start.2
  0.7 2.5 %payload.1 = bf16[112,1536]{1,0:T(8,128)(2,1)} custom-call(bf16[384,1536]{1,0:T(8,128)(2,1)} %refs_0_.1, bf16[160,384]{1,0:T(8,128)(2,1)} %bitcast.6, bf16[384]{0:T(512)(128)(2,1)} %refs_2_.1), custom_call_target="tpu_custom_call" | custom-call | tf_op jit(solution)/shard_map/payload/pallas_call | solution.py:420
  3.1 3.1 %collective-permute-start = (bf16[112,1536]{1,0:T(8,128)(2,1)}, bf16[112,1536]{1,0:T(8,128)(2,1)S(1)}, u32[]{:S(2)}, u32[]{:S(2)}) collective-permute-start(bf16[112,1536]{1,0:T(8,128)(2,1)} %payload.1), channel_id=1, source_target_pairs={{0,8},{8,16},{16,24},{24,0},{1,9},{9,17},{17,25},{25,1},{2,10},{10... | collective-permute-start | bytes 1032200 | tf_op jit(solution)/shard_map/ppermute | solution.py:28
  6.2 0.0 copy-done.4
  6.2 0.0 copy-done.2
  6.2 3.3 %pack.1 = (bf16[64,4864]{1,0:T(8,128)(2,1)S(1)}, bf16[64,4864]{1,0:T(8,128)(2,1)S(1)}, bf16[64,4864]{1,0:T(8,128)(2,1)S(1)}, bf16[64,4864]{1,0:T(8,128)(2,1)S(1)}) custom-call(bf16[4,8,8,4608]{3,2,1,0:T(8,128)(2,1)} %bitcast.10, bf16[4,8,8,160]{3,2,1,0:T(8,128)(2,1)S(1)} %bitcast.9, s32[8,8]{1,0:T(8,128)S(1)} %copy-done.4), custom_call_target="tpu_custom_call" | custom-call | tf_op jit(solution)/shard_map/pack/pallas_call | solution.py:430
  9.6 0.7 collective-permute-start.2
  10.3 1.9 %collective-permute-start.3 = (bf16[64,4864]{1,0:T(8,128)(2,1)S(1)}, bf16[64,4864]{1,0:T(8,128)(2,1)S(1)}, u32[]{:S(2)}, u32[]{:S(2)}) collective-permute-start(bf16[64,4864]{1,0:T(8,128)(2,1)S(1)} %get-tuple-element.44), channel_id=1, source_target_pairs={{0,7},{1,6},{2,1},{3,0},{4,3},{5,2},{6,5},{7,4},{8,15},{9,14},{10,... | collective-permute-start | bytes 1867784 | tf_op jit(solution)/shard_map/ppermute | solution.py:452
  12.2 4.4 %collective-permute-done.refs_8_.refs_3_ = bf16[112,1536]{1,0:T(8,128)(2,1)S(1)} collective-permute-done((bf16[112,1536]{1,0:T(8,128)(2,1)}, bf16[112,1536]{1,0:T(8,128)(2,1)S(1)}, u32[]{:S(2)}, u32[]{:S(2)}) %collective-permute-start) | collective-permute-done | bytes 344096 | tf_op jit(solution)/shard_map/ppermute | solution.py:28
  16.5 0.0 collective-permute-start.1
  16.5 11.0 %collective-permute-done.1.refs_12_.refs_7_ = bf16[112,1536]{1,0:T(8,128)(2,1)S(1)} collective-permute-done((bf16[112,1536]{1,0:T(8,128)(2,1)S(1)}, bf16[112,1536]{1,0:T(8,128)(2,1)S(1)}, u32[]{:S(2)}, u32[]{:S(2)}) %collective-permute-start.1) | collective-permute-done | bytes 344096 | tf_op jit(solution)/shard_map/ppermute | solution.py:28
  27.6 1.3 %collective-permute-start.5 = (bf16[112,1536]{1,0:T(8,128)(2,1)S(1)}, bf16[112,1536]{1,0:T(8,128)(2,1)S(1)}, u32[]{:S(2)}, u32[]{:S(2)}) collective-permute-start(bf16[112,1536]{1,0:T(8,128)(2,1)S(1)} %collective-permute-done.1.refs_12_.refs_7_), channel_id=1, source_target_pairs={{0,4},{2,6},{4,0},{6,2},{1,5},{3,7},{5,1},{7,3},{8,12},{10,14},{12... | collective-permute-start | bytes 1032200 | tf_op jit(solution)/shard_map/ppermute | solution.py:400
  28.8 0.0 collective-permute-done.2.refs_2_.refs_3_
  28.8 0.0 collective-permute-done.3.refs_3_.refs_4_
  28.8 1.5 %collective-permute-start.4 = (bf16[64,4864]{1,0:T(8,128)(2,1)S(1)}, bf16[64,4864]{1,0:T(8,128)(2,1)S(1)}, u32[]{:S(2)}, u32[]{:S(2)}) collective-permute-start(bf16[64,4864]{1,0:T(8,128)(2,1)S(1)} %get-tuple-element.45), channel_id=1, source_target_pairs={{0,1},{1,0},{2,3},{3,2},{4,5},{5,4},{6,7},{7,6},{8,9},{9,8},{10,11... | collective-permute-start | bytes 1867784 | tf_op jit(solution)/shard_map/ppermute | solution.py:28
  30.3 0.0 collective-permute-start.12
  30.3 5.6 %collective-permute-done.5.refs_13_.refs_8_ = bf16[112,1536]{1,0:T(8,128)(2,1)S(1)} collective-permute-done((bf16[112,1536]{1,0:T(8,128)(2,1)S(1)}, bf16[112,1536]{1,0:T(8,128)(2,1)S(1)}, u32[]{:S(2)}, u32[]{:S(2)}) %collective-permute-start.5) | collective-permute-done | bytes 344096 | tf_op jit(solution)/shard_map/ppermute | solution.py:400
  35.9 1.2 %collective-permute-start.6 = (bf16[112,1536]{1,0:T(8,128)(2,1)S(1)}, bf16[112,1536]{1,0:T(8,128)(2,1)S(1)}, u32[]{:S(2)}, u32[]{:S(2)}) collective-permute-start(bf16[112,1536]{1,0:T(8,128)(2,1)S(1)} %collective-permute-done.refs_8_.refs_3_), channel_id=1, source_target_pairs={{0,4},{2,6},{4,0},{6,2},{1,5},{3,7},{5,1},{7,3},{8,12},{10,14},{12... | collective-permute-start | bytes 1032200 | tf_op jit(solution)/shard_map/ppermute | solution.py:400
  37.1 0.0 collective-permute-start.7
  37.1 0.0 collective-permute-start.11
  37.1 4.7 %collective-permute-done.12.refs_16_.refs_11_ = bf16[112,1536]{1,0:T(8,128)(2,1)S(1)} collective-permute-done((bf16[112,1536]{1,0:T(8,128)(2,1)S(1)}, bf16[112,1536]{1,0:T(8,128)(2,1)S(1)}, u32[]{:S(2)}, u32[]{:S(2)}) %collective-permute-start.12) | collective-permute-done | bytes 344096 | tf_op jit(solution)/shard_map/ppermute | solution.py:28
  41.8 0.0 collective-permute-start.13
  41.8 1.2 %collective-permute-done.4.refs_1_.refs_2_ = bf16[64,4864]{1,0:T(8,128)(2,1)S(1)} collective-permute-done((bf16[64,4864]{1,0:T(8,128)(2,1)S(1)}, bf16[64,4864]{1,0:T(8,128)(2,1)S(1)}, u32[]{:S(2)}, u32[]{:S(2)}) %collective-permute-start.4) | collective-permute-done | bytes 622624 | tf_op jit(solution)/shard_map/ppermute | solution.py:28
  43.0 0.3 collective-permute-done.6.refs_9_.refs_4_
  43.3 0.0 copy-start.6
  43.3 0.1 collective-permute-start.8
  43.4 0.5 collective-permute-start.9
  43.9 2.8 %attention.1.refs_0_ = bf16[256,1536]{1,0:T(8,128)(2,1)S(1)} custom-call(bf16[64,4864]{1,0:T(8,128)(2,1)S(1)} %get-tuple-element.49.refs_0_.refs_1_, bf16[64,4864]{1,0:T(8,128)(2,1)S(1)} %collective-permute-done.4.refs_1_.refs_2_, bf16[64,4864]{1,0:T(8,128)(2,1)S(1)} %collective-permute-done.2.refs_2_.refs_3_, ...), custom_call_target="tpu_custom_call" | custom-call | tf_op jit(solution)/shard_map/attention/pallas_call | solution.py:463
  46.7 0.7 collective-permute-done.7.refs_17_.refs_12_
  47.4 0.0 collective-permute-start.10
  47.4 0.0 collective-permute-done.11.refs_15_.refs_10_
  47.4 0.5 collective-permute-start.14
  47.9 0.0 collective-permute-done.13.refs_18_.refs_13_
  47.9 0.0 collective-permute-done.8.refs_10_.refs_5_
  47.9 0.0 collective-permute-done.9.refs_11_.refs_6_
  47.9 1.1 %collective-permute-done.10.refs_14_.refs_9_ = bf16[112,1536]{1,0:T(8,128)(2,1)S(1)} collective-permute-done((bf16[112,1536]{1,0:T(8,128)(2,1)S(1)}, bf16[112,1536]{1,0:T(8,128)(2,1)S(1)}, u32[]{:S(2)}, u32[]{:S(2)}) %collective-permute-start.10) | collective-permute-done | bytes 344096 | tf_op jit(solution)/shard_map/ppermute | solution.py:400
  49.1 0.5 collective-permute-done.14.refs_19_.refs_14_
  49.6 0.0 copy-done
  49.6 0.0 copy-done.3
  49.6 3.7 %forward.1 = (bf16[40,1664]{1,0:T(8,128)(2,1)S(1)}, bf16[40,1664]{1,0:T(8,128)(2,1)S(1)}, bf16[40,1664]{1,0:T(8,128)(2,1)S(1)}, bf16[40,1664]{1,0:T(8,128)(2,1)S...) custom-call(f32[32]{0:T(128)S(1)} %copy-done.6, f32[5]{0:T(128)S(1)} %copy-done.5, ...), custom_call_target="tpu_custom_call" | custom-call | tf_op jit(solution)/shard_map/forward/pallas_call | solution.py:484
  53.3 0.2 collective-permute-start.15
  53.5 1.1 %collective-permute-start.16 = (bf16[40,1664]{1,0:T(8,128)(2,1)S(1)}, bf16[40,1664]{1,0:T(8,128)(2,1)S(1)}, u32[]{:S(2)}, u32[]{:S(2)}) collective-permute-start(bf16[40,1664]{1,0:T(8,128)(2,1)S(1)} %get-tuple-element.62), channel_id=1, source_target_pairs={{0,4},{2,6},{4,0},{6,2},{1,5},{3,7},{5,1},{7,3},{8,12},{10,14},{12... | collective-permute-start | bytes 399368 | tf_op jit(solution)/shard_map/ppermute | solution.py:400
  54.7 0.6 collective-permute-start.17
  55.3 3.6 %backward.1 = bf16[256,1536]{1,0:T(8,128)(2,1)} custom-call(f32[256,1536]{1,0:T(8,128)S(1)} %get-tuple-element.64.normed_ref, f32[256,128]{1,0:T(8,128)S(1)} %get-tuple-element.65.inv_ref, bf16[256,160]{1,0:T(8,128)(2,1)S(1)} %get-tuple-element.66.dfc_ref, bf16[384,1536]{1,0:T(8,128)(2,1)S(1)} %copy-done, bf16[160,384]{1,0:T(8,128)(2,1)S(1)} %bitcast.8, ...), custom_call_target="tpu_custom_call" | custom-call | tf_op jit(solution)/shard_map/backward/pallas_call | solution.py:499
  58.9 0.0 collective-permute-done.15.b
  58.9 1.0 %collective-permute-done.16.c = bf16[40,1664]{1,0:T(8,128)(2,1)S(1)} collective-permute-done((bf16[40,1664]{1,0:T(8,128)(2,1)S(1)}, bf16[40,1664]{1,0:T(8,128)(2,1)S(1)}, u32[]{:S(2)}, u32[]{:S(2)}) %collective-permute-start.16) | collective-permute-done | bytes 133152 | tf_op jit(solution)/shard_map/ppermute | solution.py:400
  59.9 1.7 %collective-permute-done.17.d = bf16[40,1664]{1,0:T(8,128)(2,1)S(1)} collective-permute-done((bf16[40,1664]{1,0:T(8,128)(2,1)S(1)}, bf16[40,1664]{1,0:T(8,128)(2,1)S(1)}, u32[]{:S(2)}, u32[]{:S(2)}) %collective-permute-start.17) | collective-permute-done | bytes 133152 | tf_op jit(solution)/shard_map/ppermute | solution.py:400
  61.6 0.2 lat_sum.1
  61.8 0.1 collective-permute-start.18
  61.9 1.5 %collective-permute-start.19 = (bf16[40,384]{1,0:T(8,128)(2,1)S(1)}, bf16[40,384]{1,0:T(8,128)(2,1)S(1)}, u32[]{:S(2)}, u32[]{:S(2)}) collective-permute-start(bf16[40,384]{1,0:T(8,128)(2,1)S(1)} %get-tuple-element.75), channel_id=1, source_target_pairs={{0,16},{8,24},{16,0},{24,8},{1,17},{9,25},{17,1},{25,9},{2,18},{10... | collective-permute-start | bytes 92168 | tf_op jit(solution)/shard_map/ppermute | solution.py:400
  63.5 2.8 %collective-permute-start.20 = (bf16[40,384]{1,0:T(8,128)(2,1)S(1)}, bf16[40,384]{1,0:T(8,128)(2,1)S(1)}, u32[]{:S(2)}, u32[]{:S(2)}) collective-permute-start(bf16[40,384]{1,0:T(8,128)(2,1)S(1)} %get-tuple-element.76), channel_id=1, source_target_pairs={{0,24},{8,16},{16,8},{24,0},{1,25},{9,17},{17,9},{25,1},{2,26},{10... | collective-permute-start | bytes 92168 | tf_op jit(solution)/shard_map/ppermute | solution.py:400
  66.2 0.0 collective-permute-done.18.b
  66.2 0.5 collective-permute-done.19.c
  66.8 2.4 %collective-permute-done.20.d = bf16[40,384]{1,0:T(8,128)(2,1)S(1)} collective-permute-done((bf16[40,384]{1,0:T(8,128)(2,1)S(1)}, bf16[40,384]{1,0:T(8,128)(2,1)S(1)}, u32[]{:S(2)}, u32[]{:S(2)}) %collective-permute-start.20) | collective-permute-done | bytes 30752 | tf_op jit(solution)/shard_map/ppermute | solution.py:400
  69.2 0.1 collective-permute-start.21
  69.3 1.2 %collective-permute-done.21.other_ref = bf16[48,384]{1,0:T(8,128)(2,1)S(1)} collective-permute-done((bf16[48,384]{1,0:T(8,128)(2,1)S(1)}, bf16[48,384]{1,0:T(8,128)(2,1)S(1)}, u32[]{:S(2)}, u32[]{:S(2)}) %collective-permute-start.21) | collective-permute-done | bytes 36896 | tf_op jit(solution)/shard_map/ppermute | solution.py:400
  70.5 2.0 %collective-permute-start.24 = (bf16[96,384]{1,0:T(8,128)(2,1)S(1)}, bf16[96,384]{1,0:T(8,128)(2,1)S(1)}, u32[]{:S(2)}, u32[]{:S(2)}) collective-permute-start(bf16[96,384]{1,0:T(8,128)(2,1)S(1)} %pair.1.refs_0_), channel_id=1, source_target_pairs={{0,5},{1,4},{2,7},{3,6},{4,1},{5,0},{6,3},{7,2},{8,13},{9,12},{10,... | collective-permute-start | bytes 221192 | tf_op jit(solution)/shard_map/ppermute | solution.py:539
  72.5 1.0 %collective-permute-start.23 = (bf16[96,384]{1,0:T(8,128)(2,1)S(1)}, bf16[96,384]{1,0:T(8,128)(2,1)S(1)}, u32[]{:S(2)}, u32[]{:S(2)}) collective-permute-start(bf16[96,384]{1,0:T(8,128)(2,1)S(1)} %pair.1.refs_0_), channel_id=1, source_target_pairs={{0,4},{1,5},{2,6},{3,7},{4,0},{5,1},{6,2},{7,3},{8,12},{9,13},{10,... | collective-permute-start | bytes 221192 | tf_op jit(solution)/shard_map/ppermute | solution.py:539
  73.6 0.5 collective-permute-start.22
  74.1 1.8 %collective-permute-done.24.refs_3_ = bf16[96,384]{1,0:T(8,128)(2,1)S(1)} collective-permute-done((bf16[96,384]{1,0:T(8,128)(2,1)S(1)}, bf16[96,384]{1,0:T(8,128)(2,1)S(1)}, u32[]{:S(2)}, u32[]{:S(2)}) %collective-permute-start.24) | collective-permute-done | bytes 73760 | tf_op jit(solution)/shard_map/ppermute | solution.py:539
  75.9 1.5 %collective-permute-done.23.refs_2_ = bf16[96,384]{1,0:T(8,128)(2,1)S(1)} collective-permute-done((bf16[96,384]{1,0:T(8,128)(2,1)S(1)}, bf16[96,384]{1,0:T(8,128)(2,1)S(1)}, u32[]{:S(2)}, u32[]{:S(2)}) %collective-permute-start.23) | collective-permute-done | bytes 73760 | tf_op jit(solution)/shard_map/ppermute | solution.py:539
  77.4 0.5 collective-permute-done.22.refs_1_
  77.9 0.7 join.1
  (9 shorter events, 0.1 us)
Async XLA Ops:
  0.6 5.6 %copy-start.4 = (s32[8,8]{1,0:T(8,128)S(1)}, s32[8,8]{1,0:T(8,128)}, u32[]{:S(2)}) copy-start(s32[8,8]{1,0:T(8,128)} %valid_ref.1) | copy-start | bytes 772
  0.6 5.6 %copy-start.2 = (bf16[1,4,8,8,160]{4,3,2,1,0:T(8,128)(2,1)S(1)}, bf16[1,4,8,8,160]{4,3,2,1,0:T(8,128)(2,1)}, u32[]{:S(2)}) copy-start(bf16[1,4,8,8,160]{4,3,2,1,0:T(8,128)(2,1)} %param.9) | copy-start | bytes 245764
  3.1 13.4 %collective-permute-start = (bf16[112,1536]{1,0:T(8,128)(2,1)}, bf16[112,1536]{1,0:T(8,128)(2,1)S(1)}, u32[]{:S(2)}, u32[]{:S(2)}) collective-permute-start(bf16[112,1536]{1,0:T(8,128)(2,1)} %payload.1), channel_id=1, source_target_pairs={{0,8},{8,16},{16,24},{24,0},{1,9},{9,17},{17,25},{25,1},{2,10},{10... | collective-permute-start | bytes 1032200 | tf_op jit(solution)/shard_map/ppermute | solution.py:28
  9.6 19.3 %collective-permute-start.2 = (bf16[64,4864]{1,0:T(8,128)(2,1)S(1)}, bf16[64,4864]{1,0:T(8,128)(2,1)S(1)}, u32[]{:S(2)}, u32[]{:S(2)}) collective-permute-start(bf16[64,4864]{1,0:T(8,128)(2,1)S(1)} %get-tuple-element.43), channel_id=1, source_target_pairs={{0,6},{2,0},{4,2},{6,4},{1,7},{3,1},{5,3},{7,5},{8,14},{10,8},{12,... | collective-permute-start | bytes 1867784 | tf_op jit(solution)/shard_map/ppermute | solution.py:28
  10.3 18.6 %collective-permute-start.3 = (bf16[64,4864]{1,0:T(8,128)(2,1)S(1)}, bf16[64,4864]{1,0:T(8,128)(2,1)S(1)}, u32[]{:S(2)}, u32[]{:S(2)}) collective-permute-start(bf16[64,4864]{1,0:T(8,128)(2,1)S(1)} %get-tuple-element.44), channel_id=1, source_target_pairs={{0,7},{1,6},{2,1},{3,0},{4,3},{5,2},{6,5},{7,4},{8,15},{9,14},{10,... | collective-permute-start | bytes 1867784 | tf_op jit(solution)/shard_map/ppermute | solution.py:452
  16.5 11.0 %collective-permute-start.1 = (bf16[112,1536]{1,0:T(8,128)(2,1)S(1)}, bf16[112,1536]{1,0:T(8,128)(2,1)S(1)}, u32[]{:S(2)}, u32[]{:S(2)}) collective-permute-start(bf16[112,1536]{1,0:T(8,128)(2,1)S(1)} %collective-permute-done.refs_8_.refs_3_), channel_id=1, source_target_pairs={{0,8},{8,16},{16,24},{24,0},{1,9},{9,17},{17,25},{25,1},{2,10},{10... | collective-permute-start | bytes 1032200 | tf_op jit(solution)/shard_map/ppermute | solution.py:28
  27.6 8.3 %collective-permute-start.5 = (bf16[112,1536]{1,0:T(8,128)(2,1)S(1)}, bf16[112,1536]{1,0:T(8,128)(2,1)S(1)}, u32[]{:S(2)}, u32[]{:S(2)}) collective-permute-start(bf16[112,1536]{1,0:T(8,128)(2,1)S(1)} %collective-permute-done.1.refs_12_.refs_7_), channel_id=1, source_target_pairs={{0,4},{2,6},{4,0},{6,2},{1,5},{3,7},{5,1},{7,3},{8,12},{10,14},{12... | collective-permute-start | bytes 1032200 | tf_op jit(solution)/shard_map/ppermute | solution.py:400
  28.8 14.2 %collective-permute-start.4 = (bf16[64,4864]{1,0:T(8,128)(2,1)S(1)}, bf16[64,4864]{1,0:T(8,128)(2,1)S(1)}, u32[]{:S(2)}, u32[]{:S(2)}) collective-permute-start(bf16[64,4864]{1,0:T(8,128)(2,1)S(1)} %get-tuple-element.45), channel_id=1, source_target_pairs={{0,1},{1,0},{2,3},{3,2},{4,5},{5,4},{6,7},{7,6},{8,9},{9,8},{10,11... | collective-permute-start | bytes 1867784 | tf_op jit(solution)/shard_map/ppermute | solution.py:28
  30.3 11.4 %collective-permute-start.12 = (bf16[112,1536]{1,0:T(8,128)(2,1)S(1)}, bf16[112,1536]{1,0:T(8,128)(2,1)S(1)}, u32[]{:S(2)}, u32[]{:S(2)}) collective-permute-start(bf16[112,1536]{1,0:T(8,128)(2,1)S(1)} %collective-permute-done.1.refs_12_.refs_7_), channel_id=1, source_target_pairs={{0,8},{8,16},{16,24},{24,0},{1,9},{9,17},{17,25},{25,1},{2,10},{10... | collective-permute-start | bytes 1032200 | tf_op jit(solution)/shard_map/ppermute | solution.py:28
  35.9 7.4 %collective-permute-start.6 = (bf16[112,1536]{1,0:T(8,128)(2,1)S(1)}, bf16[112,1536]{1,0:T(8,128)(2,1)S(1)}, u32[]{:S(2)}, u32[]{:S(2)}) collective-permute-start(bf16[112,1536]{1,0:T(8,128)(2,1)S(1)} %collective-permute-done.refs_8_.refs_3_), channel_id=1, source_target_pairs={{0,4},{2,6},{4,0},{6,2},{1,5},{3,7},{5,1},{7,3},{8,12},{10,14},{12... | collective-permute-start | bytes 1032200 | tf_op jit(solution)/shard_map/ppermute | solution.py:400
  37.1 10.3 %collective-permute-start.7 = (bf16[112,1536]{1,0:T(8,128)(2,1)S(1)}, bf16[112,1536]{1,0:T(8,128)(2,1)S(1)}, u32[]{:S(2)}, u32[]{:S(2)}) collective-permute-start(bf16[112,1536]{1,0:T(8,128)(2,1)S(1)} %collective-permute-done.5.refs_13_.refs_8_), channel_id=1, source_target_pairs={{0,8},{8,16},{16,24},{24,0},{1,9},{9,17},{17,25},{25,1},{2,10},{10... | collective-permute-start | bytes 1032200 | tf_op jit(solution)/shard_map/ppermute | solution.py:28
  37.1 10.3 %collective-permute-start.11 = (bf16[112,1536]{1,0:T(8,128)(2,1)S(1)}, bf16[112,1536]{1,0:T(8,128)(2,1)S(1)}, u32[]{:S(2)}, u32[]{:S(2)}) collective-permute-start(bf16[112,1536]{1,0:T(8,128)(2,1)S(1)} %collective-permute-done.5.refs_13_.refs_8_), channel_id=1, source_target_pairs={{0,2},{2,0},{4,6},{6,4},{1,3},{3,1},{5,7},{7,5},{8,10},{10,8},{12,... | collective-permute-start | bytes 1032200 | tf_op jit(solution)/shard_map/ppermute | solution.py:400
  41.8 6.1 %collective-permute-start.13 = (bf16[112,1536]{1,0:T(8,128)(2,1)S(1)}, bf16[112,1536]{1,0:T(8,128)(2,1)S(1)}, u32[]{:S(2)}, u32[]{:S(2)}) collective-permute-start(bf16[112,1536]{1,0:T(8,128)(2,1)S(1)} %collective-permute-done.12.refs_16_.refs_11_), channel_id=1, source_target_pairs={{0,2},{2,0},{4,6},{6,4},{1,3},{3,1},{5,7},{7,5},{8,10},{10,8},{12,... | collective-permute-start | bytes 1032200 | tf_op jit(solution)/shard_map/ppermute | solution.py:400
  43.3 6.3 %copy-start = (bf16[384,1536]{1,0:T(8,128)(2,1)S(1)}, bf16[384,1536]{1,0:T(8,128)(2,1)}, u32[]{:S(2)}) copy-start(bf16[384,1536]{1,0:T(8,128)(2,1)} %refs_0_.1) | copy-start | bytes 3538948
  43.3 6.3 %copy-start.1 = (bf16[384,160]{0,1:T(8,128)(2,1)S(1)}, bf16[384,160]{0,1:T(8,128)(2,1)}, u32[]{:S(2)}) copy-start(bf16[384,160]{0,1:T(8,128)(2,1)} %param.12) | copy-start | bytes 368644
  43.3 6.3 %copy-start.3 = (bf16[384]{0:T(512)(128)(2,1)S(1)}, bf16[384]{0:T(512)(128)(2,1)}, u32[]{:S(2)}) copy-start(bf16[384]{0:T(512)(128)(2,1)} %refs_2_.1) | copy-start | bytes 2308
  43.3 6.3 %copy-start.5 = (f32[5]{0:T(128)S(1)}, f32[5]{0:T(128)}, u32[]{:S(2)}) copy-start(f32[5]{0:T(128)} %var_ref.1) | copy-start | bytes 64
  43.3 6.3 %copy-start.6 = (f32[32]{0:T(128)S(1)}, f32[32]{0:T(128)}, u32[]{:S(2)}) copy-start(f32[32]{0:T(128)} %constant.2.clone.lat_ref) | copy-start | bytes 388
  43.3 4.6 %collective-permute-start.8 = (bf16[112,1536]{1,0:T(8,128)(2,1)S(1)}, bf16[112,1536]{1,0:T(8,128)(2,1)S(1)}, u32[]{:S(2)}, u32[]{:S(2)}) collective-permute-start(bf16[112,1536]{1,0:T(8,128)(2,1)S(1)} %collective-permute-done.refs_8_.refs_3_), channel_id=1, source_target_pairs={{0,2},{2,0},{4,6},{6,4},{1,3},{3,1},{5,7},{7,5},{8,10},{10,8},{12,... | collective-permute-start | bytes 1032200 | tf_op jit(solution)/shard_map/ppermute | solution.py:400
  43.4 4.5 %collective-permute-start.9 = (bf16[112,1536]{1,0:T(8,128)(2,1)S(1)}, bf16[112,1536]{1,0:T(8,128)(2,1)S(1)}, u32[]{:S(2)}, u32[]{:S(2)}) collective-permute-start(bf16[112,1536]{1,0:T(8,128)(2,1)S(1)} %collective-permute-done.6.refs_9_.refs_4_), channel_id=1, source_target_pairs={{0,2},{2,0},{4,6},{6,4},{1,3},{3,1},{5,7},{7,5},{8,10},{10,8},{12,... | collective-permute-start | bytes 1032200 | tf_op jit(solution)/shard_map/ppermute | solution.py:400
  47.4 1.7 %collective-permute-start.10 = (bf16[112,1536]{1,0:T(8,128)(2,1)S(1)}, bf16[112,1536]{1,0:T(8,128)(2,1)S(1)}, u32[]{:S(2)}, u32[]{:S(2)}) collective-permute-start(bf16[112,1536]{1,0:T(8,128)(2,1)S(1)} %collective-permute-done.1.refs_12_.refs_7_), channel_id=1, source_target_pairs={{0,2},{2,0},{4,6},{6,4},{1,3},{3,1},{5,7},{7,5},{8,10},{10,8},{12,... | collective-permute-start | bytes 1032200 | tf_op jit(solution)/shard_map/ppermute | solution.py:400
  47.4 2.1 %collective-permute-start.14 = (bf16[112,1536]{1,0:T(8,128)(2,1)S(1)}, bf16[112,1536]{1,0:T(8,128)(2,1)S(1)}, u32[]{:S(2)}, u32[]{:S(2)}) collective-permute-start(bf16[112,1536]{1,0:T(8,128)(2,1)S(1)} %collective-permute-done.7.refs_17_.refs_12_), channel_id=1, source_target_pairs={{0,2},{2,0},{4,6},{6,4},{1,3},{3,1},{5,7},{7,5},{8,10},{10,8},{12,... | collective-permute-start | bytes 1032200 | tf_op jit(solution)/shard_map/ppermute | solution.py:400
  53.3 5.6 %collective-permute-start.15 = (bf16[40,1664]{1,0:T(8,128)(2,1)S(1)}, bf16[40,1664]{1,0:T(8,128)(2,1)S(1)}, u32[]{:S(2)}, u32[]{:S(2)}) collective-permute-start(bf16[40,1664]{1,0:T(8,128)(2,1)S(1)} %get-tuple-element.61), channel_id=1, source_target_pairs={{0,2},{2,0},{4,6},{6,4},{1,3},{3,1},{5,7},{7,5},{8,10},{10,8},{12,... | collective-permute-start | bytes 399368 | tf_op jit(solution)/shard_map/ppermute | solution.py:400
  53.5 6.4 %collective-permute-start.16 = (bf16[40,1664]{1,0:T(8,128)(2,1)S(1)}, bf16[40,1664]{1,0:T(8,128)(2,1)S(1)}, u32[]{:S(2)}, u32[]{:S(2)}) collective-permute-start(bf16[40,1664]{1,0:T(8,128)(2,1)S(1)} %get-tuple-element.62), channel_id=1, source_target_pairs={{0,4},{2,6},{4,0},{6,2},{1,5},{3,7},{5,1},{7,3},{8,12},{10,14},{12... | collective-permute-start | bytes 399368 | tf_op jit(solution)/shard_map/ppermute | solution.py:400
  54.7 7.0 %collective-permute-start.17 = (bf16[40,1664]{1,0:T(8,128)(2,1)S(1)}, bf16[40,1664]{1,0:T(8,128)(2,1)S(1)}, u32[]{:S(2)}, u32[]{:S(2)}) collective-permute-start(bf16[40,1664]{1,0:T(8,128)(2,1)S(1)} %get-tuple-element.63), channel_id=1, source_target_pairs={{0,6},{2,4},{4,2},{6,0},{1,7},{3,5},{5,3},{7,1},{8,14},{10,12},{12... | collective-permute-start | bytes 399368 | tf_op jit(solution)/shard_map/ppermute | solution.py:400
  61.8 4.4 %collective-permute-start.18 = (bf16[40,384]{1,0:T(8,128)(2,1)S(1)}, bf16[40,384]{1,0:T(8,128)(2,1)S(1)}, u32[]{:S(2)}, u32[]{:S(2)}) collective-permute-start(bf16[40,384]{1,0:T(8,128)(2,1)S(1)} %get-tuple-element.74), channel_id=1, source_target_pairs={{0,8},{8,0},{16,24},{24,16},{1,9},{9,1},{17,25},{25,17},{2,10},{10... | collective-permute-start | bytes 92168 | tf_op jit(solution)/shard_map/ppermute | solution.py:400
  61.9 4.8 %collective-permute-start.19 = (bf16[40,384]{1,0:T(8,128)(2,1)S(1)}, bf16[40,384]{1,0:T(8,128)(2,1)S(1)}, u32[]{:S(2)}, u32[]{:S(2)}) collective-permute-start(bf16[40,384]{1,0:T(8,128)(2,1)S(1)} %get-tuple-element.75), channel_id=1, source_target_pairs={{0,16},{8,24},{16,0},{24,8},{1,17},{9,25},{17,1},{25,9},{2,18},{10... | collective-permute-start | bytes 92168 | tf_op jit(solution)/shard_map/ppermute | solution.py:400
  63.5 5.7 %collective-permute-start.20 = (bf16[40,384]{1,0:T(8,128)(2,1)S(1)}, bf16[40,384]{1,0:T(8,128)(2,1)S(1)}, u32[]{:S(2)}, u32[]{:S(2)}) collective-permute-start(bf16[40,384]{1,0:T(8,128)(2,1)S(1)} %get-tuple-element.76), channel_id=1, source_target_pairs={{0,24},{8,16},{16,8},{24,0},{1,25},{9,17},{17,9},{25,1},{2,26},{10... | collective-permute-start | bytes 92168 | tf_op jit(solution)/shard_map/ppermute | solution.py:400
  69.2 1.3 %collective-permute-start.21 = (bf16[48,384]{1,0:T(8,128)(2,1)S(1)}, bf16[48,384]{1,0:T(8,128)(2,1)S(1)}, u32[]{:S(2)}, u32[]{:S(2)}) collective-permute-start(bf16[48,384]{1,0:T(8,128)(2,1)S(1)} %dp_sum.1.mine_ref), channel_id=1, source_target_pairs={{0,2},{2,0},{4,6},{6,4},{1,3},{3,1},{5,7},{7,5},{8,10},{10,8},{12,... | collective-permute-start | bytes 110600 | tf_op jit(solution)/shard_map/ppermute | solution.py:400
  70.5 5.4 %collective-permute-start.24 = (bf16[96,384]{1,0:T(8,128)(2,1)S(1)}, bf16[96,384]{1,0:T(8,128)(2,1)S(1)}, u32[]{:S(2)}, u32[]{:S(2)}) collective-permute-start(bf16[96,384]{1,0:T(8,128)(2,1)S(1)} %pair.1.refs_0_), channel_id=1, source_target_pairs={{0,5},{1,4},{2,7},{3,6},{4,1},{5,0},{6,3},{7,2},{8,13},{9,12},{10,... | collective-permute-start | bytes 221192 | tf_op jit(solution)/shard_map/ppermute | solution.py:539
  72.5 4.9 %collective-permute-start.23 = (bf16[96,384]{1,0:T(8,128)(2,1)S(1)}, bf16[96,384]{1,0:T(8,128)(2,1)S(1)}, u32[]{:S(2)}, u32[]{:S(2)}) collective-permute-start(bf16[96,384]{1,0:T(8,128)(2,1)S(1)} %pair.1.refs_0_), channel_id=1, source_target_pairs={{0,4},{1,5},{2,6},{3,7},{4,0},{5,1},{6,2},{7,3},{8,12},{9,13},{10,... | collective-permute-start | bytes 221192 | tf_op jit(solution)/shard_map/ppermute | solution.py:539
  73.6 4.4 %collective-permute-start.22 = (bf16[96,384]{1,0:T(8,128)(2,1)S(1)}, bf16[96,384]{1,0:T(8,128)(2,1)S(1)}, u32[]{:S(2)}, u32[]{:S(2)}) collective-permute-start(bf16[96,384]{1,0:T(8,128)(2,1)S(1)} %pair.1.refs_0_), channel_id=1, source_target_pairs={{0,1},{1,0},{2,3},{3,2},{4,5},{5,4},{6,7},{7,6},{8,9},{9,8},{10,11... | collective-permute-start | bytes 221192 | tf_op jit(solution)/shard_map/ppermute | solution.py:539

commit v14 on v13

--- a/solution.py
+++ b/solution.py
@@ -283,7 +283,7 @@
     owned, refs = refs[:3], refs[3:]
     pieces, refs = refs[:PIECES], refs[PIECES:]
     ts, refs = refs[:4], refs[4:]
-    normed_ref, inv_ref, dfc_ref, hidden_ref, w_all, ug_all, term = refs
+    normed_ref, inv_ref, dfc_ref, loss_ref, hidden_ref, w_all, ug_all, term = refs
     lat_place = lax.axis_index("lat")
     assemble(*owned, pieces, w_all, ug_all)
     tokens, width = normed_ref.shape
@@ -320,12 +320,11 @@
         dfc, hidden_ref[...], (((0,), (0,)), ((), ())), preferred_element_type=F32
     )
     loss = jnp.sum(jnp.sum(weight * misfit * misfit, axis=1, keepdims=True), axis=0, keepdims=True)
+    loss_ref[...] = jnp.broadcast_to(loss, loss_ref.shape)
     rows = ts[0].shape[0]
-    block = loss_block(loss, rows).astype(BF)
     for b, ref in enumerate(ts):
         at = pl.multiple_of((lat_place ^ b) * rows, 8)
-        ref[:, :width] = term[pl.ds(at, rows), :].astype(BF)
-        ref[:, width:] = block
+        ref[...] = term[pl.ds(at, rows), :].astype(BF)
 
 
 def backward_kernel(normed_ref, inv_ref, dfc_ref, *refs):
@@ -354,15 +353,13 @@
     return (a[...].astype(F32) + b[...].astype(F32)) + (c[...].astype(F32) + d[...].astype(F32))
 
 
-def lat_sum_kernel(a, b, c, d, z0, z1, z2, z3, loss_ref, total_ref):
+def lat_sum_kernel(a, b, c, d, z0, z1, z2, z3, total_ref):
     total_ref[...] = add4(a, b, c, d)
     zi = lax.axis_index("dp")
-    rows, width = z0.shape
+    width = z0.shape[1]
     for k, ref in enumerate((z0, z1, z2, z3)):
         at = pl.multiple_of((zi ^ k) * width, 128)
         ref[...] = total_ref[:, pl.ds(at, width)].astype(BF)
-    loss = jnp.sum(total_ref[0:1, 4 * width :], axis=1, keepdims=True)
-    loss_ref[...] = jnp.broadcast_to(loss, loss_ref.shape)
 
 
 def dp_sum_kernel(loss_ref, a, b, c, d, o_ref):
@@ -390,10 +387,12 @@
             at = pl.multiple_of((2 * (chip ^ a) + n) * rows, 8)
             both = [pieces[2 * a + b][held * n : held * n + rows, :].astype(F32) for b in range(2)]
             o_ref[pl.ds(at, rows), :] = (both[0] + both[1]) / counts[0]
-    sums = [
-        jnp.sum(p[rows : rows + 1, 0:128].astype(F32), axis=1, keepdims=True) for p in pieces[:2]
-    ]
-    loss_ref[...] = jnp.broadcast_to((sums[0] + sums[1]) / counts[1], loss_ref.shape)
+    def part(p, n):
+        return jnp.sum(p[held * n + rows : held * n + rows + 1, 0:128].astype(F32), axis=1, keepdims=True)
+
+    chips = [part(p, 0) + part(p, 1) for p in pieces]
+    loss = (chips[0] + chips[1]) + (chips[2] + chips[3])
+    loss_ref[...] = jnp.broadcast_to(loss / counts[1], loss_ref.shape)
 
 
 def swap(array, axis, bit):
@@ -459,7 +458,10 @@
     ring1_late, across2 = barrier((ring1, across2))
     across1 = swap(ring1_late, "lat", 2)
     tiles = [own, east, south, diag]
-    *tiles, ring1, across1, ring2 = barrier((*tiles, ring1, across1, ring2))
+    across2_swapped = swap(across2, "lat", 1)
+    *tiles, ring1, across1, ring2, across2_swapped = barrier(
+        (*tiles, ring1, across1, ring2, across2_swapped)
+    )
     ctx = pl.pallas_call(
         attention_kernel,
         out_shape=shape((tokens, width), BF),
@@ -469,9 +471,9 @@
         name="attention",
     )(*tiles)
     ctx, across3 = barrier((ctx, across3))
-    pieces = []
-    for ring, across in ((ring1, across1), (ring2, across2), (ring3, across3)):
-        pieces += [ring, across, swap(ring, "lat", 1), swap(across, "lat", 1)]
+    pieces = [ring1, across1, swap(ring1, "lat", 1), swap(across1, "lat", 1)]
+    pieces += [ring2, across2, swap(ring2, "lat", 1), across2_swapped]
+    pieces += [ring3, across3, swap(ring3, "lat", 1), swap(across3, "lat", 1)]
 
     piece = span // lat
     extra_specs = [
@@ -481,13 +483,14 @@
         pltpu.VMEM((dp * rows, width), BF),
         pltpu.VMEM((UGROWS, dp * rows), BF),
     ]
-    *terms, normed, inv, dfc = pl.pallas_call(
+    *terms, normed, inv, dfc, loss = pl.pallas_call(
         forward_kernel,
         grid=(1,),
-        out_shape=[shape((piece, width + 128), BF)] * 4
-        + [shape((tokens, width), F32), shape((tokens, 128), F32), shape((tokens, span), BF)],
+        out_shape=[shape((piece, width), BF)] * 4
+        + [shape((tokens, width), F32), shape((tokens, 128), F32), shape((tokens, span), BF)]
+        + [shape((8, 128), F32)],
         in_specs=[SMEM] * 2 + [VMEM] + extra_specs + [VMEM] * (3 + PIECES),
-        out_specs=[VMEM] * 7,
+        out_specs=[VMEM] * 8,
         scratch_shapes=[pltpu.VMEM((tokens, width), BF)]
         + assembly
         + [pltpu.VMEM((span, width), F32)],
@@ -507,12 +510,12 @@
     )(normed, inv, dfc, w_out, unpatch_t, norm_gain, *pieces)
     *terms, grad_context = barrier((*terms, grad_context))
 
-    *parts, loss = pl.pallas_call(
+    parts = pl.pallas_call(
         lat_sum_kernel,
-        out_shape=[shape((piece, rows), BF)] * 4 + [shape((8, 128), F32)],
+        out_shape=[shape((piece, rows), BF)] * 4,
         in_specs=[VMEM] * 4,
-        out_specs=[VMEM] * 5,
-        scratch_shapes=[pltpu.VMEM((piece, width + 128), F32)],
+        out_specs=[VMEM] * 4,
+        scratch_shapes=[pltpu.VMEM((piece, width), F32)],
         compiler_params=params(4),
         name="lat_sum",
     )(*terms)

time: 78.8 us -> 79.1 us (level)
    ppermute x6, waiting for transfers between devices: 22.1 us -> 23.9 us  [from_behind(): lax.ppermute(array, axis, [(i, (i + by) % length) for i in range(length)])]
    ppermute x15, waiting for transfers between devices: 14.4 us -> 13.2 us  [swap(): lax.ppermute(array, axis, [(i, i ^ bit) for i in range(lax.axis_size(axis...]
  transfers between devices with their start and end apart: 25 -> 25, of which waited for: 17 -> 16; matrix products, arithmetic and copies ran while one was open for 0% -> 0% of each run, Pallas kernels for 12% -> 12%
where the time goes in v14:
time: 79.1 us; the launch traced here: 78.9 us
  waiting for transfers between devices  40.9 us (52%)
  starting transfers between devices  20.3 us (26%)
  Pallas kernels  16.9 us (21%)
  between operations  0.8 us (1%)
    ppermute x6, waiting for transfers between devices, from_behind(): lax.ppermute(array, axis, [(i, (i + by) % length) for i in range(length)])  23.9 us
    ppermute x15, waiting for transfers between devices, swap(): lax.ppermute(array, axis, [(i, i ^ bit) for i in range(lax.axis_size(axis...  13.2 us
    ppermute x15, starting transfers between devices, swap(): lax.ppermute(array, axis, [(i, i ^ bit) for i in range(lax.axis_size(axis...  9.56 us
    ppermute x6, starting transfers between devices, from_behind(): lax.ppermute(array, axis, [(i, (i + by) % length) for i in range(length)])  5.31 us
    ppermute x3, waiting for transfers between devices, shards(): plane.append(lax.ppermute(chip, ('lat', 'lon'), pairs))  3.82 us
    pallas_call x1, Pallas kernels, shards(): pl.pallas_call(forward_kernel, grid=(1,), out_shape=[shape((piece, width)...  3.71 us
    pallas_call x1, Pallas kernels, shards(): pl.pallas_call(backward_kernel, out_shape=shape((tokens, width), BF), in_...  3.64 us
    ppermute x3, starting transfers between devices, shards(): plane.append(lax.ppermute(chip, ('lat', 'lon'), pairs))  3.55 us
  transfers between devices with their start and end apart: 25, of which 16 were waited for; matrix products, arithmetic and copies ran while one was open for 0% of the time, Pallas kernels for 12%

profile of v14, /device:TPU:0, one launch (start us, length us, event | category | flops | bytes accessed | tf_op | source)
XLA Modules:
  0.0 78.9 jit_solution(5281257271465314534)
XLA Ops:
  0.6 0.0 copy-start.4
  0.6 0.0 copy-start.2
  0.7 2.5 %payload.1 = bf16[112,1536]{1,0:T(8,128)(2,1)} custom-call(bf16[384,1536]{1,0:T(8,128)(2,1)} %refs_0_.1, bf16[160,384]{1,0:T(8,128)(2,1)} %bitcast.6, bf16[384]{0:T(512)(128)(2,1)} %refs_2_.1), custom_call_target="tpu_custom_call" | custom-call | tf_op jit(solution)/shard_map/payload/pallas_call | solution.py:419
  3.1 3.1 %collective-permute-start = (bf16[112,1536]{1,0:T(8,128)(2,1)}, bf16[112,1536]{1,0:T(8,128)(2,1)S(1)}, u32[]{:S(2)}, u32[]{:S(2)}) collective-permute-start(bf16[112,1536]{1,0:T(8,128)(2,1)} %payload.1), channel_id=1, source_target_pairs={{0,8},{8,16},{16,24},{24,0},{1,9},{9,17},{17,25},{25,1},{2,10},{10... | collective-permute-start | bytes 1032200 | tf_op jit(solution)/shard_map/ppermute | solution.py:28
  6.2 0.0 copy-done.4
  6.2 3.3 %pack.1 = (bf16[64,4864]{1,0:T(8,128)(2,1)S(1)}, bf16[64,4864]{1,0:T(8,128)(2,1)S(1)}, bf16[64,4864]{1,0:T(8,128)(2,1)S(1)}, bf16[64,4864]{1,0:T(8,128)(2,1)S(1)}) custom-call(bf16[4,8,8,4608]{3,2,1,0:T(8,128)(2,1)} %bitcast.10, bf16[4,8,8,160]{3,2,1,0:T(8,128)(2,1)S(1)} %bitcast.9, s32[8,8]{1,0:T(8,128)S(1)} %copy-done.4), custom_call_target="tpu_custom_call" | custom-call | tf_op jit(solution)/shard_map/pack/pallas_call | solution.py:429
  9.6 0.7 collective-permute-start.2
  10.3 1.9 %collective-permute-start.3 = (bf16[64,4864]{1,0:T(8,128)(2,1)S(1)}, bf16[64,4864]{1,0:T(8,128)(2,1)S(1)}, u32[]{:S(2)}, u32[]{:S(2)}) collective-permute-start(bf16[64,4864]{1,0:T(8,128)(2,1)S(1)} %get-tuple-element.45), channel_id=1, source_target_pairs={{0,7},{1,6},{2,1},{3,0},{4,3},{5,2},{6,5},{7,4},{8,15},{9,14},{10,... | collective-permute-start | bytes 1867784 | tf_op jit(solution)/shard_map/ppermute | solution.py:451
  12.2 4.4 %collective-permute-done.refs_8_.refs_3_ = bf16[112,1536]{1,0:T(8,128)(2,1)S(1)} collective-permute-done((bf16[112,1536]{1,0:T(8,128)(2,1)}, bf16[112,1536]{1,0:T(8,128)(2,1)S(1)}, u32[]{:S(2)}, u32[]{:S(2)}) %collective-permute-start) | collective-permute-done | bytes 344096 | tf_op jit(solution)/shard_map/ppermute | solution.py:28
  16.5 0.0 collective-permute-start.1
  16.5 11.0 %collective-permute-done.1.refs_12_.refs_7_ = bf16[112,1536]{1,0:T(8,128)(2,1)S(1)} collective-permute-done((bf16[112,1536]{1,0:T(8,128)(2,1)S(1)}, bf16[112,1536]{1,0:T(8,128)(2,1)S(1)}, u32[]{:S(2)}, u32[]{:S(2)}) %collective-permute-start.1) | collective-permute-done | bytes 344096 | tf_op jit(solution)/shard_map/ppermute | solution.py:28
  27.6 1.3 %collective-permute-start.5 = (bf16[112,1536]{1,0:T(8,128)(2,1)S(1)}, bf16[112,1536]{1,0:T(8,128)(2,1)S(1)}, u32[]{:S(2)}, u32[]{:S(2)}) collective-permute-start(bf16[112,1536]{1,0:T(8,128)(2,1)S(1)} %collective-permute-done.1.refs_12_.refs_7_), channel_id=1, source_target_pairs={{0,4},{2,6},{4,0},{6,2},{1,5},{3,7},{5,1},{7,3},{8,12},{10,14},{12... | collective-permute-start | bytes 1032200 | tf_op jit(solution)/shard_map/ppermute | solution.py:399
  28.8 0.0 collective-permute-done.2.refs_2_.refs_3_
  28.8 0.0 collective-permute-done.3.refs_3_.refs_4_
  28.8 1.5 %collective-permute-start.4 = (bf16[64,4864]{1,0:T(8,128)(2,1)S(1)}, bf16[64,4864]{1,0:T(8,128)(2,1)S(1)}, u32[]{:S(2)}, u32[]{:S(2)}) collective-permute-start(bf16[64,4864]{1,0:T(8,128)(2,1)S(1)} %get-tuple-element.46), channel_id=1, source_target_pairs={{0,1},{1,0},{2,3},{3,2},{4,5},{5,4},{6,7},{7,6},{8,9},{9,8},{10,11... | collective-permute-start | bytes 1867784 | tf_op jit(solution)/shard_map/ppermute | solution.py:28
  30.3 0.0 collective-permute-start.12
  30.3 5.6 %collective-permute-done.5.refs_13_.refs_8_ = bf16[112,1536]{1,0:T(8,128)(2,1)S(1)} collective-permute-done((bf16[112,1536]{1,0:T(8,128)(2,1)S(1)}, bf16[112,1536]{1,0:T(8,128)(2,1)S(1)}, u32[]{:S(2)}, u32[]{:S(2)}) %collective-permute-start.5) | collective-permute-done | bytes 344096 | tf_op jit(solution)/shard_map/ppermute | solution.py:399
  35.9 1.2 %collective-permute-start.6 = (bf16[112,1536]{1,0:T(8,128)(2,1)S(1)}, bf16[112,1536]{1,0:T(8,128)(2,1)S(1)}, u32[]{:S(2)}, u32[]{:S(2)}) collective-permute-start(bf16[112,1536]{1,0:T(8,128)(2,1)S(1)} %collective-permute-done.refs_8_.refs_3_), channel_id=1, source_target_pairs={{0,4},{2,6},{4,0},{6,2},{1,5},{3,7},{5,1},{7,3},{8,12},{10,14},{12... | collective-permute-start | bytes 1032200 | tf_op jit(solution)/shard_map/ppermute | solution.py:399
  37.1 0.0 collective-permute-start.7
  37.1 0.0 collective-permute-start.8
  37.1 3.0 %collective-permute-done.12.refs_16_.refs_11_ = bf16[112,1536]{1,0:T(8,128)(2,1)S(1)} collective-permute-done((bf16[112,1536]{1,0:T(8,128)(2,1)S(1)}, bf16[112,1536]{1,0:T(8,128)(2,1)S(1)}, u32[]{:S(2)}, u32[]{:S(2)}) %collective-permute-start.12) | collective-permute-done | bytes 344096 | tf_op jit(solution)/shard_map/ppermute | solution.py:28
  40.0 0.0 collective-permute-start.13
  40.0 3.0 %collective-permute-done.4.refs_1_.refs_2_ = bf16[64,4864]{1,0:T(8,128)(2,1)S(1)} collective-permute-done((bf16[64,4864]{1,0:T(8,128)(2,1)S(1)}, bf16[64,4864]{1,0:T(8,128)(2,1)S(1)}, u32[]{:S(2)}, u32[]{:S(2)}) %collective-permute-start.4) | collective-permute-done | bytes 622624 | tf_op jit(solution)/shard_map/ppermute | solution.py:28
  43.0 0.3 collective-permute-done.6.refs_9_.refs_4_
  43.3 0.0 collective-permute-done.7.refs_15_.refs_10_
  43.3 0.0 copy-start.5
  43.3 0.0 copy-start.6
  43.3 0.1 collective-permute-start.9
  43.4 0.5 collective-permute-start.10
  43.9 0.1 collective-permute-start.11
  44.0 2.8 %attention.1.refs_0_ = bf16[256,1536]{1,0:T(8,128)(2,1)S(1)} custom-call(bf16[64,4864]{1,0:T(8,128)(2,1)S(1)} %get-tuple-element.51.refs_0_.refs_1_, bf16[64,4864]{1,0:T(8,128)(2,1)S(1)} %collective-permute-done.4.refs_1_.refs_2_, bf16[64,4864]{1,0:T(8,128)(2,1)S(1)} %collective-permute-done.2.refs_2_.refs_3_, ...), custom_call_target="tpu_custom_call" | custom-call | tf_op jit(solution)/shard_map/attention/pallas_call | solution.py:465
  46.8 2.5 %collective-permute-done.8.refs_17_.refs_12_ = bf16[112,1536]{1,0:T(8,128)(2,1)S(1)} collective-permute-done((bf16[112,1536]{1,0:T(8,128)(2,1)S(1)}, bf16[112,1536]{1,0:T(8,128)(2,1)S(1)}, u32[]{:S(2)}, u32[]{:S(2)}) %collective-permute-start.8) | collective-permute-done | bytes 344096 | tf_op jit(solution)/shard_map/ppermute | solution.py:28
  49.3 0.0 collective-permute-start.14
  49.4 0.0 collective-permute-done.13.refs_18_.refs_13_
  49.4 0.0 collective-permute-done.9.refs_10_.refs_5_
  49.4 0.0 collective-permute-done.10.refs_11_.refs_6_
  49.4 0.0 collective-permute-done.11.refs_14_.refs_9_
  49.4 1.6 %collective-permute-done.14.refs_19_.refs_14_ = bf16[112,1536]{1,0:T(8,128)(2,1)S(1)} collective-permute-done((bf16[112,1536]{1,0:T(8,128)(2,1)S(1)}, bf16[112,1536]{1,0:T(8,128)(2,1)S(1)}, u32[]{:S(2)}, u32[]{:S(2)}) %collective-permute-start.14) | collective-permute-done | bytes 344096 | tf_op jit(solution)/shard_map/ppermute | solution.py:399
  51.0 0.0 copy-done.5
  51.0 0.0 copy-done.6
  51.0 3.7 %forward.1 = (bf16[40,1536]{1,0:T(8,128)(2,1)S(1)}, bf16[40,1536]{1,0:T(8,128)(2,1)S(1)}, bf16[40,1536]{1,0:T(8,128)(2,1)S(1)}, bf16[40,1536]{1,0:T(8,128)(2,1)S...) custom-call(f32[32]{0:T(128)S(1)} %copy-done.6, ...), custom_call_target="tpu_custom_call" | custom-call | tf_op jit(solution)/shard_map/forward/pallas_call | solution.py:486
  54.7 0.2 collective-permute-start.15
  54.9 0.9 %collective-permute-start.16 = (bf16[40,1536]{1,0:T(8,128)(2,1)S(1)}, bf16[40,1536]{1,0:T(8,128)(2,1)S(1)}, u32[]{:S(2)}, u32[]{:S(2)}) collective-permute-start(bf16[40,1536]{1,0:T(8,128)(2,1)S(1)} %get-tuple-element.64), channel_id=1, source_target_pairs={{0,4},{2,6},{4,0},{6,2},{1,5},{3,7},{5,1},{7,3},{8,12},{10,14},{12... | collective-permute-start | bytes 368648 | tf_op jit(solution)/shard_map/ppermute | solution.py:399
  55.8 0.9 %collective-permute-start.17 = (bf16[40,1536]{1,0:T(8,128)(2,1)S(1)}, bf16[40,1536]{1,0:T(8,128)(2,1)S(1)}, u32[]{:S(2)}, u32[]{:S(2)}) collective-permute-start(bf16[40,1536]{1,0:T(8,128)(2,1)S(1)} %get-tuple-element.65), channel_id=1, source_target_pairs={{0,6},{2,4},{4,2},{6,0},{1,7},{3,5},{5,3},{7,1},{8,14},{10,12},{12... | collective-permute-start | bytes 368648 | tf_op jit(solution)/shard_map/ppermute | solution.py:399
  56.7 3.6 %backward.1 = bf16[256,1536]{1,0:T(8,128)(2,1)} custom-call(f32[256,1536]{1,0:T(8,128)S(1)} %get-tuple-element.66.normed_ref, f32[256,128]{1,0:T(8,128)S(1)} %get-tuple-element.67.inv_ref, bf16[256,160]{1,0:T(8,128)(2,1)S(1)} %get-tuple-element.68.dfc_ref, bf16[384,1536]{1,0:T(8,128)(2,1)S(1)} %copy-done, bf16[160,384]{1,0:T(8,128)(2,1)S(1)} %bitcast.8, ...), custom_call_target="tpu_custom_call" | custom-call | tf_op jit(solution)/shard_map/backward/pallas_call | solution.py:502
  60.3 0.0 collective-permute-done.15.b
  60.3 0.8 collective-permute-done.16.c
  61.1 1.5 %collective-permute-done.17.d = bf16[40,1536]{1,0:T(8,128)(2,1)S(1)} collective-permute-done((bf16[40,1536]{1,0:T(8,128)(2,1)S(1)}, bf16[40,1536]{1,0:T(8,128)(2,1)S(1)}, u32[]{:S(2)}, u32[]{:S(2)}) %collective-permute-start.17) | collective-permute-done | bytes 122912 | tf_op jit(solution)/shard_map/ppermute | solution.py:399
  62.6 0.1 lat_sum.1
  62.7 0.1 collective-permute-start.18
  62.8 0.1 collective-permute-start.19
  62.9 4.3 %collective-permute-start.20 = (bf16[40,384]{1,0:T(8,128)(2,1)S(1)}, bf16[40,384]{1,0:T(8,128)(2,1)S(1)}, u32[]{:S(2)}, u32[]{:S(2)}) collective-permute-start(bf16[40,384]{1,0:T(8,128)(2,1)S(1)} %get-tuple-element.78), channel_id=1, source_target_pairs={{0,24},{8,16},{16,8},{24,0},{1,25},{9,17},{17,9},{25,1},{2,26},{10... | collective-permute-start | bytes 92168 | tf_op jit(solution)/shard_map/ppermute | solution.py:399
  67.2 0.0 collective-permute-done.18.b
  67.2 0.5 collective-permute-done.19.c
  67.7 1.7 %collective-permute-done.20.d = bf16[40,384]{1,0:T(8,128)(2,1)S(1)} collective-permute-done((bf16[40,384]{1,0:T(8,128)(2,1)S(1)}, bf16[40,384]{1,0:T(8,128)(2,1)S(1)}, u32[]{:S(2)}, u32[]{:S(2)}) %collective-permute-start.20) | collective-permute-done | bytes 30752 | tf_op jit(solution)/shard_map/ppermute | solution.py:399
  69.5 0.1 collective-permute-start.21
  69.6 1.2 %collective-permute-done.21.other_ref = bf16[48,384]{1,0:T(8,128)(2,1)S(1)} collective-permute-done((bf16[48,384]{1,0:T(8,128)(2,1)S(1)}, bf16[48,384]{1,0:T(8,128)(2,1)S(1)}, u32[]{:S(2)}, u32[]{:S(2)}) %collective-permute-start.21) | collective-permute-done | bytes 36896 | tf_op jit(solution)/shard_map/ppermute | solution.py:399
  70.8 1.5 %collective-permute-start.24 = (bf16[96,384]{1,0:T(8,128)(2,1)S(1)}, bf16[96,384]{1,0:T(8,128)(2,1)S(1)}, u32[]{:S(2)}, u32[]{:S(2)}) collective-permute-start(bf16[96,384]{1,0:T(8,128)(2,1)S(1)} %pair.1.refs_0_), channel_id=1, source_target_pairs={{0,5},{1,4},{2,7},{3,6},{4,1},{5,0},{6,3},{7,2},{8,13},{9,12},{10,... | collective-permute-start | bytes 221192 | tf_op jit(solution)/shard_map/ppermute | solution.py:542
  72.3 1.5 %collective-permute-start.23 = (bf16[96,384]{1,0:T(8,128)(2,1)S(1)}, bf16[96,384]{1,0:T(8,128)(2,1)S(1)}, u32[]{:S(2)}, u32[]{:S(2)}) collective-permute-start(bf16[96,384]{1,0:T(8,128)(2,1)S(1)} %pair.1.refs_0_), channel_id=1, source_target_pairs={{0,4},{1,5},{2,6},{3,7},{4,0},{5,1},{6,2},{7,3},{8,12},{9,13},{10,... | collective-permute-start | bytes 221192 | tf_op jit(solution)/shard_map/ppermute | solution.py:542
  73.8 0.5 collective-permute-start.22
  74.4 2.0 %collective-permute-done.24.refs_3_ = bf16[96,384]{1,0:T(8,128)(2,1)S(1)} collective-permute-done((bf16[96,384]{1,0:T(8,128)(2,1)S(1)}, bf16[96,384]{1,0:T(8,128)(2,1)S(1)}, u32[]{:S(2)}, u32[]{:S(2)}) %collective-permute-start.24) | collective-permute-done | bytes 73760 | tf_op jit(solution)/shard_map/ppermute | solution.py:542
  76.3 1.3 %collective-permute-done.23.refs_2_ = bf16[96,384]{1,0:T(8,128)(2,1)S(1)} collective-permute-done((bf16[96,384]{1,0:T(8,128)(2,1)S(1)}, bf16[96,384]{1,0:T(8,128)(2,1)S(1)}, u32[]{:S(2)}, u32[]{:S(2)}) %collective-permute-start.23) | collective-permute-done | bytes 73760 | tf_op jit(solution)/shard_map/ppermute | solution.py:542
  77.7 0.5 collective-permute-done.22.refs_1_
  78.2 0.7 join.1
  (9 shorter events, 0.1 us)
Async XLA Ops:
  0.6 5.6 %copy-start.4 = (s32[8,8]{1,0:T(8,128)S(1)}, s32[8,8]{1,0:T(8,128)}, u32[]{:S(2)}) copy-start(s32[8,8]{1,0:T(8,128)} %valid_ref.1) | copy-start | bytes 772
  0.6 5.6 %copy-start.2 = (bf16[1,4,8,8,160]{4,3,2,1,0:T(8,128)(2,1)S(1)}, bf16[1,4,8,8,160]{4,3,2,1,0:T(8,128)(2,1)}, u32[]{:S(2)}) copy-start(bf16[1,4,8,8,160]{4,3,2,1,0:T(8,128)(2,1)} %param.9) | copy-start | bytes 245764
  3.1 13.4 %collective-permute-start = (bf16[112,1536]{1,0:T(8,128)(2,1)}, bf16[112,1536]{1,0:T(8,128)(2,1)S(1)}, u32[]{:S(2)}, u32[]{:S(2)}) collective-permute-start(bf16[112,1536]{1,0:T(8,128)(2,1)} %payload.1), channel_id=1, source_target_pairs={{0,8},{8,16},{16,24},{24,0},{1,9},{9,17},{17,25},{25,1},{2,10},{10... | collective-permute-start | bytes 1032200 | tf_op jit(solution)/shard_map/ppermute | solution.py:28
  9.6 19.3 %collective-permute-start.2 = (bf16[64,4864]{1,0:T(8,128)(2,1)S(1)}, bf16[64,4864]{1,0:T(8,128)(2,1)S(1)}, u32[]{:S(2)}, u32[]{:S(2)}) collective-permute-start(bf16[64,4864]{1,0:T(8,128)(2,1)S(1)} %get-tuple-element.44), channel_id=1, source_target_pairs={{0,6},{2,0},{4,2},{6,4},{1,7},{3,1},{5,3},{7,5},{8,14},{10,8},{12,... | collective-permute-start | bytes 1867784 | tf_op jit(solution)/shard_map/ppermute | solution.py:28
  10.3 18.6 %collective-permute-start.3 = (bf16[64,4864]{1,0:T(8,128)(2,1)S(1)}, bf16[64,4864]{1,0:T(8,128)(2,1)S(1)}, u32[]{:S(2)}, u32[]{:S(2)}) collective-permute-start(bf16[64,4864]{1,0:T(8,128)(2,1)S(1)} %get-tuple-element.45), channel_id=1, source_target_pairs={{0,7},{1,6},{2,1},{3,0},{4,3},{5,2},{6,5},{7,4},{8,15},{9,14},{10,... | collective-permute-start | bytes 1867784 | tf_op jit(solution)/shard_map/ppermute | solution.py:451
  16.5 11.0 %collective-permute-start.1 = (bf16[112,1536]{1,0:T(8,128)(2,1)S(1)}, bf16[112,1536]{1,0:T(8,128)(2,1)S(1)}, u32[]{:S(2)}, u32[]{:S(2)}) collective-permute-start(bf16[112,1536]{1,0:T(8,128)(2,1)S(1)} %collective-permute-done.refs_8_.refs_3_), channel_id=1, source_target_pairs={{0,8},{8,16},{16,24},{24,0},{1,9},{9,17},{17,25},{25,1},{2,10},{10... | collective-permute-start | bytes 1032200 | tf_op jit(solution)/shard_map/ppermute | solution.py:28
  27.6 8.3 %collective-permute-start.5 = (bf16[112,1536]{1,0:T(8,128)(2,1)S(1)}, bf16[112,1536]{1,0:T(8,128)(2,1)S(1)}, u32[]{:S(2)}, u32[]{:S(2)}) collective-permute-start(bf16[112,1536]{1,0:T(8,128)(2,1)S(1)} %collective-permute-done.1.refs_12_.refs_7_), channel_id=1, source_target_pairs={{0,4},{2,6},{4,0},{6,2},{1,5},{3,7},{5,1},{7,3},{8,12},{10,14},{12... | collective-permute-start | bytes 1032200 | tf_op jit(solution)/shard_map/ppermute | solution.py:399
  28.8 14.2 %collective-permute-start.4 = (bf16[64,4864]{1,0:T(8,128)(2,1)S(1)}, bf16[64,4864]{1,0:T(8,128)(2,1)S(1)}, u32[]{:S(2)}, u32[]{:S(2)}) collective-permute-start(bf16[64,4864]{1,0:T(8,128)(2,1)S(1)} %get-tuple-element.46), channel_id=1, source_target_pairs={{0,1},{1,0},{2,3},{3,2},{4,5},{5,4},{6,7},{7,6},{8,9},{9,8},{10,11... | collective-permute-start | bytes 1867784 | tf_op jit(solution)/shard_map/ppermute | solution.py:28
  30.3 9.7 %collective-permute-start.12 = (bf16[112,1536]{1,0:T(8,128)(2,1)S(1)}, bf16[112,1536]{1,0:T(8,128)(2,1)S(1)}, u32[]{:S(2)}, u32[]{:S(2)}) collective-permute-start(bf16[112,1536]{1,0:T(8,128)(2,1)S(1)} %collective-permute-done.1.refs_12_.refs_7_), channel_id=1, source_target_pairs={{0,8},{8,16},{16,24},{24,0},{1,9},{9,17},{17,25},{25,1},{2,10},{10... | collective-permute-start | bytes 1032200 | tf_op jit(solution)/shard_map/ppermute | solution.py:28
  35.9 7.4 %collective-permute-start.6 = (bf16[112,1536]{1,0:T(8,128)(2,1)S(1)}, bf16[112,1536]{1,0:T(8,128)(2,1)S(1)}, u32[]{:S(2)}, u32[]{:S(2)}) collective-permute-start(bf16[112,1536]{1,0:T(8,128)(2,1)S(1)} %collective-permute-done.refs_8_.refs_3_), channel_id=1, source_target_pairs={{0,4},{2,6},{4,0},{6,2},{1,5},{3,7},{5,1},{7,3},{8,12},{10,14},{12... | collective-permute-start | bytes 1032200 | tf_op jit(solution)/shard_map/ppermute | solution.py:399
  37.1 6.2 %collective-permute-start.7 = (bf16[112,1536]{1,0:T(8,128)(2,1)S(1)}, bf16[112,1536]{1,0:T(8,128)(2,1)S(1)}, u32[]{:S(2)}, u32[]{:S(2)}) collective-permute-start(bf16[112,1536]{1,0:T(8,128)(2,1)S(1)} %collective-permute-done.5.refs_13_.refs_8_), channel_id=1, source_target_pairs={{0,2},{2,0},{4,6},{6,4},{1,3},{3,1},{5,7},{7,5},{8,10},{10,8},{12,... | collective-permute-start | bytes 1032200 | tf_op jit(solution)/shard_map/ppermute | solution.py:399
  37.1 12.3 %collective-permute-start.8 = (bf16[112,1536]{1,0:T(8,128)(2,1)S(1)}, bf16[112,1536]{1,0:T(8,128)(2,1)S(1)}, u32[]{:S(2)}, u32[]{:S(2)}) collective-permute-start(bf16[112,1536]{1,0:T(8,128)(2,1)S(1)} %collective-permute-done.5.refs_13_.refs_8_), channel_id=1, source_target_pairs={{0,8},{8,16},{16,24},{24,0},{1,9},{9,17},{17,25},{25,1},{2,10},{10... | collective-permute-start | bytes 1032200 | tf_op jit(solution)/shard_map/ppermute | solution.py:28
  40.0 9.3 %collective-permute-start.13 = (bf16[112,1536]{1,0:T(8,128)(2,1)S(1)}, bf16[112,1536]{1,0:T(8,128)(2,1)S(1)}, u32[]{:S(2)}, u32[]{:S(2)}) collective-permute-start(bf16[112,1536]{1,0:T(8,128)(2,1)S(1)} %collective-permute-done.12.refs_16_.refs_11_), channel_id=1, source_target_pairs={{0,2},{2,0},{4,6},{6,4},{1,3},{3,1},{5,7},{7,5},{8,10},{10,8},{12,... | collective-permute-start | bytes 1032200 | tf_op jit(solution)/shard_map/ppermute | solution.py:399
  43.3 7.7 %copy-start = (bf16[384,1536]{1,0:T(8,128)(2,1)S(1)}, bf16[384,1536]{1,0:T(8,128)(2,1)}, u32[]{:S(2)}) copy-start(bf16[384,1536]{1,0:T(8,128)(2,1)} %refs_0_.1) | copy-start | bytes 3538948
  43.3 7.7 %copy-start.1 = (bf16[384,160]{0,1:T(8,128)(2,1)S(1)}, bf16[384,160]{0,1:T(8,128)(2,1)}, u32[]{:S(2)}) copy-start(bf16[384,160]{0,1:T(8,128)(2,1)} %param.12) | copy-start | bytes 368644
  43.3 7.7 %copy-start.3 = (bf16[384]{0:T(512)(128)(2,1)S(1)}, bf16[384]{0:T(512)(128)(2,1)}, u32[]{:S(2)}) copy-start(bf16[384]{0:T(512)(128)(2,1)} %refs_2_.1) | copy-start | bytes 2308
  43.3 7.7 %copy-start.5 = (f32[5]{0:T(128)S(1)}, f32[5]{0:T(128)}, u32[]{:S(2)}) copy-start(f32[5]{0:T(128)} %var_ref.1) | copy-start | bytes 64
  43.3 7.7 %copy-start.6 = (f32[32]{0:T(128)S(1)}, f32[32]{0:T(128)}, u32[]{:S(2)}) copy-start(f32[32]{0:T(128)} %constant.2.clone.lat_ref) | copy-start | bytes 388
  43.3 6.0 %collective-permute-start.9 = (bf16[112,1536]{1,0:T(8,128)(2,1)S(1)}, bf16[112,1536]{1,0:T(8,128)(2,1)S(1)}, u32[]{:S(2)}, u32[]{:S(2)}) collective-permute-start(bf16[112,1536]{1,0:T(8,128)(2,1)S(1)} %collective-permute-done.refs_8_.refs_3_), channel_id=1, source_target_pairs={{0,2},{2,0},{4,6},{6,4},{1,3},{3,1},{5,7},{7,5},{8,10},{10,8},{12,... | collective-permute-start | bytes 1032200 | tf_op jit(solution)/shard_map/ppermute | solution.py:399
  43.4 5.9 %collective-permute-start.10 = (bf16[112,1536]{1,0:T(8,128)(2,1)S(1)}, bf16[112,1536]{1,0:T(8,128)(2,1)S(1)}, u32[]{:S(2)}, u32[]{:S(2)}) collective-permute-start(bf16[112,1536]{1,0:T(8,128)(2,1)S(1)} %collective-permute-done.6.refs_9_.refs_4_), channel_id=1, source_target_pairs={{0,2},{2,0},{4,6},{6,4},{1,3},{3,1},{5,7},{7,5},{8,10},{10,8},{12,... | collective-permute-start | bytes 1032200 | tf_op jit(solution)/shard_map/ppermute | solution.py:399
  43.9 5.5 %collective-permute-start.11 = (bf16[112,1536]{1,0:T(8,128)(2,1)S(1)}, bf16[112,1536]{1,0:T(8,128)(2,1)S(1)}, u32[]{:S(2)}, u32[]{:S(2)}) collective-permute-start(bf16[112,1536]{1,0:T(8,128)(2,1)S(1)} %collective-permute-done.1.refs_12_.refs_7_), channel_id=1, source_target_pairs={{0,2},{2,0},{4,6},{6,4},{1,3},{3,1},{5,7},{7,5},{8,10},{10,8},{12,... | collective-permute-start | bytes 1032200 | tf_op jit(solution)/shard_map/ppermute | solution.py:399
  49.3 1.7 %collective-permute-start.14 = (bf16[112,1536]{1,0:T(8,128)(2,1)S(1)}, bf16[112,1536]{1,0:T(8,128)(2,1)S(1)}, u32[]{:S(2)}, u32[]{:S(2)}) collective-permute-start(bf16[112,1536]{1,0:T(8,128)(2,1)S(1)} %collective-permute-done.8.refs_17_.refs_12_), channel_id=1, source_target_pairs={{0,2},{2,0},{4,6},{6,4},{1,3},{3,1},{5,7},{7,5},{8,10},{10,8},{12,... | collective-permute-start | bytes 1032200 | tf_op jit(solution)/shard_map/ppermute | solution.py:399
  54.7 5.6 %collective-permute-start.15 = (bf16[40,1536]{1,0:T(8,128)(2,1)S(1)}, bf16[40,1536]{1,0:T(8,128)(2,1)S(1)}, u32[]{:S(2)}, u32[]{:S(2)}) collective-permute-start(bf16[40,1536]{1,0:T(8,128)(2,1)S(1)} %get-tuple-element.63), channel_id=1, source_target_pairs={{0,2},{2,0},{4,6},{6,4},{1,3},{3,1},{5,7},{7,5},{8,10},{10,8},{12,... | collective-permute-start | bytes 368648 | tf_op jit(solution)/shard_map/ppermute | solution.py:399
  54.9 6.2 %collective-permute-start.16 = (bf16[40,1536]{1,0:T(8,128)(2,1)S(1)}, bf16[40,1536]{1,0:T(8,128)(2,1)S(1)}, u32[]{:S(2)}, u32[]{:S(2)}) collective-permute-start(bf16[40,1536]{1,0:T(8,128)(2,1)S(1)} %get-tuple-element.64), channel_id=1, source_target_pairs={{0,4},{2,6},{4,0},{6,2},{1,5},{3,7},{5,1},{7,3},{8,12},{10,14},{12... | collective-permute-start | bytes 368648 | tf_op jit(solution)/shard_map/ppermute | solution.py:399
  55.8 6.8 %collective-permute-start.17 = (bf16[40,1536]{1,0:T(8,128)(2,1)S(1)}, bf16[40,1536]{1,0:T(8,128)(2,1)S(1)}, u32[]{:S(2)}, u32[]{:S(2)}) collective-permute-start(bf16[40,1536]{1,0:T(8,128)(2,1)S(1)} %get-tuple-element.65), channel_id=1, source_target_pairs={{0,6},{2,4},{4,2},{6,0},{1,7},{3,5},{5,3},{7,1},{8,14},{10,12},{12... | collective-permute-start | bytes 368648 | tf_op jit(solution)/shard_map/ppermute | solution.py:399
  62.7 4.5 %collective-permute-start.18 = (bf16[40,384]{1,0:T(8,128)(2,1)S(1)}, bf16[40,384]{1,0:T(8,128)(2,1)S(1)}, u32[]{:S(2)}, u32[]{:S(2)}) collective-permute-start(bf16[40,384]{1,0:T(8,128)(2,1)S(1)} %get-tuple-element.76), channel_id=1, source_target_pairs={{0,8},{8,0},{16,24},{24,16},{1,9},{9,1},{17,25},{25,17},{2,10},{10... | collective-permute-start | bytes 92168 | tf_op jit(solution)/shard_map/ppermute | solution.py:399
  62.8 4.9 %collective-permute-start.19 = (bf16[40,384]{1,0:T(8,128)(2,1)S(1)}, bf16[40,384]{1,0:T(8,128)(2,1)S(1)}, u32[]{:S(2)}, u32[]{:S(2)}) collective-permute-start(bf16[40,384]{1,0:T(8,128)(2,1)S(1)} %get-tuple-element.77), channel_id=1, source_target_pairs={{0,16},{8,24},{16,0},{24,8},{1,17},{9,25},{17,1},{25,9},{2,18},{10... | collective-permute-start | bytes 92168 | tf_op jit(solution)/shard_map/ppermute | solution.py:399
  62.9 6.5 %collective-permute-start.20 = (bf16[40,384]{1,0:T(8,128)(2,1)S(1)}, bf16[40,384]{1,0:T(8,128)(2,1)S(1)}, u32[]{:S(2)}, u32[]{:S(2)}) collective-permute-start(bf16[40,384]{1,0:T(8,128)(2,1)S(1)} %get-tuple-element.78), channel_id=1, source_target_pairs={{0,24},{8,16},{16,8},{24,0},{1,25},{9,17},{17,9},{25,1},{2,26},{10... | collective-permute-start | bytes 92168 | tf_op jit(solution)/shard_map/ppermute | solution.py:399
  69.5 1.3 %collective-permute-start.21 = (bf16[48,384]{1,0:T(8,128)(2,1)S(1)}, bf16[48,384]{1,0:T(8,128)(2,1)S(1)}, u32[]{:S(2)}, u32[]{:S(2)}) collective-permute-start(bf16[48,384]{1,0:T(8,128)(2,1)S(1)} %dp_sum.1.mine_ref), channel_id=1, source_target_pairs={{0,2},{2,0},{4,6},{6,4},{1,3},{3,1},{5,7},{7,5},{8,10},{10,8},{12,... | collective-permute-start | bytes 110600 | tf_op jit(solution)/shard_map/ppermute | solution.py:399
  70.8 5.5 %collective-permute-start.24 = (bf16[96,384]{1,0:T(8,128)(2,1)S(1)}, bf16[96,384]{1,0:T(8,128)(2,1)S(1)}, u32[]{:S(2)}, u32[]{:S(2)}) collective-permute-start(bf16[96,384]{1,0:T(8,128)(2,1)S(1)} %pair.1.refs_0_), channel_id=1, source_target_pairs={{0,5},{1,4},{2,7},{3,6},{4,1},{5,0},{6,3},{7,2},{8,13},{9,12},{10,... | collective-permute-start | bytes 221192 | tf_op jit(solution)/shard_map/ppermute | solution.py:542
  72.3 5.4 %collective-permute-start.23 = (bf16[96,384]{1,0:T(8,128)(2,1)S(1)}, bf16[96,384]{1,0:T(8,128)(2,1)S(1)}, u32[]{:S(2)}, u32[]{:S(2)}) collective-permute-start(bf16[96,384]{1,0:T(8,128)(2,1)S(1)} %pair.1.refs_0_), channel_id=1, source_target_pairs={{0,4},{1,5},{2,6},{3,7},{4,0},{5,1},{6,2},{7,3},{8,12},{9,13},{10,... | collective-permute-start | bytes 221192 | tf_op jit(solution)/shard_map/ppermute | solution.py:542
  73.8 4.4 %collective-permute-start.22 = (bf16[96,384]{1,0:T(8,128)(2,1)S(1)}, bf16[96,384]{1,0:T(8,128)(2,1)S(1)}, u32[]{:S(2)}, u32[]{:S(2)}) collective-permute-start(bf16[96,384]{1,0:T(8,128)(2,1)S(1)} %pair.1.refs_0_), channel_id=1, source_target_pairs={{0,1},{1,0},{2,3},{3,2},{4,5},{5,4},{6,7},{7,6},{8,9},{9,8},{10,11... | collective-permute-start | bytes 221192 | tf_op jit(solution)/shard_map/ppermute | solution.py:542

commit v15 on v14

--- a/solution.py
+++ b/solution.py
@@ -458,10 +458,7 @@
     ring1_late, across2 = barrier((ring1, across2))
     across1 = swap(ring1_late, "lat", 2)
     tiles = [own, east, south, diag]
-    across2_swapped = swap(across2, "lat", 1)
-    *tiles, ring1, across1, ring2, across2_swapped = barrier(
-        (*tiles, ring1, across1, ring2, across2_swapped)
-    )
+    *tiles, ring1, across1, ring2 = barrier((*tiles, ring1, across1, ring2))
     ctx = pl.pallas_call(
         attention_kernel,
         out_shape=shape((tokens, width), BF),
@@ -471,9 +468,9 @@
         name="attention",
     )(*tiles)
     ctx, across3 = barrier((ctx, across3))
-    pieces = [ring1, across1, swap(ring1, "lat", 1), swap(across1, "lat", 1)]
-    pieces += [ring2, across2, swap(ring2, "lat", 1), across2_swapped]
-    pieces += [ring3, across3, swap(ring3, "lat", 1), swap(across3, "lat", 1)]
+    pieces = []
+    for ring, across in ((ring1, across1), (ring2, across2), (ring3, across3)):
+        pieces += [ring, across, swap(ring, "lat", 1), swap(across, "lat", 1)]
 
     piece = span // lat
     extra_specs = [

time: 79.1 us -> 78.4 us (level)
  waiting for transfers between devices: 40.9 us -> 39.8 us
    ppermute x6, waiting for transfers between devices: 23.9 us -> 22 us  [from_behind(): lax.ppermute(array, axis, [(i, (i + by) % length) for i in range(length)])]
  transfers between devices with their start and end apart: 25 -> 25, of which waited for: 16 -> 17; matrix products, arithmetic and copies ran while one was open for 0% -> 0% of each run, Pallas kernels for 12% -> 13%
where the time goes in v15:
time: 78.4 us; the launch traced here: 78.2 us
  waiting for transfers between devices  39.8 us (51%)
  starting transfers between devices  20.7 us (26%)
  Pallas kernels  16.9 us (22%)
    ppermute x6, waiting for transfers between devices, from_behind(): lax.ppermute(array, axis, [(i, (i + by) % length) for i in range(length)])  22 us
    ppermute x15, waiting for transfers between devices, swap(): lax.ppermute(array, axis, [(i, i ^ bit) for i in range(lax.axis_size(axis...  14 us
    ppermute x15, starting transfers between devices, swap(): lax.ppermute(array, axis, [(i, i ^ bit) for i in range(lax.axis_size(axis...  9.99 us
    ppermute x6, starting transfers between devices, from_behind(): lax.ppermute(array, axis, [(i, (i + by) % length) for i in range(length)])  5.31 us
    ppermute x3, waiting for transfers between devices, shards(): plane.append(lax.ppermute(chip, ('lat', 'lon'), pairs))  3.83 us
    pallas_call x1, Pallas kernels, shards(): pl.pallas_call(forward_kernel, grid=(1,), out_shape=[shape((piece, width)...  3.71 us
    pallas_call x1, Pallas kernels, shards(): pl.pallas_call(backward_kernel, out_shape=shape((tokens, width), BF), in_...  3.64 us
    ppermute x3, starting transfers between devices, shards(): plane.append(lax.ppermute(chip, ('lat', 'lon'), pairs))  3.55 us
  transfers between devices with their start and end apart: 25, of which 17 were waited for; matrix products, arithmetic and copies ran while one was open for 0% of the time, Pallas kernels for 13%

profile of v15, /device:TPU:0, one launch (start us, length us, event | category | flops | bytes accessed | tf_op | source)
XLA Modules:
  0.0 78.2 jit_solution(16932425394682454918)
XLA Ops:
  0.6 0.0 copy-start.4
  0.6 0.0 copy-start.2
  0.7 2.5 %payload.1 = bf16[112,1536]{1,0:T(8,128)(2,1)} custom-call(bf16[384,1536]{1,0:T(8,128)(2,1)} %refs_0_.1, bf16[160,384]{1,0:T(8,128)(2,1)} %bitcast.6, bf16[384]{0:T(512)(128)(2,1)} %refs_2_.1), custom_call_target="tpu_custom_call" | custom-call | tf_op jit(solution)/shard_map/payload/pallas_call | solution.py:419
  3.1 3.1 %collective-permute-start = (bf16[112,1536]{1,0:T(8,128)(2,1)}, bf16[112,1536]{1,0:T(8,128)(2,1)S(1)}, u32[]{:S(2)}, u32[]{:S(2)}) collective-permute-start(bf16[112,1536]{1,0:T(8,128)(2,1)} %payload.1), channel_id=1, source_target_pairs={{0,8},{8,16},{16,24},{24,0},{1,9},{9,17},{17,25},{25,1},{2,10},{10... | collective-permute-start | bytes 1032200 | tf_op jit(solution)/shard_map/ppermute | solution.py:28
  6.2 0.0 copy-done.4
  6.2 0.0 copy-done.2
  6.2 3.3 %pack.1 = (bf16[64,4864]{1,0:T(8,128)(2,1)S(1)}, bf16[64,4864]{1,0:T(8,128)(2,1)S(1)}, bf16[64,4864]{1,0:T(8,128)(2,1)S(1)}, bf16[64,4864]{1,0:T(8,128)(2,1)S(1)}) custom-call(bf16[4,8,8,4608]{3,2,1,0:T(8,128)(2,1)} %bitcast.10, bf16[4,8,8,160]{3,2,1,0:T(8,128)(2,1)S(1)} %bitcast.9, s32[8,8]{1,0:T(8,128)S(1)} %copy-done.4), custom_call_target="tpu_custom_call" | custom-call | tf_op jit(solution)/shard_map/pack/pallas_call | solution.py:429
  9.6 0.7 collective-permute-start.2
  10.3 1.9 %collective-permute-start.3 = (bf16[64,4864]{1,0:T(8,128)(2,1)S(1)}, bf16[64,4864]{1,0:T(8,128)(2,1)S(1)}, u32[]{:S(2)}, u32[]{:S(2)}) collective-permute-start(bf16[64,4864]{1,0:T(8,128)(2,1)S(1)} %get-tuple-element.44), channel_id=1, source_target_pairs={{0,7},{1,6},{2,1},{3,0},{4,3},{5,2},{6,5},{7,4},{8,15},{9,14},{10,... | collective-permute-start | bytes 1867784 | tf_op jit(solution)/shard_map/ppermute | solution.py:451
  12.2 4.4 %collective-permute-done.refs_8_.refs_3_ = bf16[112,1536]{1,0:T(8,128)(2,1)S(1)} collective-permute-done((bf16[112,1536]{1,0:T(8,128)(2,1)}, bf16[112,1536]{1,0:T(8,128)(2,1)S(1)}, u32[]{:S(2)}, u32[]{:S(2)}) %collective-permute-start) | collective-permute-done | bytes 344096 | tf_op jit(solution)/shard_map/ppermute | solution.py:28
  16.5 0.0 collective-permute-start.1
  16.5 11.0 %collective-permute-done.1.refs_12_.refs_7_ = bf16[112,1536]{1,0:T(8,128)(2,1)S(1)} collective-permute-done((bf16[112,1536]{1,0:T(8,128)(2,1)S(1)}, bf16[112,1536]{1,0:T(8,128)(2,1)S(1)}, u32[]{:S(2)}, u32[]{:S(2)}) %collective-permute-start.1) | collective-permute-done | bytes 344096 | tf_op jit(solution)/shard_map/ppermute | solution.py:28
  27.6 1.3 %collective-permute-start.5 = (bf16[112,1536]{1,0:T(8,128)(2,1)S(1)}, bf16[112,1536]{1,0:T(8,128)(2,1)S(1)}, u32[]{:S(2)}, u32[]{:S(2)}) collective-permute-start(bf16[112,1536]{1,0:T(8,128)(2,1)S(1)} %collective-permute-done.1.refs_12_.refs_7_), channel_id=1, source_target_pairs={{0,4},{2,6},{4,0},{6,2},{1,5},{3,7},{5,1},{7,3},{8,12},{10,14},{12... | collective-permute-start | bytes 1032200 | tf_op jit(solution)/shard_map/ppermute | solution.py:399
  28.8 0.0 collective-permute-done.2.refs_2_.refs_3_
  28.8 0.0 collective-permute-done.3.refs_3_.refs_4_
  28.8 1.5 %collective-permute-start.4 = (bf16[64,4864]{1,0:T(8,128)(2,1)S(1)}, bf16[64,4864]{1,0:T(8,128)(2,1)S(1)}, u32[]{:S(2)}, u32[]{:S(2)}) collective-permute-start(bf16[64,4864]{1,0:T(8,128)(2,1)S(1)} %get-tuple-element.45), channel_id=1, source_target_pairs={{0,1},{1,0},{2,3},{3,2},{4,5},{5,4},{6,7},{7,6},{8,9},{9,8},{10,11... | collective-permute-start | bytes 1867784 | tf_op jit(solution)/shard_map/ppermute | solution.py:28
  30.3 0.0 collective-permute-start.12
  30.3 5.6 %collective-permute-done.5.refs_13_.refs_8_ = bf16[112,1536]{1,0:T(8,128)(2,1)S(1)} collective-permute-done((bf16[112,1536]{1,0:T(8,128)(2,1)S(1)}, bf16[112,1536]{1,0:T(8,128)(2,1)S(1)}, u32[]{:S(2)}, u32[]{:S(2)}) %collective-permute-start.5) | collective-permute-done | bytes 344096 | tf_op jit(solution)/shard_map/ppermute | solution.py:399
  35.9 1.2 %collective-permute-start.6 = (bf16[112,1536]{1,0:T(8,128)(2,1)S(1)}, bf16[112,1536]{1,0:T(8,128)(2,1)S(1)}, u32[]{:S(2)}, u32[]{:S(2)}) collective-permute-start(bf16[112,1536]{1,0:T(8,128)(2,1)S(1)} %collective-permute-done.refs_8_.refs_3_), channel_id=1, source_target_pairs={{0,4},{2,6},{4,0},{6,2},{1,5},{3,7},{5,1},{7,3},{8,12},{10,14},{12... | collective-permute-start | bytes 1032200 | tf_op jit(solution)/shard_map/ppermute | solution.py:399
  37.1 0.0 collective-permute-start.7
  37.1 0.0 collective-permute-start.11
  37.1 4.7 %collective-permute-done.12.refs_16_.refs_11_ = bf16[112,1536]{1,0:T(8,128)(2,1)S(1)} collective-permute-done((bf16[112,1536]{1,0:T(8,128)(2,1)S(1)}, bf16[112,1536]{1,0:T(8,128)(2,1)S(1)}, u32[]{:S(2)}, u32[]{:S(2)}) %collective-permute-start.12) | collective-permute-done | bytes 344096 | tf_op jit(solution)/shard_map/ppermute | solution.py:28
  41.8 0.0 collective-permute-start.13
  41.8 1.2 %collective-permute-done.4.refs_1_.refs_2_ = bf16[64,4864]{1,0:T(8,128)(2,1)S(1)} collective-permute-done((bf16[64,4864]{1,0:T(8,128)(2,1)S(1)}, bf16[64,4864]{1,0:T(8,128)(2,1)S(1)}, u32[]{:S(2)}, u32[]{:S(2)}) %collective-permute-start.4) | collective-permute-done | bytes 622624 | tf_op jit(solution)/shard_map/ppermute | solution.py:28
  43.0 0.3 collective-permute-done.6.refs_9_.refs_4_
  43.3 0.0 copy-start.6
  43.3 0.1 collective-permute-start.8
  43.4 0.5 collective-permute-start.9
  43.9 2.8 %attention.1.refs_0_ = bf16[256,1536]{1,0:T(8,128)(2,1)S(1)} custom-call(bf16[64,4864]{1,0:T(8,128)(2,1)S(1)} %get-tuple-element.49.refs_0_.refs_1_, bf16[64,4864]{1,0:T(8,128)(2,1)S(1)} %collective-permute-done.4.refs_1_.refs_2_, bf16[64,4864]{1,0:T(8,128)(2,1)S(1)} %collective-permute-done.2.refs_2_.refs_3_, ...), custom_call_target="tpu_custom_call" | custom-call | tf_op jit(solution)/shard_map/attention/pallas_call | solution.py:462
  46.7 0.7 collective-permute-done.7.refs_17_.refs_12_
  47.4 0.0 collective-permute-start.10
  47.4 0.0 collective-permute-done.11.refs_15_.refs_10_
  47.4 0.5 collective-permute-start.14
  47.9 0.0 collective-permute-done.13.refs_18_.refs_13_
  47.9 0.0 collective-permute-done.8.refs_10_.refs_5_
  47.9 0.0 collective-permute-done.9.refs_11_.refs_6_
  47.9 1.1 %collective-permute-done.10.refs_14_.refs_9_ = bf16[112,1536]{1,0:T(8,128)(2,1)S(1)} collective-permute-done((bf16[112,1536]{1,0:T(8,128)(2,1)S(1)}, bf16[112,1536]{1,0:T(8,128)(2,1)S(1)}, u32[]{:S(2)}, u32[]{:S(2)}) %collective-permute-start.10) | collective-permute-done | bytes 344096 | tf_op jit(solution)/shard_map/ppermute | solution.py:399
  49.1 0.5 collective-permute-done.14.refs_19_.refs_14_
  49.6 0.0 copy-done.5
  49.6 0.0 copy-done.6
  49.6 3.7 %forward.1 = (bf16[40,1536]{1,0:T(8,128)(2,1)S(1)}, bf16[40,1536]{1,0:T(8,128)(2,1)S(1)}, bf16[40,1536]{1,0:T(8,128)(2,1)S(1)}, bf16[40,1536]{1,0:T(8,128)(2,1)S...) custom-call(f32[32]{0:T(128)S(1)} %copy-done.6, ...), custom_call_target="tpu_custom_call" | custom-call | tf_op jit(solution)/shard_map/forward/pallas_call | solution.py:483
  53.3 0.2 collective-permute-start.15
  53.5 1.1 %collective-permute-start.16 = (bf16[40,1536]{1,0:T(8,128)(2,1)S(1)}, bf16[40,1536]{1,0:T(8,128)(2,1)S(1)}, u32[]{:S(2)}, u32[]{:S(2)}) collective-permute-start(bf16[40,1536]{1,0:T(8,128)(2,1)S(1)} %get-tuple-element.62), channel_id=1, source_target_pairs={{0,4},{2,6},{4,0},{6,2},{1,5},{3,7},{5,1},{7,3},{8,12},{10,14},{12... | collective-permute-start | bytes 368648 | tf_op jit(solution)/shard_map/ppermute | solution.py:399
  54.6 0.6 collective-permute-start.17
  55.2 3.6 %backward.1 = bf16[256,1536]{1,0:T(8,128)(2,1)} custom-call(f32[256,1536]{1,0:T(8,128)S(1)} %get-tuple-element.64.normed_ref, f32[256,128]{1,0:T(8,128)S(1)} %get-tuple-element.65.inv_ref, bf16[256,160]{1,0:T(8,128)(2,1)S(1)} %get-tuple-element.66.dfc_ref, bf16[384,1536]{1,0:T(8,128)(2,1)S(1)} %copy-done, bf16[160,384]{1,0:T(8,128)(2,1)S(1)} %bitcast.8, ...), custom_call_target="tpu_custom_call" | custom-call | tf_op jit(solution)/shard_map/backward/pallas_call | solution.py:499
  58.9 0.0 collective-permute-done.15.b
  58.9 0.8 collective-permute-done.16.c
  59.7 1.5 %collective-permute-done.17.d = bf16[40,1536]{1,0:T(8,128)(2,1)S(1)} collective-permute-done((bf16[40,1536]{1,0:T(8,128)(2,1)S(1)}, bf16[40,1536]{1,0:T(8,128)(2,1)S(1)}, u32[]{:S(2)}, u32[]{:S(2)}) %collective-permute-start.17) | collective-permute-done | bytes 122912 | tf_op jit(solution)/shard_map/ppermute | solution.py:399
  61.2 0.1 lat_sum.1
  61.3 0.2 collective-permute-start.18
  61.5 1.5 %collective-permute-start.19 = (bf16[40,384]{1,0:T(8,128)(2,1)S(1)}, bf16[40,384]{1,0:T(8,128)(2,1)S(1)}, u32[]{:S(2)}, u32[]{:S(2)}) collective-permute-start(bf16[40,384]{1,0:T(8,128)(2,1)S(1)} %get-tuple-element.75), channel_id=1, source_target_pairs={{0,16},{8,24},{16,0},{24,8},{1,17},{9,25},{17,1},{25,9},{2,18},{10... | collective-permute-start | bytes 92168 | tf_op jit(solution)/shard_map/ppermute | solution.py:399
  63.0 2.7 %collective-permute-start.20 = (bf16[40,384]{1,0:T(8,128)(2,1)S(1)}, bf16[40,384]{1,0:T(8,128)(2,1)S(1)}, u32[]{:S(2)}, u32[]{:S(2)}) collective-permute-start(bf16[40,384]{1,0:T(8,128)(2,1)S(1)} %get-tuple-element.76), channel_id=1, source_target_pairs={{0,24},{8,16},{16,8},{24,0},{1,25},{9,17},{17,9},{25,1},{2,26},{10... | collective-permute-start | bytes 92168 | tf_op jit(solution)/shard_map/ppermute | solution.py:399
  65.8 0.0 collective-permute-done.18.b
  65.8 0.6 collective-permute-done.19.c
  66.3 2.4 %collective-permute-done.20.d = bf16[40,384]{1,0:T(8,128)(2,1)S(1)} collective-permute-done((bf16[40,384]{1,0:T(8,128)(2,1)S(1)}, bf16[40,384]{1,0:T(8,128)(2,1)S(1)}, u32[]{:S(2)}, u32[]{:S(2)}) %collective-permute-start.20) | collective-permute-done | bytes 30752 | tf_op jit(solution)/shard_map/ppermute | solution.py:399
  68.8 0.1 collective-permute-start.21
  68.9 1.2 %collective-permute-done.21.other_ref = bf16[48,384]{1,0:T(8,128)(2,1)S(1)} collective-permute-done((bf16[48,384]{1,0:T(8,128)(2,1)S(1)}, bf16[48,384]{1,0:T(8,128)(2,1)S(1)}, u32[]{:S(2)}, u32[]{:S(2)}) %collective-permute-start.21) | collective-permute-done | bytes 36896 | tf_op jit(solution)/shard_map/ppermute | solution.py:399
  70.1 2.0 %collective-permute-start.24 = (bf16[96,384]{1,0:T(8,128)(2,1)S(1)}, bf16[96,384]{1,0:T(8,128)(2,1)S(1)}, u32[]{:S(2)}, u32[]{:S(2)}) collective-permute-start(bf16[96,384]{1,0:T(8,128)(2,1)S(1)} %pair.1.refs_0_), channel_id=1, source_target_pairs={{0,5},{1,4},{2,7},{3,6},{4,1},{5,0},{6,3},{7,2},{8,13},{9,12},{10,... | collective-permute-start | bytes 221192 | tf_op jit(solution)/shard_map/ppermute | solution.py:539
  72.1 1.0 %collective-permute-start.23 = (bf16[96,384]{1,0:T(8,128)(2,1)S(1)}, bf16[96,384]{1,0:T(8,128)(2,1)S(1)}, u32[]{:S(2)}, u32[]{:S(2)}) collective-permute-start(bf16[96,384]{1,0:T(8,128)(2,1)S(1)} %pair.1.refs_0_), channel_id=1, source_target_pairs={{0,4},{1,5},{2,6},{3,7},{4,0},{5,1},{6,2},{7,3},{8,12},{9,13},{10,... | collective-permute-start | bytes 221192 | tf_op jit(solution)/shard_map/ppermute | solution.py:539
  73.1 0.5 collective-permute-start.22
  73.6 1.8 %collective-permute-done.24.refs_3_ = bf16[96,384]{1,0:T(8,128)(2,1)S(1)} collective-permute-done((bf16[96,384]{1,0:T(8,128)(2,1)S(1)}, bf16[96,384]{1,0:T(8,128)(2,1)S(1)}, u32[]{:S(2)}, u32[]{:S(2)}) %collective-permute-start.24) | collective-permute-done | bytes 73760 | tf_op jit(solution)/shard_map/ppermute | solution.py:539
  75.5 1.5 %collective-permute-done.23.refs_2_ = bf16[96,384]{1,0:T(8,128)(2,1)S(1)} collective-permute-done((bf16[96,384]{1,0:T(8,128)(2,1)S(1)}, bf16[96,384]{1,0:T(8,128)(2,1)S(1)}, u32[]{:S(2)}, u32[]{:S(2)}) %collective-permute-start.23) | collective-permute-done | bytes 73760 | tf_op jit(solution)/shard_map/ppermute | solution.py:539
  77.0 0.5 collective-permute-done.22.refs_1_
  77.5 0.7 join.1
  (9 shorter events, 0.1 us)
Async XLA Ops:
  0.6 5.6 %copy-start.4 = (s32[8,8]{1,0:T(8,128)S(1)}, s32[8,8]{1,0:T(8,128)}, u32[]{:S(2)}) copy-start(s32[8,8]{1,0:T(8,128)} %valid_ref.1) | copy-start | bytes 772
  0.6 5.6 %copy-start.2 = (bf16[1,4,8,8,160]{4,3,2,1,0:T(8,128)(2,1)S(1)}, bf16[1,4,8,8,160]{4,3,2,1,0:T(8,128)(2,1)}, u32[]{:S(2)}) copy-start(bf16[1,4,8,8,160]{4,3,2,1,0:T(8,128)(2,1)} %param.9) | copy-start | bytes 245764
  3.1 13.4 %collective-permute-start = (bf16[112,1536]{1,0:T(8,128)(2,1)}, bf16[112,1536]{1,0:T(8,128)(2,1)S(1)}, u32[]{:S(2)}, u32[]{:S(2)}) collective-permute-start(bf16[112,1536]{1,0:T(8,128)(2,1)} %payload.1), channel_id=1, source_target_pairs={{0,8},{8,16},{16,24},{24,0},{1,9},{9,17},{17,25},{25,1},{2,10},{10... | collective-permute-start | bytes 1032200 | tf_op jit(solution)/shard_map/ppermute | solution.py:28
  9.6 19.3 %collective-permute-start.2 = (bf16[64,4864]{1,0:T(8,128)(2,1)S(1)}, bf16[64,4864]{1,0:T(8,128)(2,1)S(1)}, u32[]{:S(2)}, u32[]{:S(2)}) collective-permute-start(bf16[64,4864]{1,0:T(8,128)(2,1)S(1)} %get-tuple-element.43), channel_id=1, source_target_pairs={{0,6},{2,0},{4,2},{6,4},{1,7},{3,1},{5,3},{7,5},{8,14},{10,8},{12,... | collective-permute-start | bytes 1867784 | tf_op jit(solution)/shard_map/ppermute | solution.py:28
  10.3 18.6 %collective-permute-start.3 = (bf16[64,4864]{1,0:T(8,128)(2,1)S(1)}, bf16[64,4864]{1,0:T(8,128)(2,1)S(1)}, u32[]{:S(2)}, u32[]{:S(2)}) collective-permute-start(bf16[64,4864]{1,0:T(8,128)(2,1)S(1)} %get-tuple-element.44), channel_id=1, source_target_pairs={{0,7},{1,6},{2,1},{3,0},{4,3},{5,2},{6,5},{7,4},{8,15},{9,14},{10,... | collective-permute-start | bytes 1867784 | tf_op jit(solution)/shard_map/ppermute | solution.py:451
  16.5 11.0 %collective-permute-start.1 = (bf16[112,1536]{1,0:T(8,128)(2,1)S(1)}, bf16[112,1536]{1,0:T(8,128)(2,1)S(1)}, u32[]{:S(2)}, u32[]{:S(2)}) collective-permute-start(bf16[112,1536]{1,0:T(8,128)(2,1)S(1)} %collective-permute-done.refs_8_.refs_3_), channel_id=1, source_target_pairs={{0,8},{8,16},{16,24},{24,0},{1,9},{9,17},{17,25},{25,1},{2,10},{10... | collective-permute-start | bytes 1032200 | tf_op jit(solution)/shard_map/ppermute | solution.py:28
  27.6 8.3 %collective-permute-start.5 = (bf16[112,1536]{1,0:T(8,128)(2,1)S(1)}, bf16[112,1536]{1,0:T(8,128)(2,1)S(1)}, u32[]{:S(2)}, u32[]{:S(2)}) collective-permute-start(bf16[112,1536]{1,0:T(8,128)(2,1)S(1)} %collective-permute-done.1.refs_12_.refs_7_), channel_id=1, source_target_pairs={{0,4},{2,6},{4,0},{6,2},{1,5},{3,7},{5,1},{7,3},{8,12},{10,14},{12... | collective-permute-start | bytes 1032200 | tf_op jit(solution)/shard_map/ppermute | solution.py:399
  28.8 14.2 %collective-permute-start.4 = (bf16[64,4864]{1,0:T(8,128)(2,1)S(1)}, bf16[64,4864]{1,0:T(8,128)(2,1)S(1)}, u32[]{:S(2)}, u32[]{:S(2)}) collective-permute-start(bf16[64,4864]{1,0:T(8,128)(2,1)S(1)} %get-tuple-element.45), channel_id=1, source_target_pairs={{0,1},{1,0},{2,3},{3,2},{4,5},{5,4},{6,7},{7,6},{8,9},{9,8},{10,11... | collective-permute-start | bytes 1867784 | tf_op jit(solution)/shard_map/ppermute | solution.py:28
  30.3 11.4 %collective-permute-start.12 = (bf16[112,1536]{1,0:T(8,128)(2,1)S(1)}, bf16[112,1536]{1,0:T(8,128)(2,1)S(1)}, u32[]{:S(2)}, u32[]{:S(2)}) collective-permute-start(bf16[112,1536]{1,0:T(8,128)(2,1)S(1)} %collective-permute-done.1.refs_12_.refs_7_), channel_id=1, source_target_pairs={{0,8},{8,16},{16,24},{24,0},{1,9},{9,17},{17,25},{25,1},{2,10},{10... | collective-permute-start | bytes 1032200 | tf_op jit(solution)/shard_map/ppermute | solution.py:28
  35.9 7.4 %collective-permute-start.6 = (bf16[112,1536]{1,0:T(8,128)(2,1)S(1)}, bf16[112,1536]{1,0:T(8,128)(2,1)S(1)}, u32[]{:S(2)}, u32[]{:S(2)}) collective-permute-start(bf16[112,1536]{1,0:T(8,128)(2,1)S(1)} %collective-permute-done.refs_8_.refs_3_), channel_id=1, source_target_pairs={{0,4},{2,6},{4,0},{6,2},{1,5},{3,7},{5,1},{7,3},{8,12},{10,14},{12... | collective-permute-start | bytes 1032200 | tf_op jit(solution)/shard_map/ppermute | solution.py:399
  37.1 10.3 %collective-permute-start.7 = (bf16[112,1536]{1,0:T(8,128)(2,1)S(1)}, bf16[112,1536]{1,0:T(8,128)(2,1)S(1)}, u32[]{:S(2)}, u32[]{:S(2)}) collective-permute-start(bf16[112,1536]{1,0:T(8,128)(2,1)S(1)} %collective-permute-done.5.refs_13_.refs_8_), channel_id=1, source_target_pairs={{0,8},{8,16},{16,24},{24,0},{1,9},{9,17},{17,25},{25,1},{2,10},{10... | collective-permute-start | bytes 1032200 | tf_op jit(solution)/shard_map/ppermute | solution.py:28
  37.1 10.3 %collective-permute-start.11 = (bf16[112,1536]{1,0:T(8,128)(2,1)S(1)}, bf16[112,1536]{1,0:T(8,128)(2,1)S(1)}, u32[]{:S(2)}, u32[]{:S(2)}) collective-permute-start(bf16[112,1536]{1,0:T(8,128)(2,1)S(1)} %collective-permute-done.5.refs_13_.refs_8_), channel_id=1, source_target_pairs={{0,2},{2,0},{4,6},{6,4},{1,3},{3,1},{5,7},{7,5},{8,10},{10,8},{12,... | collective-permute-start | bytes 1032200 | tf_op jit(solution)/shard_map/ppermute | solution.py:399
  41.8 6.1 %collective-permute-start.13 = (bf16[112,1536]{1,0:T(8,128)(2,1)S(1)}, bf16[112,1536]{1,0:T(8,128)(2,1)S(1)}, u32[]{:S(2)}, u32[]{:S(2)}) collective-permute-start(bf16[112,1536]{1,0:T(8,128)(2,1)S(1)} %collective-permute-done.12.refs_16_.refs_11_), channel_id=1, source_target_pairs={{0,2},{2,0},{4,6},{6,4},{1,3},{3,1},{5,7},{7,5},{8,10},{10,8},{12,... | collective-permute-start | bytes 1032200 | tf_op jit(solution)/shard_map/ppermute | solution.py:399
  43.3 6.3 %copy-start = (bf16[384,1536]{1,0:T(8,128)(2,1)S(1)}, bf16[384,1536]{1,0:T(8,128)(2,1)}, u32[]{:S(2)}) copy-start(bf16[384,1536]{1,0:T(8,128)(2,1)} %refs_0_.1) | copy-start | bytes 3538948
  43.3 6.3 %copy-start.1 = (bf16[384,160]{0,1:T(8,128)(2,1)S(1)}, bf16[384,160]{0,1:T(8,128)(2,1)}, u32[]{:S(2)}) copy-start(bf16[384,160]{0,1:T(8,128)(2,1)} %param.12) | copy-start | bytes 368644
  43.3 6.3 %copy-start.3 = (bf16[384]{0:T(512)(128)(2,1)S(1)}, bf16[384]{0:T(512)(128)(2,1)}, u32[]{:S(2)}) copy-start(bf16[384]{0:T(512)(128)(2,1)} %refs_2_.1) | copy-start | bytes 2308
  43.3 6.3 %copy-start.5 = (f32[5]{0:T(128)S(1)}, f32[5]{0:T(128)}, u32[]{:S(2)}) copy-start(f32[5]{0:T(128)} %var_ref.1) | copy-start | bytes 64
  43.3 6.3 %copy-start.6 = (f32[32]{0:T(128)S(1)}, f32[32]{0:T(128)}, u32[]{:S(2)}) copy-start(f32[32]{0:T(128)} %constant.2.clone.lat_ref) | copy-start | bytes 388
  43.3 4.6 %collective-permute-start.8 = (bf16[112,1536]{1,0:T(8,128)(2,1)S(1)}, bf16[112,1536]{1,0:T(8,128)(2,1)S(1)}, u32[]{:S(2)}, u32[]{:S(2)}) collective-permute-start(bf16[112,1536]{1,0:T(8,128)(2,1)S(1)} %collective-permute-done.refs_8_.refs_3_), channel_id=1, source_target_pairs={{0,2},{2,0},{4,6},{6,4},{1,3},{3,1},{5,7},{7,5},{8,10},{10,8},{12,... | collective-permute-start | bytes 1032200 | tf_op jit(solution)/shard_map/ppermute | solution.py:399
  43.4 4.5 %collective-permute-start.9 = (bf16[112,1536]{1,0:T(8,128)(2,1)S(1)}, bf16[112,1536]{1,0:T(8,128)(2,1)S(1)}, u32[]{:S(2)}, u32[]{:S(2)}) collective-permute-start(bf16[112,1536]{1,0:T(8,128)(2,1)S(1)} %collective-permute-done.6.refs_9_.refs_4_), channel_id=1, source_target_pairs={{0,2},{2,0},{4,6},{6,4},{1,3},{3,1},{5,7},{7,5},{8,10},{10,8},{12,... | collective-permute-start | bytes 1032200 | tf_op jit(solution)/shard_map/ppermute | solution.py:399
  47.4 1.7 %collective-permute-start.10 = (bf16[112,1536]{1,0:T(8,128)(2,1)S(1)}, bf16[112,1536]{1,0:T(8,128)(2,1)S(1)}, u32[]{:S(2)}, u32[]{:S(2)}) collective-permute-start(bf16[112,1536]{1,0:T(8,128)(2,1)S(1)} %collective-permute-done.1.refs_12_.refs_7_), channel_id=1, source_target_pairs={{0,2},{2,0},{4,6},{6,4},{1,3},{3,1},{5,7},{7,5},{8,10},{10,8},{12,... | collective-permute-start | bytes 1032200 | tf_op jit(solution)/shard_map/ppermute | solution.py:399
  47.4 2.1 %collective-permute-start.14 = (bf16[112,1536]{1,0:T(8,128)(2,1)S(1)}, bf16[112,1536]{1,0:T(8,128)(2,1)S(1)}, u32[]{:S(2)}, u32[]{:S(2)}) collective-permute-start(bf16[112,1536]{1,0:T(8,128)(2,1)S(1)} %collective-permute-done.7.refs_17_.refs_12_), channel_id=1, source_target_pairs={{0,2},{2,0},{4,6},{6,4},{1,3},{3,1},{5,7},{7,5},{8,10},{10,8},{12,... | collective-permute-start | bytes 1032200 | tf_op jit(solution)/shard_map/ppermute | solution.py:399
  53.3 5.6 %collective-permute-start.15 = (bf16[40,1536]{1,0:T(8,128)(2,1)S(1)}, bf16[40,1536]{1,0:T(8,128)(2,1)S(1)}, u32[]{:S(2)}, u32[]{:S(2)}) collective-permute-start(bf16[40,1536]{1,0:T(8,128)(2,1)S(1)} %get-tuple-element.61), channel_id=1, source_target_pairs={{0,2},{2,0},{4,6},{6,4},{1,3},{3,1},{5,7},{7,5},{8,10},{10,8},{12,... | collective-permute-start | bytes 368648 | tf_op jit(solution)/shard_map/ppermute | solution.py:399
  53.5 6.2 %collective-permute-start.16 = (bf16[40,1536]{1,0:T(8,128)(2,1)S(1)}, bf16[40,1536]{1,0:T(8,128)(2,1)S(1)}, u32[]{:S(2)}, u32[]{:S(2)}) collective-permute-start(bf16[40,1536]{1,0:T(8,128)(2,1)S(1)} %get-tuple-element.62), channel_id=1, source_target_pairs={{0,4},{2,6},{4,0},{6,2},{1,5},{3,7},{5,1},{7,3},{8,12},{10,14},{12... | collective-permute-start | bytes 368648 | tf_op jit(solution)/shard_map/ppermute | solution.py:399
  54.6 6.5 %collective-permute-start.17 = (bf16[40,1536]{1,0:T(8,128)(2,1)S(1)}, bf16[40,1536]{1,0:T(8,128)(2,1)S(1)}, u32[]{:S(2)}, u32[]{:S(2)}) collective-permute-start(bf16[40,1536]{1,0:T(8,128)(2,1)S(1)} %get-tuple-element.63), channel_id=1, source_target_pairs={{0,6},{2,4},{4,2},{6,0},{1,7},{3,5},{5,3},{7,1},{8,14},{10,12},{12... | collective-permute-start | bytes 368648 | tf_op jit(solution)/shard_map/ppermute | solution.py:399
  61.3 4.5 %collective-permute-start.18 = (bf16[40,384]{1,0:T(8,128)(2,1)S(1)}, bf16[40,384]{1,0:T(8,128)(2,1)S(1)}, u32[]{:S(2)}, u32[]{:S(2)}) collective-permute-start(bf16[40,384]{1,0:T(8,128)(2,1)S(1)} %get-tuple-element.74), channel_id=1, source_target_pairs={{0,8},{8,0},{16,24},{24,16},{1,9},{9,1},{17,25},{25,17},{2,10},{10... | collective-permute-start | bytes 92168 | tf_op jit(solution)/shard_map/ppermute | solution.py:399
  61.5 4.8 %collective-permute-start.19 = (bf16[40,384]{1,0:T(8,128)(2,1)S(1)}, bf16[40,384]{1,0:T(8,128)(2,1)S(1)}, u32[]{:S(2)}, u32[]{:S(2)}) collective-permute-start(bf16[40,384]{1,0:T(8,128)(2,1)S(1)} %get-tuple-element.75), channel_id=1, source_target_pairs={{0,16},{8,24},{16,0},{24,8},{1,17},{9,25},{17,1},{25,9},{2,18},{10... | collective-permute-start | bytes 92168 | tf_op jit(solution)/shard_map/ppermute | solution.py:399
  63.0 5.7 %collective-permute-start.20 = (bf16[40,384]{1,0:T(8,128)(2,1)S(1)}, bf16[40,384]{1,0:T(8,128)(2,1)S(1)}, u32[]{:S(2)}, u32[]{:S(2)}) collective-permute-start(bf16[40,384]{1,0:T(8,128)(2,1)S(1)} %get-tuple-element.76), channel_id=1, source_target_pairs={{0,24},{8,16},{16,8},{24,0},{1,25},{9,17},{17,9},{25,1},{2,26},{10... | collective-permute-start | bytes 92168 | tf_op jit(solution)/shard_map/ppermute | solution.py:399
  68.8 1.3 %collective-permute-start.21 = (bf16[48,384]{1,0:T(8,128)(2,1)S(1)}, bf16[48,384]{1,0:T(8,128)(2,1)S(1)}, u32[]{:S(2)}, u32[]{:S(2)}) collective-permute-start(bf16[48,384]{1,0:T(8,128)(2,1)S(1)} %dp_sum.1.mine_ref), channel_id=1, source_target_pairs={{0,2},{2,0},{4,6},{6,4},{1,3},{3,1},{5,7},{7,5},{8,10},{10,8},{12,... | collective-permute-start | bytes 110600 | tf_op jit(solution)/shard_map/ppermute | solution.py:399
  70.1 5.4 %collective-permute-start.24 = (bf16[96,384]{1,0:T(8,128)(2,1)S(1)}, bf16[96,384]{1,0:T(8,128)(2,1)S(1)}, u32[]{:S(2)}, u32[]{:S(2)}) collective-permute-start(bf16[96,384]{1,0:T(8,128)(2,1)S(1)} %pair.1.refs_0_), channel_id=1, source_target_pairs={{0,5},{1,4},{2,7},{3,6},{4,1},{5,0},{6,3},{7,2},{8,13},{9,12},{10,... | collective-permute-start | bytes 221192 | tf_op jit(solution)/shard_map/ppermute | solution.py:539
  72.1 4.9 %collective-permute-start.23 = (bf16[96,384]{1,0:T(8,128)(2,1)S(1)}, bf16[96,384]{1,0:T(8,128)(2,1)S(1)}, u32[]{:S(2)}, u32[]{:S(2)}) collective-permute-start(bf16[96,384]{1,0:T(8,128)(2,1)S(1)} %pair.1.refs_0_), channel_id=1, source_target_pairs={{0,4},{1,5},{2,6},{3,7},{4,0},{5,1},{6,2},{7,3},{8,12},{9,13},{10,... | collective-permute-start | bytes 221192 | tf_op jit(solution)/shard_map/ppermute | solution.py:539
  73.1 4.4 %collective-permute-start.22 = (bf16[96,384]{1,0:T(8,128)(2,1)S(1)}, bf16[96,384]{1,0:T(8,128)(2,1)S(1)}, u32[]{:S(2)}, u32[]{:S(2)}) collective-permute-start(bf16[96,384]{1,0:T(8,128)(2,1)S(1)} %pair.1.refs_0_), channel_id=1, source_target_pairs={{0,1},{1,0},{2,3},{3,2},{4,5},{5,4},{6,7},{7,6},{8,9},{9,8},{10,11... | collective-permute-start | bytes 221192 | tf_op jit(solution)/shard_map/ppermute | solution.py:539

commit v16 on v15

--- a/solution.py
+++ b/solution.py
@@ -458,7 +458,8 @@
     ring1_late, across2 = barrier((ring1, across2))
     across1 = swap(ring1_late, "lat", 2)
     tiles = [own, east, south, diag]
-    *tiles, ring1, across1, ring2 = barrier((*tiles, ring1, across1, ring2))
+    ring1_swapped = swap(ring1, "lat", 1)
+    *tiles, across1, ring2, ring1_swapped = barrier((*tiles, across1, ring2, ring1_swapped))
     ctx = pl.pallas_call(
         attention_kernel,
         out_shape=shape((tokens, width), BF),
@@ -468,8 +469,8 @@
         name="attention",
     )(*tiles)
     ctx, across3 = barrier((ctx, across3))
-    pieces = []
-    for ring, across in ((ring1, across1), (ring2, across2), (ring3, across3)):
+    pieces = [ring1, across1, ring1_swapped, swap(across1, "lat", 1)]
+    for ring, across in ((ring2, across2), (ring3, across3)):
         pieces += [ring, across, swap(ring, "lat", 1), swap(across, "lat", 1)]
 
     piece = span // lat

time: 78.4 us -> 78.8 us (level)
  waiting for transfers between devices: 39.8 us -> 40.7 us
    ppermute x6, waiting for transfers between devices: 22 us -> 24.6 us  [from_behind(): lax.ppermute(array, axis, [(i, (i + by) % length) for i in range(length)])]
    ppermute x3, waiting for transfers between devices: 3.83 us -> 2.87 us  [shards(): plane.append(lax.ppermute(chip, ('lat', 'lon'), pairs))]
  transfers between devices with their start and end apart: 25 -> 25, of which waited for: 17 -> 14; matrix products, arithmetic and copies ran while one was open for 0% -> 0% of each run, Pallas kernels for 13% -> 12%
where the time goes in v16:
time: 78.8 us; the launch traced here: 78.6 us
  waiting for transfers between devices  40.7 us (52%)
  starting transfers between devices  20.2 us (26%)
  Pallas kernels  16.8 us (21%)
  between operations  0.79 us (1%)
    ppermute x6, waiting for transfers between devices, from_behind(): lax.ppermute(array, axis, [(i, (i + by) % length) for i in range(length)])  24.6 us
    ppermute x15, waiting for transfers between devices, swap(): lax.ppermute(array, axis, [(i, i ^ bit) for i in range(lax.axis_size(axis...  13.3 us
    ppermute x15, starting transfers between devices, swap(): lax.ppermute(array, axis, [(i, i ^ bit) for i in range(lax.axis_size(axis...  9.49 us
    ppermute x6, starting transfers between devices, from_behind(): lax.ppermute(array, axis, [(i, (i + by) % length) for i in range(length)])  5.31 us
    pallas_call x1, Pallas kernels, shards(): pl.pallas_call(forward_kernel, grid=(1,), out_shape=[shape((piece, width)...  3.7 us
    pallas_call x1, Pallas kernels, shards(): pl.pallas_call(backward_kernel, out_shape=shape((tokens, width), BF), in_...  3.61 us
    ppermute x3, starting transfers between devices, shards(): plane.append(lax.ppermute(chip, ('lat', 'lon'), pairs))  3.55 us
    pallas_call x1, Pallas kernels, shards(): pl.pallas_call(pack_kernel, out_shape=[shape((n, 3 * width + EXTRA), BF)...  3.32 us
  transfers between devices with their start and end apart: 25, of which 14 were waited for; matrix products, arithmetic and copies ran while one was open for 0% of the time, Pallas kernels for 12%

profile of v16, /device:TPU:0, one launch (start us, length us, event | category | flops | bytes accessed | tf_op | source)
XLA Modules:
  0.0 78.6 jit_solution(7420771020103441372)
XLA Ops:
  0.6 0.0 copy-start.4
  0.6 0.0 copy-start.2
  0.7 2.5 %payload.1 = bf16[112,1536]{1,0:T(8,128)(2,1)} custom-call(bf16[384,1536]{1,0:T(8,128)(2,1)} %refs_0_.1, bf16[160,384]{1,0:T(8,128)(2,1)} %bitcast.6, bf16[384]{0:T(512)(128)(2,1)} %refs_2_.1), custom_call_target="tpu_custom_call" | custom-call | tf_op jit(solution)/shard_map/payload/pallas_call | solution.py:419
  3.1 3.1 %collective-permute-start = (bf16[112,1536]{1,0:T(8,128)(2,1)}, bf16[112,1536]{1,0:T(8,128)(2,1)S(1)}, u32[]{:S(2)}, u32[]{:S(2)}) collective-permute-start(bf16[112,1536]{1,0:T(8,128)(2,1)} %payload.1), channel_id=1, source_target_pairs={{0,8},{8,16},{16,24},{24,0},{1,9},{9,17},{17,25},{25,1},{2,10},{10... | collective-permute-start | bytes 1032200 | tf_op jit(solution)/shard_map/ppermute | solution.py:28
  6.2 0.0 copy-done.4
  6.2 0.0 copy-done.2
  6.2 3.3 %pack.1 = (bf16[64,4864]{1,0:T(8,128)(2,1)S(1)}, bf16[64,4864]{1,0:T(8,128)(2,1)S(1)}, bf16[64,4864]{1,0:T(8,128)(2,1)S(1)}, bf16[64,4864]{1,0:T(8,128)(2,1)S(1)}) custom-call(bf16[4,8,8,4608]{3,2,1,0:T(8,128)(2,1)} %bitcast.10, bf16[4,8,8,160]{3,2,1,0:T(8,128)(2,1)S(1)} %bitcast.9, s32[8,8]{1,0:T(8,128)S(1)} %copy-done.4), custom_call_target="tpu_custom_call" | custom-call | tf_op jit(solution)/shard_map/pack/pallas_call | solution.py:429
  9.6 0.7 collective-permute-start.2
  10.3 1.9 %collective-permute-start.3 = (bf16[64,4864]{1,0:T(8,128)(2,1)S(1)}, bf16[64,4864]{1,0:T(8,128)(2,1)S(1)}, u32[]{:S(2)}, u32[]{:S(2)}) collective-permute-start(bf16[64,4864]{1,0:T(8,128)(2,1)S(1)} %get-tuple-element.44), channel_id=1, source_target_pairs={{0,7},{1,6},{2,1},{3,0},{4,3},{5,2},{6,5},{7,4},{8,15},{9,14},{10,... | collective-permute-start | bytes 1867784 | tf_op jit(solution)/shard_map/ppermute | solution.py:451
  12.2 4.4 %collective-permute-done.refs_8_.refs_3_ = bf16[112,1536]{1,0:T(8,128)(2,1)S(1)} collective-permute-done((bf16[112,1536]{1,0:T(8,128)(2,1)}, bf16[112,1536]{1,0:T(8,128)(2,1)S(1)}, u32[]{:S(2)}, u32[]{:S(2)}) %collective-permute-start) | collective-permute-done | bytes 344096 | tf_op jit(solution)/shard_map/ppermute | solution.py:28
  16.5 0.0 collective-permute-start.1
  16.5 11.0 %collective-permute-done.1.refs_12_.refs_7_ = bf16[112,1536]{1,0:T(8,128)(2,1)S(1)} collective-permute-done((bf16[112,1536]{1,0:T(8,128)(2,1)S(1)}, bf16[112,1536]{1,0:T(8,128)(2,1)S(1)}, u32[]{:S(2)}, u32[]{:S(2)}) %collective-permute-start.1) | collective-permute-done | bytes 344096 | tf_op jit(solution)/shard_map/ppermute | solution.py:28
  27.6 1.3 %collective-permute-start.5 = (bf16[112,1536]{1,0:T(8,128)(2,1)S(1)}, bf16[112,1536]{1,0:T(8,128)(2,1)S(1)}, u32[]{:S(2)}, u32[]{:S(2)}) collective-permute-start(bf16[112,1536]{1,0:T(8,128)(2,1)S(1)} %collective-permute-done.1.refs_12_.refs_7_), channel_id=1, source_target_pairs={{0,4},{2,6},{4,0},{6,2},{1,5},{3,7},{5,1},{7,3},{8,12},{10,14},{12... | collective-permute-start | bytes 1032200 | tf_op jit(solution)/shard_map/ppermute | solution.py:399
  28.8 0.0 collective-permute-done.2.refs_2_.refs_3_
  28.8 0.0 collective-permute-done.3.refs_3_.refs_4_
  28.8 1.5 %collective-permute-start.4 = (bf16[64,4864]{1,0:T(8,128)(2,1)S(1)}, bf16[64,4864]{1,0:T(8,128)(2,1)S(1)}, u32[]{:S(2)}, u32[]{:S(2)}) collective-permute-start(bf16[64,4864]{1,0:T(8,128)(2,1)S(1)} %get-tuple-element.45), channel_id=1, source_target_pairs={{0,1},{1,0},{2,3},{3,2},{4,5},{5,4},{6,7},{7,6},{8,9},{9,8},{10,11... | collective-permute-start | bytes 1867784 | tf_op jit(solution)/shard_map/ppermute | solution.py:28
  30.3 0.0 collective-permute-start.7
  30.3 0.0 collective-permute-start.12
  30.3 5.5 %collective-permute-done.5.refs_13_.refs_8_ = bf16[112,1536]{1,0:T(8,128)(2,1)S(1)} collective-permute-done((bf16[112,1536]{1,0:T(8,128)(2,1)S(1)}, bf16[112,1536]{1,0:T(8,128)(2,1)S(1)}, u32[]{:S(2)}, u32[]{:S(2)}) %collective-permute-start.5) | collective-permute-done | bytes 344096 | tf_op jit(solution)/shard_map/ppermute | solution.py:399
  35.9 1.2 %collective-permute-start.6 = (bf16[112,1536]{1,0:T(8,128)(2,1)S(1)}, bf16[112,1536]{1,0:T(8,128)(2,1)S(1)}, u32[]{:S(2)}, u32[]{:S(2)}) collective-permute-start(bf16[112,1536]{1,0:T(8,128)(2,1)S(1)} %collective-permute-done.refs_8_.refs_3_), channel_id=1, source_target_pairs={{0,4},{2,6},{4,0},{6,2},{1,5},{3,7},{5,1},{7,3},{8,12},{10,14},{12... | collective-permute-start | bytes 1032200 | tf_op jit(solution)/shard_map/ppermute | solution.py:399
  37.1 0.0 collective-permute-start.8
  37.1 0.0 collective-permute-done.7.refs_10_.refs_5_
  37.1 0.0 collective-permute-start.11
  37.1 5.9 %collective-permute-done.12.refs_16_.refs_11_ = bf16[112,1536]{1,0:T(8,128)(2,1)S(1)} collective-permute-done((bf16[112,1536]{1,0:T(8,128)(2,1)S(1)}, bf16[112,1536]{1,0:T(8,128)(2,1)S(1)}, u32[]{:S(2)}, u32[]{:S(2)}) %collective-permute-start.12) | collective-permute-done | bytes 344096 | tf_op jit(solution)/shard_map/ppermute | solution.py:28
  43.0 0.0 collective-permute-start.13
  43.0 0.0 collective-permute-done.4.refs_1_.refs_2_
  43.0 0.3 collective-permute-done.6.refs_9_.refs_4_
  43.3 0.0 copy-start.6
  43.3 0.3 collective-permute-start.9
  43.6 0.3 collective-permute-start.10
  43.9 2.8 %attention.1.refs_0_ = bf16[256,1536]{1,0:T(8,128)(2,1)S(1)} custom-call(bf16[64,4864]{1,0:T(8,128)(2,1)S(1)} %get-tuple-element.49.refs_0_.refs_1_, bf16[64,4864]{1,0:T(8,128)(2,1)S(1)} %collective-permute-done.4.refs_1_.refs_2_, bf16[64,4864]{1,0:T(8,128)(2,1)S(1)} %collective-permute-done.2.refs_2_.refs_3_, ...), custom_call_target="tpu_custom_call" | custom-call | tf_op jit(solution)/shard_map/attention/pallas_call | solution.py:463
  46.7 3.2 %collective-permute-done.8.refs_17_.refs_12_ = bf16[112,1536]{1,0:T(8,128)(2,1)S(1)} collective-permute-done((bf16[112,1536]{1,0:T(8,128)(2,1)S(1)}, bf16[112,1536]{1,0:T(8,128)(2,1)S(1)}, u32[]{:S(2)}, u32[]{:S(2)}) %collective-permute-start.8) | collective-permute-done | bytes 344096 | tf_op jit(solution)/shard_map/ppermute | solution.py:28
  50.0 0.0 collective-permute-start.14
  50.0 0.0 collective-permute-done.11.refs_15_.refs_10_
  50.0 0.0 collective-permute-done.13.refs_18_.refs_13_
  50.0 0.0 collective-permute-done.9.refs_11_.refs_6_
  50.0 0.0 collective-permute-done.10.refs_14_.refs_9_
  50.0 1.6 %collective-permute-done.14.refs_19_.refs_14_ = bf16[112,1536]{1,0:T(8,128)(2,1)S(1)} collective-permute-done((bf16[112,1536]{1,0:T(8,128)(2,1)S(1)}, bf16[112,1536]{1,0:T(8,128)(2,1)S(1)}, u32[]{:S(2)}, u32[]{:S(2)}) %collective-permute-start.14) | collective-permute-done | bytes 344096 | tf_op jit(solution)/shard_map/ppermute | solution.py:399
  51.6 0.0 copy-done
  51.6 0.0 copy-done.1
  51.7 3.7 %forward.1 = (bf16[40,1536]{1,0:T(8,128)(2,1)S(1)}, bf16[40,1536]{1,0:T(8,128)(2,1)S(1)}, bf16[40,1536]{1,0:T(8,128)(2,1)S(1)}, bf16[40,1536]{1,0:T(8,128)(2,1)S...) custom-call(f32[32]{0:T(128)S(1)} %copy-done.6, ...), custom_call_target="tpu_custom_call" | custom-call | tf_op jit(solution)/shard_map/forward/pallas_call | solution.py:484
  55.4 0.2 collective-permute-start.15
  55.6 0.5 collective-permute-start.16
  56.1 1.2 %collective-permute-start.17 = (bf16[40,1536]{1,0:T(8,128)(2,1)S(1)}, bf16[40,1536]{1,0:T(8,128)(2,1)S(1)}, u32[]{:S(2)}, u32[]{:S(2)}) collective-permute-start(bf16[40,1536]{1,0:T(8,128)(2,1)S(1)} %get-tuple-element.63), channel_id=1, source_target_pairs={{0,6},{2,4},{4,2},{6,0},{1,7},{3,5},{5,3},{7,1},{8,14},{10,12},{12... | collective-permute-start | bytes 368648 | tf_op jit(solution)/shard_map/ppermute | solution.py:399
  57.3 3.6 %backward.1 = bf16[256,1536]{1,0:T(8,128)(2,1)} custom-call(f32[256,1536]{1,0:T(8,128)S(1)} %get-tuple-element.64.normed_ref, f32[256,128]{1,0:T(8,128)S(1)} %get-tuple-element.65.inv_ref, bf16[256,160]{1,0:T(8,128)(2,1)S(1)} %get-tuple-element.66.dfc_ref, bf16[384,1536]{1,0:T(8,128)(2,1)S(1)} %copy-done, bf16[160,384]{1,0:T(8,128)(2,1)S(1)} %bitcast.8, ...), custom_call_target="tpu_custom_call" | custom-call | tf_op jit(solution)/shard_map/backward/pallas_call | solution.py:500
  60.9 0.0 collective-permute-done.15.b
  60.9 0.8 %collective-permute-done.16.c = bf16[40,1536]{1,0:T(8,128)(2,1)S(1)} collective-permute-done((bf16[40,1536]{1,0:T(8,128)(2,1)S(1)}, bf16[40,1536]{1,0:T(8,128)(2,1)S(1)}, u32[]{:S(2)}, u32[]{:S(2)}) %collective-permute-start.16) | collective-permute-done | bytes 122912 | tf_op jit(solution)/shard_map/ppermute | solution.py:399
  61.7 1.5 %collective-permute-done.17.d = bf16[40,1536]{1,0:T(8,128)(2,1)S(1)} collective-permute-done((bf16[40,1536]{1,0:T(8,128)(2,1)S(1)}, bf16[40,1536]{1,0:T(8,128)(2,1)S(1)}, u32[]{:S(2)}, u32[]{:S(2)}) %collective-permute-start.17) | collective-permute-done | bytes 122912 | tf_op jit(solution)/shard_map/ppermute | solution.py:399
  63.3 0.1 lat_sum.1
  63.4 0.1 collective-permute-start.18
  63.4 0.1 collective-permute-start.19
  63.6 4.3 %collective-permute-start.20 = (bf16[40,384]{1,0:T(8,128)(2,1)S(1)}, bf16[40,384]{1,0:T(8,128)(2,1)S(1)}, u32[]{:S(2)}, u32[]{:S(2)}) collective-permute-start(bf16[40,384]{1,0:T(8,128)(2,1)S(1)} %get-tuple-element.76), channel_id=1, source_target_pairs={{0,24},{8,16},{16,8},{24,0},{1,25},{9,17},{17,9},{25,1},{2,26},{10... | collective-permute-start | bytes 92168 | tf_op jit(solution)/shard_map/ppermute | solution.py:399
  67.8 0.0 collective-permute-done.18.b
  67.8 0.5 collective-permute-done.19.c
  68.4 1.7 %collective-permute-done.20.d = bf16[40,384]{1,0:T(8,128)(2,1)S(1)} collective-permute-done((bf16[40,384]{1,0:T(8,128)(2,1)S(1)}, bf16[40,384]{1,0:T(8,128)(2,1)S(1)}, u32[]{:S(2)}, u32[]{:S(2)}) %collective-permute-start.20) | collective-permute-done | bytes 30752 | tf_op jit(solution)/shard_map/ppermute | solution.py:399
  70.1 0.1 collective-permute-start.21
  70.2 1.2 %collective-permute-done.21.other_ref = bf16[48,384]{1,0:T(8,128)(2,1)S(1)} collective-permute-done((bf16[48,384]{1,0:T(8,128)(2,1)S(1)}, bf16[48,384]{1,0:T(8,128)(2,1)S(1)}, u32[]{:S(2)}, u32[]{:S(2)}) %collective-permute-start.21) | collective-permute-done | bytes 36896 | tf_op jit(solution)/shard_map/ppermute | solution.py:399
  71.4 0.8 %collective-permute-start.24 = (bf16[96,384]{1,0:T(8,128)(2,1)S(1)}, bf16[96,384]{1,0:T(8,128)(2,1)S(1)}, u32[]{:S(2)}, u32[]{:S(2)}) collective-permute-start(bf16[96,384]{1,0:T(8,128)(2,1)S(1)} %pair.1.refs_0_), channel_id=1, source_target_pairs={{0,5},{1,4},{2,7},{3,6},{4,1},{5,0},{6,3},{7,2},{8,13},{9,12},{10,... | collective-permute-start | bytes 221192 | tf_op jit(solution)/shard_map/ppermute | solution.py:540
  72.2 1.3 %collective-permute-start.23 = (bf16[96,384]{1,0:T(8,128)(2,1)S(1)}, bf16[96,384]{1,0:T(8,128)(2,1)S(1)}, u32[]{:S(2)}, u32[]{:S(2)}) collective-permute-start(bf16[96,384]{1,0:T(8,128)(2,1)S(1)} %pair.1.refs_0_), channel_id=1, source_target_pairs={{0,4},{1,5},{2,6},{3,7},{4,0},{5,1},{6,2},{7,3},{8,12},{9,13},{10,... | collective-permute-start | bytes 221192 | tf_op jit(solution)/shard_map/ppermute | solution.py:540
  73.5 1.5 %collective-permute-start.22 = (bf16[96,384]{1,0:T(8,128)(2,1)S(1)}, bf16[96,384]{1,0:T(8,128)(2,1)S(1)}, u32[]{:S(2)}, u32[]{:S(2)}) collective-permute-start(bf16[96,384]{1,0:T(8,128)(2,1)S(1)} %pair.1.refs_0_), channel_id=1, source_target_pairs={{0,1},{1,0},{2,3},{3,2},{4,5},{5,4},{6,7},{7,6},{8,9},{9,8},{10,11... | collective-permute-start | bytes 221192 | tf_op jit(solution)/shard_map/ppermute | solution.py:540
  75.0 2.5 %collective-permute-done.24.refs_3_ = bf16[96,384]{1,0:T(8,128)(2,1)S(1)} collective-permute-done((bf16[96,384]{1,0:T(8,128)(2,1)S(1)}, bf16[96,384]{1,0:T(8,128)(2,1)S(1)}, u32[]{:S(2)}, u32[]{:S(2)}) %collective-permute-start.24) | collective-permute-done | bytes 73760 | tf_op jit(solution)/shard_map/ppermute | solution.py:540
  77.5 0.3 collective-permute-done.23.refs_2_
  77.9 0.0 collective-permute-done.22.refs_1_
  77.9 0.7 join.1
  (9 shorter events, 0.1 us)
Async XLA Ops:
  0.6 5.6 %copy-start.4 = (s32[8,8]{1,0:T(8,128)S(1)}, s32[8,8]{1,0:T(8,128)}, u32[]{:S(2)}) copy-start(s32[8,8]{1,0:T(8,128)} %valid_ref.1) | copy-start | bytes 772
  0.6 5.6 %copy-start.2 = (bf16[1,4,8,8,160]{4,3,2,1,0:T(8,128)(2,1)S(1)}, bf16[1,4,8,8,160]{4,3,2,1,0:T(8,128)(2,1)}, u32[]{:S(2)}) copy-start(bf16[1,4,8,8,160]{4,3,2,1,0:T(8,128)(2,1)} %param.9) | copy-start | bytes 245764
  3.1 13.4 %collective-permute-start = (bf16[112,1536]{1,0:T(8,128)(2,1)}, bf16[112,1536]{1,0:T(8,128)(2,1)S(1)}, u32[]{:S(2)}, u32[]{:S(2)}) collective-permute-start(bf16[112,1536]{1,0:T(8,128)(2,1)} %payload.1), channel_id=1, source_target_pairs={{0,8},{8,16},{16,24},{24,0},{1,9},{9,17},{17,25},{25,1},{2,10},{10... | collective-permute-start | bytes 1032200 | tf_op jit(solution)/shard_map/ppermute | solution.py:28
  9.6 19.3 %collective-permute-start.2 = (bf16[64,4864]{1,0:T(8,128)(2,1)S(1)}, bf16[64,4864]{1,0:T(8,128)(2,1)S(1)}, u32[]{:S(2)}, u32[]{:S(2)}) collective-permute-start(bf16[64,4864]{1,0:T(8,128)(2,1)S(1)} %get-tuple-element.43), channel_id=1, source_target_pairs={{0,6},{2,0},{4,2},{6,4},{1,7},{3,1},{5,3},{7,5},{8,14},{10,8},{12,... | collective-permute-start | bytes 1867784 | tf_op jit(solution)/shard_map/ppermute | solution.py:28
  10.3 18.6 %collective-permute-start.3 = (bf16[64,4864]{1,0:T(8,128)(2,1)S(1)}, bf16[64,4864]{1,0:T(8,128)(2,1)S(1)}, u32[]{:S(2)}, u32[]{:S(2)}) collective-permute-start(bf16[64,4864]{1,0:T(8,128)(2,1)S(1)} %get-tuple-element.44), channel_id=1, source_target_pairs={{0,7},{1,6},{2,1},{3,0},{4,3},{5,2},{6,5},{7,4},{8,15},{9,14},{10,... | collective-permute-start | bytes 1867784 | tf_op jit(solution)/shard_map/ppermute | solution.py:451
  16.5 11.0 %collective-permute-start.1 = (bf16[112,1536]{1,0:T(8,128)(2,1)S(1)}, bf16[112,1536]{1,0:T(8,128)(2,1)S(1)}, u32[]{:S(2)}, u32[]{:S(2)}) collective-permute-start(bf16[112,1536]{1,0:T(8,128)(2,1)S(1)} %collective-permute-done.refs_8_.refs_3_), channel_id=1, source_target_pairs={{0,8},{8,16},{16,24},{24,0},{1,9},{9,17},{17,25},{25,1},{2,10},{10... | collective-permute-start | bytes 1032200 | tf_op jit(solution)/shard_map/ppermute | solution.py:28
  27.6 8.3 %collective-permute-start.5 = (bf16[112,1536]{1,0:T(8,128)(2,1)S(1)}, bf16[112,1536]{1,0:T(8,128)(2,1)S(1)}, u32[]{:S(2)}, u32[]{:S(2)}) collective-permute-start(bf16[112,1536]{1,0:T(8,128)(2,1)S(1)} %collective-permute-done.1.refs_12_.refs_7_), channel_id=1, source_target_pairs={{0,4},{2,6},{4,0},{6,2},{1,5},{3,7},{5,1},{7,3},{8,12},{10,14},{12... | collective-permute-start | bytes 1032200 | tf_op jit(solution)/shard_map/ppermute | solution.py:399
  28.8 14.2 %collective-permute-start.4 = (bf16[64,4864]{1,0:T(8,128)(2,1)S(1)}, bf16[64,4864]{1,0:T(8,128)(2,1)S(1)}, u32[]{:S(2)}, u32[]{:S(2)}) collective-permute-start(bf16[64,4864]{1,0:T(8,128)(2,1)S(1)} %get-tuple-element.45), channel_id=1, source_target_pairs={{0,1},{1,0},{2,3},{3,2},{4,5},{5,4},{6,7},{7,6},{8,9},{9,8},{10,11... | collective-permute-start | bytes 1867784 | tf_op jit(solution)/shard_map/ppermute | solution.py:28
  30.3 6.7 %collective-permute-start.7 = (bf16[112,1536]{1,0:T(8,128)(2,1)S(1)}, bf16[112,1536]{1,0:T(8,128)(2,1)S(1)}, u32[]{:S(2)}, u32[]{:S(2)}) collective-permute-start(bf16[112,1536]{1,0:T(8,128)(2,1)S(1)} %collective-permute-done.refs_8_.refs_3_), channel_id=1, source_target_pairs={{0,2},{2,0},{4,6},{6,4},{1,3},{3,1},{5,7},{7,5},{8,10},{10,8},{12,... | collective-permute-start | bytes 1032200 | tf_op jit(solution)/shard_map/ppermute | solution.py:399
  30.3 12.7 %collective-permute-start.12 = (bf16[112,1536]{1,0:T(8,128)(2,1)S(1)}, bf16[112,1536]{1,0:T(8,128)(2,1)S(1)}, u32[]{:S(2)}, u32[]{:S(2)}) collective-permute-start(bf16[112,1536]{1,0:T(8,128)(2,1)S(1)} %collective-permute-done.1.refs_12_.refs_7_), channel_id=1, source_target_pairs={{0,8},{8,16},{16,24},{24,0},{1,9},{9,17},{17,25},{25,1},{2,10},{10... | collective-permute-start | bytes 1032200 | tf_op jit(solution)/shard_map/ppermute | solution.py:28
  35.9 7.4 %collective-permute-start.6 = (bf16[112,1536]{1,0:T(8,128)(2,1)S(1)}, bf16[112,1536]{1,0:T(8,128)(2,1)S(1)}, u32[]{:S(2)}, u32[]{:S(2)}) collective-permute-start(bf16[112,1536]{1,0:T(8,128)(2,1)S(1)} %collective-permute-done.refs_8_.refs_3_), channel_id=1, source_target_pairs={{0,4},{2,6},{4,0},{6,2},{1,5},{3,7},{5,1},{7,3},{8,12},{10,14},{12... | collective-permute-start | bytes 1032200 | tf_op jit(solution)/shard_map/ppermute | solution.py:399
  37.1 12.9 %collective-permute-start.8 = (bf16[112,1536]{1,0:T(8,128)(2,1)S(1)}, bf16[112,1536]{1,0:T(8,128)(2,1)S(1)}, u32[]{:S(2)}, u32[]{:S(2)}) collective-permute-start(bf16[112,1536]{1,0:T(8,128)(2,1)S(1)} %collective-permute-done.5.refs_13_.refs_8_), channel_id=1, source_target_pairs={{0,8},{8,16},{16,24},{24,0},{1,9},{9,17},{17,25},{25,1},{2,10},{10... | collective-permute-start | bytes 1032200 | tf_op jit(solution)/shard_map/ppermute | solution.py:28
  37.1 12.9 %collective-permute-start.11 = (bf16[112,1536]{1,0:T(8,128)(2,1)S(1)}, bf16[112,1536]{1,0:T(8,128)(2,1)S(1)}, u32[]{:S(2)}, u32[]{:S(2)}) collective-permute-start(bf16[112,1536]{1,0:T(8,128)(2,1)S(1)} %collective-permute-done.5.refs_13_.refs_8_), channel_id=1, source_target_pairs={{0,2},{2,0},{4,6},{6,4},{1,3},{3,1},{5,7},{7,5},{8,10},{10,8},{12,... | collective-permute-start | bytes 1032200 | tf_op jit(solution)/shard_map/ppermute | solution.py:399
  43.0 7.0 %collective-permute-start.13 = (bf16[112,1536]{1,0:T(8,128)(2,1)S(1)}, bf16[112,1536]{1,0:T(8,128)(2,1)S(1)}, u32[]{:S(2)}, u32[]{:S(2)}) collective-permute-start(bf16[112,1536]{1,0:T(8,128)(2,1)S(1)} %collective-permute-done.12.refs_16_.refs_11_), channel_id=1, source_target_pairs={{0,2},{2,0},{4,6},{6,4},{1,3},{3,1},{5,7},{7,5},{8,10},{10,8},{12,... | collective-permute-start | bytes 1032200 | tf_op jit(solution)/shard_map/ppermute | solution.py:399
  43.3 8.3 %copy-start = (bf16[384,1536]{1,0:T(8,128)(2,1)S(1)}, bf16[384,1536]{1,0:T(8,128)(2,1)}, u32[]{:S(2)}) copy-start(bf16[384,1536]{1,0:T(8,128)(2,1)} %refs_0_.1) | copy-start | bytes 3538948
  43.3 8.3 %copy-start.1 = (bf16[384,160]{0,1:T(8,128)(2,1)S(1)}, bf16[384,160]{0,1:T(8,128)(2,1)}, u32[]{:S(2)}) copy-start(bf16[384,160]{0,1:T(8,128)(2,1)} %param.12) | copy-start | bytes 368644
  43.3 8.3 %copy-start.3 = (bf16[384]{0:T(512)(128)(2,1)S(1)}, bf16[384]{0:T(512)(128)(2,1)}, u32[]{:S(2)}) copy-start(bf16[384]{0:T(512)(128)(2,1)} %refs_2_.1) | copy-start | bytes 2308
  43.3 8.3 %copy-start.5 = (f32[5]{0:T(128)S(1)}, f32[5]{0:T(128)}, u32[]{:S(2)}) copy-start(f32[5]{0:T(128)} %var_ref.1) | copy-start | bytes 64
  43.3 8.4 %copy-start.6 = (f32[32]{0:T(128)S(1)}, f32[32]{0:T(128)}, u32[]{:S(2)}) copy-start(f32[32]{0:T(128)} %constant.2.clone.lat_ref) | copy-start | bytes 388
  43.3 6.7 %collective-permute-start.9 = (bf16[112,1536]{1,0:T(8,128)(2,1)S(1)}, bf16[112,1536]{1,0:T(8,128)(2,1)S(1)}, u32[]{:S(2)}, u32[]{:S(2)}) collective-permute-start(bf16[112,1536]{1,0:T(8,128)(2,1)S(1)} %collective-permute-done.6.refs_9_.refs_4_), channel_id=1, source_target_pairs={{0,2},{2,0},{4,6},{6,4},{1,3},{3,1},{5,7},{7,5},{8,10},{10,8},{12,... | collective-permute-start | bytes 1032200 | tf_op jit(solution)/shard_map/ppermute | solution.py:399
  43.6 6.4 %collective-permute-start.10 = (bf16[112,1536]{1,0:T(8,128)(2,1)S(1)}, bf16[112,1536]{1,0:T(8,128)(2,1)S(1)}, u32[]{:S(2)}, u32[]{:S(2)}) collective-permute-start(bf16[112,1536]{1,0:T(8,128)(2,1)S(1)} %collective-permute-done.1.refs_12_.refs_7_), channel_id=1, source_target_pairs={{0,2},{2,0},{4,6},{6,4},{1,3},{3,1},{5,7},{7,5},{8,10},{10,8},{12,... | collective-permute-start | bytes 1032200 | tf_op jit(solution)/shard_map/ppermute | solution.py:399
  50.0 1.7 %collective-permute-start.14 = (bf16[112,1536]{1,0:T(8,128)(2,1)S(1)}, bf16[112,1536]{1,0:T(8,128)(2,1)S(1)}, u32[]{:S(2)}, u32[]{:S(2)}) collective-permute-start(bf16[112,1536]{1,0:T(8,128)(2,1)S(1)} %collective-permute-done.8.refs_17_.refs_12_), channel_id=1, source_target_pairs={{0,2},{2,0},{4,6},{6,4},{1,3},{3,1},{5,7},{7,5},{8,10},{10,8},{12,... | collective-permute-start | bytes 1032200 | tf_op jit(solution)/shard_map/ppermute | solution.py:399
  55.4 5.5 %collective-permute-start.15 = (bf16[40,1536]{1,0:T(8,128)(2,1)S(1)}, bf16[40,1536]{1,0:T(8,128)(2,1)S(1)}, u32[]{:S(2)}, u32[]{:S(2)}) collective-permute-start(bf16[40,1536]{1,0:T(8,128)(2,1)S(1)} %get-tuple-element.61), channel_id=1, source_target_pairs={{0,2},{2,0},{4,6},{6,4},{1,3},{3,1},{5,7},{7,5},{8,10},{10,8},{12,... | collective-permute-start | bytes 368648 | tf_op jit(solution)/shard_map/ppermute | solution.py:399
  55.6 6.2 %collective-permute-start.16 = (bf16[40,1536]{1,0:T(8,128)(2,1)S(1)}, bf16[40,1536]{1,0:T(8,128)(2,1)S(1)}, u32[]{:S(2)}, u32[]{:S(2)}) collective-permute-start(bf16[40,1536]{1,0:T(8,128)(2,1)S(1)} %get-tuple-element.62), channel_id=1, source_target_pairs={{0,4},{2,6},{4,0},{6,2},{1,5},{3,7},{5,1},{7,3},{8,12},{10,14},{12... | collective-permute-start | bytes 368648 | tf_op jit(solution)/shard_map/ppermute | solution.py:399
  56.1 7.2 %collective-permute-start.17 = (bf16[40,1536]{1,0:T(8,128)(2,1)S(1)}, bf16[40,1536]{1,0:T(8,128)(2,1)S(1)}, u32[]{:S(2)}, u32[]{:S(2)}) collective-permute-start(bf16[40,1536]{1,0:T(8,128)(2,1)S(1)} %get-tuple-element.63), channel_id=1, source_target_pairs={{0,6},{2,4},{4,2},{6,0},{1,7},{3,5},{5,3},{7,1},{8,14},{10,12},{12... | collective-permute-start | bytes 368648 | tf_op jit(solution)/shard_map/ppermute | solution.py:399
  63.4 4.5 %collective-permute-start.18 = (bf16[40,384]{1,0:T(8,128)(2,1)S(1)}, bf16[40,384]{1,0:T(8,128)(2,1)S(1)}, u32[]{:S(2)}, u32[]{:S(2)}) collective-permute-start(bf16[40,384]{1,0:T(8,128)(2,1)S(1)} %get-tuple-element.74), channel_id=1, source_target_pairs={{0,8},{8,0},{16,24},{24,16},{1,9},{9,1},{17,25},{25,17},{2,10},{10... | collective-permute-start | bytes 92168 | tf_op jit(solution)/shard_map/ppermute | solution.py:399
  63.4 4.9 %collective-permute-start.19 = (bf16[40,384]{1,0:T(8,128)(2,1)S(1)}, bf16[40,384]{1,0:T(8,128)(2,1)S(1)}, u32[]{:S(2)}, u32[]{:S(2)}) collective-permute-start(bf16[40,384]{1,0:T(8,128)(2,1)S(1)} %get-tuple-element.75), channel_id=1, source_target_pairs={{0,16},{8,24},{16,0},{24,8},{1,17},{9,25},{17,1},{25,9},{2,18},{10... | collective-permute-start | bytes 92168 | tf_op jit(solution)/shard_map/ppermute | solution.py:399
  63.6 6.5 %collective-permute-start.20 = (bf16[40,384]{1,0:T(8,128)(2,1)S(1)}, bf16[40,384]{1,0:T(8,128)(2,1)S(1)}, u32[]{:S(2)}, u32[]{:S(2)}) collective-permute-start(bf16[40,384]{1,0:T(8,128)(2,1)S(1)} %get-tuple-element.76), channel_id=1, source_target_pairs={{0,24},{8,16},{16,8},{24,0},{1,25},{9,17},{17,9},{25,1},{2,26},{10... | collective-permute-start | bytes 92168 | tf_op jit(solution)/shard_map/ppermute | solution.py:399
  70.1 1.3 %collective-permute-start.21 = (bf16[48,384]{1,0:T(8,128)(2,1)S(1)}, bf16[48,384]{1,0:T(8,128)(2,1)S(1)}, u32[]{:S(2)}, u32[]{:S(2)}) collective-permute-start(bf16[48,384]{1,0:T(8,128)(2,1)S(1)} %dp_sum.1.mine_ref), channel_id=1, source_target_pairs={{0,2},{2,0},{4,6},{6,4},{1,3},{3,1},{5,7},{7,5},{8,10},{10,8},{12,... | collective-permute-start | bytes 110600 | tf_op jit(solution)/shard_map/ppermute | solution.py:399
  71.4 6.1 %collective-permute-start.24 = (bf16[96,384]{1,0:T(8,128)(2,1)S(1)}, bf16[96,384]{1,0:T(8,128)(2,1)S(1)}, u32[]{:S(2)}, u32[]{:S(2)}) collective-permute-start(bf16[96,384]{1,0:T(8,128)(2,1)S(1)} %pair.1.refs_0_), channel_id=1, source_target_pairs={{0,5},{1,4},{2,7},{3,6},{4,1},{5,0},{6,3},{7,2},{8,13},{9,12},{10,... | collective-permute-start | bytes 221192 | tf_op jit(solution)/shard_map/ppermute | solution.py:540
  72.2 5.6 %collective-permute-start.23 = (bf16[96,384]{1,0:T(8,128)(2,1)S(1)}, bf16[96,384]{1,0:T(8,128)(2,1)S(1)}, u32[]{:S(2)}, u32[]{:S(2)}) collective-permute-start(bf16[96,384]{1,0:T(8,128)(2,1)S(1)} %pair.1.refs_0_), channel_id=1, source_target_pairs={{0,4},{1,5},{2,6},{3,7},{4,0},{5,1},{6,2},{7,3},{8,12},{9,13},{10,... | collective-permute-start | bytes 221192 | tf_op jit(solution)/shard_map/ppermute | solution.py:540
  73.5 4.4 %collective-permute-start.22 = (bf16[96,384]{1,0:T(8,128)(2,1)S(1)}, bf16[96,384]{1,0:T(8,128)(2,1)S(1)}, u32[]{:S(2)}, u32[]{:S(2)}) collective-permute-start(bf16[96,384]{1,0:T(8,128)(2,1)S(1)} %pair.1.refs_0_), channel_id=1, source_target_pairs={{0,1},{1,0},{2,3},{3,2},{4,5},{5,4},{6,7},{7,6},{8,9},{9,8},{10,11... | collective-permute-start | bytes 221192 | tf_op jit(solution)/shard_map/ppermute | solution.py:540

commit v17 on v15

--- a/solution.py
+++ b/solution.py
@@ -495,7 +495,7 @@
         name="forward",
     )(lat_table, var_weight, ctx, *tiles, w_out, unpatch_t, norm_gain, *pieces)
 
-    terms = [terms[0]] + [swap(terms[b], "lat", b) for b in (1, 2, 3)]
+    terms = [terms[0]] + [swap(terms[b], "lat", b) for b in (3, 2, 1)]
     grad_context = pl.pallas_call(
         backward_kernel,
         out_shape=shape((tokens, width), BF),
@@ -516,7 +516,7 @@
         compiler_params=params(4),
         name="lat_sum",
     )(*terms)
-    parts = [parts[0]] + [swap(parts[k], "dp", k) for k in (1, 2, 3)]
+    parts = [parts[0]] + [swap(parts[k], "dp", k) for k in (3, 2, 1)]
     mine = pl.pallas_call(
         dp_sum_kernel,
         out_shape=shape((piece + 8, rows), BF),

time: 78.4 us -> 77.6 us (0.990)
  transfers between devices with their start and end apart: 25 -> 25, of which waited for: 17 -> 16; matrix products, arithmetic and copies ran while one was open for 0% -> 0% of each run, Pallas kernels for 13% -> 13%
where the time goes in v17:
time: 77.6 us; the launch traced here: 77.5 us
  waiting for transfers between devices  39.1 us (50%)
  starting transfers between devices  20.7 us (27%)
  Pallas kernels  16.9 us (22%)
    ppermute x6, waiting for transfers between devices, from_behind(): lax.ppermute(array, axis, [(i, (i + by) % length) for i in range(length)])  22 us
    ppermute x15, waiting for transfers between devices, swap(): lax.ppermute(array, axis, [(i, i ^ bit) for i in range(lax.axis_size(axis...  13.5 us
    ppermute x15, starting transfers between devices, swap(): lax.ppermute(array, axis, [(i, i ^ bit) for i in range(lax.axis_size(axis...  9.98 us
    ppermute x6, starting transfers between devices, from_behind(): lax.ppermute(array, axis, [(i, (i + by) % length) for i in range(length)])  5.31 us
    pallas_call x1, Pallas kernels, shards(): pl.pallas_call(forward_kernel, grid=(1,), out_shape=[shape((piece, width)...  3.71 us
    pallas_call x1, Pallas kernels, shards(): pl.pallas_call(backward_kernel, out_shape=shape((tokens, width), BF), in_...  3.64 us
    ppermute x3, waiting for transfers between devices, shards(): plane.append(lax.ppermute(chip, ('lat', 'lon'), pairs))  3.58 us
    ppermute x3, starting transfers between devices, shards(): plane.append(lax.ppermute(chip, ('lat', 'lon'), pairs))  3.55 us
  transfers between devices with their start and end apart: 25, of which 16 were waited for; matrix products, arithmetic and copies ran while one was open for 0% of the time, Pallas kernels for 13%

profile of v17, /device:TPU:0, one launch (start us, length us, event | category | flops | bytes accessed | tf_op | source)
XLA Modules:
  0.0 77.5 jit_solution(5140371212546638494)
XLA Ops:
  0.6 0.0 copy-start.4
  0.6 0.0 copy-start.2
  0.7 2.5 %payload.1 = bf16[112,1536]{1,0:T(8,128)(2,1)} custom-call(bf16[384,1536]{1,0:T(8,128)(2,1)} %refs_0_.1, bf16[160,384]{1,0:T(8,128)(2,1)} %bitcast.6, bf16[384]{0:T(512)(128)(2,1)} %refs_2_.1), custom_call_target="tpu_custom_call" | custom-call | tf_op jit(solution)/shard_map/payload/pallas_call | solution.py:419
  3.1 3.1 %collective-permute-start = (bf16[112,1536]{1,0:T(8,128)(2,1)}, bf16[112,1536]{1,0:T(8,128)(2,1)S(1)}, u32[]{:S(2)}, u32[]{:S(2)}) collective-permute-start(bf16[112,1536]{1,0:T(8,128)(2,1)} %payload.1), channel_id=1, source_target_pairs={{0,8},{8,16},{16,24},{24,0},{1,9},{9,17},{17,25},{25,1},{2,10},{10... | collective-permute-start | bytes 1032200 | tf_op jit(solution)/shard_map/ppermute | solution.py:28
  6.2 0.0 copy-done.4
  6.2 0.0 copy-done.2
  6.2 3.3 %pack.1 = (bf16[64,4864]{1,0:T(8,128)(2,1)S(1)}, bf16[64,4864]{1,0:T(8,128)(2,1)S(1)}, bf16[64,4864]{1,0:T(8,128)(2,1)S(1)}, bf16[64,4864]{1,0:T(8,128)(2,1)S(1)}) custom-call(bf16[4,8,8,4608]{3,2,1,0:T(8,128)(2,1)} %bitcast.10, bf16[4,8,8,160]{3,2,1,0:T(8,128)(2,1)S(1)} %bitcast.9, s32[8,8]{1,0:T(8,128)S(1)} %copy-done.4), custom_call_target="tpu_custom_call" | custom-call | tf_op jit(solution)/shard_map/pack/pallas_call | solution.py:429
  9.6 0.7 collective-permute-start.2
  10.3 1.9 %collective-permute-start.3 = (bf16[64,4864]{1,0:T(8,128)(2,1)S(1)}, bf16[64,4864]{1,0:T(8,128)(2,1)S(1)}, u32[]{:S(2)}, u32[]{:S(2)}) collective-permute-start(bf16[64,4864]{1,0:T(8,128)(2,1)S(1)} %get-tuple-element.44), channel_id=1, source_target_pairs={{0,7},{1,6},{2,1},{3,0},{4,3},{5,2},{6,5},{7,4},{8,15},{9,14},{10,... | collective-permute-start | bytes 1867784 | tf_op jit(solution)/shard_map/ppermute | solution.py:451
  12.2 4.4 %collective-permute-done.refs_8_.refs_3_ = bf16[112,1536]{1,0:T(8,128)(2,1)S(1)} collective-permute-done((bf16[112,1536]{1,0:T(8,128)(2,1)}, bf16[112,1536]{1,0:T(8,128)(2,1)S(1)}, u32[]{:S(2)}, u32[]{:S(2)}) %collective-permute-start) | collective-permute-done | bytes 344096 | tf_op jit(solution)/shard_map/ppermute | solution.py:28
  16.5 0.0 collective-permute-start.1
  16.5 11.0 %collective-permute-done.1.refs_12_.refs_7_ = bf16[112,1536]{1,0:T(8,128)(2,1)S(1)} collective-permute-done((bf16[112,1536]{1,0:T(8,128)(2,1)S(1)}, bf16[112,1536]{1,0:T(8,128)(2,1)S(1)}, u32[]{:S(2)}, u32[]{:S(2)}) %collective-permute-start.1) | collective-permute-done | bytes 344096 | tf_op jit(solution)/shard_map/ppermute | solution.py:28
  27.6 1.3 %collective-permute-start.5 = (bf16[112,1536]{1,0:T(8,128)(2,1)S(1)}, bf16[112,1536]{1,0:T(8,128)(2,1)S(1)}, u32[]{:S(2)}, u32[]{:S(2)}) collective-permute-start(bf16[112,1536]{1,0:T(8,128)(2,1)S(1)} %collective-permute-done.1.refs_12_.refs_7_), channel_id=1, source_target_pairs={{0,4},{2,6},{4,0},{6,2},{1,5},{3,7},{5,1},{7,3},{8,12},{10,14},{12... | collective-permute-start | bytes 1032200 | tf_op jit(solution)/shard_map/ppermute | solution.py:399
  28.8 0.0 collective-permute-done.2.refs_2_.refs_3_
  28.8 0.0 collective-permute-done.3.refs_3_.refs_4_
  28.8 1.5 %collective-permute-start.4 = (bf16[64,4864]{1,0:T(8,128)(2,1)S(1)}, bf16[64,4864]{1,0:T(8,128)(2,1)S(1)}, u32[]{:S(2)}, u32[]{:S(2)}) collective-permute-start(bf16[64,4864]{1,0:T(8,128)(2,1)S(1)} %get-tuple-element.45), channel_id=1, source_target_pairs={{0,1},{1,0},{2,3},{3,2},{4,5},{5,4},{6,7},{7,6},{8,9},{9,8},{10,11... | collective-permute-start | bytes 1867784 | tf_op jit(solution)/shard_map/ppermute | solution.py:28
  30.3 0.0 collective-permute-start.12
  30.3 5.6 %collective-permute-done.5.refs_13_.refs_8_ = bf16[112,1536]{1,0:T(8,128)(2,1)S(1)} collective-permute-done((bf16[112,1536]{1,0:T(8,128)(2,1)S(1)}, bf16[112,1536]{1,0:T(8,128)(2,1)S(1)}, u32[]{:S(2)}, u32[]{:S(2)}) %collective-permute-start.5) | collective-permute-done | bytes 344096 | tf_op jit(solution)/shard_map/ppermute | solution.py:399
  35.9 1.2 %collective-permute-start.6 = (bf16[112,1536]{1,0:T(8,128)(2,1)S(1)}, bf16[112,1536]{1,0:T(8,128)(2,1)S(1)}, u32[]{:S(2)}, u32[]{:S(2)}) collective-permute-start(bf16[112,1536]{1,0:T(8,128)(2,1)S(1)} %collective-permute-done.refs_8_.refs_3_), channel_id=1, source_target_pairs={{0,4},{2,6},{4,0},{6,2},{1,5},{3,7},{5,1},{7,3},{8,12},{10,14},{12... | collective-permute-start | bytes 1032200 | tf_op jit(solution)/shard_map/ppermute | solution.py:399
  37.1 0.0 collective-permute-start.7
  37.1 0.0 collective-permute-start.11
  37.1 4.7 %collective-permute-done.12.refs_16_.refs_11_ = bf16[112,1536]{1,0:T(8,128)(2,1)S(1)} collective-permute-done((bf16[112,1536]{1,0:T(8,128)(2,1)S(1)}, bf16[112,1536]{1,0:T(8,128)(2,1)S(1)}, u32[]{:S(2)}, u32[]{:S(2)}) %collective-permute-start.12) | collective-permute-done | bytes 344096 | tf_op jit(solution)/shard_map/ppermute | solution.py:28
  41.8 0.0 collective-permute-start.13
  41.8 1.2 %collective-permute-done.4.refs_1_.refs_2_ = bf16[64,4864]{1,0:T(8,128)(2,1)S(1)} collective-permute-done((bf16[64,4864]{1,0:T(8,128)(2,1)S(1)}, bf16[64,4864]{1,0:T(8,128)(2,1)S(1)}, u32[]{:S(2)}, u32[]{:S(2)}) %collective-permute-start.4) | collective-permute-done | bytes 622624 | tf_op jit(solution)/shard_map/ppermute | solution.py:28
  43.0 0.3 collective-permute-done.6.refs_9_.refs_4_
  43.3 0.0 copy-start.6
  43.3 0.1 collective-permute-start.8
  43.4 0.5 collective-permute-start.9
  43.9 2.8 %attention.1.refs_0_ = bf16[256,1536]{1,0:T(8,128)(2,1)S(1)} custom-call(bf16[64,4864]{1,0:T(8,128)(2,1)S(1)} %get-tuple-element.49.refs_0_.refs_1_, bf16[64,4864]{1,0:T(8,128)(2,1)S(1)} %collective-permute-done.4.refs_1_.refs_2_, bf16[64,4864]{1,0:T(8,128)(2,1)S(1)} %collective-permute-done.2.refs_2_.refs_3_, ...), custom_call_target="tpu_custom_call" | custom-call | tf_op jit(solution)/shard_map/attention/pallas_call | solution.py:462
  46.7 0.7 collective-permute-done.7.refs_17_.refs_12_
  47.4 0.0 collective-permute-start.10
  47.4 0.0 collective-permute-done.11.refs_15_.refs_10_
  47.4 0.5 collective-permute-start.14
  47.9 0.0 collective-permute-done.13.refs_18_.refs_13_
  47.9 0.0 collective-permute-done.8.refs_10_.refs_5_
  47.9 0.0 collective-permute-done.9.refs_11_.refs_6_
  47.9 1.1 %collective-permute-done.10.refs_14_.refs_9_ = bf16[112,1536]{1,0:T(8,128)(2,1)S(1)} collective-permute-done((bf16[112,1536]{1,0:T(8,128)(2,1)S(1)}, bf16[112,1536]{1,0:T(8,128)(2,1)S(1)}, u32[]{:S(2)}, u32[]{:S(2)}) %collective-permute-start.10) | collective-permute-done | bytes 344096 | tf_op jit(solution)/shard_map/ppermute | solution.py:399
  49.1 0.5 collective-permute-done.14.refs_19_.refs_14_
  49.6 0.0 copy-done
  49.6 0.0 copy-done.1
  49.6 3.7 %forward.1 = (bf16[40,1536]{1,0:T(8,128)(2,1)S(1)}, bf16[40,1536]{1,0:T(8,128)(2,1)S(1)}, bf16[40,1536]{1,0:T(8,128)(2,1)S(1)}, bf16[40,1536]{1,0:T(8,128)(2,1)S...) custom-call(f32[32]{0:T(128)S(1)} %copy-done.6, ...), custom_call_target="tpu_custom_call" | custom-call | tf_op jit(solution)/shard_map/forward/pallas_call | solution.py:483
  53.3 0.9 %collective-permute-start.15 = (bf16[40,1536]{1,0:T(8,128)(2,1)S(1)}, bf16[40,1536]{1,0:T(8,128)(2,1)S(1)}, u32[]{:S(2)}, u32[]{:S(2)}) collective-permute-start(bf16[40,1536]{1,0:T(8,128)(2,1)S(1)} %get-tuple-element.61), channel_id=1, source_target_pairs={{0,6},{2,4},{4,2},{6,0},{1,7},{3,5},{5,3},{7,1},{8,14},{10,12},{12... | collective-permute-start | bytes 368648 | tf_op jit(solution)/shard_map/ppermute | solution.py:399
  54.2 0.9 %collective-permute-start.16 = (bf16[40,1536]{1,0:T(8,128)(2,1)S(1)}, bf16[40,1536]{1,0:T(8,128)(2,1)S(1)}, u32[]{:S(2)}, u32[]{:S(2)}) collective-permute-start(bf16[40,1536]{1,0:T(8,128)(2,1)S(1)} %get-tuple-element.62), channel_id=1, source_target_pairs={{0,4},{2,6},{4,0},{6,2},{1,5},{3,7},{5,1},{7,3},{8,12},{10,14},{12... | collective-permute-start | bytes 368648 | tf_op jit(solution)/shard_map/ppermute | solution.py:399
  55.2 0.1 collective-permute-start.17
  55.2 3.6 %backward.1 = bf16[256,1536]{1,0:T(8,128)(2,1)} custom-call(f32[256,1536]{1,0:T(8,128)S(1)} %get-tuple-element.64.normed_ref, f32[256,128]{1,0:T(8,128)S(1)} %get-tuple-element.65.inv_ref, bf16[256,160]{1,0:T(8,128)(2,1)S(1)} %get-tuple-element.66.dfc_ref, bf16[384,1536]{1,0:T(8,128)(2,1)S(1)} %copy-done, bf16[160,384]{1,0:T(8,128)(2,1)S(1)} %bitcast.8, ...), custom_call_target="tpu_custom_call" | custom-call | tf_op jit(solution)/shard_map/backward/pallas_call | solution.py:499
  58.9 0.0 collective-permute-done.15.b
  58.9 2.7 %collective-permute-done.16.c = bf16[40,1536]{1,0:T(8,128)(2,1)S(1)} collective-permute-done((bf16[40,1536]{1,0:T(8,128)(2,1)S(1)}, bf16[40,1536]{1,0:T(8,128)(2,1)S(1)}, u32[]{:S(2)}, u32[]{:S(2)}) %collective-permute-start.16) | collective-permute-done | bytes 122912 | tf_op jit(solution)/shard_map/ppermute | solution.py:399
  61.6 0.0 collective-permute-done.17.d
  61.6 0.1 lat_sum.1
  61.7 1.2 %collective-permute-start.18 = (bf16[40,384]{1,0:T(8,128)(2,1)S(1)}, bf16[40,384]{1,0:T(8,128)(2,1)S(1)}, u32[]{:S(2)}, u32[]{:S(2)}) collective-permute-start(bf16[40,384]{1,0:T(8,128)(2,1)S(1)} %get-tuple-element.74), channel_id=1, source_target_pairs={{0,24},{8,16},{16,8},{24,0},{1,25},{9,17},{17,9},{25,1},{2,26},{10... | collective-permute-start | bytes 92168 | tf_op jit(solution)/shard_map/ppermute | solution.py:399
  62.9 0.6 collective-permute-start.19
  63.5 2.7 %collective-permute-start.20 = (bf16[40,384]{1,0:T(8,128)(2,1)S(1)}, bf16[40,384]{1,0:T(8,128)(2,1)S(1)}, u32[]{:S(2)}, u32[]{:S(2)}) collective-permute-start(bf16[40,384]{1,0:T(8,128)(2,1)S(1)} %get-tuple-element.76), channel_id=1, source_target_pairs={{0,8},{8,0},{16,24},{24,16},{1,9},{9,1},{17,25},{25,17},{2,10},{10... | collective-permute-start | bytes 92168 | tf_op jit(solution)/shard_map/ppermute | solution.py:399
  66.2 1.6 %collective-permute-done.18.b = bf16[40,384]{1,0:T(8,128)(2,1)S(1)} collective-permute-done((bf16[40,384]{1,0:T(8,128)(2,1)S(1)}, bf16[40,384]{1,0:T(8,128)(2,1)S(1)}, u32[]{:S(2)}, u32[]{:S(2)}) %collective-permute-start.18) | collective-permute-done | bytes 30752 | tf_op jit(solution)/shard_map/ppermute | solution.py:399
  67.8 0.5 collective-permute-done.19.c
  68.3 0.0 collective-permute-done.20.d
  68.3 0.1 collective-permute-start.21
  68.4 1.2 %collective-permute-done.21.other_ref = bf16[48,384]{1,0:T(8,128)(2,1)S(1)} collective-permute-done((bf16[48,384]{1,0:T(8,128)(2,1)S(1)}, bf16[48,384]{1,0:T(8,128)(2,1)S(1)}, u32[]{:S(2)}, u32[]{:S(2)}) %collective-permute-start.21) | collective-permute-done | bytes 36896 | tf_op jit(solution)/shard_map/ppermute | solution.py:399
  69.6 1.8 %collective-permute-start.24 = (bf16[96,384]{1,0:T(8,128)(2,1)S(1)}, bf16[96,384]{1,0:T(8,128)(2,1)S(1)}, u32[]{:S(2)}, u32[]{:S(2)}) collective-permute-start(bf16[96,384]{1,0:T(8,128)(2,1)S(1)} %pair.1.refs_0_), channel_id=1, source_target_pairs={{0,5},{1,4},{2,7},{3,6},{4,1},{5,0},{6,3},{7,2},{8,13},{9,12},{10,... | collective-permute-start | bytes 221192 | tf_op jit(solution)/shard_map/ppermute | solution.py:539
  71.4 1.0 %collective-permute-start.23 = (bf16[96,384]{1,0:T(8,128)(2,1)S(1)}, bf16[96,384]{1,0:T(8,128)(2,1)S(1)}, u32[]{:S(2)}, u32[]{:S(2)}) collective-permute-start(bf16[96,384]{1,0:T(8,128)(2,1)S(1)} %pair.1.refs_0_), channel_id=1, source_target_pairs={{0,4},{1,5},{2,6},{3,7},{4,0},{5,1},{6,2},{7,3},{8,12},{9,13},{10,... | collective-permute-start | bytes 221192 | tf_op jit(solution)/shard_map/ppermute | solution.py:539
  72.4 0.8 collective-permute-start.22
  73.2 1.8 %collective-permute-done.24.refs_3_ = bf16[96,384]{1,0:T(8,128)(2,1)S(1)} collective-permute-done((bf16[96,384]{1,0:T(8,128)(2,1)S(1)}, bf16[96,384]{1,0:T(8,128)(2,1)S(1)}, u32[]{:S(2)}, u32[]{:S(2)}) %collective-permute-start.24) | collective-permute-done | bytes 73760 | tf_op jit(solution)/shard_map/ppermute | solution.py:539
  75.0 1.5 %collective-permute-done.23.refs_2_ = bf16[96,384]{1,0:T(8,128)(2,1)S(1)} collective-permute-done((bf16[96,384]{1,0:T(8,128)(2,1)S(1)}, bf16[96,384]{1,0:T(8,128)(2,1)S(1)}, u32[]{:S(2)}, u32[]{:S(2)}) %collective-permute-start.23) | collective-permute-done | bytes 73760 | tf_op jit(solution)/shard_map/ppermute | solution.py:539
  76.5 0.3 collective-permute-done.22.refs_1_
  76.7 0.7 join.1
  (9 shorter events, 0.1 us)
Async XLA Ops:
  0.6 5.6 %copy-start.4 = (s32[8,8]{1,0:T(8,128)S(1)}, s32[8,8]{1,0:T(8,128)}, u32[]{:S(2)}) copy-start(s32[8,8]{1,0:T(8,128)} %valid_ref.1) | copy-start | bytes 772
  0.6 5.6 %copy-start.2 = (bf16[1,4,8,8,160]{4,3,2,1,0:T(8,128)(2,1)S(1)}, bf16[1,4,8,8,160]{4,3,2,1,0:T(8,128)(2,1)}, u32[]{:S(2)}) copy-start(bf16[1,4,8,8,160]{4,3,2,1,0:T(8,128)(2,1)} %param.9) | copy-start | bytes 245764
  3.1 13.4 %collective-permute-start = (bf16[112,1536]{1,0:T(8,128)(2,1)}, bf16[112,1536]{1,0:T(8,128)(2,1)S(1)}, u32[]{:S(2)}, u32[]{:S(2)}) collective-permute-start(bf16[112,1536]{1,0:T(8,128)(2,1)} %payload.1), channel_id=1, source_target_pairs={{0,8},{8,16},{16,24},{24,0},{1,9},{9,17},{17,25},{25,1},{2,10},{10... | collective-permute-start | bytes 1032200 | tf_op jit(solution)/shard_map/ppermute | solution.py:28
  9.6 19.3 %collective-permute-start.2 = (bf16[64,4864]{1,0:T(8,128)(2,1)S(1)}, bf16[64,4864]{1,0:T(8,128)(2,1)S(1)}, u32[]{:S(2)}, u32[]{:S(2)}) collective-permute-start(bf16[64,4864]{1,0:T(8,128)(2,1)S(1)} %get-tuple-element.43), channel_id=1, source_target_pairs={{0,6},{2,0},{4,2},{6,4},{1,7},{3,1},{5,3},{7,5},{8,14},{10,8},{12,... | collective-permute-start | bytes 1867784 | tf_op jit(solution)/shard_map/ppermute | solution.py:28
  10.3 18.6 %collective-permute-start.3 = (bf16[64,4864]{1,0:T(8,128)(2,1)S(1)}, bf16[64,4864]{1,0:T(8,128)(2,1)S(1)}, u32[]{:S(2)}, u32[]{:S(2)}) collective-permute-start(bf16[64,4864]{1,0:T(8,128)(2,1)S(1)} %get-tuple-element.44), channel_id=1, source_target_pairs={{0,7},{1,6},{2,1},{3,0},{4,3},{5,2},{6,5},{7,4},{8,15},{9,14},{10,... | collective-permute-start | bytes 1867784 | tf_op jit(solution)/shard_map/ppermute | solution.py:451
  16.5 11.0 %collective-permute-start.1 = (bf16[112,1536]{1,0:T(8,128)(2,1)S(1)}, bf16[112,1536]{1,0:T(8,128)(2,1)S(1)}, u32[]{:S(2)}, u32[]{:S(2)}) collective-permute-start(bf16[112,1536]{1,0:T(8,128)(2,1)S(1)} %collective-permute-done.refs_8_.refs_3_), channel_id=1, source_target_pairs={{0,8},{8,16},{16,24},{24,0},{1,9},{9,17},{17,25},{25,1},{2,10},{10... | collective-permute-start | bytes 1032200 | tf_op jit(solution)/shard_map/ppermute | solution.py:28
  27.6 8.3 %collective-permute-start.5 = (bf16[112,1536]{1,0:T(8,128)(2,1)S(1)}, bf16[112,1536]{1,0:T(8,128)(2,1)S(1)}, u32[]{:S(2)}, u32[]{:S(2)}) collective-permute-start(bf16[112,1536]{1,0:T(8,128)(2,1)S(1)} %collective-permute-done.1.refs_12_.refs_7_), channel_id=1, source_target_pairs={{0,4},{2,6},{4,0},{6,2},{1,5},{3,7},{5,1},{7,3},{8,12},{10,14},{12... | collective-permute-start | bytes 1032200 | tf_op jit(solution)/shard_map/ppermute | solution.py:399
  28.8 14.2 %collective-permute-start.4 = (bf16[64,4864]{1,0:T(8,128)(2,1)S(1)}, bf16[64,4864]{1,0:T(8,128)(2,1)S(1)}, u32[]{:S(2)}, u32[]{:S(2)}) collective-permute-start(bf16[64,4864]{1,0:T(8,128)(2,1)S(1)} %get-tuple-element.45), channel_id=1, source_target_pairs={{0,1},{1,0},{2,3},{3,2},{4,5},{5,4},{6,7},{7,6},{8,9},{9,8},{10,11... | collective-permute-start | bytes 1867784 | tf_op jit(solution)/shard_map/ppermute | solution.py:28
  30.3 11.4 %collective-permute-start.12 = (bf16[112,1536]{1,0:T(8,128)(2,1)S(1)}, bf16[112,1536]{1,0:T(8,128)(2,1)S(1)}, u32[]{:S(2)}, u32[]{:S(2)}) collective-permute-start(bf16[112,1536]{1,0:T(8,128)(2,1)S(1)} %collective-permute-done.1.refs_12_.refs_7_), channel_id=1, source_target_pairs={{0,8},{8,16},{16,24},{24,0},{1,9},{9,17},{17,25},{25,1},{2,10},{10... | collective-permute-start | bytes 1032200 | tf_op jit(solution)/shard_map/ppermute | solution.py:28
  35.9 7.4 %collective-permute-start.6 = (bf16[112,1536]{1,0:T(8,128)(2,1)S(1)}, bf16[112,1536]{1,0:T(8,128)(2,1)S(1)}, u32[]{:S(2)}, u32[]{:S(2)}) collective-permute-start(bf16[112,1536]{1,0:T(8,128)(2,1)S(1)} %collective-permute-done.refs_8_.refs_3_), channel_id=1, source_target_pairs={{0,4},{2,6},{4,0},{6,2},{1,5},{3,7},{5,1},{7,3},{8,12},{10,14},{12... | collective-permute-start | bytes 1032200 | tf_op jit(solution)/shard_map/ppermute | solution.py:399
  37.1 10.3 %collective-permute-start.7 = (bf16[112,1536]{1,0:T(8,128)(2,1)S(1)}, bf16[112,1536]{1,0:T(8,128)(2,1)S(1)}, u32[]{:S(2)}, u32[]{:S(2)}) collective-permute-start(bf16[112,1536]{1,0:T(8,128)(2,1)S(1)} %collective-permute-done.5.refs_13_.refs_8_), channel_id=1, source_target_pairs={{0,8},{8,16},{16,24},{24,0},{1,9},{9,17},{17,25},{25,1},{2,10},{10... | collective-permute-start | bytes 1032200 | tf_op jit(solution)/shard_map/ppermute | solution.py:28
  37.1 10.3 %collective-permute-start.11 = (bf16[112,1536]{1,0:T(8,128)(2,1)S(1)}, bf16[112,1536]{1,0:T(8,128)(2,1)S(1)}, u32[]{:S(2)}, u32[]{:S(2)}) collective-permute-start(bf16[112,1536]{1,0:T(8,128)(2,1)S(1)} %collective-permute-done.5.refs_13_.refs_8_), channel_id=1, source_target_pairs={{0,2},{2,0},{4,6},{6,4},{1,3},{3,1},{5,7},{7,5},{8,10},{10,8},{12,... | collective-permute-start | bytes 1032200 | tf_op jit(solution)/shard_map/ppermute | solution.py:399
  41.8 6.1 %collective-permute-start.13 = (bf16[112,1536]{1,0:T(8,128)(2,1)S(1)}, bf16[112,1536]{1,0:T(8,128)(2,1)S(1)}, u32[]{:S(2)}, u32[]{:S(2)}) collective-permute-start(bf16[112,1536]{1,0:T(8,128)(2,1)S(1)} %collective-permute-done.12.refs_16_.refs_11_), channel_id=1, source_target_pairs={{0,2},{2,0},{4,6},{6,4},{1,3},{3,1},{5,7},{7,5},{8,10},{10,8},{12,... | collective-permute-start | bytes 1032200 | tf_op jit(solution)/shard_map/ppermute | solution.py:399
  43.3 6.3 %copy-start = (bf16[384,1536]{1,0:T(8,128)(2,1)S(1)}, bf16[384,1536]{1,0:T(8,128)(2,1)}, u32[]{:S(2)}) copy-start(bf16[384,1536]{1,0:T(8,128)(2,1)} %refs_0_.1) | copy-start | bytes 3538948
  43.3 6.3 %copy-start.1 = (bf16[384,160]{0,1:T(8,128)(2,1)S(1)}, bf16[384,160]{0,1:T(8,128)(2,1)}, u32[]{:S(2)}) copy-start(bf16[384,160]{0,1:T(8,128)(2,1)} %param.12) | copy-start | bytes 368644
  43.3 6.3 %copy-start.3 = (bf16[384]{0:T(512)(128)(2,1)S(1)}, bf16[384]{0:T(512)(128)(2,1)}, u32[]{:S(2)}) copy-start(bf16[384]{0:T(512)(128)(2,1)} %refs_2_.1) | copy-start | bytes 2308
  43.3 6.3 %copy-start.5 = (f32[5]{0:T(128)S(1)}, f32[5]{0:T(128)}, u32[]{:S(2)}) copy-start(f32[5]{0:T(128)} %var_ref.1) | copy-start | bytes 64
  43.3 6.3 %copy-start.6 = (f32[32]{0:T(128)S(1)}, f32[32]{0:T(128)}, u32[]{:S(2)}) copy-start(f32[32]{0:T(128)} %constant.2.clone.lat_ref) | copy-start | bytes 388
  43.3 4.6 %collective-permute-start.8 = (bf16[112,1536]{1,0:T(8,128)(2,1)S(1)}, bf16[112,1536]{1,0:T(8,128)(2,1)S(1)}, u32[]{:S(2)}, u32[]{:S(2)}) collective-permute-start(bf16[112,1536]{1,0:T(8,128)(2,1)S(1)} %collective-permute-done.refs_8_.refs_3_), channel_id=1, source_target_pairs={{0,2},{2,0},{4,6},{6,4},{1,3},{3,1},{5,7},{7,5},{8,10},{10,8},{12,... | collective-permute-start | bytes 1032200 | tf_op jit(solution)/shard_map/ppermute | solution.py:399
  43.4 4.5 %collective-permute-start.9 = (bf16[112,1536]{1,0:T(8,128)(2,1)S(1)}, bf16[112,1536]{1,0:T(8,128)(2,1)S(1)}, u32[]{:S(2)}, u32[]{:S(2)}) collective-permute-start(bf16[112,1536]{1,0:T(8,128)(2,1)S(1)} %collective-permute-done.6.refs_9_.refs_4_), channel_id=1, source_target_pairs={{0,2},{2,0},{4,6},{6,4},{1,3},{3,1},{5,7},{7,5},{8,10},{10,8},{12,... | collective-permute-start | bytes 1032200 | tf_op jit(solution)/shard_map/ppermute | solution.py:399
  47.4 1.7 %collective-permute-start.10 = (bf16[112,1536]{1,0:T(8,128)(2,1)S(1)}, bf16[112,1536]{1,0:T(8,128)(2,1)S(1)}, u32[]{:S(2)}, u32[]{:S(2)}) collective-permute-start(bf16[112,1536]{1,0:T(8,128)(2,1)S(1)} %collective-permute-done.1.refs_12_.refs_7_), channel_id=1, source_target_pairs={{0,2},{2,0},{4,6},{6,4},{1,3},{3,1},{5,7},{7,5},{8,10},{10,8},{12,... | collective-permute-start | bytes 1032200 | tf_op jit(solution)/shard_map/ppermute | solution.py:399
  47.4 2.1 %collective-permute-start.14 = (bf16[112,1536]{1,0:T(8,128)(2,1)S(1)}, bf16[112,1536]{1,0:T(8,128)(2,1)S(1)}, u32[]{:S(2)}, u32[]{:S(2)}) collective-permute-start(bf16[112,1536]{1,0:T(8,128)(2,1)S(1)} %collective-permute-done.7.refs_17_.refs_12_), channel_id=1, source_target_pairs={{0,2},{2,0},{4,6},{6,4},{1,3},{3,1},{5,7},{7,5},{8,10},{10,8},{12,... | collective-permute-start | bytes 1032200 | tf_op jit(solution)/shard_map/ppermute | solution.py:399
  53.3 5.6 %collective-permute-start.15 = (bf16[40,1536]{1,0:T(8,128)(2,1)S(1)}, bf16[40,1536]{1,0:T(8,128)(2,1)S(1)}, u32[]{:S(2)}, u32[]{:S(2)}) collective-permute-start(bf16[40,1536]{1,0:T(8,128)(2,1)S(1)} %get-tuple-element.61), channel_id=1, source_target_pairs={{0,6},{2,4},{4,2},{6,0},{1,7},{3,5},{5,3},{7,1},{8,14},{10,12},{12... | collective-permute-start | bytes 368648 | tf_op jit(solution)/shard_map/ppermute | solution.py:399
  54.2 7.4 %collective-permute-start.16 = (bf16[40,1536]{1,0:T(8,128)(2,1)S(1)}, bf16[40,1536]{1,0:T(8,128)(2,1)S(1)}, u32[]{:S(2)}, u32[]{:S(2)}) collective-permute-start(bf16[40,1536]{1,0:T(8,128)(2,1)S(1)} %get-tuple-element.62), channel_id=1, source_target_pairs={{0,4},{2,6},{4,0},{6,2},{1,5},{3,7},{5,1},{7,3},{8,12},{10,14},{12... | collective-permute-start | bytes 368648 | tf_op jit(solution)/shard_map/ppermute | solution.py:399
  55.2 6.5 %collective-permute-start.17 = (bf16[40,1536]{1,0:T(8,128)(2,1)S(1)}, bf16[40,1536]{1,0:T(8,128)(2,1)S(1)}, u32[]{:S(2)}, u32[]{:S(2)}) collective-permute-start(bf16[40,1536]{1,0:T(8,128)(2,1)S(1)} %get-tuple-element.63), channel_id=1, source_target_pairs={{0,2},{2,0},{4,6},{6,4},{1,3},{3,1},{5,7},{7,5},{8,10},{10,8},{12,... | collective-permute-start | bytes 368648 | tf_op jit(solution)/shard_map/ppermute | solution.py:399
  61.7 6.0 %collective-permute-start.18 = (bf16[40,384]{1,0:T(8,128)(2,1)S(1)}, bf16[40,384]{1,0:T(8,128)(2,1)S(1)}, u32[]{:S(2)}, u32[]{:S(2)}) collective-permute-start(bf16[40,384]{1,0:T(8,128)(2,1)S(1)} %get-tuple-element.74), channel_id=1, source_target_pairs={{0,24},{8,16},{16,8},{24,0},{1,25},{9,17},{17,9},{25,1},{2,26},{10... | collective-permute-start | bytes 92168 | tf_op jit(solution)/shard_map/ppermute | solution.py:399
  62.9 5.3 %collective-permute-start.19 = (bf16[40,384]{1,0:T(8,128)(2,1)S(1)}, bf16[40,384]{1,0:T(8,128)(2,1)S(1)}, u32[]{:S(2)}, u32[]{:S(2)}) collective-permute-start(bf16[40,384]{1,0:T(8,128)(2,1)S(1)} %get-tuple-element.75), channel_id=1, source_target_pairs={{0,16},{8,24},{16,0},{24,8},{1,17},{9,25},{17,1},{25,9},{2,18},{10... | collective-permute-start | bytes 92168 | tf_op jit(solution)/shard_map/ppermute | solution.py:399
  63.5 4.7 %collective-permute-start.20 = (bf16[40,384]{1,0:T(8,128)(2,1)S(1)}, bf16[40,384]{1,0:T(8,128)(2,1)S(1)}, u32[]{:S(2)}, u32[]{:S(2)}) collective-permute-start(bf16[40,384]{1,0:T(8,128)(2,1)S(1)} %get-tuple-element.76), channel_id=1, source_target_pairs={{0,8},{8,0},{16,24},{24,16},{1,9},{9,1},{17,25},{25,17},{2,10},{10... | collective-permute-start | bytes 92168 | tf_op jit(solution)/shard_map/ppermute | solution.py:399
  68.3 1.3 %collective-permute-start.21 = (bf16[48,384]{1,0:T(8,128)(2,1)S(1)}, bf16[48,384]{1,0:T(8,128)(2,1)S(1)}, u32[]{:S(2)}, u32[]{:S(2)}) collective-permute-start(bf16[48,384]{1,0:T(8,128)(2,1)S(1)} %dp_sum.1.mine_ref), channel_id=1, source_target_pairs={{0,2},{2,0},{4,6},{6,4},{1,3},{3,1},{5,7},{7,5},{8,10},{10,8},{12,... | collective-permute-start | bytes 110600 | tf_op jit(solution)/shard_map/ppermute | solution.py:399
  69.6 5.4 %collective-permute-start.24 = (bf16[96,384]{1,0:T(8,128)(2,1)S(1)}, bf16[96,384]{1,0:T(8,128)(2,1)S(1)}, u32[]{:S(2)}, u32[]{:S(2)}) collective-permute-start(bf16[96,384]{1,0:T(8,128)(2,1)S(1)} %pair.1.refs_0_), channel_id=1, source_target_pairs={{0,5},{1,4},{2,7},{3,6},{4,1},{5,0},{6,3},{7,2},{8,13},{9,12},{10,... | collective-permute-start | bytes 221192 | tf_op jit(solution)/shard_map/ppermute | solution.py:539
  71.4 5.1 %collective-permute-start.23 = (bf16[96,384]{1,0:T(8,128)(2,1)S(1)}, bf16[96,384]{1,0:T(8,128)(2,1)S(1)}, u32[]{:S(2)}, u32[]{:S(2)}) collective-permute-start(bf16[96,384]{1,0:T(8,128)(2,1)S(1)} %pair.1.refs_0_), channel_id=1, source_target_pairs={{0,4},{1,5},{2,6},{3,7},{4,0},{5,1},{6,2},{7,3},{8,12},{9,13},{10,... | collective-permute-start | bytes 221192 | tf_op jit(solution)/shard_map/ppermute | solution.py:539
  72.4 4.4 %collective-permute-start.22 = (bf16[96,384]{1,0:T(8,128)(2,1)S(1)}, bf16[96,384]{1,0:T(8,128)(2,1)S(1)}, u32[]{:S(2)}, u32[]{:S(2)}) collective-permute-start(bf16[96,384]{1,0:T(8,128)(2,1)S(1)} %pair.1.refs_0_), channel_id=1, source_target_pairs={{0,1},{1,0},{2,3},{3,2},{4,5},{5,4},{6,7},{7,6},{8,9},{9,8},{10,11... | collective-permute-start | bytes 221192 | tf_op jit(solution)/shard_map/ppermute | solution.py:539
